TPU v7x, 32 devices: a whole 2x2x4 slice. The times are simulated.
32 devices in a mesh: dp: 8 (over y, x, core), tensor: 4 (over z).
Axes of the slice: x: 2, y: 2, z: 4, core: 2. Of those that a mesh axis runs over, the one named last changes fastest.
Arguments:
- hidden_in: bfloat16 [3, 4096, 768], P(None, ('dp', 'tensor')), may hold values from -6 to 6
- segment_ids: int32 [3, 32, 128], P(None, ('dp', 'tensor')), may hold values from 0 to 7, never falling along the last dimension, each value on 1 to 32 neighbouring positions
- pooled_grad: float32 [3, 32, 8, 768], P(None, ('dp', 'tensor')), may hold values from -96 to 96
- qkv_weight: bfloat16 [3, 768, 768], P(None, 'dp', 'tensor'), may hold values from -0.21875 to 0.21875
- qv_bias: bfloat16 [2, 768], P(None, ('dp', 'tensor')), may hold values from -1.1953125 to 1.1953125
- out_weight: bfloat16 [768, 768], P('tensor', 'dp'), may hold values from -0.875 to 0.875
- out_bias: bfloat16 [768], P(('dp', 'tensor')), may hold values from -1.1953125 to 1.1953125
- norm1_gain: bfloat16 [768], P(('dp', 'tensor')), may hold values from 0.099609375 to 1.8984375
- norm1_shift: bfloat16 [768], P(('dp', 'tensor')), may hold values from -1.1953125 to 1.1953125
- up_weight: bfloat16 [768, 3072], P('dp', 'tensor'), may hold values from -0.21875 to 0.21875
- up_bias: bfloat16 [3072], P(('dp', 'tensor')), may hold values from -1.1953125 to 1.1953125
- down_weight: bfloat16 [3072, 768], P('tensor', 'dp'), may hold values from -0.109375 to 0.109375
- down_bias: bfloat16 [768], P(('dp', 'tensor')), may hold values from -1.1953125 to 1.1953125
- norm2_gain: bfloat16 [768], P(('dp', 'tensor')), may hold values from 0.099609375 to 1.8984375
- norm2_shift: bfloat16 [768], P(('dp', 'tensor')), may hold values from -1.1953125 to 1.1953125
Outputs:
- pooled_out: float32 [3, 32, 8, 768], P(None, ('dp', 'tensor'))
- input_grad: float32 [3, 4096, 768], P(None, ('dp', 'tensor'))
- qkv_weight_grad: float32 [3, 768, 768], P(None, 'dp', 'tensor')
- qv_bias_grad: float32 [2, 768], P(None, ('dp', 'tensor'))
- out_weight_grad: float32 [768, 768], P('tensor', 'dp')
- out_bias_grad: float32 [768], P(('dp', 'tensor'))
- norm1_gain_grad: float32 [768], P(('dp', 'tensor'))
- norm1_shift_grad: float32 [768], P(('dp', 'tensor'))
- up_weight_grad: float32 [768, 3072], P('dp', 'tensor')
- up_bias_grad: float32 [3072], P(('dp', 'tensor'))
- down_weight_grad: float32 [3072, 768], P('tensor', 'dp')
- down_bias_grad: float32 [768], P(('dp', 'tensor'))
- norm2_gain_grad: float32 [768], P(('dp', 'tensor'))
- norm2_shift_grad: float32 [768], P(('dp', 'tensor'))
Inputs may be any that keep to these rules, and one draw needn't show every extreme that they name: `segment_ids`: in every row of 128 tokens the segment numbers never fall, each number from 0 to 7 occurs on 1 to 32 consecutive tokens, and some sentence has exactly 32 tokens.
All inputs are finite; a program needn't handle non-finite values.
Results may differ from a plain program's by a relative error of at most 0.013.
Values may be sent and summed in bfloat16 or wider, within the bound.
No kernel may reach another device: no remote copies, remote signals or barrier semaphores. Data moves between devices by JAX's collectives and lax.ppermute only.
A program may use at most 128 MiB of HBM per device.

v0:
```python
from functools import partial

import jax
import jax.numpy as jnp
from jax import lax
from jax.sharding import PartitionSpec as P

HD = 64


EPS = 1e-12
NEG = -1000000000.0
highest = lax.Precision.HIGHEST


def round_low(values):
    return lax.optimization_barrier(values.astype(jnp.bfloat16)).astype(jnp.float32)


def normalize(values, gain, shift):
    center = values - jnp.mean(values, axis=-1, keepdims=True)
    inverse = lax.rsqrt(jnp.mean(center * center, axis=-1, keepdims=True) + EPS)
    normed = center * inverse
    return (normed * gain + shift, normed, inverse)


def normalize_back(grad_out, normed, inverse, gain):
    scaled = grad_out * gain
    grad_in = inverse * (
        scaled
        - jnp.mean(scaled, axis=-1, keepdims=True)
        - normed * jnp.mean(scaled * normed, axis=-1, keepdims=True)
    )
    return (grad_in, jnp.sum(grad_out * normed, axis=0), jnp.sum(grad_out, axis=0))


def block_size(seq_count, seq_len):
    largest = max(1, 512 // seq_len)
    chosen = 1
    for trial in range(1, seq_count + 1):
        if seq_count % trial == 0 and trial <= largest:
            chosen = trial
    return chosen


def masked_scores(query_blk, key_blk, seg_blk, score_scale):
    raw_scores = (
        jnp.einsum("gqhd,gkhd->ghqk", query_blk, key_blk, preferred_element_type=jnp.float32)
        * score_scale
    )
    same_segment = seg_blk[:, None, :, None] == seg_blk[:, None, None, :]
    return jnp.where(same_segment, raw_scores, NEG)


def per_device(
    hidden_in,
    segment_ids,
    pooled_grad,
    qkv_weight,
    qv_bias,
    out_weight,
    out_bias,
    norm1_gain,
    norm1_shift,
    up_weight,
    up_bias,
    down_weight,
    down_bias,
    norm2_gain,
    norm2_shift,
):
    micro_total = hidden_in.shape[0]
    rows_local = hidden_in.shape[1]
    model_width = hidden_in.shape[2]
    seq_len = segment_ids.shape[2]
    seqs_local = segment_ids.shape[1]
    seg_count = pooled_grad.shape[2]
    tensor_rank = lax.axis_index("tensor")
    score_scale = float(HD) ** (-0.5)
    gathered = (
        lax.all_gather(qv_bias, ("dp", "tensor"), axis=1, tiled=True),
        lax.all_gather(out_bias, ("dp", "tensor"), axis=0, tiled=True),
        lax.all_gather(norm1_gain, ("dp", "tensor"), axis=0, tiled=True),
        lax.all_gather(norm1_shift, ("dp", "tensor"), axis=0, tiled=True),
        lax.all_gather(up_bias, ("dp", "tensor"), axis=0, tiled=True),
        lax.all_gather(down_bias, ("dp", "tensor"), axis=0, tiled=True),
        lax.all_gather(norm2_gain, ("dp", "tensor"), axis=0, tiled=True),
        lax.all_gather(norm2_shift, ("dp", "tensor"), axis=0, tiled=True),
    )
    qv_full, bias_out, gain_one, shift_one, up_full, bias_down, gain_two, shift_two = tuple(
        (item.astype(jnp.float32) for item in gathered)
    )
    head_cols = qkv_weight.shape[2]
    hidden_cols = up_weight.shape[1]
    heads_local = head_cols // HD
    bias_query = lax.dynamic_slice_in_dim(qv_full[0], tensor_rank * head_cols, head_cols)
    bias_value = lax.dynamic_slice_in_dim(qv_full[1], tensor_rank * head_cols, head_cols)
    bias_up = lax.dynamic_slice_in_dim(up_full, tensor_rank * hidden_cols, hidden_cols)

    def fetch_weights():
        return (
            lax.all_gather(qkv_weight, "dp", axis=1, tiled=True),
            lax.all_gather(out_weight, "dp", axis=1, tiled=True),
            lax.all_gather(up_weight, "dp", axis=0, tiled=True),
            lax.all_gather(down_weight, "dp", axis=1, tiled=True),
        )

    full_shapes = (
        (3, model_width, head_cols),
        (head_cols, model_width),
        (model_width, hidden_cols),
        (hidden_cols, model_width),
    )
    totals = tuple((jnp.zeros(shape_now, jnp.float32) for shape_now in full_shapes))
    qv_grad_local = jnp.zeros((2, head_cols), jnp.float32)
    up_bias_local = jnp.zeros((hidden_cols,), jnp.float32)
    out_bias_part = jnp.zeros((model_width,), jnp.float32)
    down_bias_part = jnp.zeros((model_width,), jnp.float32)
    gain_one_part = jnp.zeros((model_width,), jnp.float32)
    shift_one_part = jnp.zeros((model_width,), jnp.float32)
    gain_two_part = jnp.zeros((model_width,), jnp.float32)
    shift_two_part = jnp.zeros((model_width,), jnp.float32)
    pooled_list = []
    input_list = []
    for batch_index in range(micro_total):
        qkv_now, out_now, up_now, down_now = fetch_weights()
        x_rows = hidden_in[batch_index]
        seg_rows = segment_ids[batch_index]
        x_group, seg_group = (
            lax.all_gather(x_rows, "tensor", axis=0, tiled=True),
            lax.all_gather(seg_rows, "tensor", axis=0, tiled=True),
        )
        tokens_all = x_group.shape[0]
        projected = jnp.einsum("rd,cde->cre", x_group, qkv_now, preferred_element_type=jnp.float32)
        query_rows = (projected[0] + bias_query).astype(jnp.bfloat16)
        key_rows = projected[1].astype(jnp.bfloat16)
        value_rows = (projected[2] + bias_value).astype(jnp.bfloat16)
        seq_group = seg_group.shape[0]
        per_block = block_size(seq_group, seq_len)
        block_total = seq_group // per_block

        def split_heads(tensor_in):
            return tensor_in.reshape(block_total, per_block, seq_len, heads_local, HD)

        seg_blocks = seg_group.reshape(block_total, per_block, seq_len)
        query_blocks = split_heads(query_rows)
        key_blocks = split_heads(key_rows)
        value_blocks = split_heads(value_rows)

        def attend_forward(inputs):
            query_blk, key_blk, value_blk, seg_blk = inputs
            scores = masked_scores(query_blk, key_blk, seg_blk, score_scale)
            row_max = jnp.max(scores, axis=-1, keepdims=True)
            exp_scores = jnp.exp(scores - row_max)
            row_sum = jnp.sum(exp_scores, axis=-1, keepdims=True)
            prob_low = (exp_scores / row_sum).astype(jnp.bfloat16)
            attended_blk = jnp.einsum(
                "ghqk,gkhd->gqhd", prob_low, value_blk, preferred_element_type=jnp.float32
            )
            return (attended_blk.astype(jnp.bfloat16), (row_max + jnp.log(row_sum))[..., 0])

        attended, lse_blocks = lax.map(
            attend_forward, (query_blocks, key_blocks, value_blocks, seg_blocks)
        )
        att_rows = attended.reshape(tokens_all, head_cols)
        branch_one = lax.psum_scatter(
            jnp.dot(att_rows, out_now, preferred_element_type=jnp.float32),
            "tensor",
            scatter_dimension=0,
            tiled=True,
        )
        pre_one = branch_one + bias_out + x_rows.astype(jnp.float32)
        out_one, normed_one, inverse_one = normalize(pre_one, gain_one, shift_one)
        normed_group = lax.all_gather(out_one.astype(jnp.bfloat16), "tensor", axis=0, tiled=True)
        up_act = jnp.dot(normed_group, up_now, preferred_element_type=jnp.float32) + bias_up
        hidden_act = jax.nn.gelu(up_act, approximate=False).astype(jnp.bfloat16)
        branch_two = lax.psum_scatter(
            jnp.dot(hidden_act, down_now, preferred_element_type=jnp.float32),
            "tensor",
            scatter_dimension=0,
            tiled=True,
        )
        pre_two = branch_two + bias_down + out_one
        out_two, normed_two, inverse_two = normalize(pre_two, gain_two, shift_two)
        onehot = (
            seg_rows[:, :, None] == jnp.arange(seg_count, dtype=jnp.int32)[None, None, :]
        ).astype(jnp.float32)
        counts = jnp.sum(onehot, axis=1)
        sums = jnp.einsum(
            "lts,ltd->lsd",
            onehot,
            out_two.reshape(seqs_local, seq_len, model_width),
            precision=highest,
        )
        pooled_list.append(sums / counts[:, :, None])
        grad_out = jnp.einsum(
            "lts,lsd->ltd", onehot, pooled_grad[batch_index] / counts[:, :, None], precision=highest
        ).reshape(rows_local, model_width)
        grad_pre_two, gain_two_now, shift_two_now = normalize_back(
            grad_out, normed_two, inverse_two, gain_two
        )
        gain_two_part = gain_two_part + gain_two_now
        shift_two_part = shift_two_part + shift_two_now
        down_bias_part = down_bias_part + jnp.sum(grad_pre_two, axis=0)
        qkv_back, out_back, up_back, down_back = fetch_weights()
        ffn_grad_group = lax.all_gather(
            grad_pre_two.astype(jnp.bfloat16), "tensor", axis=0, tiled=True
        )
        batch_down = jnp.einsum(
            "rf,rd->fd", hidden_act, ffn_grad_group, preferred_element_type=jnp.float32
        )
        hidden_grad = jnp.einsum(
            "rd,fd->rf", ffn_grad_group, down_back, preferred_element_type=jnp.float32
        )
        gelu_value, gelu_pull = jax.vjp(partial(jax.nn.gelu, approximate=False), up_act)
        up_grad = gelu_pull(hidden_grad)[0].astype(jnp.bfloat16)
        up_bias_local = up_bias_local + jnp.sum(up_grad.astype(jnp.float32), axis=0)
        batch_up = jnp.einsum(
            "rd,rf->df", normed_group, up_grad, preferred_element_type=jnp.float32
        )
        normed_back = lax.psum_scatter(
            jnp.einsum("rf,df->rd", up_grad, up_back, preferred_element_type=jnp.float32),
            "tensor",
            scatter_dimension=0,
            tiled=True,
        )
        normed_grad = round_low(normed_back) + grad_pre_two
        grad_pre_one, gain_one_now, shift_one_now = normalize_back(
            normed_grad, normed_one, inverse_one, gain_one
        )
        gain_one_part = gain_one_part + gain_one_now
        shift_one_part = shift_one_part + shift_one_now
        out_bias_part = out_bias_part + jnp.sum(grad_pre_one, axis=0)
        attn_grad_group = lax.all_gather(
            grad_pre_one.astype(jnp.bfloat16), "tensor", axis=0, tiled=True
        )
        batch_out = jnp.einsum(
            "re,rd->ed", att_rows, attn_grad_group, preferred_element_type=jnp.float32
        )
        att_grad = jnp.einsum(
            "rd,ed->re", attn_grad_group, out_back, preferred_element_type=jnp.float32
        ).astype(jnp.bfloat16)
        att_grad_blocks = split_heads(att_grad)

        def attend_backward(inputs):
            query_blk, key_blk, value_blk, seg_blk, lse_blk, grad_blk = inputs
            scores = masked_scores(query_blk, key_blk, seg_blk, score_scale)
            prob_rows = jnp.exp(scores - lse_blk[..., None])
            value_grad = jnp.einsum(
                "ghqk,gqhd->gkhd",
                prob_rows.astype(jnp.bfloat16),
                grad_blk,
                preferred_element_type=jnp.float32,
            )
            prob_grad = jnp.einsum(
                "gqhd,gkhd->ghqk", grad_blk, value_blk, preferred_element_type=jnp.float32
            )
            score_grad = prob_rows * (
                prob_grad - jnp.sum(prob_rows * prob_grad, axis=-1, keepdims=True)
            )
            score_low = score_grad.astype(jnp.bfloat16)
            query_grad = (
                jnp.einsum(
                    "ghqk,gkhd->gqhd", score_low, key_blk, preferred_element_type=jnp.float32
                )
                * score_scale
            )
            key_grad = (
                jnp.einsum(
                    "ghqk,gqhd->gkhd", score_low, query_blk, preferred_element_type=jnp.float32
                )
                * score_scale
            )
            return (
                query_grad.astype(jnp.bfloat16),
                key_grad.astype(jnp.bfloat16),
                value_grad.astype(jnp.bfloat16),
            )

        query_grads, key_grads, value_grads = lax.map(
            attend_backward,
            (query_blocks, key_blocks, value_blocks, seg_blocks, lse_blocks, att_grad_blocks),
        )
        qkv_grad = jnp.stack(
            [
                query_grads.reshape(tokens_all, head_cols),
                key_grads.reshape(tokens_all, head_cols),
                value_grads.reshape(tokens_all, head_cols),
            ]
        )
        qv_grad_local = qv_grad_local + jnp.stack(
            [
                jnp.sum(qkv_grad[0].astype(jnp.float32), axis=0),
                jnp.sum(qkv_grad[2].astype(jnp.float32), axis=0),
            ]
        )
        batch_qkv = jnp.einsum("rd,cre->cde", x_group, qkv_grad, preferred_element_type=jnp.float32)
        input_back = lax.psum_scatter(
            jnp.einsum(
                "cre,cde->rd", qkv_grad, qkv_back, preferred_element_type=jnp.float32
            ).astype(jnp.bfloat16),
            "tensor",
            scatter_dimension=0,
            tiled=True,
        ).astype(jnp.float32)
        input_list.append(input_back + grad_pre_one)
        totals = tuple(
            (
                running + update
                for running, update in zip(totals, (batch_qkv, batch_out, batch_up, batch_down))
            )
        )
    final_qkv = lax.psum_scatter(totals[0], "dp", scatter_dimension=1, tiled=True)
    final_out = lax.psum_scatter(totals[1], "dp", scatter_dimension=1, tiled=True)
    final_up = lax.psum_scatter(totals[2], "dp", scatter_dimension=0, tiled=True)
    final_down = lax.psum_scatter(totals[3], "dp", scatter_dimension=1, tiled=True)
    qv_place = lax.dynamic_update_slice_in_dim(
        jnp.zeros((2, model_width), jnp.float32), qv_grad_local, tensor_rank * head_cols, 1
    )
    up_place = lax.dynamic_update_slice_in_dim(
        jnp.zeros(up_full.shape, jnp.float32), up_bias_local, tensor_rank * hidden_cols, 0
    )
    vector_out = (
        lax.psum_scatter(qv_place, ("dp", "tensor"), scatter_dimension=1, tiled=True),
        lax.psum_scatter(out_bias_part, ("dp", "tensor"), scatter_dimension=0, tiled=True),
        lax.psum_scatter(gain_one_part, ("dp", "tensor"), scatter_dimension=0, tiled=True),
        lax.psum_scatter(shift_one_part, ("dp", "tensor"), scatter_dimension=0, tiled=True),
        lax.psum_scatter(up_place, ("dp", "tensor"), scatter_dimension=0, tiled=True),
        lax.psum_scatter(down_bias_part, ("dp", "tensor"), scatter_dimension=0, tiled=True),
        lax.psum_scatter(gain_two_part, ("dp", "tensor"), scatter_dimension=0, tiled=True),
        lax.psum_scatter(shift_two_part, ("dp", "tensor"), scatter_dimension=0, tiled=True),
    )
    return (
        jnp.stack(pooled_list),
        jnp.stack(input_list),
        final_qkv,
        vector_out[0],
        final_out,
        vector_out[1],
        vector_out[2],
        vector_out[3],
        final_up,
        vector_out[4],
        final_down,
        vector_out[5],
        vector_out[6],
        vector_out[7],
    )


def solution(mesh):
    return jax.shard_map(
        per_device,
        mesh=mesh,
        in_specs=(
            P(None, ("dp", "tensor"), None),
            P(None, ("dp", "tensor"), None),
            P(None, ("dp", "tensor"), None, None),
            P(None, "dp", "tensor"),
            P(None, ("dp", "tensor")),
            P("tensor", "dp"),
            P(("dp", "tensor")),
            P(("dp", "tensor")),
            P(("dp", "tensor")),
            P("dp", "tensor"),
            P(("dp", "tensor")),
            P("tensor", "dp"),
            P(("dp", "tensor")),
            P(("dp", "tensor")),
            P(("dp", "tensor")),
        ),
        out_specs=(
            P(None, ("dp", "tensor"), None, None),
            P(None, ("dp", "tensor"), None),
            P(None, "dp", "tensor"),
            P(None, ("dp", "tensor")),
            P("tensor", "dp"),
            P(("dp", "tensor")),
            P(("dp", "tensor")),
            P(("dp", "tensor")),
            P("dp", "tensor"),
            P(("dp", "tensor")),
            P("tensor", "dp"),
            P(("dp", "tensor")),
            P(("dp", "tensor")),
            P(("dp", "tensor")),
        ),
        check_vma=False,
    )
```

profile of v0, /device:TPU:0, one launch (start us, length us, event | category | flops | bytes accessed | tf_op | source)
XLA Modules:
  0.0 913.5 jit_solution(8620162350987136270)
XLA Ops:
  9.1 1.8 fusion.187
  10.9 21.3 %all-gather.4 = bf16[1,512,768]{2,1,0:T(8,128)(2,1)S(1)} all-gather(bf16[1,128,768]{2,1,0:T(8,128)(2,1)S(1)} %get-tuple-element.326), channel_id=6, replica_groups=mesh['dp'=8,'tensor'=4] {'tensor'}, dimensions={1}, use_global_device_ids=true | all-gather | bytes 983040 | tf_op jit(solution)/shard_map/all_gather | solution.py:130
  32.2 13.2 %all_gather.101 = bf16[3,768,192]{2,0,1:T(4,128)(2,1)S(1)} all-gather(bf16[3,96,192]{2,0,1:T(4,128)(2,1)S(1)} %copy.216), channel_id=1, replica_groups=mesh['dp'=8,'tensor'=4] {'dp'}, dimensions={1}, use_global_device_ids=true | all-gather | bytes 995328 | tf_op jit(solution)/shard_map/all_gather | solution.py:102
  47.5 9.2 %all-gather.5 = s32[4,1,128]{2,1,0:T(1,128)S(1)} all-gather(s32[1,1,128]{2,1,0:T(1,128)S(1)} %get-tuple-element.363), channel_id=7, replica_groups=mesh['dp'=8,'tensor'=4] {'tensor'}, dimensions={0}, use_global_device_ids=true | all-gather | bytes 2560 | tf_op jit(solution)/shard_map/all_gather | solution.py:131
  56.7 63.2 %all-gather.6 = bf16[32,24,2]{1,2,0:T(2,128)(2,1)S(1)} all-gather(bf16[1,24,2]{1,2,0:T(2,128)(2,1)S(1)} %bitcast.271), channel_id=1, replica_groups=mesh['dp'=8,'tensor'=4] {'dp','tensor'}, dimensions={0}, use_global_device_ids=true | all-gather | bytes 3168 | tf_op jit(solution)/shard_map/all_gather | solution.py:81
  121.5 8.4 all_gather.105
  135.7 27.3 %all-gather.2 = bf16[1,512,768]{2,1,0:T(8,128)(2,1)S(1)} all-gather(bf16[1,128,768]{2,1,0:T(8,128)(2,1)S(1)} %copy-done.79), channel_id=4, replica_groups=mesh['dp'=8,'tensor'=4] {'tensor'}, dimensions={1}, use_global_device_ids=true | all-gather | bytes 983040 | tf_op jit(solution)/shard_map/all_gather | solution.py:130
  166.5 12.2 %all-gather.3 = s32[4,1,128]{2,1,0:T(1,128)S(1)} all-gather(s32[1,1,128]{2,1,0:T(1,128)S(1)} %copy-done.149), channel_id=5, replica_groups=mesh['dp'=8,'tensor'=4] {'tensor'}, dimensions={0}, use_global_device_ids=true | all-gather | bytes 2560 | tf_op jit(solution)/shard_map/all_gather | solution.py:131
  182.2 22.7 %all-gather = bf16[1,512,768]{2,1,0:T(8,128)(2,1)S(1)} all-gather(bf16[1,128,768]{2,1,0:T(8,128)(2,1)S(1)} %get-tuple-element.325), channel_id=2, replica_groups=mesh['dp'=8,'tensor'=4] {'tensor'}, dimensions={1}, use_global_device_ids=true | all-gather | bytes 983040 | tf_op jit(solution)/shard_map/all_gather | solution.py:130
  204.9 2.6 convolution_bitcast_fusion.2
  211.0 11.9 %all-gather.1 = s32[4,1,128]{2,1,0:T(1,128)S(1)} all-gather(s32[1,1,128]{2,1,0:T(1,128)S(1)} %copy-done.148), channel_id=3, replica_groups=mesh['dp'=8,'tensor'=4] {'tensor'}, dimensions={0}, use_global_device_ids=true | all-gather | bytes 2560 | tf_op jit(solution)/shard_map/all_gather | solution.py:131
  230.0 39.8 %all-reduce.16 = (bf16[768]{0:T(1024)(128)(2,1)S(1)}, bf16[768]{0:T(1024)(128)(2,1)S(1)}, bf16[768]{0:T(1024)(128)(2,1)S(1)}, bf16[3072]{0:T(1024)(128)(2,1)S(1)...) all-reduce(bf16[768]{0:T(1024)(128)(2,1)S(1)} %dynamic-update-slice, ...), channel_id=1, replica_groups=mesh['dp'=8,'tensor'=4] {'dp','tensor'}, use_global_device_ids=true, to_apply=%add | all-reduce | flops 7680 | bytes 30720
  271.7 1.7 fusion.177
  275.8 18.6 %all_gather.121 = bf16[512,768]{1,0:T(8,128)(2,1)} all-gather(bf16[128,768]{1,0:T(8,128)(2,1)S(1)} %get-tuple-element.334), channel_id=1, replica_groups=mesh['dp'=8,'tensor'=4] {'tensor'}, dimensions={0}, use_global_device_ids=true | all-gather | bytes 983040 | tf_op jit(solution)/shard_map/all_gather | solution.py:174
  294.4 7.2 multiply_convert_fusion
  301.7 3.5 fusion.194
  305.2 22.7 %all_gather.118 = bf16[512,768]{1,0:T(8,128)(2,1)S(1)} all-gather(bf16[128,768]{1,0:T(8,128)(2,1)} %get-tuple-element.333), channel_id=1, replica_groups=mesh['dp'=8,'tensor'=4] {'tensor'}, dimensions={0}, use_global_device_ids=true | all-gather | bytes 983040 | tf_op jit(solution)/shard_map/all_gather | solution.py:174
  327.9 6.7 multiply_convert_fusion.1
  335.5 2.0 fusion.193
  337.6 22.6 %all_gather.109 = bf16[512,768]{1,0:T(8,128)(2,1)S(1)} all-gather(bf16[128,768]{1,0:T(8,128)(2,1)} %get-tuple-element.332), channel_id=1, replica_groups=mesh['dp'=8,'tensor'=4] {'tensor'}, dimensions={0}, use_global_device_ids=true | all-gather | bytes 983040 | tf_op jit(solution)/shard_map/all_gather | solution.py:174
  360.2 6.8 multiply_convert_fusion.2
  367.9 2.0 fusion.192
  375.6 1.9 fusion.137
  377.5 14.4 %reduce-scatter.28.cloned.1.call-done = f32[128,768]{1,0:T(8,128)} async-done(((f32[512,768]{1,0:T(8,128)}), f32[128,768]{1,0:T(8,128)}) %reduce-scatter.28.cloned.1.call-update) | async-done | bytes 393232 | tf_op jit(solution)/shard_map/reduce_scatter | solution.py:177
  391.9 36.4 %reduce-scatter.24.cloned.1.call-done = f32[128,768]{1,0:T(8,128)} async-done(((f32[512,768]{1,0:T(8,128)}), f32[128,768]{1,0:T(8,128)}) %reduce-scatter.24.cloned.1.call-update) | async-done | bytes 393232 | tf_op jit(solution)/shard_map/reduce_scatter | solution.py:177
  428.4 1.9 fusion.175
  431.0 1.8 multiply_reduce_fusion.5
  432.9 2.0 fusion.172
  436.2 18.1 %all_gather.126 = bf16[512,768]{1,0:T(8,128)(2,1)S(1)} all-gather(bf16[128,768]{1,0:T(8,128)(2,1)S(1)} %get-tuple-element.357), channel_id=1, replica_groups=mesh['dp'=8,'tensor'=4] {'tensor'}, dimensions={0}, use_global_device_ids=true | all-gather | bytes 983040 | tf_op jit(solution)/shard_map/all_gather | solution.py:206
  454.4 1.8 convert_reduce_fusion
  457.0 2.0 fusion.197
  459.1 25.1 %all_gather.122 = bf16[512,768]{1,0:T(8,128)(2,1)S(1)} all-gather(bf16[128,768]{1,0:T(8,128)(2,1)} %get-tuple-element.291), channel_id=1, replica_groups=mesh['dp'=8,'tensor'=4] {'tensor'}, dimensions={0}, use_global_device_ids=true | all-gather | bytes 983040 | tf_op jit(solution)/shard_map/all_gather | solution.py:206
  484.1 4.3 convert_reduce_fusion.2
  489.5 2.0 fusion.195
  491.5 23.0 %all_gather.124 = bf16[512,768]{1,0:T(8,128)(2,1)S(1)} all-gather(bf16[128,768]{1,0:T(8,128)(2,1)} %get-tuple-element.293), channel_id=1, replica_groups=mesh['dp'=8,'tensor'=4] {'tensor'}, dimensions={0}, use_global_device_ids=true | all-gather | bytes 983040 | tf_op jit(solution)/shard_map/all_gather | solution.py:206
  514.5 4.3 convert_reduce_fusion.1
  519.7 2.0 fusion.196
  525.1 1.7 convert_element_type.420
  526.8 19.5 %reduce-scatter.34.cloned.1.call-done = f32[128,768]{1,0:T(8,128)} async-done(((f32[512,768]{1,0:T(8,128)}), f32[128,768]{1,0:T(8,128)}) %reduce-scatter.34.cloned.1.call-update) | async-done | bytes 393232 | tf_op jit(solution)/shard_map/reduce_scatter | solution.py:221
  548.0 1.9 multiply_reduce_fusion.8
  551.0 31.9 %reduce-scatter.38.cloned.1.call-done = f32[128,768]{1,0:T(8,128)} async-done(((f32[512,768]{1,0:T(8,128)}), f32[128,768]{1,0:T(8,128)}) %reduce-scatter.38.cloned.1.call-update) | async-done | bytes 393232 | tf_op jit(solution)/shard_map/reduce_scatter | solution.py:221
  583.9 2.8 fusion.170
  586.7 18.5 %all_gather.123 = bf16[512,768]{1,0:T(8,128)(2,1)S(1)} all-gather(bf16[128,768]{1,0:T(8,128)(2,1)S(1)} %convert_element_type.390), channel_id=1, replica_groups=mesh['dp'=8,'tensor'=4] {'tensor'}, dimensions={0}, use_global_device_ids=true | all-gather | bytes 983040 | tf_op jit(solution)/shard_map/all_gather | solution.py:234
  607.7 1.7 fusion.169
  610.1 17.5 %all_gather.125 = bf16[512,768]{1,0:T(8,128)(2,1)S(1)} all-gather(bf16[128,768]{1,0:T(8,128)(2,1)S(1)} %convert_element_type.406), channel_id=1, replica_groups=mesh['dp'=8,'tensor'=4] {'tensor'}, dimensions={0}, use_global_device_ids=true | all-gather | bytes 983040 | tf_op jit(solution)/shard_map/all_gather | solution.py:234
  628.8 1.7 squeeze.132
  630.4 2.6 convert_reduce_fusion.5
  638.8 17.5 %all_gather.127 = bf16[512,768]{1,0:T(8,128)(2,1)S(1)} all-gather(bf16[128,768]{1,0:T(8,128)(2,1)} %convert_element_type.422), channel_id=1, replica_groups=mesh['dp'=8,'tensor'=4] {'tensor'}, dimensions={0}, use_global_device_ids=true | all-gather | bytes 983040 | tf_op jit(solution)/shard_map/all_gather | solution.py:234
  662.4 1.7 constant_dynamic-update-slice_fusion.5
  664.1 1.8 convert_reduce_fusion.7
  671.2 2.9 bitcast_convert_fusion.1
  679.5 1.8 bitcast_convert_fusion.2
  683.7 1.7 bitcast_convert_fusion
  685.8 1.8 fusion.44
  688.9 1.8 add_bitcast_fusion
  690.7 2.9 copy.281
  693.7 2.8 reshape.805
  700.1 2.3 add_add_fusion
  706.0 2.3 add_add_fusion.1
  714.3 41.2 %all-reduce.15 = (f32[2,768]{1,0:T(2,128)S(1)}, f32[768]{0:T(1024)S(1)}, f32[768]{0:T(1024)S(1)}, f32[768]{0:T(1024)S(1)}, f32[3072]{0:T(1024)S(1)}, /*index=5*/...) all-reduce(f32[2,768]{1,0:T(2,128)S(1)} %dynamic_update_slice.38, ...), channel_id=21, replica_groups=mesh['dp'=8,'tensor'=4] {'dp','tensor'}, use_global_device_ids=true, to_apply=%region_55.56.clone | all-reduce | flops 9216 | bytes 73728
  763.8 6.3 reduce-scatter.44.cloned.1.call-done
  772.2 40.8 %reduce-scatter.50.cloned.1.call-done = f32[96,576]{1,0:T(8,128)} async-done(((f32[768,576]{1,0:T(8,128)}), f32[96,576]{1,0:T(8,128)}) %reduce-scatter.50.cloned.1.call-update) | async-done | bytes 221200
  814.9 44.6 %reduce-scatter.48.cloned.1.call-done = f32[768,96]{0,1:T(8,128)} async-done(((f32[768,768]{0,1:T(8,128)}), f32[768,96]{0,1:T(8,128)}) %reduce-scatter.48.cloned.1.call-update) | async-done | bytes 294928 | tf_op jit(solution)/shard_map/reduce_scatter | solution.py:316
  859.6 46.2 %reduce-scatter.46.cloned.1.call-done = f32[96,768]{1,0:T(8,128)} async-done(((f32[768,768]{1,0:T(8,128)}), f32[96,768]{1,0:T(8,128)}) %reduce-scatter.46.cloned.1.call-update) | async-done | bytes 294928 | tf_op jit(solution)/shard_map/reduce_scatter | solution.py:315
  (583 shorter events, 106.6 us)
Async XLA Ops:
  8.0 263.7 %reduce-scatter.30.cloned.1.call-start = ((), (), s32[]{:S(2)}) async-start(), calls=%async_computation.22 | async-start | bytes 1966080 | tf_op jit(solution)/shard_map/reduce_scatter | solution.py:166
  32.2 14.1 %copy-start.27 = (bf16[1,512,768]{2,1,0:T(8,128)(2,1)}, bf16[1,512,768]{2,1,0:T(8,128)(2,1)S(1)}, u32[]{:S(2)}) copy-start(bf16[1,512,768]{2,1,0:T(8,128)(2,1)S(1)} %all-gather.4) | copy-start | bytes 2359300
  45.4 117.5 %copy-start.58 = (bf16[3,768,192]{2,0,1:T(4,128)(2,1)}, bf16[3,768,192]{2,0,1:T(4,128)(2,1)S(1)}, u32[]{:S(2)}) copy-start(bf16[3,768,192]{2,0,1:T(4,128)(2,1)S(1)} %all_gather.101) | copy-start | bytes 2654212
  46.3 10.4 %copy-start.154 = (bf16[2,24]{1,0:T(2,128)(2,1)S(1)}, bf16[2,24]{1,0:T(2,128)(2,1)}, u32[]{:S(2)}) copy-start(bf16[2,24]{1,0:T(2,128)(2,1)} %param.19) | copy-start | bytes 292
  46.3 74.3 %copy-start.88 = (bf16[192,96]{1,0:T(8,128)(2,1)S(1)}, bf16[192,96]{1,0:T(8,128)(2,1)}, u32[]{:S(2)}) copy-start(bf16[192,96]{1,0:T(8,128)(2,1)} %param.20) | copy-start | bytes 110596
  120.4 12.1 %copy-start.91 = (f32[3,64]{1,0:T(4,128)}, f32[3,64]{1,0:T(4,128)S(1)}, u32[]{:S(2)}) copy-start(f32[3,64]{1,0:T(4,128)S(1)} %add.410) | copy-start | bytes 2308
  135.6 136.1 %reduce-scatter.26.cloned.1.call-start = ((), (), s32[]{:S(2)}) async-start(), calls=%async_computation.20 | async-start | bytes 1966080 | tf_op jit(solution)/shard_map/reduce_scatter | solution.py:166
  164.9 14.0 %copy-start.55 = (bf16[4,128,3,64]{1,0,3,2:T(4,128)(2,1)}, bf16[4,128,3,64]{1,0,3,2:T(4,128)(2,1)S(1)}, u32[]{:S(2)}) copy-start(bf16[4,128,3,64]{1,0,3,2:T(4,128)(2,1)S(1)} %convert_element_type.368) | copy-start | bytes 589828
  166.3 14.0 %copy-start.65 = (f32[4,128,3,64]{1,0,3,2:T(4,128)}, f32[4,128,3,64]{1,0,3,2:T(4,128)S(1)}, u32[]{:S(2)}) copy-start(f32[4,128,3,64]{1,0,3,2:T(4,128)S(1)} %squeeze.124) | copy-start | bytes 1179652
  166.4 13.7 %copy-start.92 = (f32[3,64]{1,0:T(4,128)S(1)}, f32[3,64]{1,0:T(4,128)}, u32[]{:S(2)}) copy-start(f32[3,64]{1,0:T(4,128)} %copy-done.91) | copy-start | bytes 2308
  166.5 13.8 %copy-start.14 = (f32[4,128,3,64]{1,0,3,2:T(4,128)}, f32[4,128,3,64]{1,0,3,2:T(4,128)S(1)}, u32[]{:S(2)}) copy-start(f32[4,128,3,64]{1,0,3,2:T(4,128)S(1)} %squeeze.126) | copy-start | bytes 1179652
  182.1 89.6 %reduce-scatter.22.cloned.1.call-start = ((), (), s32[]{:S(2)}) async-start(), calls=%async_computation.16 | async-start | bytes 1966080 | tf_op jit(solution)/shard_map/reduce_scatter | solution.py:166
  208.6 14.4 %copy-start.53 = (bf16[4,128,3,64]{1,0,3,2:T(4,128)(2,1)}, bf16[4,128,3,64]{1,0,3,2:T(4,128)(2,1)S(1)}, u32[]{:S(2)}) copy-start(bf16[4,128,3,64]{1,0,3,2:T(4,128)(2,1)S(1)} %convert_element_type.351) | copy-start | bytes 589828
  210.9 12.9 %copy-start.12 = (f32[4,128,3,64]{1,0,3,2:T(4,128)}, f32[4,128,3,64]{1,0,3,2:T(4,128)S(1)}, u32[]{:S(2)}) copy-start(f32[4,128,3,64]{1,0,3,2:T(4,128)S(1)} %squeeze.122) | copy-start | bytes 1179652
  210.9 12.6 %copy-start.63 = (f32[4,128,3,64]{1,0,3,2:T(4,128)S(1)}, f32[4,128,3,64]{1,0,3,2:T(4,128)}, u32[]{:S(2)}) copy-start(f32[4,128,3,64]{1,0,3,2:T(4,128)} %squeeze.120) | copy-start | bytes 1179652
  226.7 67.8 %all-gather.10.cloned.1.call-start = ((), (), s32[]{:S(2)}) async-start(), calls=%async_computation.17 | async-start | bytes 1327104 | tf_op jit(solution)/shard_map/all_gather | solution.py:104
  227.2 74.4 %all-gather.12.cloned.1.call-start = ((), (), s32[]{:S(2)}) async-start(), calls=%async_computation.18 | async-start | bytes 1327104 | tf_op jit(solution)/shard_map/all_gather | solution.py:105
  227.8 149.7 %reduce-scatter.32.cloned.1.call-start = ((), (), s32[]{:S(2)}) async-start(), calls=%async_computation.23 | async-start | bytes 1966080 | tf_op jit(solution)/shard_map/reduce_scatter | solution.py:177
  305.2 86.8 %reduce-scatter.28.cloned.1.call-start = ((), (), s32[]{:S(2)}) async-start(), calls=%async_computation.21 | async-start | bytes 1966080 | tf_op jit(solution)/shard_map/reduce_scatter | solution.py:177
  327.9 6.7 copy-start.6
  327.9 7.6 copy-start.158
  337.5 90.9 %reduce-scatter.24.cloned.1.call-start = ((), (), s32[]{:S(2)}) async-start(), calls=%async_computation.19 | async-start | bytes 1966080 | tf_op jit(solution)/shard_map/reduce_scatter | solution.py:177
  360.2 6.9 copy-start.8
  360.2 7.7 copy-start.159
  369.9 155.2 %reduce-scatter.42.cloned.1.call-start = ((), (), s32[]{:S(2)}) async-start(), calls=%async_computation.28 | async-start | bytes 1966080 | tf_op jit(solution)/shard_map/reduce_scatter | solution.py:221
  432.9 21.5 %copy-start.169 = (f32[512,768]{1,0:T(8,128)S(1)}, f32[512,768]{1,0:T(8,128)}, u32[]{:S(2)}) copy-start(f32[512,768]{1,0:T(8,128)} %get-tuple-element.373) | copy-start | bytes 4718596
  435.0 19.4 %copy-start.160 = (bf16[768,768]{0,1:T(8,128)(2,1)S(1)}, bf16[768,768]{0,1:T(8,128)(2,1)}, u32[]{:S(2)}) copy-start(bf16[768,768]{0,1:T(8,128)(2,1)} %all-gather.12.cloned.1.call-done) | copy-start | bytes 3538948
  435.0 19.4 %copy-start.168 = (f32[512,768]{1,0:T(8,128)S(1)}, f32[512,768]{1,0:T(8,128)}, u32[]{:S(2)}) copy-start(f32[512,768]{1,0:T(8,128)} %get-tuple-element.312) | copy-start | bytes 4718596
  459.0 87.3 %reduce-scatter.34.cloned.1.call-start = ((), (), s32[]{:S(2)}) async-start(), calls=%async_computation.24 | async-start | bytes 1966080 | tf_op jit(solution)/shard_map/reduce_scatter | solution.py:221
  484.1 5.3 copy-start.156
  491.5 91.4 %reduce-scatter.38.cloned.1.call-start = ((), (), s32[]{:S(2)}) async-start(), calls=%async_computation.26 | async-start | bytes 1966080 | tf_op jit(solution)/shard_map/reduce_scatter | solution.py:221
  514.5 5.2 copy-start.157
  521.7 238.5 %reduce-scatter.52.cloned.1.call-start = ((), (), s32[]{:S(2)}) async-start(), calls=%async_computation.33 | async-start | bytes 884736
  586.7 20.9 %copy-start.19 = (f32[128,768]{1,0:T(8,128)}, f32[128,768]{1,0:T(8,128)S(1)}, u32[]{:S(2)}) copy-start(f32[128,768]{1,0:T(8,128)S(1)} %get-tuple-element.288) | copy-start | bytes 1179652
  586.7 19.7 %copy-start.48 = (bf16[4,128,3,64]{1,0,3,2:T(4,128)(2,1)S(1)}, bf16[4,128,3,64]{1,0,3,2:T(4,128)(2,1)}, u32[]{:S(2)}) copy-start(bf16[4,128,3,64]{1,0,3,2:T(4,128)(2,1)} %copy-done.47) | copy-start | bytes 589828
  627.7 5.3 copy-start.93
  638.8 19.0 %copy-start.45 = (bf16[4,128,3,64]{1,0,3,2:T(4,128)(2,1)S(1)}, bf16[4,128,3,64]{1,0,3,2:T(4,128)(2,1)}, u32[]{:S(2)}) copy-start(bf16[4,128,3,64]{1,0,3,2:T(4,128)(2,1)} %copy-done.44) | copy-start | bytes 589828
  659.3 102.5 %reduce-scatter.40.cloned.1.call-start = ((), (), s32[]{:S(2)}) async-start(), calls=%async_computation.27 | async-start | bytes 983040 | tf_op jit(solution)/shard_map/reduce_scatter | solution.py:298
  662.4 6.7 copy-start.64
  674.1 88.7 %reduce-scatter.36.cloned.1.call-start = ((), (), s32[]{:S(2)}) async-start(), calls=%async_computation.25 | async-start | bytes 983040 | tf_op jit(solution)/shard_map/reduce_scatter | solution.py:298
  681.3 88.8 %reduce-scatter.44.cloned.1.call-start = ((), (), s32[]{:S(2)}) async-start(), calls=%async_computation.29 | async-start | bytes 983040 | tf_op jit(solution)/shard_map/reduce_scatter | solution.py:298
  685.5 127.6 %reduce-scatter.50.cloned.1.call-start = ((), (), s32[]{:S(2)}) async-start(), calls=%async_computation.32 | async-start | bytes 2211840
  696.6 163.0 %reduce-scatter.48.cloned.1.call-start = ((), (), s32[]{:S(2)}) async-start(), calls=%async_computation.31 | async-start | bytes 2654208 | tf_op jit(solution)/shard_map/reduce_scatter | solution.py:316
  702.5 203.3 %reduce-scatter.46.cloned.1.call-start = ((), (), s32[]{:S(2)}) async-start(), calls=%async_computation.30 | async-start | bytes 2654208 | tf_op jit(solution)/shard_map/reduce_scatter | solution.py:315
  708.5 4.9 copy-start.121
  708.5 5.0 copy-start.122
  708.5 5.1 copy-start.123
  708.5 5.2 copy-start.119
  708.5 5.3 copy-start.120
  708.6 5.6 copy-start.104
  708.6 5.6 copy-start.110
  708.6 5.6 copy-start.111
  708.6 5.6 copy-start.103
  708.6 5.6 copy-start.108
  708.6 5.6 copy-start.109
  708.6 5.6 copy-start.102
  708.6 5.6 copy-start.106
  708.6 5.6 copy-start.107
  708.7 5.6 copy-start.105
  708.7 5.6 copy-start.112
  708.7 5.6 copy-start.113
  708.7 53.2 %copy-start.24 = (f32[128,768]{1,0:T(8,128)S(1)}, f32[128,768]{1,0:T(8,128)}, u32[]{:S(2)}) copy-start(f32[128,768]{1,0:T(8,128)} %copy-done.23) | copy-start | bytes 1179652
  709.3 53.5 %copy-start.20 = (f32[128,768]{1,0:T(8,128)S(1)}, f32[128,768]{1,0:T(8,128)}, u32[]{:S(2)}) copy-start(f32[128,768]{1,0:T(8,128)} %copy-done.19) | copy-start | bytes 1179652
  711.5 58.7 %copy-start.22 = (f32[128,768]{1,0:T(8,128)S(1)}, f32[128,768]{1,0:T(8,128)}, u32[]{:S(2)}) copy-start(f32[128,768]{1,0:T(8,128)} %get-tuple-element.356) | copy-start | bytes 1179652
  (124 other events, 291.1 us)
Sparse Core Ops, SparseCore 0:
  135.7 43.5 reduce-scatter.29
  182.2 40.4 reduce-scatter.25
  226.8 33.9 reduce-scatter.21
  305.3 49.1 reduce-scatter.31
  356.7 35.2 reduce-scatter.27
  394.1 34.2 reduce-scatter.23
  459.1 49.3 reduce-scatter.41
  510.8 35.4 reduce-scatter.33
  548.6 34.2 reduce-scatter.37
Sparse Core Ops, SparseCore 1:
  229.0 21.3 all-gather.9
  252.1 24.0 all-gather.11
  659.4 35.0 reduce-scatter.51
  696.8 23.0 reduce-scatter.39
  722.2 23.4 reduce-scatter.35
  748.0 22.1 reduce-scatter.43
  773.4 39.6 reduce-scatter.49
  817.2 42.3 reduce-scatter.47
  863.4 42.3 reduce-scatter.45
where the time goes:
time: 923 us; the launch traced here: 914 us
  blocking collectives  454 us (49%)
  waiting for transfers between devices  242 us (26%)
  matrix products  103 us (11%)
  local copies, waits for them, and re-layouts  58.1 us (6%)
  other arithmetic  37.3 us (4%)
  between operations  18.5 us (2%)
    unnamed x2, blocking collectives  81 us
    all_gather x3, blocking collectives, per_device(): lax.all_gather(x_rows, 'tensor', axis=0, tiled=True)  71.3 us
    all_gather x3, blocking collectives, per_device(): lax.all_gather(grad_pre_two.astype(jnp.bfloat16), 'tensor', axis=0, tiled...  66.2 us
    all_gather x3, blocking collectives, per_device(): lax.all_gather(out_one.astype(jnp.bfloat16), 'tensor', axis=0, tiled=True)  63.9 us
    all_gather x1, blocking collectives, per_device(): lax.all_gather(qv_bias, ('dp', 'tensor'), axis=1, tiled=True)  63.2 us
    all_gather x3, blocking collectives, per_device(): lax.all_gather(grad_pre_one.astype(jnp.bfloat16), 'tensor', axis=0, tiled...  53.5 us
    reduce_scatter x3, waiting for transfers between devices, per_device(): lax.psum_scatter(jnp.einsum('rf,df->rd', up_grad, up_back, preferred_elem...  51.4 us
    reduce_scatter x3, waiting for transfers between devices, per_device(): lax.psum_scatter(jnp.dot(hidden_act, down_now, preferred_element_type=jnp...  50.9 us
  transfers between devices with their start and end apart: 18, of which 8 were waited for; matrix products, arithmetic and copies ran while one was open for 15% of the time, Pallas kernels for 0%

commit v1 on v0

v1 whole, which is shorter than its diff:
```python
from functools import partial

import jax
import jax.numpy as jnp
from jax import lax
from jax.sharding import PartitionSpec as P

HD = 64
EPS = 1e-12
NEG = -1000000000.0
AXES = ("dp", "tensor")
f32 = jnp.float32
bf16 = jnp.bfloat16


def mm(spec, a, b):
    return jnp.einsum(spec, a, b, preferred_element_type=f32)


def normalize(values, gain, shift):
    center = values - jnp.mean(values, axis=-1, keepdims=True)
    inverse = lax.rsqrt(jnp.mean(center * center, axis=-1, keepdims=True) + EPS)
    normed = center * inverse
    return normed * gain + shift, normed, inverse


def normalize_back(grad_out, normed, inverse, gain):
    scaled = grad_out * gain
    return inverse * (
        scaled
        - jnp.mean(scaled, axis=-1, keepdims=True)
        - normed * jnp.mean(scaled * normed, axis=-1, keepdims=True)
    )


def per_device(
    hidden_in, segment_ids, pooled_grad, qkv_weight, qv_bias, out_weight, out_bias,
    norm1_gain, norm1_shift, up_weight, up_bias, down_weight, down_bias, norm2_gain, norm2_shift,
):
    n_dp, n_t = lax.axis_size("dp"), lax.axis_size("tensor")
    rows = qkv_weight.shape[1]
    hc = qkv_weight.shape[2]
    fc = up_weight.shape[1]
    D = rows * n_dp
    micro, tokens = hidden_in.shape[0], hidden_in.shape[1]
    seqs, L = segment_ids.shape[1], segment_ids.shape[2]
    G = micro * seqs
    T = micro * tokens
    segs = pooled_grad.shape[2]
    H = D // HD
    cols = 4 * hc + 2 * fc

    vecs = [qv_bias[0], qv_bias[1], out_bias, norm1_gain, norm1_shift, up_bias, down_bias, norm2_gain, norm2_shift]
    vlen = [v.shape[0] for v in vecs]
    vec = jnp.concatenate(vecs)
    main = jnp.concatenate(
        [qkv_weight[0], qkv_weight[1], qkv_weight[2], out_weight.T, up_weight, down_weight.T], axis=1
    )
    full = lax.all_gather(main, "dp", axis=0, tiled=True)
    full = lax.all_gather(full, "tensor", axis=0)
    vfull = lax.all_gather(lax.all_gather(vec, "tensor"), "dp").reshape(n_dp * n_t, -1).astype(f32)

    def take(lo, width):
        return full[:, :, lo : lo + width].transpose(1, 0, 2).reshape(D, n_t * width)

    wq, wk, wv, wot = (take(c * hc, hc) for c in range(4))
    wu, wdt = take(4 * hc, fc), take(4 * hc + fc, fc)
    offs = [0]
    for n in vlen:
        offs.append(offs[-1] + n)
    bq, bv, bo, g1, s1, bu, bd, g2, s2 = (vfull[:, offs[j] : offs[j + 1]].reshape(-1) for j in range(9))

    x = hidden_in.reshape(T, D)
    seg = segment_ids.reshape(G, L)
    heads = (G, L, H, HD)
    q = (mm("rd,de->re", x, wq) + bq).astype(bf16).reshape(heads)
    k = mm("rd,de->re", x, wk).astype(bf16).reshape(heads)
    v = (mm("rd,de->re", x, wv) + bv).astype(bf16).reshape(heads)
    scale = float(HD) ** -0.5
    same = seg[:, None, :, None] == seg[:, None, None, :]
    s = jnp.where(same, mm("gqhd,gkhd->ghqk", q, k) * scale, NEG)
    e = jnp.exp(s - jnp.max(s, axis=-1, keepdims=True))
    pf = e / jnp.sum(e, axis=-1, keepdims=True)
    pb = pf.astype(bf16)
    o = mm("ghqk,gkhd->gqhd", pb, v).astype(bf16).reshape(T, D)
    a = mm("re,de->rd", o, wot) + bo + x.astype(f32)
    n1, x1, r1 = normalize(a, g1, s1)
    n1b = n1.astype(bf16)
    u = mm("rd,df->rf", n1b, wu) + bu
    z, pull = jax.vjp(partial(jax.nn.gelu, approximate=False), u)
    z = z.astype(bf16)
    b = mm("rf,df->rd", z, wdt) + bd + n1
    y, x2, r2 = normalize(b, g2, s2)
    onehot = (seg[:, :, None] == jnp.arange(segs, dtype=jnp.int32)).astype(f32)
    counts = jnp.sum(onehot, axis=1)
    hi = lax.Precision.HIGHEST
    pooled = jnp.einsum("gls,gld->gsd", onehot, y.reshape(G, L, D), precision=hi) / counts[:, :, None]
    dy = jnp.einsum("gls,gsd->gld", onehot, pooled_grad.reshape(G, segs, D) / counts[:, :, None], precision=hi).reshape(T, D)
    db = normalize_back(dy, x2, r2, g2)
    g_g2, g_s2, g_bd = jnp.sum(dy * x2, 0), jnp.sum(dy, 0), jnp.sum(db, 0)
    dbb = db.astype(bf16)
    g_wdt = mm("rd,rf->df", dbb, z)
    du = pull(mm("rd,df->rf", dbb, wdt))[0].astype(bf16)
    g_wu = mm("rd,rf->df", n1b, du)
    g_bu = jnp.sum(du.astype(f32), 0)
    dn1 = mm("rf,df->rd", du, wu).astype(bf16).astype(f32) + db
    da = normalize_back(dn1, x1, r1, g1)
    g_g1, g_s1, g_bo = jnp.sum(dn1 * x1, 0), jnp.sum(dn1, 0), jnp.sum(da, 0)
    dab = da.astype(bf16)
    g_wot = mm("rd,re->de", dab, o)
    do = mm("rd,de->re", dab, wot).astype(bf16).reshape(heads)
    dp = mm("gqhd,gkhd->ghqk", do, v)
    ds = (pf * (dp - jnp.sum(pf * dp, axis=-1, keepdims=True))).astype(bf16)
    dv = mm("ghqk,gqhd->gkhd", pb, do).astype(bf16).reshape(T, D)
    dq = (mm("ghqk,gkhd->gqhd", ds, k) * scale).astype(bf16).reshape(T, D)
    dk = (mm("ghqk,gqhd->gkhd", ds, q) * scale).astype(bf16).reshape(T, D)
    g_q, g_k, g_v = (mm("rd,re->de", x, dd) for dd in (dq, dk, dv))
    g_bq, g_bv = jnp.sum(dq.astype(f32), 0), jnp.sum(dv.astype(f32), 0)
    dx = mm("re,de->rd", dq, wq) + mm("re,de->rd", dk, wk) + mm("re,de->rd", dv, wv) + da

    def blocks(g):
        return g.astype(bf16).reshape(D, n_t, -1).transpose(1, 0, 2)

    gfull = jnp.concatenate([blocks(g) for g in (g_q, g_k, g_v, g_wot, g_wu, g_wdt)], axis=2)
    gvec = jnp.concatenate(
        [g.reshape(n_dp * n_t, -1) for g in (g_bq, g_bv, g_bo, g_g1, g_s1, g_bu, g_bd, g_g2, g_s2)], axis=1
    )
    gmine = lax.psum_scatter(gfull, "tensor", scatter_dimension=0)
    gmine = lax.psum_scatter(gmine, "dp", scatter_dimension=0, tiled=True).astype(f32)
    gv = lax.psum_scatter(gvec, AXES, scatter_dimension=0)
    vo = [gv[offs[j] : offs[j + 1]] for j in range(9)]
    return (
        pooled.reshape(micro, seqs, segs, D),
        dx.reshape(micro, tokens, D),
        jnp.stack([gmine[:, c * hc : (c + 1) * hc] for c in range(3)]),
        jnp.stack([vo[0], vo[1]]),
        gmine[:, 3 * hc : 4 * hc].T,
        vo[2], vo[3], vo[4],
        gmine[:, 4 * hc : 4 * hc + fc],
        vo[5],
        gmine[:, 4 * hc + fc :].T,
        vo[6], vo[7], vo[8],
    )


def solution(mesh):
    both = P(AXES)
    row3 = P(None, AXES)
    return jax.shard_map(
        per_device,
        mesh=mesh,
        in_specs=(
            row3, row3, row3, P(None, "dp", "tensor"), row3, P("tensor", "dp"), both, both, both,
            P("dp", "tensor"), both, P("tensor", "dp"), both, both, both,
        ),
        out_specs=(
            row3, row3, P(None, "dp", "tensor"), row3, P("tensor", "dp"), both, both, both,
            P("dp", "tensor"), both, P("tensor", "dp"), both, both, both,
        ),
        check_vma=False,
    )
```

time: 923 us -> 772 us (0.84)
  blocking collectives: 454 us -> 62.4 us
  waiting for transfers between devices: 242 us -> 489 us
  local copies, waits for them, and re-layouts: 58.1 us -> 105 us
  other arithmetic: 37.3 us -> 9.89 us
  matrix products: 103 us -> 79.4 us
    all_gather x18 -> x1, blocking collectives: 373 us -> 8.97 us  [per_device(): lax.all_gather(lax.all_gather(vec, 'tensor'), 'dp').reshape(n_dp * n_t, -1)]
    all_gather x2, waiting for transfers between devices: 0.01 us -> 253 us  [the longest x1 216 us: per_device(): full = lax.all_gather(full, 'tensor', axis=0)]
    transpose x0 -> x11, local copies, waits for them, and re-layouts: none -> 46.7 us  [the longest x8 37.8 us: take(): return full[:, :, lo:lo + width].transpose(1, 0, 2).reshape(D, n_t * width)]
    unnamed x20 -> x4, waiting for transfers between devices: 42.1 us -> 0.07 us
    reduce_scatter x14 -> x2, waiting for transfers between devices: 199 us -> 237 us  [the longest x1 236 us: per_device(): gmine = lax.psum_scatter(gfull, 'tensor', scatter_dimension=0)]
    unnamed x376 -> x135, local copies, waits for them, and re-layouts: 39 us -> 5.07 us
    unnamed x2, blocking collectives: 81 us -> 53.4 us
    dot_general x60 -> x25, matrix products: 103 us -> 77 us  [the longest x23 74.5 us: mm(): return jnp.einsum(spec, a, b, preferred_element_type=f32)]
  transfers between devices with their start and end apart: 18 -> 4, of which waited for: 8 -> 4; matrix products, arithmetic and copies ran while one was open for 15% -> 2% of each run, Pallas kernels for 0% -> 0%
where the time goes in v1:
time: 772 us; the launch traced here: 762 us
  waiting for transfers between devices  489 us (63%)
  local copies, waits for them, and re-layouts  105 us (14%)
  matrix products  79.4 us (10%)
  blocking collectives  62.4 us (8%)
  between operations  15.6 us (2%)
  other arithmetic  9.89 us (1%)
    reduce_scatter x1, waiting for transfers between devices, per_device(): gmine = lax.psum_scatter(gfull, 'tensor', scatter_dimension=0)  236 us
    all_gather x1, waiting for transfers between devices, per_device(): full = lax.all_gather(full, 'tensor', axis=0)  216 us
    dot_general x23, matrix products, mm(): return jnp.einsum(spec, a, b, preferred_element_type=f32)  74.5 us
    unnamed x2, blocking collectives  53.4 us
    transpose x8, local copies, waits for them, and re-layouts, take(): return full[:, :, lo:lo + width].transpose(1, 0, 2).reshape(D, n_t * width)  37.8 us
    all_gather x1, waiting for transfers between devices, per_device(): full = lax.all_gather(main, 'dp', axis=0, tiled=True)  36.8 us
    concatenate x1, local copies, waits for them, and re-layouts, per_device(): jnp.concatenate([blocks(g) for g in (g_q, g_k, g_v, g_wot, g_wu, g_wdt)],...  21.7 us
  transfers between devices with their start and end apart: 4, of which 4 were waited for; matrix products, arithmetic and copies ran while one was open for 2% of the time, Pallas kernels for 0%

profile of v1, /device:TPU:0, one launch (start us, length us, event | category | flops | bytes accessed | tf_op | source)
XLA Modules:
  0.0 762.0 jit_solution(15456504163924318695)
XLA Ops:
  7.2 0.9 copy.108
  8.1 0.9 slice_bitcast_fusion.11
  9.0 1.9 concatenate.12
  10.9 36.8 %all-gather.7.cloned.1.call-done = bf16[768,2304]{1,0:T(8,128)(2,1)} async-done(((bf16[96,2304]{1,0:T(8,128)(2,1)}), bf16[768,2304]{1,0:T(8,128)(2,1)}) %all-gather.7.cloned.1.call-update) | async-done | bytes 3538960 | tf_op jit(solution)/shard_map/all_gather | solution.py:59
  50.1 11.7 %all-reduce = bf16[1152]{0:T(1024)(128)(2,1)S(1)} all-reduce(bf16[1152]{0:T(1024)(128)(2,1)S(1)} %dynamic-update-slice), channel_id=3, replica_groups=mesh['dp'=8,'tensor'=4] {'tensor'}, use_global_device_ids=true, to_apply=%add | all-reduce | flops 1152 | bytes 4608
  61.8 9.0 %all-gather.3 = bf16[8,4,288]{2,1,0:T(4,128)(2,1)S(1)} all-gather(bf16[1,4,288]{2,1,0:T(4,128)(2,1)S(1)} %reshape.268), channel_id=4, replica_groups=mesh['dp'=8,'tensor'=4] {'dp'}, dimensions={0}, use_global_device_ids=true | all-gather | bytes 20736 | tf_op jit(solution)/shard_map/all_gather | solution.py:61
  74.8 1.3 fusion.84
  76.7 0.7 broadcast_compare_fusion
  77.4 215.8 %all-gather.9.cloned.1.call-done = bf16[3072,2304]{1,0:T(8,128)(2,1)} async-done(((bf16[768,2304]{1,0:T(8,128)(2,1)}), bf16[3072,2304]{1,0:T(8,128)(2,1)}) %all-gather.9.cloned.1.call-update) | async-done | bytes 14155792 | tf_op jit(solution)/shard_map/all_gather | solution.py:60
  293.2 7.3 slice_bitcast_fusion.4
  300.5 7.9 %slice_bitcast_fusion = (bf16[768,4,768]{2,0,1:T(8,128)(2,1)}, bf16[768,4,768]{2,0,1:T(8,128)(2,1)}) fusion(bf16[4,768,2304]{2,1,0:T(8,128)(2,1)} %bitcast.194), kind=kLoop, calls=%fused_computation.7 | loop fusion | bytes 18874368 | tf_op jit(solution)/shard_map/transpose | solution.py:64
  308.4 6.6 copy.119
  315.1 2.6 copy.110
  317.7 2.9 fusion.22
  320.6 2.0 reshape.228
  322.6 2.8 copy.117
  325.3 2.5 copy.111
  327.8 3.0 fusion.17
  330.9 2.6 reshape.230
  333.5 1.5 copy.109
  334.9 2.3 fusion.23
  337.3 1.0 reshape.226
  338.3 2.4 fusion.89
  340.7 2.5 fusion.18
  343.7 0.8 fusion.94
  344.8 0.7 add_rsqrt_fusion.1
  345.6 6.7 copy.118
  352.3 14.2 %multiply_convert_fusion = (bf16[384,3072]{1,0:T(8,128)(2,1)S(1)}, f32[384,3072]{1,0:T(8,128)S(1)}, f32[384,3072]{1,0:T(8,128)S(1)}) fusion(f32[3072]{0:T(1024)} %add.126, bf16[768,3072]{0,1:T(8,128)(2,1)} %bitcast.201, f32[384,768]{1,0:T(8,128)S(1)} %get-tuple-element.119, f32[768]{0:T(1024)} %add.123, f32[768]{0:T(1024)S(1)} %mul.154, ...), kind=kOutput, calls=%fused_computation.11 | convolution fusion | flops 1891270656 | bytes 17716224 | tf_op jit(solution)/shard_map/rd,df->rf/dot_general | solution.py:17
  366.5 5.3 fusion.95
  372.1 1.0 fusion.24
  373.1 2.1 fusion.85
  375.2 7.6 %convert_reduce_fusion = (f32[3072]{0:T(1024)}, bf16[384,3072]{1,0:T(8,128)(2,1)S(1)}) fusion(f32[384,3072]{1,0:T(8,128)S(1)} %get-tuple-element.83, f32[384,3072]{1,0:T(8,128)S(1)} %get-tuple-element.120, bf16[768,3072]{0,1:T(8,128)(2,1)} %bitcast.200, f32[384,768]{1,0:T(8,128)S(1)} %get-tuple-element.79), kind=kOutput, calls=%fused_computation.9 | convolution fusion | flops 1831105536 | bytes 17707008 | tf_op jit(solution)/shard_map/rd,df->rf/dot_general | solution.py:17
  382.9 2.9 multiply_reduce_fusion.1
  385.8 1.0 fusion.86
  386.8 1.5 convolution_convert_fusion.7
  388.3 1.8 convolution_convert_fusion.2
  390.1 1.0 reshape.274
  391.1 1.3 copy.121
  392.4 4.2 convert_reduce_fusion.1
  398.4 1.8 fusion.20
  400.1 1.3 convert_reduce_fusion.2
  401.5 4.8 convolution_convert_fusion.1
  406.2 4.4 convolution_convert_fusion
  410.6 1.9 copy.135
  412.5 1.7 copy.131
  414.2 1.4 copy.128
  415.6 1.4 copy.125
  417.1 1.9 convolution_convert_fusion.3
  418.9 2.6 copy.134
  421.5 3.1 convolution_convert_fusion.4
  424.6 2.5 copy.133
  427.1 3.1 convolution_convert_fusion.5
  430.3 2.5 copy.132
  432.8 8.0 %bitcast_bitcast_fusion = (bf16[4,768,768]{2,1,0:T(8,128)(2,1)}, bf16[4,768,768]{2,1,0:T(8,128)(2,1)}) fusion(bf16[96,4,8,768]{3,2,1,0:T(8,128)(2,1)} %bitcast.207, bf16[96,4,8,768]{3,2,1,0:T(8,128)(2,1)} %bitcast.206), kind=kLoop, calls=%fused_computation.5 | loop fusion | bytes 18874368 | tf_op jit(solution)/shard_map/transpose | solution.py:122
  440.8 21.7 %concatenate.14 = bf16[4,768,2304]{2,1,0:T(8,128)(2,1)} concatenate(bf16[4,768,192]{2,1,0:T(8,128)(2,1)} %bitcast.198, bf16[4,768,192]{2,1,0:T(8,128)(2,1)} %bitcast.197, bf16[4,768,192]{2,1,0:T(8,128)(2,1)} %bitcast.196, bf16[4,768,192]{2,1,0:T(8,128)(2,1)S(1)} %bitcast.195, bf16[4,768,768]{2,1,0:T(8,128)(2,1)} %get-tuple-element.136, bf16[4,768,768]{2,1,0:T(8,128)(2,1)} %get-tuple-element.135), dimensions={2} | concatenate | bytes 28311552 | tf_op jit(solution)/shard_map/concatenate | solution.py:124
  462.6 235.5 %reduce-scatter.3.cloned.1.call-done = bf16[1,768,2304]{2,1,0:T(8,128)(2,1)} async-done(((bf16[4,768,2304]{2,1,0:T(8,128)(2,1)}), bf16[1,768,2304]{2,1,0:T(8,128)(2,1)}) %reduce-scatter.3.cloned.1.call-update) | async-done | bytes 3538960 | tf_op jit(solution)/shard_map/reduce_scatter | solution.py:128
  699.8 41.8 %all-reduce.1 = f32[32,288]{1,0:T(8,128)S(1)} all-reduce(f32[32,288]{1,0:T(8,128)S(1)} %concatenate.15), channel_id=7, replica_groups=mesh['dp'=8,'tensor'=4] {'dp','tensor'}, use_global_device_ids=true, to_apply=%region_23.24.clone | all-reduce | flops 9216 | bytes 73728
  743.3 1.1 fusion.28
  744.5 2.3 fusion.35
  748.1 1.7 fusion.8
  749.8 1.0 reduce-scatter.5.cloned.1.call-done
  750.8 1.1 convert_element_type.162
  752.8 0.7 copy.139
  754.3 0.7 slice.189
  (185 shorter events, 15.5 us)
Async XLA Ops:
  7.2 40.5 %all-gather.7.cloned.1.call-start = ((), (), s32[]{:S(2)}) async-start(), calls=%async_computation.2 | async-start | bytes 3981312 | tf_op jit(solution)/shard_map/all_gather | solution.py:59
  10.9 282.3 %all-gather.9.cloned.1.call-start = ((), (), s32[]{:S(2)}) async-start(), calls=%async_computation.5 | async-start | bytes 17694720 | tf_op jit(solution)/shard_map/all_gather | solution.py:60
  47.7 1.9 copy-start.45
  47.7 1.9 copy-start.47
  47.7 1.9 copy-start.48
  47.7 2.0 copy-start.49
  47.7 1.9 copy-start.50
  47.7 1.9 copy-start.51
  47.8 1.9 copy-start.52
  47.8 1.9 copy-start.53
  47.8 27.0 %copy-start.21 = (f32[3,1,8,768]{3,2,1,0:T(8,128)S(1)}, f32[3,1,8,768]{3,2,1,0:T(8,128)}, u32[]{:S(2)}) copy-start(f32[3,1,8,768]{3,2,1,0:T(8,128)} %param.17) | copy-start | bytes 221188
  47.8 650.3 %reduce-scatter.3.cloned.1.call-start = ((), (), s32[]{:S(2)}) async-start(), calls=%async_computation.3 | async-start | bytes 17694720 | tf_op jit(solution)/shard_map/reduce_scatter | solution.py:128
  71.8 294.6 %copy-start.29 = (f32[768]{0:T(1024)}, f32[768]{0:T(1024)S(1)}, u32[]{:S(2)}) copy-start(f32[768]{0:T(1024)S(1)} %mul.154) | copy-start | bytes 9220
  74.8 218.4 %copy-start.25 = (f32[3,8]{1,0:T(4,128)}, f32[3,8]{1,0:T(4,128)S(1)}, u32[]{:S(2)}) copy-start(f32[3,8]{1,0:T(4,128)S(1)} %convert_reduce_fusion.3) | copy-start | bytes 292
  315.1 2.6 copy-start.54
  322.6 15.7 %copy-start.7 = (bf16[3,128,12,64]{1,0,3,2:T(4,128)(2,1)}, bf16[3,128,12,64]{1,0,3,2:T(4,128)(2,1)S(1)}, u32[]{:S(2)}) copy-start(bf16[3,128,12,64]{1,0,3,2:T(4,128)(2,1)S(1)} %reshape.228) | copy-start | bytes 1769476
  334.9 3.3 copy-start.9
  334.9 3.3 copy-start.22
  340.7 2.5 copy-start.23
  340.7 3.0 copy-start.5
  340.7 3.0 copy-start.55
  343.7 0.9 copy-start.11
  344.6 41.2 %copy-start = (f32[384,768]{1,0:T(8,128)}, f32[384,768]{1,0:T(8,128)S(1)}, u32[]{:S(2)}) copy-start(f32[384,768]{1,0:T(8,128)S(1)} %get-tuple-element.119) | copy-start | bytes 3538948
  352.3 14.2 %copy-start.36 = (f32[384]{0:T(512)S(1)}, f32[384]{0:T(512)}, u32[]{:S(2)}) copy-start(f32[384]{0:T(512)} %add_rsqrt_fusion.1) | copy-start | bytes 4612
  352.3 14.2 %copy-start.40 = (f32[768]{0:T(1024)S(1)}, f32[768]{0:T(1024)}, u32[]{:S(2)}) copy-start(f32[768]{0:T(1024)} %add.123) | copy-start | bytes 9220
  352.3 14.2 %copy-start.44 = (f32[768]{0:T(1024)S(1)}, f32[768]{0:T(1024)}, u32[]{:S(2)}) copy-start(f32[768]{0:T(1024)} %add.129) | copy-start | bytes 9220
  366.5 5.3 copy-start.58
  371.8 1.3 copy-start.34
  371.8 1.3 copy-start.38
  373.1 9.7 %slice-start = ((s8[4718592]{0:T(1024)(128)(4,1)}), s8[4194304]{0:T(1024)(128)(4,1)S(1)}, s32[]{:S(2)}) async-start(s8[4718592]{0:T(1024)(128)(4,1)} %bitcast.202), calls=%async_computation.6 | async-start | bytes 8388608
  375.2 7.6 %copy-start.18 = (f32[384,768]{1,0:T(8,128)}, f32[384,768]{1,0:T(8,128)S(1)}, u32[]{:S(2)}) copy-start(f32[384,768]{1,0:T(8,128)S(1)} %get-tuple-element.79) | copy-start | bytes 3538948
  375.2 7.6 %slice-start.1 = ((s8[4718592]{0:T(1024)(128)(4,1)}), s8[524288]{0:T(1024)(128)(4,1)S(1)}, s32[]{:S(2)}) async-start(s8[4718592]{0:T(1024)(128)(4,1)} %bitcast.202), calls=%async_computation.7 | async-start | bytes 1048576
  375.2 7.6 %copy-start.30 = (f32[768]{0:T(1024)S(1)}, f32[768]{0:T(1024)}, u32[]{:S(2)}) copy-start(f32[768]{0:T(1024)} %copy-done.29) | copy-start | bytes 9220
  382.9 2.9 copy-start.60
  386.8 1.5 copy-start.12
  388.3 1.8 copy-start.16
  391.1 1.3 copy-start.24
  392.4 4.2 copy-start.13
  392.4 4.2 copy-start.20
  397.2 1.1 copy-start.8
  398.4 1.8 copy-start.10
  398.4 3.1 copy-start.61
  400.1 1.3 copy-start.1
  400.1 1.3 copy-start.31
  400.1 1.3 copy-start.37
  400.1 1.3 copy-start.41
  401.4 4.8 copy-start.19
  401.4 4.8 copy-start.59
  412.5 1.7 copy-start.14
  412.5 3.1 copy-start.15
  414.2 2.8 copy-start.56
  462.6 288.3 %reduce-scatter.5.cloned.1.call-start = ((), (), s32[]{:S(2)}) async-start(), calls=%async_computation.4 | async-start | bytes 3981312 | tf_op jit(solution)/shard_map/reduce_scatter | solution.py:129
  698.2 0.9 copy-start.32
  698.2 0.9 copy-start.33
  698.2 1.0 copy-start.43
  698.2 1.1 copy-start.28
  698.2 1.2 copy-start.42
  698.2 1.3 copy-start.39
  698.2 45.1 %copy-start.2 = (f32[384,768]{1,0:T(8,128)S(1)}, f32[384,768]{1,0:T(8,128)}, u32[]{:S(2)}) copy-start(f32[384,768]{1,0:T(8,128)} %get-tuple-element.90) | copy-start | bytes 3538948
  698.2 45.1 %copy-start.26 = (f32[3,8]{1,0:T(4,128)S(1)}, f32[3,8]{1,0:T(4,128)}, u32[]{:S(2)}) copy-start(f32[3,8]{1,0:T(4,128)} %copy-done.25) | copy-start | bytes 292
  744.5 2.3 copy-start.3
  744.5 2.3 copy-start.6
  746.8 1.3 copy-start.4
  750.8 3.5 copy-start.17
  (4 other events, 2.8 us)
Sparse Core Ops, SparseCore 0:
  11.0 36.6 all-gather.6
  49.3 243.9 all-gather.8
  462.7 235.4 reduce-scatter.2
  701.5 49.2 reduce-scatter.4

commit v2 on v1

v2 whole, which is shorter than its diff:
```python
from functools import partial

import jax
import jax.numpy as jnp
from jax import lax
from jax.experimental import pallas as pl
from jax.experimental.pallas import tpu as pltpu
from jax.sharding import PartitionSpec as P

HD = 64
EPS = 1e-12
NEG = -1000000000.0
SCALE = float(HD) ** -0.5
AXES = ("dp", "tensor")
f32 = jnp.float32
bf16 = jnp.bfloat16
HI = lax.Precision.HIGHEST
BLK = 96
VMEM_LIMIT = 40 * 1024 * 1024


def nn(a, b):
    return lax.dot_general(a, b, (((1,), (0,)), ((), ())), preferred_element_type=f32)


def nt(a, b):
    return lax.dot_general(a, b, (((1,), (1,)), ((), ())), preferred_element_type=f32)


def tn(a, b):
    return lax.dot_general(a, b, (((0,), (0,)), ((), ())), preferred_element_type=f32)


def mean_last(v):
    return jnp.sum(v, axis=-1, keepdims=True) * (1.0 / v.shape[-1])


def normalize(values):
    center = values - mean_last(values)
    inverse = lax.rsqrt(mean_last(center * center) + EPS)
    return center * inverse, inverse


def normalize_back(scaled, normed, inverse):
    return inverse * (scaled - mean_last(scaled) - normed * mean_last(scaled * normed))


def col_sum(v):
    return jnp.sum(v, axis=0, keepdims=True)


def attention_forward(x_ref, w_ref, bq_ref, bv_ref, segc_ref, segr_ref, vec_ref,
                      qkv_ref, p_ref, o_ref, n1_ref, x1_ref, r1_ref, n1b_ref, acc_ref):
    step = pl.program_id(0)
    hc = bq_ref.shape[-1]
    rows, length = segr_ref.shape
    x = x_ref[...]
    w = w_ref[...].reshape(x.shape[1], w_ref.shape[-1])
    qkv = nn(x, w[:, : 3 * hc])
    q = (qkv[:, :hc] + bq_ref[0]).astype(bf16)
    k = qkv[:, hc : 2 * hc].astype(bf16)
    v = (qkv[:, 2 * hc :] + bv_ref[0]).astype(bf16)
    qkv_ref[0, :, :hc] = q
    qkv_ref[0, :, hc : 2 * hc] = k
    qkv_ref[0, :, 2 * hc :] = v
    parts = []
    for g in range(rows):
        span = slice(g * length, (g + 1) * length)
        same = segc_ref[span, :] == segr_ref[g : g + 1, :]
        heads = []
        for h in range(hc // HD):
            cut = slice(h * HD, (h + 1) * HD)
            s = jnp.where(same, nt(q[span, cut], k[span, cut]) * SCALE, NEG)
            e = jnp.exp(s - jnp.max(s, axis=-1, keepdims=True))
            p = e / jnp.sum(e, axis=-1, keepdims=True)
            p_ref[0, g * (hc // HD) + h] = p
            heads.append(nn(p.astype(bf16), v[span, cut]).astype(bf16))
        parts.append(jnp.concatenate(heads, axis=1))
    o = jnp.concatenate(parts, axis=0)
    o_ref[0] = o
    add = nt(o, w[:, 3 * hc :])

    @pl.when(step == 0)
    def _():
        acc_ref[...] = add

    @pl.when(step > 0)
    def _():
        acc_ref[...] += add

    @pl.when(step == pl.num_programs(0) - 1)
    def _():
        a = acc_ref[...] + vec_ref[0:1, :] + x_ref[...].astype(f32)
        normed, inverse = normalize(a)
        n1 = normed * vec_ref[1:2, :] + vec_ref[2:3, :]
        n1_ref[...] = n1
        x1_ref[...] = normed
        r1_ref[...] = inverse
        n1b_ref[...] = n1.astype(bf16)


def erf(v):
    return lax.erf(v)


def up_forward(n_ref, w_ref, b_ref, z_ref, d_ref):
    w = w_ref[...].reshape(n_ref.shape[1], w_ref.shape[-1])
    u = nn(n_ref[...], w) + b_ref[0]
    phi = 0.5 + 0.5 * erf(u * (0.5**0.5))
    z_ref[0] = (u * phi).astype(bf16)
    d_ref[0] = phi + u * (jnp.exp(-0.5 * u * u) * 0.3989422804014327)


def down_forward(z_ref, w_ref, n1_ref, vec_ref, segc_ref, segr_ref, pg_ref,
                 pooled_ref, db_ref, dbb_ref, sums_ref, acc_ref):
    step = pl.program_id(0)
    width = n1_ref.shape[1]
    w = w_ref[...].reshape(width, w_ref.shape[-1])
    add = nt(z_ref[0], w)

    @pl.when(step == 0)
    def _():
        acc_ref[...] = add

    @pl.when(step > 0)
    def _():
        acc_ref[...] += add

    @pl.when(step == pl.num_programs(0) - 1)
    def _():
        rows, length = segr_ref.shape
        segs = pg_ref.shape[1]
        b = acc_ref[...] + vec_ref[3:4, :] + n1_ref[...]
        x2, r2 = normalize(b)
        y = x2 * vec_ref[4:5, :] + vec_ref[5:6, :]
        grads = []
        for g in range(rows):
            span = slice(g * length, (g + 1) * length)
            ids = lax.broadcasted_iota(jnp.int32, (segs, length), 0)
            hot_t = (ids == segr_ref[g : g + 1, :]).astype(f32)
            idc = lax.broadcasted_iota(jnp.int32, (length, segs), 1)
            hot = (idc == segc_ref[span, :]).astype(f32)
            count = jnp.sum(hot_t, axis=1, keepdims=True)
            sums = lax.dot_general(hot_t, y[span, :], (((1,), (0,)), ((), ())),
                                   precision=HI, preferred_element_type=f32)
            pooled_ref[g] = sums / count
            grads.append(lax.dot_general(hot, pg_ref[g] / count, (((1,), (0,)), ((), ())),
                                         precision=HI, preferred_element_type=f32))
        dy = jnp.concatenate(grads, axis=0)
        db = normalize_back(dy * vec_ref[4:5, :], x2, r2)
        db_ref[...] = db
        dbb_ref[...] = db.astype(bf16)
        sums_ref[0:1, :] = col_sum(db)
        sums_ref[1:2, :] = col_sum(dy * x2)
        sums_ref[2:3, :] = col_sum(dy)


def put_halves(grad, keep_ref, send_ref):
    half = grad.shape[0] // 2
    low = grad.astype(bf16)
    keep_ref[:, :, :BLK, :] = low[:half].reshape(half // BLK, 1, BLK, grad.shape[1])
    send_ref[:, :, :BLK, :] = low[half:].reshape(half // BLK, 1, BLK, grad.shape[1])


def down_weight(dbb_ref, z_ref, keep_ref, send_ref):
    put_halves(tn(dbb_ref[...], z_ref[0]), keep_ref, send_ref)


def up_backward(dbb_ref, wd_ref, wu_ref, d_ref, n1b_ref, db_ref, x1_ref, r1_ref, vec_ref,
                keep_ref, send_ref, bu_ref, da_ref, dab_ref, sums_ref, acc_ref):
    step = pl.program_id(0)
    width = dbb_ref.shape[1]
    wd = wd_ref[...].reshape(width, wd_ref.shape[-1])
    wu = wu_ref[...].reshape(width, wu_ref.shape[-1])
    du = (nn(dbb_ref[...], wd) * d_ref[0]).astype(bf16)
    bu_ref[0] = col_sum(du.astype(f32))
    put_halves(tn(n1b_ref[...], du), keep_ref, send_ref)
    add = nt(du, wu)

    @pl.when(step == 0)
    def _():
        acc_ref[...] = add

    @pl.when(step > 0)
    def _():
        acc_ref[...] += add

    @pl.when(step == pl.num_programs(0) - 1)
    def _():
        dn1 = acc_ref[...].astype(bf16).astype(f32) + db_ref[...]
        da = normalize_back(dn1 * vec_ref[1:2, :], x1_ref[...], r1_ref[...])
        da_ref[...] = da
        dab_ref[...] = da.astype(bf16)
        sums_ref[0:1, :] = col_sum(da)
        sums_ref[1:2, :] = col_sum(dn1 * x1_ref[...])
        sums_ref[2:3, :] = col_sum(dn1)


def attention_backward(dab_ref, x_ref, w_ref, qkv_ref, p_ref, o_ref, da_ref, perm_ref,
                       keep_ref, send_ref, bqv_ref, dx_ref, acc_ref):
    step = pl.program_id(0)
    width = x_ref.shape[1]
    hc = o_ref.shape[-1]
    w = w_ref[...].reshape(width, w_ref.shape[-1])
    dab = dab_ref[...]
    do = nn(dab, w[:, 3 * hc :]).astype(bf16)
    qkv = qkv_ref[0]
    n_heads = hc // HD
    rows = p_ref.shape[1] // n_heads
    length = p_ref.shape[2]
    pieces = [[], [], []]
    for g in range(rows):
        span = slice(g * length, (g + 1) * length)
        here = [[], [], []]
        for h in range(n_heads):
            lo = h * HD
            q = qkv[span, lo : lo + HD]
            k = qkv[span, hc + lo : hc + lo + HD]
            v = qkv[span, 2 * hc + lo : 2 * hc + lo + HD]
            g_o = do[span, lo : lo + HD]
            p = p_ref[0, g * n_heads + h]
            dp = nt(g_o, v)
            ds = (p * (dp - jnp.sum(p * dp, axis=-1, keepdims=True))).astype(bf16)
            here[0].append((nn(ds, k) * SCALE).astype(bf16))
            here[1].append((tn(ds, q) * SCALE).astype(bf16))
            here[2].append(tn(p.astype(bf16), g_o).astype(bf16))
        for c in range(3):
            pieces[c].append(jnp.concatenate(here[c], axis=1))
    grads = [jnp.concatenate(piece, axis=0) for piece in pieces]
    bqv_ref[0, 0:1, :] = col_sum(grads[0].astype(f32))
    bqv_ref[0, 1:2, :] = col_sum(grads[2].astype(f32))
    dqkv = jnp.concatenate(grads, axis=1)
    keep_ref[:, :, BLK:, :] = jnp.zeros((*keep_ref.shape[:2], keep_ref.shape[2] - BLK, keep_ref.shape[3]), bf16)
    send_ref[:, :, BLK:, :] = jnp.zeros((*send_ref.shape[:2], send_ref.shape[2] - BLK, send_ref.shape[3]), bf16)
    put_halves(jnp.concatenate([tn(x_ref[...], dqkv), tn(dab, o_ref[0])], axis=1), keep_ref, send_ref)
    add = nt(dqkv, w[:, : 3 * hc])

    @pl.when(step == 0)
    def _():
        acc_ref[...] = add

    @pl.when(step > 0)
    def _():
        acc_ref[...] += add

    @pl.when(step == pl.num_programs(0) - 1)
    def _():
        dx = acc_ref[...] + da_ref[...]
        high = dx.astype(bf16)
        rest = dx - high.astype(f32)
        mid = rest.astype(bf16)
        low = (rest - mid.astype(f32)).astype(bf16)
        perm = perm_ref[...]
        dx_ref[...] = nt(high, perm) + nt(mid, perm) + nt(low, perm)


def whole(a):
    nd = a.ndim
    return pl.BlockSpec(a.shape, lambda s: (0,) * nd, pipeline_mode=pl.Buffered(1))


def lead(a):
    nd = a.ndim
    return pl.BlockSpec((1,) + a.shape[1:], lambda s: (s,) + (0,) * (nd - 1))


def weight(a):
    if a.ndim == 5:
        return pl.BlockSpec((a.shape[0], 1, a.shape[2], BLK, a.shape[4]), lambda s: (0, s, 0, 0, 0))
    return pl.BlockSpec((a.shape[0], 1, BLK, a.shape[3]), lambda s: (0, s, 0, 0))


def half_spec(h):
    return pl.BlockSpec((h.shape[0], 1) + h.shape[2:], lambda s: (0, s, 0, 0))


def sds(shape, dtype):
    return jax.ShapeDtypeStruct(shape, dtype)


def call(body, name, n_t, ins, outs, scratch, flops):
    moved = sum(a.size * a.dtype.itemsize for a, _ in ins) + sum(a.size * a.dtype.itemsize for a, _ in outs)
    return pl.pallas_call(
        body,
        name=name,
        grid=(n_t,),
        in_specs=[s for _, s in ins],
        out_specs=[s for _, s in outs],
        out_shape=[a for a, _ in outs],
        scratch_shapes=scratch,
        compiler_params=pltpu.CompilerParams(
            dimension_semantics=("arbitrary",), vmem_limit_bytes=VMEM_LIMIT
        ),
        cost_estimate=pl.CostEstimate(flops=flops, transcendentals=0, bytes_accessed=moved),
    )(*[a for a, _ in ins])


def flips(shape):
    n_dp, n_t = shape
    size = n_dp * n_t
    core = n_t
    x_bit, y_bit = 2 * core, 4 * core

    def table(bit_of):
        return [(i, i ^ bit_of(i)) for i in range(size)]

    return {
        "a": table(lambda i: 1),
        "b": table(lambda i: 2),
        "C": table(lambda i: core),
        "2": table(lambda i: x_bit if i & core else y_bit),
        "3": table(lambda i: y_bit if i & core else x_bit),
    }


def gather_all(v, order, tables):
    held = v[None]
    for stage in order:
        held = jnp.concatenate([held, lax.ppermute(held, AXES, tables[stage])])
    return held


def scatter_all(keep, send, order, tables):
    for n, stage in enumerate(order):
        got = lax.ppermute(send, AXES, tables[stage])
        total = keep.astype(f32) + got.astype(f32)
        half = total.shape[0] // 2
        if n + 1 < len(order):
            keep, send = total[:half], total[half:].astype(bf16)
    return total[0]


def per_device(
    hidden_in, segment_ids, pooled_grad, qkv_weight, qv_bias, out_weight, out_bias,
    norm1_gain, norm1_shift, up_weight, up_bias, down_weight_in, down_bias, norm2_gain, norm2_shift,
):
    n_dp, n_t = lax.axis_size("dp"), lax.axis_size("tensor")
    at_dp, at_t = lax.axis_index("dp"), lax.axis_index("tensor")
    hc, fc = qkv_weight.shape[2], up_weight.shape[1]
    rows = qkv_weight.shape[1]
    D = rows * n_dp
    micro, tokens = hidden_in.shape[0], hidden_in.shape[1]
    seqs, L = segment_ids.shape[1], segment_ids.shape[2]
    G, T = micro * seqs, micro * tokens
    segs = pooled_grad.shape[2]
    n_i = D // BLK
    pairwise = (n_dp, n_t) == (8, 4) and 4 * hc == fc

    d_parts = [out_bias, norm1_gain, norm1_shift, down_bias, norm2_gain, norm2_shift]
    e_parts = [qv_bias[0], qv_bias[1], up_bias]
    dv, ev = out_bias.shape[0], sum(p.shape[0] for p in e_parts)
    vec = jnp.concatenate(d_parts + e_parts)
    nd = len(d_parts) * dv
    heads_in = jnp.concatenate([qkv_weight[0], qkv_weight[1], qkv_weight[2], out_weight.T], axis=1)
    down_t = down_weight_in.T

    if pairwise:
        tables = flips((n_dp, n_t))
        pad = jnp.zeros((8, 4 * hc), bf16)
        pad = lax.dynamic_update_slice(pad, vec[None], (0, 0))
        first = jnp.concatenate([heads_in, pad], axis=0)
        w_qo = gather_all(first, "2ab3C", tables).reshape(4, n_t, 2, BLK + 8, 4 * hc)
        w_up = gather_all(up_weight, "ab23C", tables).reshape(n_i, n_t, BLK, fc)
        w_down = gather_all(down_t, "ab23C", tables).reshape(n_i, n_t, BLK, fc)
        vecs = w_qo[:, :, :, BLK, : vec.shape[0]].transpose(0, 2, 1, 3).reshape(n_i * n_t, -1)
        rel = jnp.arange(n_i)
        core = (at_dp & 1) ^ (rel >> 2)
        s3, s2 = (rel >> 1) & 1, rel & 1
        dy, dx = jnp.where(core == 0, s2, s3), jnp.where(core == 0, s3, s2)
        absolute = ((((at_dp >> 2) & 1) ^ dy) << 2) | ((((at_dp >> 1) & 1) ^ dx) << 1) | core
        t_of = at_t ^ jnp.arange(n_t)
        i_p = jnp.repeat(absolute, n_t)
        t_p = jnp.tile(t_of, n_i)
        to_d = jnp.repeat(rel, n_t) * n_t + t_p
        to_e = (((i_p * n_t) // n_i) ^ at_t) * n_i + (i_p * n_t + t_p) % n_i
        slot = jnp.arange(n_i * n_t)
        hot_d = (to_d[None, :] == slot[:, None]).astype(bf16)
        hot_e = (to_e[None, :] == slot[:, None]).astype(bf16)
        d_all = nn(hot_d, vecs[:, :nd])
        e_all = nn(hot_e, vecs[:, nd:])
        d_now = jnp.arange(D)
        source = absolute[d_now // BLK] * BLK + d_now % BLK
        perm = (jnp.arange(D)[:, None] == source[None, :]).astype(bf16)
    else:
        main = jnp.concatenate([heads_in, up_weight, down_t], axis=1)
        full = lax.all_gather(lax.all_gather(main, "dp", axis=0, tiled=True), "tensor", axis=0)
        full = full.reshape(n_t, n_i, BLK, -1).transpose(1, 0, 2, 3)
        w_qo, w_up, w_down = full[..., : 4 * hc], full[..., 4 * hc : 4 * hc + fc], full[..., 4 * hc + fc :]
        vecs = lax.all_gather(lax.all_gather(vec, "tensor"), "dp").reshape(n_dp * n_t, -1).astype(f32)
        d_all, e_all = vecs[:, :nd], vecs[:, nd:]
        perm = (jnp.arange(D)[:, None] == jnp.arange(D)[None, :]).astype(bf16)

    vec_d = jnp.concatenate([d_all[:, j * dv : (j + 1) * dv].reshape(1, D) for j in range(6)])
    b_q = e_all[:, :dv].reshape(n_t, 1, hc)
    b_v = e_all[:, dv : 2 * dv].reshape(n_t, 1, hc)
    b_u = e_all[:, 2 * dv :].reshape(n_t, 1, fc)

    x = nn(hidden_in.reshape(T, D), perm).astype(bf16)
    seg_r = segment_ids.reshape(G, L)
    seg_c = segment_ids.reshape(T, 1)
    pg = jnp.einsum("gsd,de->gse", pooled_grad.reshape(G, segs, D), perm.astype(f32), precision=HI)
    n_pairs = G * (hc // HD)
    flop = 2 * T * D

    qkv, prob, o, n1, x1, r1, n1b = call(
        attention_forward, "attention_forward", n_t,
        [(x, whole(x)), (w_qo, weight(w_qo)), (b_q, lead(b_q)), (b_v, lead(b_v)), (seg_c, whole(seg_c)),
         (seg_r, whole(seg_r)), (vec_d, whole(vec_d))],
        [(a, lead(a)) for a in (sds((n_t, T, 3 * hc), bf16), sds((n_t, n_pairs, L, L), f32), sds((n_t, T, hc), bf16))]
        + [(a, whole(a)) for a in (sds((T, D), f32), sds((T, D), f32), sds((T, 1), f32), sds((T, D), bf16))],
        [pltpu.VMEM((T, D), f32)], flop * 4 * D,
    )
    z, dgelu = call(
        up_forward, "up_forward", n_t,
        [(n1b, whole(n1b)), (w_up, weight(w_up)), (b_u, lead(b_u))],
        [(a, lead(a)) for a in (sds((n_t, T, fc), bf16), sds((n_t, T, fc), f32))], [], flop * n_t * fc,
    )
    pooled, db, dbb, sums2 = call(
        down_forward, "down_forward", n_t,
        [(z, lead(z)), (w_down, weight(w_down)), (n1, whole(n1)), (vec_d, whole(vec_d)), (seg_c, whole(seg_c)),
         (seg_r, whole(seg_r)), (pg, whole(pg))],
        [(a, whole(a)) for a in (sds((G, segs, D), f32), sds((T, D), f32), sds((T, D), bf16), sds((3, D), f32))],
        [pltpu.VMEM((T, D), f32)], flop * n_t * fc,
    )
    half = sds((n_i // 2, n_t, BLK, fc), bf16)
    down_keep, down_send = call(
        down_weight, "down_weight", n_t, [(dbb, whole(dbb)), (z, lead(z))],
        [(half, half_spec(half))] * 2, [], flop * n_t * fc,
    )
    up_keep, up_send, g_bu, da, dab, sums1 = call(
        up_backward, "up_backward", n_t,
        [(dbb, whole(dbb)), (w_down, weight(w_down)), (w_up, weight(w_up)), (dgelu, lead(dgelu)), (n1b, whole(n1b)),
         (db, whole(db)), (x1, whole(x1)), (r1, whole(r1)), (vec_d, whole(vec_d))],
        [(half, half_spec(half))] * 2 + [(a, lead(a)) for a in (sds((n_t, 1, fc), f32),)]
        + [(a, whole(a)) for a in (sds((T, D), f32), sds((T, D), bf16), sds((3, D), f32))],
        [pltpu.VMEM((T, D), f32)], 3 * flop * n_t * fc,
    )
    half_qo = sds((n_i // 2, n_t, BLK + 8, 4 * hc), bf16)
    qo_keep, qo_send, g_bqv, dx = call(
        attention_backward, "attention_backward", n_t,
        [(dab, whole(dab)), (x, whole(x)), (w_qo, weight(w_qo)), (qkv, lead(qkv)), (prob, lead(prob)), (o, lead(o)),
         (da, whole(da)), (perm, whole(perm))],
        [(half_qo, half_spec(half_qo))] * 2 + [(a, lead(a)) for a in (sds((n_t, 2, hc), f32),)]
        + [(a, whole(a)) for a in (sds((T, D), f32),)],
        [pltpu.VMEM((T, D), f32)], 2 * flop * 4 * D,
    )
    pooled = jnp.einsum("gse,de->gsd", pooled, perm.astype(f32), precision=HI)

    g_d = jnp.concatenate([v.reshape(n_dp * n_t, dv) for v in (*sums1, *sums2)], axis=1)
    g_e = jnp.concatenate(
        [g_bqv[:, 0].reshape(n_dp * n_t, dv), g_bqv[:, 1].reshape(n_dp * n_t, dv), g_bu.reshape(n_dp * n_t, -1)], axis=1
    )
    if pairwise:
        g_vec = jnp.concatenate([tn(hot_d, g_d.astype(bf16)), tn(hot_e, g_e.astype(bf16))], axis=1).astype(bf16)
        g_vec = g_vec.reshape(2, n_i // 2, n_t, 1, -1)
        qo_keep = lax.dynamic_update_slice(qo_keep, g_vec[0], (0, 0, BLK, 0))
        qo_send = lax.dynamic_update_slice(qo_send, g_vec[1], (0, 0, BLK, 0))

        def flat(a):
            return a.reshape((-1,) + a.shape[2:])

        g_down = scatter_all(flat(down_keep), flat(down_send), "C32ba", tables)
        g_up = scatter_all(flat(up_keep), flat(up_send), "C32ba", tables)
        g_qo = scatter_all(flat(qo_keep), flat(qo_send), "C32ba", tables)
        g_v = g_qo[BLK, : vec.shape[0]]
        g_qo = g_qo[:BLK]
    else:
        def joined(keep, send):
            g = jnp.concatenate([keep, send])[:, :, :BLK]
            return g.transpose(1, 0, 2, 3).reshape(n_t, D, -1)

        g_full = jnp.concatenate([joined(qo_keep, qo_send), joined(up_keep, up_send), joined(down_keep, down_send)], axis=2)
        mine = lax.psum_scatter(g_full, "tensor", scatter_dimension=0)
        mine = lax.psum_scatter(mine, "dp", scatter_dimension=0, tiled=True).astype(f32)
        g_qo, g_up, g_down = mine[:, : 4 * hc], mine[:, 4 * hc : 4 * hc + fc], mine[:, 4 * hc + fc :]
        g_v = lax.psum_scatter(jnp.concatenate([g_d, g_e], axis=1), AXES, scatter_dimension=0)
    vo = [g_v[j * dv : (j + 1) * dv] for j in range(8)]
    return (
        pooled.reshape(micro, seqs, segs, D),
        dx.reshape(micro, tokens, D),
        jnp.stack([g_qo[:, c * hc : (c + 1) * hc] for c in range(3)]),
        jnp.stack([vo[6], vo[7]]),
        g_qo[:, 3 * hc :].T,
        vo[0], vo[1], vo[2],
        g_up,
        g_v[8 * dv :],
        g_down.T,
        vo[3], vo[4], vo[5],
    )


def solution(mesh):
    both = P(AXES)
    row3 = P(None, AXES)
    return jax.shard_map(
        per_device,
        mesh=mesh,
        in_specs=(
            row3, row3, row3, P(None, "dp", "tensor"), row3, P("tensor", "dp"), both, both, both,
            P("dp", "tensor"), both, P("tensor", "dp"), both, both, both,
        ),
        out_specs=(
            row3, row3, P(None, "dp", "tensor"), row3, P("tensor", "dp"), both, both, both,
            P("dp", "tensor"), both, P("tensor", "dp"), both, both, both,
        ),
        check_vma=False,
    )
```

time: 772 us -> 330 us (0.43); the launches traced: 762 us -> 329 us
  waiting for transfers between devices: 489 us -> 146 us
  matrix products: 79.4 us -> 4.85 us
  Pallas kernels: 0 us -> 66 us
  blocking collectives: 62.4 us -> 0 us
  local copies, waits for them, and re-layouts: 105 us -> 59.7 us
  starting transfers between devices: 0.16 us -> 32.5 us
  between operations: 15.6 us -> 1.37 us
  other arithmetic: 9.89 us -> 18.7 us
    all_gather x2 -> x0, waiting for transfers between devices: 253 us -> none  [the longest x1 216 us: per_device(): full = lax.all_gather(full, 'tensor', axis=0)]
    reduce_scatter x2 -> x0, waiting for transfers between devices: 237 us -> none  [the longest x1 236 us: per_device(): gmine = lax.psum_scatter(gfull, 'tensor', scatter_dimension=0)]
    ppermute x0 -> x30, waiting for transfers between devices: none -> 146 us  [the longest x15 83 us: scatter_all(): got = lax.ppermute(send, AXES, tables[stage])]
    dot_general x25 -> x7, matrix products: 77 us -> 4.85 us  [the longest x3 1.86 us: nn(): lax.dot_general(a, b, (((1,), (0,)), ((), ())), preferred_element_type=f32)]
    pallas_call x0 -> x6, Pallas kernels: none -> 66 us  [call(): pl.pallas_call(body, name=name, grid=(n_t,), in_specs=[s for _, s in ins]...]
    unnamed x2 -> x0, blocking collectives: 53.4 us -> none
    transpose x11 -> x2, local copies, waits for them, and re-layouts: 46.7 us -> 0.12 us  [the longest x1 0.11 us: per_device(): g_qo[:, 3 * hc:]]
    ppermute x0 -> x30, starting transfers between devices: none -> 32.5 us  [the longest x15 18.5 us: gather_all(): held = jnp.concatenate([held, lax.ppermute(held, AXES, tables[stage])])]
  transfers between devices with their start and end apart: 4 -> 30, of which waited for: 4 -> 16; matrix products, arithmetic and copies ran while one was open for 2% -> 17% of each run, Pallas kernels for 0% -> 11%
where the time goes in v2:
time: 330 us; the launch traced here: 329 us
  waiting for transfers between devices  146 us (44%)
  Pallas kernels  66 us (20%)
  local copies, waits for them, and re-layouts  59.7 us (18%)
  starting transfers between devices  32.5 us (10%)
  other arithmetic  18.7 us (6%)
  matrix products  4.85 us (1%)
    ppermute x15, waiting for transfers between devices, scatter_all(): got = lax.ppermute(send, AXES, tables[stage])  83 us
    pallas_call x6, Pallas kernels, call(): pl.pallas_call(body, name=name, grid=(n_t,), in_specs=[s for _, s in ins]...  66 us
    ppermute x15, waiting for transfers between devices, gather_all(): held = jnp.concatenate([held, lax.ppermute(held, AXES, tables[stage])])  62.9 us
    unnamed x76, local copies, waits for them, and re-layouts  31.6 us
    ppermute x15, starting transfers between devices, gather_all(): held = jnp.concatenate([held, lax.ppermute(held, AXES, tables[stage])])  18.5 us
    ppermute x15, starting transfers between devices, scatter_all(): got = lax.ppermute(send, AXES, tables[stage])  14 us
    concatenate x6, local copies, waits for them, and re-layouts, gather_all(): held = jnp.concatenate([held, lax.ppermute(held, AXES, tables[stage])])  11.7 us
    add x13, other arithmetic, scatter_all(): total = keep.astype(f32) + got.astype(f32)  7.52 us
  transfers between devices with their start and end apart: 30, of which 16 were waited for; matrix products, arithmetic and copies ran while one was open for 17% of the time, Pallas kernels for 11%

profile of v2, /device:TPU:0, one launch (start us, length us, event | category | flops | bytes accessed | tf_op | source)
XLA Modules:
  0.0 328.9 jit_solution(4448280065554514802)
XLA Ops:
  0.7 3.1 collective-permute-start.10
  5.4 4.8 %concatenate.82 = bf16[288]{0:T(512)(128)(2,1)S(1)} concatenate(bf16[24]{0:T(256)(128)(2,1)} %param.21, bf16[24]{0:T(256)(128)(2,1)} %param.22, bf16[24]{0:T(256)(128)(2,1)} %param.23, bf16[24]{0:T(256)(128)(2,1)} %param.27, bf16[24]{0:T(256)(128)(2,1)} %param.28, bf16[24]{0:T(256)(128)(2,1)} %param.29, bf16[24]{0:T(256)(128)(2,1)S(1)} %get-tuple-element.174, ...), dimensions={0} | concatenate | bytes 1152 | tf_op jit(solution)/shard_map/concatenate | solution.py:352
  11.8 1.5 collective-permute-start
  13.8 0.9 pad_maximum_fusion.8
  14.7 2.7 collective-permute-start.11
  17.4 1.6 collective-permute-start.1
  19.1 1.6 constant_dynamic-update-slice_fusion.26
  20.7 2.6 collective-permute-done.5
  23.3 8.6 %collective-permute-done.11 = bf16[2,96,768]{2,1,0:T(8,128)(2,1)S(1)} collective-permute-done((bf16[2,96,768]{2,1,0:T(8,128)(2,1)S(1)}, bf16[2,96,768]{2,1,0:T(8,128)(2,1)S(1)}, u32[]{:S(2)}, u32[]{:S(2)}) %collective-permute-start.11) | collective-permute-done | bytes 294944 | tf_op jit(solution)/shard_map/ppermute | solution.py:319
  32.3 3.4 %collective-permute-done.1 = bf16[2,104,768]{2,1,0:T(8,128)(2,1)S(1)} collective-permute-done((bf16[2,104,768]{2,1,0:T(8,128)(2,1)S(1)}, bf16[2,104,768]{2,1,0:T(8,128)(2,1)S(1)}, u32[]{:S(2)}, u32[]{:S(2)}) %collective-permute-start.1) | collective-permute-done | bytes 319520 | tf_op jit(solution)/shard_map/ppermute | solution.py:319
  36.9 21.3 %collective-permute-done.6 = bf16[2,96,768]{2,1,0:T(8,128)(2,1)S(1)} collective-permute-done((bf16[2,96,768]{2,1,0:T(8,128)(2,1)S(1)}, bf16[2,96,768]{2,1,0:T(8,128)(2,1)S(1)}, u32[]{:S(2)}, u32[]{:S(2)}) %collective-permute-start.6) | collective-permute-done | bytes 294944 | tf_op jit(solution)/shard_map/ppermute | solution.py:319
  60.0 1.9 collective-permute-start.13
  61.9 8.2 %collective-permute-done.2 = bf16[4,104,768]{2,1,0:T(8,128)(2,1)S(1)} collective-permute-done((bf16[4,104,768]{2,1,0:T(8,128)(2,1)S(1)}, bf16[4,104,768]{2,1,0:T(8,128)(2,1)S(1)}, u32[]{:S(2)}, u32[]{:S(2)}) %collective-permute-start.2) | collective-permute-done | bytes 639008 | tf_op jit(solution)/shard_map/ppermute | solution.py:319
  71.4 3.2 collective-permute-done.7
  80.1 1.1 constant_dynamic-update-slice_fusion.1
  81.3 1.2 constant_dynamic-update-slice_fusion.22
  82.5 7.5 %collective-permute-done.3 = bf16[8,104,768]{2,1,0:T(8,128)(2,1)S(1)} collective-permute-done((bf16[8,104,768]{2,1,0:T(8,128)(2,1)S(1)}, bf16[8,104,768]{2,1,0:T(8,128)(2,1)S(1)}, u32[]{:S(2)}, u32[]{:S(2)}) %collective-permute-start.3) | collective-permute-done | bytes 1277984 | tf_op jit(solution)/shard_map/ppermute | solution.py:319
  90.0 1.7 constant_dynamic-update-slice_fusion
  91.7 2.7 collective-permute-start.4
  94.4 8.2 %collective-permute-done.8 = bf16[8,96,768]{2,1,0:T(8,128)(2,1)S(1)} collective-permute-done((bf16[8,96,768]{2,1,0:T(8,128)(2,1)S(1)}, bf16[8,96,768]{2,1,0:T(8,128)(2,1)S(1)}, u32[]{:S(2)}, u32[]{:S(2)}) %collective-permute-start.8) | collective-permute-done | bytes 1179680 | tf_op jit(solution)/shard_map/ppermute | solution.py:319
  102.7 1.2 constant_dynamic-update-slice_fusion.11
  103.9 2.2 copy-done.16
  106.1 2.4 collective-permute-start.9
  109.8 4.6 %fusion.42 = s32[768]{0:T(1024)S(1)} fusion(s32[]{:T(128)} %bitcast.1, s32[]{:T(128)} %bitcast.2, s32[]{:T(128)} %bitcast.3, s32[]{:T(128)} %bitcast.4, s32[]{:T(128)} %bitcast.5, s32[]{:T(128)} %bitcast.7, s32[]{:T(128)} %bitcast.6), kind=kLoop, calls=%fused_computation.143 | loop fusion | flops 17664 | bytes 3100 | tf_op jit(solution)/shard_map/gather | solution.py:382
  116.3 1.5 fusion.8.x_ref
  117.9 2.0 constant_dynamic-update-slice_fusion.27
  119.9 1.3 copy-done.17
  121.2 2.2 constant_dynamic-update-slice_fusion.16
  123.5 2.2 copy-done.18
  125.7 3.4 %constant_dynamic-update-slice_fusion.5 = bf16[32,104,768]{2,1,0:T(8,128)(2,1)} fusion(bf16[32,104,768]{2,1,0:T(8,128)(2,1)} %get-tuple-element.119, bf16[16,104,768]{2,1,0:T(8,128)(2,1)} %collective-permute-done.4), kind=kLoop, calls=%fused_computation.69 | loop fusion | bytes 5111808 | tf_op jit(solution)/shard_map/concatenate | solution.py:319
  129.0 1.0 slice.305
  131.5 1.1 copy-done.14
  132.5 16.8 %attention_forward.1 = (bf16[4,384,576]{2,1,0:T(8,128)(2,1)S(1)}, f32[4,9,128,128]{3,2,1,0:T(8,128)S(1)}, bf16[4,384,192]{2,1,0:T(8,128)(2,1)S(1)}, f32[384,768]...) custom-call(bf16[384,768]{1,0:T(8,128)(2,1)S(1)} %copy-done.14, ...), custom_call_target="tpu_custom_call" | custom-call | flops 1811939328 | bytes 13398528 | tf_op jit(solution)/shard_map/attention_forward/pallas_call | solution.py:283
  149.3 1.3 copy-done.10
  151.5 2.5 copy-done.19
  154.0 3.9 %up_forward.1 = (bf16[4,384,768]{2,1,0:T(8,128)(2,1)S(1)}, f32[4,384,768]{2,1,0:T(8,128)S(1)}) custom-call(bf16[384,768]{1,0:T(8,128)(2,1)S(1)} %get-tuple-element.39.n_ref.n1b_ref, bf16[8,4,96,768]{3,2,1,0:T(8,128)(2,1)S(1)} %bitcast.117, f32[4,1,768]{2,1,0:T(1,128)S(1)} %reshape.253.b_ref), custom_call_target="tpu_custom_call" | custom-call | flops 1811939328 | bytes 12398592 | tf_op jit(solution)/shard_map/up_forward/pallas_call | solution.py:283
  158.0 2.1 copy-done.21
  160.1 5.5 %down_forward.1 = (f32[3,8,768]{2,1,0:T(8,128)S(1)}, f32[384,768]{1,0:T(8,128)S(1)}, bf16[384,768]{1,0:T(8,128)(2,1)S(1)}, f32[3,768]{1,0:T(4,128)S(1)}) custom-call(bf16[4,384,768]{2,1,0:T(8,128)(2,1)S(1)} %get-tuple-element.40.z_ref, bf16[8,4,96,768]{3,2,1,0:T(8,128)(2,1)S(1)} %bitcast.113, f32[384,768]{1,0:T(8,128)S(1)} %get-tuple-element.41.n1_ref, ...), custom_call_target="tpu_custom_call" | custom-call | flops 1811939328 | bytes 10205184 | tf_op jit(solution)/shard_map/down_forward/pallas_call | solution.py:283
  165.6 4.2 %down_weight.1 = (bf16[4,4,96,768]{3,2,1,0:T(8,128)(2,1)S(1)}, bf16[4,4,96,768]{3,2,1,0:T(8,128)(2,1)}) custom-call(bf16[384,768]{1,0:T(8,128)(2,1)S(1)} %get-tuple-element.43.dbb_ref, bf16[4,384,768]{2,1,0:T(8,128)(2,1)S(1)} %get-tuple-element.40.z_ref), custom_call_target="tpu_custom_call" | custom-call | flops 1811939328 | bytes 7667712 | tf_op jit(solution)/shard_map/down_weight/pallas_call | solution.py:283
  169.8 1.5 copy-done.7
  171.3 11.9 %up_backward.1 = (bf16[4,4,96,768]{3,2,1,0:T(8,128)(2,1)S(1)}, bf16[4,4,96,768]{3,2,1,0:T(8,128)(2,1)}, f32[4,1,768]{2,1,0:T(1,128)S(1)}, f32[384,768]{1,0:T(8,1...) custom-call(bf16[384,768]{1,0:T(8,128)(2,1)S(1)} %get-tuple-element.43.dbb_ref, ...), custom_call_target="tpu_custom_call" | custom-call | flops 5435817984 | bytes 24224256 | tf_op jit(solution)/shard_map/up_backward/pallas_call | solution.py:283
  183.2 1.5 copy-done.8
  185.1 23.7 %attention_backward.1 = (bf16[4,4,104,768]{3,2,1,0:T(8,128)(2,1)S(1)}, bf16[4,4,104,768]{3,2,1,0:T(8,128)(2,1)S(1)}, f32[4,2,192]{2,1,0:T(2,128)S(1)}, f32[384,768]{1,0:T(8,128)}) custom-call(bf16[384,768]{1,0:T(8,128)(2,1)S(1)} %get-tuple-element.48.dab_ref, bf16[384,768]{1,0:T(8,128)(2,1)S(1)} %copy-done.15, bf16[4,4,2,104,768]{4,3,2,1,0:T(8,128)(2,1)} %bitcast.17.w_ref, ...), custom_call_target="tpu_custom_call" | custom-call | flops 3623878656 | bytes 19666944 | tf_op jit(solution)/shard_map/attention_backward/pallas_call | solution.py:283
  208.9 1.4 copy-done.5
  210.3 1.5 copy-done.20
  213.4 1.9 dynamic_update_slice.11
  215.4 1.9 dynamic_update_slice.10
  217.3 2.9 convert_add_fusion.1
  220.4 1.8 collective-permute-start.26
  222.2 2.4 convert_add_fusion.2
  224.7 1.5 collective-permute-start.21
  227.7 1.8 fusion.15
  229.5 7.2 %collective-permute-done.26 = bf16[8,96,768]{2,1,0:T(8,128)(2,1)S(1)} collective-permute-done((bf16[8,96,768]{2,1,0:T(8,128)(2,1)S(1)}, bf16[8,96,768]{2,1,0:T(8,128)(2,1)S(1)}, u32[]{:S(2)}, u32[]{:S(2)}) %collective-permute-start.26) | collective-permute-done | bytes 1179680 | tf_op jit(solution)/shard_map/ppermute | solution.py:325
  237.0 1.8 collective-permute-start.27
  238.8 16.8 %collective-permute-done.21 = bf16[8,96,768]{2,1,0:T(8,128)(2,1)S(1)} collective-permute-done((bf16[8,96,768]{2,1,0:T(8,128)(2,1)S(1)}, bf16[8,96,768]{2,1,0:T(8,128)(2,1)S(1)}, u32[]{:S(2)}, u32[]{:S(2)}) %collective-permute-start.21) | collective-permute-done | bytes 1179680 | tf_op jit(solution)/shard_map/ppermute | solution.py:325
  256.0 1.8 collective-permute-start.22
  257.8 17.8 %collective-permute-done.16 = bf16[8,104,768]{2,1,0:T(8,128)(2,1)S(1)} collective-permute-done((bf16[8,104,768]{2,1,0:T(8,128)(2,1)S(1)}, bf16[8,104,768]{2,1,0:T(8,128)(2,1)S(1)}, u32[]{:S(2)}, u32[]{:S(2)}) %collective-permute-start.16) | collective-permute-done | bytes 1277984 | tf_op jit(solution)/shard_map/ppermute | solution.py:325
  276.0 1.8 collective-permute-start.17
  278.3 3.0 collective-permute-start.23
  281.3 19.7 %collective-permute-done.28 = bf16[2,96,768]{2,1,0:T(8,128)(2,1)S(1)} collective-permute-done((bf16[2,96,768]{2,1,0:T(8,128)(2,1)S(1)}, bf16[2,96,768]{2,1,0:T(8,128)(2,1)S(1)}, u32[]{:S(2)}, u32[]{:S(2)}) %collective-permute-start.28) | collective-permute-done | bytes 294944 | tf_op jit(solution)/shard_map/ppermute | solution.py:325
  302.2 12.0 %collective-permute-done.23 = bf16[2,96,768]{2,1,0:T(8,128)(2,1)S(1)} collective-permute-done((bf16[2,96,768]{2,1,0:T(8,128)(2,1)S(1)}, bf16[2,96,768]{2,1,0:T(8,128)(2,1)S(1)}, u32[]{:S(2)}, u32[]{:S(2)}) %collective-permute-start.23) | collective-permute-done | bytes 294944 | tf_op jit(solution)/shard_map/ppermute | solution.py:325
  315.1 5.0 %collective-permute-done.18 = bf16[2,104,768]{2,1,0:T(8,128)(2,1)S(1)} collective-permute-done((bf16[2,104,768]{2,1,0:T(8,128)(2,1)S(1)}, bf16[2,104,768]{2,1,0:T(8,128)(2,1)S(1)}, u32[]{:S(2)}, u32[]{:S(2)}) %collective-permute-start.18) | collective-permute-done | bytes 319520 | tf_op jit(solution)/shard_map/ppermute | solution.py:325
  320.2 1.3 collective-permute-done.24
  322.3 3.2 collective-permute-done.19
  (192 shorter events, 31.5 us)
Async XLA Ops:
  0.6 115.7 %copy-start = (bf16[3,128,768]{2,1,0:T(8,128)(2,1)S(1)}, bf16[3,128,768]{2,1,0:T(8,128)(2,1)}, u32[]{:S(2)}) copy-start(bf16[3,128,768]{2,1,0:T(8,128)(2,1)} %param.15) | copy-start | bytes 1769476
  0.7 31.2 %copy-start.24 = (bf16[768,96]{0,1:T(8,128)(2,1)S(1)}, bf16[768,96]{0,1:T(8,128)(2,1)}, u32[]{:S(2)}) copy-start(bf16[768,96]{0,1:T(8,128)(2,1)} %param.26) | copy-start | bytes 442372
  0.7 22.5 %copy-start.25 = (bf16[96,768]{1,0:T(8,128)(2,1)S(1)}, bf16[96,768]{1,0:T(8,128)(2,1)}, u32[]{:S(2)}) copy-start(bf16[96,768]{1,0:T(8,128)(2,1)} %param.24) | copy-start | bytes 442372
  0.7 13.1 %collective-permute-start.10 = (bf16[1,96,768]{2,1,0:T(8,128)(2,1)}, bf16[1,96,768]{2,1,0:T(8,128)(2,1)S(1)}, u32[]{:S(2)}, u32[]{:S(2)}) collective-permute-start(bf16[1,96,768]{2,1,0:T(8,128)(2,1)} %bitcast.119), channel_id=1, source_target_pairs={{0,1},{1,0},{2,3},{3,2},{4,5},{5,4},{6,7},{7,6},{8,9},{9,8},{10,11... | collective-permute-start | bytes 442376 | tf_op jit(solution)/shard_map/ppermute | solution.py:319
  11.8 5.6 %collective-permute-start = (bf16[1,104,768]{2,1,0:T(8,128)(2,1)S(1)}, bf16[1,104,768]{2,1,0:T(8,128)(2,1)S(1)}, u32[]{:S(2)}, u32[]{:S(2)}) collective-permute-start(bf16[1,104,768]{2,1,0:T(8,128)(2,1)S(1)} %get-tuple-element.117), channel_id=1, source_target_pairs={{0,16},{1,17},{2,18},{3,19},{4,12},{5,13},{6,14},{7,15},{8,24},{9,... | collective-permute-start | bytes 479240 | tf_op jit(solution)/shard_map/ppermute | solution.py:319
  13.3 9.9 %collective-permute-start.5 = (bf16[1,96,768]{2,1,0:T(8,128)(2,1)}, bf16[1,96,768]{2,1,0:T(8,128)(2,1)S(1)}, u32[]{:S(2)}, u32[]{:S(2)}) collective-permute-start(bf16[1,96,768]{2,1,0:T(8,128)(2,1)} %bitcast.123), channel_id=1, source_target_pairs={{0,1},{1,0},{2,3},{3,2},{4,5},{5,4},{6,7},{7,6},{8,9},{9,8},{10,11... | collective-permute-start | bytes 442376 | tf_op jit(solution)/shard_map/ppermute | solution.py:319
  14.7 17.2 %collective-permute-start.11 = (bf16[2,96,768]{2,1,0:T(8,128)(2,1)S(1)}, bf16[2,96,768]{2,1,0:T(8,128)(2,1)S(1)}, u32[]{:S(2)}, u32[]{:S(2)}) collective-permute-start(bf16[2,96,768]{2,1,0:T(8,128)(2,1)S(1)} %pad_maximum_fusion.8), channel_id=1, source_target_pairs={{0,2},{1,3},{2,0},{3,1},{4,6},{5,7},{6,4},{7,5},{8,10},{9,11},{10,... | collective-permute-start | bytes 884744 | tf_op jit(solution)/shard_map/ppermute | solution.py:319
  17.4 18.3 %collective-permute-start.1 = (bf16[2,104,768]{2,1,0:T(8,128)(2,1)S(1)}, bf16[2,104,768]{2,1,0:T(8,128)(2,1)S(1)}, u32[]{:S(2)}, u32[]{:S(2)}) collective-permute-start(bf16[2,104,768]{2,1,0:T(8,128)(2,1)S(1)} %pad_maximum_fusion.6), channel_id=1, source_target_pairs={{0,1},{1,0},{2,3},{3,2},{4,5},{5,4},{6,7},{7,6},{8,9},{9,8},{10,11... | collective-permute-start | bytes 958472 | tf_op jit(solution)/shard_map/ppermute | solution.py:319
  23.3 34.9 %collective-permute-start.6 = (bf16[2,96,768]{2,1,0:T(8,128)(2,1)S(1)}, bf16[2,96,768]{2,1,0:T(8,128)(2,1)S(1)}, u32[]{:S(2)}, u32[]{:S(2)}) collective-permute-start(bf16[2,96,768]{2,1,0:T(8,128)(2,1)S(1)} %pad_maximum_fusion.7), channel_id=1, source_target_pairs={{0,2},{1,3},{2,0},{3,1},{4,6},{5,7},{6,4},{7,5},{8,10},{9,11},{10,... | collective-permute-start | bytes 884744 | tf_op jit(solution)/shard_map/ppermute | solution.py:319
  32.0 28.0 %collective-permute-start.12 = (bf16[4,96,768]{2,1,0:T(8,128)(2,1)S(1)}, bf16[4,96,768]{2,1,0:T(8,128)(2,1)S(1)}, u32[]{:S(2)}, u32[]{:S(2)}) collective-permute-start(bf16[4,96,768]{2,1,0:T(8,128)(2,1)S(1)} %pad_maximum_fusion.5), channel_id=1, source_target_pairs={{0,16},{1,17},{2,18},{3,19},{4,12},{5,13},{6,14},{7,15},{8,24},{9,... | collective-permute-start | bytes 1769480 | tf_op jit(solution)/shard_map/ppermute | solution.py:319
  35.7 34.3 %collective-permute-start.2 = (bf16[4,104,768]{2,1,0:T(8,128)(2,1)S(1)}, bf16[4,104,768]{2,1,0:T(8,128)(2,1)S(1)}, u32[]{:S(2)}, u32[]{:S(2)}) collective-permute-start(bf16[4,104,768]{2,1,0:T(8,128)(2,1)S(1)} %pad_maximum_fusion.3), channel_id=1, source_target_pairs={{0,2},{1,3},{2,0},{3,1},{4,6},{5,7},{6,4},{7,5},{8,10},{9,11},{10,... | collective-permute-start | bytes 1916936 | tf_op jit(solution)/shard_map/ppermute | solution.py:319
  58.2 16.3 %collective-permute-start.7 = (bf16[4,96,768]{2,1,0:T(8,128)(2,1)S(1)}, bf16[4,96,768]{2,1,0:T(8,128)(2,1)S(1)}, u32[]{:S(2)}, u32[]{:S(2)}) collective-permute-start(bf16[4,96,768]{2,1,0:T(8,128)(2,1)S(1)} %pad_maximum_fusion.4), channel_id=1, source_target_pairs={{0,16},{1,17},{2,18},{3,19},{4,12},{5,13},{6,14},{7,15},{8,24},{9,... | collective-permute-start | bytes 1769480 | tf_op jit(solution)/shard_map/ppermute | solution.py:319
  60.0 21.2 %collective-permute-start.13 = (bf16[8,96,768]{2,1,0:T(8,128)(2,1)S(1)}, bf16[8,96,768]{2,1,0:T(8,128)(2,1)S(1)}, u32[]{:S(2)}, u32[]{:S(2)}) collective-permute-start(bf16[8,96,768]{2,1,0:T(8,128)(2,1)S(1)} %pad_maximum_fusion.2), channel_id=1, source_target_pairs={{0,8},{1,9},{2,10},{3,11},{4,20},{5,21},{6,22},{7,23},{8,0},{9,1},... | collective-permute-start | bytes 3538952 | tf_op jit(solution)/shard_map/ppermute | solution.py:319
  70.2 19.8 %collective-permute-start.3 = (bf16[8,104,768]{2,1,0:T(8,128)(2,1)S(1)}, bf16[8,104,768]{2,1,0:T(8,128)(2,1)S(1)}, u32[]{:S(2)}, u32[]{:S(2)}) collective-permute-start(bf16[8,104,768]{2,1,0:T(8,128)(2,1)S(1)} %pad_maximum_fusion), channel_id=1, source_target_pairs={{0,8},{1,9},{2,10},{3,11},{4,20},{5,21},{6,22},{7,23},{8,0},{9,1},... | collective-permute-start | bytes 3833864 | tf_op jit(solution)/shard_map/ppermute | solution.py:319
  74.7 28.0 %collective-permute-start.8 = (bf16[8,96,768]{2,1,0:T(8,128)(2,1)S(1)}, bf16[8,96,768]{2,1,0:T(8,128)(2,1)S(1)}, u32[]{:S(2)}, u32[]{:S(2)}) collective-permute-start(bf16[8,96,768]{2,1,0:T(8,128)(2,1)S(1)} %pad_maximum_fusion.1), channel_id=1, source_target_pairs={{0,8},{1,9},{2,10},{3,11},{4,20},{5,21},{6,22},{7,23},{8,0},{9,1},... | collective-permute-start | bytes 3538952 | tf_op jit(solution)/shard_map/ppermute | solution.py:319
  82.5 21.4 %copy-start.2 = (bf16[32,96,768]{2,1,0:T(8,128)(2,1)}, bf16[32,96,768]{2,1,0:T(8,128)(2,1)S(1)}, u32[]{:S(2)}) copy-start(bf16[32,96,768]{2,1,0:T(8,128)(2,1)S(1)} %get-tuple-element.121) | copy-start | bytes 14155780
  82.5 35.3 %collective-permute-start.14 = (bf16[16,96,768]{2,1,0:T(8,128)(2,1)}, bf16[16,96,768]{2,1,0:T(8,128)(2,1)}, u32[]{:S(2)}, u32[]{:S(2)}) collective-permute-start(bf16[16,96,768]{2,1,0:T(8,128)(2,1)} %get-tuple-element.120), channel_id=1, source_target_pairs={{0,4},{1,5},{2,6},{3,7},{4,0},{5,1},{6,2},{7,3},{8,12},{9,13},{10,... | collective-permute-start | bytes 7077896 | tf_op jit(solution)/shard_map/ppermute | solution.py:319
  91.7 17.1 %copy-start.26 = (s32[3,1,128]{2,1,0:T(1,128)S(1)}, s32[3,1,128]{2,1,0:T(1,128)}, u32[]{:S(2)}) copy-start(s32[3,1,128]{2,1,0:T(1,128)} %param.16) | copy-start | bytes 4612
  91.7 23.3 %copy-start.27 = (f32[3,1,8,768]{3,2,1,0:T(8,128)S(1)}, f32[3,1,8,768]{3,2,1,0:T(8,128)}, u32[]{:S(2)}) copy-start(f32[3,1,8,768]{3,2,1,0:T(8,128)} %param.17) | copy-start | bytes 221188
  91.7 31.7 %collective-permute-start.4 = (bf16[16,104,768]{2,1,0:T(8,128)(2,1)}, bf16[16,104,768]{2,1,0:T(8,128)(2,1)}, u32[]{:S(2)}, u32[]{:S(2)}) collective-permute-start(bf16[16,104,768]{2,1,0:T(8,128)(2,1)} %get-tuple-element.118), channel_id=1, source_target_pairs={{0,4},{1,5},{2,6},{3,7},{4,0},{5,1},{6,2},{7,3},{8,12},{9,13},{10,... | collective-permute-start | bytes 7667720 | tf_op jit(solution)/shard_map/ppermute | solution.py:319
  103.9 2.2 copy-start.16
  106.1 13.8 %collective-permute-start.9 = (bf16[16,96,768]{2,1,0:T(8,128)(2,1)}, bf16[16,96,768]{2,1,0:T(8,128)(2,1)}, u32[]{:S(2)}, u32[]{:S(2)}) collective-permute-start(bf16[16,96,768]{2,1,0:T(8,128)(2,1)} %get-tuple-element.122), channel_id=1, source_target_pairs={{0,4},{1,5},{2,6},{3,7},{4,0},{5,1},{6,2},{7,3},{8,12},{9,13},{10,... | collective-permute-start | bytes 7077896 | tf_op jit(solution)/shard_map/ppermute | solution.py:319
  115.1 2.8 copy-start.3
  117.9 3.4 %copy-start.17 = (bf16[32,96,768]{2,1,0:T(8,128)(2,1)S(1)}, bf16[32,96,768]{2,1,0:T(8,128)(2,1)}, u32[]{:S(2)}) copy-start(bf16[32,96,768]{2,1,0:T(8,128)(2,1)} %copy-done.16) | copy-start | bytes 14155780
  119.8 3.6 %copy-start.4 = (bf16[32,96,768]{2,1,0:T(8,128)(2,1)}, bf16[32,96,768]{2,1,0:T(8,128)(2,1)S(1)}, u32[]{:S(2)}) copy-start(bf16[32,96,768]{2,1,0:T(8,128)(2,1)S(1)} %constant_dynamic-update-slice_fusion.27) | copy-start | bytes 14155780
  123.4 2.2 copy-start.18
  130.8 29.3 %slice-start = ((s8[4718592]{0:T(1024)(128)(4,1)}), s8[524288]{0:T(1024)(128)(4,1)S(1)}, s32[]{:S(2)}) async-start(s8[4718592]{0:T(1024)(128)(4,1)} %bitcast.111), calls=%async_computation | async-start | bytes 1048576
  131.5 1.1 copy-start.14
  132.5 27.5 %slice-start.1 = ((s8[4718592]{0:T(1024)(128)(4,1)}), s8[4194304]{0:T(1024)(128)(4,1)S(1)}, s32[]{:S(2)}) async-start(s8[4718592]{0:T(1024)(128)(4,1)} %bitcast.111), calls=%async_computation.1 | async-start | bytes 8388608
  149.3 1.3 copy-start.10
  150.6 0.9 copy-start.12
  151.5 6.5 %copy-start.22 = (bf16[384,768]{1,0:T(8,128)(2,1)}, bf16[384,768]{1,0:T(8,128)(2,1)S(1)}, u32[]{:S(2)}) copy-start(bf16[384,768]{1,0:T(8,128)(2,1)S(1)} %get-tuple-element.39.n_ref.n1b_ref) | copy-start | bytes 1769476
  151.5 2.5 copy-start.19
  158.0 2.1 copy-start.21
  165.6 5.7 %copy-start.23 = (bf16[384,768]{1,0:T(8,128)(2,1)S(1)}, bf16[384,768]{1,0:T(8,128)(2,1)}, u32[]{:S(2)}) copy-start(bf16[384,768]{1,0:T(8,128)(2,1)} %copy-done.22) | copy-start | bytes 1769476
  169.8 1.5 copy-start.7
  171.3 46.0 %collective-permute-start.25 = (bf16[16,96,768]{2,1,0:T(8,128)(2,1)}, bf16[16,96,768]{2,1,0:T(8,128)(2,1)}, u32[]{:S(2)}, u32[]{:S(2)}) collective-permute-start(bf16[16,96,768]{2,1,0:T(8,128)(2,1)} %bitcast.48), channel_id=1, source_target_pairs={{0,4},{1,5},{2,6},{3,7},{4,0},{5,1},{6,2},{7,3},{8,12},{9,13},{10,... | collective-permute-start | bytes 7077896 | tf_op jit(solution)/shard_map/ppermute | solution.py:325
  171.3 13.8 %copy-start.11 = (bf16[4,384,576]{2,1,0:T(8,128)(2,1)S(1)}, bf16[4,384,576]{2,1,0:T(8,128)(2,1)}, u32[]{:S(2)}) copy-start(bf16[4,384,576]{2,1,0:T(8,128)(2,1)} %copy-done.10) | copy-start | bytes 5308420
  171.3 13.9 %copy-start.13 = (bf16[4,384,192]{2,1,0:T(8,128)(2,1)S(1)}, bf16[4,384,192]{2,1,0:T(8,128)(2,1)}, u32[]{:S(2)}) copy-start(bf16[4,384,192]{2,1,0:T(8,128)(2,1)} %copy-done.12) | copy-start | bytes 1769476
  171.3 13.8 %copy-start.15 = (bf16[384,768]{1,0:T(8,128)(2,1)S(1)}, bf16[384,768]{1,0:T(8,128)(2,1)}, u32[]{:S(2)}) copy-start(bf16[384,768]{1,0:T(8,128)(2,1)} %fusion.8.x_ref) | copy-start | bytes 1769476
  183.2 1.5 copy-start.8
  184.6 37.6 %collective-permute-start.20 = (bf16[16,96,768]{2,1,0:T(8,128)(2,1)}, bf16[16,96,768]{2,1,0:T(8,128)(2,1)}, u32[]{:S(2)}, u32[]{:S(2)}) collective-permute-start(bf16[16,96,768]{2,1,0:T(8,128)(2,1)} %bitcast.44), channel_id=1, source_target_pairs={{0,4},{1,5},{2,6},{3,7},{4,0},{5,1},{6,2},{7,3},{8,12},{9,13},{10,... | collective-permute-start | bytes 7077896 | tf_op jit(solution)/shard_map/ppermute | solution.py:325
  208.9 1.4 copy-start.5
  210.3 1.5 copy-start.20
  215.4 10.9 %collective-permute-start.15 = (bf16[16,104,768]{2,1,0:T(8,128)(2,1)}, bf16[16,104,768]{2,1,0:T(8,128)(2,1)S(1)}, u32[]{:S(2)}, u32[]{:S(2)}) collective-permute-start(bf16[16,104,768]{2,1,0:T(8,128)(2,1)} %bitcast.118), channel_id=1, source_target_pairs={{0,4},{1,5},{2,6},{3,7},{4,0},{5,1},{6,2},{7,3},{8,12},{9,13},{10,... | collective-permute-start | bytes 7667720 | tf_op jit(solution)/shard_map/ppermute | solution.py:325
  220.2 1.9 copy-start.9
  220.4 16.3 %collective-permute-start.26 = (bf16[8,96,768]{2,1,0:T(8,128)(2,1)S(1)}, bf16[8,96,768]{2,1,0:T(8,128)(2,1)S(1)}, u32[]{:S(2)}, u32[]{:S(2)}) collective-permute-start(bf16[8,96,768]{2,1,0:T(8,128)(2,1)S(1)} %slice.417), channel_id=1, source_target_pairs={{0,8},{1,9},{2,10},{3,11},{4,20},{5,21},{6,22},{7,23},{8,0},{9,1},... | collective-permute-start | bytes 3538952 | tf_op jit(solution)/shard_map/ppermute | solution.py:325
  222.2 4.0 %copy-start.6 = (bf16[4,4,104,768]{3,2,1,0:T(8,128)(2,1)S(1)}, bf16[4,4,104,768]{3,2,1,0:T(8,128)(2,1)}, u32[]{:S(2)}) copy-start(bf16[4,4,104,768]{3,2,1,0:T(8,128)(2,1)} %dynamic_update_slice.10) | copy-start | bytes 7667716
  224.7 30.9 %collective-permute-start.21 = (bf16[8,96,768]{2,1,0:T(8,128)(2,1)S(1)}, bf16[8,96,768]{2,1,0:T(8,128)(2,1)S(1)}, u32[]{:S(2)}, u32[]{:S(2)}) collective-permute-start(bf16[8,96,768]{2,1,0:T(8,128)(2,1)S(1)} %slice.418), channel_id=1, source_target_pairs={{0,8},{1,9},{2,10},{3,11},{4,20},{5,21},{6,22},{7,23},{8,0},{9,1},... | collective-permute-start | bytes 3538952 | tf_op jit(solution)/shard_map/ppermute | solution.py:325
  227.0 48.6 %collective-permute-start.16 = (bf16[8,104,768]{2,1,0:T(8,128)(2,1)S(1)}, bf16[8,104,768]{2,1,0:T(8,128)(2,1)S(1)}, u32[]{:S(2)}, u32[]{:S(2)}) collective-permute-start(bf16[8,104,768]{2,1,0:T(8,128)(2,1)S(1)} %slice.416), channel_id=1, source_target_pairs={{0,8},{1,9},{2,10},{3,11},{4,20},{5,21},{6,22},{7,23},{8,0},{9,1},... | collective-permute-start | bytes 3833864 | tf_op jit(solution)/shard_map/ppermute | solution.py:325
  237.0 40.9 %collective-permute-start.27 = (bf16[4,96,768]{2,1,0:T(8,128)(2,1)S(1)}, bf16[4,96,768]{2,1,0:T(8,128)(2,1)S(1)}, u32[]{:S(2)}, u32[]{:S(2)}) collective-permute-start(bf16[4,96,768]{2,1,0:T(8,128)(2,1)S(1)} %slice.420), channel_id=1, source_target_pairs={{0,16},{1,17},{2,18},{3,19},{4,12},{5,13},{6,14},{7,15},{8,24},{9,... | collective-permute-start | bytes 1769480 | tf_op jit(solution)/shard_map/ppermute | solution.py:325
  256.0 22.2 %collective-permute-start.22 = (bf16[4,96,768]{2,1,0:T(8,128)(2,1)S(1)}, bf16[4,96,768]{2,1,0:T(8,128)(2,1)S(1)}, u32[]{:S(2)}, u32[]{:S(2)}) collective-permute-start(bf16[4,96,768]{2,1,0:T(8,128)(2,1)S(1)} %slice.421), channel_id=1, source_target_pairs={{0,16},{1,17},{2,18},{3,19},{4,12},{5,13},{6,14},{7,15},{8,24},{9,... | collective-permute-start | bytes 1769480 | tf_op jit(solution)/shard_map/ppermute | solution.py:325
  276.0 25.1 %collective-permute-start.17 = (bf16[4,104,768]{2,1,0:T(8,128)(2,1)S(1)}, bf16[4,104,768]{2,1,0:T(8,128)(2,1)S(1)}, u32[]{:S(2)}, u32[]{:S(2)}) collective-permute-start(bf16[4,104,768]{2,1,0:T(8,128)(2,1)S(1)} %slice.419), channel_id=1, source_target_pairs={{0,16},{1,17},{2,18},{3,19},{4,12},{5,13},{6,14},{7,15},{8,24},{9,... | collective-permute-start | bytes 1916936 | tf_op jit(solution)/shard_map/ppermute | solution.py:325
  278.0 22.9 %collective-permute-start.28 = (bf16[2,96,768]{2,1,0:T(8,128)(2,1)S(1)}, bf16[2,96,768]{2,1,0:T(8,128)(2,1)S(1)}, u32[]{:S(2)}, u32[]{:S(2)}) collective-permute-start(bf16[2,96,768]{2,1,0:T(8,128)(2,1)S(1)} %slice.423), channel_id=1, source_target_pairs={{0,2},{1,3},{2,0},{3,1},{4,6},{5,7},{6,4},{7,5},{8,10},{9,11},{10,... | collective-permute-start | bytes 884744 | tf_op jit(solution)/shard_map/ppermute | solution.py:325
  278.3 35.8 %collective-permute-start.23 = (bf16[2,96,768]{2,1,0:T(8,128)(2,1)S(1)}, bf16[2,96,768]{2,1,0:T(8,128)(2,1)S(1)}, u32[]{:S(2)}, u32[]{:S(2)}) collective-permute-start(bf16[2,96,768]{2,1,0:T(8,128)(2,1)S(1)} %slice.424), channel_id=1, source_target_pairs={{0,2},{1,3},{2,0},{3,1},{4,6},{5,7},{6,4},{7,5},{8,10},{9,11},{10,... | collective-permute-start | bytes 884744 | tf_op jit(solution)/shard_map/ppermute | solution.py:325
  301.0 13.3 %collective-permute-start.29 = (bf16[1,96,768]{2,1,0:T(8,128)(2,1)S(1)}, bf16[1,96,768]{2,1,0:T(8,128)(2,1)S(1)}, u32[]{:S(2)}, u32[]{:S(2)}) collective-permute-start(bf16[1,96,768]{2,1,0:T(8,128)(2,1)S(1)} %slice.426), channel_id=1, source_target_pairs={{0,1},{1,0},{2,3},{3,2},{4,5},{5,4},{6,7},{7,6},{8,9},{9,8},{10,11... | collective-permute-start | bytes 442376 | tf_op jit(solution)/shard_map/ppermute | solution.py:325
  301.3 18.7 %collective-permute-start.18 = (bf16[2,104,768]{2,1,0:T(8,128)(2,1)S(1)}, bf16[2,104,768]{2,1,0:T(8,128)(2,1)S(1)}, u32[]{:S(2)}, u32[]{:S(2)}) collective-permute-start(bf16[2,104,768]{2,1,0:T(8,128)(2,1)S(1)} %slice.422), channel_id=1, source_target_pairs={{0,2},{1,3},{2,0},{3,1},{4,6},{5,7},{6,4},{7,5},{8,10},{9,11},{10,... | collective-permute-start | bytes 958472 | tf_op jit(solution)/shard_map/ppermute | solution.py:325
  314.2 7.3 %collective-permute-start.24 = (bf16[1,96,768]{2,1,0:T(8,128)(2,1)S(1)}, bf16[1,96,768]{2,1,0:T(8,128)(2,1)S(1)}, u32[]{:S(2)}, u32[]{:S(2)}) collective-permute-start(bf16[1,96,768]{2,1,0:T(8,128)(2,1)S(1)} %slice.427), channel_id=1, source_target_pairs={{0,1},{1,0},{2,3},{3,2},{4,5},{5,4},{6,7},{7,6},{8,9},{9,8},{10,11... | collective-permute-start | bytes 442376 | tf_op jit(solution)/shard_map/ppermute | solution.py:325
  320.1 8.9 %copy-start.1 = (bf16[3,128,768]{2,1,0:T(8,128)(2,1)S(1)}, bf16[3,128,768]{2,1,0:T(8,128)(2,1)}, u32[]{:S(2)}) copy-start(bf16[3,128,768]{2,1,0:T(8,128)(2,1)} %param.15) | copy-start | bytes 1769476
  320.2 5.3 %collective-permute-start.19 = (bf16[1,104,768]{2,1,0:T(8,128)(2,1)S(1)}, bf16[1,104,768]{2,1,0:T(8,128)(2,1)S(1)}, u32[]{:S(2)}, u32[]{:S(2)}) collective-permute-start(bf16[1,104,768]{2,1,0:T(8,128)(2,1)S(1)} %slice.425), channel_id=1, source_target_pairs={{0,1},{1,0},{2,3},{3,2},{4,5},{5,4},{6,7},{7,6},{8,9},{9,8},{10,11... | collective-permute-start | bytes 479240 | tf_op jit(solution)/shard_map/ppermute | solution.py:325

commit v3 on v2

v3 whole, which is shorter than its diff:
```python
from functools import partial

import jax
import jax.numpy as jnp
from jax import lax
from jax.experimental import pallas as pl
from jax.experimental.pallas import tpu as pltpu
from jax.sharding import PartitionSpec as P

HD = 64
EPS = 1e-12
NEG = -1000000000.0
SCALE = float(HD) ** -0.5
AXES = ("dp", "tensor")
f32 = jnp.float32
bf16 = jnp.bfloat16
HI = lax.Precision.HIGHEST
BLK = 96
VMEM_LIMIT = 24 * 1024 * 1024
COST = 30_000_000


def nn(a, b):
    return lax.dot_general(a, b, (((1,), (0,)), ((), ())), preferred_element_type=f32)


def nt(a, b):
    return lax.dot_general(a, b, (((1,), (1,)), ((), ())), preferred_element_type=f32)


def tn(a, b):
    return lax.dot_general(a, b, (((0,), (0,)), ((), ())), preferred_element_type=f32)


def mean_last(v):
    return jnp.sum(v, axis=-1, keepdims=True) * (1.0 / v.shape[-1])


def normalize(values):
    center = values - mean_last(values)
    inverse = lax.rsqrt(mean_last(center * center) + EPS)
    return center * inverse, inverse


def normalize_back(scaled, normed, inverse):
    return inverse * (scaled - mean_last(scaled) - normed * mean_last(scaled * normed))


def col_sum(v):
    return jnp.sum(v, axis=0, keepdims=True)


def pack(qkv_ref, out_ref, down_ref, ob_ref, g1_ref, s1_ref, db_ref, g2_ref, s2_ref, qv_ref, ub_ref, first_ref, down_t_ref):
    rows, hc = qkv_ref.shape[1:]
    eye = (lax.broadcasted_iota(jnp.int32, (rows, rows), 0) == lax.broadcasted_iota(jnp.int32, (rows, rows), 1)).astype(bf16)
    for c in range(3):
        first_ref[:rows, c * hc : (c + 1) * hc] = qkv_ref[c]
    first_ref[:rows, 3 * hc :] = nt(eye, out_ref[...]).astype(bf16)
    down_t_ref[...] = nt(eye, down_ref[...]).astype(bf16)
    parts = [r[...].astype(f32) for r in (ob_ref, g1_ref, s1_ref, db_ref, g2_ref, s2_ref, qv_ref)]
    short = jnp.concatenate(parts, axis=0).astype(bf16)
    count, size = short.shape
    wide = first_ref.shape[1]

    def spread(values, at):
        lane = lax.broadcasted_iota(jnp.int32, (values.shape[1], wide), 1) - at
        return nn(values, (lax.rem(lane + values.shape[1] * wide, values.shape[1]) == lax.broadcasted_iota(jnp.int32, lane.shape, 0)).astype(bf16))

    lane = lax.broadcasted_iota(jnp.int32, (count, wide), 1)
    start = lax.broadcasted_iota(jnp.int32, (count, wide), 0) * size
    row = col_sum(jnp.where((lane >= start) & (lane < start + size), spread(short, 0), 0.0))
    total, long = count * size, ub_ref.shape[1]
    lane = lax.broadcasted_iota(jnp.int32, (1, wide), 1)
    row = jnp.where((lane >= total) & (lane < total + long), spread(ub_ref[...], total), row)
    extra = first_ref.shape[0] - rows
    here = lax.broadcasted_iota(jnp.int32, (extra, wide), 0)
    first_ref[rows:, :] = jnp.where(here == 0, row, 0.0).astype(bf16)


def stacked(values, hc):
    head = lax.broadcasted_iota(jnp.int32, (1, hc), 1) // HD
    return jnp.concatenate([values * (head == h).astype(f32).astype(bf16) for h in range(hc // HD)], axis=0)


def own_columns(blocks, hc):
    n_heads = hc // HD
    length = blocks.shape[0] // n_heads
    head = lax.broadcasted_iota(jnp.int32, (1, hc), 1) // HD
    out = blocks[:length]
    for h in range(1, n_heads):
        out = jnp.where(head == h, blocks[h * length : (h + 1) * length], out)
    return out


def sections(values, length):
    return [values[:, c : c + length] for c in range(0, values.shape[1], length)]


def attention_forward(x_ref, w0_ref, w1_ref, w2_ref, w3_ref, bq_ref, bv_ref, segc_ref, segr_ref, vec_ref,
                      qkv_ref, p_ref, o_ref, n1_ref, x1_ref, r1_ref, n1b_ref, n1t_ref, acc_ref):
    step = pl.program_id(0)
    hc = bq_ref.shape[-1]
    rows, length = segr_ref.shape
    x = x_ref[...]
    w = rows_of((w0_ref, w1_ref, w2_ref, w3_ref))
    qkv = nn(x, w[:, : 3 * hc])
    q = (qkv[:, :hc] + bq_ref[0]).astype(bf16) * bf16(SCALE)
    k = qkv[:, hc : 2 * hc].astype(bf16)
    v = (qkv[:, 2 * hc :] + bv_ref[0]).astype(bf16)
    qkv_ref[0, :, :hc] = q
    qkv_ref[0, :, hc : 2 * hc] = k
    qkv_ref[0, :, 2 * hc :] = v
    spans = [slice(g * length, (g + 1) * length) for g in range(rows)]
    scores = [nt(q[span], stacked(k[span], hc)) for span in spans]
    probs = []
    for g, span in enumerate(spans):
        same = segc_ref[span, :] == segr_ref[g : g + 1, :]
        parts = []
        for s in sections(scores[g], length):
            s = jnp.where(same, s, NEG)
            e = jnp.exp(s - jnp.max(s, axis=-1, keepdims=True))
            parts.append(e * (1.0 / jnp.sum(e, axis=-1, keepdims=True)))
        probs.append(jnp.concatenate(parts, axis=1))
    for g, span in enumerate(spans):
        p_ref[0, g] = probs[g]
        o_ref[0, span, :] = nn(probs[g].astype(bf16), stacked(v[span], hc)).astype(bf16)
    add = nt(o_ref[0], w[:, 3 * hc :])

    @pl.when(step == 0)
    def _():
        acc_ref[...] = add

    @pl.when(step > 0)
    def _():
        acc_ref[...] += add

    @pl.when(step == pl.num_programs(0) - 1)
    def _():
        a = acc_ref[...] + vec_ref[0:1, :] + x_ref[...].astype(f32)
        normed, inverse = normalize(a)
        n1 = normed * vec_ref[1:2, :] + vec_ref[2:3, :]
        n1_ref[...] = n1
        x1_ref[...] = normed
        r1_ref[...] = inverse
        low = n1.astype(bf16)
        n1b_ref[...] = low
        n1t_ref[...] = low.T


def rows_of(refs):
    return jnp.concatenate([r[...].reshape(r.shape[0] * r.shape[2], r.shape[3]) for r in refs], axis=0)


def up_forward(n_ref, w0_ref, w1_ref, w2_ref, w3_ref, b_ref, z_ref, d_ref):
    u = nn(n_ref[...], rows_of((w0_ref, w1_ref, w2_ref, w3_ref))) + b_ref[0]
    phi = 0.5 + 0.5 * lax.erf(u * (0.5**0.5))
    z_ref[0] = (u * phi).astype(bf16)
    d_ref[0] = phi + u * (jnp.exp(-0.5 * u * u) * 0.3989422804014327)


def down_forward(z_ref, w0_ref, w1_ref, w2_ref, w3_ref, n1_ref, vec_ref, segc_ref, segr_ref, pg_ref,
                 pooled_ref, db_ref, dbb_ref, dbt_ref, sums_ref, acc_ref):
    step = pl.program_id(0)
    add = nt(z_ref[0], rows_of((w0_ref, w1_ref, w2_ref, w3_ref)))

    @pl.when(step == 0)
    def _():
        acc_ref[...] = add

    @pl.when(step > 0)
    def _():
        acc_ref[...] += add

    @pl.when(step == pl.num_programs(0) - 1)
    def _():
        rows, length = segr_ref.shape
        segs = pg_ref.shape[1]
        b = acc_ref[...] + vec_ref[3:4, :] + n1_ref[...]
        x2, r2 = normalize(b)
        y = x2 * vec_ref[4:5, :] + vec_ref[5:6, :]
        grads = []
        for g in range(rows):
            span = slice(g * length, (g + 1) * length)
            ids = lax.broadcasted_iota(jnp.int32, (segs, length), 0)
            hot_t = (ids == segr_ref[g : g + 1, :]).astype(f32)
            idc = lax.broadcasted_iota(jnp.int32, (length, segs), 1)
            hot = (idc == segc_ref[span, :]).astype(f32)
            count = jnp.sum(hot_t, axis=1, keepdims=True)
            sums = lax.dot_general(hot_t, y[span, :], (((1,), (0,)), ((), ())),
                                   precision=HI, preferred_element_type=f32)
            pooled_ref[g] = sums / count
            grads.append(lax.dot_general(hot, pg_ref[g] / count, (((1,), (0,)), ((), ())),
                                         precision=HI, preferred_element_type=f32))
        dy = jnp.concatenate(grads, axis=0)
        db = normalize_back(dy * vec_ref[4:5, :], x2, r2)
        db_ref[...] = db
        low = db.astype(bf16)
        dbb_ref[...] = low
        dbt_ref[...] = low.T
        sums_ref[0:1, :] = col_sum(db)
        sums_ref[1:2, :] = col_sum(dy * x2)
        sums_ref[2:3, :] = col_sum(dy)


def put(grad, ref):
    ref[:, :, :BLK, :] = grad.astype(bf16).reshape(grad.shape[0] // BLK, 1, BLK, grad.shape[1])


def down_weight(dbt_ref, z_ref, out_ref):
    put(nn(dbt_ref[...], z_ref[0]), out_ref)


def up_backward(dbb_ref, w0_ref, w1_ref, w2_ref, w3_ref, d_ref, n1t_ref, keep_ref, send_ref, du_ref, bu_ref):
    width = dbb_ref.shape[1]
    du = (nn(dbb_ref[...], rows_of((w0_ref, w1_ref, w2_ref, w3_ref))) * d_ref[0]).astype(bf16)
    du_ref[0] = du
    bu_ref[0] = col_sum(du.astype(f32))
    grad = nn(n1t_ref[...], du)
    put(grad[width // 2 :], send_ref)
    put(grad[: width // 2], keep_ref)


def norm_backward(du_ref, w0_ref, w1_ref, w2_ref, w3_ref, db_ref, x1_ref, r1_ref, vec_ref, da_ref, dab_ref, dat_ref, sums_ref, acc_ref):
    step = pl.program_id(0)
    add = nt(du_ref[0], rows_of((w0_ref, w1_ref, w2_ref, w3_ref)))

    @pl.when(step == 0)
    def _():
        acc_ref[...] = add

    @pl.when(step > 0)
    def _():
        acc_ref[...] += add

    @pl.when(step == pl.num_programs(0) - 1)
    def _():
        dn1 = acc_ref[...].astype(bf16).astype(f32) + db_ref[...]
        da = normalize_back(dn1 * vec_ref[1:2, :], x1_ref[...], r1_ref[...])
        da_ref[...] = da
        low = da.astype(bf16)
        dab_ref[...] = low
        dat_ref[...] = low.T
        sums_ref[0:1, :] = col_sum(da)
        sums_ref[1:2, :] = col_sum(dn1 * x1_ref[...])
        sums_ref[2:3, :] = col_sum(dn1)


def attention_backward(dab_ref, w0_ref, w1_ref, w2_ref, w3_ref, qkv_ref, p_ref, dqkv_ref, bqv_ref):
    hc = bqv_ref.shape[-1]
    dab = dab_ref[...]
    w = rows_of([r.at[:, :, :, 3 * hc :] for r in (w0_ref, w1_ref, w2_ref, w3_ref)])
    do = nn(dab, w).astype(bf16)
    qkv = qkv_ref[0]
    rows, length = p_ref.shape[1], p_ref.shape[2]
    spans = [slice(g * length, (g + 1) * length) for g in range(rows)]
    q = [qkv[span, :hc] for span in spans]
    k = [stacked(qkv[span, hc : 2 * hc], hc) for span in spans]
    dps = [nt(do[span], stacked(qkv[span, 2 * hc :], hc)) for span in spans]
    dss = []
    for g in range(rows):
        parts = []
        for p, dp in zip(sections(p_ref[0, g], length), sections(dps[g], length)):
            pd = p * dp
            parts.append((pd - p * jnp.sum(pd, axis=-1, keepdims=True)).astype(bf16))
        dss.append(jnp.concatenate(parts, axis=1))
    for g, span in enumerate(spans):
        dqkv_ref[0, span, :hc] = (nn(dss[g], k[g]) * SCALE).astype(bf16)
        dqkv_ref[0, span, hc : 2 * hc] = own_columns(tn(dss[g], q[g]), hc).astype(bf16)
        dqkv_ref[0, span, 2 * hc :] = own_columns(tn(p_ref[0, g].astype(bf16), do[span]), hc).astype(bf16)
    dqkv = dqkv_ref[0]
    bqv_ref[0, 0:1, :] = col_sum(dqkv[:, :hc].astype(f32))
    bqv_ref[0, 1:2, :] = col_sum(dqkv[:, 2 * hc :].astype(f32))


def attention_weights(xt_ref, dat_ref, dqkv_ref, o_ref, vec_ref, keep_ref, send_ref):
    half = xt_ref.shape[0] // 2
    for n, ref in enumerate((keep_ref, send_ref)):
        count = ref.shape[0]
        ref[:, :, BLK:, :] = vec_ref[n * count : (n + 1) * count]
    grad = jnp.concatenate([nn(xt_ref[...], dqkv_ref[0]), nn(dat_ref[...], o_ref[0])], axis=1)
    put(grad[half:], send_ref)
    put(grad[:half], keep_ref)


def input_backward(dqkv_ref, w0_ref, w1_ref, w2_ref, w3_ref, da_ref, perm_ref, dx_ref, acc_ref):
    step = pl.program_id(0)
    cols = dqkv_ref.shape[-1]
    w = rows_of((w0_ref, w1_ref, w2_ref, w3_ref))
    add = nt(dqkv_ref[0], w[:, :cols])

    @pl.when(step == 0)
    def _():
        acc_ref[...] = add

    @pl.when(step > 0)
    def _():
        acc_ref[...] += add

    @pl.when(step == pl.num_programs(0) - 1)
    def _():
        dx = acc_ref[...] + da_ref[...]
        high = dx.astype(bf16)
        rest = dx - high.astype(f32)
        mid = rest.astype(bf16)
        low = (rest - mid.astype(f32)).astype(bf16)
        perm = perm_ref[...]
        dx_ref[...] = nt(high, perm) + nt(mid, perm) + nt(low, perm)


def whole(a):
    nd = len(a.shape)
    return pl.BlockSpec(a.shape, lambda s: (0,) * nd, pipeline_mode=pl.Buffered(1))


def lead(a):
    nd = len(a.shape)
    return pl.BlockSpec((1,) + a.shape[1:], lambda s: (s,) + (0,) * (nd - 1))


def weight(a):
    return pl.BlockSpec((a.shape[0], 1, BLK, a.shape[3]), lambda s: (0, s, 0, 0))


def half_spec(h):
    return pl.BlockSpec((h.shape[0], 1) + h.shape[2:], lambda s: (0, s, 0, 0))


def sds(shape, dtype):
    return jax.ShapeDtypeStruct(shape, dtype)


def far(shape, dtype):
    return pltpu.HBM(shape, dtype)


def call(body, n_t, micros, ins, outs, scratch=()):
    return pl.pallas_call(
        body,
        name=body.__name__,
        grid=(n_t,),
        in_specs=[s for _, s in ins],
        out_specs=[s for _, s in outs],
        out_shape=[a for a, _ in outs],
        scratch_shapes=list(scratch),
        compiler_params=pltpu.CompilerParams(
            dimension_semantics=("arbitrary",), vmem_limit_bytes=VMEM_LIMIT
        ),
        cost_estimate=pl.CostEstimate(flops=int(micros * COST), transcendentals=0, bytes_accessed=0),
    )(*[a for a, _ in ins])


def flips(n_dp, n_t):
    size = n_dp * n_t
    core = n_t
    x_bit, y_bit = 2 * core, 4 * core

    def table(bit_of):
        return [(i, i ^ bit_of(i)) for i in range(size)]

    return {
        "Z": [table(lambda i, d=d: d) for d in range(1, n_t)],
        "C": [table(lambda i: core)],
        "2": [table(lambda i: x_bit if i & core else y_bit)],
        "3": [table(lambda i: y_bit if i & core else x_bit)],
    }


def after(value, *done):
    return lax.optimization_barrier((value, *done))[0] if done else value


class Gather:
    def __init__(self, value, tables):
        self.held, self.tables = [value[None]], tables

    def stage(self, name, *done):
        got = [lax.ppermute(after(h, *done), AXES, t) for t in self.tables[name] for h in self.held]
        self.held = [jnp.concatenate(self.held + got)] if name in "Z2" else self.held + got
        return got

    def pieces(self, n_t):
        return [h.reshape(h.shape[0] // n_t, n_t, *h.shape[1:]) for h in self.held]


class Scatter:
    def __init__(self, keep, send, tables):
        self.keep, self.send, self.tables = keep, [send], tables

    def stage(self, name, parts, *done):
        got = [lax.ppermute(after(s, *done), AXES, t) for s, t in zip(self.send, self.tables[name], strict=True)]
        size = self.keep.shape[0] // parts

        def share(j):
            cut = slice(j * size, (j + 1) * size)
            return sum((g[cut].astype(f32) for g in got), self.keep[cut].astype(f32))

        self.send = [share(j).astype(bf16) for j in range(1, parts)]
        self.keep = share(0) if size <= 4 else share(0).astype(bf16)
        return got


def per_device(
    hidden_in, segment_ids, pooled_grad, qkv_weight, qv_bias, out_weight, out_bias,
    norm1_gain, norm1_shift, up_weight, up_bias, down_weight_in, down_bias, norm2_gain, norm2_shift,
):
    n_dp, n_t = lax.axis_size("dp"), lax.axis_size("tensor")
    at_dp, at_t = lax.axis_index("dp"), lax.axis_index("tensor")
    hc, fc = qkv_weight.shape[2], up_weight.shape[1]
    rows = qkv_weight.shape[1]
    D = rows * n_dp
    micro, tokens = hidden_in.shape[0], hidden_in.shape[1]
    seqs, L = segment_ids.shape[1], segment_ids.shape[2]
    G, T = micro * seqs, micro * tokens
    segs = pooled_grad.shape[2]
    n_i = D // BLK
    pairwise = (n_dp, n_t) == (8, 4) and 4 * hc == fc

    d_parts = [out_bias, norm1_gain, norm1_shift, down_bias, norm2_gain, norm2_shift]
    e_parts = [qv_bias[0], qv_bias[1], up_bias]
    dv = out_bias.shape[0]
    n_vec = sum(p.shape[0] for p in d_parts + e_parts)
    nd = len(d_parts) * dv

    if pairwise:
        tables = flips(n_dp, n_t)
        packed = (qkv_weight, out_weight, down_weight_in, *[p[None] for p in d_parts], qv_bias, up_bias[None])
        packed, down_t = pl.pallas_call(
            pack, name="pack", out_shape=[sds((BLK + 8, 4 * hc), bf16), sds((BLK, fc), bf16)]
        )(*packed)
        first = Gather(packed, tables)
        middle = Gather(up_weight, tables)
        last = Gather(down_t, tables)
        done = first.stage("Z")

        rel = jnp.arange(n_i)
        core = (at_dp & 1) ^ (rel >> 2)
        s3, s2 = (rel >> 1) & 1, rel & 1
        dy, dx = jnp.where(core == 0, s2, s3), jnp.where(core == 0, s3, s2)
        absolute = ((((at_dp >> 2) & 1) ^ dy) << 2) | ((((at_dp >> 1) & 1) ^ dx) << 1) | core
        i_p = jnp.broadcast_to(absolute[:, None], (n_i, n_t)).reshape(-1)
        t_p = jnp.broadcast_to((at_t ^ jnp.arange(n_t))[None], (n_i, n_t)).reshape(-1)
        to_d = jnp.broadcast_to(rel[:, None], (n_i, n_t)).reshape(-1) * n_t + t_p
        to_e = (((i_p * n_t) // n_i) ^ at_t) * n_i + (i_p * n_t + t_p) % n_i
        slot = jnp.arange(n_i * n_t)
        hot_d = (to_d[None, :] == slot[:, None]).astype(bf16)
        hot_e = (to_e[None, :] == slot[:, None]).astype(bf16)
        lane = jnp.arange(D)
        hot_i = (absolute[:, None] == rel[None, :])
        same_block = jnp.repeat(jnp.repeat(hot_i.T, BLK, axis=0), BLK, axis=1)
        perm = (same_block & ((lane[:, None] % BLK) == (lane[None, :] % BLK))).astype(bf16)
    else:
        perm = (jnp.arange(D)[:, None] == jnp.arange(D)[None, :]).astype(bf16)
    x = nn(hidden_in.reshape(T, D), perm).astype(bf16)
    x_t = lax.dot_general(perm, hidden_in.reshape(T, D), (((0,), (1,)), ((), ())), preferred_element_type=f32).astype(bf16)
    pg = jnp.einsum("gsd,de->gse", pooled_grad.reshape(G, segs, D), perm.astype(f32), precision=HI)
    seg_r = segment_ids.reshape(G, L)
    seg_c = segment_ids.reshape(T, 1)

    if pairwise:
        done = first.stage("2", x, x_t, pg, hot_d, hot_e) + middle.stage("Z", *done)
        done = first.stage("3", *done) + middle.stage("2", *done) + last.stage("Z", *done)
        first.stage("C", *done)
        done = middle.stage("3", *done) + last.stage("2", *done)
        w_qo = first.pieces(n_t)
        vecs = jnp.concatenate([w[:, :, BLK, : n_vec].reshape(-1, n_vec) for w in w_qo])
        d_all = nn(hot_d, vecs[:, :nd])
        e_all = nn(hot_e, vecs[:, nd:])
    else:
        heads_in = [qkv_weight[0], qkv_weight[1], qkv_weight[2], out_weight.T]
        main = jnp.concatenate([*heads_in, up_weight, down_weight_in.T], axis=1)
        vec = jnp.concatenate(d_parts + e_parts)
        full = lax.all_gather(lax.all_gather(main, "dp", axis=0, tiled=True), "tensor", axis=0)
        full = full.reshape(n_t, n_i, BLK, -1).transpose(1, 0, 2, 3)
        quarters = [full[j * n_i // 4 : (j + 1) * n_i // 4] for j in range(4)]
        w_qo = [w[..., : 4 * hc] for w in quarters]
        w_up = [w[..., 4 * hc : 4 * hc + fc] for w in quarters]
        w_down = [w[..., 4 * hc + fc :] for w in quarters]
        vecs = lax.all_gather(lax.all_gather(vec, "tensor"), "dp").reshape(n_dp * n_t, -1).astype(f32)
        d_all, e_all = vecs[:, :nd], vecs[:, nd:]

    vec_d = jnp.concatenate([d_all[:, j * dv : (j + 1) * dv].reshape(1, D) for j in range(6)])
    b_q = e_all[:, :dv].reshape(n_t, 1, hc)
    b_v = e_all[:, dv : 2 * dv].reshape(n_t, 1, hc)
    b_u = e_all[:, 2 * dv :].reshape(n_t, 1, fc)
    hl = hc // HD * L

    def leads(*arrays):
        return [(a, lead(a)) for a in arrays]

    def wholes(*arrays):
        return [(a, whole(a)) for a in arrays]

    def weights(*arrays):
        return [(a, weight(a)) for a in arrays]

    if pairwise:
        last.stage("3", *done)
        middle.stage("C", *done)
    qkv, prob, o, n1, x1, r1, n1b, n1_t = call(
        attention_forward, n_t, 10,
        wholes(x) + weights(*w_qo) + leads(b_q, b_v) + wholes(seg_c, seg_r, vec_d),
        leads(far((n_t, T, 3 * hc), bf16), far((n_t, G, L, hl), f32), far((n_t, T, hc), bf16))
        + wholes(sds((T, D), f32), far((T, D), f32), far((T, 1), f32), sds((T, D), bf16), far((D, T), bf16)),
        [pltpu.VMEM((T, D), f32)],
    )
    if pairwise:
        last.stage("C", n1b)
        w_up, w_down = middle.pieces(n_t), last.pieces(n_t)
    z, dgelu = call(
        up_forward, n_t, 4, wholes(n1b) + weights(*w_up) + leads(b_u),
        leads(sds((n_t, T, fc), bf16), sds((n_t, T, fc), f32)),
    )
    pooled, db, dbb, db_t, sums2 = call(
        down_forward, n_t, 5.5, leads(z) + weights(*w_down) + wholes(n1, vec_d, seg_c, seg_r, pg),
        wholes(sds((G, segs, D), f32), sds((T, D), f32), sds((T, D), bf16), sds((D, T), bf16), sds((3, D), f32)),
        [pltpu.VMEM((T, D), f32)],
    )
    half = sds((n_i // 2, n_t, BLK, fc), bf16)

    def halves(h):
        return [(h, half_spec(h))]

    def side_of(side):
        return [(db_t, pl.BlockSpec((D // 2, T), lambda s: (side, 0), pipeline_mode=pl.Buffered(1)))]

    down_send = call(down_weight, n_t, 2.2, side_of(1) + leads(z), halves(half))[0]
    down_keep = call(down_weight, n_t, 2.2, side_of(0) + leads(z), halves(half))[0]

    def flat(a):
        return a.reshape((-1,) + a.shape[2:])

    if pairwise:
        s_down = Scatter(flat(down_keep), flat(down_send), tables)
        s_down.stage("C", 2)
        dbb = after(dbb, down_keep)
    up_keep, up_send, du, g_bu = call(
        up_backward, n_t, 7, wholes(dbb) + weights(*w_down) + leads(dgelu) + wholes(n1_t),
        halves(half) * 2 + leads(sds((n_t, T, fc), bf16), sds((n_t, 1, fc), f32)),
    )
    if pairwise:
        s_up = Scatter(flat(up_keep), flat(up_send), tables)
        got3 = s_down.stage("3", 2)
        got_uc = s_up.stage("C", 2)
    da, dab, da_t, sums1 = call(
        norm_backward, n_t, 4, leads(du) + weights(*w_up) + wholes(db, x1, r1, vec_d),
        wholes(sds((T, D), f32), sds((T, D), bf16), sds((D, T), bf16), sds((3, D), f32)), [pltpu.VMEM((T, D), f32)],
    )
    if pairwise:
        dab = after(dab, *got_uc)
    dqkv, g_bqv = call(
        attention_backward, n_t, 8, wholes(dab) + weights(*w_qo) + leads(qkv, prob),
        leads(sds((n_t, T, 3 * hc), bf16), sds((n_t, 2, hc), f32)),
    )
    if pairwise:
        got_d2, got_u3 = s_down.stage("2", n_t), s_up.stage("3", 2)
        da_t = after(da_t, *got3, *got_u3)
    g_d = jnp.concatenate([v.reshape(n_dp * n_t, dv) for v in (*sums1, *sums2)], axis=1)
    g_e = jnp.concatenate(
        [g_bqv[:, 0].reshape(n_dp * n_t, dv), g_bqv[:, 1].reshape(n_dp * n_t, dv), g_bu.reshape(n_dp * n_t, -1)], axis=1
    )
    if pairwise:
        g_vec = jnp.concatenate([tn(hot_d, g_d.astype(bf16)), tn(hot_e, g_e.astype(bf16))], axis=1).astype(bf16)
        g_vec = jnp.pad(g_vec.reshape(n_i, n_t, 1, -1), ((0, 0), (0, 0), (0, 7), (0, 4 * hc - n_vec)))
    else:
        g_vec = jnp.zeros((n_i, n_t, 8, 4 * hc), bf16)
    half_qo = sds((n_i // 2, n_t, BLK + 8, 4 * hc), bf16)
    qo_keep, qo_send = call(
        attention_weights, n_t, 5,
        wholes(x_t, da_t) + leads(dqkv, o) + [(g_vec, pl.BlockSpec((n_i, 1, 8, 4 * hc), lambda s: (0, s, 0, 0)))],
        halves(half_qo) * 2,
    )
    if pairwise:
        s_qo = Scatter(flat(qo_keep), flat(qo_send), tables)
        s_qo.stage("C", 2)
        dqkv = after(dqkv, qo_send)
    dx = call(
        input_backward, n_t, 4, leads(dqkv) + weights(*w_qo) + wholes(da, perm), wholes(sds((T, D), f32)),
        [pltpu.VMEM((T, D), f32)],
    )[0]
    pooled = jnp.einsum("gse,de->gsd", pooled, perm.astype(f32), precision=HI)

    if pairwise:
        s_down.stage("Z", 1)
        s_up.stage("2", n_t)
        s_qo.stage("3", 2)
        s_up.stage("Z", 1)
        s_qo.stage("2", n_t, dx)
        s_qo.stage("Z", 1)
        g_down, g_up, g_qo = s_down.keep[0], s_up.keep[0], s_qo.keep[0]
        g_v = g_qo[BLK, : n_vec]
        g_qo = g_qo[:BLK]
    else:
        def joined(keep, send):
            g = jnp.concatenate([keep, send])[:, :, :BLK]
            return g.transpose(1, 0, 2, 3).reshape(n_t, D, -1)

        g_full = jnp.concatenate([joined(qo_keep, qo_send), joined(up_keep, up_send), joined(down_keep, down_send)], axis=2)
        mine = lax.psum_scatter(g_full, "tensor", scatter_dimension=0)
        mine = lax.psum_scatter(mine, "dp", scatter_dimension=0, tiled=True).astype(f32)
        g_qo, g_up, g_down = mine[:, : 4 * hc], mine[:, 4 * hc : 4 * hc + fc], mine[:, 4 * hc + fc :]
        g_v = lax.psum_scatter(jnp.concatenate([g_d, g_e], axis=1), AXES, scatter_dimension=0)
    vo = [g_v[j * dv : (j + 1) * dv] for j in range(8)]
    return (
        pooled.reshape(micro, seqs, segs, D),
        dx.reshape(micro, tokens, D),
        jnp.stack([g_qo[:, c * hc : (c + 1) * hc] for c in range(3)]),
        jnp.stack([vo[6], vo[7]]),
        g_qo[:, 3 * hc :].T,
        vo[0], vo[1], vo[2],
        g_up,
        g_v[8 * dv :],
        g_down.T,
        vo[3], vo[4], vo[5],
    )


def solution(mesh):
    both = P(AXES)
    row3 = P(None, AXES)
    return jax.shard_map(
        per_device,
        mesh=mesh,
        in_specs=(
            row3, row3, row3, P(None, "dp", "tensor"), row3, P("tensor", "dp"), both, both, both,
            P("dp", "tensor"), both, P("tensor", "dp"), both, both, both,
        ),
        out_specs=(
            row3, row3, P(None, "dp", "tensor"), row3, P("tensor", "dp"), both, both, both,
            P("dp", "tensor"), both, P("tensor", "dp"), both, both, both,
        ),
        check_vma=False,
    )
```

time: 330 us -> 252 us (0.76)
  waiting for transfers between devices: 146 us -> 76.2 us
  local copies, waits for them, and re-layouts: 59.7 us -> 40.8 us
  starting transfers between devices: 32.5 us -> 49.7 us
  Pallas kernels: 66 us -> 60.5 us
    ppermute x30 -> x39, waiting for transfers between devices: 146 us -> 76.2 us  [the longest x21 40.2 us: stage(): lax.ppermute(after(h, *done), AXES, t)]
    ppermute x30 -> x39, starting transfers between devices: 32.5 us -> 49.7 us  [the longest x18 25.7 us: stage(): lax.ppermute(after(s, *done), AXES, t)]
    concatenate x7 -> x6, local copies, waits for them, and re-layouts: 16.5 us -> 3.94 us  [the longest x3 3.9 us: stage(): jnp.concatenate(self.held + got)]
    convert_element_type x1 -> x10, other arithmetic: 0.42 us -> 9.58 us  [the longest x3 5.29 us: stage(): self.keep = share(0) if size <= 4 else share(0).astype(bf16)]
    add x15 -> x2, other arithmetic: 8.2 us -> 0.11 us  [the longest x1 0.1 us: share(): return sum((g[cut].astype(f32) for g in got), self.keep[cut].astype(f32))]
    pallas_call x6 -> x11, Pallas kernels: 66 us -> 60.5 us  [the longest x10 58.5 us: call(): pl.pallas_call(body, name=body.__name__, grid=(n_t,), in_specs=[s for _,...]
    gather x2 -> x0, other arithmetic: 4.77 us -> none  [per_device(): source = absolute[d_now // BLK] * BLK + d_now % BLK]
    unnamed x76 -> x108, local copies, waits for them, and re-layouts: 31.6 us -> 27.4 us
  transfers between devices with their start and end apart: 30 -> 39, of which waited for: 16 -> 17; matrix products, arithmetic and copies ran while one was open for 17% -> 15% of each run, Pallas kernels for 11% -> 18%
where the time goes in v3:
time: 252 us; the launch traced here: 251 us
  waiting for transfers between devices  76.2 us (30%)
  Pallas kernels  60.5 us (24%)
  starting transfers between devices  49.7 us (20%)
  local copies, waits for them, and re-layouts  40.8 us (16%)
  other arithmetic  17.2 us (7%)
  matrix products  5.22 us (2%)
    pallas_call x10, Pallas kernels, call(): pl.pallas_call(body, name=body.__name__, grid=(n_t,), in_specs=[s for _,...  58.5 us
    ppermute x21, waiting for transfers between devices, stage(): lax.ppermute(after(h, *done), AXES, t)  40.2 us
    ppermute x18, waiting for transfers between devices, stage(): lax.ppermute(after(s, *done), AXES, t)  35.9 us
    unnamed x108, local copies, waits for them, and re-layouts  27.4 us
    ppermute x18, starting transfers between devices, stage(): lax.ppermute(after(s, *done), AXES, t)  25.7 us
    ppermute x21, starting transfers between devices, stage(): lax.ppermute(after(h, *done), AXES, t)  24 us
    convert_element_type x3, other arithmetic, stage(): self.keep = share(0) if size <= 4 else share(0).astype(bf16)  5.29 us
  transfers between devices with their start and end apart: 39, of which 17 were waited for; matrix products, arithmetic and copies ran while one was open for 15% of the time, Pallas kernels for 18%

profile of v3, /device:TPU:0, one launch (start us, length us, event | category | flops | bytes accessed | tf_op | source)
XLA Modules:
  0.0 251.0 jit_solution(9066463019994900260)
XLA Ops:
  0.7 1.8 copy.53.down_ref
  2.4 2.0 pack.1
  4.5 3.0 %collective-permute-start = (bf16[1,104,768]{2,1,0:T(8,128)(2,1)}, bf16[1,104,768]{2,1,0:T(8,128)(2,1)S(1)}, u32[]{:S(2)}, u32[]{:S(2)}) collective-permute-start(bf16[1,104,768]{2,1,0:T(8,128)(2,1)} %bitcast.130), channel_id=1, source_target_pairs={{0,1},{1,0},{2,3},{3,2},{4,5},{5,4},{6,7},{7,6},{8,9},{9,8},{10,11... | collective-permute-start | bytes 479240 | tf_op jit(solution)/shard_map/ppermute | solution.py:377
  7.5 2.6 %collective-permute-start.1 = (bf16[1,104,768]{2,1,0:T(8,128)(2,1)}, bf16[1,104,768]{2,1,0:T(8,128)(2,1)S(1)}, u32[]{:S(2)}, u32[]{:S(2)}) collective-permute-start(bf16[1,104,768]{2,1,0:T(8,128)(2,1)} %bitcast.131), channel_id=1, source_target_pairs={{0,2},{1,3},{2,0},{3,1},{4,6},{5,7},{6,4},{7,5},{8,10},{9,11},{10,... | collective-permute-start | bytes 479240 | tf_op jit(solution)/shard_map/ppermute | solution.py:377
  12.9 1.3 collective-permute-done
  14.2 8.3 %collective-permute-done.1 = bf16[1,104,768]{2,1,0:T(8,128)(2,1)S(1)} collective-permute-done((bf16[1,104,768]{2,1,0:T(8,128)(2,1)}, bf16[1,104,768]{2,1,0:T(8,128)(2,1)S(1)}, u32[]{:S(2)}, u32[]{:S(2)}) %collective-permute-start.1) | collective-permute-done | bytes 159776 | tf_op jit(solution)/shard_map/ppermute | solution.py:377
  23.4 1.5 collective-permute-start.3
  25.0 2.6 %collective-permute-start.4 = (bf16[1,96,768]{2,1,0:T(8,128)(2,1)S(1)}, bf16[1,96,768]{2,1,0:T(8,128)(2,1)S(1)}, u32[]{:S(2)}, u32[]{:S(2)}) collective-permute-start(bf16[1,96,768]{2,1,0:T(8,128)(2,1)S(1)} %bitcast.134), channel_id=1, source_target_pairs={{0,1},{1,0},{2,3},{3,2},{4,5},{5,4},{6,7},{7,6},{8,9},{9,8},{10,11... | collective-permute-start | bytes 442376 | tf_op jit(solution)/shard_map/ppermute | solution.py:377
  27.6 1.1 collective-permute-start.5
  28.7 1.4 collective-permute-start.6
  30.2 3.9 %collective-permute-done.3 = bf16[4,104,768]{2,1,0:T(8,128)(2,1)S(1)} collective-permute-done((bf16[4,104,768]{2,1,0:T(8,128)(2,1)}, bf16[4,104,768]{2,1,0:T(8,128)(2,1)S(1)}, u32[]{:S(2)}, u32[]{:S(2)}) %collective-permute-start.3) | collective-permute-done | bytes 639008 | tf_op jit(solution)/shard_map/ppermute | solution.py:377
  34.1 6.2 %collective-permute-done.5 = bf16[1,96,768]{2,1,0:T(8,128)(2,1)S(1)} collective-permute-done((bf16[1,96,768]{2,1,0:T(8,128)(2,1)S(1)}, bf16[1,96,768]{2,1,0:T(8,128)(2,1)S(1)}, u32[]{:S(2)}, u32[]{:S(2)}) %collective-permute-start.5) | collective-permute-done | bytes 147488 | tf_op jit(solution)/shard_map/ppermute | solution.py:377
  42.4 1.6 collective-permute-start.8
  45.0 1.6 constant_dynamic-update-slice_fusion.12
  46.6 1.6 constant_dynamic-update-slice_fusion.11
  48.2 2.1 collective-permute-start.9
  50.3 1.1 collective-permute-start.10
  51.4 1.5 collective-permute-start.11
  53.6 5.5 %collective-permute-done.8 = bf16[4,96,768]{2,1,0:T(8,128)(2,1)} collective-permute-done((bf16[4,96,768]{2,1,0:T(8,128)(2,1)}, bf16[4,96,768]{2,1,0:T(8,128)(2,1)}, u32[]{:S(2)}, u32[]{:S(2)}) %collective-permute-start.8) | collective-permute-done | bytes 589856 | tf_op jit(solution)/shard_map/ppermute | solution.py:377
  59.0 1.9 constant_dynamic-update-slice_fusion.9
  61.0 2.0 collective-permute-done.10
  63.1 1.5 collective-permute-start.14
  65.1 1.1 copy.55.x_ref
  66.5 2.1 pad_maximum_fusion.2
  71.1 10.7 %collective-permute-done.15 = bf16[4,96,768]{2,1,0:T(8,128)(2,1)} collective-permute-done((bf16[4,96,768]{2,1,0:T(8,128)(2,1)}, bf16[4,96,768]{2,1,0:T(8,128)(2,1)}, u32[]{:S(2)}, u32[]{:S(2)}) %collective-permute-start.15) | collective-permute-done | bytes 589856 | tf_op jit(solution)/shard_map/ppermute | solution.py:377
  81.8 1.9 constant_dynamic-update-slice_fusion.14
  83.7 2.2 collective-permute-done.14
  85.9 1.5 collective-permute-start.18
  94.6 10.4 %attention_forward.1 = (bf16[4,384,576]{2,1,0:T(8,128)(2,1)}, f32[4,3,128,384]{3,2,1,0:T(8,128)}, bf16[4,384,192]{2,1,0:T(8,128)(2,1)}, f32[384,768]{1,0:T(8,128...) custom-call(bf16[384,768]{1,0:T(8,128)(2,1)S(1)} %copy-done.6, ...), custom_call_target="tpu_custom_call" | custom-call | flops 300000000 | tf_op jit(solution)/shard_map/attention_forward/pallas_call | solution.py:337
  108.6 5.4 %up_forward.1 = (bf16[4,384,768]{2,1,0:T(8,128)(2,1)S(1)}, f32[4,384,768]{2,1,0:T(8,128)S(1)}) custom-call(bf16[384,768]{1,0:T(8,128)(2,1)S(1)} %copy-done.17, bf16[2,4,96,768]{3,2,1,0:T(8,128)(2,1)} %bitcast.21.w0_ref, bf16[2,4,96,768]{3,2,1,0:T(8,128)(2,1)} %bitcast.22.w1_ref, bf16[2,4,96,768]{3,2,1,0:T(8,128)(2,1)} %bitcast.23.w2_ref, ...), custom_call_target="tpu_custom_call" | custom-call | flops 120000000 | tf_op jit(solution)/shard_map/up_forward/pallas_call | solution.py:337
  114.0 7.1 %down_forward.1 = (f32[3,8,768]{2,1,0:T(8,128)S(1)}, f32[384,768]{1,0:T(8,128)S(1)}, bf16[384,768]{1,0:T(8,128)(2,1)S(1)}, bf16[768,384]{1,0:T(8,128)(2,1)S(1)}, f32[3,768]{1,0:T(4,128)S(1)}) custom-call(bf16[4,384,768]{2,1,0:T(8,128)(2,1)S(1)} %get-tuple-element.76.z_ref, bf16[2,4,96,768]{3,2,1,0:T(8,128)(2,1)} %bitcast.25.w0_ref, ...), custom_call_target="tpu_custom_call" | custom-call | flops 165000000 | tf_op jit(solution)/shard_map/down_forward/pallas_call | solution.py:337
  121.1 2.0 down_weight.3
  123.2 2.0 down_weight.2
  125.2 7.1 %up_backward.1 = (bf16[4,4,96,768]{3,2,1,0:T(8,128)(2,1)S(1)}, bf16[4,4,96,768]{3,2,1,0:T(8,128)(2,1)S(1)}, bf16[4,384,768]{2,1,0:T(8,128)(2,1)S(1)}, f32[4,1,768]{2,1,0:T(1,128)S(1)}) custom-call(bf16[384,768]{1,0:T(8,128)(2,1)S(1)} %get-tuple-element.84.dbb_ref, bf16[2,4,96,768]{3,2,1,0:T(8,128)(2,1)} %bitcast.25.w0_ref, ...), custom_call_target="tpu_custom_call" | custom-call | flops 210000000 | tf_op jit(solution)/shard_map/up_backward/pallas_call | solution.py:337
  133.2 2.2 fusion.2
  137.0 2.3 fusion.3
  139.8 6.0 %norm_backward.1 = (f32[384,768]{1,0:T(8,128)S(1)}, bf16[384,768]{1,0:T(8,128)(2,1)S(1)}, bf16[768,384]{1,0:T(8,128)(2,1)S(1)}, f32[3,768]{1,0:T(4,128)S(1)}) custom-call(bf16[4,384,768]{2,1,0:T(8,128)(2,1)S(1)} %get-tuple-element.87.du_ref, bf16[2,4,96,768]{3,2,1,0:T(8,128)(2,1)} %bitcast.21.w0_ref, bf16[2,4,96,768]{3,2,1,0:T(8,128)(2,1)} %bitcast.22.w1_ref, ...), custom_call_target="tpu_custom_call" | custom-call | flops 120000000 | tf_op jit(solution)/shard_map/norm_backward/pallas_call | solution.py:337
  149.7 1.7 copy-done.5
  151.3 1.5 copy-done.7
  152.9 1.1 copy-done.15
  153.9 6.9 %attention_backward.1 = (bf16[4,384,576]{2,1,0:T(8,128)(2,1)S(1)}, f32[4,2,192]{2,1,0:T(2,128)S(1)}) custom-call(bf16[384,768]{1,0:T(8,128)(2,1)S(1)} %copy-done.15, bf16[2,4,104,768]{3,2,1,0:T(8,128)(2,1)S(1)} %bitcast.112, bf16[2,4,104,768]{3,2,1,0:T(8,128)(2,1)S(1)} %bitcast.116, bf16[2,4,104,768]{3,2,1,0:T(8,128)(2,1)} %bitcast.18.w2_ref, ...), custom_call_target="tpu_custom_call" | custom-call | flops 240000000 | tf_op jit(solution)/shard_map/attention_backward/pallas_call | solution.py:337
  160.9 1.3 copy-done.2
  162.8 1.8 collective-permute-done.24
  164.6 1.5 copy-done.3
  166.1 1.1 copy-done.13
  167.3 1.1 copy-done.19
  168.3 4.4 %attention_weights.1 = (bf16[4,4,104,768]{3,2,1,0:T(8,128)(2,1)S(1)}, bf16[4,4,104,768]{3,2,1,0:T(8,128)(2,1)S(1)}) custom-call(bf16[768,384]{1,0:T(8,128)(2,1)S(1)} %convolution_convert_fusion.xt_ref, bf16[768,384]{1,0:T(8,128)(2,1)S(1)} %copy-done.19, bf16[4,384,576]{2,1,0:T(8,128)(2,1)S(1)} %copy-done.3, bf16[4,384,192]{2,1,0:T(8,128)(2,1)S(1)} %copy-done.13, ...), custom_call_target="tpu_custom_call" | custom-call | flops 150000000 | tf_op jit(solution)/shard_map/attention_weights/pallas_call | solution.py:337
  173.0 4.6 %collective-permute-done.25 = bf16[16,104,768]{2,1,0:T(8,128)(2,1)S(1)} collective-permute-done((bf16[16,104,768]{2,1,0:T(8,128)(2,1)S(1)}, bf16[16,104,768]{2,1,0:T(8,128)(2,1)S(1)}, u32[]{:S(2)}, u32[]{:S(2)}) %collective-permute-start.25) | collective-permute-done | bytes 2555936 | tf_op jit(solution)/shard_map/ppermute | solution.py:390
  181.1 1.6 add_convert_fusion.1
  183.4 1.7 add_convert_fusion.2
  185.0 1.5 collective-permute-start.31
  186.6 2.0 fusion.11
  188.5 7.2 %input_backward.1 = f32[384,768]{1,0:T(8,128)} custom-call(bf16[4,384,576]{2,1,0:T(8,128)(2,1)S(1)} %copy-done.4, bf16[2,4,104,768]{3,2,1,0:T(8,128)(2,1)S(1)} %bitcast.113, bf16[2,4,104,768]{3,2,1,0:T(8,128)(2,1)S(1)} %bitcast.117, bf16[2,4,104,768]{3,2,1,0:T(8,128)(2,1)} %bitcast.18.w2_ref, bf16[2,4,104,768]{3,2,1,0:T(8,128)(2,1)} %bitcast.19.w3_ref, ...), custom_call_target="tpu_custom_call" | custom-call | flops 120000000 | tf_op jit(solution)/shard_map/input_backward/pallas_call | solution.py:337
  195.7 10.5 %collective-permute-done.26 = bf16[8,104,768]{2,1,0:T(8,128)(2,1)S(1)} collective-permute-done((bf16[8,104,768]{2,1,0:T(8,128)(2,1)S(1)}, bf16[8,104,768]{2,1,0:T(8,128)(2,1)S(1)}, u32[]{:S(2)}, u32[]{:S(2)}) %collective-permute-start.26) | collective-permute-done | bytes 1277984 | tf_op jit(solution)/shard_map/ppermute | solution.py:390
  206.6 2.5 collective-permute-start.36
  209.1 2.2 collective-permute-start.37
  211.3 1.4 collective-permute-start.38
  213.4 4.4 %collective-permute-done.36 = bf16[1,96,768]{2,1,0:T(8,128)(2,1)S(1)} collective-permute-done((bf16[1,96,768]{2,1,0:T(8,128)(2,1)S(1)}, bf16[1,96,768]{2,1,0:T(8,128)(2,1)S(1)}, u32[]{:S(2)}, u32[]{:S(2)}) %collective-permute-start.36) | collective-permute-done | bytes 147488 | tf_op jit(solution)/shard_map/ppermute | solution.py:390
  218.7 5.3 %collective-permute-done.37 = bf16[1,96,768]{2,1,0:T(8,128)(2,1)S(1)} collective-permute-done((bf16[1,96,768]{2,1,0:T(8,128)(2,1)S(1)}, bf16[1,96,768]{2,1,0:T(8,128)(2,1)S(1)}, u32[]{:S(2)}, u32[]{:S(2)}) %collective-permute-start.37) | collective-permute-done | bytes 147488 | tf_op jit(solution)/shard_map/ppermute | solution.py:390
  223.9 2.8 %collective-permute-start.34 = (bf16[1,96,768]{2,1,0:T(8,128)(2,1)S(1)}, bf16[1,96,768]{2,1,0:T(8,128)(2,1)S(1)}, u32[]{:S(2)}, u32[]{:S(2)}) collective-permute-start(bf16[1,96,768]{2,1,0:T(8,128)(2,1)S(1)} %get-tuple-element.187), channel_id=1, source_target_pairs={{0,3},{1,2},{2,1},{3,0},{4,7},{5,6},{6,5},{7,4},{8,11},{9,10},{10,... | collective-permute-start | bytes 442376 | tf_op jit(solution)/shard_map/ppermute | solution.py:390
  227.6 7.4 %collective-permute-start.28 = (bf16[1,104,768]{2,1,0:T(8,128)(2,1)S(1)}, bf16[1,104,768]{2,1,0:T(8,128)(2,1)S(1)}, u32[]{:S(2)}, u32[]{:S(2)}) collective-permute-start(bf16[1,104,768]{2,1,0:T(8,128)(2,1)S(1)} %get-tuple-element.180), channel_id=1, source_target_pairs={{0,1},{1,0},{2,3},{3,2},{4,5},{5,4},{6,7},{7,6},{8,9},{9,8},{10,11... | collective-permute-start | bytes 479240 | tf_op jit(solution)/shard_map/ppermute | solution.py:390
  235.1 2.0 collective-permute-start.29
  237.1 1.4 collective-permute-start.30
  240.1 7.4 %collective-permute-done.29 = bf16[1,104,768]{2,1,0:T(8,128)(2,1)S(1)} collective-permute-done((bf16[1,104,768]{2,1,0:T(8,128)(2,1)S(1)}, bf16[1,104,768]{2,1,0:T(8,128)(2,1)S(1)}, u32[]{:S(2)}, u32[]{:S(2)}) %collective-permute-start.29) | collective-permute-done | bytes 159776 | tf_op jit(solution)/shard_map/ppermute | solution.py:390
  (229 shorter events, 41.3 us)
Async XLA Ops:
  0.6 10.3 %copy-start = (bf16[3,128,768]{2,1,0:T(8,128)(2,1)S(1)}, bf16[3,128,768]{2,1,0:T(8,128)(2,1)}, u32[]{:S(2)}) copy-start(bf16[3,128,768]{2,1,0:T(8,128)(2,1)} %param.15) | copy-start | bytes 1769476
  4.5 9.7 %collective-permute-start = (bf16[1,104,768]{2,1,0:T(8,128)(2,1)}, bf16[1,104,768]{2,1,0:T(8,128)(2,1)S(1)}, u32[]{:S(2)}, u32[]{:S(2)}) collective-permute-start(bf16[1,104,768]{2,1,0:T(8,128)(2,1)} %bitcast.130), channel_id=1, source_target_pairs={{0,1},{1,0},{2,3},{3,2},{4,5},{5,4},{6,7},{7,6},{8,9},{9,8},{10,11... | collective-permute-start | bytes 479240 | tf_op jit(solution)/shard_map/ppermute | solution.py:377
  7.5 15.0 %collective-permute-start.1 = (bf16[1,104,768]{2,1,0:T(8,128)(2,1)}, bf16[1,104,768]{2,1,0:T(8,128)(2,1)S(1)}, u32[]{:S(2)}, u32[]{:S(2)}) collective-permute-start(bf16[1,104,768]{2,1,0:T(8,128)(2,1)} %bitcast.131), channel_id=1, source_target_pairs={{0,2},{1,3},{2,0},{3,1},{4,6},{5,7},{6,4},{7,5},{8,10},{9,11},{10,... | collective-permute-start | bytes 479240 | tf_op jit(solution)/shard_map/ppermute | solution.py:377
  10.1 12.4 %collective-permute-start.2 = (bf16[1,104,768]{2,1,0:T(8,128)(2,1)}, bf16[1,104,768]{2,1,0:T(8,128)(2,1)S(1)}, u32[]{:S(2)}, u32[]{:S(2)}) collective-permute-start(bf16[1,104,768]{2,1,0:T(8,128)(2,1)} %bitcast.132), channel_id=1, source_target_pairs={{0,3},{1,2},{2,1},{3,0},{4,7},{5,6},{6,5},{7,4},{8,11},{9,10},{10,... | collective-permute-start | bytes 479240 | tf_op jit(solution)/shard_map/ppermute | solution.py:377
  11.0 11.5 %copy-start.24 = (bf16[104,768]{1,0:T(8,128)(2,1)S(1)}, bf16[104,768]{1,0:T(8,128)(2,1)}, u32[]{:S(2)}) copy-start(bf16[104,768]{1,0:T(8,128)(2,1)} %get-tuple-element.62) | copy-start | bytes 479236
  11.8 13.2 %copy-start.25 = (bf16[96,768]{1,0:T(8,128)(2,1)S(1)}, bf16[96,768]{1,0:T(8,128)(2,1)}, u32[]{:S(2)}) copy-start(bf16[96,768]{1,0:T(8,128)(2,1)} %param.24) | copy-start | bytes 442372
  23.4 10.6 %collective-permute-start.3 = (bf16[4,104,768]{2,1,0:T(8,128)(2,1)}, bf16[4,104,768]{2,1,0:T(8,128)(2,1)S(1)}, u32[]{:S(2)}, u32[]{:S(2)}) collective-permute-start(bf16[4,104,768]{2,1,0:T(8,128)(2,1)} %pad_maximum_fusion), channel_id=1, source_target_pairs={{0,16},{1,17},{2,18},{3,19},{4,12},{5,13},{6,14},{7,15},{8,24},{9,... | collective-permute-start | bytes 1916936 | tf_op jit(solution)/shard_map/ppermute | solution.py:377
  25.0 15.9 %copy-start.26 = (bf16[96,768]{1,0:T(8,128)(2,1)S(1)}, bf16[96,768]{1,0:T(8,128)(2,1)}, u32[]{:S(2)}) copy-start(bf16[96,768]{1,0:T(8,128)(2,1)} %param.24) | copy-start | bytes 442372
  25.0 9.1 %collective-permute-start.4 = (bf16[1,96,768]{2,1,0:T(8,128)(2,1)S(1)}, bf16[1,96,768]{2,1,0:T(8,128)(2,1)S(1)}, u32[]{:S(2)}, u32[]{:S(2)}) collective-permute-start(bf16[1,96,768]{2,1,0:T(8,128)(2,1)S(1)} %bitcast.134), channel_id=1, source_target_pairs={{0,1},{1,0},{2,3},{3,2},{4,5},{5,4},{6,7},{7,6},{8,9},{9,8},{10,11... | collective-permute-start | bytes 442376 | tf_op jit(solution)/shard_map/ppermute | solution.py:377
  27.6 12.7 %collective-permute-start.5 = (bf16[1,96,768]{2,1,0:T(8,128)(2,1)S(1)}, bf16[1,96,768]{2,1,0:T(8,128)(2,1)S(1)}, u32[]{:S(2)}, u32[]{:S(2)}) collective-permute-start(bf16[1,96,768]{2,1,0:T(8,128)(2,1)S(1)} %bitcast.135), channel_id=1, source_target_pairs={{0,2},{1,3},{2,0},{3,1},{4,6},{5,7},{6,4},{7,5},{8,10},{9,11},{10,... | collective-permute-start | bytes 442376 | tf_op jit(solution)/shard_map/ppermute | solution.py:377
  28.7 11.7 %collective-permute-start.6 = (bf16[1,96,768]{2,1,0:T(8,128)(2,1)S(1)}, bf16[1,96,768]{2,1,0:T(8,128)(2,1)S(1)}, u32[]{:S(2)}, u32[]{:S(2)}) collective-permute-start(bf16[1,96,768]{2,1,0:T(8,128)(2,1)S(1)} %bitcast.136), channel_id=1, source_target_pairs={{0,3},{1,2},{2,1},{3,0},{4,7},{5,6},{6,5},{7,4},{8,11},{9,10},{10,... | collective-permute-start | bytes 442376 | tf_op jit(solution)/shard_map/ppermute | solution.py:377
  30.2 14.2 %copy-start.27 = (bf16[96,768]{1,0:T(8,128)(2,1)S(1)}, bf16[96,768]{1,0:T(8,128)(2,1)}, u32[]{:S(2)}) copy-start(bf16[96,768]{1,0:T(8,128)(2,1)} %get-tuple-element.67) | copy-start | bytes 442372
  34.1 8.3 %copy-start.34 = (bf16[1,96,768]{2,1,0:T(8,128)(2,1)}, bf16[1,96,768]{2,1,0:T(8,128)(2,1)S(1)}, u32[]{:S(2)}) copy-start(bf16[1,96,768]{2,1,0:T(8,128)(2,1)S(1)} %collective-permute-done.4) | copy-start | bytes 442372
  40.4 3.6 %copy-start.35 = (bf16[1,96,768]{2,1,0:T(8,128)(2,1)}, bf16[1,96,768]{2,1,0:T(8,128)(2,1)S(1)}, u32[]{:S(2)}) copy-start(bf16[1,96,768]{2,1,0:T(8,128)(2,1)S(1)} %collective-permute-done.5) | copy-start | bytes 442372
  40.4 22.7 %collective-permute-start.7 = (bf16[8,104,768]{2,1,0:T(8,128)(2,1)S(1)}, bf16[8,104,768]{2,1,0:T(8,128)(2,1)S(1)}, u32[]{:S(2)}, u32[]{:S(2)}) collective-permute-start(bf16[8,104,768]{2,1,0:T(8,128)(2,1)S(1)} %constant_dynamic-update-slice_fusion), channel_id=1, source_target_pairs={{0,8},{1,9},{2,10},{3,11},{4,20},{5,21},{6,22},{7,23},{8,0},{9,1},... | collective-permute-start | bytes 3833864 | tf_op jit(solution)/shard_map/ppermute | solution.py:377
  42.4 16.6 %collective-permute-start.8 = (bf16[4,96,768]{2,1,0:T(8,128)(2,1)}, bf16[4,96,768]{2,1,0:T(8,128)(2,1)}, u32[]{:S(2)}, u32[]{:S(2)}) collective-permute-start(bf16[4,96,768]{2,1,0:T(8,128)(2,1)} %pad_maximum_fusion.1), channel_id=1, source_target_pairs={{0,16},{1,17},{2,18},{3,19},{4,12},{5,13},{6,14},{7,15},{8,24},{9,... | collective-permute-start | bytes 1769480 | tf_op jit(solution)/shard_map/ppermute | solution.py:377
  48.2 12.8 %collective-permute-start.9 = (bf16[1,96,768]{2,1,0:T(8,128)(2,1)S(1)}, bf16[1,96,768]{2,1,0:T(8,128)(2,1)S(1)}, u32[]{:S(2)}, u32[]{:S(2)}) collective-permute-start(bf16[1,96,768]{2,1,0:T(8,128)(2,1)S(1)} %bitcast.139), channel_id=1, source_target_pairs={{0,1},{1,0},{2,3},{3,2},{4,5},{5,4},{6,7},{7,6},{8,9},{9,8},{10,11... | collective-permute-start | bytes 442376 | tf_op jit(solution)/shard_map/ppermute | solution.py:377
  50.3 12.7 %collective-permute-start.10 = (bf16[1,96,768]{2,1,0:T(8,128)(2,1)S(1)}, bf16[1,96,768]{2,1,0:T(8,128)(2,1)S(1)}, u32[]{:S(2)}, u32[]{:S(2)}) collective-permute-start(bf16[1,96,768]{2,1,0:T(8,128)(2,1)S(1)} %bitcast.140), channel_id=1, source_target_pairs={{0,2},{1,3},{2,0},{3,1},{4,6},{5,7},{6,4},{7,5},{8,10},{9,11},{10,... | collective-permute-start | bytes 442376 | tf_op jit(solution)/shard_map/ppermute | solution.py:377
  51.4 11.6 %collective-permute-start.11 = (bf16[1,96,768]{2,1,0:T(8,128)(2,1)S(1)}, bf16[1,96,768]{2,1,0:T(8,128)(2,1)S(1)}, u32[]{:S(2)}, u32[]{:S(2)}) collective-permute-start(bf16[1,96,768]{2,1,0:T(8,128)(2,1)S(1)} %bitcast.141), channel_id=1, source_target_pairs={{0,3},{1,2},{2,1},{3,0},{4,7},{5,6},{6,5},{7,4},{8,11},{9,10},{10,... | collective-permute-start | bytes 442376 | tf_op jit(solution)/shard_map/ppermute | solution.py:377
  53.5 12.7 %copy-start.40 = (s32[3,1,128]{2,1,0:T(1,128)S(1)}, s32[3,1,128]{2,1,0:T(1,128)}, u32[]{:S(2)}) copy-start(s32[3,1,128]{2,1,0:T(1,128)} %param.16) | copy-start | bytes 4612
  61.0 3.6 %copy-start.28 = (bf16[1,96,768]{2,1,0:T(8,128)(2,1)}, bf16[1,96,768]{2,1,0:T(8,128)(2,1)S(1)}, u32[]{:S(2)}) copy-start(bf16[1,96,768]{2,1,0:T(8,128)(2,1)S(1)} %collective-permute-done.9) | copy-start | bytes 442372
  63.0 2.1 copy-start.32
  63.1 22.8 %collective-permute-start.14 = (bf16[8,96,768]{2,1,0:T(8,128)(2,1)}, bf16[8,96,768]{2,1,0:T(8,128)(2,1)}, u32[]{:S(2)}, u32[]{:S(2)}) collective-permute-start(bf16[8,96,768]{2,1,0:T(8,128)(2,1)} %constant_dynamic-update-slice_fusion.9), channel_id=1, source_target_pairs={{0,8},{1,9},{2,10},{3,11},{4,20},{5,21},{6,22},{7,23},{8,0},{9,1},... | collective-permute-start | bytes 3538952 | tf_op jit(solution)/shard_map/ppermute | solution.py:377
  64.6 23.4 %collective-permute-start.12 = (bf16[8,104,768]{2,1,0:T(8,128)(2,1)S(1)}, bf16[8,104,768]{2,1,0:T(8,128)(2,1)}, u32[]{:S(2)}, u32[]{:S(2)}) collective-permute-start(bf16[8,104,768]{2,1,0:T(8,128)(2,1)S(1)} %constant_dynamic-update-slice_fusion), channel_id=1, source_target_pairs={{0,4},{1,5},{2,6},{3,7},{4,0},{5,1},{6,2},{7,3},{8,12},{9,13},{10,... | collective-permute-start | bytes 3833864 | tf_op jit(solution)/shard_map/ppermute | solution.py:377
  64.6 24.2 %collective-permute-start.13 = (bf16[8,104,768]{2,1,0:T(8,128)(2,1)S(1)}, bf16[8,104,768]{2,1,0:T(8,128)(2,1)}, u32[]{:S(2)}, u32[]{:S(2)}) collective-permute-start(bf16[8,104,768]{2,1,0:T(8,128)(2,1)S(1)} %collective-permute-done.7), channel_id=1, source_target_pairs={{0,4},{1,5},{2,6},{3,7},{4,0},{5,1},{6,2},{7,3},{8,12},{9,13},{10,... | collective-permute-start | bytes 3833864 | tf_op jit(solution)/shard_map/ppermute | solution.py:377
  65.1 24.6 %copy-start.41 = (s32[32]{0:T(128)}, s32[32]{0:T(128)S(1)}, u32[]{:S(2)}) copy-start(s32[32]{0:T(128)S(1)} %get-tuple-element.209) | copy-start | bytes 388
  65.1 27.2 %copy-start.43 = (s32[32]{0:T(128)}, s32[32]{0:T(128)S(1)}, u32[]{:S(2)}) copy-start(s32[32]{0:T(128)S(1)} %get-tuple-element.210) | copy-start | bytes 388
  66.4 2.6 %copy-start.29 = (bf16[1,96,768]{2,1,0:T(8,128)(2,1)S(1)}, bf16[1,96,768]{2,1,0:T(8,128)(2,1)}, u32[]{:S(2)}) copy-start(bf16[1,96,768]{2,1,0:T(8,128)(2,1)} %copy-done.28) | copy-start | bytes 442372
  66.4 3.2 %copy-start.31 = (bf16[1,96,768]{2,1,0:T(8,128)(2,1)S(1)}, bf16[1,96,768]{2,1,0:T(8,128)(2,1)}, u32[]{:S(2)}) copy-start(bf16[1,96,768]{2,1,0:T(8,128)(2,1)} %copy-done.30) | copy-start | bytes 442372
  66.4 3.9 %copy-start.33 = (bf16[1,96,768]{2,1,0:T(8,128)(2,1)S(1)}, bf16[1,96,768]{2,1,0:T(8,128)(2,1)}, u32[]{:S(2)}) copy-start(bf16[1,96,768]{2,1,0:T(8,128)(2,1)} %copy-done.32) | copy-start | bytes 442372
  68.5 13.3 %collective-permute-start.15 = (bf16[4,96,768]{2,1,0:T(8,128)(2,1)}, bf16[4,96,768]{2,1,0:T(8,128)(2,1)}, u32[]{:S(2)}, u32[]{:S(2)}) collective-permute-start(bf16[4,96,768]{2,1,0:T(8,128)(2,1)} %pad_maximum_fusion.2), channel_id=1, source_target_pairs={{0,16},{1,17},{2,18},{3,19},{4,12},{5,13},{6,14},{7,15},{8,24},{9,... | collective-permute-start | bytes 1769480 | tf_op jit(solution)/shard_map/ppermute | solution.py:377
  85.9 20.9 %collective-permute-start.18 = (bf16[8,96,768]{2,1,0:T(8,128)(2,1)}, bf16[8,96,768]{2,1,0:T(8,128)(2,1)}, u32[]{:S(2)}, u32[]{:S(2)}) collective-permute-start(bf16[8,96,768]{2,1,0:T(8,128)(2,1)} %constant_dynamic-update-slice_fusion.14), channel_id=1, source_target_pairs={{0,8},{1,9},{2,10},{3,11},{4,20},{5,21},{6,22},{7,23},{8,0},{9,1},... | collective-permute-start | bytes 3538952 | tf_op jit(solution)/shard_map/ppermute | solution.py:377
  87.4 20.1 %collective-permute-start.17 = (bf16[8,96,768]{2,1,0:T(8,128)(2,1)}, bf16[8,96,768]{2,1,0:T(8,128)(2,1)}, u32[]{:S(2)}, u32[]{:S(2)}) collective-permute-start(bf16[8,96,768]{2,1,0:T(8,128)(2,1)} %collective-permute-done.14), channel_id=1, source_target_pairs={{0,4},{1,5},{2,6},{3,7},{4,0},{5,1},{6,2},{7,3},{8,12},{9,13},{10,... | collective-permute-start | bytes 3538952 | tf_op jit(solution)/shard_map/ppermute | solution.py:377
  87.4 20.1 %collective-permute-start.16 = (bf16[8,96,768]{2,1,0:T(8,128)(2,1)}, bf16[8,96,768]{2,1,0:T(8,128)(2,1)}, u32[]{:S(2)}, u32[]{:S(2)}) collective-permute-start(bf16[8,96,768]{2,1,0:T(8,128)(2,1)} %constant_dynamic-update-slice_fusion.9), channel_id=1, source_target_pairs={{0,4},{1,5},{2,6},{3,7},{4,0},{5,1},{6,2},{7,3},{8,12},{9,13},{10,... | collective-permute-start | bytes 3538952 | tf_op jit(solution)/shard_map/ppermute | solution.py:377
  106.8 7.1 %collective-permute-start.19 = (bf16[8,96,768]{2,1,0:T(8,128)(2,1)}, bf16[8,96,768]{2,1,0:T(8,128)(2,1)}, u32[]{:S(2)}, u32[]{:S(2)}) collective-permute-start(bf16[8,96,768]{2,1,0:T(8,128)(2,1)} %constant_dynamic-update-slice_fusion.14), channel_id=1, source_target_pairs={{0,4},{1,5},{2,6},{3,7},{4,0},{5,1},{6,2},{7,3},{8,12},{9,13},{10,... | collective-permute-start | bytes 3538952 | tf_op jit(solution)/shard_map/ppermute | solution.py:377
  106.8 7.1 %collective-permute-start.20 = (bf16[8,96,768]{2,1,0:T(8,128)(2,1)}, bf16[8,96,768]{2,1,0:T(8,128)(2,1)}, u32[]{:S(2)}, u32[]{:S(2)}) collective-permute-start(bf16[8,96,768]{2,1,0:T(8,128)(2,1)} %collective-permute-done.18), channel_id=1, source_target_pairs={{0,4},{1,5},{2,6},{3,7},{4,0},{5,1},{6,2},{7,3},{8,12},{9,13},{10,... | collective-permute-start | bytes 3538952 | tf_op jit(solution)/shard_map/ppermute | solution.py:377
  108.6 5.4 %copy-start.9 = (f32[384,768]{1,0:T(8,128)S(1)}, f32[384,768]{1,0:T(8,128)}, u32[]{:S(2)}) copy-start(f32[384,768]{1,0:T(8,128)} %copy-done.8) | copy-start | bytes 3538948
  123.1 2.1 copy-start.20
  123.1 10.0 %collective-permute-start.22 = (bf16[16,96,768]{2,1,0:T(8,128)(2,1)S(1)}, bf16[16,96,768]{2,1,0:T(8,128)(2,1)S(1)}, u32[]{:S(2)}, u32[]{:S(2)}) collective-permute-start(bf16[16,96,768]{2,1,0:T(8,128)(2,1)S(1)} %bitcast.119), channel_id=1, source_target_pairs={{0,4},{1,5},{2,6},{3,7},{4,0},{5,1},{6,2},{7,3},{8,12},{9,13},{10,... | collective-permute-start | bytes 7077896 | tf_op jit(solution)/shard_map/ppermute | solution.py:390
  132.3 4.7 %collective-permute-start.21 = (bf16[16,96,768]{2,1,0:T(8,128)(2,1)S(1)}, bf16[16,96,768]{2,1,0:T(8,128)(2,1)S(1)}, u32[]{:S(2)}, u32[]{:S(2)}) collective-permute-start(bf16[16,96,768]{2,1,0:T(8,128)(2,1)S(1)} %bitcast.123), channel_id=1, source_target_pairs={{0,4},{1,5},{2,6},{3,7},{4,0},{5,1},{6,2},{7,3},{8,12},{9,13},{10,... | collective-permute-start | bytes 7077896 | tf_op jit(solution)/shard_map/ppermute | solution.py:390
  135.4 27.3 %collective-permute-start.23 = (bf16[8,96,768]{2,1,0:T(8,128)(2,1)}, bf16[8,96,768]{2,1,0:T(8,128)(2,1)}, u32[]{:S(2)}, u32[]{:S(2)}) collective-permute-start(bf16[8,96,768]{2,1,0:T(8,128)(2,1)} %get-tuple-element.171), channel_id=1, source_target_pairs={{0,8},{1,9},{2,10},{3,11},{4,20},{5,21},{6,22},{7,23},{8,0},{9,1},... | collective-permute-start | bytes 3538952 | tf_op jit(solution)/shard_map/ppermute | solution.py:390
  137.0 2.8 %copy-start.12 = (f32[384,768]{1,0:T(8,128)S(1)}, f32[384,768]{1,0:T(8,128)}, u32[]{:S(2)}) copy-start(f32[384,768]{1,0:T(8,128)} %get-tuple-element.89.x1_ref) | copy-start | bytes 3538948
  137.0 2.8 %copy-start.21 = (f32[384,1]{1,0:T(8,128)S(1)}, f32[384,1]{1,0:T(8,128)}, u32[]{:S(2)}) copy-start(f32[384,1]{1,0:T(8,128)} %get-tuple-element.90.r1_ref) | copy-start | bytes 4612
  139.3 25.3 %collective-permute-start.24 = (bf16[8,96,768]{2,1,0:T(8,128)(2,1)}, bf16[8,96,768]{2,1,0:T(8,128)(2,1)}, u32[]{:S(2)}, u32[]{:S(2)}) collective-permute-start(bf16[8,96,768]{2,1,0:T(8,128)(2,1)} %get-tuple-element.177), channel_id=1, source_target_pairs={{0,8},{1,9},{2,10},{3,11},{4,20},{5,21},{6,22},{7,23},{8,0},{9,1},... | collective-permute-start | bytes 3538952 | tf_op jit(solution)/shard_map/ppermute | solution.py:390
  139.8 9.5 %copy-start.42 = (s32[32]{0:T(128)S(1)}, s32[32]{0:T(128)}, u32[]{:S(2)}) copy-start(s32[32]{0:T(128)} %copy-done.41) | copy-start | bytes 388
  153.9 8.4 %copy-start.44 = (s32[32]{0:T(128)S(1)}, s32[32]{0:T(128)}, u32[]{:S(2)}) copy-start(s32[32]{0:T(128)} %copy-done.43) | copy-start | bytes 388
  172.7 4.9 %collective-permute-start.25 = (bf16[16,104,768]{2,1,0:T(8,128)(2,1)S(1)}, bf16[16,104,768]{2,1,0:T(8,128)(2,1)S(1)}, u32[]{:S(2)}, u32[]{:S(2)}) collective-permute-start(bf16[16,104,768]{2,1,0:T(8,128)(2,1)S(1)} %bitcast.122), channel_id=1, source_target_pairs={{0,4},{1,5},{2,6},{3,7},{4,0},{5,1},{6,2},{7,3},{8,12},{9,13},{10,... | collective-permute-start | bytes 7667720 | tf_op jit(solution)/shard_map/ppermute | solution.py:390
  178.4 27.8 %collective-permute-start.26 = (bf16[8,104,768]{2,1,0:T(8,128)(2,1)S(1)}, bf16[8,104,768]{2,1,0:T(8,128)(2,1)S(1)}, u32[]{:S(2)}, u32[]{:S(2)}) collective-permute-start(bf16[8,104,768]{2,1,0:T(8,128)(2,1)S(1)} %get-tuple-element.165), channel_id=1, source_target_pairs={{0,8},{1,9},{2,10},{3,11},{4,20},{5,21},{6,22},{7,23},{8,0},{9,1},... | collective-permute-start | bytes 3833864 | tf_op jit(solution)/shard_map/ppermute | solution.py:390
  181.1 2.2 copy-start.23
  182.7 23.8 %collective-permute-start.35 = (bf16[4,96,768]{2,1,0:T(8,128)(2,1)S(1)}, bf16[4,96,768]{2,1,0:T(8,128)(2,1)S(1)}, u32[]{:S(2)}, u32[]{:S(2)}) collective-permute-start(bf16[4,96,768]{2,1,0:T(8,128)(2,1)S(1)} %get-tuple-element.168), channel_id=1, source_target_pairs={{0,16},{1,17},{2,18},{3,19},{4,12},{5,13},{6,14},{7,15},{8,24},{9,... | collective-permute-start | bytes 1769480 | tf_op jit(solution)/shard_map/ppermute | solution.py:390
  183.4 5.2 %copy-start.4 = (bf16[4,384,576]{2,1,0:T(8,128)(2,1)S(1)}, bf16[4,384,576]{2,1,0:T(8,128)(2,1)}, u32[]{:S(2)}) copy-start(bf16[4,384,576]{2,1,0:T(8,128)(2,1)} %copy-done.2) | copy-start | bytes 5308420
  185.0 3.5 %copy-start.11 = (f32[384,768]{1,0:T(8,128)S(1)}, f32[384,768]{1,0:T(8,128)}, u32[]{:S(2)}) copy-start(f32[384,768]{1,0:T(8,128)} %copy-done.10) | copy-start | bytes 3538948
  185.0 27.7 %collective-permute-start.31 = (bf16[4,96,768]{2,1,0:T(8,128)(2,1)S(1)}, bf16[4,96,768]{2,1,0:T(8,128)(2,1)S(1)}, u32[]{:S(2)}, u32[]{:S(2)}) collective-permute-start(bf16[4,96,768]{2,1,0:T(8,128)(2,1)S(1)} %get-tuple-element.174), channel_id=1, source_target_pairs={{0,16},{1,17},{2,18},{3,19},{4,12},{5,13},{6,14},{7,15},{8,24},{9,... | collective-permute-start | bytes 1769480 | tf_op jit(solution)/shard_map/ppermute | solution.py:390
  206.5 21.1 %collective-permute-start.27 = (bf16[4,104,768]{2,1,0:T(8,128)(2,1)S(1)}, bf16[4,104,768]{2,1,0:T(8,128)(2,1)S(1)}, u32[]{:S(2)}, u32[]{:S(2)}) collective-permute-start(bf16[4,104,768]{2,1,0:T(8,128)(2,1)S(1)} %get-tuple-element.109), channel_id=1, source_target_pairs={{0,16},{1,17},{2,18},{3,19},{4,12},{5,13},{6,14},{7,15},{8,24},{9,... | collective-permute-start | bytes 1916936 | tf_op jit(solution)/shard_map/ppermute | solution.py:390
  206.6 11.2 %collective-permute-start.36 = (bf16[1,96,768]{2,1,0:T(8,128)(2,1)S(1)}, bf16[1,96,768]{2,1,0:T(8,128)(2,1)S(1)}, u32[]{:S(2)}, u32[]{:S(2)}) collective-permute-start(bf16[1,96,768]{2,1,0:T(8,128)(2,1)S(1)} %get-tuple-element.183), channel_id=1, source_target_pairs={{0,1},{1,0},{2,3},{3,2},{4,5},{5,4},{6,7},{7,6},{8,9},{9,8},{10,11... | collective-permute-start | bytes 442376 | tf_op jit(solution)/shard_map/ppermute | solution.py:390
  209.1 14.9 %collective-permute-start.37 = (bf16[1,96,768]{2,1,0:T(8,128)(2,1)S(1)}, bf16[1,96,768]{2,1,0:T(8,128)(2,1)S(1)}, u32[]{:S(2)}, u32[]{:S(2)}) collective-permute-start(bf16[1,96,768]{2,1,0:T(8,128)(2,1)S(1)} %get-tuple-element.185), channel_id=1, source_target_pairs={{0,2},{1,3},{2,0},{3,1},{4,6},{5,7},{6,4},{7,5},{8,10},{9,11},{10,... | collective-permute-start | bytes 442376 | tf_op jit(solution)/shard_map/ppermute | solution.py:390
  211.3 15.5 %collective-permute-start.38 = (bf16[1,96,768]{2,1,0:T(8,128)(2,1)S(1)}, bf16[1,96,768]{2,1,0:T(8,128)(2,1)S(1)}, u32[]{:S(2)}, u32[]{:S(2)}) collective-permute-start(bf16[1,96,768]{2,1,0:T(8,128)(2,1)S(1)} %get-tuple-element.184), channel_id=1, source_target_pairs={{0,3},{1,2},{2,1},{3,0},{4,7},{5,6},{6,5},{7,4},{8,11},{9,10},{10,... | collective-permute-start | bytes 442376 | tf_op jit(solution)/shard_map/ppermute | solution.py:390
  212.8 24.3 %collective-permute-start.32 = (bf16[1,96,768]{2,1,0:T(8,128)(2,1)S(1)}, bf16[1,96,768]{2,1,0:T(8,128)(2,1)S(1)}, u32[]{:S(2)}, u32[]{:S(2)}) collective-permute-start(bf16[1,96,768]{2,1,0:T(8,128)(2,1)S(1)} %get-tuple-element.186), channel_id=1, source_target_pairs={{0,1},{1,0},{2,3},{3,2},{4,5},{5,4},{6,7},{7,6},{8,9},{9,8},{10,11... | collective-permute-start | bytes 442376 | tf_op jit(solution)/shard_map/ppermute | solution.py:390
  217.8 20.6 %collective-permute-start.33 = (bf16[1,96,768]{2,1,0:T(8,128)(2,1)S(1)}, bf16[1,96,768]{2,1,0:T(8,128)(2,1)S(1)}, u32[]{:S(2)}, u32[]{:S(2)}) collective-permute-start(bf16[1,96,768]{2,1,0:T(8,128)(2,1)S(1)} %get-tuple-element.188), channel_id=1, source_target_pairs={{0,2},{1,3},{2,0},{3,1},{4,6},{5,7},{6,4},{7,5},{8,10},{9,11},{10,... | collective-permute-start | bytes 442376 | tf_op jit(solution)/shard_map/ppermute | solution.py:390
  223.9 14.5 %collective-permute-start.34 = (bf16[1,96,768]{2,1,0:T(8,128)(2,1)S(1)}, bf16[1,96,768]{2,1,0:T(8,128)(2,1)S(1)}, u32[]{:S(2)}, u32[]{:S(2)}) collective-permute-start(bf16[1,96,768]{2,1,0:T(8,128)(2,1)S(1)} %get-tuple-element.187), channel_id=1, source_target_pairs={{0,3},{1,2},{2,1},{3,0},{4,7},{5,6},{6,5},{7,4},{8,11},{9,10},{10,... | collective-permute-start | bytes 442376 | tf_op jit(solution)/shard_map/ppermute | solution.py:390
  227.6 12.5 %collective-permute-start.28 = (bf16[1,104,768]{2,1,0:T(8,128)(2,1)S(1)}, bf16[1,104,768]{2,1,0:T(8,128)(2,1)S(1)}, u32[]{:S(2)}, u32[]{:S(2)}) collective-permute-start(bf16[1,104,768]{2,1,0:T(8,128)(2,1)S(1)} %get-tuple-element.180), channel_id=1, source_target_pairs={{0,1},{1,0},{2,3},{3,2},{4,5},{5,4},{6,7},{7,6},{8,9},{9,8},{10,11... | collective-permute-start | bytes 479240 | tf_op jit(solution)/shard_map/ppermute | solution.py:390
  235.1 12.5 %collective-permute-start.29 = (bf16[1,104,768]{2,1,0:T(8,128)(2,1)S(1)}, bf16[1,104,768]{2,1,0:T(8,128)(2,1)S(1)}, u32[]{:S(2)}, u32[]{:S(2)}) collective-permute-start(bf16[1,104,768]{2,1,0:T(8,128)(2,1)S(1)} %get-tuple-element.182), channel_id=1, source_target_pairs={{0,2},{1,3},{2,0},{3,1},{4,6},{5,7},{6,4},{7,5},{8,10},{9,11},{10,... | collective-permute-start | bytes 479240 | tf_op jit(solution)/shard_map/ppermute | solution.py:390
  237.1 10.5 %collective-permute-start.30 = (bf16[1,104,768]{2,1,0:T(8,128)(2,1)S(1)}, bf16[1,104,768]{2,1,0:T(8,128)(2,1)S(1)}, u32[]{:S(2)}, u32[]{:S(2)}) collective-permute-start(bf16[1,104,768]{2,1,0:T(8,128)(2,1)S(1)} %get-tuple-element.181), channel_id=1, source_target_pairs={{0,3},{1,2},{2,1},{3,0},{4,7},{5,6},{6,5},{7,4},{8,11},{9,10},{10,... | collective-permute-start | bytes 479240 | tf_op jit(solution)/shard_map/ppermute | solution.py:390
  247.5 3.5 %copy-start.1 = (bf16[3,128,768]{2,1,0:T(8,128)(2,1)S(1)}, bf16[3,128,768]{2,1,0:T(8,128)(2,1)}, u32[]{:S(2)}) copy-start(bf16[3,128,768]{2,1,0:T(8,128)(2,1)} %param.15) | copy-start | bytes 1769476
  (20 other events, 22.3 us)

commit v4 on v3

--- a/solution.py
+++ b/solution.py
@@ -96,17 +96,86 @@
     return [values[:, c : c + length] for c in range(0, values.shape[1], length)]
 
 
-def attention_forward(x_ref, w0_ref, w1_ref, w2_ref, w3_ref, bq_ref, bv_ref, segc_ref, segr_ref, vec_ref,
-                      qkv_ref, p_ref, o_ref, n1_ref, x1_ref, r1_ref, n1b_ref, n1t_ref, acc_ref):
+def rows_of(refs):
+    return jnp.concatenate([r[...].reshape(-1, r.shape[3]) for r in refs], axis=0)
+
+
+def accumulate(acc_ref, step, add):
+    @pl.when(step == 0)
+    def _():
+        acc_ref[...] = add
+
+    @pl.when(step > 0)
+    def _():
+        acc_ref[...] += add
+
+
+def iota(shape, axis):
+    return lax.broadcasted_iota(jnp.int32, shape, axis)
+
+
+def picks(count, first, wide, size):
+    return (iota((count, wide), 0) == first + lax.rem(iota((1, wide), 1), size)).astype(bf16)
+
+
+def belongs(count, wide, size, period):
+    lane, row = iota((1, wide), 1), lax.rem(iota((count, 1), 0), period)
+    return (lane >= row * size) & (lane < (row + 1) * size)
+
+
+def read_vectors(rows, hot_d, hot_e, sizes):
+    n_d, dv, bu, width, hc, fc, n_t = sizes
+    count = rows.shape[0]
+    per = count // n_t
+    d_all = nn(hot_d, rows[:, : n_d * dv]).astype(bf16)
+    mine = belongs(count, width, dv, count)
+    d_rows = [col_sum(jnp.where(mine, nn(d_all, picks(n_d * dv, j * dv, width, dv)), 0.0)) for j in range(n_d)]
+    e_all = nn(hot_e, rows[:, n_d * dv : n_d * dv + 2 * dv + bu]).astype(bf16)
+    out = []
+    for first, size, wide in ((0, dv, hc), (dv, dv, hc), (2 * dv, bu, fc)):
+        spread = jnp.where(belongs(count, wide, size, per), nn(e_all, picks(e_all.shape[1], first, wide, size)), 0.0)
+        out.append(jnp.sum(spread.reshape(n_t, per, wide), axis=1, keepdims=True))
+    return jnp.concatenate(d_rows, axis=0), out
+
+
+def write_vectors(d_rows, e_rows, hot_d, hot_e, sizes):
+    n_d, dv, bu, width, hc, fc, n_t = sizes
+    count = hot_d.shape[0]
+    per = count // n_t
+    mine = belongs(count, width, dv, count)
+    d_all = sum(
+        nt(jnp.where(mine, d_rows[j : j + 1, :], 0.0).astype(bf16), picks(n_d * dv, j * dv, width, dv)) for j in range(n_d)
+    ).astype(bf16)
+    e_all = 0.0
+    for value, first, size, wide in zip(e_rows, (0, dv, 2 * dv), (dv, dv, bu), (hc, hc, fc), strict=True):
+        spread = jnp.broadcast_to(value, (n_t, per, wide)).reshape(count, wide)
+        spread = jnp.where(belongs(count, wide, size, per), spread, 0.0).astype(bf16)
+        e_all = e_all + nt(spread, picks(2 * dv + bu, first, wide, size))
+    return jnp.concatenate([tn(hot_d, d_all), tn(hot_e, e_all.astype(bf16))], axis=1)
+
+
+def attention_forward(sizes, x_ref, w0_ref, w1_ref, w2_ref, w3_ref, v0_ref, v1_ref, v2_ref, v3_ref, hd_ref, he_ref,
+                      segc_ref, segr_ref, qkv_ref, p_ref, o_ref, n1_ref, x1_ref, r1_ref, n1b_ref, n1t_ref, n1s_ref,
+                      vec_ref, bu_ref, acc_ref, bq_ref, bv_ref):
     step = pl.program_id(0)
     hc = bq_ref.shape[-1]
+
+    @pl.when(step == 0)
+    def _():
+        rows = jnp.concatenate([r[:, :, 0, :].reshape(-1, r.shape[3]) for r in (v0_ref, v1_ref, v2_ref, v3_ref)], axis=0)
+        d_rows, (b_q, b_v, b_u) = read_vectors(rows, hd_ref[...], he_ref[...], sizes)
+        vec_ref[...] = d_rows
+        bq_ref[...] = b_q
+        bv_ref[...] = b_v
+        bu_ref[...] = b_u
+
     rows, length = segr_ref.shape
     x = x_ref[...]
     w = rows_of((w0_ref, w1_ref, w2_ref, w3_ref))
     qkv = nn(x, w[:, : 3 * hc])
-    q = (qkv[:, :hc] + bq_ref[0]).astype(bf16) * bf16(SCALE)
+    q = (qkv[:, :hc] + bq_ref[step]).astype(bf16) * bf16(SCALE)
     k = qkv[:, hc : 2 * hc].astype(bf16)
-    v = (qkv[:, 2 * hc :] + bv_ref[0]).astype(bf16)
+    v = (qkv[:, 2 * hc :] + bv_ref[step]).astype(bf16)
     qkv_ref[0, :, :hc] = q
     qkv_ref[0, :, hc : 2 * hc] = k
     qkv_ref[0, :, 2 * hc :] = v
@@ -123,16 +192,11 @@
         probs.append(jnp.concatenate(parts, axis=1))
     for g, span in enumerate(spans):
         p_ref[0, g] = probs[g]
-        o_ref[0, span, :] = nn(probs[g].astype(bf16), stacked(v[span], hc)).astype(bf16)
-    add = nt(o_ref[0], w[:, 3 * hc :])
-
-    @pl.when(step == 0)
-    def _():
-        acc_ref[...] = add
-
-    @pl.when(step > 0)
-    def _():
-        acc_ref[...] += add
+        o_ref[0, span, :hc] = nn(probs[g].astype(bf16), stacked(v[span], hc)).astype(bf16)
+    o_ref[0, :, hc:] = jnp.zeros((o_ref.shape[1], o_ref.shape[2] - hc), bf16)
+    add = nt(o_ref[0, :, :hc], w[:, 3 * hc :])
+
+    accumulate(acc_ref, step, add)
 
     @pl.when(step == pl.num_programs(0) - 1)
     def _():
@@ -144,11 +208,9 @@
         r1_ref[...] = inverse
         low = n1.astype(bf16)
         n1b_ref[...] = low
-        n1t_ref[...] = low.T
-
-
-def rows_of(refs):
-    return jnp.concatenate([r[...].reshape(r.shape[0] * r.shape[2], r.shape[3]) for r in refs], axis=0)
+        turned = low.T
+        n1t_ref[...] = turned[: low.shape[1] // 2]
+        n1s_ref[...] = turned[low.shape[1] // 2 :]
 
 
 def up_forward(n_ref, w0_ref, w1_ref, w2_ref, w3_ref, b_ref, z_ref, d_ref):
@@ -159,17 +221,11 @@
 
 
 def down_forward(z_ref, w0_ref, w1_ref, w2_ref, w3_ref, n1_ref, vec_ref, segc_ref, segr_ref, pg_ref,
-                 pooled_ref, db_ref, dbb_ref, dbt_ref, sums_ref, acc_ref):
+                 pooled_ref, db_ref, dbb_ref, dbt_ref, dbs_ref, sums_ref, acc_ref):
     step = pl.program_id(0)
     add = nt(z_ref[0], rows_of((w0_ref, w1_ref, w2_ref, w3_ref)))
 
-    @pl.when(step == 0)
-    def _():
-        acc_ref[...] = add
-
-    @pl.when(step > 0)
-    def _():
-        acc_ref[...] += add
+    accumulate(acc_ref, step, add)
 
     @pl.when(step == pl.num_programs(0) - 1)
     def _():
@@ -196,7 +252,9 @@
         db_ref[...] = db
         low = db.astype(bf16)
         dbb_ref[...] = low
-        dbt_ref[...] = low.T
+        turned = low.T
+        dbt_ref[...] = turned[: low.shape[1] // 2]
+        dbs_ref[...] = turned[low.shape[1] // 2 :]
         sums_ref[0:1, :] = col_sum(db)
         sums_ref[1:2, :] = col_sum(dy * x2)
         sums_ref[2:3, :] = col_sum(dy)
@@ -206,31 +264,43 @@
     ref[:, :, :BLK, :] = grad.astype(bf16).reshape(grad.shape[0] // BLK, 1, BLK, grad.shape[1])
 
 
-def down_weight(dbt_ref, z_ref, out_ref):
-    put(nn(dbt_ref[...], z_ref[0]), out_ref)
-
-
-def up_backward(dbb_ref, w0_ref, w1_ref, w2_ref, w3_ref, d_ref, n1t_ref, keep_ref, send_ref, du_ref, bu_ref):
-    width = dbb_ref.shape[1]
+def hidden_backward(dbb_ref, w0_ref, w1_ref, w2_ref, w3_ref, d_ref, du_ref, bu_ref):
     du = (nn(dbb_ref[...], rows_of((w0_ref, w1_ref, w2_ref, w3_ref))) * d_ref[0]).astype(bf16)
     du_ref[0] = du
     bu_ref[0] = col_sum(du.astype(f32))
-    grad = nn(n1t_ref[...], du)
-    put(grad[width // 2 :], send_ref)
-    put(grad[: width // 2], keep_ref)
-
-
-def norm_backward(du_ref, w0_ref, w1_ref, w2_ref, w3_ref, db_ref, x1_ref, r1_ref, vec_ref, da_ref, dab_ref, dat_ref, sums_ref, acc_ref):
+
+
+def step_value(refs, width):
+    if len(refs) == 1:
+        return refs[0][0, :, :width]
+    return jnp.where(pl.program_id(0) < pl.num_programs(0) // 2, refs[0][0, :, :width], refs[1][0, :, :width])
+
+
+def weight_gradient(groups, vectors, *refs):
+    refs = list(refs)
+    parts = []
+    for pairs, split, width in groups:
+        total = None
+        for _ in range(pairs):
+            add = nn(refs.pop(0)[...], step_value([refs.pop(0) for _ in range(split)], width))
+            total = add if total is None else total + add
+        parts.append(total)
+    grad = jnp.concatenate(parts, axis=1)
+    extra = sum(refs.pop(0)[0].astype(f32) for _ in range(vectors)) if vectors else None
+    half = grad.shape[0] // 2
+    for n, ref in enumerate(refs):
+        put(grad[n * half : (n + 1) * half], ref)
+        if vectors:
+            for j in range(ref.shape[0]):
+                row = extra[n * ref.shape[0] + j : n * ref.shape[0] + j + 1]
+                tail = ref.shape[2] - BLK
+                ref[j, 0, BLK:, :] = jnp.where(iota((tail, row.shape[1]), 0) == 0, row, 0.0).astype(bf16)
+
+
+def norm_backward(du_ref, w0_ref, w1_ref, w2_ref, w3_ref, db_ref, x1_ref, r1_ref, vec_ref,
+                  da_ref, dab_ref, dat_ref, das_ref, sums_ref, acc_ref):
     step = pl.program_id(0)
-    add = nt(du_ref[0], rows_of((w0_ref, w1_ref, w2_ref, w3_ref)))
-
-    @pl.when(step == 0)
-    def _():
-        acc_ref[...] = add
-
-    @pl.when(step > 0)
-    def _():
-        acc_ref[...] += add
+    accumulate(acc_ref, step, nt(du_ref[0], rows_of((w0_ref, w1_ref, w2_ref, w3_ref))))
 
     @pl.when(step == pl.num_programs(0) - 1)
     def _():
@@ -239,14 +309,18 @@
         da_ref[...] = da
         low = da.astype(bf16)
         dab_ref[...] = low
-        dat_ref[...] = low.T
+        turned = low.T
+        dat_ref[...] = turned[: low.shape[1] // 2]
+        das_ref[...] = turned[low.shape[1] // 2 :]
         sums_ref[0:1, :] = col_sum(da)
         sums_ref[1:2, :] = col_sum(dn1 * x1_ref[...])
         sums_ref[2:3, :] = col_sum(dn1)
 
 
-def attention_backward(dab_ref, w0_ref, w1_ref, w2_ref, w3_ref, qkv_ref, p_ref, dqkv_ref, bqv_ref):
-    hc = bqv_ref.shape[-1]
+def attention_backward(sizes, dab_ref, w0_ref, w1_ref, w2_ref, w3_ref, qkv_ref, p_ref, s1_ref, s2_ref, gu_ref, hd_ref, he_ref,
+                       low_ref, high_ref, keep_ref, send_ref, bq_ref, bv_ref, dqkv_ref):
+    step = pl.program_id(0)
+    hc = bq_ref.shape[-1]
     dab = dab_ref[...]
     w = rows_of([r.at[:, :, :, 3 * hc :] for r in (w0_ref, w1_ref, w2_ref, w3_ref)])
     do = nn(dab, w).astype(bf16)
@@ -264,37 +338,44 @@
             parts.append((pd - p * jnp.sum(pd, axis=-1, keepdims=True)).astype(bf16))
         dss.append(jnp.concatenate(parts, axis=1))
     for g, span in enumerate(spans):
-        dqkv_ref[0, span, :hc] = (nn(dss[g], k[g]) * SCALE).astype(bf16)
-        dqkv_ref[0, span, hc : 2 * hc] = own_columns(tn(dss[g], q[g]), hc).astype(bf16)
-        dqkv_ref[0, span, 2 * hc :] = own_columns(tn(p_ref[0, g].astype(bf16), do[span]), hc).astype(bf16)
-    dqkv = dqkv_ref[0]
-    bqv_ref[0, 0:1, :] = col_sum(dqkv[:, :hc].astype(f32))
-    bqv_ref[0, 1:2, :] = col_sum(dqkv[:, 2 * hc :].astype(f32))
-
-
-def attention_weights(xt_ref, dat_ref, dqkv_ref, o_ref, vec_ref, keep_ref, send_ref):
-    half = xt_ref.shape[0] // 2
-    for n, ref in enumerate((keep_ref, send_ref)):
-        count = ref.shape[0]
-        ref[:, :, BLK:, :] = vec_ref[n * count : (n + 1) * count]
-    grad = jnp.concatenate([nn(xt_ref[...], dqkv_ref[0]), nn(dat_ref[...], o_ref[0])], axis=1)
-    put(grad[half:], send_ref)
-    put(grad[:half], keep_ref)
-
-
-def input_backward(dqkv_ref, w0_ref, w1_ref, w2_ref, w3_ref, da_ref, perm_ref, dx_ref, acc_ref):
+        dqkv_ref[span, :hc] = (nn(dss[g], k[g]) * SCALE).astype(bf16)
+        dqkv_ref[span, hc : 2 * hc] = own_columns(tn(dss[g], q[g]), hc).astype(bf16)
+        dqkv_ref[span, 2 * hc : 3 * hc] = own_columns(tn(p_ref[0, g].astype(bf16), do[span]), hc).astype(bf16)
+    dqkv_ref[:, 3 * hc :] = jnp.zeros((dqkv_ref.shape[0], dqkv_ref.shape[1] - 3 * hc), bf16)
+    dqkv = dqkv_ref[...]
+    half_steps = pl.num_programs(0) // 2
+
+    @pl.when(step < half_steps)
+    def _():
+        low_ref[0] = dqkv
+
+    @pl.when(step >= half_steps)
+    def _():
+        high_ref[0] = dqkv
+
+    bq_ref[step] = col_sum(dqkv[:, :hc].astype(f32))
+    bv_ref[step] = col_sum(dqkv[:, 2 * hc : 3 * hc].astype(f32))
+
+    @pl.when(step == pl.num_programs(0) - 1)
+    def _():
+        d_rows = jnp.concatenate([s1_ref[...], s2_ref[...]], axis=0)
+        rows = write_vectors(d_rows, (bq_ref[...], bv_ref[...], gu_ref[...]), hd_ref[...], he_ref[...], sizes)
+        half, n_t = rows.shape[0] // 2, bq_ref.shape[0]
+        rows = jnp.concatenate([rows, jnp.zeros((rows.shape[0], keep_ref.shape[-1] - rows.shape[1]), f32)], axis=1)
+        for n, ref in enumerate((keep_ref, send_ref)):
+            for t in range(n_t):
+                for j in range(half // n_t):
+                    at = n * half + j * n_t + t
+                    ref[t, j : j + 1, :] = rows[at : at + 1]
+
+
+def input_backward(low_ref, high_ref, w0_ref, w1_ref, w2_ref, w3_ref, da_ref, perm_ref, dx_ref, acc_ref):
     step = pl.program_id(0)
-    cols = dqkv_ref.shape[-1]
+    cols = 3 * w0_ref.shape[-1] // 4
     w = rows_of((w0_ref, w1_ref, w2_ref, w3_ref))
-    add = nt(dqkv_ref[0], w[:, :cols])
-
-    @pl.when(step == 0)
-    def _():
-        acc_ref[...] = add
-
-    @pl.when(step > 0)
-    def _():
-        acc_ref[...] += add
+    add = nt(step_value((low_ref, high_ref), cols), w[:, :cols])
+
+    accumulate(acc_ref, step, add)
 
     @pl.when(step == pl.num_programs(0) - 1)
     def _():
@@ -336,7 +417,6 @@
 def call(body, n_t, micros, ins, outs, scratch=()):
     return pl.pallas_call(
         body,
-        name=body.__name__,
         grid=(n_t,),
         in_specs=[s for _, s in ins],
         out_specs=[s for _, s in outs],
@@ -369,14 +449,24 @@
     return lax.optimization_barrier((value, *done))[0] if done else value
 
 
+def swap(value, tables, *done):
+    return lax.ppermute(after(value, *done), AXES, tables["C"][0])
+
+
 class Gather:
     def __init__(self, value, tables):
         self.held, self.tables = [value[None]], tables
 
-    def stage(self, name, *done):
-        got = [lax.ppermute(after(h, *done), AXES, t) for t in self.tables[name] for h in self.held]
+    def send(self, name, *done, parts=None):
+        sent = self.held if parts is None else [self.held[j] for j in parts]
+        return [lax.ppermute(after(h, *done), AXES, t) for t in self.tables[name] for h in sent]
+
+    def take(self, name, got):
         self.held = [jnp.concatenate(self.held + got)] if name in "Z2" else self.held + got
         return got
+
+    def stage(self, name, *done, parts=None):
+        return self.take(name, self.send(name, *done, parts=parts))
 
     def pieces(self, n_t):
         return [h.reshape(h.shape[0] // n_t, n_t, *h.shape[1:]) for h in self.held]
@@ -395,7 +485,7 @@
             return sum((g[cut].astype(f32) for g in got), self.keep[cut].astype(f32))
 
         self.send = [share(j).astype(bf16) for j in range(1, parts)]
-        self.keep = share(0) if size <= 4 else share(0).astype(bf16)
+        self.keep = share(0)
         return got
 
 
@@ -421,18 +511,18 @@
     n_vec = sum(p.shape[0] for p in d_parts + e_parts)
     nd = len(d_parts) * dv
 
+    sizes = (6, dv, up_bias.shape[0], D, hc, fc, n_t) if pairwise else (6, D // (n_i * n_t), n_t * fc // (n_i * n_t), D, hc, fc, n_t)
+    slot = jnp.arange(n_i * n_t)
+    rel = jnp.arange(n_i)
     if pairwise:
         tables = flips(n_dp, n_t)
         packed = (qkv_weight, out_weight, down_weight_in, *[p[None] for p in d_parts], qv_bias, up_bias[None])
         packed, down_t = pl.pallas_call(
-            pack, name="pack", out_shape=[sds((BLK + 8, 4 * hc), bf16), sds((BLK, fc), bf16)]
+            pack, out_shape=[sds((BLK + 8, 4 * hc), bf16), sds((BLK, fc), bf16)]
         )(*packed)
-        first = Gather(packed, tables)
-        middle = Gather(up_weight, tables)
-        last = Gather(down_t, tables)
+        first, middle, last = Gather(packed, tables), Gather(up_weight, tables), Gather(down_t, tables)
         done = first.stage("Z")
 
-        rel = jnp.arange(n_i)
         core = (at_dp & 1) ^ (rel >> 2)
         s3, s2 = (rel >> 1) & 1, rel & 1
         dy, dx = jnp.where(core == 0, s2, s3), jnp.where(core == 0, s3, s2)
@@ -441,48 +531,47 @@
         t_p = jnp.broadcast_to((at_t ^ jnp.arange(n_t))[None], (n_i, n_t)).reshape(-1)
         to_d = jnp.broadcast_to(rel[:, None], (n_i, n_t)).reshape(-1) * n_t + t_p
         to_e = (((i_p * n_t) // n_i) ^ at_t) * n_i + (i_p * n_t + t_p) % n_i
-        slot = jnp.arange(n_i * n_t)
-        hot_d = (to_d[None, :] == slot[:, None]).astype(bf16)
-        hot_e = (to_e[None, :] == slot[:, None]).astype(bf16)
-        lane = jnp.arange(D)
-        hot_i = (absolute[:, None] == rel[None, :])
-        same_block = jnp.repeat(jnp.repeat(hot_i.T, BLK, axis=0), BLK, axis=1)
-        perm = (same_block & ((lane[:, None] % BLK) == (lane[None, :] % BLK))).astype(bf16)
     else:
-        perm = (jnp.arange(D)[:, None] == jnp.arange(D)[None, :]).astype(bf16)
+        absolute, to_d, to_e = rel, slot, slot
+    hot_d = (to_d[None, :] == slot[:, None]).astype(bf16)
+    hot_e = (to_e[None, :] == slot[:, None]).astype(bf16)
+    lane = jnp.arange(D)
+    same_block = jnp.repeat(jnp.repeat((absolute[:, None] == rel[None, :]).T, BLK, axis=0), BLK, axis=1)
+    perm = (same_block & ((lane[:, None] % BLK) == (lane[None, :] % BLK))).astype(bf16)
     x = nn(hidden_in.reshape(T, D), perm).astype(bf16)
     x_t = lax.dot_general(perm, hidden_in.reshape(T, D), (((0,), (1,)), ((), ())), preferred_element_type=f32).astype(bf16)
+    x_keep, x_send = x_t[: D // 2], x_t[D // 2 :]
     pg = jnp.einsum("gsd,de->gse", pooled_grad.reshape(G, segs, D), perm.astype(f32), precision=HI)
     seg_r = segment_ids.reshape(G, L)
     seg_c = segment_ids.reshape(T, 1)
 
     if pairwise:
-        done = first.stage("2", x, x_t, pg, hot_d, hot_e) + middle.stage("Z", *done)
+        done = first.stage("2", x, x_keep, x_send, pg, hot_d, hot_e) + middle.stage("Z", *done)
+        x_other = swap(x_send, tables, *done)
         done = first.stage("3", *done) + middle.stage("2", *done) + last.stage("Z", *done)
         first.stage("C", *done)
-        done = middle.stage("3", *done) + last.stage("2", *done)
+        got_u3, got_d2 = middle.send("3", *done), last.send("2", *done)
         w_qo = first.pieces(n_t)
-        vecs = jnp.concatenate([w[:, :, BLK, : n_vec].reshape(-1, n_vec) for w in w_qo])
-        d_all = nn(hot_d, vecs[:, :nd])
-        e_all = nn(hot_e, vecs[:, nd:])
     else:
         heads_in = [qkv_weight[0], qkv_weight[1], qkv_weight[2], out_weight.T]
         main = jnp.concatenate([*heads_in, up_weight, down_weight_in.T], axis=1)
         vec = jnp.concatenate(d_parts + e_parts)
         full = lax.all_gather(lax.all_gather(main, "dp", axis=0, tiled=True), "tensor", axis=0)
         full = full.reshape(n_t, n_i, BLK, -1).transpose(1, 0, 2, 3)
+        vecs = lax.all_gather(lax.all_gather(vec, "tensor"), "dp").reshape(n_dp * n_t, -1)
+        cuts = [j * dv for j in range(9)] + [n_vec]
+        rows8 = jnp.concatenate([vecs[:, a:b].reshape(n_i * n_t, -1) for a, b in zip(cuts[:-1], cuts[1:])], axis=1)
+        rows8 = jnp.pad(rows8.reshape(n_i, n_t, 1, -1), ((0, 0), (0, 0), (0, 7), (0, 4 * hc - rows8.shape[1])))
         quarters = [full[j * n_i // 4 : (j + 1) * n_i // 4] for j in range(4)]
-        w_qo = [w[..., : 4 * hc] for w in quarters]
+        w_qo = [
+            jnp.concatenate([w[..., : 4 * hc], rows8[j * n_i // 4 : (j + 1) * n_i // 4]], axis=2)
+            for j, w in enumerate(quarters)
+        ]
         w_up = [w[..., 4 * hc : 4 * hc + fc] for w in quarters]
         w_down = [w[..., 4 * hc + fc :] for w in quarters]
-        vecs = lax.all_gather(lax.all_gather(vec, "tensor"), "dp").reshape(n_dp * n_t, -1).astype(f32)
-        d_all, e_all = vecs[:, :nd], vecs[:, nd:]
-
-    vec_d = jnp.concatenate([d_all[:, j * dv : (j + 1) * dv].reshape(1, D) for j in range(6)])
-    b_q = e_all[:, :dv].reshape(n_t, 1, hc)
-    b_v = e_all[:, dv : 2 * dv].reshape(n_t, 1, hc)
-    b_u = e_all[:, 2 * dv :].reshape(n_t, 1, fc)
+
     hl = hc // HD * L
+    o_wide, q_wide = -(-hc // 128) * 128, -(-3 * hc // 128) * 128
 
     def leads(*arrays):
         return [(a, lead(a)) for a in arrays]
@@ -493,112 +582,142 @@
     def weights(*arrays):
         return [(a, weight(a)) for a in arrays]
 
-    if pairwise:
-        last.stage("3", *done)
-        middle.stage("C", *done)
-    qkv, prob, o, n1, x1, r1, n1b, n1_t = call(
-        attention_forward, n_t, 10,
-        wholes(x) + weights(*w_qo) + leads(b_q, b_v) + wholes(seg_c, seg_r, vec_d),
-        leads(far((n_t, T, 3 * hc), bf16), far((n_t, G, L, hl), f32), far((n_t, T, hc), bf16))
-        + wholes(sds((T, D), f32), far((T, D), f32), far((T, 1), f32), sds((T, D), bf16), far((D, T), bf16)),
-        [pltpu.VMEM((T, D), f32)],
+    tails = [
+        (w, pl.BlockSpec((w.shape[0], n_t, 8, w.shape[3]), lambda s: (0, 0, BLK // 8, 0), pipeline_mode=pl.Buffered(1)))
+        for w in w_qo
+    ]
+    turned = (D // 2, T)
+    qkv, prob, o, n1, x1, r1, n1b, n1_keep, n1_send, vec_d, b_u = call(
+        partial(attention_forward, sizes), n_t, 10,
+        wholes(x) + weights(*w_qo) + tails + wholes(hot_d, hot_e, seg_c, seg_r),
+        leads(far((n_t, T, 3 * hc), bf16), far((n_t, G, L, hl), f32), far((n_t, T, o_wide), bf16))
+        + wholes(sds((T, D), f32), far((T, D), f32), far((T, 1), f32), sds((T, D), bf16), far(turned, bf16), far(turned, bf16))
+        + wholes(sds((6, D), f32), sds((n_t, 1, fc), f32)),
+        [pltpu.VMEM((T, D), f32), pltpu.VMEM((n_t, 1, hc), f32), pltpu.VMEM((n_t, 1, hc), f32)],
     )
     if pairwise:
-        last.stage("C", n1b)
+        last.take("2", [after(g, n1b) for g in got_d2])
+        middle.take("3", got_u3)
+        last.stage("3", *got_u3)
+        middle.stage("C", n1b)
+        last.take("C", last.send("C", n1b, parts=(0,)))
+        last.take("C", last.send("C", parts=(1,)))
         w_up, w_down = middle.pieces(n_t), last.pieces(n_t)
+        n1_other = swap(n1_send, tables)
+        o_other = swap(o, tables)
     z, dgelu = call(
         up_forward, n_t, 4, wholes(n1b) + weights(*w_up) + leads(b_u),
         leads(sds((n_t, T, fc), bf16), sds((n_t, T, fc), f32)),
     )
-    pooled, db, dbb, db_t, sums2 = call(
+    if pairwise:
+        z_other = swap(z, tables)
+    pooled, db, dbb, db_keep, db_send, sums2 = call(
         down_forward, n_t, 5.5, leads(z) + weights(*w_down) + wholes(n1, vec_d, seg_c, seg_r, pg),
-        wholes(sds((G, segs, D), f32), sds((T, D), f32), sds((T, D), bf16), sds((D, T), bf16), sds((3, D), f32)),
+        wholes(sds((G, segs, D), f32), sds((T, D), f32), sds((T, D), bf16), sds(turned, bf16), sds(turned, bf16), sds((3, D), f32)),
         [pltpu.VMEM((T, D), f32)],
     )
-    half = sds((n_i // 2, n_t, BLK, fc), bf16)
-
-    def halves(h):
-        return [(h, half_spec(h))]
-
-    def side_of(side):
-        return [(db_t, pl.BlockSpec((D // 2, T), lambda s: (side, 0), pipeline_mode=pl.Buffered(1)))]
-
-    down_send = call(down_weight, n_t, 2.2, side_of(1) + leads(z), halves(half))[0]
-    down_keep = call(down_weight, n_t, 2.2, side_of(0) + leads(z), halves(half))[0]
+
+    def gradient(groups, vectors=()):
+        ins, kinds = [], []
+        for width, *pairs in groups:
+            kinds.append((len(pairs), len(pairs[0][1]), width))
+            for lhs, values in pairs:
+                ins += wholes(lhs) + (leads(*values) if len(values) == 1 else halved(*values))
+        out = sds((n_i // 4, n_t, BLK + (8 if vectors else 0), sum(k[2] for k in kinds)), bf16)
+        return call(partial(weight_gradient, kinds, len(vectors)), n_t, 4, ins + leads(*vectors), [(out, half_spec(out))] * 2)
+
+    def halved(low, high):
+        block = (1,) + low.shape[1:]
+        return [
+            (low, pl.BlockSpec(block, lambda s: (jnp.minimum(s, n_t // 2 - 1), 0, 0))),
+            (high, pl.BlockSpec(block, lambda s: (jnp.maximum(s - n_t // 2, 0), 0, 0))),
+        ]
 
     def flat(a):
         return a.reshape((-1,) + a.shape[2:])
 
-    if pairwise:
+    du, g_bu = call(
+        hidden_backward, n_t, 3.5, wholes(dbb) + weights(*w_down) + leads(dgelu),
+        leads(sds((n_t, T, fc), bf16), sds((n_t, 1, fc), f32)),
+    )
+    if pairwise:
+        db_other = swap(db_send, tables)
+        du_other = swap(du, tables)
+        down_keep, down_send = gradient([[fc, (after(db_keep, g_bu), [z]), (db_other, [z_other])]])
         s_down = Scatter(flat(down_keep), flat(down_send), tables)
-        s_down.stage("C", 2)
-        dbb = after(dbb, down_keep)
-    up_keep, up_send, du, g_bu = call(
-        up_backward, n_t, 7, wholes(dbb) + weights(*w_down) + leads(dgelu) + wholes(n1_t),
-        halves(half) * 2 + leads(sds((n_t, T, fc), bf16), sds((n_t, 1, fc), f32)),
+        got_d3 = s_down.stage("3", 2)
+        du_next = after(du, down_keep)
+    else:
+        du_next = du
+    da, dab, da_keep, da_send, sums1 = call(
+        norm_backward, n_t, 5, leads(du_next) + weights(*w_up) + wholes(db, x1, r1, vec_d),
+        wholes(sds((T, D), f32), sds((T, D), bf16), sds(turned, bf16), sds(turned, bf16), sds((3, D), f32)),
+        [pltpu.VMEM((T, D), f32)],
     )
     if pairwise:
+        da_other = swap(da_send, tables)
+        up_keep, up_send = gradient([[fc, (after(n1_keep, da_keep), [du]), (n1_other, [du_other])]])
         s_up = Scatter(flat(up_keep), flat(up_send), tables)
-        got3 = s_down.stage("3", 2)
-        got_uc = s_up.stage("C", 2)
-    da, dab, da_t, sums1 = call(
-        norm_backward, n_t, 4, leads(du) + weights(*w_up) + wholes(db, x1, r1, vec_d),
-        wholes(sds((T, D), f32), sds((T, D), bf16), sds((D, T), bf16), sds((3, D), f32)), [pltpu.VMEM((T, D), f32)],
+        got_u3 = s_up.stage("3", 2)
+        dab = after(dab, up_keep)
+    rows = sds((n_t, n_i // 2, 4 * hc), f32)
+    if pairwise:
+        dab = after(dab, *got_d3)
+    dq_half = sds((n_t // 2, T, q_wide), bf16)
+    *dq, v_keep, v_send = call(
+        partial(attention_backward, sizes), n_t, 8,
+        wholes(dab) + weights(*w_qo) + leads(qkv, prob) + wholes(sums1, sums2, g_bu, hot_d, hot_e),
+        halved(dq_half, dq_half) + wholes(rows, rows),
+        [pltpu.VMEM((n_t, 1, hc), f32), pltpu.VMEM((n_t, 1, hc), f32), pltpu.VMEM((T, q_wide), bf16)],
     )
-    if pairwise:
-        dab = after(dab, *got_uc)
-    dqkv, g_bqv = call(
-        attention_backward, n_t, 8, wholes(dab) + weights(*w_qo) + leads(qkv, prob),
-        leads(sds((n_t, T, 3 * hc), bf16), sds((n_t, 2, hc), f32)),
-    )
-    if pairwise:
-        got_d2, got_u3 = s_down.stage("2", n_t), s_up.stage("3", 2)
-        da_t = after(da_t, *got3, *got_u3)
-    g_d = jnp.concatenate([v.reshape(n_dp * n_t, dv) for v in (*sums1, *sums2)], axis=1)
-    g_e = jnp.concatenate(
-        [g_bqv[:, 0].reshape(n_dp * n_t, dv), g_bqv[:, 1].reshape(n_dp * n_t, dv), g_bu.reshape(n_dp * n_t, -1)], axis=1
-    )
-    if pairwise:
-        g_vec = jnp.concatenate([tn(hot_d, g_d.astype(bf16)), tn(hot_e, g_e.astype(bf16))], axis=1).astype(bf16)
-        g_vec = jnp.pad(g_vec.reshape(n_i, n_t, 1, -1), ((0, 0), (0, 0), (0, 7), (0, 4 * hc - n_vec)))
-    else:
-        g_vec = jnp.zeros((n_i, n_t, 8, 4 * hc), bf16)
-    half_qo = sds((n_i // 2, n_t, BLK + 8, 4 * hc), bf16)
-    qo_keep, qo_send = call(
-        attention_weights, n_t, 5,
-        wholes(x_t, da_t) + leads(dqkv, o) + [(g_vec, pl.BlockSpec((n_i, 1, 8, 4 * hc), lambda s: (0, s, 0, 0)))],
-        halves(half_qo) * 2,
-    )
-    if pairwise:
+    dq_next = dq
+    if pairwise:
+        dq_other = [swap(d, tables) for d in dq]
+        v_other = swap(v_send, tables)
+        got_d2 = s_down.stage("2", n_t)
+        x_now = after(x_keep, *got_d2, *got_u3)
+        qo_keep, qo_send = gradient(
+            [[3 * hc, (x_now, dq), (x_other, dq_other)], [hc, (da_keep, [o]), (da_other, [o_other])]], (v_keep, v_other)
+        )
         s_qo = Scatter(flat(qo_keep), flat(qo_send), tables)
-        s_qo.stage("C", 2)
-        dqkv = after(dqkv, qo_send)
+        got_z = s_down.stage("Z", 1)
+        got_u2 = s_up.stage("2", n_t)
+        got_q3 = s_qo.stage("3", 2)
+        dq_next = [after(d, qo_keep) for d in dq]
     dx = call(
-        input_backward, n_t, 4, leads(dqkv) + weights(*w_qo) + wholes(da, perm), wholes(sds((T, D), f32)),
+        input_backward, n_t, 4, halved(*dq_next) + weights(*w_qo) + wholes(da, perm), wholes(sds((T, D), f32)),
         [pltpu.VMEM((T, D), f32)],
     )[0]
     pooled = jnp.einsum("gse,de->gsd", pooled, perm.astype(f32), precision=HI)
 
     if pairwise:
-        s_down.stage("Z", 1)
-        s_up.stage("2", n_t)
-        s_qo.stage("3", 2)
-        s_up.stage("Z", 1)
-        s_qo.stage("2", n_t, dx)
-        s_qo.stage("Z", 1)
+        got = s_up.stage("Z", 1)
+        s_qo.stage("2", n_t, dx, *got_z, *got_u2)
+        s_qo.stage("Z", 1, *got)
         g_down, g_up, g_qo = s_down.keep[0], s_up.keep[0], s_qo.keep[0]
-        g_v = g_qo[BLK, : n_vec]
+        g_v = g_qo[BLK, :n_vec]
         g_qo = g_qo[:BLK]
     else:
-        def joined(keep, send):
-            g = jnp.concatenate([keep, send])[:, :, :BLK]
+        def joined(*halves_of):
+            g = jnp.concatenate([part[:, :, :BLK] for half in halves_of for part in half])
             return g.transpose(1, 0, 2, 3).reshape(n_t, D, -1)
 
-        g_full = jnp.concatenate([joined(qo_keep, qo_send), joined(up_keep, up_send), joined(down_keep, down_send)], axis=2)
+        x_h, n1_h, db_h, da_h = (x_keep, x_send), (n1_keep, n1_send), (db_keep, db_send), (da_keep, da_send)
+        g_full = jnp.concatenate([
+            joined(*[gradient([[3 * hc, (x_h[j], dq)], [hc, (da_h[j], [o])]]) for j in range(2)]),
+            joined(*[gradient([[fc, (n1_h[j], [du])]]) for j in range(2)]),
+            joined(*[gradient([[fc, (db_h[j], [z])]]) for j in range(2)]),
+        ], axis=2)
         mine = lax.psum_scatter(g_full, "tensor", scatter_dimension=0)
         mine = lax.psum_scatter(mine, "dp", scatter_dimension=0, tiled=True).astype(f32)
         g_qo, g_up, g_down = mine[:, : 4 * hc], mine[:, 4 * hc : 4 * hc + fc], mine[:, 4 * hc + fc :]
-        g_v = lax.psum_scatter(jnp.concatenate([g_d, g_e], axis=1), AXES, scatter_dimension=0)
+        g_rows = jnp.stack([v_keep, v_send]).transpose(0, 2, 1, 3).reshape(n_i * n_t, -1)
+        dv_c, bu_c = sizes[1], sizes[2]
+        cuts = [j * dv_c for j in range(9)] + [8 * dv_c + bu_c]
+        g_v = jnp.concatenate(
+            [g_rows[:, a:b].reshape(n_dp * n_t, -1) for a, b in zip(cuts[:-1], cuts[1:])], axis=1
+        )
+        g_v = lax.psum_scatter(g_v, AXES, scatter_dimension=0)
     vo = [g_v[j * dv : (j + 1) * dv] for j in range(8)]
     return (
         pooled.reshape(micro, seqs, segs, D),

time: 252 us -> 231 us (0.917)
  local copies, waits for them, and re-layouts: 40.8 us -> 11.4 us
  waiting for transfers between devices: 76.2 us -> 102 us
  other arithmetic: 17.2 us -> 6.57 us
  starting transfers between devices: 49.7 us -> 46.4 us
    unnamed x108 -> x63, local copies, waits for them, and re-layouts: 27.4 us -> 5.53 us
    ppermute x21 -> x31, waiting for transfers between devices: 40.2 us -> 60.1 us  [the longest x21 54.5 us: send(): lax.ppermute(after(h, *done), AXES, t)]
    ppermute x18 -> x15, waiting for transfers between devices: 35.9 us -> 41.8 us  [stage(): lax.ppermute(after(s, *done), AXES, t)]
    convert_element_type x3 -> x1, other arithmetic: 5.29 us -> 0.01 us  [per_device(): hot_d = (to_d[None, :] == slot[:, None]).astype(bf16)]
    convert_element_type x6 -> x4, other arithmetic: 3.81 us -> 0.54 us  [stage(): self.send = [share(j).astype(bf16) for j in range(1, parts)]]
    concatenate x8 -> x3, local copies, waits for them, and re-layouts: 4.08 us -> 0.95 us  [take(): jnp.concatenate(self.held + got)]
    ppermute x18 -> x15, starting transfers between devices: 25.7 us -> 22.8 us  [stage(): lax.ppermute(after(s, *done), AXES, t)]
    concatenate x4 -> x3, other arithmetic: 4 us -> 1.42 us  [take(): jnp.concatenate(self.held + got)]
  transfers between devices with their start and end apart: 39 -> 46, of which waited for: 17 -> 22; matrix products, arithmetic and copies ran while one was open for 15% -> 7% of each run, Pallas kernels for 18% -> 23%
where the time goes in v4:
time: 231 us
  waiting for transfers between devices  102 us (44%)
  Pallas kernels  59.6 us (26%)
  starting transfers between devices  46.4 us (20%)
  local copies, waits for them, and re-layouts  11.4 us (5%)
  other arithmetic  6.57 us (3%)
  matrix products  3.78 us (2%)
    pallas_call x10, Pallas kernels, call(): pl.pallas_call(body, grid=(n_t,), in_specs=[s for _, s in ins], out_specs...  57.5 us
    ppermute x21, waiting for transfers between devices, send(): lax.ppermute(after(h, *done), AXES, t)  54.5 us
    ppermute x15, waiting for transfers between devices, stage(): lax.ppermute(after(s, *done), AXES, t)  41.8 us
    ppermute x15, starting transfers between devices, stage(): lax.ppermute(after(s, *done), AXES, t)  22.8 us
    ppermute x21, starting transfers between devices, send(): lax.ppermute(after(h, *done), AXES, t)  20.9 us
    ppermute x10, waiting for transfers between devices, swap(): return lax.ppermute(after(value, *done), AXES, tables['C'][0])  5.59 us
    unnamed x63, local copies, waits for them, and re-layouts  5.53 us
  transfers between devices with their start and end apart: 46, of which 22 were waited for; matrix products, arithmetic and copies ran while one was open for 7% of the time, Pallas kernels for 23%

profile of v4, /device:TPU:0, one launch (start us, length us, event | category | flops | bytes accessed | tf_op | source)
XLA Modules:
  0.0 230.9 jit_solution(5765020481076523998)
XLA Ops:
  0.7 1.8 copy.33.down_ref
  2.4 2.0 shard_map.254
  4.5 3.0 %collective-permute-start = (bf16[1,104,768]{2,1,0:T(8,128)(2,1)}, bf16[1,104,768]{2,1,0:T(8,128)(2,1)S(1)}, u32[]{:S(2)}, u32[]{:S(2)}) collective-permute-start(bf16[1,104,768]{2,1,0:T(8,128)(2,1)} %bitcast.141), channel_id=1, source_target_pairs={{0,1},{1,0},{2,3},{3,2},{4,5},{5,4},{6,7},{7,6},{8,9},{9,8},{10,11... | collective-permute-start | bytes 479240 | tf_op jit(solution)/shard_map/ppermute | solution.py:462
  7.5 2.6 %collective-permute-start.1 = (bf16[1,104,768]{2,1,0:T(8,128)(2,1)}, bf16[1,104,768]{2,1,0:T(8,128)(2,1)S(1)}, u32[]{:S(2)}, u32[]{:S(2)}) collective-permute-start(bf16[1,104,768]{2,1,0:T(8,128)(2,1)} %bitcast.142), channel_id=1, source_target_pairs={{0,2},{1,3},{2,0},{3,1},{4,6},{5,7},{6,4},{7,5},{8,10},{9,11},{10,... | collective-permute-start | bytes 479240 | tf_op jit(solution)/shard_map/ppermute | solution.py:462
  11.2 0.8 convolution_convert_fusion
  12.1 0.9 fusion.44
  13.0 1.0 convolution_bitcast_fusion.pg_ref
  14.2 8.3 %collective-permute-done.1 = bf16[1,104,768]{2,1,0:T(8,128)(2,1)S(1)} collective-permute-done((bf16[1,104,768]{2,1,0:T(8,128)(2,1)}, bf16[1,104,768]{2,1,0:T(8,128)(2,1)S(1)}, u32[]{:S(2)}, u32[]{:S(2)}) %collective-permute-start.1) | collective-permute-done | bytes 159776 | tf_op jit(solution)/shard_map/ppermute | solution.py:462
  22.6 1.6 collective-permute-start.3
  24.2 2.6 %collective-permute-start.4 = (bf16[1,96,768]{2,1,0:T(8,128)(2,1)S(1)}, bf16[1,96,768]{2,1,0:T(8,128)(2,1)S(1)}, u32[]{:S(2)}, u32[]{:S(2)}) collective-permute-start(bf16[1,96,768]{2,1,0:T(8,128)(2,1)S(1)} %bitcast.145), channel_id=1, source_target_pairs={{0,1},{1,0},{2,3},{3,2},{4,5},{5,4},{6,7},{7,6},{8,9},{9,8},{10,11... | collective-permute-start | bytes 442376 | tf_op jit(solution)/shard_map/ppermute | solution.py:462
  26.9 1.1 collective-permute-start.5
  27.9 1.4 collective-permute-start.6
  29.4 3.7 %collective-permute-done.3 = bf16[4,104,768]{2,1,0:T(8,128)(2,1)S(1)} collective-permute-done((bf16[4,104,768]{2,1,0:T(8,128)(2,1)S(1)}, bf16[4,104,768]{2,1,0:T(8,128)(2,1)S(1)}, u32[]{:S(2)}, u32[]{:S(2)}) %collective-permute-start.3) | collective-permute-done | bytes 639008 | tf_op jit(solution)/shard_map/ppermute | solution.py:462
  33.1 6.4 %collective-permute-done.5 = bf16[1,96,768]{2,1,0:T(8,128)(2,1)S(1)} collective-permute-done((bf16[1,96,768]{2,1,0:T(8,128)(2,1)S(1)}, bf16[1,96,768]{2,1,0:T(8,128)(2,1)S(1)}, u32[]{:S(2)}, u32[]{:S(2)}) %collective-permute-start.5) | collective-permute-done | bytes 147488 | tf_op jit(solution)/shard_map/ppermute | solution.py:462
  40.2 1.6 collective-permute-start.8
  41.8 3.3 %collective-permute-start.10 = (bf16[1,96,768]{2,1,0:T(8,128)(2,1)S(1)}, bf16[1,96,768]{2,1,0:T(8,128)(2,1)S(1)}, u32[]{:S(2)}, u32[]{:S(2)}) collective-permute-start(bf16[1,96,768]{2,1,0:T(8,128)(2,1)S(1)} %bitcast.150), channel_id=1, source_target_pairs={{0,2},{1,3},{2,0},{3,1},{4,6},{5,7},{6,4},{7,5},{8,10},{9,11},{10,... | collective-permute-start | bytes 442376 | tf_op jit(solution)/shard_map/ppermute | solution.py:462
  45.1 1.2 collective-permute-start.11
  46.3 0.7 constant_dynamic-update-slice_fusion.9
  47.0 0.7 constant_dynamic-update-slice_fusion.8
  47.6 7.0 %collective-permute-done.10 = bf16[1,96,768]{2,1,0:T(8,128)(2,1)S(1)} collective-permute-done((bf16[1,96,768]{2,1,0:T(8,128)(2,1)S(1)}, bf16[1,96,768]{2,1,0:T(8,128)(2,1)S(1)}, u32[]{:S(2)}, u32[]{:S(2)}) %collective-permute-start.10) | collective-permute-done | bytes 147488 | tf_op jit(solution)/shard_map/ppermute | solution.py:462
  54.6 0.7 collective-permute-done.9
  55.3 1.1 collective-permute-done.8
  56.5 4.2 %collective-permute-done.7 = bf16[8,104,768]{2,1,0:T(8,128)(2,1)S(1)} collective-permute-done((bf16[8,104,768]{2,1,0:T(8,128)(2,1)S(1)}, bf16[8,104,768]{2,1,0:T(8,128)(2,1)S(1)}, u32[]{:S(2)}, u32[]{:S(2)}) %collective-permute-start.7) | collective-permute-done | bytes 1277984 | tf_op jit(solution)/shard_map/ppermute | solution.py:462
  62.5 0.9 constant_dynamic-update-slice_fusion.5
  63.7 1.3 copy.35.x_ref
  65.2 1.3 pad_maximum_fusion.2
  66.9 11.7 %shard_map.255 = (bf16[4,384,576]{2,1,0:T(8,128)(2,1)}, f32[4,3,128,384]{3,2,1,0:T(8,128)}, bf16[4,384,256]{2,1,0:T(8,128)(2,1)}, f32[384,768]{1,0:T(8,128)S(1)}...) custom-call(bf16[384,768]{1,0:T(8,128)(2,1)S(1)} %copy.35.x_ref, ...), custom_call_target="tpu_custom_call" | custom-call | flops 300000000 | tf_op jit(solution)/shard_map/pallas_call | solution.py:418
  78.7 4.1 %collective-permute-done.17 = bf16[4,96,768]{2,1,0:T(8,128)(2,1)S(1)} collective-permute-done((bf16[4,96,768]{2,1,0:T(8,128)(2,1)S(1)}, bf16[4,96,768]{2,1,0:T(8,128)(2,1)S(1)}, u32[]{:S(2)}, u32[]{:S(2)}) %collective-permute-start.17) | collective-permute-done | bytes 589856 | tf_op jit(solution)/shard_map/ppermute | solution.py:462
  82.8 3.4 %collective-permute-done.14 = bf16[8,96,768]{2,1,0:T(8,128)(2,1)} collective-permute-done((bf16[8,96,768]{2,1,0:T(8,128)(2,1)}, bf16[8,96,768]{2,1,0:T(8,128)(2,1)}, u32[]{:S(2)}, u32[]{:S(2)}) %collective-permute-start.14) | collective-permute-done | bytes 1179680 | tf_op jit(solution)/shard_map/ppermute | solution.py:462
  87.0 15.4 %collective-permute-done.18 = bf16[8,96,768]{2,1,0:T(8,128)(2,1)S(1)} collective-permute-done((bf16[8,96,768]{2,1,0:T(8,128)(2,1)S(1)}, bf16[8,96,768]{2,1,0:T(8,128)(2,1)S(1)}, u32[]{:S(2)}, u32[]{:S(2)}) %collective-permute-start.18) | collective-permute-done | bytes 1179680 | tf_op jit(solution)/shard_map/ppermute | solution.py:462
  102.4 4.9 %shard_map.256 = (bf16[4,384,768]{2,1,0:T(8,128)(2,1)S(1)}, f32[4,384,768]{2,1,0:T(8,128)S(1)}) custom-call(bf16[384,768]{1,0:T(8,128)(2,1)S(1)} %get-tuple-element.88.n_ref, bf16[2,4,96,768]{3,2,1,0:T(8,128)(2,1)} %bitcast.21.w0_ref, bf16[2,4,96,768]{3,2,1,0:T(8,128)(2,1)} %bitcast.22.w1_ref, bf16[2,4,96,768]{3,2,1,0:T(8,128)(2,1)S(1)} %bitcast.127, ...), custom_call_target="tpu_custom_call" | custom-call | flops 120000000 | tf_op jit(solution)/shard_map/pallas_call | solution.py:418
  107.9 5.7 %shard_map.257 = (f32[3,8,768]{2,1,0:T(8,128)S(1)}, f32[384,768]{1,0:T(8,128)S(1)}, bf16[384,768]{1,0:T(8,128)(2,1)S(1)}, bf16[384,384]{1,0:T(8,128)(2,1)S(1)}, ...) custom-call(bf16[4,384,768]{2,1,0:T(8,128)(2,1)S(1)} %get-tuple-element.93.z_ref.refs_1_, ...), custom_call_target="tpu_custom_call" | custom-call | flops 165000000 | tf_op jit(solution)/shard_map/pallas_call | solution.py:418
  113.6 3.0 %shard_map.258 = (bf16[4,384,768]{2,1,0:T(8,128)(2,1)S(1)}, f32[4,1,768]{2,1,0:T(1,128)S(1)}) custom-call(bf16[384,768]{1,0:T(8,128)(2,1)S(1)} %get-tuple-element.101.dbb_ref, bf16[2,4,96,768]{3,2,1,0:T(8,128)(2,1)S(1)} %bitcast.118, bf16[2,4,96,768]{3,2,1,0:T(8,128)(2,1)S(1)} %bitcast.120, bf16[2,4,96,768]{3,2,1,0:T(8,128)(2,1)S(1)} %bitcast.122, ...), custom_call_target="tpu_custom_call" | custom-call | flops 105000000 | tf_op jit(solution)/shard_map/pallas_call | solution.py:418
  117.2 4.4 %collective-permute-done.21.refs_2_ = bf16[384,384]{1,0:T(8,128)(2,1)S(1)} collective-permute-done((bf16[384,384]{1,0:T(8,128)(2,1)S(1)}, bf16[384,384]{1,0:T(8,128)(2,1)S(1)}, u32[]{:S(2)}, u32[]{:S(2)}) %collective-permute-start.21) | collective-permute-done | bytes 294944 | tf_op jit(solution)/shard_map/ppermute | solution.py:453
  121.7 3.2 %shard_map.259 = (bf16[2,4,96,768]{3,2,1,0:T(8,128)(2,1)S(1)}, bf16[2,4,96,768]{3,2,1,0:T(8,128)(2,1)S(1)}) custom-call(bf16[384,384]{1,0:T(8,128)(2,1)S(1)} %get-tuple-element.106.refs_0_, bf16[4,384,768]{2,1,0:T(8,128)(2,1)S(1)} %get-tuple-element.93.z_ref.refs_1_, bf16[384,384]{1,0:T(8,128)(2,1)S(1)} %collective-permute-done.21.refs_2_, ...), custom_call_target="tpu_custom_call" | custom-call | flops 120000000 | tf_op jit(solution)/shard_map/pallas_call | solution.py:418
  125.3 5.6 %shard_map.260 = (f32[384,768]{1,0:T(8,128)S(1)}, bf16[384,768]{1,0:T(8,128)(2,1)S(1)}, bf16[384,384]{1,0:T(8,128)(2,1)S(1)}, bf16[384,384]{1,0:T(8,128)(2,1)S(1)}, f32[3,768]{1,0:T(4,128)S(1)}) custom-call(bf16[4,384,768]{2,1,0:T(8,128)(2,1)S(1)} %get-tuple-element.109.du_ref.refs_1_, bf16[2,4,96,768]{3,2,1,0:T(8,128)(2,1)} %bitcast.21.w0_ref, ...), custom_call_target="tpu_custom_call" | custom-call | flops 150000000 | tf_op jit(solution)/shard_map/pallas_call | solution.py:418
  130.9 3.3 %shard_map.261 = (bf16[2,4,96,768]{3,2,1,0:T(8,128)(2,1)S(1)}, bf16[2,4,96,768]{3,2,1,0:T(8,128)(2,1)S(1)}) custom-call(bf16[384,384]{1,0:T(8,128)(2,1)S(1)} %copy-done.7, bf16[4,384,768]{2,1,0:T(8,128)(2,1)S(1)} %get-tuple-element.109.du_ref.refs_1_, bf16[384,384]{1,0:T(8,128)(2,1)S(1)} %collective-permute-done.23.refs_2_, ...), custom_call_target="tpu_custom_call" | custom-call | flops 120000000 | tf_op jit(solution)/shard_map/pallas_call | solution.py:418
  134.2 1.8 collective-permute-start.27
  136.0 5.2 %collective-permute-done.25 = bf16[8,96,768]{2,1,0:T(8,128)(2,1)S(1)} collective-permute-done((bf16[8,96,768]{2,1,0:T(8,128)(2,1)S(1)}, bf16[8,96,768]{2,1,0:T(8,128)(2,1)S(1)}, u32[]{:S(2)}, u32[]{:S(2)}) %collective-permute-start.25) | collective-permute-done | bytes 1179680 | tf_op jit(solution)/shard_map/ppermute | solution.py:480
  141.2 8.7 %shard_map.262 = (bf16[2,384,640]{2,1,0:T(8,128)(2,1)S(1)}, bf16[2,384,640]{2,1,0:T(8,128)(2,1)S(1)}, f32[4,4,768]{2,1,0:T(4,128)S(1)}, f32[4,4,768]{2,1,0:T(4,128)S(1)}) custom-call(bf16[384,768]{1,0:T(8,128)(2,1)S(1)} %get-tuple-element.121.dab_ref, bf16[2,4,104,768]{3,2,1,0:T(8,128)(2,1)S(1)} %bitcast.111, bf16[2,4,104,768]{3,2,1,0:T(8,128)(2,1)S(1)} %bitcast.115, ...), custom_call_target="tpu_custom_call" | custom-call | flops 240000000 | tf_op jit(solution)/shard_map/pallas_call | solution.py:418
  151.6 9.1 %collective-permute-done.26 = bf16[4,96,768]{2,1,0:T(8,128)(2,1)S(1)} collective-permute-done((bf16[4,96,768]{2,1,0:T(8,128)(2,1)S(1)}, bf16[4,96,768]{2,1,0:T(8,128)(2,1)S(1)}, u32[]{:S(2)}, u32[]{:S(2)}) %collective-permute-start.26) | collective-permute-done | bytes 589856 | tf_op jit(solution)/shard_map/ppermute | solution.py:480
  161.2 1.1 collective-permute-done.31.refs_8_
  162.3 4.2 %shard_map.263 = (bf16[2,4,104,768]{3,2,1,0:T(8,128)(2,1)S(1)}, bf16[2,4,104,768]{3,2,1,0:T(8,128)(2,1)S(1)}) custom-call(bf16[384,384]{1,0:T(8,128)(2,1)S(1)} %copy-done.4, bf16[2,384,640]{2,1,0:T(8,128)(2,1)S(1)} %get-tuple-element.136.refs_1_.low_ref, bf16[2,384,640]{2,1,0:T(8,128)(2,1)S(1)} %get-tuple-element.137.refs_2_.high_ref, ...), custom_call_target="tpu_custom_call" | custom-call | flops 120000000 | tf_op jit(solution)/shard_map/pallas_call | solution.py:418
  167.1 0.7 copy.38
  168.9 4.0 %collective-permute-start.35 = (bf16[1,96,768]{2,1,0:T(8,128)(2,1)S(1)}, bf16[1,96,768]{2,1,0:T(8,128)(2,1)S(1)}, u32[]{:S(2)}, u32[]{:S(2)}) collective-permute-start(bf16[1,96,768]{2,1,0:T(8,128)(2,1)S(1)} %get-tuple-element.188), channel_id=1, source_target_pairs={{0,1},{1,0},{2,3},{3,2},{4,5},{5,4},{6,7},{7,6},{8,9},{9,8},{10,11... | collective-permute-start | bytes 442376 | tf_op jit(solution)/shard_map/ppermute | solution.py:480
  173.0 2.0 collective-permute-start.36
  175.0 1.4 collective-permute-start.37
  176.3 7.2 %shard_map.264 = f32[384,768]{1,0:T(8,128)} custom-call(bf16[2,384,640]{2,1,0:T(8,128)(2,1)S(1)} %get-tuple-element.136.refs_1_.low_ref, bf16[2,384,640]{2,1,0:T(8,128)(2,1)S(1)} %get-tuple-element.137.refs_2_.high_ref, bf16[2,4,104,768]{3,2,1,0:T(8,128)(2,1)S(1)} %bitcast.112, bf16[2,4,104,768]{3,2,1,0:T(8,128)(2,1)S(1)} %bitcast.116, ...), custom_call_target="tpu_custom_call" | custom-call | flops 120000000 | tf_op jit(solution)/shard_map/pallas_call | solution.py:418
  183.6 6.6 %collective-permute-done.34 = bf16[8,104,768]{2,1,0:T(8,128)(2,1)S(1)} collective-permute-done((bf16[8,104,768]{2,1,0:T(8,128)(2,1)S(1)}, bf16[8,104,768]{2,1,0:T(8,128)(2,1)S(1)}, u32[]{:S(2)}, u32[]{:S(2)}) %collective-permute-start.34) | collective-permute-done | bytes 1277984 | tf_op jit(solution)/shard_map/ppermute | solution.py:480
  190.9 2.0 fusion.8
  192.8 0.8 fusion.20
  193.7 3.7 %collective-permute-start.40 = (bf16[1,96,768]{2,1,0:T(8,128)(2,1)S(1)}, bf16[1,96,768]{2,1,0:T(8,128)(2,1)S(1)}, u32[]{:S(2)}, u32[]{:S(2)}) collective-permute-start(bf16[1,96,768]{2,1,0:T(8,128)(2,1)S(1)} %get-tuple-element.185), channel_id=1, source_target_pairs={{0,1},{1,0},{2,3},{3,2},{4,5},{5,4},{6,7},{7,6},{8,9},{9,8},{10,11... | collective-permute-start | bytes 442376 | tf_op jit(solution)/shard_map/ppermute | solution.py:480
  197.4 2.0 collective-permute-start.41
  199.4 1.4 collective-permute-start.42
  201.1 1.1 collective-permute-done.40
  202.2 9.1 %collective-permute-done.41 = bf16[1,96,768]{2,1,0:T(8,128)(2,1)S(1)} collective-permute-done((bf16[1,96,768]{2,1,0:T(8,128)(2,1)S(1)}, bf16[1,96,768]{2,1,0:T(8,128)(2,1)S(1)}, u32[]{:S(2)}, u32[]{:S(2)}) %collective-permute-start.41) | collective-permute-done | bytes 147488 | tf_op jit(solution)/shard_map/ppermute | solution.py:480
  211.3 2.1 collective-permute-start.43
  213.5 1.2 collective-permute-start.44
  214.7 1.5 collective-permute-start.45
  216.1 0.8 fusion.24
  216.9 1.6 collective-permute-done.43
  218.5 8.9 %collective-permute-done.44 = bf16[1,104,768]{2,1,0:T(8,128)(2,1)S(1)} collective-permute-done((bf16[1,104,768]{2,1,0:T(8,128)(2,1)S(1)}, bf16[1,104,768]{2,1,0:T(8,128)(2,1)S(1)}, u32[]{:S(2)}, u32[]{:S(2)}) %collective-permute-start.44) | collective-permute-done | bytes 159776 | tf_op jit(solution)/shard_map/ppermute | solution.py:480
  228.8 0.7 copy.40
  230.1 0.7 pad_maximum_fusion.3
  (148 shorter events, 14.1 us)
Async XLA Ops:
  0.6 10.6 %copy-start = (bf16[3,128,768]{2,1,0:T(8,128)(2,1)S(1)}, bf16[3,128,768]{2,1,0:T(8,128)(2,1)}, u32[]{:S(2)}) copy-start(bf16[3,128,768]{2,1,0:T(8,128)(2,1)} %param.15) | copy-start | bytes 1769476
  4.5 9.7 %collective-permute-start = (bf16[1,104,768]{2,1,0:T(8,128)(2,1)}, bf16[1,104,768]{2,1,0:T(8,128)(2,1)S(1)}, u32[]{:S(2)}, u32[]{:S(2)}) collective-permute-start(bf16[1,104,768]{2,1,0:T(8,128)(2,1)} %bitcast.141), channel_id=1, source_target_pairs={{0,1},{1,0},{2,3},{3,2},{4,5},{5,4},{6,7},{7,6},{8,9},{9,8},{10,11... | collective-permute-start | bytes 479240 | tf_op jit(solution)/shard_map/ppermute | solution.py:462
  7.5 15.0 %collective-permute-start.1 = (bf16[1,104,768]{2,1,0:T(8,128)(2,1)}, bf16[1,104,768]{2,1,0:T(8,128)(2,1)S(1)}, u32[]{:S(2)}, u32[]{:S(2)}) collective-permute-start(bf16[1,104,768]{2,1,0:T(8,128)(2,1)} %bitcast.142), channel_id=1, source_target_pairs={{0,2},{1,3},{2,0},{3,1},{4,6},{5,7},{6,4},{7,5},{8,10},{9,11},{10,... | collective-permute-start | bytes 479240 | tf_op jit(solution)/shard_map/ppermute | solution.py:462
  10.1 12.4 %collective-permute-start.2 = (bf16[1,104,768]{2,1,0:T(8,128)(2,1)}, bf16[1,104,768]{2,1,0:T(8,128)(2,1)S(1)}, u32[]{:S(2)}, u32[]{:S(2)}) collective-permute-start(bf16[1,104,768]{2,1,0:T(8,128)(2,1)} %bitcast.143), channel_id=1, source_target_pairs={{0,3},{1,2},{2,1},{3,0},{4,7},{5,6},{6,5},{7,4},{8,11},{9,10},{10,... | collective-permute-start | bytes 479240 | tf_op jit(solution)/shard_map/ppermute | solution.py:462
  12.0 10.6 %copy-start.9 = (bf16[768,384]{1,0:T(8,128)(2,1)}, bf16[768,384]{1,0:T(8,128)(2,1)S(1)}, u32[]{:S(2)}) copy-start(bf16[768,384]{1,0:T(8,128)(2,1)S(1)} %convolution_convert_fusion) | copy-start | bytes 1769476
  12.1 10.5 %copy-start.10 = (bf16[104,768]{1,0:T(8,128)(2,1)S(1)}, bf16[104,768]{1,0:T(8,128)(2,1)}, u32[]{:S(2)}) copy-start(bf16[104,768]{1,0:T(8,128)(2,1)} %get-tuple-element.79) | copy-start | bytes 479236
  13.0 11.2 %copy-start.11 = (bf16[96,768]{1,0:T(8,128)(2,1)S(1)}, bf16[96,768]{1,0:T(8,128)(2,1)}, u32[]{:S(2)}) copy-start(bf16[96,768]{1,0:T(8,128)(2,1)} %param.24) | copy-start | bytes 442372
  22.6 10.5 %collective-permute-start.3 = (bf16[4,104,768]{2,1,0:T(8,128)(2,1)S(1)}, bf16[4,104,768]{2,1,0:T(8,128)(2,1)S(1)}, u32[]{:S(2)}, u32[]{:S(2)}) collective-permute-start(bf16[4,104,768]{2,1,0:T(8,128)(2,1)S(1)} %pad_maximum_fusion), channel_id=1, source_target_pairs={{0,16},{1,17},{2,18},{3,19},{4,12},{5,13},{6,14},{7,15},{8,24},{9,... | collective-permute-start | bytes 1916936 | tf_op jit(solution)/shard_map/ppermute | solution.py:462
  24.2 8.9 %collective-permute-start.4 = (bf16[1,96,768]{2,1,0:T(8,128)(2,1)S(1)}, bf16[1,96,768]{2,1,0:T(8,128)(2,1)S(1)}, u32[]{:S(2)}, u32[]{:S(2)}) collective-permute-start(bf16[1,96,768]{2,1,0:T(8,128)(2,1)S(1)} %bitcast.145), channel_id=1, source_target_pairs={{0,1},{1,0},{2,3},{3,2},{4,5},{5,4},{6,7},{7,6},{8,9},{9,8},{10,11... | collective-permute-start | bytes 442376 | tf_op jit(solution)/shard_map/ppermute | solution.py:462
  26.9 12.7 %collective-permute-start.5 = (bf16[1,96,768]{2,1,0:T(8,128)(2,1)S(1)}, bf16[1,96,768]{2,1,0:T(8,128)(2,1)S(1)}, u32[]{:S(2)}, u32[]{:S(2)}) collective-permute-start(bf16[1,96,768]{2,1,0:T(8,128)(2,1)S(1)} %bitcast.146), channel_id=1, source_target_pairs={{0,2},{1,3},{2,0},{3,1},{4,6},{5,7},{6,4},{7,5},{8,10},{9,11},{10,... | collective-permute-start | bytes 442376 | tf_op jit(solution)/shard_map/ppermute | solution.py:462
  27.9 11.6 %collective-permute-start.6 = (bf16[1,96,768]{2,1,0:T(8,128)(2,1)S(1)}, bf16[1,96,768]{2,1,0:T(8,128)(2,1)S(1)}, u32[]{:S(2)}, u32[]{:S(2)}) collective-permute-start(bf16[1,96,768]{2,1,0:T(8,128)(2,1)S(1)} %bitcast.147), channel_id=1, source_target_pairs={{0,3},{1,2},{2,1},{3,0},{4,7},{5,6},{6,5},{7,4},{8,11},{9,10},{10,... | collective-permute-start | bytes 442376 | tf_op jit(solution)/shard_map/ppermute | solution.py:462
  29.4 12.4 %copy-start.12 = (bf16[96,768]{1,0:T(8,128)(2,1)S(1)}, bf16[96,768]{1,0:T(8,128)(2,1)}, u32[]{:S(2)}) copy-start(bf16[96,768]{1,0:T(8,128)(2,1)} %get-tuple-element.84) | copy-start | bytes 442372
  39.6 21.1 %collective-permute-start.7 = (bf16[8,104,768]{2,1,0:T(8,128)(2,1)S(1)}, bf16[8,104,768]{2,1,0:T(8,128)(2,1)S(1)}, u32[]{:S(2)}, u32[]{:S(2)}) collective-permute-start(bf16[8,104,768]{2,1,0:T(8,128)(2,1)S(1)} %constant_dynamic-update-slice_fusion), channel_id=1, source_target_pairs={{0,8},{1,9},{2,10},{3,11},{4,20},{5,21},{6,22},{7,23},{8,0},{9,1},... | collective-permute-start | bytes 3833864 | tf_op jit(solution)/shard_map/ppermute | solution.py:462
  40.2 16.3 %collective-permute-start.8 = (bf16[4,96,768]{2,1,0:T(8,128)(2,1)S(1)}, bf16[4,96,768]{2,1,0:T(8,128)(2,1)S(1)}, u32[]{:S(2)}, u32[]{:S(2)}) collective-permute-start(bf16[4,96,768]{2,1,0:T(8,128)(2,1)S(1)} %pad_maximum_fusion.1), channel_id=1, source_target_pairs={{0,16},{1,17},{2,18},{3,19},{4,12},{5,13},{6,14},{7,15},{8,24},{9,... | collective-permute-start | bytes 1769480 | tf_op jit(solution)/shard_map/ppermute | solution.py:462
  41.8 12.8 %collective-permute-start.10 = (bf16[1,96,768]{2,1,0:T(8,128)(2,1)S(1)}, bf16[1,96,768]{2,1,0:T(8,128)(2,1)S(1)}, u32[]{:S(2)}, u32[]{:S(2)}) collective-permute-start(bf16[1,96,768]{2,1,0:T(8,128)(2,1)S(1)} %bitcast.150), channel_id=1, source_target_pairs={{0,2},{1,3},{2,0},{3,1},{4,6},{5,7},{6,4},{7,5},{8,10},{9,11},{10,... | collective-permute-start | bytes 442376 | tf_op jit(solution)/shard_map/ppermute | solution.py:462
  45.1 9.6 %collective-permute-start.11 = (bf16[1,96,768]{2,1,0:T(8,128)(2,1)S(1)}, bf16[1,96,768]{2,1,0:T(8,128)(2,1)S(1)}, u32[]{:S(2)}, u32[]{:S(2)}) collective-permute-start(bf16[1,96,768]{2,1,0:T(8,128)(2,1)S(1)} %bitcast.151), channel_id=1, source_target_pairs={{0,3},{1,2},{2,1},{3,0},{4,7},{5,6},{6,5},{7,4},{8,11},{9,10},{10,... | collective-permute-start | bytes 442376 | tf_op jit(solution)/shard_map/ppermute | solution.py:462
  46.3 9.0 %collective-permute-start.9 = (bf16[1,96,768]{2,1,0:T(8,128)(2,1)S(1)}, bf16[1,96,768]{2,1,0:T(8,128)(2,1)S(1)}, u32[]{:S(2)}, u32[]{:S(2)}) collective-permute-start(bf16[1,96,768]{2,1,0:T(8,128)(2,1)S(1)} %bitcast.152), channel_id=1, source_target_pairs={{0,1},{1,0},{2,3},{3,2},{4,5},{5,4},{6,7},{7,6},{8,9},{9,8},{10,11... | collective-permute-start | bytes 442376 | tf_op jit(solution)/shard_map/ppermute | solution.py:462
  54.6 7.2 %copy-start.14 = (bf16[1,96,768]{2,1,0:T(8,128)(2,1)}, bf16[1,96,768]{2,1,0:T(8,128)(2,1)S(1)}, u32[]{:S(2)}) copy-start(bf16[1,96,768]{2,1,0:T(8,128)(2,1)S(1)} %collective-permute-done.10) | copy-start | bytes 442372
  54.6 7.2 %copy-start.16 = (bf16[1,96,768]{2,1,0:T(8,128)(2,1)}, bf16[1,96,768]{2,1,0:T(8,128)(2,1)S(1)}, u32[]{:S(2)}) copy-start(bf16[1,96,768]{2,1,0:T(8,128)(2,1)S(1)} %collective-permute-done.11) | copy-start | bytes 442372
  55.3 8.0 %copy-start.18 = (bf16[1,96,768]{2,1,0:T(8,128)(2,1)}, bf16[1,96,768]{2,1,0:T(8,128)(2,1)S(1)}, u32[]{:S(2)}) copy-start(bf16[1,96,768]{2,1,0:T(8,128)(2,1)S(1)} %collective-permute-done.9) | copy-start | bytes 442372
  60.7 6.2 %collective-permute-start.13 = (bf16[8,104,768]{2,1,0:T(8,128)(2,1)S(1)}, bf16[8,104,768]{2,1,0:T(8,128)(2,1)}, u32[]{:S(2)}, u32[]{:S(2)}) collective-permute-start(bf16[8,104,768]{2,1,0:T(8,128)(2,1)S(1)} %collective-permute-done.7), channel_id=1, source_target_pairs={{0,4},{1,5},{2,6},{3,7},{4,0},{5,1},{6,2},{7,3},{8,12},{9,13},{10,... | collective-permute-start | bytes 3833864 | tf_op jit(solution)/shard_map/ppermute | solution.py:462
  60.7 6.3 %collective-permute-start.12 = (bf16[8,104,768]{2,1,0:T(8,128)(2,1)S(1)}, bf16[8,104,768]{2,1,0:T(8,128)(2,1)}, u32[]{:S(2)}, u32[]{:S(2)}) collective-permute-start(bf16[8,104,768]{2,1,0:T(8,128)(2,1)S(1)} %constant_dynamic-update-slice_fusion), channel_id=1, source_target_pairs={{0,4},{1,5},{2,6},{3,7},{4,0},{5,1},{6,2},{7,3},{8,12},{9,13},{10,... | collective-permute-start | bytes 3833864 | tf_op jit(solution)/shard_map/ppermute | solution.py:462
  62.5 2.5 %copy-start.22 = (s32[3,1,128]{2,1,0:T(1,128)S(1)}, s32[3,1,128]{2,1,0:T(1,128)}, u32[]{:S(2)}) copy-start(s32[3,1,128]{2,1,0:T(1,128)} %param.16) | copy-start | bytes 4612
  63.4 22.8 %collective-permute-start.14 = (bf16[8,96,768]{2,1,0:T(8,128)(2,1)}, bf16[8,96,768]{2,1,0:T(8,128)(2,1)}, u32[]{:S(2)}, u32[]{:S(2)}) collective-permute-start(bf16[8,96,768]{2,1,0:T(8,128)(2,1)} %constant_dynamic-update-slice_fusion.5), channel_id=1, source_target_pairs={{0,8},{1,9},{2,10},{3,11},{4,20},{5,21},{6,22},{7,23},{8,0},{9,1},... | collective-permute-start | bytes 3538952 | tf_op jit(solution)/shard_map/ppermute | solution.py:462
  66.4 16.3 %collective-permute-start.17 = (bf16[4,96,768]{2,1,0:T(8,128)(2,1)S(1)}, bf16[4,96,768]{2,1,0:T(8,128)(2,1)S(1)}, u32[]{:S(2)}, u32[]{:S(2)}) collective-permute-start(bf16[4,96,768]{2,1,0:T(8,128)(2,1)S(1)} %pad_maximum_fusion.2), channel_id=1, source_target_pairs={{0,16},{1,17},{2,18},{3,19},{4,12},{5,13},{6,14},{7,15},{8,24},{9,... | collective-permute-start | bytes 1769480 | tf_op jit(solution)/shard_map/ppermute | solution.py:462
  86.2 16.2 %collective-permute-start.18 = (bf16[8,96,768]{2,1,0:T(8,128)(2,1)S(1)}, bf16[8,96,768]{2,1,0:T(8,128)(2,1)S(1)}, u32[]{:S(2)}, u32[]{:S(2)}) collective-permute-start(bf16[8,96,768]{2,1,0:T(8,128)(2,1)S(1)} %constant_dynamic-update-slice_fusion.10), channel_id=1, source_target_pairs={{0,8},{1,9},{2,10},{3,11},{4,20},{5,21},{6,22},{7,23},{8,0},{9,1},... | collective-permute-start | bytes 3538952 | tf_op jit(solution)/shard_map/ppermute | solution.py:462
  86.5 15.9 %collective-permute-start.16 = (bf16[8,96,768]{2,1,0:T(8,128)(2,1)}, bf16[8,96,768]{2,1,0:T(8,128)(2,1)S(1)}, u32[]{:S(2)}, u32[]{:S(2)}) collective-permute-start(bf16[8,96,768]{2,1,0:T(8,128)(2,1)} %collective-permute-done.14), channel_id=1, source_target_pairs={{0,4},{1,5},{2,6},{3,7},{4,0},{5,1},{6,2},{7,3},{8,12},{9,13},{10,... | collective-permute-start | bytes 3538952 | tf_op jit(solution)/shard_map/ppermute | solution.py:462
  86.5 15.9 %collective-permute-start.15 = (bf16[8,96,768]{2,1,0:T(8,128)(2,1)}, bf16[8,96,768]{2,1,0:T(8,128)(2,1)S(1)}, u32[]{:S(2)}, u32[]{:S(2)}) collective-permute-start(bf16[8,96,768]{2,1,0:T(8,128)(2,1)} %constant_dynamic-update-slice_fusion.5), channel_id=1, source_target_pairs={{0,4},{1,5},{2,6},{3,7},{4,0},{5,1},{6,2},{7,3},{8,12},{9,13},{10,... | collective-permute-start | bytes 3538952 | tf_op jit(solution)/shard_map/ppermute | solution.py:462
  87.0 20.9 %collective-permute-start.19 = (bf16[8,96,768]{2,1,0:T(8,128)(2,1)S(1)}, bf16[8,96,768]{2,1,0:T(8,128)(2,1)S(1)}, u32[]{:S(2)}, u32[]{:S(2)}) collective-permute-start(bf16[8,96,768]{2,1,0:T(8,128)(2,1)S(1)} %constant_dynamic-update-slice_fusion.10), channel_id=1, source_target_pairs={{0,4},{1,5},{2,6},{3,7},{4,0},{5,1},{6,2},{7,3},{8,12},{9,13},{10,... | collective-permute-start | bytes 3538952 | tf_op jit(solution)/shard_map/ppermute | solution.py:462
  102.4 5.5 %collective-permute-start.20 = (bf16[8,96,768]{2,1,0:T(8,128)(2,1)S(1)}, bf16[8,96,768]{2,1,0:T(8,128)(2,1)S(1)}, u32[]{:S(2)}, u32[]{:S(2)}) collective-permute-start(bf16[8,96,768]{2,1,0:T(8,128)(2,1)S(1)} %collective-permute-done.18), channel_id=1, source_target_pairs={{0,4},{1,5},{2,6},{3,7},{4,0},{5,1},{6,2},{7,3},{8,12},{9,13},{10,... | collective-permute-start | bytes 3538952 | tf_op jit(solution)/shard_map/ppermute | solution.py:462
  107.4 14.3 %collective-permute-start.22 = (bf16[4,384,768]{2,1,0:T(8,128)(2,1)S(1)}, bf16[4,384,768]{2,1,0:T(8,128)(2,1)S(1)}, u32[]{:S(2)}, u32[]{:S(2)}) collective-permute-start(bf16[4,384,768]{2,1,0:T(8,128)(2,1)S(1)} %get-tuple-element.93.z_ref.refs_1_), channel_id=1, source_target_pairs={{0,4},{1,5},{2,6},{3,7},{4,0},{5,1},{6,2},{7,3},{8,12},{9,13},{10,... | collective-permute-start | bytes 7077896 | tf_op jit(solution)/shard_map/ppermute | solution.py:453
  116.6 14.3 %collective-permute-start.24 = (bf16[4,384,768]{2,1,0:T(8,128)(2,1)S(1)}, bf16[4,384,768]{2,1,0:T(8,128)(2,1)S(1)}, u32[]{:S(2)}, u32[]{:S(2)}) collective-permute-start(bf16[4,384,768]{2,1,0:T(8,128)(2,1)S(1)} %get-tuple-element.109.du_ref.refs_1_), channel_id=1, source_target_pairs={{0,4},{1,5},{2,6},{3,7},{4,0},{5,1},{6,2},{7,3},{8,12},{9,13},{10,... | collective-permute-start | bytes 7077896 | tf_op jit(solution)/shard_map/ppermute | solution.py:453
  116.7 4.9 %collective-permute-start.21 = (bf16[384,384]{1,0:T(8,128)(2,1)S(1)}, bf16[384,384]{1,0:T(8,128)(2,1)S(1)}, u32[]{:S(2)}, u32[]{:S(2)}) collective-permute-start(bf16[384,384]{1,0:T(8,128)(2,1)S(1)} %get-tuple-element.107), channel_id=1, source_target_pairs={{0,4},{1,5},{2,6},{3,7},{4,0},{5,1},{6,2},{7,3},{8,12},{9,13},{10,... | collective-permute-start | bytes 884744 | tf_op jit(solution)/shard_map/ppermute | solution.py:453
  117.2 8.1 %copy-start.23 = (bf16[384,384]{1,0:T(8,128)(2,1)S(1)}, bf16[384,384]{1,0:T(8,128)(2,1)}, u32[]{:S(2)}) copy-start(bf16[384,384]{1,0:T(8,128)(2,1)} %get-tuple-element.117) | copy-start | bytes 884740
  117.2 8.1 %copy-start.5 = (f32[384,768]{1,0:T(8,128)S(1)}, f32[384,768]{1,0:T(8,128)}, u32[]{:S(2)}) copy-start(f32[384,768]{1,0:T(8,128)} %get-tuple-element.111.x1_ref) | copy-start | bytes 3538948
  117.2 8.1 %copy-start.8 = (f32[384,1]{1,0:T(8,128)S(1)}, f32[384,1]{1,0:T(8,128)}, u32[]{:S(2)}) copy-start(f32[384,1]{1,0:T(8,128)} %get-tuple-element.112.r1_ref) | copy-start | bytes 4612
  124.9 16.3 %collective-permute-start.25 = (bf16[8,96,768]{2,1,0:T(8,128)(2,1)S(1)}, bf16[8,96,768]{2,1,0:T(8,128)(2,1)S(1)}, u32[]{:S(2)}, u32[]{:S(2)}) collective-permute-start(bf16[8,96,768]{2,1,0:T(8,128)(2,1)S(1)} %bitcast.133), channel_id=1, source_target_pairs={{0,8},{1,9},{2,10},{3,11},{4,20},{5,21},{6,22},{7,23},{8,0},{9,1},... | collective-permute-start | bytes 3538952 | tf_op jit(solution)/shard_map/ppermute | solution.py:480
  125.3 5.6 %collective-permute-start.23 = (bf16[384,384]{1,0:T(8,128)(2,1)S(1)}, bf16[384,384]{1,0:T(8,128)(2,1)S(1)}, u32[]{:S(2)}, u32[]{:S(2)}) collective-permute-start(bf16[384,384]{1,0:T(8,128)(2,1)S(1)} %copy-done.23), channel_id=1, source_target_pairs={{0,4},{1,5},{2,6},{3,7},{4,0},{5,1},{6,2},{7,3},{8,12},{9,13},{10,... | collective-permute-start | bytes 884744 | tf_op jit(solution)/shard_map/ppermute | solution.py:453
  125.3 5.6 %copy-start.7 = (bf16[384,384]{1,0:T(8,128)(2,1)S(1)}, bf16[384,384]{1,0:T(8,128)(2,1)}, u32[]{:S(2)}) copy-start(bf16[384,384]{1,0:T(8,128)(2,1)} %get-tuple-element.116.refs_0_) | copy-start | bytes 884740
  130.9 5.1 %copy-start.20 = (bf16[384,384]{1,0:T(8,128)(2,1)S(1)}, bf16[384,384]{1,0:T(8,128)(2,1)}, u32[]{:S(2)}) copy-start(bf16[384,384]{1,0:T(8,128)(2,1)} %get-tuple-element.130) | copy-start | bytes 884740
  130.9 10.3 %copy-start.2 = (f32[4,3,128,384]{3,2,1,0:T(8,128)S(1)}, f32[4,3,128,384]{3,2,1,0:T(8,128)}, u32[]{:S(2)}) copy-start(f32[4,3,128,384]{3,2,1,0:T(8,128)} %get-tuple-element.123.p_ref) | copy-start | bytes 7077892
  130.9 10.3 %copy-start.3 = (bf16[4,384,576]{2,1,0:T(8,128)(2,1)S(1)}, bf16[4,384,576]{2,1,0:T(8,128)(2,1)}, u32[]{:S(2)}) copy-start(bf16[4,384,576]{2,1,0:T(8,128)(2,1)} %get-tuple-element.122.qkv_ref) | copy-start | bytes 5308420
  134.2 26.5 %collective-permute-start.27 = (bf16[8,96,768]{2,1,0:T(8,128)(2,1)S(1)}, bf16[8,96,768]{2,1,0:T(8,128)(2,1)S(1)}, u32[]{:S(2)}, u32[]{:S(2)}) collective-permute-start(bf16[8,96,768]{2,1,0:T(8,128)(2,1)S(1)} %bitcast.132), channel_id=1, source_target_pairs={{0,8},{1,9},{2,10},{3,11},{4,20},{5,21},{6,22},{7,23},{8,0},{9,1},... | collective-permute-start | bytes 3538952 | tf_op jit(solution)/shard_map/ppermute | solution.py:480
  136.0 15.0 %collective-permute-start.28 = (bf16[384,384]{1,0:T(8,128)(2,1)S(1)}, bf16[384,384]{1,0:T(8,128)(2,1)S(1)}, u32[]{:S(2)}, u32[]{:S(2)}) collective-permute-start(bf16[384,384]{1,0:T(8,128)(2,1)S(1)} %copy-done.20), channel_id=1, source_target_pairs={{0,4},{1,5},{2,6},{3,7},{4,0},{5,1},{6,2},{7,3},{8,12},{9,13},{10,... | collective-permute-start | bytes 884744 | tf_op jit(solution)/shard_map/ppermute | solution.py:453
  149.9 12.4 %collective-permute-start.29 = (bf16[2,384,640]{2,1,0:T(8,128)(2,1)S(1)}, bf16[2,384,640]{2,1,0:T(8,128)(2,1)S(1)}, u32[]{:S(2)}, u32[]{:S(2)}) collective-permute-start(bf16[2,384,640]{2,1,0:T(8,128)(2,1)S(1)} %get-tuple-element.136.refs_1_.low_ref), channel_id=1, source_target_pairs={{0,4},{1,5},{2,6},{3,7},{4,0},{5,1},{6,2},{7,3},{8,12},{9,13},{10,... | collective-permute-start | bytes 2949128 | tf_op jit(solution)/shard_map/ppermute | solution.py:453
  150.0 12.4 %copy-start.4 = (bf16[384,384]{1,0:T(8,128)(2,1)S(1)}, bf16[384,384]{1,0:T(8,128)(2,1)}, u32[]{:S(2)}) copy-start(bf16[384,384]{1,0:T(8,128)(2,1)} %get-tuple-element.128.refs_0_) | copy-start | bytes 884740
  150.0 12.3 %collective-permute-start.30 = (bf16[2,384,640]{2,1,0:T(8,128)(2,1)S(1)}, bf16[2,384,640]{2,1,0:T(8,128)(2,1)S(1)}, u32[]{:S(2)}, u32[]{:S(2)}) collective-permute-start(bf16[2,384,640]{2,1,0:T(8,128)(2,1)S(1)} %get-tuple-element.137.refs_2_.high_ref), channel_id=1, source_target_pairs={{0,4},{1,5},{2,6},{3,7},{4,0},{5,1},{6,2},{7,3},{8,12},{9,13},{10,... | collective-permute-start | bytes 2949128 | tf_op jit(solution)/shard_map/ppermute | solution.py:453
  150.7 9.9 %collective-permute-start.26 = (bf16[4,96,768]{2,1,0:T(8,128)(2,1)S(1)}, bf16[4,96,768]{2,1,0:T(8,128)(2,1)S(1)}, u32[]{:S(2)}, u32[]{:S(2)}) collective-permute-start(bf16[4,96,768]{2,1,0:T(8,128)(2,1)S(1)} %get-tuple-element.179), channel_id=1, source_target_pairs={{0,16},{1,17},{2,18},{3,19},{4,12},{5,13},{6,14},{7,15},{8,24},{9,... | collective-permute-start | bytes 1769480 | tf_op jit(solution)/shard_map/ppermute | solution.py:480
  151.1 10.1 %collective-permute-start.32 = (bf16[4,384,256]{2,1,0:T(8,128)(2,1)S(1)}, bf16[4,384,256]{2,1,0:T(8,128)(2,1)S(1)}, u32[]{:S(2)}, u32[]{:S(2)}) collective-permute-start(bf16[4,384,256]{2,1,0:T(8,128)(2,1)S(1)} %copy-done.6), channel_id=1, source_target_pairs={{0,4},{1,5},{2,6},{3,7},{4,0},{5,1},{6,2},{7,3},{8,12},{9,13},{10,... | collective-permute-start | bytes 2359304 | tf_op jit(solution)/shard_map/ppermute | solution.py:453
  160.7 1.6 collective-permute-start.31
  160.7 1.6 collective-permute-start.33
  166.6 23.6 %collective-permute-start.34 = (bf16[8,104,768]{2,1,0:T(8,128)(2,1)S(1)}, bf16[8,104,768]{2,1,0:T(8,128)(2,1)S(1)}, u32[]{:S(2)}, u32[]{:S(2)}) collective-permute-start(bf16[8,104,768]{2,1,0:T(8,128)(2,1)S(1)} %bitcast.131), channel_id=1, source_target_pairs={{0,8},{1,9},{2,10},{3,11},{4,20},{5,21},{6,22},{7,23},{8,0},{9,1},... | collective-permute-start | bytes 3833864 | tf_op jit(solution)/shard_map/ppermute | solution.py:480
  168.0 22.5 %collective-permute-start.38 = (bf16[4,96,768]{2,1,0:T(8,128)(2,1)S(1)}, bf16[4,96,768]{2,1,0:T(8,128)(2,1)S(1)}, u32[]{:S(2)}, u32[]{:S(2)}) collective-permute-start(bf16[4,96,768]{2,1,0:T(8,128)(2,1)S(1)} %get-tuple-element.177), channel_id=1, source_target_pairs={{0,16},{1,17},{2,18},{3,19},{4,12},{5,13},{6,14},{7,15},{8,24},{9,... | collective-permute-start | bytes 1769480 | tf_op jit(solution)/shard_map/ppermute | solution.py:480
  168.9 21.5 %collective-permute-start.35 = (bf16[1,96,768]{2,1,0:T(8,128)(2,1)S(1)}, bf16[1,96,768]{2,1,0:T(8,128)(2,1)S(1)}, u32[]{:S(2)}, u32[]{:S(2)}) collective-permute-start(bf16[1,96,768]{2,1,0:T(8,128)(2,1)S(1)} %get-tuple-element.188), channel_id=1, source_target_pairs={{0,1},{1,0},{2,3},{3,2},{4,5},{5,4},{6,7},{7,6},{8,9},{9,8},{10,11... | collective-permute-start | bytes 442376 | tf_op jit(solution)/shard_map/ppermute | solution.py:480
  173.0 17.5 %collective-permute-start.36 = (bf16[1,96,768]{2,1,0:T(8,128)(2,1)S(1)}, bf16[1,96,768]{2,1,0:T(8,128)(2,1)S(1)}, u32[]{:S(2)}, u32[]{:S(2)}) collective-permute-start(bf16[1,96,768]{2,1,0:T(8,128)(2,1)S(1)} %get-tuple-element.187), channel_id=1, source_target_pairs={{0,2},{1,3},{2,0},{3,1},{4,6},{5,7},{6,4},{7,5},{8,10},{9,11},{10,... | collective-permute-start | bytes 442376 | tf_op jit(solution)/shard_map/ppermute | solution.py:480
  175.0 15.5 %collective-permute-start.37 = (bf16[1,96,768]{2,1,0:T(8,128)(2,1)S(1)}, bf16[1,96,768]{2,1,0:T(8,128)(2,1)S(1)}, u32[]{:S(2)}, u32[]{:S(2)}) collective-permute-start(bf16[1,96,768]{2,1,0:T(8,128)(2,1)S(1)} %get-tuple-element.186), channel_id=1, source_target_pairs={{0,3},{1,2},{2,1},{3,0},{4,7},{5,6},{6,5},{7,4},{8,11},{9,10},{10,... | collective-permute-start | bytes 442376 | tf_op jit(solution)/shard_map/ppermute | solution.py:480
  190.5 10.5 %collective-permute-start.39 = (bf16[4,104,768]{2,1,0:T(8,128)(2,1)S(1)}, bf16[4,104,768]{2,1,0:T(8,128)(2,1)S(1)}, u32[]{:S(2)}, u32[]{:S(2)}) collective-permute-start(bf16[4,104,768]{2,1,0:T(8,128)(2,1)S(1)} %get-tuple-element.140), channel_id=1, source_target_pairs={{0,16},{1,17},{2,18},{3,19},{4,12},{5,13},{6,14},{7,15},{8,24},{9,... | collective-permute-start | bytes 1916936 | tf_op jit(solution)/shard_map/ppermute | solution.py:480
  193.7 8.5 %collective-permute-start.40 = (bf16[1,96,768]{2,1,0:T(8,128)(2,1)S(1)}, bf16[1,96,768]{2,1,0:T(8,128)(2,1)S(1)}, u32[]{:S(2)}, u32[]{:S(2)}) collective-permute-start(bf16[1,96,768]{2,1,0:T(8,128)(2,1)S(1)} %get-tuple-element.185), channel_id=1, source_target_pairs={{0,1},{1,0},{2,3},{3,2},{4,5},{5,4},{6,7},{7,6},{8,9},{9,8},{10,11... | collective-permute-start | bytes 442376 | tf_op jit(solution)/shard_map/ppermute | solution.py:480
  197.4 13.9 %collective-permute-start.41 = (bf16[1,96,768]{2,1,0:T(8,128)(2,1)S(1)}, bf16[1,96,768]{2,1,0:T(8,128)(2,1)S(1)}, u32[]{:S(2)}, u32[]{:S(2)}) collective-permute-start(bf16[1,96,768]{2,1,0:T(8,128)(2,1)S(1)} %get-tuple-element.184), channel_id=1, source_target_pairs={{0,2},{1,3},{2,0},{3,1},{4,6},{5,7},{6,4},{7,5},{8,10},{9,11},{10,... | collective-permute-start | bytes 442376 | tf_op jit(solution)/shard_map/ppermute | solution.py:480
  199.4 11.9 %collective-permute-start.42 = (bf16[1,96,768]{2,1,0:T(8,128)(2,1)S(1)}, bf16[1,96,768]{2,1,0:T(8,128)(2,1)S(1)}, u32[]{:S(2)}, u32[]{:S(2)}) collective-permute-start(bf16[1,96,768]{2,1,0:T(8,128)(2,1)S(1)} %get-tuple-element.183), channel_id=1, source_target_pairs={{0,3},{1,2},{2,1},{3,0},{4,7},{5,6},{6,5},{7,4},{8,11},{9,10},{10,... | collective-permute-start | bytes 442376 | tf_op jit(solution)/shard_map/ppermute | solution.py:480
  211.3 7.2 %collective-permute-start.43 = (bf16[1,104,768]{2,1,0:T(8,128)(2,1)S(1)}, bf16[1,104,768]{2,1,0:T(8,128)(2,1)S(1)}, u32[]{:S(2)}, u32[]{:S(2)}) collective-permute-start(bf16[1,104,768]{2,1,0:T(8,128)(2,1)S(1)} %get-tuple-element.141), channel_id=1, source_target_pairs={{0,1},{1,0},{2,3},{3,2},{4,5},{5,4},{6,7},{7,6},{8,9},{9,8},{10,11... | collective-permute-start | bytes 479240 | tf_op jit(solution)/shard_map/ppermute | solution.py:480
  213.5 13.9 %collective-permute-start.44 = (bf16[1,104,768]{2,1,0:T(8,128)(2,1)S(1)}, bf16[1,104,768]{2,1,0:T(8,128)(2,1)S(1)}, u32[]{:S(2)}, u32[]{:S(2)}) collective-permute-start(bf16[1,104,768]{2,1,0:T(8,128)(2,1)S(1)} %get-tuple-element.142), channel_id=1, source_target_pairs={{0,2},{1,3},{2,0},{3,1},{4,6},{5,7},{6,4},{7,5},{8,10},{9,11},{10,... | collective-permute-start | bytes 479240 | tf_op jit(solution)/shard_map/ppermute | solution.py:480
  214.7 12.7 %collective-permute-start.45 = (bf16[1,104,768]{2,1,0:T(8,128)(2,1)S(1)}, bf16[1,104,768]{2,1,0:T(8,128)(2,1)S(1)}, u32[]{:S(2)}, u32[]{:S(2)}) collective-permute-start(bf16[1,104,768]{2,1,0:T(8,128)(2,1)S(1)} %get-tuple-element.143), channel_id=1, source_target_pairs={{0,3},{1,2},{2,1},{3,0},{4,7},{5,6},{6,5},{7,4},{8,11},{9,10},{10,... | collective-permute-start | bytes 479240 | tf_op jit(solution)/shard_map/ppermute | solution.py:480
  227.4 3.5 %copy-start.1 = (bf16[3,128,768]{2,1,0:T(8,128)(2,1)S(1)}, bf16[3,128,768]{2,1,0:T(8,128)(2,1)}, u32[]{:S(2)}) copy-start(bf16[3,128,768]{2,1,0:T(8,128)(2,1)} %param.15) | copy-start | bytes 1769476
  (6 other events, 8.8 us)

commit v5 on v4

--- a/solution.py
+++ b/solution.py
@@ -18,6 +18,7 @@
 BLK = 96
 VMEM_LIMIT = 24 * 1024 * 1024
 COST = 30_000_000
+NORM = 2000
 
 
 def nn(a, b):
@@ -50,13 +51,12 @@
     return jnp.sum(v, axis=0, keepdims=True)
 
 
-def pack(qkv_ref, out_ref, down_ref, ob_ref, g1_ref, s1_ref, db_ref, g2_ref, s2_ref, qv_ref, ub_ref, first_ref, down_t_ref):
+def pack(qkv_ref, out_ref, ob_ref, g1_ref, s1_ref, db_ref, g2_ref, s2_ref, qv_ref, ub_ref, first_ref):
     rows, hc = qkv_ref.shape[1:]
     eye = (lax.broadcasted_iota(jnp.int32, (rows, rows), 0) == lax.broadcasted_iota(jnp.int32, (rows, rows), 1)).astype(bf16)
     for c in range(3):
         first_ref[:rows, c * hc : (c + 1) * hc] = qkv_ref[c]
     first_ref[:rows, 3 * hc :] = nt(eye, out_ref[...]).astype(bf16)
-    down_t_ref[...] = nt(eye, down_ref[...]).astype(bf16)
     parts = [r[...].astype(f32) for r in (ob_ref, g1_ref, s1_ref, db_ref, g2_ref, s2_ref, qv_ref)]
     short = jnp.concatenate(parts, axis=0).astype(bf16)
     count, size = short.shape
@@ -402,6 +402,10 @@
     return pl.BlockSpec((a.shape[0], 1, BLK, a.shape[3]), lambda s: (0, s, 0, 0))
 
 
+def weight_t(a):
+    return pl.BlockSpec((1, a.shape[1], BLK, a.shape[3]), lambda s: (s, 0, 0, 0))
+
+
 def half_spec(h):
     return pl.BlockSpec((h.shape[0], 1) + h.shape[2:], lambda s: (0, s, 0, 0))
 
@@ -457,9 +461,9 @@
     def __init__(self, value, tables):
         self.held, self.tables = [value[None]], tables
 
-    def send(self, name, *done, parts=None):
+    def send(self, name, *done, parts=None, tables=None):
         sent = self.held if parts is None else [self.held[j] for j in parts]
-        return [lax.ppermute(after(h, *done), AXES, t) for t in self.tables[name] for h in sent]
+        return [lax.ppermute(after(h, *done), AXES, t) for t in self.tables[name][tables or slice(None)] for h in sent]
 
     def take(self, name, got):
         self.held = [jnp.concatenate(self.held + got)] if name in "Z2" else self.held + got
@@ -468,8 +472,8 @@
     def stage(self, name, *done, parts=None):
         return self.take(name, self.send(name, *done, parts=parts))
 
-    def pieces(self, n_t):
-        return [h.reshape(h.shape[0] // n_t, n_t, *h.shape[1:]) for h in self.held]
+    def pieces(self, *lead):
+        return [h.reshape(*lead, *h.shape[1:]) for h in self.held]
 
 
 class Scatter:
@@ -516,12 +520,10 @@
     rel = jnp.arange(n_i)
     if pairwise:
         tables = flips(n_dp, n_t)
-        packed = (qkv_weight, out_weight, down_weight_in, *[p[None] for p in d_parts], qv_bias, up_bias[None])
-        packed, down_t = pl.pallas_call(
-            pack, out_shape=[sds((BLK + 8, 4 * hc), bf16), sds((BLK, fc), bf16)]
-        )(*packed)
-        first, middle, last = Gather(packed, tables), Gather(up_weight, tables), Gather(down_t, tables)
-        done = first.stage("Z")
+        packed = (qkv_weight, out_weight, *[p[None] for p in d_parts], qv_bias, up_bias[None])
+        packed = pl.pallas_call(pack, out_shape=sds((BLK + 8, 4 * hc), bf16))(*packed)
+        first, middle, last = Gather(packed, tables), Gather(up_weight, tables), Gather(down_weight_in.T, tables)
+        done = first.stage("Z") + last.stage("2")
 
         core = (at_dp & 1) ^ (rel >> 2)
         s3, s2 = (rel >> 1) & 1, rel & 1
@@ -546,12 +548,13 @@
     seg_c = segment_ids.reshape(T, 1)
 
     if pairwise:
-        done = first.stage("2", x, x_keep, x_send, pg, hot_d, hot_e) + middle.stage("Z", *done)
+        done = first.stage("2", *done, x, x_keep, x_send, pg, hot_d, hot_e) + middle.stage("Z", *done)
         x_other = swap(x_send, tables, *done)
-        done = first.stage("3", *done) + middle.stage("2", *done) + last.stage("Z", *done)
+        near_z = last.send("Z", *done, tables=slice(0, 2))
+        done = first.stage("3", *done) + middle.stage("2", *done) + near_z
         first.stage("C", *done)
-        got_u3, got_d2 = middle.send("3", *done), last.send("2", *done)
-        w_qo = first.pieces(n_t)
+        got_u3, far_z = middle.send("3", *done), last.send("Z", *done, tables=slice(2, None))
+        w_qo = first.pieces(2, n_t)
     else:
         heads_in = [qkv_weight[0], qkv_weight[1], qkv_weight[2], out_weight.T]
         main = jnp.concatenate([*heads_in, up_weight, down_weight_in.T], axis=1)
@@ -568,7 +571,7 @@
             for j, w in enumerate(quarters)
         ]
         w_up = [w[..., 4 * hc : 4 * hc + fc] for w in quarters]
-        w_down = [w[..., 4 * hc + fc :] for w in quarters]
+        w_down = [w[..., 4 * hc + fc :].transpose(1, 0, 2, 3) for w in quarters]
 
     hl = hc // HD * L
     o_wide, q_wide = -(-hc // 128) * 128, -(-3 * hc // 128) * 128
@@ -581,6 +584,9 @@
 
     def weights(*arrays):
         return [(a, weight(a)) for a in arrays]
+
+    def weights_t(*arrays):
+        return [(a, weight_t(a)) for a in arrays]
 
     tails = [
         (w, pl.BlockSpec((w.shape[0], n_t, 8, w.shape[3]), lambda s: (0, 0, BLK // 8, 0), pipeline_mode=pl.Buffered(1)))
@@ -596,15 +602,16 @@
         [pltpu.VMEM((T, D), f32), pltpu.VMEM((n_t, 1, hc), f32), pltpu.VMEM((n_t, 1, hc), f32)],
     )
     if pairwise:
-        last.take("2", [after(g, n1b) for g in got_d2])
-        middle.take("3", got_u3)
+        last.take("Z", near_z + [after(g, n1b) for g in far_z])
+        middle.take("3", [after(g, n1b) for g in got_u3])
         last.stage("3", *got_u3)
-        middle.stage("C", n1b)
+        middle.stage("C", n1b, *far_z)
         last.take("C", last.send("C", n1b, parts=(0,)))
         last.take("C", last.send("C", parts=(1,)))
-        w_up, w_down = middle.pieces(n_t), last.pieces(n_t)
+        w_up, w_down = middle.pieces(2, n_t), last.pieces(n_t, 2)
         n1_other = swap(n1_send, tables)
         o_other = swap(o, tables)
+        pg = after(pg, x_other, n1_other, o_other)
     z, dgelu = call(
         up_forward, n_t, 4, wholes(n1b) + weights(*w_up) + leads(b_u),
         leads(sds((n_t, T, fc), bf16), sds((n_t, T, fc), f32)),
@@ -612,7 +619,7 @@
     if pairwise:
         z_other = swap(z, tables)
     pooled, db, dbb, db_keep, db_send, sums2 = call(
-        down_forward, n_t, 5.5, leads(z) + weights(*w_down) + wholes(n1, vec_d, seg_c, seg_r, pg),
+        down_forward, n_t, 5.5, leads(z) + weights_t(*w_down) + wholes(n1, vec_d, seg_c, seg_r, pg),
         wholes(sds((G, segs, D), f32), sds((T, D), f32), sds((T, D), bf16), sds(turned, bf16), sds(turned, bf16), sds((3, D), f32)),
         [pltpu.VMEM((T, D), f32)],
     )
@@ -637,7 +644,7 @@
         return a.reshape((-1,) + a.shape[2:])
 
     du, g_bu = call(
-        hidden_backward, n_t, 3.5, wholes(dbb) + weights(*w_down) + leads(dgelu),
+        hidden_backward, n_t, 3.5, wholes(dbb) + weights_t(*w_down) + leads(dgelu),
         leads(sds((n_t, T, fc), bf16), sds((n_t, 1, fc), f32)),
     )
     if pairwise:
@@ -650,7 +657,7 @@
     else:
         du_next = du
     da, dab, da_keep, da_send, sums1 = call(
-        norm_backward, n_t, 5, leads(du_next) + weights(*w_up) + wholes(db, x1, r1, vec_d),
+        norm_backward, n_t, NORM, leads(du_next) + weights(*w_up) + wholes(db, x1, r1, vec_d),
         wholes(sds((T, D), f32), sds((T, D), bf16), sds(turned, bf16), sds(turned, bf16), sds((3, D), f32)),
         [pltpu.VMEM((T, D), f32)],
     )
@@ -662,7 +669,7 @@
         dab = after(dab, up_keep)
     rows = sds((n_t, n_i // 2, 4 * hc), f32)
     if pairwise:
-        dab = after(dab, *got_d3)
+        dab = after(dab, da_other, *got_d3)
     dq_half = sds((n_t // 2, T, q_wide), bf16)
     *dq, v_keep, v_send = call(
         partial(attention_backward, sizes), n_t, 8,
@@ -670,12 +677,16 @@
         halved(dq_half, dq_half) + wholes(rows, rows),
         [pltpu.VMEM((n_t, 1, hc), f32), pltpu.VMEM((n_t, 1, hc), f32), pltpu.VMEM((T, q_wide), bf16)],
     )
-    dq_next = dq
     if pairwise:
         dq_other = [swap(d, tables) for d in dq]
         v_other = swap(v_send, tables)
         got_d2 = s_down.stage("2", n_t)
-        x_now = after(x_keep, *got_d2, *got_u3)
+    dx = call(
+        input_backward, n_t, 4, halved(*dq) + weights(*w_qo) + wholes(da, perm), wholes(sds((T, D), f32)),
+        [pltpu.VMEM((T, D), f32)],
+    )[0]
+    if pairwise:
+        x_now = after(x_keep, dx, *got_d2, *got_u3)
         qo_keep, qo_send = gradient(
             [[3 * hc, (x_now, dq), (x_other, dq_other)], [hc, (da_keep, [o]), (da_other, [o_other])]], (v_keep, v_other)
         )
@@ -683,16 +694,11 @@
         got_z = s_down.stage("Z", 1)
         got_u2 = s_up.stage("2", n_t)
         got_q3 = s_qo.stage("3", 2)
-        dq_next = [after(d, qo_keep) for d in dq]
-    dx = call(
-        input_backward, n_t, 4, halved(*dq_next) + weights(*w_qo) + wholes(da, perm), wholes(sds((T, D), f32)),
-        [pltpu.VMEM((T, D), f32)],
-    )[0]
     pooled = jnp.einsum("gse,de->gsd", pooled, perm.astype(f32), precision=HI)
 
     if pairwise:
         got = s_up.stage("Z", 1)
-        s_qo.stage("2", n_t, dx, *got_z, *got_u2)
+        s_qo.stage("2", n_t, *got_z, *got_u2, pooled, s_down.keep, got[0])
         s_qo.stage("Z", 1, *got)
         g_down, g_up, g_qo = s_down.keep[0], s_up.keep[0], s_qo.keep[0]
         g_v = g_qo[BLK, :n_vec]

time: 231 us -> 214 us (0.926)
  waiting for transfers between devices: 102 us -> 80.2 us
  starting transfers between devices: 46.4 us -> 52.6 us
    ppermute x21, waiting for transfers between devices: 54.5 us -> 38.1 us  [send(): lax.ppermute(after(h, *done), AXES, t)]
    ppermute x21, starting transfers between devices: 20.9 us -> 26.3 us  [send(): lax.ppermute(after(h, *done), AXES, t)]
    ppermute x15, waiting for transfers between devices: 41.8 us -> 36.9 us  [stage(): lax.ppermute(after(s, *done), AXES, t)]
    unnamed x63 -> x64, local copies, waits for them, and re-layouts: 5.53 us -> 4 us
  transfers between devices with their start and end apart: 46 -> 46, of which waited for: 22 -> 19; matrix products, arithmetic and copies ran while one was open for 7% -> 8% of each run, Pallas kernels for 23% -> 25%
where the time goes in v5:
time: 214 us
  waiting for transfers between devices  80.2 us (37%)
  Pallas kernels  59.1 us (28%)
  starting transfers between devices  52.6 us (25%)
  local copies, waits for them, and re-layouts  10.8 us (5%)
  other arithmetic  6.16 us (3%)
  matrix products  3.78 us (2%)
    pallas_call x10, Pallas kernels, call(): pl.pallas_call(body, grid=(n_t,), in_specs=[s for _, s in ins], out_specs...  57.1 us
    ppermute x21, waiting for transfers between devices, send(): lax.ppermute(after(h, *done), AXES, t)  38.1 us
    ppermute x15, waiting for transfers between devices, stage(): lax.ppermute(after(s, *done), AXES, t)  36.9 us
    ppermute x21, starting transfers between devices, send(): lax.ppermute(after(h, *done), AXES, t)  26.3 us
    ppermute x15, starting transfers between devices, stage(): lax.ppermute(after(s, *done), AXES, t)  23.5 us
    ppermute x10, waiting for transfers between devices, swap(): return lax.ppermute(after(value, *done), AXES, tables['C'][0])  5.27 us
  transfers between devices with their start and end apart: 46, of which 19 were waited for; matrix products, arithmetic and copies ran while one was open for 8% of the time, Pallas kernels for 25%

profile of v5, /device:TPU:0, one launch (start us, length us, event | category | flops | bytes accessed | tf_op | source)
XLA Modules:
  0.0 213.9 jit_solution(11670122156780467133)
XLA Ops:
  0.7 2.0 shard_map.254
  2.6 3.0 %collective-permute-start = (bf16[1,104,768]{2,1,0:T(8,128)(2,1)}, bf16[1,104,768]{2,1,0:T(8,128)(2,1)S(1)}, u32[]{:S(2)}, u32[]{:S(2)}) collective-permute-start(bf16[1,104,768]{2,1,0:T(8,128)(2,1)} %bitcast.136), channel_id=1, source_target_pairs={{0,1},{1,0},{2,3},{3,2},{4,5},{5,4},{6,7},{7,6},{8,9},{9,8},{10,11... | collective-permute-start | bytes 479240 | tf_op jit(solution)/shard_map/ppermute | solution.py:466
  5.7 2.6 %collective-permute-start.1 = (bf16[1,104,768]{2,1,0:T(8,128)(2,1)}, bf16[1,104,768]{2,1,0:T(8,128)(2,1)S(1)}, u32[]{:S(2)}, u32[]{:S(2)}) collective-permute-start(bf16[1,104,768]{2,1,0:T(8,128)(2,1)} %bitcast.137), channel_id=1, source_target_pairs={{0,2},{1,3},{2,0},{3,1},{4,6},{5,7},{6,4},{7,5},{8,10},{9,11},{10,... | collective-permute-start | bytes 479240 | tf_op jit(solution)/shard_map/ppermute | solution.py:466
  8.3 1.7 collective-permute-start.3
  11.1 0.8 convolution_convert_fusion
  12.0 0.9 fusion.40
  12.9 1.0 convolution_bitcast_fusion.pg_ref
  14.0 6.7 %collective-permute-done.1 = bf16[1,104,768]{2,1,0:T(8,128)(2,1)S(1)} collective-permute-done((bf16[1,104,768]{2,1,0:T(8,128)(2,1)}, bf16[1,104,768]{2,1,0:T(8,128)(2,1)S(1)}, u32[]{:S(2)}, u32[]{:S(2)}) %collective-permute-start.1) | collective-permute-done | bytes 159776 | tf_op jit(solution)/shard_map/ppermute | solution.py:466
  20.8 1.6 collective-permute-start.4
  22.4 2.6 %collective-permute-start.5 = (bf16[1,96,768]{2,1,0:T(8,128)(2,1)S(1)}, bf16[1,96,768]{2,1,0:T(8,128)(2,1)S(1)}, u32[]{:S(2)}, u32[]{:S(2)}) collective-permute-start(bf16[1,96,768]{2,1,0:T(8,128)(2,1)S(1)} %bitcast.143), channel_id=1, source_target_pairs={{0,1},{1,0},{2,3},{3,2},{4,5},{5,4},{6,7},{7,6},{8,9},{9,8},{10,11... | collective-permute-start | bytes 442376 | tf_op jit(solution)/shard_map/ppermute | solution.py:466
  25.1 1.1 collective-permute-start.6
  26.1 1.4 collective-permute-start.7
  27.6 3.7 %collective-permute-done.4 = bf16[4,104,768]{2,1,0:T(8,128)(2,1)S(1)} collective-permute-done((bf16[4,104,768]{2,1,0:T(8,128)(2,1)S(1)}, bf16[4,104,768]{2,1,0:T(8,128)(2,1)S(1)}, u32[]{:S(2)}, u32[]{:S(2)}) %collective-permute-start.4) | collective-permute-done | bytes 639008 | tf_op jit(solution)/shard_map/ppermute | solution.py:466
  31.3 6.5 %collective-permute-done.6 = bf16[1,96,768]{2,1,0:T(8,128)(2,1)S(1)} collective-permute-done((bf16[1,96,768]{2,1,0:T(8,128)(2,1)S(1)}, bf16[1,96,768]{2,1,0:T(8,128)(2,1)S(1)}, u32[]{:S(2)}, u32[]{:S(2)}) %collective-permute-start.6) | collective-permute-done | bytes 147488 | tf_op jit(solution)/shard_map/ppermute | solution.py:466
  38.6 1.6 collective-permute-start.9
  40.9 0.7 pad_maximum_fusion.2
  41.6 2.1 %collective-permute-start.10 = (bf16[2,96,768]{2,1,0:T(8,128)(2,1)}, bf16[2,96,768]{2,1,0:T(8,128)(2,1)S(1)}, u32[]{:S(2)}, u32[]{:S(2)}) collective-permute-start(bf16[2,96,768]{2,1,0:T(8,128)(2,1)} %pad_maximum_fusion.2), channel_id=1, source_target_pairs={{0,1},{1,0},{2,3},{3,2},{4,5},{5,4},{6,7},{7,6},{8,9},{9,8},{10,11... | collective-permute-start | bytes 884744 | tf_op jit(solution)/shard_map/ppermute | solution.py:466
  43.8 1.1 collective-permute-start.11
  46.9 8.4 %collective-permute-done.10 = bf16[2,96,768]{2,1,0:T(8,128)(2,1)S(1)} collective-permute-done((bf16[2,96,768]{2,1,0:T(8,128)(2,1)}, bf16[2,96,768]{2,1,0:T(8,128)(2,1)S(1)}, u32[]{:S(2)}, u32[]{:S(2)}) %collective-permute-start.10) | collective-permute-done | bytes 294944 | tf_op jit(solution)/shard_map/ppermute | solution.py:466
  55.3 3.5 %collective-permute-done.8 = bf16[8,104,768]{2,1,0:T(8,128)(2,1)S(1)} collective-permute-done((bf16[8,104,768]{2,1,0:T(8,128)(2,1)S(1)}, bf16[8,104,768]{2,1,0:T(8,128)(2,1)S(1)}, u32[]{:S(2)}, u32[]{:S(2)}) %collective-permute-start.8) | collective-permute-done | bytes 1277984 | tf_op jit(solution)/shard_map/ppermute | solution.py:466
  59.3 0.9 constant_dynamic-update-slice_fusion.5
  60.5 3.6 %collective-permute-start.15 = (bf16[2,96,768]{2,1,0:T(8,128)(2,1)}, bf16[2,96,768]{2,1,0:T(8,128)(2,1)}, u32[]{:S(2)}, u32[]{:S(2)}) collective-permute-start(bf16[2,96,768]{2,1,0:T(8,128)(2,1)} %pad_maximum_fusion.2), channel_id=1, source_target_pairs={{0,3},{1,2},{2,1},{3,0},{4,7},{5,6},{6,5},{7,4},{8,11},{9,10},{10,... | collective-permute-start | bytes 884744 | tf_op jit(solution)/shard_map/ppermute | solution.py:466
  64.1 1.3 copy.33.x_ref
  65.6 11.7 %shard_map.255 = (bf16[4,384,576]{2,1,0:T(8,128)(2,1)}, f32[4,3,128,384]{3,2,1,0:T(8,128)}, bf16[4,384,256]{2,1,0:T(8,128)(2,1)}, f32[384,768]{1,0:T(8,128)S(1)}...) custom-call(bf16[384,768]{1,0:T(8,128)(2,1)S(1)} %copy.33.x_ref, ...), custom_call_target="tpu_custom_call" | custom-call | flops 300000000 | tf_op jit(solution)/shard_map/pallas_call | solution.py:422
  78.3 1.0 constant_dynamic-update-slice_fusion.10
  79.3 1.3 collective-permute-start.18
  80.6 1.5 collective-permute-done.16
  82.2 5.0 %shard_map.256 = (bf16[4,384,768]{2,1,0:T(8,128)(2,1)S(1)}, f32[4,384,768]{2,1,0:T(8,128)S(1)}) custom-call(bf16[384,768]{1,0:T(8,128)(2,1)S(1)} %get-tuple-element.84.n_ref, bf16[2,4,96,768]{3,2,1,0:T(8,128)(2,1)} %bitcast.23.w0_ref, bf16[2,4,96,768]{3,2,1,0:T(8,128)(2,1)} %bitcast.24.w1_ref, bf16[2,4,96,768]{3,2,1,0:T(8,128)(2,1)S(1)} %bitcast.125, ...), custom_call_target="tpu_custom_call" | custom-call | flops 120000000 | tf_op jit(solution)/shard_map/pallas_call | solution.py:422
  87.8 7.8 %collective-permute-done.18 = bf16[8,96,768]{2,1,0:T(8,128)(2,1)S(1)} collective-permute-done((bf16[8,96,768]{2,1,0:T(8,128)(2,1)S(1)}, bf16[8,96,768]{2,1,0:T(8,128)(2,1)S(1)}, u32[]{:S(2)}, u32[]{:S(2)}) %collective-permute-start.18) | collective-permute-done | bytes 1179680 | tf_op jit(solution)/shard_map/ppermute | solution.py:466
  96.2 3.8 %collective-permute-done.21.refs_3_ = bf16[384,384]{1,0:T(8,128)(2,1)S(1)} collective-permute-done((bf16[384,384]{1,0:T(8,128)(2,1)S(1)}, bf16[384,384]{1,0:T(8,128)(2,1)S(1)}, u32[]{:S(2)}, u32[]{:S(2)}) %collective-permute-start.21) | collective-permute-done | bytes 294944 | tf_op jit(solution)/shard_map/ppermute | solution.py:457
  100.1 1.4 collective-permute-done.22.refs_2_
  101.6 5.3 %shard_map.257 = (f32[3,8,768]{2,1,0:T(8,128)S(1)}, f32[384,768]{1,0:T(8,128)S(1)}, bf16[384,768]{1,0:T(8,128)(2,1)S(1)}, bf16[384,384]{1,0:T(8,128)(2,1)S(1)}, ...) custom-call(bf16[4,384,768]{2,1,0:T(8,128)(2,1)S(1)} %get-tuple-element.91.z_ref.refs_1_, ...), custom_call_target="tpu_custom_call" | custom-call | flops 165000000 | tf_op jit(solution)/shard_map/pallas_call | solution.py:422
  107.1 2.7 %shard_map.258 = (bf16[4,384,768]{2,1,0:T(8,128)(2,1)S(1)}, f32[4,1,768]{2,1,0:T(1,128)S(1)}) custom-call(bf16[384,768]{1,0:T(8,128)(2,1)S(1)} %get-tuple-element.102.dbb_ref, bf16[4,2,96,768]{3,2,1,0:T(8,128)(2,1)S(1)} %bitcast.116, bf16[4,2,96,768]{3,2,1,0:T(8,128)(2,1)S(1)} %bitcast.118, bf16[4,2,96,768]{3,2,1,0:T(8,128)(2,1)S(1)} %bitcast.120, ...), custom_call_target="tpu_custom_call" | custom-call | flops 105000000 | tf_op jit(solution)/shard_map/pallas_call | solution.py:422
  110.2 3.3 %shard_map.259 = (bf16[2,4,96,768]{3,2,1,0:T(8,128)(2,1)S(1)}, bf16[2,4,96,768]{3,2,1,0:T(8,128)(2,1)S(1)}) custom-call(bf16[384,384]{1,0:T(8,128)(2,1)S(1)} %get-tuple-element.107.refs_0_, bf16[4,384,768]{2,1,0:T(8,128)(2,1)S(1)} %get-tuple-element.91.z_ref.refs_1_, bf16[384,384]{1,0:T(8,128)(2,1)S(1)} %collective-permute-done.24.refs_2_, ...), custom_call_target="tpu_custom_call" | custom-call | flops 120000000 | tf_op jit(solution)/shard_map/pallas_call | solution.py:422
  113.5 1.3 collective-permute-start.28
  114.8 5.5 %shard_map.260 = (f32[384,768]{1,0:T(8,128)S(1)}, bf16[384,768]{1,0:T(8,128)(2,1)S(1)}, bf16[384,384]{1,0:T(8,128)(2,1)S(1)}, bf16[384,384]{1,0:T(8,128)(2,1)S(1)}, f32[3,768]{1,0:T(4,128)S(1)}) custom-call(bf16[4,384,768]{2,1,0:T(8,128)(2,1)S(1)} %get-tuple-element.110.du_ref.refs_1_, bf16[2,4,96,768]{3,2,1,0:T(8,128)(2,1)} %bitcast.23.w0_ref, ...), custom_call_target="tpu_custom_call" | custom-call | flops 60000002048 | tf_op jit(solution)/shard_map/pallas_call | solution.py:422
  120.5 3.3 %shard_map.261 = (bf16[2,4,96,768]{3,2,1,0:T(8,128)(2,1)S(1)}, bf16[2,4,96,768]{3,2,1,0:T(8,128)(2,1)S(1)}) custom-call(bf16[384,384]{1,0:T(8,128)(2,1)S(1)} %copy-done.6, bf16[4,384,768]{2,1,0:T(8,128)(2,1)S(1)} %get-tuple-element.110.du_ref.refs_1_, bf16[384,384]{1,0:T(8,128)(2,1)S(1)} %collective-permute-done.22.refs_2_, ...), custom_call_target="tpu_custom_call" | custom-call | flops 120000000 | tf_op jit(solution)/shard_map/pallas_call | solution.py:422
  123.7 0.8 collective-permute-start.30
  124.6 5.2 %collective-permute-done.28 = bf16[8,96,768]{2,1,0:T(8,128)(2,1)S(1)} collective-permute-done((bf16[8,96,768]{2,1,0:T(8,128)(2,1)S(1)}, bf16[8,96,768]{2,1,0:T(8,128)(2,1)S(1)}, u32[]{:S(2)}, u32[]{:S(2)}) %collective-permute-start.28) | collective-permute-done | bytes 1179680 | tf_op jit(solution)/shard_map/ppermute | solution.py:484
  129.8 8.7 %shard_map.262 = (bf16[2,384,640]{2,1,0:T(8,128)(2,1)S(1)}, bf16[2,384,640]{2,1,0:T(8,128)(2,1)S(1)}, f32[4,4,768]{2,1,0:T(4,128)S(1)}, f32[4,4,768]{2,1,0:T(4,128)S(1)}) custom-call(bf16[384,768]{1,0:T(8,128)(2,1)S(1)} %get-tuple-element.122.dab_ref, bf16[2,4,104,768]{3,2,1,0:T(8,128)(2,1)S(1)} %bitcast.109, bf16[2,4,104,768]{3,2,1,0:T(8,128)(2,1)S(1)} %bitcast.113, ...), custom_call_target="tpu_custom_call" | custom-call | flops 240000000 | tf_op jit(solution)/shard_map/pallas_call | solution.py:422
  141.9 7.3 %shard_map.263 = f32[384,768]{1,0:T(8,128)} custom-call(bf16[2,384,640]{2,1,0:T(8,128)(2,1)S(1)} %get-tuple-element.127.low_ref.refs_1_, bf16[2,384,640]{2,1,0:T(8,128)(2,1)S(1)} %get-tuple-element.128.high_ref.refs_2_, bf16[2,4,104,768]{3,2,1,0:T(8,128)(2,1)S(1)} %bitcast.110, bf16[2,4,104,768]{3,2,1,0:T(8,128)(2,1)S(1)} %bitcast.114, ...), custom_call_target="tpu_custom_call" | custom-call | flops 120000000 | tf_op jit(solution)/shard_map/pallas_call | solution.py:422
  149.3 4.3 %shard_map.264 = (bf16[2,4,104,768]{3,2,1,0:T(8,128)(2,1)S(1)}, bf16[2,4,104,768]{3,2,1,0:T(8,128)(2,1)S(1)}) custom-call(bf16[384,384]{1,0:T(8,128)(2,1)S(1)} %copy-done.4, bf16[2,384,640]{2,1,0:T(8,128)(2,1)S(1)} %get-tuple-element.127.low_ref.refs_1_, bf16[2,384,640]{2,1,0:T(8,128)(2,1)S(1)} %get-tuple-element.128.high_ref.refs_2_, ...), custom_call_target="tpu_custom_call" | custom-call | flops 120000000 | tf_op jit(solution)/shard_map/pallas_call | solution.py:422
  153.7 1.3 collective-permute-start.34
  155.3 0.9 collective-permute-start.38
  156.3 2.9 %collective-permute-start.35 = (bf16[1,96,768]{2,1,0:T(8,128)(2,1)S(1)}, bf16[1,96,768]{2,1,0:T(8,128)(2,1)S(1)}, u32[]{:S(2)}, u32[]{:S(2)}) collective-permute-start(bf16[1,96,768]{2,1,0:T(8,128)(2,1)S(1)} %get-tuple-element.184), channel_id=1, source_target_pairs={{0,1},{1,0},{2,3},{3,2},{4,5},{5,4},{6,7},{7,6},{8,9},{9,8},{10,11... | collective-permute-start | bytes 442376 | tf_op jit(solution)/shard_map/ppermute | solution.py:484
  159.2 1.2 collective-permute-start.36
  160.4 1.4 collective-permute-start.37
  161.8 2.0 fusion
  163.7 1.6 collective-permute-done.35
  165.3 7.9 %collective-permute-done.36 = bf16[1,96,768]{2,1,0:T(8,128)(2,1)S(1)} collective-permute-done((bf16[1,96,768]{2,1,0:T(8,128)(2,1)S(1)}, bf16[1,96,768]{2,1,0:T(8,128)(2,1)S(1)}, u32[]{:S(2)}, u32[]{:S(2)}) %collective-permute-start.36) | collective-permute-done | bytes 147488 | tf_op jit(solution)/shard_map/ppermute | solution.py:484
  173.2 0.8 fusion.23
  174.1 2.5 %collective-permute-start.39 = (bf16[1,96,768]{2,1,0:T(8,128)(2,1)S(1)}, bf16[1,96,768]{2,1,0:T(8,128)(2,1)S(1)}, u32[]{:S(2)}, u32[]{:S(2)}) collective-permute-start(bf16[1,96,768]{2,1,0:T(8,128)(2,1)S(1)} %get-tuple-element.181), channel_id=1, source_target_pairs={{0,1},{1,0},{2,3},{3,2},{4,5},{5,4},{6,7},{7,6},{8,9},{9,8},{10,11... | collective-permute-start | bytes 442376 | tf_op jit(solution)/shard_map/ppermute | solution.py:484
  177.6 2.1 collective-permute-done.39
  180.2 3.2 %collective-permute-start.41 = (bf16[1,96,768]{2,1,0:T(8,128)(2,1)S(1)}, bf16[1,96,768]{2,1,0:T(8,128)(2,1)S(1)}, u32[]{:S(2)}, u32[]{:S(2)}) collective-permute-start(bf16[1,96,768]{2,1,0:T(8,128)(2,1)S(1)} %get-tuple-element.180), channel_id=1, source_target_pairs={{0,2},{1,3},{2,0},{3,1},{4,6},{5,7},{6,4},{7,5},{8,10},{9,11},{10,... | collective-permute-start | bytes 442376 | tf_op jit(solution)/shard_map/ppermute | solution.py:484
  183.3 1.2 collective-permute-start.42
  184.6 5.6 %collective-permute-done.40 = bf16[4,104,768]{2,1,0:T(8,128)(2,1)S(1)} collective-permute-done((bf16[4,104,768]{2,1,0:T(8,128)(2,1)S(1)}, bf16[4,104,768]{2,1,0:T(8,128)(2,1)S(1)}, u32[]{:S(2)}, u32[]{:S(2)}) %collective-permute-start.40) | collective-permute-done | bytes 639008 | tf_op jit(solution)/shard_map/ppermute | solution.py:484
  190.3 2.8 %collective-permute-done.41 = bf16[1,96,768]{2,1,0:T(8,128)(2,1)S(1)} collective-permute-done((bf16[1,96,768]{2,1,0:T(8,128)(2,1)S(1)}, bf16[1,96,768]{2,1,0:T(8,128)(2,1)S(1)}, u32[]{:S(2)}, u32[]{:S(2)}) %collective-permute-start.41) | collective-permute-done | bytes 147488 | tf_op jit(solution)/shard_map/ppermute | solution.py:484
  193.0 3.2 %collective-permute-start.43 = (bf16[1,104,768]{2,1,0:T(8,128)(2,1)S(1)}, bf16[1,104,768]{2,1,0:T(8,128)(2,1)S(1)}, u32[]{:S(2)}, u32[]{:S(2)}) collective-permute-start(bf16[1,104,768]{2,1,0:T(8,128)(2,1)S(1)} %get-tuple-element.137), channel_id=1, source_target_pairs={{0,1},{1,0},{2,3},{3,2},{4,5},{5,4},{6,7},{7,6},{8,9},{9,8},{10,11... | collective-permute-start | bytes 479240 | tf_op jit(solution)/shard_map/ppermute | solution.py:484
  196.2 1.0 collective-permute-start.44
  197.2 1.5 collective-permute-start.45
  198.7 0.8 fusion.17
  199.5 2.0 collective-permute-done.43
  201.5 8.8 %collective-permute-done.44 = bf16[1,104,768]{2,1,0:T(8,128)(2,1)S(1)} collective-permute-done((bf16[1,104,768]{2,1,0:T(8,128)(2,1)S(1)}, bf16[1,104,768]{2,1,0:T(8,128)(2,1)S(1)}, u32[]{:S(2)}, u32[]{:S(2)}) %collective-permute-start.44) | collective-permute-done | bytes 159776 | tf_op jit(solution)/shard_map/ppermute | solution.py:484
  211.8 0.7 copy.38
  (149 shorter events, 17.1 us)
Async XLA Ops:
  0.6 10.5 %copy-start = (bf16[3,128,768]{2,1,0:T(8,128)(2,1)S(1)}, bf16[3,128,768]{2,1,0:T(8,128)(2,1)}, u32[]{:S(2)}) copy-start(bf16[3,128,768]{2,1,0:T(8,128)(2,1)} %param.15) | copy-start | bytes 1769476
  2.6 11.3 %collective-permute-start = (bf16[1,104,768]{2,1,0:T(8,128)(2,1)}, bf16[1,104,768]{2,1,0:T(8,128)(2,1)S(1)}, u32[]{:S(2)}, u32[]{:S(2)}) collective-permute-start(bf16[1,104,768]{2,1,0:T(8,128)(2,1)} %bitcast.136), channel_id=1, source_target_pairs={{0,1},{1,0},{2,3},{3,2},{4,5},{5,4},{6,7},{7,6},{8,9},{9,8},{10,11... | collective-permute-start | bytes 479240 | tf_op jit(solution)/shard_map/ppermute | solution.py:466
  5.7 15.0 %collective-permute-start.1 = (bf16[1,104,768]{2,1,0:T(8,128)(2,1)}, bf16[1,104,768]{2,1,0:T(8,128)(2,1)S(1)}, u32[]{:S(2)}, u32[]{:S(2)}) collective-permute-start(bf16[1,104,768]{2,1,0:T(8,128)(2,1)} %bitcast.137), channel_id=1, source_target_pairs={{0,2},{1,3},{2,0},{3,1},{4,6},{5,7},{6,4},{7,5},{8,10},{9,11},{10,... | collective-permute-start | bytes 479240 | tf_op jit(solution)/shard_map/ppermute | solution.py:466
  8.3 12.4 %collective-permute-start.2 = (bf16[1,104,768]{2,1,0:T(8,128)(2,1)}, bf16[1,104,768]{2,1,0:T(8,128)(2,1)S(1)}, u32[]{:S(2)}, u32[]{:S(2)}) collective-permute-start(bf16[1,104,768]{2,1,0:T(8,128)(2,1)} %bitcast.138), channel_id=1, source_target_pairs={{0,3},{1,2},{2,1},{3,0},{4,7},{5,6},{6,5},{7,4},{8,11},{9,10},{10,... | collective-permute-start | bytes 479240 | tf_op jit(solution)/shard_map/ppermute | solution.py:466
  8.3 12.5 %collective-permute-start.3 = (bf16[1,96,768]{2,1,0:T(8,128)(2,1)}, bf16[1,96,768]{2,1,0:T(8,128)(2,1)S(1)}, u32[]{:S(2)}, u32[]{:S(2)}) collective-permute-start(bf16[1,96,768]{2,1,0:T(8,128)(2,1)} %bitcast.147), channel_id=1, source_target_pairs={{0,16},{1,17},{2,18},{3,19},{4,12},{5,13},{6,14},{7,15},{8,24},{9,... | collective-permute-start | bytes 442376 | tf_op jit(solution)/shard_map/ppermute | solution.py:466
  11.9 8.9 %copy-start.9 = (bf16[768,384]{1,0:T(8,128)(2,1)}, bf16[768,384]{1,0:T(8,128)(2,1)S(1)}, u32[]{:S(2)}) copy-start(bf16[768,384]{1,0:T(8,128)(2,1)S(1)} %convolution_convert_fusion) | copy-start | bytes 1769476
  12.0 8.7 %copy-start.10 = (bf16[104,768]{1,0:T(8,128)(2,1)S(1)}, bf16[104,768]{1,0:T(8,128)(2,1)}, u32[]{:S(2)}) copy-start(bf16[104,768]{1,0:T(8,128)(2,1)} %shard_map.254) | copy-start | bytes 479236
  12.9 9.5 %copy-start.11 = (bf16[96,768]{1,0:T(8,128)(2,1)S(1)}, bf16[96,768]{1,0:T(8,128)(2,1)}, u32[]{:S(2)}) copy-start(bf16[96,768]{1,0:T(8,128)(2,1)} %param.24) | copy-start | bytes 442372
  20.8 10.5 %collective-permute-start.4 = (bf16[4,104,768]{2,1,0:T(8,128)(2,1)S(1)}, bf16[4,104,768]{2,1,0:T(8,128)(2,1)S(1)}, u32[]{:S(2)}, u32[]{:S(2)}) collective-permute-start(bf16[4,104,768]{2,1,0:T(8,128)(2,1)S(1)} %pad_maximum_fusion), channel_id=1, source_target_pairs={{0,16},{1,17},{2,18},{3,19},{4,12},{5,13},{6,14},{7,15},{8,24},{9,... | collective-permute-start | bytes 1916936 | tf_op jit(solution)/shard_map/ppermute | solution.py:466
  22.4 8.9 %collective-permute-start.5 = (bf16[1,96,768]{2,1,0:T(8,128)(2,1)S(1)}, bf16[1,96,768]{2,1,0:T(8,128)(2,1)S(1)}, u32[]{:S(2)}, u32[]{:S(2)}) collective-permute-start(bf16[1,96,768]{2,1,0:T(8,128)(2,1)S(1)} %bitcast.143), channel_id=1, source_target_pairs={{0,1},{1,0},{2,3},{3,2},{4,5},{5,4},{6,7},{7,6},{8,9},{9,8},{10,11... | collective-permute-start | bytes 442376 | tf_op jit(solution)/shard_map/ppermute | solution.py:466
  25.1 12.7 %collective-permute-start.6 = (bf16[1,96,768]{2,1,0:T(8,128)(2,1)S(1)}, bf16[1,96,768]{2,1,0:T(8,128)(2,1)S(1)}, u32[]{:S(2)}, u32[]{:S(2)}) collective-permute-start(bf16[1,96,768]{2,1,0:T(8,128)(2,1)S(1)} %bitcast.144), channel_id=1, source_target_pairs={{0,2},{1,3},{2,0},{3,1},{4,6},{5,7},{6,4},{7,5},{8,10},{9,11},{10,... | collective-permute-start | bytes 442376 | tf_op jit(solution)/shard_map/ppermute | solution.py:466
  26.1 11.6 %collective-permute-start.7 = (bf16[1,96,768]{2,1,0:T(8,128)(2,1)S(1)}, bf16[1,96,768]{2,1,0:T(8,128)(2,1)S(1)}, u32[]{:S(2)}, u32[]{:S(2)}) collective-permute-start(bf16[1,96,768]{2,1,0:T(8,128)(2,1)S(1)} %bitcast.145), channel_id=1, source_target_pairs={{0,3},{1,2},{2,1},{3,0},{4,7},{5,6},{6,5},{7,4},{8,11},{9,10},{10,... | collective-permute-start | bytes 442376 | tf_op jit(solution)/shard_map/ppermute | solution.py:466
  27.6 13.3 %copy-start.12 = (bf16[768,96]{0,1:T(8,128)(2,1)S(1)}, bf16[768,96]{0,1:T(8,128)(2,1)}, u32[]{:S(2)}) copy-start(bf16[768,96]{0,1:T(8,128)(2,1)} %param.26) | copy-start | bytes 442372
  27.6 13.3 %copy-start.15 = (bf16[1,96,768]{2,1,0:T(8,128)(2,1)S(1)}, bf16[1,96,768]{2,1,0:T(8,128)(2,1)}, u32[]{:S(2)}) copy-start(bf16[1,96,768]{2,1,0:T(8,128)(2,1)} %copy-done.14) | copy-start | bytes 442372
  37.8 21.1 %collective-permute-start.8 = (bf16[8,104,768]{2,1,0:T(8,128)(2,1)S(1)}, bf16[8,104,768]{2,1,0:T(8,128)(2,1)S(1)}, u32[]{:S(2)}, u32[]{:S(2)}) collective-permute-start(bf16[8,104,768]{2,1,0:T(8,128)(2,1)S(1)} %constant_dynamic-update-slice_fusion), channel_id=1, source_target_pairs={{0,8},{1,9},{2,10},{3,11},{4,20},{5,21},{6,22},{7,23},{8,0},{9,1},... | collective-permute-start | bytes 3833864 | tf_op jit(solution)/shard_map/ppermute | solution.py:466
  38.6 16.7 %collective-permute-start.9 = (bf16[4,96,768]{2,1,0:T(8,128)(2,1)S(1)}, bf16[4,96,768]{2,1,0:T(8,128)(2,1)S(1)}, u32[]{:S(2)}, u32[]{:S(2)}) collective-permute-start(bf16[4,96,768]{2,1,0:T(8,128)(2,1)S(1)} %pad_maximum_fusion.1), channel_id=1, source_target_pairs={{0,16},{1,17},{2,18},{3,19},{4,12},{5,13},{6,14},{7,15},{8,24},{9,... | collective-permute-start | bytes 1769480 | tf_op jit(solution)/shard_map/ppermute | solution.py:466
  41.6 13.6 %collective-permute-start.10 = (bf16[2,96,768]{2,1,0:T(8,128)(2,1)}, bf16[2,96,768]{2,1,0:T(8,128)(2,1)S(1)}, u32[]{:S(2)}, u32[]{:S(2)}) collective-permute-start(bf16[2,96,768]{2,1,0:T(8,128)(2,1)} %pad_maximum_fusion.2), channel_id=1, source_target_pairs={{0,1},{1,0},{2,3},{3,2},{4,5},{5,4},{6,7},{7,6},{8,9},{9,8},{10,11... | collective-permute-start | bytes 884744 | tf_op jit(solution)/shard_map/ppermute | solution.py:466
  43.8 11.5 %collective-permute-start.11 = (bf16[2,96,768]{2,1,0:T(8,128)(2,1)}, bf16[2,96,768]{2,1,0:T(8,128)(2,1)S(1)}, u32[]{:S(2)}, u32[]{:S(2)}) collective-permute-start(bf16[2,96,768]{2,1,0:T(8,128)(2,1)} %pad_maximum_fusion.2), channel_id=1, source_target_pairs={{0,2},{1,3},{2,0},{3,1},{4,6},{5,7},{6,4},{7,5},{8,10},{9,11},{10,... | collective-permute-start | bytes 884744 | tf_op jit(solution)/shard_map/ppermute | solution.py:466
  46.9 18.5 %copy-start.23 = (s32[3,1,128]{2,1,0:T(1,128)S(1)}, s32[3,1,128]{2,1,0:T(1,128)}, u32[]{:S(2)}) copy-start(s32[3,1,128]{2,1,0:T(1,128)} %param.16) | copy-start | bytes 4612
  55.3 5.2 %copy-start.17 = (bf16[2,96,768]{2,1,0:T(8,128)(2,1)}, bf16[2,96,768]{2,1,0:T(8,128)(2,1)S(1)}, u32[]{:S(2)}) copy-start(bf16[2,96,768]{2,1,0:T(8,128)(2,1)S(1)} %collective-permute-done.10) | copy-start | bytes 884740
  58.8 6.7 %collective-permute-start.13 = (bf16[8,104,768]{2,1,0:T(8,128)(2,1)S(1)}, bf16[8,104,768]{2,1,0:T(8,128)(2,1)}, u32[]{:S(2)}, u32[]{:S(2)}) collective-permute-start(bf16[8,104,768]{2,1,0:T(8,128)(2,1)S(1)} %collective-permute-done.8), channel_id=1, source_target_pairs={{0,4},{1,5},{2,6},{3,7},{4,0},{5,1},{6,2},{7,3},{8,12},{9,13},{10,... | collective-permute-start | bytes 3833864 | tf_op jit(solution)/shard_map/ppermute | solution.py:466
  58.8 6.7 %collective-permute-start.12 = (bf16[8,104,768]{2,1,0:T(8,128)(2,1)S(1)}, bf16[8,104,768]{2,1,0:T(8,128)(2,1)}, u32[]{:S(2)}, u32[]{:S(2)}) collective-permute-start(bf16[8,104,768]{2,1,0:T(8,128)(2,1)S(1)} %constant_dynamic-update-slice_fusion), channel_id=1, source_target_pairs={{0,4},{1,5},{2,6},{3,7},{4,0},{5,1},{6,2},{7,3},{8,12},{9,13},{10,... | collective-permute-start | bytes 3833864 | tf_op jit(solution)/shard_map/ppermute | solution.py:466
  60.2 17.1 %collective-permute-start.14 = (bf16[8,96,768]{2,1,0:T(8,128)(2,1)}, bf16[8,96,768]{2,1,0:T(8,128)(2,1)}, u32[]{:S(2)}, u32[]{:S(2)}) collective-permute-start(bf16[8,96,768]{2,1,0:T(8,128)(2,1)} %constant_dynamic-update-slice_fusion.5), channel_id=1, source_target_pairs={{0,8},{1,9},{2,10},{3,11},{4,20},{5,21},{6,22},{7,23},{8,0},{9,1},... | collective-permute-start | bytes 3538952 | tf_op jit(solution)/shard_map/ppermute | solution.py:466
  60.5 16.9 %collective-permute-start.15 = (bf16[2,96,768]{2,1,0:T(8,128)(2,1)}, bf16[2,96,768]{2,1,0:T(8,128)(2,1)}, u32[]{:S(2)}, u32[]{:S(2)}) collective-permute-start(bf16[2,96,768]{2,1,0:T(8,128)(2,1)} %pad_maximum_fusion.2), channel_id=1, source_target_pairs={{0,3},{1,2},{2,1},{3,0},{4,7},{5,6},{6,5},{7,4},{8,11},{9,10},{10,... | collective-permute-start | bytes 884744 | tf_op jit(solution)/shard_map/ppermute | solution.py:466
  65.6 12.4 %copy-start.13 = (bf16[768,96]{0,1:T(8,128)(2,1)S(1)}, bf16[768,96]{0,1:T(8,128)(2,1)}, u32[]{:S(2)}) copy-start(bf16[768,96]{0,1:T(8,128)(2,1)} %param.26) | copy-start | bytes 442372
  65.6 12.4 %copy-start.16 = (bf16[1,96,768]{2,1,0:T(8,128)(2,1)S(1)}, bf16[1,96,768]{2,1,0:T(8,128)(2,1)}, u32[]{:S(2)}) copy-start(bf16[1,96,768]{2,1,0:T(8,128)(2,1)} %copy-done.14) | copy-start | bytes 442372
  65.6 12.4 %copy-start.18 = (bf16[2,96,768]{2,1,0:T(8,128)(2,1)S(1)}, bf16[2,96,768]{2,1,0:T(8,128)(2,1)}, u32[]{:S(2)}) copy-start(bf16[2,96,768]{2,1,0:T(8,128)(2,1)} %copy-done.17) | copy-start | bytes 884740
  77.4 3.3 %collective-permute-start.17 = (bf16[8,96,768]{2,1,0:T(8,128)(2,1)}, bf16[8,96,768]{2,1,0:T(8,128)(2,1)S(1)}, u32[]{:S(2)}, u32[]{:S(2)}) collective-permute-start(bf16[8,96,768]{2,1,0:T(8,128)(2,1)} %collective-permute-done.14), channel_id=1, source_target_pairs={{0,4},{1,5},{2,6},{3,7},{4,0},{5,1},{6,2},{7,3},{8,12},{9,13},{10,... | collective-permute-start | bytes 3538952 | tf_op jit(solution)/shard_map/ppermute | solution.py:466
  77.4 4.7 %collective-permute-start.16 = (bf16[8,96,768]{2,1,0:T(8,128)(2,1)}, bf16[8,96,768]{2,1,0:T(8,128)(2,1)S(1)}, u32[]{:S(2)}, u32[]{:S(2)}) collective-permute-start(bf16[8,96,768]{2,1,0:T(8,128)(2,1)} %constant_dynamic-update-slice_fusion.5), channel_id=1, source_target_pairs={{0,4},{1,5},{2,6},{3,7},{4,0},{5,1},{6,2},{7,3},{8,12},{9,13},{10,... | collective-permute-start | bytes 3538952 | tf_op jit(solution)/shard_map/ppermute | solution.py:466
  79.3 16.3 %collective-permute-start.18 = (bf16[8,96,768]{2,1,0:T(8,128)(2,1)S(1)}, bf16[8,96,768]{2,1,0:T(8,128)(2,1)S(1)}, u32[]{:S(2)}, u32[]{:S(2)}) collective-permute-start(bf16[8,96,768]{2,1,0:T(8,128)(2,1)S(1)} %constant_dynamic-update-slice_fusion.10), channel_id=1, source_target_pairs={{0,8},{1,9},{2,10},{3,11},{4,20},{5,21},{6,22},{7,23},{8,0},{9,1},... | collective-permute-start | bytes 3538952 | tf_op jit(solution)/shard_map/ppermute | solution.py:466
  82.2 13.4 %copy-start.5 = (bf16[4,384,256]{2,1,0:T(8,128)(2,1)S(1)}, bf16[4,384,256]{2,1,0:T(8,128)(2,1)}, u32[]{:S(2)}) copy-start(bf16[4,384,256]{2,1,0:T(8,128)(2,1)} %get-tuple-element.99.refs_7_) | copy-start | bytes 2359300
  82.2 13.9 %copy-start.21 = (bf16[384,384]{1,0:T(8,128)(2,1)S(1)}, bf16[384,384]{1,0:T(8,128)(2,1)}, u32[]{:S(2)}) copy-start(bf16[384,384]{1,0:T(8,128)(2,1)} %get-tuple-element.97) | copy-start | bytes 884740
  82.2 17.8 %copy-start.24 = (bf16[384,384]{1,0:T(8,128)(2,1)S(1)}, bf16[384,384]{1,0:T(8,128)(2,1)}, u32[]{:S(2)}) copy-start(bf16[384,384]{1,0:T(8,128)(2,1)} %get-tuple-element.98) | copy-start | bytes 884740
  87.2 23.0 %collective-permute-start.25 = (bf16[4,384,768]{2,1,0:T(8,128)(2,1)S(1)}, bf16[4,384,768]{2,1,0:T(8,128)(2,1)S(1)}, u32[]{:S(2)}, u32[]{:S(2)}) collective-permute-start(bf16[4,384,768]{2,1,0:T(8,128)(2,1)S(1)} %get-tuple-element.91.z_ref.refs_1_), channel_id=1, source_target_pairs={{0,4},{1,5},{2,6},{3,7},{4,0},{5,1},{6,2},{7,3},{8,12},{9,13},{10,... | collective-permute-start | bytes 7077896 | tf_op jit(solution)/shard_map/ppermute | solution.py:457
  87.4 14.2 %collective-permute-start.19 = (bf16[8,96,768]{2,1,0:T(8,128)(2,1)S(1)}, bf16[8,96,768]{2,1,0:T(8,128)(2,1)S(1)}, u32[]{:S(2)}, u32[]{:S(2)}) collective-permute-start(bf16[8,96,768]{2,1,0:T(8,128)(2,1)S(1)} %constant_dynamic-update-slice_fusion.10), channel_id=1, source_target_pairs={{0,4},{1,5},{2,6},{3,7},{4,0},{5,1},{6,2},{7,3},{8,12},{9,13},{10,... | collective-permute-start | bytes 3538952 | tf_op jit(solution)/shard_map/ppermute | solution.py:466
  95.6 6.0 %collective-permute-start.20 = (bf16[8,96,768]{2,1,0:T(8,128)(2,1)S(1)}, bf16[8,96,768]{2,1,0:T(8,128)(2,1)S(1)}, u32[]{:S(2)}, u32[]{:S(2)}) collective-permute-start(bf16[8,96,768]{2,1,0:T(8,128)(2,1)S(1)} %collective-permute-done.18), channel_id=1, source_target_pairs={{0,4},{1,5},{2,6},{3,7},{4,0},{5,1},{6,2},{7,3},{8,12},{9,13},{10,... | collective-permute-start | bytes 3538952 | tf_op jit(solution)/shard_map/ppermute | solution.py:466
  95.6 6.0 %collective-permute-start.23 = (bf16[4,384,256]{2,1,0:T(8,128)(2,1)S(1)}, bf16[4,384,256]{2,1,0:T(8,128)(2,1)S(1)}, u32[]{:S(2)}, u32[]{:S(2)}) collective-permute-start(bf16[4,384,256]{2,1,0:T(8,128)(2,1)S(1)} %copy-done.5), channel_id=1, source_target_pairs={{0,4},{1,5},{2,6},{3,7},{4,0},{5,1},{6,2},{7,3},{8,12},{9,13},{10,... | collective-permute-start | bytes 2359304 | tf_op jit(solution)/shard_map/ppermute | solution.py:457
  96.1 3.9 %collective-permute-start.21 = (bf16[384,384]{1,0:T(8,128)(2,1)S(1)}, bf16[384,384]{1,0:T(8,128)(2,1)S(1)}, u32[]{:S(2)}, u32[]{:S(2)}) collective-permute-start(bf16[384,384]{1,0:T(8,128)(2,1)S(1)} %copy-done.21), channel_id=1, source_target_pairs={{0,4},{1,5},{2,6},{3,7},{4,0},{5,1},{6,2},{7,3},{8,12},{9,13},{10,... | collective-permute-start | bytes 884744 | tf_op jit(solution)/shard_map/ppermute | solution.py:457
  100.0 1.6 collective-permute-start.22
  106.9 3.3 %collective-permute-start.24 = (bf16[384,384]{1,0:T(8,128)(2,1)S(1)}, bf16[384,384]{1,0:T(8,128)(2,1)S(1)}, u32[]{:S(2)}, u32[]{:S(2)}) collective-permute-start(bf16[384,384]{1,0:T(8,128)(2,1)S(1)} %get-tuple-element.108), channel_id=1, source_target_pairs={{0,4},{1,5},{2,6},{3,7},{4,0},{5,1},{6,2},{7,3},{8,12},{9,13},{10,... | collective-permute-start | bytes 884744 | tf_op jit(solution)/shard_map/ppermute | solution.py:457
  109.8 10.6 %collective-permute-start.26 = (bf16[4,384,768]{2,1,0:T(8,128)(2,1)S(1)}, bf16[4,384,768]{2,1,0:T(8,128)(2,1)S(1)}, u32[]{:S(2)}, u32[]{:S(2)}) collective-permute-start(bf16[4,384,768]{2,1,0:T(8,128)(2,1)S(1)} %get-tuple-element.110.du_ref.refs_1_), channel_id=1, source_target_pairs={{0,4},{1,5},{2,6},{3,7},{4,0},{5,1},{6,2},{7,3},{8,12},{9,13},{10,... | collective-permute-start | bytes 7077896 | tf_op jit(solution)/shard_map/ppermute | solution.py:457
  113.5 16.3 %collective-permute-start.28 = (bf16[8,96,768]{2,1,0:T(8,128)(2,1)S(1)}, bf16[8,96,768]{2,1,0:T(8,128)(2,1)S(1)}, u32[]{:S(2)}, u32[]{:S(2)}) collective-permute-start(bf16[8,96,768]{2,1,0:T(8,128)(2,1)S(1)} %bitcast.131), channel_id=1, source_target_pairs={{0,8},{1,9},{2,10},{3,11},{4,20},{5,21},{6,22},{7,23},{8,0},{9,1},... | collective-permute-start | bytes 3538952 | tf_op jit(solution)/shard_map/ppermute | solution.py:484
  114.8 5.6 %copy-start.6 = (bf16[384,384]{1,0:T(8,128)(2,1)S(1)}, bf16[384,384]{1,0:T(8,128)(2,1)}, u32[]{:S(2)}) copy-start(bf16[384,384]{1,0:T(8,128)(2,1)} %get-tuple-element.117.refs_0_) | copy-start | bytes 884740
  120.3 4.2 %collective-permute-start.27 = (bf16[384,384]{1,0:T(8,128)(2,1)S(1)}, bf16[384,384]{1,0:T(8,128)(2,1)S(1)}, u32[]{:S(2)}, u32[]{:S(2)}) collective-permute-start(bf16[384,384]{1,0:T(8,128)(2,1)S(1)} %get-tuple-element.120), channel_id=1, source_target_pairs={{0,4},{1,5},{2,6},{3,7},{4,0},{5,1},{6,2},{7,3},{8,12},{9,13},{10,... | collective-permute-start | bytes 884744 | tf_op jit(solution)/shard_map/ppermute | solution.py:457
  120.4 9.3 %copy-start.2 = (f32[4,3,128,384]{3,2,1,0:T(8,128)S(1)}, f32[4,3,128,384]{3,2,1,0:T(8,128)}, u32[]{:S(2)}) copy-start(f32[4,3,128,384]{3,2,1,0:T(8,128)} %get-tuple-element.124.p_ref) | copy-start | bytes 7077892
  120.4 9.3 %copy-start.3 = (bf16[4,384,576]{2,1,0:T(8,128)(2,1)S(1)}, bf16[4,384,576]{2,1,0:T(8,128)(2,1)}, u32[]{:S(2)}) copy-start(bf16[4,384,576]{2,1,0:T(8,128)(2,1)} %get-tuple-element.123.qkv_ref) | copy-start | bytes 5308420
  123.7 25.6 %collective-permute-start.30 = (bf16[8,96,768]{2,1,0:T(8,128)(2,1)S(1)}, bf16[8,96,768]{2,1,0:T(8,128)(2,1)S(1)}, u32[]{:S(2)}, u32[]{:S(2)}) collective-permute-start(bf16[8,96,768]{2,1,0:T(8,128)(2,1)S(1)} %bitcast.130), channel_id=1, source_target_pairs={{0,8},{1,9},{2,10},{3,11},{4,20},{5,21},{6,22},{7,23},{8,0},{9,1},... | collective-permute-start | bytes 3538952 | tf_op jit(solution)/shard_map/ppermute | solution.py:484
  138.5 10.8 %collective-permute-start.31 = (bf16[2,384,640]{2,1,0:T(8,128)(2,1)S(1)}, bf16[2,384,640]{2,1,0:T(8,128)(2,1)S(1)}, u32[]{:S(2)}, u32[]{:S(2)}) collective-permute-start(bf16[2,384,640]{2,1,0:T(8,128)(2,1)S(1)} %get-tuple-element.127.low_ref.refs_1_), channel_id=1, source_target_pairs={{0,4},{1,5},{2,6},{3,7},{4,0},{5,1},{6,2},{7,3},{8,12},{9,13},{10,... | collective-permute-start | bytes 2949128 | tf_op jit(solution)/shard_map/ppermute | solution.py:457
  138.6 10.7 %collective-permute-start.32 = (bf16[2,384,640]{2,1,0:T(8,128)(2,1)S(1)}, bf16[2,384,640]{2,1,0:T(8,128)(2,1)S(1)}, u32[]{:S(2)}, u32[]{:S(2)}) collective-permute-start(bf16[2,384,640]{2,1,0:T(8,128)(2,1)S(1)} %get-tuple-element.128.high_ref.refs_2_), channel_id=1, source_target_pairs={{0,4},{1,5},{2,6},{3,7},{4,0},{5,1},{6,2},{7,3},{8,12},{9,13},{10,... | collective-permute-start | bytes 2949128 | tf_op jit(solution)/shard_map/ppermute | solution.py:457
  139.3 9.9 %collective-permute-start.29 = (bf16[4,96,768]{2,1,0:T(8,128)(2,1)S(1)}, bf16[4,96,768]{2,1,0:T(8,128)(2,1)S(1)}, u32[]{:S(2)}, u32[]{:S(2)}) collective-permute-start(bf16[4,96,768]{2,1,0:T(8,128)(2,1)S(1)} %get-tuple-element.175), channel_id=1, source_target_pairs={{0,16},{1,17},{2,18},{3,19},{4,12},{5,13},{6,14},{7,15},{8,24},{9,... | collective-permute-start | bytes 1769480 | tf_op jit(solution)/shard_map/ppermute | solution.py:484
  140.8 8.5 %collective-permute-start.33 = (f32[4,4,768]{2,1,0:T(4,128)S(1)}, f32[4,4,768]{2,1,0:T(4,128)S(1)}, u32[]{:S(2)}, u32[]{:S(2)}) collective-permute-start(f32[4,4,768]{2,1,0:T(4,128)S(1)} %get-tuple-element.133), channel_id=1, source_target_pairs={{0,4},{1,5},{2,6},{3,7},{4,0},{5,1},{6,2},{7,3},{8,12},{9,13},{10,... | collective-permute-start | bytes 147464 | tf_op jit(solution)/shard_map/ppermute | solution.py:457
  141.9 7.4 %copy-start.4 = (bf16[384,384]{1,0:T(8,128)(2,1)S(1)}, bf16[384,384]{1,0:T(8,128)(2,1)}, u32[]{:S(2)}) copy-start(bf16[384,384]{1,0:T(8,128)(2,1)} %get-tuple-element.131.refs_0_) | copy-start | bytes 884740
  153.7 23.6 %collective-permute-start.34 = (bf16[8,104,768]{2,1,0:T(8,128)(2,1)S(1)}, bf16[8,104,768]{2,1,0:T(8,128)(2,1)S(1)}, u32[]{:S(2)}, u32[]{:S(2)}) collective-permute-start(bf16[8,104,768]{2,1,0:T(8,128)(2,1)S(1)} %bitcast.129), channel_id=1, source_target_pairs={{0,8},{1,9},{2,10},{3,11},{4,20},{5,21},{6,22},{7,23},{8,0},{9,1},... | collective-permute-start | bytes 3833864 | tf_op jit(solution)/shard_map/ppermute | solution.py:484
  155.3 18.8 %collective-permute-start.38 = (bf16[4,96,768]{2,1,0:T(8,128)(2,1)S(1)}, bf16[4,96,768]{2,1,0:T(8,128)(2,1)S(1)}, u32[]{:S(2)}, u32[]{:S(2)}) collective-permute-start(bf16[4,96,768]{2,1,0:T(8,128)(2,1)S(1)} %get-tuple-element.173), channel_id=1, source_target_pairs={{0,16},{1,17},{2,18},{3,19},{4,12},{5,13},{6,14},{7,15},{8,24},{9,... | collective-permute-start | bytes 1769480 | tf_op jit(solution)/shard_map/ppermute | solution.py:484
  156.3 9.0 %collective-permute-start.35 = (bf16[1,96,768]{2,1,0:T(8,128)(2,1)S(1)}, bf16[1,96,768]{2,1,0:T(8,128)(2,1)S(1)}, u32[]{:S(2)}, u32[]{:S(2)}) collective-permute-start(bf16[1,96,768]{2,1,0:T(8,128)(2,1)S(1)} %get-tuple-element.184), channel_id=1, source_target_pairs={{0,1},{1,0},{2,3},{3,2},{4,5},{5,4},{6,7},{7,6},{8,9},{9,8},{10,11... | collective-permute-start | bytes 442376 | tf_op jit(solution)/shard_map/ppermute | solution.py:484
  159.2 14.0 %collective-permute-start.36 = (bf16[1,96,768]{2,1,0:T(8,128)(2,1)S(1)}, bf16[1,96,768]{2,1,0:T(8,128)(2,1)S(1)}, u32[]{:S(2)}, u32[]{:S(2)}) collective-permute-start(bf16[1,96,768]{2,1,0:T(8,128)(2,1)S(1)} %get-tuple-element.183), channel_id=1, source_target_pairs={{0,2},{1,3},{2,0},{3,1},{4,6},{5,7},{6,4},{7,5},{8,10},{9,11},{10,... | collective-permute-start | bytes 442376 | tf_op jit(solution)/shard_map/ppermute | solution.py:484
  160.4 12.8 %collective-permute-start.37 = (bf16[1,96,768]{2,1,0:T(8,128)(2,1)S(1)}, bf16[1,96,768]{2,1,0:T(8,128)(2,1)S(1)}, u32[]{:S(2)}, u32[]{:S(2)}) collective-permute-start(bf16[1,96,768]{2,1,0:T(8,128)(2,1)S(1)} %get-tuple-element.182), channel_id=1, source_target_pairs={{0,3},{1,2},{2,1},{3,0},{4,7},{5,6},{6,5},{7,4},{8,11},{9,10},{10,... | collective-permute-start | bytes 442376 | tf_op jit(solution)/shard_map/ppermute | solution.py:484
  174.1 5.6 %collective-permute-start.39 = (bf16[1,96,768]{2,1,0:T(8,128)(2,1)S(1)}, bf16[1,96,768]{2,1,0:T(8,128)(2,1)S(1)}, u32[]{:S(2)}, u32[]{:S(2)}) collective-permute-start(bf16[1,96,768]{2,1,0:T(8,128)(2,1)S(1)} %get-tuple-element.181), channel_id=1, source_target_pairs={{0,1},{1,0},{2,3},{3,2},{4,5},{5,4},{6,7},{7,6},{8,9},{9,8},{10,11... | collective-permute-start | bytes 442376 | tf_op jit(solution)/shard_map/ppermute | solution.py:484
  179.7 10.4 %collective-permute-start.40 = (bf16[4,104,768]{2,1,0:T(8,128)(2,1)S(1)}, bf16[4,104,768]{2,1,0:T(8,128)(2,1)S(1)}, u32[]{:S(2)}, u32[]{:S(2)}) collective-permute-start(bf16[4,104,768]{2,1,0:T(8,128)(2,1)S(1)} %get-tuple-element.136), channel_id=1, source_target_pairs={{0,16},{1,17},{2,18},{3,19},{4,12},{5,13},{6,14},{7,15},{8,24},{9,... | collective-permute-start | bytes 1916936 | tf_op jit(solution)/shard_map/ppermute | solution.py:484
  180.2 12.8 %collective-permute-start.41 = (bf16[1,96,768]{2,1,0:T(8,128)(2,1)S(1)}, bf16[1,96,768]{2,1,0:T(8,128)(2,1)S(1)}, u32[]{:S(2)}, u32[]{:S(2)}) collective-permute-start(bf16[1,96,768]{2,1,0:T(8,128)(2,1)S(1)} %get-tuple-element.180), channel_id=1, source_target_pairs={{0,2},{1,3},{2,0},{3,1},{4,6},{5,7},{6,4},{7,5},{8,10},{9,11},{10,... | collective-permute-start | bytes 442376 | tf_op jit(solution)/shard_map/ppermute | solution.py:484
  183.3 9.7 %collective-permute-start.42 = (bf16[1,96,768]{2,1,0:T(8,128)(2,1)S(1)}, bf16[1,96,768]{2,1,0:T(8,128)(2,1)S(1)}, u32[]{:S(2)}, u32[]{:S(2)}) collective-permute-start(bf16[1,96,768]{2,1,0:T(8,128)(2,1)S(1)} %get-tuple-element.179), channel_id=1, source_target_pairs={{0,3},{1,2},{2,1},{3,0},{4,7},{5,6},{6,5},{7,4},{8,11},{9,10},{10,... | collective-permute-start | bytes 442376 | tf_op jit(solution)/shard_map/ppermute | solution.py:484
  193.0 8.5 %collective-permute-start.43 = (bf16[1,104,768]{2,1,0:T(8,128)(2,1)S(1)}, bf16[1,104,768]{2,1,0:T(8,128)(2,1)S(1)}, u32[]{:S(2)}, u32[]{:S(2)}) collective-permute-start(bf16[1,104,768]{2,1,0:T(8,128)(2,1)S(1)} %get-tuple-element.137), channel_id=1, source_target_pairs={{0,1},{1,0},{2,3},{3,2},{4,5},{5,4},{6,7},{7,6},{8,9},{9,8},{10,11... | collective-permute-start | bytes 479240 | tf_op jit(solution)/shard_map/ppermute | solution.py:484
  196.2 14.2 %collective-permute-start.44 = (bf16[1,104,768]{2,1,0:T(8,128)(2,1)S(1)}, bf16[1,104,768]{2,1,0:T(8,128)(2,1)S(1)}, u32[]{:S(2)}, u32[]{:S(2)}) collective-permute-start(bf16[1,104,768]{2,1,0:T(8,128)(2,1)S(1)} %get-tuple-element.138), channel_id=1, source_target_pairs={{0,2},{1,3},{2,0},{3,1},{4,6},{5,7},{6,4},{7,5},{8,10},{9,11},{10,... | collective-permute-start | bytes 479240 | tf_op jit(solution)/shard_map/ppermute | solution.py:484
  197.2 13.1 %collective-permute-start.45 = (bf16[1,104,768]{2,1,0:T(8,128)(2,1)S(1)}, bf16[1,104,768]{2,1,0:T(8,128)(2,1)S(1)}, u32[]{:S(2)}, u32[]{:S(2)}) collective-permute-start(bf16[1,104,768]{2,1,0:T(8,128)(2,1)S(1)} %get-tuple-element.139), channel_id=1, source_target_pairs={{0,3},{1,2},{2,1},{3,0},{4,7},{5,6},{6,5},{7,4},{8,11},{9,10},{10,... | collective-permute-start | bytes 479240 | tf_op jit(solution)/shard_map/ppermute | solution.py:484
  (7 other events, 22.4 us)

commit v6 on v5

--- a/solution.py
+++ b/solution.py
@@ -19,6 +19,7 @@
 VMEM_LIMIT = 24 * 1024 * 1024
 COST = 30_000_000
 NORM = 2000
+SMALL = pltpu.CompilerParams(vmem_limit_bytes=8 * 1024 * 1024)
 
 
 def nn(a, b):
@@ -75,6 +76,14 @@
     extra = first_ref.shape[0] - rows
     here = lax.broadcasted_iota(jnp.int32, (extra, wide), 0)
     first_ref[rows:, :] = jnp.where(here == 0, row, 0.0).astype(bf16)
+
+
+def reorder(h_ref, perm_ref, x_ref, keep_ref, send_ref):
+    x = nn(h_ref[...], perm_ref[...]).astype(bf16)
+    x_ref[...] = x
+    turned = x.T
+    keep_ref[...] = turned[: x.shape[1] // 2]
+    send_ref[...] = turned[x.shape[1] // 2 :]
 
 
 def stacked(values, hc):
@@ -276,23 +285,27 @@
     return jnp.where(pl.program_id(0) < pl.num_programs(0) // 2, refs[0][0, :, :width], refs[1][0, :, :width])
 
 
-def weight_gradient(groups, vectors, *refs):
+def weight_gradient(groups, vectors, which, *refs):
     refs = list(refs)
     parts = []
     for pairs, split, width in groups:
         total = None
         for _ in range(pairs):
-            add = nn(refs.pop(0)[...], step_value([refs.pop(0) for _ in range(split)], width))
+            rows = refs.pop(0)
+            half = rows.shape[0] // 2
+            rows = rows[...] if which is None else rows[which * half : (which + 1) * half, :]
+            add = nn(rows, step_value([refs.pop(0) for _ in range(split)], width))
             total = add if total is None else total + add
         parts.append(total)
     grad = jnp.concatenate(parts, axis=1)
     extra = sum(refs.pop(0)[0].astype(f32) for _ in range(vectors)) if vectors else None
-    half = grad.shape[0] // 2
+    half = grad.shape[0] // len(refs)
     for n, ref in enumerate(refs):
         put(grad[n * half : (n + 1) * half], ref)
         if vectors:
             for j in range(ref.shape[0]):
-                row = extra[n * ref.shape[0] + j : n * ref.shape[0] + j + 1]
+                at = (n if which is None else which) * ref.shape[0] + j
+                row = extra[at : at + 1]
                 tail = ref.shape[2] - BLK
                 ref[j, 0, BLK:, :] = jnp.where(iota((tail, row.shape[1]), 0) == 0, row, 0.0).astype(bf16)
 
@@ -540,9 +553,10 @@
     lane = jnp.arange(D)
     same_block = jnp.repeat(jnp.repeat((absolute[:, None] == rel[None, :]).T, BLK, axis=0), BLK, axis=1)
     perm = (same_block & ((lane[:, None] % BLK) == (lane[None, :] % BLK))).astype(bf16)
-    x = nn(hidden_in.reshape(T, D), perm).astype(bf16)
-    x_t = lax.dot_general(perm, hidden_in.reshape(T, D), (((0,), (1,)), ((), ())), preferred_element_type=f32).astype(bf16)
-    x_keep, x_send = x_t[: D // 2], x_t[D // 2 :]
+    turned = (D // 2, T)
+    x, x_keep, x_send = pl.pallas_call(
+        reorder, out_shape=[sds((T, D), bf16), sds(turned, bf16), sds(turned, bf16)], compiler_params=SMALL
+    )(hidden_in.reshape(T, D), perm)
     pg = jnp.einsum("gsd,de->gse", pooled_grad.reshape(G, segs, D), perm.astype(f32), precision=HI)
     seg_r = segment_ids.reshape(G, L)
     seg_c = segment_ids.reshape(T, 1)
@@ -553,6 +567,7 @@
         near_z = last.send("Z", *done, tables=slice(0, 2))
         done = first.stage("3", *done) + middle.stage("2", *done) + near_z
         first.stage("C", *done)
+        x = after(x, x_other)
         got_u3, far_z = middle.send("3", *done), last.send("Z", *done, tables=slice(2, None))
         w_qo = first.pieces(2, n_t)
     else:
@@ -592,7 +607,6 @@
         (w, pl.BlockSpec((w.shape[0], n_t, 8, w.shape[3]), lambda s: (0, 0, BLK // 8, 0), pipeline_mode=pl.Buffered(1)))
         for w in w_qo
     ]
-    turned = (D // 2, T)
     qkv, prob, o, n1, x1, r1, n1b, n1_keep, n1_send, vec_d, b_u = call(
         partial(attention_forward, sizes), n_t, 10,
         wholes(x) + weights(*w_qo) + tails + wholes(hot_d, hot_e, seg_c, seg_r),
@@ -611,7 +625,7 @@
         w_up, w_down = middle.pieces(2, n_t), last.pieces(n_t, 2)
         n1_other = swap(n1_send, tables)
         o_other = swap(o, tables)
-        pg = after(pg, x_other, n1_other, o_other)
+        b_u = after(b_u, n1_other, o_other)
     z, dgelu = call(
         up_forward, n_t, 4, wholes(n1b) + weights(*w_up) + leads(b_u),
         leads(sds((n_t, T, fc), bf16), sds((n_t, T, fc), f32)),
@@ -624,14 +638,21 @@
         [pltpu.VMEM((T, D), f32)],
     )
 
-    def gradient(groups, vectors=()):
+    def gradient(groups, vectors=(), at_once=True):
         ins, kinds = [], []
         for width, *pairs in groups:
             kinds.append((len(pairs), len(pairs[0][1]), width))
             for lhs, values in pairs:
                 ins += wholes(lhs) + (leads(*values) if len(values) == 1 else halved(*values))
         out = sds((n_i // 4, n_t, BLK + (8 if vectors else 0), sum(k[2] for k in kinds)), bf16)
-        return call(partial(weight_gradient, kinds, len(vectors)), n_t, 4, ins + leads(*vectors), [(out, half_spec(out))] * 2)
+
+        def share(which):
+            return call(
+                partial(weight_gradient, kinds, len(vectors), which), n_t, 2, ins + leads(*vectors),
+                [(out, half_spec(out))] * (2 if which is None else 1),
+            )
+
+        return share(None) if at_once else (share(0)[0], share(1)[0])
 
     def halved(low, high):
         block = (1,) + low.shape[1:]
@@ -650,10 +671,11 @@
     if pairwise:
         db_other = swap(db_send, tables)
         du_other = swap(du, tables)
-        down_keep, down_send = gradient([[fc, (after(db_keep, g_bu), [z]), (db_other, [z_other])]])
+        down_keep, down_send = gradient([[fc, (after(db_keep, g_bu), [z]), (db_other, [z_other])]], at_once=False)
         s_down = Scatter(flat(down_keep), flat(down_send), tables)
         got_d3 = s_down.stage("3", 2)
-        du_next = after(du, down_keep)
+        du_next = after(du, down_send)
+        dab_after = down_keep
     else:
         du_next = du
     da, dab, da_keep, da_send, sums1 = call(
@@ -669,7 +691,7 @@
         dab = after(dab, up_keep)
     rows = sds((n_t, n_i // 2, 4 * hc), f32)
     if pairwise:
-        dab = after(dab, da_other, *got_d3)
+        dab = after(dab, da_other, dab_after, *got_d3)
     dq_half = sds((n_t // 2, T, q_wide), bf16)
     *dq, v_keep, v_send = call(
         partial(attention_backward, sizes), n_t, 8,
@@ -681,24 +703,25 @@
         dq_other = [swap(d, tables) for d in dq]
         v_other = swap(v_send, tables)
         got_d2 = s_down.stage("2", n_t)
+    pooled = jnp.einsum("gse,de->gsd", pooled, perm.astype(f32), precision=HI)
+    if pairwise:
+        x_now = after(x_keep, *got_u3)
+        qo_keep, qo_send = gradient(
+            [[3 * hc, (x_now, dq), (x_other, dq_other)], [hc, (da_keep, [o]), (da_other, [o_other])]], (v_keep, v_other)
+        )
+        s_qo = Scatter(flat(qo_keep), flat(qo_send), tables)
+        got_u2 = s_up.stage("2", n_t)
+        got_q3 = s_qo.stage("3", 2, *got_d2, *got_u2)
+        got_z = s_down.stage("Z", 1)
+        dq = [after(d, pooled, qo_keep) for d in dq]
     dx = call(
         input_backward, n_t, 4, halved(*dq) + weights(*w_qo) + wholes(da, perm), wholes(sds((T, D), f32)),
         [pltpu.VMEM((T, D), f32)],
     )[0]
-    if pairwise:
-        x_now = after(x_keep, dx, *got_d2, *got_u3)
-        qo_keep, qo_send = gradient(
-            [[3 * hc, (x_now, dq), (x_other, dq_other)], [hc, (da_keep, [o]), (da_other, [o_other])]], (v_keep, v_other)
-        )
-        s_qo = Scatter(flat(qo_keep), flat(qo_send), tables)
-        got_z = s_down.stage("Z", 1)
-        got_u2 = s_up.stage("2", n_t)
-        got_q3 = s_qo.stage("3", 2)
-    pooled = jnp.einsum("gse,de->gsd", pooled, perm.astype(f32), precision=HI)
 
     if pairwise:
         got = s_up.stage("Z", 1)
-        s_qo.stage("2", n_t, *got_z, *got_u2, pooled, s_down.keep, got[0])
+        s_qo.stage("2", n_t, dx, *got_z)
         s_qo.stage("Z", 1, *got)
         g_down, g_up, g_qo = s_down.keep[0], s_up.keep[0], s_qo.keep[0]
         g_v = g_qo[BLK, :n_vec]

time: 214 us -> 207 us (0.967)
  waiting for transfers between devices: 80.2 us -> 72.4 us
  starting transfers between devices: 52.6 us -> 48.6 us
  Pallas kernels: 59.1 us -> 61.9 us
    ppermute x15, waiting for transfers between devices: 36.9 us -> 33.8 us  [stage(): lax.ppermute(after(s, *done), AXES, t)]
    unnamed x64, local copies, waits for them, and re-layouts: 4 us -> 7.07 us
    ppermute x10, waiting for transfers between devices: 5.27 us -> 2.84 us  [swap(): return lax.ppermute(after(value, *done), AXES, tables['C'][0])]
    ppermute x21, waiting for transfers between devices: 38.1 us -> 35.8 us  [send(): lax.ppermute(after(h, *done), AXES, t)]
    pallas_call x10 -> x11, Pallas kernels: 57.1 us -> 58.5 us  [call(): pl.pallas_call(body, grid=(n_t,), in_specs=[s for _, s in ins], out_specs...]
  transfers between devices with their start and end apart: 46 -> 46, of which waited for: 19 -> 20; matrix products, arithmetic and copies ran while one was open for 8% -> 9% of each run, Pallas kernels for 25% -> 29%
where the time goes in v6:
time: 207 us
  waiting for transfers between devices  72.4 us (35%)
  Pallas kernels  61.9 us (30%)
  starting transfers between devices  48.6 us (23%)
  local copies, waits for them, and re-layouts  11.7 us (6%)
  other arithmetic  8.07 us (4%)
  matrix products  2.99 us (1%)
    pallas_call x11, Pallas kernels, call(): pl.pallas_call(body, grid=(n_t,), in_specs=[s for _, s in ins], out_specs...  58.5 us
    ppermute x21, waiting for transfers between devices, send(): lax.ppermute(after(h, *done), AXES, t)  35.8 us
    ppermute x15, waiting for transfers between devices, stage(): lax.ppermute(after(s, *done), AXES, t)  33.8 us
    ppermute x21, starting transfers between devices, send(): lax.ppermute(after(h, *done), AXES, t)  25.3 us
    ppermute x15, starting transfers between devices, stage(): lax.ppermute(after(s, *done), AXES, t)  21.8 us
    unnamed x64, local copies, waits for them, and re-layouts  7.07 us
  transfers between devices with their start and end apart: 46, of which 20 were waited for; matrix products, arithmetic and copies ran while one was open for 9% of the time, Pallas kernels for 29%

profile of v6, /device:TPU:0, one launch (start us, length us, event | category | flops | bytes accessed | tf_op | source)
XLA Modules:
  0.0 206.9 jit_solution(17227057138874257829)
XLA Ops:
  0.7 2.0 shard_map.255
  2.6 5.0 %collective-permute-start.2 = (bf16[1,104,768]{2,1,0:T(8,128)(2,1)}, bf16[1,104,768]{2,1,0:T(8,128)(2,1)S(1)}, u32[]{:S(2)}, u32[]{:S(2)}) collective-permute-start(bf16[1,104,768]{2,1,0:T(8,128)(2,1)} %bitcast.136), channel_id=1, source_target_pairs={{0,3},{1,2},{2,1},{3,0},{4,7},{5,6},{6,5},{7,4},{8,11},{9,10},{10,... | collective-permute-start | bytes 479240 | tf_op jit(solution)/shard_map/ppermute | solution.py:479
  8.2 1.7 collective-permute-start.3
  12.5 1.0 convolution_bitcast_fusion.pg_ref
  13.6 1.4 shard_map.254
  15.0 6.5 %collective-permute-done.1 = bf16[1,104,768]{2,1,0:T(8,128)(2,1)} collective-permute-done((bf16[1,104,768]{2,1,0:T(8,128)(2,1)}, bf16[1,104,768]{2,1,0:T(8,128)(2,1)}, u32[]{:S(2)}, u32[]{:S(2)}) %collective-permute-start.1) | collective-permute-done | bytes 159776 | tf_op jit(solution)/shard_map/ppermute | solution.py:479
  21.5 1.1 pad_maximum_fusion
  22.6 1.6 collective-permute-start.4
  24.3 3.0 %collective-permute-start.6 = (bf16[1,96,768]{2,1,0:T(8,128)(2,1)S(1)}, bf16[1,96,768]{2,1,0:T(8,128)(2,1)S(1)}, u32[]{:S(2)}, u32[]{:S(2)}) collective-permute-start(bf16[1,96,768]{2,1,0:T(8,128)(2,1)S(1)} %bitcast.144), channel_id=1, source_target_pairs={{0,2},{1,3},{2,0},{3,1},{4,6},{5,7},{6,4},{7,5},{8,10},{9,11},{10,... | collective-permute-start | bytes 442376 | tf_op jit(solution)/shard_map/ppermute | solution.py:479
  27.3 1.3 collective-permute-start.7
  28.7 0.9 constant_dynamic-update-slice_fusion.3
  29.6 0.9 constant_dynamic-update-slice_fusion.2
  30.6 2.5 %collective-permute-done.4 = bf16[4,104,768]{2,1,0:T(8,128)(2,1)S(1)} collective-permute-done((bf16[4,104,768]{2,1,0:T(8,128)(2,1)S(1)}, bf16[4,104,768]{2,1,0:T(8,128)(2,1)S(1)}, u32[]{:S(2)}, u32[]{:S(2)}) %collective-permute-start.4) | collective-permute-done | bytes 639008 | tf_op jit(solution)/shard_map/ppermute | solution.py:479
  33.1 4.5 %collective-permute-done.6 = bf16[1,96,768]{2,1,0:T(8,128)(2,1)S(1)} collective-permute-done((bf16[1,96,768]{2,1,0:T(8,128)(2,1)S(1)}, bf16[1,96,768]{2,1,0:T(8,128)(2,1)S(1)}, u32[]{:S(2)}, u32[]{:S(2)}) %collective-permute-start.6) | collective-permute-done | bytes 147488 | tf_op jit(solution)/shard_map/ppermute | solution.py:479
  38.4 1.4 collective-permute-start.10
  40.5 1.7 pad_maximum_fusion.2
  42.2 2.3 %collective-permute-start.11 = (bf16[2,96,768]{2,1,0:T(8,128)(2,1)}, bf16[2,96,768]{2,1,0:T(8,128)(2,1)S(1)}, u32[]{:S(2)}, u32[]{:S(2)}) collective-permute-start(bf16[2,96,768]{2,1,0:T(8,128)(2,1)} %pad_maximum_fusion.2), channel_id=1, source_target_pairs={{0,1},{1,0},{2,3},{3,2},{4,5},{5,4},{6,7},{7,6},{8,9},{9,8},{10,11... | collective-permute-start | bytes 884744 | tf_op jit(solution)/shard_map/ppermute | solution.py:479
  44.5 0.8 collective-permute-start.12
  47.3 8.6 %collective-permute-done.11 = bf16[2,96,768]{2,1,0:T(8,128)(2,1)S(1)} collective-permute-done((bf16[2,96,768]{2,1,0:T(8,128)(2,1)}, bf16[2,96,768]{2,1,0:T(8,128)(2,1)S(1)}, u32[]{:S(2)}, u32[]{:S(2)}) %collective-permute-start.11) | collective-permute-done | bytes 294944 | tf_op jit(solution)/shard_map/ppermute | solution.py:479
  56.0 2.8 %collective-permute-done.12 = bf16[2,96,768]{2,1,0:T(8,128)(2,1)S(1)} collective-permute-done((bf16[2,96,768]{2,1,0:T(8,128)(2,1)}, bf16[2,96,768]{2,1,0:T(8,128)(2,1)S(1)}, u32[]{:S(2)}, u32[]{:S(2)}) %collective-permute-start.12) | collective-permute-done | bytes 294944 | tf_op jit(solution)/shard_map/ppermute | solution.py:479
  59.5 0.9 constant_dynamic-update-slice_fusion.5
  60.4 1.7 collective-permute-start.15
  62.1 2.2 %collective-permute-start.16 = (bf16[2,96,768]{2,1,0:T(8,128)(2,1)}, bf16[2,96,768]{2,1,0:T(8,128)(2,1)}, u32[]{:S(2)}, u32[]{:S(2)}) collective-permute-start(bf16[2,96,768]{2,1,0:T(8,128)(2,1)} %pad_maximum_fusion.2), channel_id=1, source_target_pairs={{0,3},{1,2},{2,1},{3,0},{4,7},{5,6},{6,5},{7,4},{8,11},{9,10},{10,... | collective-permute-start | bytes 884744 | tf_op jit(solution)/shard_map/ppermute | solution.py:479
  64.5 11.7 %shard_map.256 = (bf16[4,384,576]{2,1,0:T(8,128)(2,1)}, f32[4,3,128,384]{3,2,1,0:T(8,128)}, bf16[4,384,256]{2,1,0:T(8,128)(2,1)}, f32[384,768]{1,0:T(8,128)S(1)}...) custom-call(bf16[384,768]{1,0:T(8,128)(2,1)S(1)} %get-tuple-element., ...), custom_call_target="tpu_custom_call" | custom-call | flops 300000000 | tf_op jit(solution)/shard_map/pallas_call | solution.py:435
  77.4 1.0 constant_dynamic-update-slice_fusion.13
  78.5 1.0 constant_dynamic-update-slice_fusion.10
  79.5 1.8 collective-permute-start.21
  81.3 1.7 collective-permute-done.19.refs_2_
  83.0 4.9 %shard_map.257 = (bf16[4,384,768]{2,1,0:T(8,128)(2,1)S(1)}, f32[4,384,768]{2,1,0:T(8,128)S(1)}) custom-call(bf16[384,768]{1,0:T(8,128)(2,1)S(1)} %get-tuple-element.94.n_ref, bf16[2,4,96,768]{3,2,1,0:T(8,128)(2,1)} %bitcast.23.w0_ref, bf16[2,4,96,768]{3,2,1,0:T(8,128)(2,1)} %bitcast.24.w1_ref, bf16[2,4,96,768]{3,2,1,0:T(8,128)(2,1)S(1)} %bitcast.125, ...), custom_call_target="tpu_custom_call" | custom-call | flops 120000000 | tf_op jit(solution)/shard_map/pallas_call | solution.py:435
  88.5 7.2 %collective-permute-done.21 = bf16[8,96,768]{2,1,0:T(8,128)(2,1)S(1)} collective-permute-done((bf16[8,96,768]{2,1,0:T(8,128)(2,1)S(1)}, bf16[8,96,768]{2,1,0:T(8,128)(2,1)S(1)}, u32[]{:S(2)}, u32[]{:S(2)}) %collective-permute-start.21) | collective-permute-done | bytes 1179680 | tf_op jit(solution)/shard_map/ppermute | solution.py:479
  95.7 2.8 %collective-permute-done.23 = bf16[8,96,768]{2,1,0:T(8,128)(2,1)S(1)} collective-permute-done((bf16[8,96,768]{2,1,0:T(8,128)(2,1)S(1)}, bf16[8,96,768]{2,1,0:T(8,128)(2,1)S(1)}, u32[]{:S(2)}, u32[]{:S(2)}) %collective-permute-start.23) | collective-permute-done | bytes 1179680 | tf_op jit(solution)/shard_map/ppermute | solution.py:479
  98.6 5.3 %shard_map.258 = (f32[3,8,768]{2,1,0:T(8,128)S(1)}, f32[384,768]{1,0:T(8,128)S(1)}, bf16[384,768]{1,0:T(8,128)(2,1)S(1)}, bf16[384,384]{1,0:T(8,128)(2,1)S(1)}, ...) custom-call(bf16[4,384,768]{2,1,0:T(8,128)(2,1)S(1)} %get-tuple-element.104.z_ref.refs_1_, ...), custom_call_target="tpu_custom_call" | custom-call | flops 165000000 | tf_op jit(solution)/shard_map/pallas_call | solution.py:435
  104.1 2.7 %shard_map.259 = (bf16[4,384,768]{2,1,0:T(8,128)(2,1)S(1)}, f32[4,1,768]{2,1,0:T(1,128)S(1)}) custom-call(bf16[384,768]{1,0:T(8,128)(2,1)S(1)} %get-tuple-element.111.dbb_ref, bf16[4,2,96,768]{3,2,1,0:T(8,128)(2,1)S(1)} %bitcast.117, bf16[4,2,96,768]{3,2,1,0:T(8,128)(2,1)S(1)} %bitcast.119, bf16[4,2,96,768]{3,2,1,0:T(8,128)(2,1)S(1)} %bitcast.121, ...), custom_call_target="tpu_custom_call" | custom-call | flops 105000000 | tf_op jit(solution)/shard_map/pallas_call | solution.py:435
  107.2 1.9 shard_map.260
  109.2 1.8 collective-permute-start.28
  111.0 5.5 %shard_map.261 = (f32[384,768]{1,0:T(8,128)S(1)}, bf16[384,768]{1,0:T(8,128)(2,1)S(1)}, bf16[384,384]{1,0:T(8,128)(2,1)S(1)}, bf16[384,384]{1,0:T(8,128)(2,1)S(1)}, f32[3,768]{1,0:T(4,128)S(1)}) custom-call(bf16[4,384,768]{2,1,0:T(8,128)(2,1)S(1)} %get-tuple-element.118.du_ref.refs_1_, bf16[2,4,96,768]{3,2,1,0:T(8,128)(2,1)} %bitcast.23.w0_ref, ...), custom_call_target="tpu_custom_call" | custom-call | flops 60000002048 | tf_op jit(solution)/shard_map/pallas_call | solution.py:435
  116.5 3.3 %shard_map.262 = (bf16[2,4,96,768]{3,2,1,0:T(8,128)(2,1)S(1)}, bf16[2,4,96,768]{3,2,1,0:T(8,128)(2,1)S(1)}) custom-call(bf16[384,384]{1,0:T(8,128)(2,1)S(1)} %copy-done.10, bf16[4,384,768]{2,1,0:T(8,128)(2,1)S(1)} %get-tuple-element.118.du_ref.refs_1_, bf16[384,384]{1,0:T(8,128)(2,1)S(1)} %collective-permute-done.19.refs_2_, ...), custom_call_target="tpu_custom_call" | custom-call | flops 60000000 | tf_op jit(solution)/shard_map/pallas_call | solution.py:435
  120.2 1.9 shard_map.263
  122.1 3.3 %collective-permute-done.28 = bf16[8,96,768]{2,1,0:T(8,128)(2,1)S(1)} collective-permute-done((bf16[8,96,768]{2,1,0:T(8,128)(2,1)S(1)}, bf16[8,96,768]{2,1,0:T(8,128)(2,1)S(1)}, u32[]{:S(2)}, u32[]{:S(2)}) %collective-permute-start.28) | collective-permute-done | bytes 1179680 | tf_op jit(solution)/shard_map/ppermute | solution.py:497
  125.4 8.7 %shard_map.264 = (bf16[2,384,640]{2,1,0:T(8,128)(2,1)S(1)}, bf16[2,384,640]{2,1,0:T(8,128)(2,1)S(1)}, f32[4,4,768]{2,1,0:T(4,128)S(1)}, f32[4,4,768]{2,1,0:T(4,128)S(1)}) custom-call(bf16[384,768]{1,0:T(8,128)(2,1)S(1)} %get-tuple-element.129.dab_ref, bf16[2,4,104,768]{3,2,1,0:T(8,128)(2,1)S(1)} %bitcast.110, bf16[2,4,104,768]{3,2,1,0:T(8,128)(2,1)S(1)} %bitcast.114, ...), custom_call_target="tpu_custom_call" | custom-call | flops 240000000 | tf_op jit(solution)/shard_map/pallas_call | solution.py:435
  135.4 3.0 %collective-permute-done.29 = bf16[8,96,768]{2,1,0:T(8,128)(2,1)S(1)} collective-permute-done((bf16[8,96,768]{2,1,0:T(8,128)(2,1)S(1)}, bf16[8,96,768]{2,1,0:T(8,128)(2,1)S(1)}, u32[]{:S(2)}, u32[]{:S(2)}) %collective-permute-start.29) | collective-permute-done | bytes 1179680 | tf_op jit(solution)/shard_map/ppermute | solution.py:497
  139.1 1.1 collective-permute-done.32.refs_11_
  140.2 5.3 %shard_map.265 = (bf16[2,4,104,768]{3,2,1,0:T(8,128)(2,1)S(1)}, bf16[2,4,104,768]{3,2,1,0:T(8,128)(2,1)S(1)}) custom-call(bf16[384,384]{1,0:T(8,128)(2,1)S(1)} %copy-done.9, bf16[2,384,640]{2,1,0:T(8,128)(2,1)S(1)} %get-tuple-element.141.refs_1_.low_ref, bf16[2,384,640]{2,1,0:T(8,128)(2,1)S(1)} %get-tuple-element.142.refs_2_.high_ref, ...), custom_call_target="tpu_custom_call" | custom-call | flops 60000000 | tf_op jit(solution)/shard_map/pallas_call | solution.py:435
  145.6 5.7 %collective-permute-done.34 = bf16[4,96,768]{2,1,0:T(8,128)(2,1)S(1)} collective-permute-done((bf16[4,96,768]{2,1,0:T(8,128)(2,1)S(1)}, bf16[4,96,768]{2,1,0:T(8,128)(2,1)S(1)}, u32[]{:S(2)}, u32[]{:S(2)}) %collective-permute-start.34) | collective-permute-done | bytes 589856 | tf_op jit(solution)/shard_map/ppermute | solution.py:497
  151.3 1.7 collective-permute-start.35
  153.0 2.0 fusion
  155.0 2.6 %collective-permute-start.36 = (bf16[1,96,768]{2,1,0:T(8,128)(2,1)S(1)}, bf16[1,96,768]{2,1,0:T(8,128)(2,1)S(1)}, u32[]{:S(2)}, u32[]{:S(2)}) collective-permute-start(bf16[1,96,768]{2,1,0:T(8,128)(2,1)S(1)} %get-tuple-element.194), channel_id=1, source_target_pairs={{0,1},{1,0},{2,3},{3,2},{4,5},{5,4},{6,7},{7,6},{8,9},{9,8},{10,11... | collective-permute-start | bytes 442376 | tf_op jit(solution)/shard_map/ppermute | solution.py:497
  157.6 0.8 collective-permute-start.37
  158.4 1.6 collective-permute-start.38
  160.0 7.3 %shard_map.266 = f32[384,768]{1,0:T(8,128)} custom-call(bf16[2,384,640]{2,1,0:T(8,128)(2,1)S(1)} %get-tuple-element.141.refs_1_.low_ref, bf16[2,384,640]{2,1,0:T(8,128)(2,1)S(1)} %get-tuple-element.142.refs_2_.high_ref, bf16[2,4,104,768]{3,2,1,0:T(8,128)(2,1)S(1)} %bitcast.111, bf16[2,4,104,768]{3,2,1,0:T(8,128)(2,1)S(1)} %bitcast.115, ...), custom_call_target="tpu_custom_call" | custom-call | flops 120000000 | tf_op jit(solution)/shard_map/pallas_call | solution.py:435
  167.3 1.2 collective-permute-done.35
  168.8 2.3 %collective-permute-done.37 = bf16[1,96,768]{2,1,0:T(8,128)(2,1)S(1)} collective-permute-done((bf16[1,96,768]{2,1,0:T(8,128)(2,1)S(1)}, bf16[1,96,768]{2,1,0:T(8,128)(2,1)S(1)}, u32[]{:S(2)}, u32[]{:S(2)}) %collective-permute-start.37) | collective-permute-done | bytes 147488 | tf_op jit(solution)/shard_map/ppermute | solution.py:497
  171.1 1.7 collective-permute-start.39
  172.8 0.8 fusion.17
  173.7 2.4 %collective-permute-start.40 = (bf16[1,96,768]{2,1,0:T(8,128)(2,1)S(1)}, bf16[1,96,768]{2,1,0:T(8,128)(2,1)S(1)}, u32[]{:S(2)}, u32[]{:S(2)}) collective-permute-start(bf16[1,96,768]{2,1,0:T(8,128)(2,1)S(1)} %get-tuple-element.191), channel_id=1, source_target_pairs={{0,1},{1,0},{2,3},{3,2},{4,5},{5,4},{6,7},{7,6},{8,9},{9,8},{10,11... | collective-permute-start | bytes 442376 | tf_op jit(solution)/shard_map/ppermute | solution.py:497
  176.1 0.8 collective-permute-start.41
  176.9 1.6 collective-permute-start.42
  178.5 3.0 %collective-permute-done.39 = bf16[4,104,768]{2,1,0:T(8,128)(2,1)S(1)} collective-permute-done((bf16[4,104,768]{2,1,0:T(8,128)(2,1)S(1)}, bf16[4,104,768]{2,1,0:T(8,128)(2,1)S(1)}, u32[]{:S(2)}, u32[]{:S(2)}) %collective-permute-start.39) | collective-permute-done | bytes 639008 | tf_op jit(solution)/shard_map/ppermute | solution.py:497
  181.6 6.5 %collective-permute-done.41 = bf16[1,96,768]{2,1,0:T(8,128)(2,1)S(1)} collective-permute-done((bf16[1,96,768]{2,1,0:T(8,128)(2,1)S(1)}, bf16[1,96,768]{2,1,0:T(8,128)(2,1)S(1)}, u32[]{:S(2)}, u32[]{:S(2)}) %collective-permute-start.41) | collective-permute-done | bytes 147488 | tf_op jit(solution)/shard_map/ppermute | solution.py:497
  188.1 1.9 collective-permute-start.45
  190.0 3.7 %collective-permute-start.44 = (bf16[1,104,768]{2,1,0:T(8,128)(2,1)S(1)}, bf16[1,104,768]{2,1,0:T(8,128)(2,1)S(1)}, u32[]{:S(2)}, u32[]{:S(2)}) collective-permute-start(bf16[1,104,768]{2,1,0:T(8,128)(2,1)S(1)} %get-tuple-element.148), channel_id=1, source_target_pairs={{0,2},{1,3},{2,0},{3,1},{4,6},{5,7},{6,4},{7,5},{8,10},{9,11},{10,... | collective-permute-start | bytes 479240 | tf_op jit(solution)/shard_map/ppermute | solution.py:497
  193.7 0.8 fusion.21
  194.5 2.4 %collective-permute-done.45 = bf16[1,104,768]{2,1,0:T(8,128)(2,1)S(1)} collective-permute-done((bf16[1,104,768]{2,1,0:T(8,128)(2,1)S(1)}, bf16[1,104,768]{2,1,0:T(8,128)(2,1)S(1)}, u32[]{:S(2)}, u32[]{:S(2)}) %collective-permute-start.45) | collective-permute-done | bytes 159776 | tf_op jit(solution)/shard_map/ppermute | solution.py:497
  196.9 6.4 %collective-permute-done.44 = bf16[1,104,768]{2,1,0:T(8,128)(2,1)S(1)} collective-permute-done((bf16[1,104,768]{2,1,0:T(8,128)(2,1)S(1)}, bf16[1,104,768]{2,1,0:T(8,128)(2,1)S(1)}, u32[]{:S(2)}, u32[]{:S(2)}) %collective-permute-start.44) | collective-permute-done | bytes 159776 | tf_op jit(solution)/shard_map/ppermute | solution.py:497
  (148 shorter events, 16.5 us)
Async XLA Ops:
  0.6 11.8 %copy-start = (f32[3,1,8,768]{3,2,1,0:T(8,128)S(1)}, f32[3,1,8,768]{3,2,1,0:T(8,128)}, u32[]{:S(2)}) copy-start(f32[3,1,8,768]{3,2,1,0:T(8,128)} %param.17) | copy-start | bytes 221188
  2.6 12.4 %collective-permute-start.2 = (bf16[1,104,768]{2,1,0:T(8,128)(2,1)}, bf16[1,104,768]{2,1,0:T(8,128)(2,1)S(1)}, u32[]{:S(2)}, u32[]{:S(2)}) collective-permute-start(bf16[1,104,768]{2,1,0:T(8,128)(2,1)} %bitcast.136), channel_id=1, source_target_pairs={{0,3},{1,2},{2,1},{3,0},{4,7},{5,6},{6,5},{7,4},{8,11},{9,10},{10,... | collective-permute-start | bytes 479240 | tf_op jit(solution)/shard_map/ppermute | solution.py:479
  7.7 13.8 %collective-permute-start.1 = (bf16[1,104,768]{2,1,0:T(8,128)(2,1)}, bf16[1,104,768]{2,1,0:T(8,128)(2,1)}, u32[]{:S(2)}, u32[]{:S(2)}) collective-permute-start(bf16[1,104,768]{2,1,0:T(8,128)(2,1)} %bitcast.137), channel_id=1, source_target_pairs={{0,2},{1,3},{2,0},{3,1},{4,6},{5,7},{6,4},{7,5},{8,10},{9,11},{10,... | collective-permute-start | bytes 479240 | tf_op jit(solution)/shard_map/ppermute | solution.py:479
  7.7 13.8 %collective-permute-start = (bf16[1,104,768]{2,1,0:T(8,128)(2,1)}, bf16[1,104,768]{2,1,0:T(8,128)(2,1)}, u32[]{:S(2)}, u32[]{:S(2)}) collective-permute-start(bf16[1,104,768]{2,1,0:T(8,128)(2,1)} %bitcast.138), channel_id=1, source_target_pairs={{0,1},{1,0},{2,3},{3,2},{4,5},{5,4},{6,7},{7,6},{8,9},{9,8},{10,11... | collective-permute-start | bytes 479240 | tf_op jit(solution)/shard_map/ppermute | solution.py:479
  8.2 14.4 %collective-permute-start.3 = (bf16[1,96,768]{2,1,0:T(8,128)(2,1)}, bf16[1,96,768]{2,1,0:T(8,128)(2,1)}, u32[]{:S(2)}, u32[]{:S(2)}) collective-permute-start(bf16[1,96,768]{2,1,0:T(8,128)(2,1)} %bitcast.147), channel_id=1, source_target_pairs={{0,16},{1,17},{2,18},{3,19},{4,12},{5,13},{6,14},{7,15},{8,24},{9,... | collective-permute-start | bytes 442376 | tf_op jit(solution)/shard_map/ppermute | solution.py:479
  12.5 9.0 %copy-start.15 = (bf16[104,768]{1,0:T(8,128)(2,1)S(1)}, bf16[104,768]{1,0:T(8,128)(2,1)}, u32[]{:S(2)}) copy-start(bf16[104,768]{1,0:T(8,128)(2,1)} %shard_map.255) | copy-start | bytes 479236
  15.0 15.5 %copy-start.8 = (bf16[384,384]{1,0:T(8,128)(2,1)}, bf16[384,384]{1,0:T(8,128)(2,1)S(1)}, u32[]{:S(2)}) copy-start(bf16[384,384]{1,0:T(8,128)(2,1)S(1)} %get-tuple-element.136.refs_0_) | copy-start | bytes 884740
  15.0 9.2 %copy-start.16 = (bf16[96,768]{1,0:T(8,128)(2,1)S(1)}, bf16[96,768]{1,0:T(8,128)(2,1)}, u32[]{:S(2)}) copy-start(bf16[96,768]{1,0:T(8,128)(2,1)} %param.24) | copy-start | bytes 442372
  22.6 10.5 %collective-permute-start.4 = (bf16[4,104,768]{2,1,0:T(8,128)(2,1)S(1)}, bf16[4,104,768]{2,1,0:T(8,128)(2,1)S(1)}, u32[]{:S(2)}, u32[]{:S(2)}) collective-permute-start(bf16[4,104,768]{2,1,0:T(8,128)(2,1)S(1)} %pad_maximum_fusion), channel_id=1, source_target_pairs={{0,16},{1,17},{2,18},{3,19},{4,12},{5,13},{6,14},{7,15},{8,24},{9,... | collective-permute-start | bytes 1916936 | tf_op jit(solution)/shard_map/ppermute | solution.py:479
  24.2 8.9 %collective-permute-start.5 = (bf16[1,96,768]{2,1,0:T(8,128)(2,1)S(1)}, bf16[1,96,768]{2,1,0:T(8,128)(2,1)S(1)}, u32[]{:S(2)}, u32[]{:S(2)}) collective-permute-start(bf16[1,96,768]{2,1,0:T(8,128)(2,1)S(1)} %bitcast.143), channel_id=1, source_target_pairs={{0,1},{1,0},{2,3},{3,2},{4,5},{5,4},{6,7},{7,6},{8,9},{9,8},{10,11... | collective-permute-start | bytes 442376 | tf_op jit(solution)/shard_map/ppermute | solution.py:479
  24.3 13.3 %collective-permute-start.6 = (bf16[1,96,768]{2,1,0:T(8,128)(2,1)S(1)}, bf16[1,96,768]{2,1,0:T(8,128)(2,1)S(1)}, u32[]{:S(2)}, u32[]{:S(2)}) collective-permute-start(bf16[1,96,768]{2,1,0:T(8,128)(2,1)S(1)} %bitcast.144), channel_id=1, source_target_pairs={{0,2},{1,3},{2,0},{3,1},{4,6},{5,7},{6,4},{7,5},{8,10},{9,11},{10,... | collective-permute-start | bytes 442376 | tf_op jit(solution)/shard_map/ppermute | solution.py:479
  27.3 10.3 %collective-permute-start.7 = (bf16[1,96,768]{2,1,0:T(8,128)(2,1)S(1)}, bf16[1,96,768]{2,1,0:T(8,128)(2,1)S(1)}, u32[]{:S(2)}, u32[]{:S(2)}) collective-permute-start(bf16[1,96,768]{2,1,0:T(8,128)(2,1)S(1)} %bitcast.145), channel_id=1, source_target_pairs={{0,3},{1,2},{2,1},{3,0},{4,7},{5,6},{6,5},{7,4},{8,11},{9,10},{10,... | collective-permute-start | bytes 442376 | tf_op jit(solution)/shard_map/ppermute | solution.py:479
  30.6 10.0 %copy-start.17 = (bf16[768,96]{0,1:T(8,128)(2,1)S(1)}, bf16[768,96]{0,1:T(8,128)(2,1)}, u32[]{:S(2)}) copy-start(bf16[768,96]{0,1:T(8,128)(2,1)} %param.26) | copy-start | bytes 442372
  37.6 21.2 %collective-permute-start.9 = (bf16[8,104,768]{2,1,0:T(8,128)(2,1)S(1)}, bf16[8,104,768]{2,1,0:T(8,128)(2,1)S(1)}, u32[]{:S(2)}, u32[]{:S(2)}) collective-permute-start(bf16[8,104,768]{2,1,0:T(8,128)(2,1)S(1)} %constant_dynamic-update-slice_fusion), channel_id=1, source_target_pairs={{0,8},{1,9},{2,10},{3,11},{4,20},{5,21},{6,22},{7,23},{8,0},{9,1},... | collective-permute-start | bytes 3833864 | tf_op jit(solution)/shard_map/ppermute | solution.py:479
  38.4 20.4 %collective-permute-start.10 = (bf16[4,96,768]{2,1,0:T(8,128)(2,1)S(1)}, bf16[4,96,768]{2,1,0:T(8,128)(2,1)S(1)}, u32[]{:S(2)}, u32[]{:S(2)}) collective-permute-start(bf16[4,96,768]{2,1,0:T(8,128)(2,1)S(1)} %pad_maximum_fusion.1), channel_id=1, source_target_pairs={{0,16},{1,17},{2,18},{3,19},{4,12},{5,13},{6,14},{7,15},{8,24},{9,... | collective-permute-start | bytes 1769480 | tf_op jit(solution)/shard_map/ppermute | solution.py:479
  42.2 22.1 %copy-start.23 = (s32[3,1,128]{2,1,0:T(1,128)S(1)}, s32[3,1,128]{2,1,0:T(1,128)}, u32[]{:S(2)}) copy-start(s32[3,1,128]{2,1,0:T(1,128)} %param.16) | copy-start | bytes 4612
  42.2 13.8 %collective-permute-start.11 = (bf16[2,96,768]{2,1,0:T(8,128)(2,1)}, bf16[2,96,768]{2,1,0:T(8,128)(2,1)S(1)}, u32[]{:S(2)}, u32[]{:S(2)}) collective-permute-start(bf16[2,96,768]{2,1,0:T(8,128)(2,1)} %pad_maximum_fusion.2), channel_id=1, source_target_pairs={{0,1},{1,0},{2,3},{3,2},{4,5},{5,4},{6,7},{7,6},{8,9},{9,8},{10,11... | collective-permute-start | bytes 884744 | tf_op jit(solution)/shard_map/ppermute | solution.py:479
  44.5 14.3 %collective-permute-start.12 = (bf16[2,96,768]{2,1,0:T(8,128)(2,1)}, bf16[2,96,768]{2,1,0:T(8,128)(2,1)S(1)}, u32[]{:S(2)}, u32[]{:S(2)}) collective-permute-start(bf16[2,96,768]{2,1,0:T(8,128)(2,1)} %pad_maximum_fusion.2), channel_id=1, source_target_pairs={{0,2},{1,3},{2,0},{3,1},{4,6},{5,7},{6,4},{7,5},{8,10},{9,11},{10,... | collective-permute-start | bytes 884744 | tf_op jit(solution)/shard_map/ppermute | solution.py:479
  58.9 5.6 %collective-permute-start.13 = (bf16[8,104,768]{2,1,0:T(8,128)(2,1)S(1)}, bf16[8,104,768]{2,1,0:T(8,128)(2,1)}, u32[]{:S(2)}, u32[]{:S(2)}) collective-permute-start(bf16[8,104,768]{2,1,0:T(8,128)(2,1)S(1)} %constant_dynamic-update-slice_fusion), channel_id=1, source_target_pairs={{0,4},{1,5},{2,6},{3,7},{4,0},{5,1},{6,2},{7,3},{8,12},{9,13},{10,... | collective-permute-start | bytes 3833864 | tf_op jit(solution)/shard_map/ppermute | solution.py:479
  59.5 5.0 %collective-permute-start.14 = (bf16[8,104,768]{2,1,0:T(8,128)(2,1)S(1)}, bf16[8,104,768]{2,1,0:T(8,128)(2,1)}, u32[]{:S(2)}, u32[]{:S(2)}) collective-permute-start(bf16[8,104,768]{2,1,0:T(8,128)(2,1)S(1)} %collective-permute-done.9), channel_id=1, source_target_pairs={{0,4},{1,5},{2,6},{3,7},{4,0},{5,1},{6,2},{7,3},{8,12},{9,13},{10,... | collective-permute-start | bytes 3833864 | tf_op jit(solution)/shard_map/ppermute | solution.py:479
  60.4 16.5 %collective-permute-start.15 = (bf16[8,96,768]{2,1,0:T(8,128)(2,1)}, bf16[8,96,768]{2,1,0:T(8,128)(2,1)}, u32[]{:S(2)}, u32[]{:S(2)}) collective-permute-start(bf16[8,96,768]{2,1,0:T(8,128)(2,1)} %constant_dynamic-update-slice_fusion.5), channel_id=1, source_target_pairs={{0,8},{1,9},{2,10},{3,11},{4,20},{5,21},{6,22},{7,23},{8,0},{9,1},... | collective-permute-start | bytes 3538952 | tf_op jit(solution)/shard_map/ppermute | solution.py:479
  62.1 2.4 %collective-permute-start.8 = (bf16[384,384]{1,0:T(8,128)(2,1)}, bf16[384,384]{1,0:T(8,128)(2,1)}, u32[]{:S(2)}, u32[]{:S(2)}) collective-permute-start(bf16[384,384]{1,0:T(8,128)(2,1)} %get-tuple-element.87), channel_id=1, source_target_pairs={{0,4},{1,5},{2,6},{3,7},{4,0},{5,1},{6,2},{7,3},{8,12},{9,13},{10,... | collective-permute-start | bytes 884744 | tf_op jit(solution)/shard_map/ppermute | solution.py:470
  62.1 14.8 %collective-permute-start.16 = (bf16[2,96,768]{2,1,0:T(8,128)(2,1)}, bf16[2,96,768]{2,1,0:T(8,128)(2,1)}, u32[]{:S(2)}, u32[]{:S(2)}) collective-permute-start(bf16[2,96,768]{2,1,0:T(8,128)(2,1)} %pad_maximum_fusion.2), channel_id=1, source_target_pairs={{0,3},{1,2},{2,1},{3,0},{4,7},{5,6},{6,5},{7,4},{8,11},{9,10},{10,... | collective-permute-start | bytes 884744 | tf_op jit(solution)/shard_map/ppermute | solution.py:479
  64.5 12.9 %copy-start.18 = (bf16[768,96]{0,1:T(8,128)(2,1)S(1)}, bf16[768,96]{0,1:T(8,128)(2,1)}, u32[]{:S(2)}) copy-start(bf16[768,96]{0,1:T(8,128)(2,1)} %param.26) | copy-start | bytes 442372
  64.5 13.9 %copy-start.20 = (bf16[2,96,768]{2,1,0:T(8,128)(2,1)S(1)}, bf16[2,96,768]{2,1,0:T(8,128)(2,1)}, u32[]{:S(2)}) copy-start(bf16[2,96,768]{2,1,0:T(8,128)(2,1)} %copy-done.19) | copy-start | bytes 884740
  76.9 6.1 %collective-permute-start.17 = (bf16[8,96,768]{2,1,0:T(8,128)(2,1)}, bf16[8,96,768]{2,1,0:T(8,128)(2,1)S(1)}, u32[]{:S(2)}, u32[]{:S(2)}) collective-permute-start(bf16[8,96,768]{2,1,0:T(8,128)(2,1)} %constant_dynamic-update-slice_fusion.5), channel_id=1, source_target_pairs={{0,4},{1,5},{2,6},{3,7},{4,0},{5,1},{6,2},{7,3},{8,12},{9,13},{10,... | collective-permute-start | bytes 3538952 | tf_op jit(solution)/shard_map/ppermute | solution.py:479
  76.9 6.1 %collective-permute-start.18 = (bf16[8,96,768]{2,1,0:T(8,128)(2,1)}, bf16[8,96,768]{2,1,0:T(8,128)(2,1)S(1)}, u32[]{:S(2)}, u32[]{:S(2)}) collective-permute-start(bf16[8,96,768]{2,1,0:T(8,128)(2,1)} %collective-permute-done.15), channel_id=1, source_target_pairs={{0,4},{1,5},{2,6},{3,7},{4,0},{5,1},{6,2},{7,3},{8,12},{9,13},{10,... | collective-permute-start | bytes 3538952 | tf_op jit(solution)/shard_map/ppermute | solution.py:479
  77.4 3.9 %copy-start.24 = (bf16[384,384]{1,0:T(8,128)(2,1)S(1)}, bf16[384,384]{1,0:T(8,128)(2,1)}, u32[]{:S(2)}) copy-start(bf16[384,384]{1,0:T(8,128)(2,1)} %get-tuple-element.101) | copy-start | bytes 884740
  77.4 5.6 %collective-permute-start.20 = (bf16[4,384,256]{2,1,0:T(8,128)(2,1)}, bf16[4,384,256]{2,1,0:T(8,128)(2,1)S(1)}, u32[]{:S(2)}, u32[]{:S(2)}) collective-permute-start(bf16[4,384,256]{2,1,0:T(8,128)(2,1)} %get-tuple-element.102.refs_7_), channel_id=1, source_target_pairs={{0,4},{1,5},{2,6},{3,7},{4,0},{5,1},{6,2},{7,3},{8,12},{9,13},{10,... | collective-permute-start | bytes 2359304 | tf_op jit(solution)/shard_map/ppermute | solution.py:470
  79.5 16.3 %collective-permute-start.21 = (bf16[8,96,768]{2,1,0:T(8,128)(2,1)S(1)}, bf16[8,96,768]{2,1,0:T(8,128)(2,1)S(1)}, u32[]{:S(2)}, u32[]{:S(2)}) collective-permute-start(bf16[8,96,768]{2,1,0:T(8,128)(2,1)S(1)} %constant_dynamic-update-slice_fusion.10), channel_id=1, source_target_pairs={{0,8},{1,9},{2,10},{3,11},{4,20},{5,21},{6,22},{7,23},{8,0},{9,1},... | collective-permute-start | bytes 3538952 | tf_op jit(solution)/shard_map/ppermute | solution.py:479
  81.3 1.7 collective-permute-start.19
  87.9 19.3 %collective-permute-start.25 = (bf16[4,384,768]{2,1,0:T(8,128)(2,1)S(1)}, bf16[4,384,768]{2,1,0:T(8,128)(2,1)S(1)}, u32[]{:S(2)}, u32[]{:S(2)}) collective-permute-start(bf16[4,384,768]{2,1,0:T(8,128)(2,1)S(1)} %get-tuple-element.104.z_ref.refs_1_), channel_id=1, source_target_pairs={{0,4},{1,5},{2,6},{3,7},{4,0},{5,1},{6,2},{7,3},{8,12},{9,13},{10,... | collective-permute-start | bytes 7077896 | tf_op jit(solution)/shard_map/ppermute | solution.py:470
  88.1 7.6 %collective-permute-start.22 = (bf16[8,96,768]{2,1,0:T(8,128)(2,1)S(1)}, bf16[8,96,768]{2,1,0:T(8,128)(2,1)S(1)}, u32[]{:S(2)}, u32[]{:S(2)}) collective-permute-start(bf16[8,96,768]{2,1,0:T(8,128)(2,1)S(1)} %constant_dynamic-update-slice_fusion.10), channel_id=1, source_target_pairs={{0,4},{1,5},{2,6},{3,7},{4,0},{5,1},{6,2},{7,3},{8,12},{9,13},{10,... | collective-permute-start | bytes 3538952 | tf_op jit(solution)/shard_map/ppermute | solution.py:479
  95.7 2.8 %collective-permute-start.23 = (bf16[8,96,768]{2,1,0:T(8,128)(2,1)S(1)}, bf16[8,96,768]{2,1,0:T(8,128)(2,1)S(1)}, u32[]{:S(2)}, u32[]{:S(2)}) collective-permute-start(bf16[8,96,768]{2,1,0:T(8,128)(2,1)S(1)} %collective-permute-done.21), channel_id=1, source_target_pairs={{0,4},{1,5},{2,6},{3,7},{4,0},{5,1},{6,2},{7,3},{8,12},{9,13},{10,... | collective-permute-start | bytes 3538952 | tf_op jit(solution)/shard_map/ppermute | solution.py:479
  103.9 3.3 %collective-permute-start.24 = (bf16[384,384]{1,0:T(8,128)(2,1)S(1)}, bf16[384,384]{1,0:T(8,128)(2,1)S(1)}, u32[]{:S(2)}, u32[]{:S(2)}) collective-permute-start(bf16[384,384]{1,0:T(8,128)(2,1)S(1)} %get-tuple-element.117), channel_id=1, source_target_pairs={{0,4},{1,5},{2,6},{3,7},{4,0},{5,1},{6,2},{7,3},{8,12},{9,13},{10,... | collective-permute-start | bytes 884744 | tf_op jit(solution)/shard_map/ppermute | solution.py:470
  106.7 4.2 %copy-start.11 = (f32[384,768]{1,0:T(8,128)S(1)}, f32[384,768]{1,0:T(8,128)}, u32[]{:S(2)}) copy-start(f32[384,768]{1,0:T(8,128)} %get-tuple-element.120.x1_ref) | copy-start | bytes 3538948
  106.7 4.2 %copy-start.12 = (f32[384,1]{1,0:T(8,128)S(1)}, f32[384,1]{1,0:T(8,128)}, u32[]{:S(2)}) copy-start(f32[384,1]{1,0:T(8,128)} %get-tuple-element.121.r1_ref) | copy-start | bytes 4612
  106.8 9.7 %collective-permute-start.26 = (bf16[4,384,768]{2,1,0:T(8,128)(2,1)S(1)}, bf16[4,384,768]{2,1,0:T(8,128)(2,1)S(1)}, u32[]{:S(2)}, u32[]{:S(2)}) collective-permute-start(bf16[4,384,768]{2,1,0:T(8,128)(2,1)S(1)} %get-tuple-element.118.du_ref.refs_1_), channel_id=1, source_target_pairs={{0,4},{1,5},{2,6},{3,7},{4,0},{5,1},{6,2},{7,3},{8,12},{9,13},{10,... | collective-permute-start | bytes 7077896 | tf_op jit(solution)/shard_map/ppermute | solution.py:470
  109.2 16.3 %collective-permute-start.28 = (bf16[8,96,768]{2,1,0:T(8,128)(2,1)S(1)}, bf16[8,96,768]{2,1,0:T(8,128)(2,1)S(1)}, u32[]{:S(2)}, u32[]{:S(2)}) collective-permute-start(bf16[8,96,768]{2,1,0:T(8,128)(2,1)S(1)} %bitcast.124), channel_id=1, source_target_pairs={{0,8},{1,9},{2,10},{3,11},{4,20},{5,21},{6,22},{7,23},{8,0},{9,1},... | collective-permute-start | bytes 3538952 | tf_op jit(solution)/shard_map/ppermute | solution.py:497
  111.0 5.5 %copy-start.10 = (bf16[384,384]{1,0:T(8,128)(2,1)S(1)}, bf16[384,384]{1,0:T(8,128)(2,1)}, u32[]{:S(2)}) copy-start(bf16[384,384]{1,0:T(8,128)(2,1)} %get-tuple-element.125.refs_0_) | copy-start | bytes 884740
  119.8 18.5 %collective-permute-start.29 = (bf16[8,96,768]{2,1,0:T(8,128)(2,1)S(1)}, bf16[8,96,768]{2,1,0:T(8,128)(2,1)S(1)}, u32[]{:S(2)}, u32[]{:S(2)}) collective-permute-start(bf16[8,96,768]{2,1,0:T(8,128)(2,1)S(1)} %bitcast.133), channel_id=1, source_target_pairs={{0,8},{1,9},{2,10},{3,11},{4,20},{5,21},{6,22},{7,23},{8,0},{9,1},... | collective-permute-start | bytes 3538952 | tf_op jit(solution)/shard_map/ppermute | solution.py:497
  120.1 1.9 collective-permute-start.27
  120.2 5.3 %copy-start.4 = (f32[4,3,128,384]{3,2,1,0:T(8,128)S(1)}, f32[4,3,128,384]{3,2,1,0:T(8,128)}, u32[]{:S(2)}) copy-start(f32[4,3,128,384]{3,2,1,0:T(8,128)} %get-tuple-element.131.p_ref) | copy-start | bytes 7077892
  120.2 5.3 %copy-start.5 = (bf16[4,384,576]{2,1,0:T(8,128)(2,1)S(1)}, bf16[4,384,576]{2,1,0:T(8,128)(2,1)}, u32[]{:S(2)}) copy-start(bf16[4,384,576]{2,1,0:T(8,128)(2,1)} %get-tuple-element.130.qkv_ref) | copy-start | bytes 5308420
  134.1 6.1 %collective-permute-start.30 = (bf16[2,384,640]{2,1,0:T(8,128)(2,1)S(1)}, bf16[2,384,640]{2,1,0:T(8,128)(2,1)S(1)}, u32[]{:S(2)}, u32[]{:S(2)}) collective-permute-start(bf16[2,384,640]{2,1,0:T(8,128)(2,1)S(1)} %get-tuple-element.141.refs_1_.low_ref), channel_id=1, source_target_pairs={{0,4},{1,5},{2,6},{3,7},{4,0},{5,1},{6,2},{7,3},{8,12},{9,13},{10,... | collective-permute-start | bytes 2949128 | tf_op jit(solution)/shard_map/ppermute | solution.py:470
  134.2 6.0 %collective-permute-start.31 = (bf16[2,384,640]{2,1,0:T(8,128)(2,1)S(1)}, bf16[2,384,640]{2,1,0:T(8,128)(2,1)S(1)}, u32[]{:S(2)}, u32[]{:S(2)}) collective-permute-start(bf16[2,384,640]{2,1,0:T(8,128)(2,1)S(1)} %get-tuple-element.142.refs_2_.high_ref), channel_id=1, source_target_pairs={{0,4},{1,5},{2,6},{3,7},{4,0},{5,1},{6,2},{7,3},{8,12},{9,13},{10,... | collective-permute-start | bytes 2949128 | tf_op jit(solution)/shard_map/ppermute | solution.py:470
  135.0 5.2 %copy-start.6 = (bf16[4,384,256]{2,1,0:T(8,128)(2,1)S(1)}, bf16[4,384,256]{2,1,0:T(8,128)(2,1)}, u32[]{:S(2)}) copy-start(bf16[4,384,256]{2,1,0:T(8,128)(2,1)} %get-tuple-element.102.refs_7_) | copy-start | bytes 2359300
  135.0 5.2 %copy-start.9 = (bf16[384,384]{1,0:T(8,128)(2,1)S(1)}, bf16[384,384]{1,0:T(8,128)(2,1)}, u32[]{:S(2)}) copy-start(bf16[384,384]{1,0:T(8,128)(2,1)} %copy-done.8) | copy-start | bytes 884740
  135.0 10.6 %collective-permute-start.33 = (bf16[4,96,768]{2,1,0:T(8,128)(2,1)S(1)}, bf16[4,96,768]{2,1,0:T(8,128)(2,1)S(1)}, u32[]{:S(2)}, u32[]{:S(2)}) collective-permute-start(bf16[4,96,768]{2,1,0:T(8,128)(2,1)S(1)} %get-tuple-element.185), channel_id=1, source_target_pairs={{0,16},{1,17},{2,18},{3,19},{4,12},{5,13},{6,14},{7,15},{8,24},{9,... | collective-permute-start | bytes 1769480 | tf_op jit(solution)/shard_map/ppermute | solution.py:497
  138.6 12.7 %collective-permute-start.34 = (bf16[4,96,768]{2,1,0:T(8,128)(2,1)S(1)}, bf16[4,96,768]{2,1,0:T(8,128)(2,1)S(1)}, u32[]{:S(2)}, u32[]{:S(2)}) collective-permute-start(bf16[4,96,768]{2,1,0:T(8,128)(2,1)S(1)} %get-tuple-element.183), channel_id=1, source_target_pairs={{0,16},{1,17},{2,18},{3,19},{4,12},{5,13},{6,14},{7,15},{8,24},{9,... | collective-permute-start | bytes 1769480 | tf_op jit(solution)/shard_map/ppermute | solution.py:497
  139.0 1.2 collective-permute-start.32
  140.2 12.8 %copy-start.14 = (pred[768,768]{1,0:T(32,128)(4,1)S(1)}, pred[768,768]{1,0:T(32,128)(4,1)}, u32[]{:S(2)}) copy-start(pred[768,768]{1,0:T(32,128)(4,1)} %copy-done.13) | copy-start | bytes 1769476
  151.3 17.3 %collective-permute-start.35 = (bf16[8,104,768]{2,1,0:T(8,128)(2,1)S(1)}, bf16[8,104,768]{2,1,0:T(8,128)(2,1)S(1)}, u32[]{:S(2)}, u32[]{:S(2)}) collective-permute-start(bf16[8,104,768]{2,1,0:T(8,128)(2,1)S(1)} %bitcast.132), channel_id=1, source_target_pairs={{0,8},{1,9},{2,10},{3,11},{4,20},{5,21},{6,22},{7,23},{8,0},{9,1},... | collective-permute-start | bytes 3833864 | tf_op jit(solution)/shard_map/ppermute | solution.py:497
  154.9 5.1 %copy-start.3 = (bf16[768,768]{1,0:T(8,128)(2,1)S(1)}, bf16[768,768]{1,0:T(8,128)(2,1)}, u32[]{:S(2)}) copy-start(bf16[768,768]{1,0:T(8,128)(2,1)} %copy-done.2) | copy-start | bytes 3538948
  155.0 13.8 %collective-permute-start.36 = (bf16[1,96,768]{2,1,0:T(8,128)(2,1)S(1)}, bf16[1,96,768]{2,1,0:T(8,128)(2,1)S(1)}, u32[]{:S(2)}, u32[]{:S(2)}) collective-permute-start(bf16[1,96,768]{2,1,0:T(8,128)(2,1)S(1)} %get-tuple-element.194), channel_id=1, source_target_pairs={{0,1},{1,0},{2,3},{3,2},{4,5},{5,4},{6,7},{7,6},{8,9},{9,8},{10,11... | collective-permute-start | bytes 442376 | tf_op jit(solution)/shard_map/ppermute | solution.py:497
  157.6 13.5 %collective-permute-start.37 = (bf16[1,96,768]{2,1,0:T(8,128)(2,1)S(1)}, bf16[1,96,768]{2,1,0:T(8,128)(2,1)S(1)}, u32[]{:S(2)}, u32[]{:S(2)}) collective-permute-start(bf16[1,96,768]{2,1,0:T(8,128)(2,1)S(1)} %get-tuple-element.193), channel_id=1, source_target_pairs={{0,2},{1,3},{2,0},{3,1},{4,6},{5,7},{6,4},{7,5},{8,10},{9,11},{10,... | collective-permute-start | bytes 442376 | tf_op jit(solution)/shard_map/ppermute | solution.py:497
  158.4 12.7 %collective-permute-start.38 = (bf16[1,96,768]{2,1,0:T(8,128)(2,1)S(1)}, bf16[1,96,768]{2,1,0:T(8,128)(2,1)S(1)}, u32[]{:S(2)}, u32[]{:S(2)}) collective-permute-start(bf16[1,96,768]{2,1,0:T(8,128)(2,1)S(1)} %get-tuple-element.192), channel_id=1, source_target_pairs={{0,3},{1,2},{2,1},{3,0},{4,7},{5,6},{6,5},{7,4},{8,11},{9,10},{10,... | collective-permute-start | bytes 442376 | tf_op jit(solution)/shard_map/ppermute | solution.py:497
  171.1 10.4 %collective-permute-start.39 = (bf16[4,104,768]{2,1,0:T(8,128)(2,1)S(1)}, bf16[4,104,768]{2,1,0:T(8,128)(2,1)S(1)}, u32[]{:S(2)}, u32[]{:S(2)}) collective-permute-start(bf16[4,104,768]{2,1,0:T(8,128)(2,1)S(1)} %get-tuple-element.146), channel_id=1, source_target_pairs={{0,16},{1,17},{2,18},{3,19},{4,12},{5,13},{6,14},{7,15},{8,24},{9,... | collective-permute-start | bytes 1916936 | tf_op jit(solution)/shard_map/ppermute | solution.py:497
  173.7 8.0 %collective-permute-start.40 = (bf16[1,96,768]{2,1,0:T(8,128)(2,1)S(1)}, bf16[1,96,768]{2,1,0:T(8,128)(2,1)S(1)}, u32[]{:S(2)}, u32[]{:S(2)}) collective-permute-start(bf16[1,96,768]{2,1,0:T(8,128)(2,1)S(1)} %get-tuple-element.191), channel_id=1, source_target_pairs={{0,1},{1,0},{2,3},{3,2},{4,5},{5,4},{6,7},{7,6},{8,9},{9,8},{10,11... | collective-permute-start | bytes 442376 | tf_op jit(solution)/shard_map/ppermute | solution.py:497
  176.1 12.0 %collective-permute-start.41 = (bf16[1,96,768]{2,1,0:T(8,128)(2,1)S(1)}, bf16[1,96,768]{2,1,0:T(8,128)(2,1)S(1)}, u32[]{:S(2)}, u32[]{:S(2)}) collective-permute-start(bf16[1,96,768]{2,1,0:T(8,128)(2,1)S(1)} %get-tuple-element.190), channel_id=1, source_target_pairs={{0,2},{1,3},{2,0},{3,1},{4,6},{5,7},{6,4},{7,5},{8,10},{9,11},{10,... | collective-permute-start | bytes 442376 | tf_op jit(solution)/shard_map/ppermute | solution.py:497
  176.9 11.2 %collective-permute-start.42 = (bf16[1,96,768]{2,1,0:T(8,128)(2,1)S(1)}, bf16[1,96,768]{2,1,0:T(8,128)(2,1)S(1)}, u32[]{:S(2)}, u32[]{:S(2)}) collective-permute-start(bf16[1,96,768]{2,1,0:T(8,128)(2,1)S(1)} %get-tuple-element.189), channel_id=1, source_target_pairs={{0,3},{1,2},{2,1},{3,0},{4,7},{5,6},{6,5},{7,4},{8,11},{9,10},{10,... | collective-permute-start | bytes 442376 | tf_op jit(solution)/shard_map/ppermute | solution.py:497
  188.1 8.8 %collective-permute-start.45 = (bf16[1,104,768]{2,1,0:T(8,128)(2,1)S(1)}, bf16[1,104,768]{2,1,0:T(8,128)(2,1)S(1)}, u32[]{:S(2)}, u32[]{:S(2)}) collective-permute-start(bf16[1,104,768]{2,1,0:T(8,128)(2,1)S(1)} %get-tuple-element.149), channel_id=1, source_target_pairs={{0,3},{1,2},{2,1},{3,0},{4,7},{5,6},{6,5},{7,4},{8,11},{9,10},{10,... | collective-permute-start | bytes 479240 | tf_op jit(solution)/shard_map/ppermute | solution.py:497
  190.0 13.4 %collective-permute-start.44 = (bf16[1,104,768]{2,1,0:T(8,128)(2,1)S(1)}, bf16[1,104,768]{2,1,0:T(8,128)(2,1)S(1)}, u32[]{:S(2)}, u32[]{:S(2)}) collective-permute-start(bf16[1,104,768]{2,1,0:T(8,128)(2,1)S(1)} %get-tuple-element.148), channel_id=1, source_target_pairs={{0,2},{1,3},{2,0},{3,1},{4,6},{5,7},{6,4},{7,5},{8,10},{9,11},{10,... | collective-permute-start | bytes 479240 | tf_op jit(solution)/shard_map/ppermute | solution.py:497
  193.7 9.6 %collective-permute-start.43 = (bf16[1,104,768]{2,1,0:T(8,128)(2,1)S(1)}, bf16[1,104,768]{2,1,0:T(8,128)(2,1)S(1)}, u32[]{:S(2)}, u32[]{:S(2)}) collective-permute-start(bf16[1,104,768]{2,1,0:T(8,128)(2,1)S(1)} %get-tuple-element.147), channel_id=1, source_target_pairs={{0,1},{1,0},{2,3},{3,2},{4,5},{5,4},{6,7},{7,6},{8,9},{9,8},{10,11... | collective-permute-start | bytes 479240 | tf_op jit(solution)/shard_map/ppermute | solution.py:497
  (7 other events, 16.2 us)

commit v7 on v6

--- a/solution.py
+++ b/solution.py
@@ -19,6 +19,7 @@
 VMEM_LIMIT = 24 * 1024 * 1024
 COST = 30_000_000
 NORM = 2000
+CUT = 4
 SMALL = pltpu.CompilerParams(vmem_limit_bytes=8 * 1024 * 1024)
 
 
@@ -493,16 +494,24 @@
     def __init__(self, keep, send, tables):
         self.keep, self.send, self.tables = keep, [send], tables
 
-    def stage(self, name, parts, *done):
-        got = [lax.ppermute(after(s, *done), AXES, t) for s, t in zip(self.send, self.tables[name], strict=True)]
-        size = self.keep.shape[0] // parts
-
-        def share(j):
-            cut = slice(j * size, (j + 1) * size)
-            return sum((g[cut].astype(f32) for g in got), self.keep[cut].astype(f32))
-
-        self.send = [share(j).astype(bf16) for j in range(1, parts)]
-        self.keep = share(0)
+    def stage(self, name, parts, *done, cut=1):
+        tables = self.tables[name]
+        pieces = len(self.send) // len(tables)
+        got = [lax.ppermute(after(s, *done), AXES, tables[n // pieces]) for n, s in enumerate(self.send)]
+        size = self.keep.shape[0] // parts // cut
+
+        def piece(n):
+            at = n * size
+            total = self.keep[at : at + size].astype(f32)
+            for t in range(len(tables)):
+                mine = got[t * pieces : (t + 1) * pieces]
+                wide = mine[0].shape[0]
+                total = total + mine[at // wide][at % wide : at % wide + size].astype(f32)
+            return total
+
+        self.send = [piece(n).astype(bf16) for n in range(cut, parts * cut)]
+        kept = [piece(n) for n in range(cut)]
+        self.keep = kept[0] if cut == 1 else jnp.concatenate(kept)
         return got
 
 
@@ -711,19 +720,20 @@
         )
         s_qo = Scatter(flat(qo_keep), flat(qo_send), tables)
         got_u2 = s_up.stage("2", n_t)
-        got_q3 = s_qo.stage("3", 2, *got_d2, *got_u2)
-        got_z = s_down.stage("Z", 1)
-        dq = [after(d, pooled, qo_keep) for d in dq]
+        s_qo.stage("3", 2, *got_d2, *got_u2, pooled, cut=CUT)
+        both = Scatter(jnp.concatenate([s_down.keep, s_up.keep]), None, tables)
+        both.send = [jnp.concatenate([a, b]) for a, b in zip(s_down.send, s_up.send, strict=True)]
+        got_z = both.stage("Z", 1)
+        dq = [after(d, qo_keep) for d in dq]
     dx = call(
         input_backward, n_t, 4, halved(*dq) + weights(*w_qo) + wholes(da, perm), wholes(sds((T, D), f32)),
         [pltpu.VMEM((T, D), f32)],
     )[0]
 
     if pairwise:
-        got = s_up.stage("Z", 1)
-        s_qo.stage("2", n_t, dx, *got_z)
-        s_qo.stage("Z", 1, *got)
-        g_down, g_up, g_qo = s_down.keep[0], s_up.keep[0], s_qo.keep[0]
+        s_qo.stage("2", n_t, dx)
+        s_qo.stage("Z", 1, *got_z)
+        g_down, g_up, g_qo = both.keep[0], both.keep[1], s_qo.keep[0]
         g_v = g_qo[BLK, :n_vec]
         g_qo = g_qo[:BLK]
     else:

time: 207 us -> 202 us (0.976)
  waiting for transfers between devices: 72.4 us -> 67.7 us
    ppermute x15, waiting for transfers between devices: 33.8 us -> 30.1 us  [stage(): lax.ppermute(after(s, *done), AXES, tables[n // pieces])]
  transfers between devices with their start and end apart: 46 -> 46, of which waited for: 20 -> 16; matrix products, arithmetic and copies ran while one was open for 9% -> 9% of each run, Pallas kernels for 29% -> 30%
where the time goes in v7:
time: 202 us
  waiting for transfers between devices  67.7 us (34%)
  Pallas kernels  61.8 us (31%)
  starting transfers between devices  48.9 us (24%)
  local copies, waits for them, and re-layouts  12.5 us (6%)
  other arithmetic  6.74 us (3%)
  matrix products  2.99 us (1%)
    pallas_call x11, Pallas kernels, call(): pl.pallas_call(body, grid=(n_t,), in_specs=[s for _, s in ins], out_specs...  58.4 us
    ppermute x21, waiting for transfers between devices, send(): lax.ppermute(after(h, *done), AXES, t)  35.8 us
    ppermute x15, waiting for transfers between devices, stage(): lax.ppermute(after(s, *done), AXES, tables[n // pieces])  30.1 us
    ppermute x21, starting transfers between devices, send(): lax.ppermute(after(h, *done), AXES, t)  25.2 us
    ppermute x15, starting transfers between devices, stage(): lax.ppermute(after(s, *done), AXES, tables[n // pieces])  22.1 us
    unnamed x64, local copies, waits for them, and re-layouts  7.04 us
  transfers between devices with their start and end apart: 46, of which 16 were waited for; matrix products, arithmetic and copies ran while one was open for 9% of the time, Pallas kernels for 30%

profile of v7, /device:TPU:0, one launch (start us, length us, event | category | flops | bytes accessed | tf_op | source)
XLA Modules:
  0.0 201.9 jit_solution(12343560211532108599)
XLA Ops:
  0.7 2.0 shard_map.255
  2.6 5.0 %collective-permute-start.2 = (bf16[1,104,768]{2,1,0:T(8,128)(2,1)}, bf16[1,104,768]{2,1,0:T(8,128)(2,1)S(1)}, u32[]{:S(2)}, u32[]{:S(2)}) collective-permute-start(bf16[1,104,768]{2,1,0:T(8,128)(2,1)} %bitcast.134), channel_id=1, source_target_pairs={{0,3},{1,2},{2,1},{3,0},{4,7},{5,6},{6,5},{7,4},{8,11},{9,10},{10,... | collective-permute-start | bytes 479240 | tf_op jit(solution)/shard_map/ppermute | solution.py:480
  8.2 1.7 collective-permute-start.3
  10.5 0.7 copy.57
  12.5 1.0 convolution_bitcast_fusion.pg_ref
  13.6 1.4 shard_map.254
  15.0 6.5 %collective-permute-done.1 = bf16[1,104,768]{2,1,0:T(8,128)(2,1)} collective-permute-done((bf16[1,104,768]{2,1,0:T(8,128)(2,1)}, bf16[1,104,768]{2,1,0:T(8,128)(2,1)}, u32[]{:S(2)}, u32[]{:S(2)}) %collective-permute-start.1) | collective-permute-done | bytes 159776 | tf_op jit(solution)/shard_map/ppermute | solution.py:480
  21.5 1.1 pad_maximum_fusion
  22.6 1.6 collective-permute-start.4
  24.3 3.0 %collective-permute-start.6 = (bf16[1,96,768]{2,1,0:T(8,128)(2,1)S(1)}, bf16[1,96,768]{2,1,0:T(8,128)(2,1)S(1)}, u32[]{:S(2)}, u32[]{:S(2)}) collective-permute-start(bf16[1,96,768]{2,1,0:T(8,128)(2,1)S(1)} %bitcast.142), channel_id=1, source_target_pairs={{0,2},{1,3},{2,0},{3,1},{4,6},{5,7},{6,4},{7,5},{8,10},{9,11},{10,... | collective-permute-start | bytes 442376 | tf_op jit(solution)/shard_map/ppermute | solution.py:480
  27.3 1.3 collective-permute-start.7
  28.7 0.9 constant_dynamic-update-slice_fusion.3
  29.6 0.9 constant_dynamic-update-slice_fusion.2
  30.6 2.5 %collective-permute-done.4 = bf16[4,104,768]{2,1,0:T(8,128)(2,1)S(1)} collective-permute-done((bf16[4,104,768]{2,1,0:T(8,128)(2,1)S(1)}, bf16[4,104,768]{2,1,0:T(8,128)(2,1)S(1)}, u32[]{:S(2)}, u32[]{:S(2)}) %collective-permute-start.4) | collective-permute-done | bytes 639008 | tf_op jit(solution)/shard_map/ppermute | solution.py:480
  33.1 4.5 %collective-permute-done.6 = bf16[1,96,768]{2,1,0:T(8,128)(2,1)S(1)} collective-permute-done((bf16[1,96,768]{2,1,0:T(8,128)(2,1)S(1)}, bf16[1,96,768]{2,1,0:T(8,128)(2,1)S(1)}, u32[]{:S(2)}, u32[]{:S(2)}) %collective-permute-start.6) | collective-permute-done | bytes 147488 | tf_op jit(solution)/shard_map/ppermute | solution.py:480
  37.6 0.7 collective-permute-start.9
  38.4 1.4 collective-permute-start.10
  39.9 0.7 constant_dynamic-update-slice_fusion.9
  40.5 1.7 pad_maximum_fusion.2
  42.2 2.3 %collective-permute-start.11 = (bf16[2,96,768]{2,1,0:T(8,128)(2,1)}, bf16[2,96,768]{2,1,0:T(8,128)(2,1)S(1)}, u32[]{:S(2)}, u32[]{:S(2)}) collective-permute-start(bf16[2,96,768]{2,1,0:T(8,128)(2,1)} %pad_maximum_fusion.2), channel_id=1, source_target_pairs={{0,1},{1,0},{2,3},{3,2},{4,5},{5,4},{6,7},{7,6},{8,9},{9,8},{10,11... | collective-permute-start | bytes 884744 | tf_op jit(solution)/shard_map/ppermute | solution.py:480
  44.5 0.8 collective-permute-start.12
  45.3 0.7 constant_dynamic-update-slice_fusion.8
  46.0 0.7 constant_dynamic-update-slice_fusion.7
  47.3 8.6 %collective-permute-done.11 = bf16[2,96,768]{2,1,0:T(8,128)(2,1)S(1)} collective-permute-done((bf16[2,96,768]{2,1,0:T(8,128)(2,1)}, bf16[2,96,768]{2,1,0:T(8,128)(2,1)S(1)}, u32[]{:S(2)}, u32[]{:S(2)}) %collective-permute-start.11) | collective-permute-done | bytes 294944 | tf_op jit(solution)/shard_map/ppermute | solution.py:480
  56.0 2.8 %collective-permute-done.12 = bf16[2,96,768]{2,1,0:T(8,128)(2,1)S(1)} collective-permute-done((bf16[2,96,768]{2,1,0:T(8,128)(2,1)}, bf16[2,96,768]{2,1,0:T(8,128)(2,1)S(1)}, u32[]{:S(2)}, u32[]{:S(2)}) %collective-permute-start.12) | collective-permute-done | bytes 294944 | tf_op jit(solution)/shard_map/ppermute | solution.py:480
  59.5 0.9 constant_dynamic-update-slice_fusion.5
  60.3 1.7 collective-permute-start.15
  62.1 2.2 %collective-permute-start.16 = (bf16[2,96,768]{2,1,0:T(8,128)(2,1)}, bf16[2,96,768]{2,1,0:T(8,128)(2,1)}, u32[]{:S(2)}, u32[]{:S(2)}) collective-permute-start(bf16[2,96,768]{2,1,0:T(8,128)(2,1)} %pad_maximum_fusion.2), channel_id=1, source_target_pairs={{0,3},{1,2},{2,1},{3,0},{4,7},{5,6},{6,5},{7,4},{8,11},{9,10},{10,... | collective-permute-start | bytes 884744 | tf_op jit(solution)/shard_map/ppermute | solution.py:480
  64.5 11.7 %shard_map.256 = (bf16[4,384,576]{2,1,0:T(8,128)(2,1)}, f32[4,3,128,384]{3,2,1,0:T(8,128)}, bf16[4,384,256]{2,1,0:T(8,128)(2,1)}, f32[384,768]{1,0:T(8,128)S(1)}...) custom-call(bf16[384,768]{1,0:T(8,128)(2,1)S(1)} %get-tuple-element., ...), custom_call_target="tpu_custom_call" | custom-call | flops 300000000 | tf_op jit(solution)/shard_map/pallas_call | solution.py:436
  77.4 1.0 constant_dynamic-update-slice_fusion.13
  78.4 1.0 constant_dynamic-update-slice_fusion.10
  79.4 1.8 collective-permute-start.21
  81.2 1.7 collective-permute-done.19.refs_2_
  83.0 4.9 %shard_map.257 = (bf16[4,384,768]{2,1,0:T(8,128)(2,1)S(1)}, f32[4,384,768]{2,1,0:T(8,128)S(1)}) custom-call(bf16[384,768]{1,0:T(8,128)(2,1)S(1)} %get-tuple-element.97.n_ref, bf16[2,4,96,768]{3,2,1,0:T(8,128)(2,1)} %bitcast.23.w0_ref, bf16[2,4,96,768]{3,2,1,0:T(8,128)(2,1)} %bitcast.24.w1_ref, bf16[2,4,96,768]{3,2,1,0:T(8,128)(2,1)S(1)} %bitcast.123, ...), custom_call_target="tpu_custom_call" | custom-call | flops 120000000 | tf_op jit(solution)/shard_map/pallas_call | solution.py:436
  88.4 7.3 %collective-permute-done.21 = bf16[8,96,768]{2,1,0:T(8,128)(2,1)S(1)} collective-permute-done((bf16[8,96,768]{2,1,0:T(8,128)(2,1)S(1)}, bf16[8,96,768]{2,1,0:T(8,128)(2,1)S(1)}, u32[]{:S(2)}, u32[]{:S(2)}) %collective-permute-start.21) | collective-permute-done | bytes 1179680 | tf_op jit(solution)/shard_map/ppermute | solution.py:480
  95.7 2.8 %collective-permute-done.23 = bf16[8,96,768]{2,1,0:T(8,128)(2,1)S(1)} collective-permute-done((bf16[8,96,768]{2,1,0:T(8,128)(2,1)S(1)}, bf16[8,96,768]{2,1,0:T(8,128)(2,1)S(1)}, u32[]{:S(2)}, u32[]{:S(2)}) %collective-permute-start.23) | collective-permute-done | bytes 1179680 | tf_op jit(solution)/shard_map/ppermute | solution.py:480
  98.5 5.3 %shard_map.258 = (f32[3,8,768]{2,1,0:T(8,128)S(1)}, f32[384,768]{1,0:T(8,128)S(1)}, bf16[384,768]{1,0:T(8,128)(2,1)S(1)}, bf16[384,384]{1,0:T(8,128)(2,1)S(1)}, ...) custom-call(bf16[4,384,768]{2,1,0:T(8,128)(2,1)S(1)} %get-tuple-element.107.z_ref.refs_1_, ...), custom_call_target="tpu_custom_call" | custom-call | flops 165000000 | tf_op jit(solution)/shard_map/pallas_call | solution.py:436
  104.1 2.7 %shard_map.259 = (bf16[4,384,768]{2,1,0:T(8,128)(2,1)S(1)}, f32[4,1,768]{2,1,0:T(1,128)S(1)}) custom-call(bf16[384,768]{1,0:T(8,128)(2,1)S(1)} %get-tuple-element.114.dbb_ref, bf16[4,2,96,768]{3,2,1,0:T(8,128)(2,1)S(1)} %bitcast.112, bf16[4,2,96,768]{3,2,1,0:T(8,128)(2,1)S(1)} %bitcast.114, bf16[4,2,96,768]{3,2,1,0:T(8,128)(2,1)S(1)} %bitcast.116, ...), custom_call_target="tpu_custom_call" | custom-call | flops 105000000 | tf_op jit(solution)/shard_map/pallas_call | solution.py:436
  107.2 1.9 shard_map.260
  109.1 1.8 collective-permute-start.28
  110.9 5.5 %shard_map.261 = (f32[384,768]{1,0:T(8,128)S(1)}, bf16[384,768]{1,0:T(8,128)(2,1)S(1)}, bf16[384,384]{1,0:T(8,128)(2,1)S(1)}, bf16[384,384]{1,0:T(8,128)(2,1)S(1)}, f32[3,768]{1,0:T(4,128)S(1)}) custom-call(bf16[4,384,768]{2,1,0:T(8,128)(2,1)S(1)} %get-tuple-element.121.du_ref.refs_1_, bf16[2,4,96,768]{3,2,1,0:T(8,128)(2,1)} %bitcast.23.w0_ref, ...), custom_call_target="tpu_custom_call" | custom-call | flops 60000002048 | tf_op jit(solution)/shard_map/pallas_call | solution.py:436
  116.5 3.3 %shard_map.262 = (bf16[2,4,96,768]{3,2,1,0:T(8,128)(2,1)S(1)}, bf16[2,4,96,768]{3,2,1,0:T(8,128)(2,1)S(1)}) custom-call(bf16[384,384]{1,0:T(8,128)(2,1)S(1)} %copy-done.10, bf16[4,384,768]{2,1,0:T(8,128)(2,1)S(1)} %get-tuple-element.121.du_ref.refs_1_, bf16[384,384]{1,0:T(8,128)(2,1)S(1)} %collective-permute-done.19.refs_2_, ...), custom_call_target="tpu_custom_call" | custom-call | flops 60000000 | tf_op jit(solution)/shard_map/pallas_call | solution.py:436
  120.1 1.9 shard_map.263
  122.1 3.3 %collective-permute-done.28 = bf16[8,96,768]{2,1,0:T(8,128)(2,1)S(1)} collective-permute-done((bf16[8,96,768]{2,1,0:T(8,128)(2,1)S(1)}, bf16[8,96,768]{2,1,0:T(8,128)(2,1)S(1)}, u32[]{:S(2)}, u32[]{:S(2)}) %collective-permute-start.28) | collective-permute-done | bytes 1179680 | tf_op jit(solution)/shard_map/ppermute | solution.py:500
  125.4 8.7 %shard_map.264 = (bf16[2,384,640]{2,1,0:T(8,128)(2,1)S(1)}, bf16[2,384,640]{2,1,0:T(8,128)(2,1)S(1)}, f32[4,4,768]{2,1,0:T(4,128)S(1)}, f32[4,4,768]{2,1,0:T(4,128)S(1)}) custom-call(bf16[384,768]{1,0:T(8,128)(2,1)S(1)} %get-tuple-element.132.dab_ref, bf16[2,4,104,768]{3,2,1,0:T(8,128)(2,1)S(1)} %bitcast.105, bf16[2,4,104,768]{3,2,1,0:T(8,128)(2,1)S(1)} %bitcast.109, ...), custom_call_target="tpu_custom_call" | custom-call | flops 240000000 | tf_op jit(solution)/shard_map/pallas_call | solution.py:436
  135.3 3.0 %collective-permute-done.29 = bf16[8,96,768]{2,1,0:T(8,128)(2,1)S(1)} collective-permute-done((bf16[8,96,768]{2,1,0:T(8,128)(2,1)S(1)}, bf16[8,96,768]{2,1,0:T(8,128)(2,1)S(1)}, u32[]{:S(2)}, u32[]{:S(2)}) %collective-permute-start.29) | collective-permute-done | bytes 1179680 | tf_op jit(solution)/shard_map/ppermute | solution.py:500
  139.1 2.0 fusion
  141.1 5.3 %shard_map.265 = (bf16[2,4,104,768]{3,2,1,0:T(8,128)(2,1)S(1)}, bf16[2,4,104,768]{3,2,1,0:T(8,128)(2,1)S(1)}) custom-call(bf16[384,384]{1,0:T(8,128)(2,1)S(1)} %copy-done.9, bf16[2,384,640]{2,1,0:T(8,128)(2,1)S(1)} %get-tuple-element.144.refs_1_.low_ref, bf16[2,384,640]{2,1,0:T(8,128)(2,1)S(1)} %get-tuple-element.145.refs_2_.high_ref, ...), custom_call_target="tpu_custom_call" | custom-call | flops 60000000 | tf_op jit(solution)/shard_map/pallas_call | solution.py:436
  146.4 4.8 %collective-permute-done.34 = bf16[4,96,768]{2,1,0:T(8,128)(2,1)S(1)} collective-permute-done((bf16[4,96,768]{2,1,0:T(8,128)(2,1)S(1)}, bf16[4,96,768]{2,1,0:T(8,128)(2,1)S(1)}, u32[]{:S(2)}, u32[]{:S(2)}) %collective-permute-start.34) | collective-permute-done | bytes 589856 | tf_op jit(solution)/shard_map/ppermute | solution.py:500
  151.2 1.7 collective-permute-start.35
  153.3 2.6 %collective-permute-start.38 = (bf16[2,96,768]{2,1,0:T(8,128)(2,1)S(1)}, bf16[2,96,768]{2,1,0:T(8,128)(2,1)S(1)}, u32[]{:S(2)}, u32[]{:S(2)}) collective-permute-start(bf16[2,96,768]{2,1,0:T(8,128)(2,1)S(1)} %pad_maximum_fusion.3), channel_id=1, source_target_pairs={{0,1},{1,0},{2,3},{3,2},{4,5},{5,4},{6,7},{7,6},{8,9},{9,8},{10,11... | collective-permute-start | bytes 884744 | tf_op jit(solution)/shard_map/ppermute | solution.py:500
  155.9 0.8 collective-permute-start.39
  156.7 1.7 collective-permute-start.40
  158.4 7.3 %shard_map.266 = f32[384,768]{1,0:T(8,128)} custom-call(bf16[2,384,640]{2,1,0:T(8,128)(2,1)S(1)} %get-tuple-element.144.refs_1_.low_ref, bf16[2,384,640]{2,1,0:T(8,128)(2,1)S(1)} %get-tuple-element.145.refs_2_.high_ref, bf16[2,4,104,768]{3,2,1,0:T(8,128)(2,1)S(1)} %bitcast.106, bf16[2,4,104,768]{3,2,1,0:T(8,128)(2,1)S(1)} %bitcast.110, ...), custom_call_target="tpu_custom_call" | custom-call | flops 120000000 | tf_op jit(solution)/shard_map/pallas_call | solution.py:436
  165.7 2.8 %collective-permute-done.35 = bf16[8,104,768]{2,1,0:T(8,128)(2,1)S(1)} collective-permute-done((bf16[8,104,768]{2,1,0:T(8,128)(2,1)S(1)}, bf16[8,104,768]{2,1,0:T(8,128)(2,1)S(1)}, u32[]{:S(2)}, u32[]{:S(2)}) %collective-permute-start.35) | collective-permute-done | bytes 1277984 | tf_op jit(solution)/shard_map/ppermute | solution.py:500
  169.0 1.7 collective-permute-start.44
  171.1 8.4 %collective-permute-done.39 = bf16[2,96,768]{2,1,0:T(8,128)(2,1)S(1)} collective-permute-done((bf16[2,96,768]{2,1,0:T(8,128)(2,1)S(1)}, bf16[2,96,768]{2,1,0:T(8,128)(2,1)S(1)}, u32[]{:S(2)}, u32[]{:S(2)}) %collective-permute-start.39) | collective-permute-done | bytes 294944 | tf_op jit(solution)/shard_map/ppermute | solution.py:500
  179.6 1.2 collective-permute-start.36
  181.0 2.3 %collective-permute-start.45 = (bf16[1,104,768]{2,1,0:T(8,128)(2,1)S(1)}, bf16[1,104,768]{2,1,0:T(8,128)(2,1)S(1)}, u32[]{:S(2)}, u32[]{:S(2)}) collective-permute-start(bf16[1,104,768]{2,1,0:T(8,128)(2,1)S(1)} %get-tuple-element.155), channel_id=1, source_target_pairs={{0,3},{1,2},{2,1},{3,0},{4,7},{5,6},{6,5},{7,4},{8,11},{9,10},{10,... | collective-permute-start | bytes 479240 | tf_op jit(solution)/shard_map/ppermute | solution.py:500
  183.3 6.5 %collective-permute-start.43 = (bf16[1,104,768]{2,1,0:T(8,128)(2,1)S(1)}, bf16[1,104,768]{2,1,0:T(8,128)(2,1)S(1)}, u32[]{:S(2)}, u32[]{:S(2)}) collective-permute-start(bf16[1,104,768]{2,1,0:T(8,128)(2,1)S(1)} %get-tuple-element.153), channel_id=1, source_target_pairs={{0,2},{1,3},{2,0},{3,1},{4,6},{5,7},{6,4},{7,5},{8,10},{9,11},{10,... | collective-permute-start | bytes 479240 | tf_op jit(solution)/shard_map/ppermute | solution.py:500
  189.7 0.8 slice_bitcast_fusion.2
  190.6 7.8 %collective-permute-done.43 = bf16[1,104,768]{2,1,0:T(8,128)(2,1)S(1)} collective-permute-done((bf16[1,104,768]{2,1,0:T(8,128)(2,1)S(1)}, bf16[1,104,768]{2,1,0:T(8,128)(2,1)S(1)}, u32[]{:S(2)}, u32[]{:S(2)}) %collective-permute-start.43) | collective-permute-done | bytes 159776 | tf_op jit(solution)/shard_map/ppermute | solution.py:500
  199.9 0.7 copy.62
  201.2 0.7 pad_maximum_fusion.6
  (151 shorter events, 12.7 us)
Async XLA Ops:
  0.6 11.8 %copy-start = (f32[3,1,8,768]{3,2,1,0:T(8,128)S(1)}, f32[3,1,8,768]{3,2,1,0:T(8,128)}, u32[]{:S(2)}) copy-start(f32[3,1,8,768]{3,2,1,0:T(8,128)} %param.17) | copy-start | bytes 221188
  2.6 12.4 %collective-permute-start.2 = (bf16[1,104,768]{2,1,0:T(8,128)(2,1)}, bf16[1,104,768]{2,1,0:T(8,128)(2,1)S(1)}, u32[]{:S(2)}, u32[]{:S(2)}) collective-permute-start(bf16[1,104,768]{2,1,0:T(8,128)(2,1)} %bitcast.134), channel_id=1, source_target_pairs={{0,3},{1,2},{2,1},{3,0},{4,7},{5,6},{6,5},{7,4},{8,11},{9,10},{10,... | collective-permute-start | bytes 479240 | tf_op jit(solution)/shard_map/ppermute | solution.py:480
  7.7 13.8 %collective-permute-start.1 = (bf16[1,104,768]{2,1,0:T(8,128)(2,1)}, bf16[1,104,768]{2,1,0:T(8,128)(2,1)}, u32[]{:S(2)}, u32[]{:S(2)}) collective-permute-start(bf16[1,104,768]{2,1,0:T(8,128)(2,1)} %bitcast.135), channel_id=1, source_target_pairs={{0,2},{1,3},{2,0},{3,1},{4,6},{5,7},{6,4},{7,5},{8,10},{9,11},{10,... | collective-permute-start | bytes 479240 | tf_op jit(solution)/shard_map/ppermute | solution.py:480
  7.7 13.8 %collective-permute-start = (bf16[1,104,768]{2,1,0:T(8,128)(2,1)}, bf16[1,104,768]{2,1,0:T(8,128)(2,1)}, u32[]{:S(2)}, u32[]{:S(2)}) collective-permute-start(bf16[1,104,768]{2,1,0:T(8,128)(2,1)} %bitcast.136), channel_id=1, source_target_pairs={{0,1},{1,0},{2,3},{3,2},{4,5},{5,4},{6,7},{7,6},{8,9},{9,8},{10,11... | collective-permute-start | bytes 479240 | tf_op jit(solution)/shard_map/ppermute | solution.py:480
  8.2 14.4 %collective-permute-start.3 = (bf16[1,96,768]{2,1,0:T(8,128)(2,1)}, bf16[1,96,768]{2,1,0:T(8,128)(2,1)}, u32[]{:S(2)}, u32[]{:S(2)}) collective-permute-start(bf16[1,96,768]{2,1,0:T(8,128)(2,1)} %bitcast.145), channel_id=1, source_target_pairs={{0,16},{1,17},{2,18},{3,19},{4,12},{5,13},{6,14},{7,15},{8,24},{9,... | collective-permute-start | bytes 442376 | tf_op jit(solution)/shard_map/ppermute | solution.py:480
  11.7 3.4 %copy-start.2 = (bf16[768,768]{1,0:T(8,128)(2,1)}, bf16[768,768]{1,0:T(8,128)(2,1)S(1)}, u32[]{:S(2)}) copy-start(bf16[768,768]{1,0:T(8,128)(2,1)S(1)} %fusion.2.perm_ref) | copy-start | bytes 3538948
  12.5 9.0 %copy-start.15 = (bf16[104,768]{1,0:T(8,128)(2,1)S(1)}, bf16[104,768]{1,0:T(8,128)(2,1)}, u32[]{:S(2)}) copy-start(bf16[104,768]{1,0:T(8,128)(2,1)} %shard_map.255) | copy-start | bytes 479236
  15.0 15.5 %copy-start.8 = (bf16[384,384]{1,0:T(8,128)(2,1)}, bf16[384,384]{1,0:T(8,128)(2,1)S(1)}, u32[]{:S(2)}) copy-start(bf16[384,384]{1,0:T(8,128)(2,1)S(1)} %get-tuple-element.139.refs_0_) | copy-start | bytes 884740
  15.0 9.2 %copy-start.16 = (bf16[96,768]{1,0:T(8,128)(2,1)S(1)}, bf16[96,768]{1,0:T(8,128)(2,1)}, u32[]{:S(2)}) copy-start(bf16[96,768]{1,0:T(8,128)(2,1)} %param.24) | copy-start | bytes 442372
  22.6 10.5 %collective-permute-start.4 = (bf16[4,104,768]{2,1,0:T(8,128)(2,1)S(1)}, bf16[4,104,768]{2,1,0:T(8,128)(2,1)S(1)}, u32[]{:S(2)}, u32[]{:S(2)}) collective-permute-start(bf16[4,104,768]{2,1,0:T(8,128)(2,1)S(1)} %pad_maximum_fusion), channel_id=1, source_target_pairs={{0,16},{1,17},{2,18},{3,19},{4,12},{5,13},{6,14},{7,15},{8,24},{9,... | collective-permute-start | bytes 1916936 | tf_op jit(solution)/shard_map/ppermute | solution.py:480
  24.2 8.9 %collective-permute-start.5 = (bf16[1,96,768]{2,1,0:T(8,128)(2,1)S(1)}, bf16[1,96,768]{2,1,0:T(8,128)(2,1)S(1)}, u32[]{:S(2)}, u32[]{:S(2)}) collective-permute-start(bf16[1,96,768]{2,1,0:T(8,128)(2,1)S(1)} %bitcast.141), channel_id=1, source_target_pairs={{0,1},{1,0},{2,3},{3,2},{4,5},{5,4},{6,7},{7,6},{8,9},{9,8},{10,11... | collective-permute-start | bytes 442376 | tf_op jit(solution)/shard_map/ppermute | solution.py:480
  24.3 13.3 %collective-permute-start.6 = (bf16[1,96,768]{2,1,0:T(8,128)(2,1)S(1)}, bf16[1,96,768]{2,1,0:T(8,128)(2,1)S(1)}, u32[]{:S(2)}, u32[]{:S(2)}) collective-permute-start(bf16[1,96,768]{2,1,0:T(8,128)(2,1)S(1)} %bitcast.142), channel_id=1, source_target_pairs={{0,2},{1,3},{2,0},{3,1},{4,6},{5,7},{6,4},{7,5},{8,10},{9,11},{10,... | collective-permute-start | bytes 442376 | tf_op jit(solution)/shard_map/ppermute | solution.py:480
  27.3 10.3 %collective-permute-start.7 = (bf16[1,96,768]{2,1,0:T(8,128)(2,1)S(1)}, bf16[1,96,768]{2,1,0:T(8,128)(2,1)S(1)}, u32[]{:S(2)}, u32[]{:S(2)}) collective-permute-start(bf16[1,96,768]{2,1,0:T(8,128)(2,1)S(1)} %bitcast.143), channel_id=1, source_target_pairs={{0,3},{1,2},{2,1},{3,0},{4,7},{5,6},{6,5},{7,4},{8,11},{9,10},{10,... | collective-permute-start | bytes 442376 | tf_op jit(solution)/shard_map/ppermute | solution.py:480
  30.6 10.0 %copy-start.17 = (bf16[768,96]{0,1:T(8,128)(2,1)S(1)}, bf16[768,96]{0,1:T(8,128)(2,1)}, u32[]{:S(2)}) copy-start(bf16[768,96]{0,1:T(8,128)(2,1)} %param.26) | copy-start | bytes 442372
  37.6 21.2 %collective-permute-start.9 = (bf16[8,104,768]{2,1,0:T(8,128)(2,1)S(1)}, bf16[8,104,768]{2,1,0:T(8,128)(2,1)S(1)}, u32[]{:S(2)}, u32[]{:S(2)}) collective-permute-start(bf16[8,104,768]{2,1,0:T(8,128)(2,1)S(1)} %constant_dynamic-update-slice_fusion), channel_id=1, source_target_pairs={{0,8},{1,9},{2,10},{3,11},{4,20},{5,21},{6,22},{7,23},{8,0},{9,1},... | collective-permute-start | bytes 3833864 | tf_op jit(solution)/shard_map/ppermute | solution.py:480
  38.4 20.4 %collective-permute-start.10 = (bf16[4,96,768]{2,1,0:T(8,128)(2,1)S(1)}, bf16[4,96,768]{2,1,0:T(8,128)(2,1)S(1)}, u32[]{:S(2)}, u32[]{:S(2)}) collective-permute-start(bf16[4,96,768]{2,1,0:T(8,128)(2,1)S(1)} %pad_maximum_fusion.1), channel_id=1, source_target_pairs={{0,16},{1,17},{2,18},{3,19},{4,12},{5,13},{6,14},{7,15},{8,24},{9,... | collective-permute-start | bytes 1769480 | tf_op jit(solution)/shard_map/ppermute | solution.py:480
  42.2 22.1 %copy-start.23 = (s32[3,1,128]{2,1,0:T(1,128)S(1)}, s32[3,1,128]{2,1,0:T(1,128)}, u32[]{:S(2)}) copy-start(s32[3,1,128]{2,1,0:T(1,128)} %param.16) | copy-start | bytes 4612
  42.2 13.8 %collective-permute-start.11 = (bf16[2,96,768]{2,1,0:T(8,128)(2,1)}, bf16[2,96,768]{2,1,0:T(8,128)(2,1)S(1)}, u32[]{:S(2)}, u32[]{:S(2)}) collective-permute-start(bf16[2,96,768]{2,1,0:T(8,128)(2,1)} %pad_maximum_fusion.2), channel_id=1, source_target_pairs={{0,1},{1,0},{2,3},{3,2},{4,5},{5,4},{6,7},{7,6},{8,9},{9,8},{10,11... | collective-permute-start | bytes 884744 | tf_op jit(solution)/shard_map/ppermute | solution.py:480
  44.5 14.3 %collective-permute-start.12 = (bf16[2,96,768]{2,1,0:T(8,128)(2,1)}, bf16[2,96,768]{2,1,0:T(8,128)(2,1)S(1)}, u32[]{:S(2)}, u32[]{:S(2)}) collective-permute-start(bf16[2,96,768]{2,1,0:T(8,128)(2,1)} %pad_maximum_fusion.2), channel_id=1, source_target_pairs={{0,2},{1,3},{2,0},{3,1},{4,6},{5,7},{6,4},{7,5},{8,10},{9,11},{10,... | collective-permute-start | bytes 884744 | tf_op jit(solution)/shard_map/ppermute | solution.py:480
  58.9 5.6 %collective-permute-start.13 = (bf16[8,104,768]{2,1,0:T(8,128)(2,1)S(1)}, bf16[8,104,768]{2,1,0:T(8,128)(2,1)}, u32[]{:S(2)}, u32[]{:S(2)}) collective-permute-start(bf16[8,104,768]{2,1,0:T(8,128)(2,1)S(1)} %constant_dynamic-update-slice_fusion), channel_id=1, source_target_pairs={{0,4},{1,5},{2,6},{3,7},{4,0},{5,1},{6,2},{7,3},{8,12},{9,13},{10,... | collective-permute-start | bytes 3833864 | tf_op jit(solution)/shard_map/ppermute | solution.py:480
  59.5 5.0 %collective-permute-start.14 = (bf16[8,104,768]{2,1,0:T(8,128)(2,1)S(1)}, bf16[8,104,768]{2,1,0:T(8,128)(2,1)}, u32[]{:S(2)}, u32[]{:S(2)}) collective-permute-start(bf16[8,104,768]{2,1,0:T(8,128)(2,1)S(1)} %collective-permute-done.9), channel_id=1, source_target_pairs={{0,4},{1,5},{2,6},{3,7},{4,0},{5,1},{6,2},{7,3},{8,12},{9,13},{10,... | collective-permute-start | bytes 3833864 | tf_op jit(solution)/shard_map/ppermute | solution.py:480
  60.3 16.5 %collective-permute-start.15 = (bf16[8,96,768]{2,1,0:T(8,128)(2,1)}, bf16[8,96,768]{2,1,0:T(8,128)(2,1)}, u32[]{:S(2)}, u32[]{:S(2)}) collective-permute-start(bf16[8,96,768]{2,1,0:T(8,128)(2,1)} %constant_dynamic-update-slice_fusion.5), channel_id=1, source_target_pairs={{0,8},{1,9},{2,10},{3,11},{4,20},{5,21},{6,22},{7,23},{8,0},{9,1},... | collective-permute-start | bytes 3538952 | tf_op jit(solution)/shard_map/ppermute | solution.py:480
  62.1 2.4 %collective-permute-start.8 = (bf16[384,384]{1,0:T(8,128)(2,1)}, bf16[384,384]{1,0:T(8,128)(2,1)}, u32[]{:S(2)}, u32[]{:S(2)}) collective-permute-start(bf16[384,384]{1,0:T(8,128)(2,1)} %get-tuple-element.90), channel_id=1, source_target_pairs={{0,4},{1,5},{2,6},{3,7},{4,0},{5,1},{6,2},{7,3},{8,12},{9,13},{10,... | collective-permute-start | bytes 884744 | tf_op jit(solution)/shard_map/ppermute | solution.py:471
  62.1 14.8 %collective-permute-start.16 = (bf16[2,96,768]{2,1,0:T(8,128)(2,1)}, bf16[2,96,768]{2,1,0:T(8,128)(2,1)}, u32[]{:S(2)}, u32[]{:S(2)}) collective-permute-start(bf16[2,96,768]{2,1,0:T(8,128)(2,1)} %pad_maximum_fusion.2), channel_id=1, source_target_pairs={{0,3},{1,2},{2,1},{3,0},{4,7},{5,6},{6,5},{7,4},{8,11},{9,10},{10,... | collective-permute-start | bytes 884744 | tf_op jit(solution)/shard_map/ppermute | solution.py:480
  64.5 12.9 %copy-start.18 = (bf16[768,96]{0,1:T(8,128)(2,1)S(1)}, bf16[768,96]{0,1:T(8,128)(2,1)}, u32[]{:S(2)}) copy-start(bf16[768,96]{0,1:T(8,128)(2,1)} %param.26) | copy-start | bytes 442372
  64.5 13.9 %copy-start.20 = (bf16[2,96,768]{2,1,0:T(8,128)(2,1)S(1)}, bf16[2,96,768]{2,1,0:T(8,128)(2,1)}, u32[]{:S(2)}) copy-start(bf16[2,96,768]{2,1,0:T(8,128)(2,1)} %copy-done.19) | copy-start | bytes 884740
  76.9 6.1 %collective-permute-start.17 = (bf16[8,96,768]{2,1,0:T(8,128)(2,1)}, bf16[8,96,768]{2,1,0:T(8,128)(2,1)S(1)}, u32[]{:S(2)}, u32[]{:S(2)}) collective-permute-start(bf16[8,96,768]{2,1,0:T(8,128)(2,1)} %constant_dynamic-update-slice_fusion.5), channel_id=1, source_target_pairs={{0,4},{1,5},{2,6},{3,7},{4,0},{5,1},{6,2},{7,3},{8,12},{9,13},{10,... | collective-permute-start | bytes 3538952 | tf_op jit(solution)/shard_map/ppermute | solution.py:480
  76.9 6.1 %collective-permute-start.18 = (bf16[8,96,768]{2,1,0:T(8,128)(2,1)}, bf16[8,96,768]{2,1,0:T(8,128)(2,1)S(1)}, u32[]{:S(2)}, u32[]{:S(2)}) collective-permute-start(bf16[8,96,768]{2,1,0:T(8,128)(2,1)} %collective-permute-done.15), channel_id=1, source_target_pairs={{0,4},{1,5},{2,6},{3,7},{4,0},{5,1},{6,2},{7,3},{8,12},{9,13},{10,... | collective-permute-start | bytes 3538952 | tf_op jit(solution)/shard_map/ppermute | solution.py:480
  77.4 3.9 %copy-start.24 = (bf16[384,384]{1,0:T(8,128)(2,1)S(1)}, bf16[384,384]{1,0:T(8,128)(2,1)}, u32[]{:S(2)}) copy-start(bf16[384,384]{1,0:T(8,128)(2,1)} %get-tuple-element.104) | copy-start | bytes 884740
  77.4 5.6 %collective-permute-start.20 = (bf16[4,384,256]{2,1,0:T(8,128)(2,1)}, bf16[4,384,256]{2,1,0:T(8,128)(2,1)S(1)}, u32[]{:S(2)}, u32[]{:S(2)}) collective-permute-start(bf16[4,384,256]{2,1,0:T(8,128)(2,1)} %get-tuple-element.105.refs_7_), channel_id=1, source_target_pairs={{0,4},{1,5},{2,6},{3,7},{4,0},{5,1},{6,2},{7,3},{8,12},{9,13},{10,... | collective-permute-start | bytes 2359304 | tf_op jit(solution)/shard_map/ppermute | solution.py:471
  79.4 16.3 %collective-permute-start.21 = (bf16[8,96,768]{2,1,0:T(8,128)(2,1)S(1)}, bf16[8,96,768]{2,1,0:T(8,128)(2,1)S(1)}, u32[]{:S(2)}, u32[]{:S(2)}) collective-permute-start(bf16[8,96,768]{2,1,0:T(8,128)(2,1)S(1)} %constant_dynamic-update-slice_fusion.10), channel_id=1, source_target_pairs={{0,8},{1,9},{2,10},{3,11},{4,20},{5,21},{6,22},{7,23},{8,0},{9,1},... | collective-permute-start | bytes 3538952 | tf_op jit(solution)/shard_map/ppermute | solution.py:480
  81.2 1.7 collective-permute-start.19
  87.9 19.3 %collective-permute-start.25 = (bf16[4,384,768]{2,1,0:T(8,128)(2,1)S(1)}, bf16[4,384,768]{2,1,0:T(8,128)(2,1)S(1)}, u32[]{:S(2)}, u32[]{:S(2)}) collective-permute-start(bf16[4,384,768]{2,1,0:T(8,128)(2,1)S(1)} %get-tuple-element.107.z_ref.refs_1_), channel_id=1, source_target_pairs={{0,4},{1,5},{2,6},{3,7},{4,0},{5,1},{6,2},{7,3},{8,12},{9,13},{10,... | collective-permute-start | bytes 7077896 | tf_op jit(solution)/shard_map/ppermute | solution.py:471
  88.1 7.6 %collective-permute-start.22 = (bf16[8,96,768]{2,1,0:T(8,128)(2,1)S(1)}, bf16[8,96,768]{2,1,0:T(8,128)(2,1)S(1)}, u32[]{:S(2)}, u32[]{:S(2)}) collective-permute-start(bf16[8,96,768]{2,1,0:T(8,128)(2,1)S(1)} %constant_dynamic-update-slice_fusion.10), channel_id=1, source_target_pairs={{0,4},{1,5},{2,6},{3,7},{4,0},{5,1},{6,2},{7,3},{8,12},{9,13},{10,... | collective-permute-start | bytes 3538952 | tf_op jit(solution)/shard_map/ppermute | solution.py:480
  95.7 2.8 %collective-permute-start.23 = (bf16[8,96,768]{2,1,0:T(8,128)(2,1)S(1)}, bf16[8,96,768]{2,1,0:T(8,128)(2,1)S(1)}, u32[]{:S(2)}, u32[]{:S(2)}) collective-permute-start(bf16[8,96,768]{2,1,0:T(8,128)(2,1)S(1)} %collective-permute-done.21), channel_id=1, source_target_pairs={{0,4},{1,5},{2,6},{3,7},{4,0},{5,1},{6,2},{7,3},{8,12},{9,13},{10,... | collective-permute-start | bytes 3538952 | tf_op jit(solution)/shard_map/ppermute | solution.py:480
  103.9 3.3 %collective-permute-start.24 = (bf16[384,384]{1,0:T(8,128)(2,1)S(1)}, bf16[384,384]{1,0:T(8,128)(2,1)S(1)}, u32[]{:S(2)}, u32[]{:S(2)}) collective-permute-start(bf16[384,384]{1,0:T(8,128)(2,1)S(1)} %get-tuple-element.120), channel_id=1, source_target_pairs={{0,4},{1,5},{2,6},{3,7},{4,0},{5,1},{6,2},{7,3},{8,12},{9,13},{10,... | collective-permute-start | bytes 884744 | tf_op jit(solution)/shard_map/ppermute | solution.py:471
  106.7 4.2 %copy-start.11 = (f32[384,768]{1,0:T(8,128)S(1)}, f32[384,768]{1,0:T(8,128)}, u32[]{:S(2)}) copy-start(f32[384,768]{1,0:T(8,128)} %get-tuple-element.123.x1_ref) | copy-start | bytes 3538948
  106.7 4.2 %copy-start.12 = (f32[384,1]{1,0:T(8,128)S(1)}, f32[384,1]{1,0:T(8,128)}, u32[]{:S(2)}) copy-start(f32[384,1]{1,0:T(8,128)} %get-tuple-element.124.r1_ref) | copy-start | bytes 4612
  106.7 9.7 %collective-permute-start.26 = (bf16[4,384,768]{2,1,0:T(8,128)(2,1)S(1)}, bf16[4,384,768]{2,1,0:T(8,128)(2,1)S(1)}, u32[]{:S(2)}, u32[]{:S(2)}) collective-permute-start(bf16[4,384,768]{2,1,0:T(8,128)(2,1)S(1)} %get-tuple-element.121.du_ref.refs_1_), channel_id=1, source_target_pairs={{0,4},{1,5},{2,6},{3,7},{4,0},{5,1},{6,2},{7,3},{8,12},{9,13},{10,... | collective-permute-start | bytes 7077896 | tf_op jit(solution)/shard_map/ppermute | solution.py:471
  109.1 16.3 %collective-permute-start.28 = (bf16[8,96,768]{2,1,0:T(8,128)(2,1)S(1)}, bf16[8,96,768]{2,1,0:T(8,128)(2,1)S(1)}, u32[]{:S(2)}, u32[]{:S(2)}) collective-permute-start(bf16[8,96,768]{2,1,0:T(8,128)(2,1)S(1)} %bitcast.122), channel_id=1, source_target_pairs={{0,8},{1,9},{2,10},{3,11},{4,20},{5,21},{6,22},{7,23},{8,0},{9,1},... | collective-permute-start | bytes 3538952 | tf_op jit(solution)/shard_map/ppermute | solution.py:500
  110.9 5.5 %copy-start.10 = (bf16[384,384]{1,0:T(8,128)(2,1)S(1)}, bf16[384,384]{1,0:T(8,128)(2,1)}, u32[]{:S(2)}) copy-start(bf16[384,384]{1,0:T(8,128)(2,1)} %get-tuple-element.128.refs_0_) | copy-start | bytes 884740
  119.8 18.6 %collective-permute-start.29 = (bf16[8,96,768]{2,1,0:T(8,128)(2,1)S(1)}, bf16[8,96,768]{2,1,0:T(8,128)(2,1)S(1)}, u32[]{:S(2)}, u32[]{:S(2)}) collective-permute-start(bf16[8,96,768]{2,1,0:T(8,128)(2,1)S(1)} %bitcast.131), channel_id=1, source_target_pairs={{0,8},{1,9},{2,10},{3,11},{4,20},{5,21},{6,22},{7,23},{8,0},{9,1},... | collective-permute-start | bytes 3538952 | tf_op jit(solution)/shard_map/ppermute | solution.py:500
  120.1 1.9 collective-permute-start.27
  120.1 5.3 %copy-start.4 = (f32[4,3,128,384]{3,2,1,0:T(8,128)S(1)}, f32[4,3,128,384]{3,2,1,0:T(8,128)}, u32[]{:S(2)}) copy-start(f32[4,3,128,384]{3,2,1,0:T(8,128)} %get-tuple-element.134.p_ref) | copy-start | bytes 7077892
  120.1 5.3 %copy-start.5 = (bf16[4,384,576]{2,1,0:T(8,128)(2,1)S(1)}, bf16[4,384,576]{2,1,0:T(8,128)(2,1)}, u32[]{:S(2)}) copy-start(bf16[4,384,576]{2,1,0:T(8,128)(2,1)} %get-tuple-element.133.qkv_ref) | copy-start | bytes 5308420
  134.1 7.0 %collective-permute-start.30 = (bf16[2,384,640]{2,1,0:T(8,128)(2,1)S(1)}, bf16[2,384,640]{2,1,0:T(8,128)(2,1)S(1)}, u32[]{:S(2)}, u32[]{:S(2)}) collective-permute-start(bf16[2,384,640]{2,1,0:T(8,128)(2,1)S(1)} %get-tuple-element.144.refs_1_.low_ref), channel_id=1, source_target_pairs={{0,4},{1,5},{2,6},{3,7},{4,0},{5,1},{6,2},{7,3},{8,12},{9,13},{10,... | collective-permute-start | bytes 2949128 | tf_op jit(solution)/shard_map/ppermute | solution.py:471
  134.2 6.9 %collective-permute-start.31 = (bf16[2,384,640]{2,1,0:T(8,128)(2,1)S(1)}, bf16[2,384,640]{2,1,0:T(8,128)(2,1)S(1)}, u32[]{:S(2)}, u32[]{:S(2)}) collective-permute-start(bf16[2,384,640]{2,1,0:T(8,128)(2,1)S(1)} %get-tuple-element.145.refs_2_.high_ref), channel_id=1, source_target_pairs={{0,4},{1,5},{2,6},{3,7},{4,0},{5,1},{6,2},{7,3},{8,12},{9,13},{10,... | collective-permute-start | bytes 2949128 | tf_op jit(solution)/shard_map/ppermute | solution.py:471
  134.9 4.2 %copy-start.14 = (pred[768,768]{1,0:T(32,128)(4,1)S(1)}, pred[768,768]{1,0:T(32,128)(4,1)}, u32[]{:S(2)}) copy-start(pred[768,768]{1,0:T(32,128)(4,1)} %copy-done.13) | copy-start | bytes 1769476
  134.9 11.4 %collective-permute-start.33 = (bf16[4,96,768]{2,1,0:T(8,128)(2,1)S(1)}, bf16[4,96,768]{2,1,0:T(8,128)(2,1)S(1)}, u32[]{:S(2)}, u32[]{:S(2)}) collective-permute-start(bf16[4,96,768]{2,1,0:T(8,128)(2,1)S(1)} %get-tuple-element.208), channel_id=1, source_target_pairs={{0,16},{1,17},{2,18},{3,19},{4,12},{5,13},{6,14},{7,15},{8,24},{9,... | collective-permute-start | bytes 1769480 | tf_op jit(solution)/shard_map/ppermute | solution.py:500
  138.6 12.6 %collective-permute-start.34 = (bf16[4,96,768]{2,1,0:T(8,128)(2,1)S(1)}, bf16[4,96,768]{2,1,0:T(8,128)(2,1)S(1)}, u32[]{:S(2)}, u32[]{:S(2)}) collective-permute-start(bf16[4,96,768]{2,1,0:T(8,128)(2,1)S(1)} %get-tuple-element.210), channel_id=1, source_target_pairs={{0,16},{1,17},{2,18},{3,19},{4,12},{5,13},{6,14},{7,15},{8,24},{9,... | collective-permute-start | bytes 1769480 | tf_op jit(solution)/shard_map/ppermute | solution.py:500
  139.0 2.1 %collective-permute-start.32 = (f32[4,4,768]{2,1,0:T(4,128)S(1)}, f32[4,4,768]{2,1,0:T(4,128)S(1)}, u32[]{:S(2)}, u32[]{:S(2)}) collective-permute-start(f32[4,4,768]{2,1,0:T(4,128)S(1)} %get-tuple-element.142), channel_id=1, source_target_pairs={{0,4},{1,5},{2,6},{3,7},{4,0},{5,1},{6,2},{7,3},{8,12},{9,13},{10,... | collective-permute-start | bytes 147464 | tf_op jit(solution)/shard_map/ppermute | solution.py:471
  151.2 17.3 %collective-permute-start.35 = (bf16[8,104,768]{2,1,0:T(8,128)(2,1)S(1)}, bf16[8,104,768]{2,1,0:T(8,128)(2,1)S(1)}, u32[]{:S(2)}, u32[]{:S(2)}) collective-permute-start(bf16[8,104,768]{2,1,0:T(8,128)(2,1)S(1)} %bitcast.130), channel_id=1, source_target_pairs={{0,8},{1,9},{2,10},{3,11},{4,20},{5,21},{6,22},{7,23},{8,0},{9,1},... | collective-permute-start | bytes 3833864 | tf_op jit(solution)/shard_map/ppermute | solution.py:500
  153.2 5.2 %copy-start.3 = (bf16[768,768]{1,0:T(8,128)(2,1)S(1)}, bf16[768,768]{1,0:T(8,128)(2,1)}, u32[]{:S(2)}) copy-start(bf16[768,768]{1,0:T(8,128)(2,1)} %copy-done.2) | copy-start | bytes 3538948
  153.3 17.5 %collective-permute-start.38 = (bf16[2,96,768]{2,1,0:T(8,128)(2,1)S(1)}, bf16[2,96,768]{2,1,0:T(8,128)(2,1)S(1)}, u32[]{:S(2)}, u32[]{:S(2)}) collective-permute-start(bf16[2,96,768]{2,1,0:T(8,128)(2,1)S(1)} %pad_maximum_fusion.3), channel_id=1, source_target_pairs={{0,1},{1,0},{2,3},{3,2},{4,5},{5,4},{6,7},{7,6},{8,9},{9,8},{10,11... | collective-permute-start | bytes 884744 | tf_op jit(solution)/shard_map/ppermute | solution.py:500
  155.9 23.5 %collective-permute-start.39 = (bf16[2,96,768]{2,1,0:T(8,128)(2,1)S(1)}, bf16[2,96,768]{2,1,0:T(8,128)(2,1)S(1)}, u32[]{:S(2)}, u32[]{:S(2)}) collective-permute-start(bf16[2,96,768]{2,1,0:T(8,128)(2,1)S(1)} %pad_maximum_fusion.4), channel_id=1, source_target_pairs={{0,2},{1,3},{2,0},{3,1},{4,6},{5,7},{6,4},{7,5},{8,10},{9,11},{10,... | collective-permute-start | bytes 884744 | tf_op jit(solution)/shard_map/ppermute | solution.py:500
  156.7 22.7 %collective-permute-start.40 = (bf16[2,96,768]{2,1,0:T(8,128)(2,1)S(1)}, bf16[2,96,768]{2,1,0:T(8,128)(2,1)S(1)}, u32[]{:S(2)}, u32[]{:S(2)}) collective-permute-start(bf16[2,96,768]{2,1,0:T(8,128)(2,1)S(1)} %pad_maximum_fusion.5), channel_id=1, source_target_pairs={{0,3},{1,2},{2,1},{3,0},{4,7},{5,6},{6,5},{7,4},{8,11},{9,10},{10,... | collective-permute-start | bytes 884744 | tf_op jit(solution)/shard_map/ppermute | solution.py:500
  168.6 12.2 %collective-permute-start.37 = (bf16[1,104,768]{2,1,0:T(8,128)(2,1)S(1)}, bf16[1,104,768]{2,1,0:T(8,128)(2,1)S(1)}, u32[]{:S(2)}, u32[]{:S(2)}) collective-permute-start(bf16[1,104,768]{2,1,0:T(8,128)(2,1)S(1)} %get-tuple-element.150), channel_id=1, source_target_pairs={{0,16},{1,17},{2,18},{3,19},{4,12},{5,13},{6,14},{7,15},{8,24},{9,... | collective-permute-start | bytes 479240 | tf_op jit(solution)/shard_map/ppermute | solution.py:500
  169.0 11.8 %collective-permute-start.44 = (bf16[1,104,768]{2,1,0:T(8,128)(2,1)S(1)}, bf16[1,104,768]{2,1,0:T(8,128)(2,1)S(1)}, u32[]{:S(2)}, u32[]{:S(2)}) collective-permute-start(bf16[1,104,768]{2,1,0:T(8,128)(2,1)S(1)} %get-tuple-element.154), channel_id=1, source_target_pairs={{0,16},{1,17},{2,18},{3,19},{4,12},{5,13},{6,14},{7,15},{8,24},{9,... | collective-permute-start | bytes 479240 | tf_op jit(solution)/shard_map/ppermute | solution.py:500
  170.7 10.1 %collective-permute-start.42 = (bf16[1,104,768]{2,1,0:T(8,128)(2,1)S(1)}, bf16[1,104,768]{2,1,0:T(8,128)(2,1)S(1)}, u32[]{:S(2)}, u32[]{:S(2)}) collective-permute-start(bf16[1,104,768]{2,1,0:T(8,128)(2,1)S(1)} %get-tuple-element.152), channel_id=1, source_target_pairs={{0,16},{1,17},{2,18},{3,19},{4,12},{5,13},{6,14},{7,15},{8,24},{9,... | collective-permute-start | bytes 479240 | tf_op jit(solution)/shard_map/ppermute | solution.py:500
  179.6 11.0 %collective-permute-start.36 = (bf16[1,104,768]{2,1,0:T(8,128)(2,1)S(1)}, bf16[1,104,768]{2,1,0:T(8,128)(2,1)S(1)}, u32[]{:S(2)}, u32[]{:S(2)}) collective-permute-start(bf16[1,104,768]{2,1,0:T(8,128)(2,1)S(1)} %get-tuple-element.149), channel_id=1, source_target_pairs={{0,16},{1,17},{2,18},{3,19},{4,12},{5,13},{6,14},{7,15},{8,24},{9,... | collective-permute-start | bytes 479240 | tf_op jit(solution)/shard_map/ppermute | solution.py:500
  181.0 9.6 %collective-permute-start.45 = (bf16[1,104,768]{2,1,0:T(8,128)(2,1)S(1)}, bf16[1,104,768]{2,1,0:T(8,128)(2,1)S(1)}, u32[]{:S(2)}, u32[]{:S(2)}) collective-permute-start(bf16[1,104,768]{2,1,0:T(8,128)(2,1)S(1)} %get-tuple-element.155), channel_id=1, source_target_pairs={{0,3},{1,2},{2,1},{3,0},{4,7},{5,6},{6,5},{7,4},{8,11},{9,10},{10,... | collective-permute-start | bytes 479240 | tf_op jit(solution)/shard_map/ppermute | solution.py:500
  183.3 15.2 %collective-permute-start.43 = (bf16[1,104,768]{2,1,0:T(8,128)(2,1)S(1)}, bf16[1,104,768]{2,1,0:T(8,128)(2,1)S(1)}, u32[]{:S(2)}, u32[]{:S(2)}) collective-permute-start(bf16[1,104,768]{2,1,0:T(8,128)(2,1)S(1)} %get-tuple-element.153), channel_id=1, source_target_pairs={{0,2},{1,3},{2,0},{3,1},{4,6},{5,7},{6,4},{7,5},{8,10},{9,11},{10,... | collective-permute-start | bytes 479240 | tf_op jit(solution)/shard_map/ppermute | solution.py:500
  189.7 8.7 %collective-permute-start.41 = (bf16[1,104,768]{2,1,0:T(8,128)(2,1)S(1)}, bf16[1,104,768]{2,1,0:T(8,128)(2,1)S(1)}, u32[]{:S(2)}, u32[]{:S(2)}) collective-permute-start(bf16[1,104,768]{2,1,0:T(8,128)(2,1)S(1)} %get-tuple-element.151), channel_id=1, source_target_pairs={{0,1},{1,0},{2,3},{3,2},{4,5},{5,4},{6,7},{7,6},{8,9},{9,8},{10,11... | collective-permute-start | bytes 479240 | tf_op jit(solution)/shard_map/ppermute | solution.py:500
  198.4 3.5 %copy-start.1 = (f32[3,1,8,768]{3,2,1,0:T(8,128)S(1)}, f32[3,1,8,768]{3,2,1,0:T(8,128)}, u32[]{:S(2)}) copy-start(f32[3,1,8,768]{3,2,1,0:T(8,128)} %param.17) | copy-start | bytes 221188
  (7 other events, 14.3 us)

commit v8 on v7

--- a/solution.py
+++ b/solution.py
@@ -108,6 +108,13 @@
 
 def rows_of(refs):
     return jnp.concatenate([r[...].reshape(-1, r.shape[3]) for r in refs], axis=0)
+
+
+def thirds(values):
+    high = values.astype(bf16)
+    rest = values - high.astype(f32)
+    middle = rest.astype(bf16)
+    return high, middle, (rest - middle.astype(f32)).astype(bf16)
 
 
 def accumulate(acc_ref, step, add):
@@ -247,16 +254,12 @@
         grads = []
         for g in range(rows):
             span = slice(g * length, (g + 1) * length)
-            ids = lax.broadcasted_iota(jnp.int32, (segs, length), 0)
-            hot_t = (ids == segr_ref[g : g + 1, :]).astype(f32)
-            idc = lax.broadcasted_iota(jnp.int32, (length, segs), 1)
-            hot = (idc == segc_ref[span, :]).astype(f32)
+            hot_t = (iota((segs, length), 0) == segr_ref[g : g + 1, :]).astype(f32)
             count = jnp.sum(hot_t, axis=1, keepdims=True)
-            sums = lax.dot_general(hot_t, y[span, :], (((1,), (0,)), ((), ())),
-                                   precision=HI, preferred_element_type=f32)
-            pooled_ref[g] = sums / count
-            grads.append(lax.dot_general(hot, pg_ref[g] / count, (((1,), (0,)), ((), ())),
-                                         precision=HI, preferred_element_type=f32))
+            hot_t = hot_t.astype(bf16)
+            hot = (iota((length, segs), 1) == segc_ref[span, :]).astype(f32).astype(bf16)
+            pooled_ref[g] = sum(nn(hot_t, part) for part in thirds(y[span, :])) / count
+            grads.append(nn(jnp.concatenate([hot] * 3, axis=1), jnp.concatenate(thirds(pg_ref[g] / count), axis=0)))
         dy = jnp.concatenate(grads, axis=0)
         db = normalize_back(dy * vec_ref[4:5, :], x2, r2)
         db_ref[...] = db
@@ -394,12 +397,8 @@
     @pl.when(step == pl.num_programs(0) - 1)
     def _():
         dx = acc_ref[...] + da_ref[...]
-        high = dx.astype(bf16)
-        rest = dx - high.astype(f32)
-        mid = rest.astype(bf16)
-        low = (rest - mid.astype(f32)).astype(bf16)
         perm = perm_ref[...]
-        dx_ref[...] = nt(high, perm) + nt(mid, perm) + nt(low, perm)
+        dx_ref[...] = sum(nt(part, perm) for part in thirds(dx))
 
 
 def whole(a):

time: 202 us -> 202 us (level)
  transfers between devices with their start and end apart: 46 -> 46, of which waited for: 16 -> 16; matrix products, arithmetic and copies ran while one was open for 9% -> 9% of each run, Pallas kernels for 30% -> 29%
where the time goes in v8:
time: 202 us; the launch traced here: 201 us
  waiting for transfers between devices  67.8 us (34%)
  Pallas kernels  61.2 us (30%)
  starting transfers between devices  48.9 us (24%)
  local copies, waits for them, and re-layouts  12.5 us (6%)
  other arithmetic  6.74 us (3%)
  matrix products  2.99 us (1%)
    pallas_call x11, Pallas kernels, call(): pl.pallas_call(body, grid=(n_t,), in_specs=[s for _, s in ins], out_specs...  57.8 us
    ppermute x21, waiting for transfers between devices, send(): lax.ppermute(after(h, *done), AXES, t)  35.8 us
    ppermute x15, waiting for transfers between devices, stage(): lax.ppermute(after(s, *done), AXES, tables[n // pieces])  30.2 us
    ppermute x21, starting transfers between devices, send(): lax.ppermute(after(h, *done), AXES, t)  25.2 us
    ppermute x15, starting transfers between devices, stage(): lax.ppermute(after(s, *done), AXES, tables[n // pieces])  22.1 us
    unnamed x64, local copies, waits for them, and re-layouts  7.04 us
  transfers between devices with their start and end apart: 46, of which 16 were waited for; matrix products, arithmetic and copies ran while one was open for 9% of the time, Pallas kernels for 29%

profile of v8, /device:TPU:0, one launch (start us, length us, event | category | flops | bytes accessed | tf_op | source)
XLA Modules:
  0.0 201.3 jit_solution(7725224068357012801)
XLA Ops:
  0.7 2.0 shard_map.255
  2.6 5.0 %collective-permute-start.2 = (bf16[1,104,768]{2,1,0:T(8,128)(2,1)}, bf16[1,104,768]{2,1,0:T(8,128)(2,1)S(1)}, u32[]{:S(2)}, u32[]{:S(2)}) collective-permute-start(bf16[1,104,768]{2,1,0:T(8,128)(2,1)} %bitcast.134), channel_id=1, source_target_pairs={{0,3},{1,2},{2,1},{3,0},{4,7},{5,6},{6,5},{7,4},{8,11},{9,10},{10,... | collective-permute-start | bytes 479240 | tf_op jit(solution)/shard_map/ppermute | solution.py:479
  8.2 1.7 collective-permute-start.3
  10.5 0.7 copy.57
  12.5 1.0 convolution_bitcast_fusion.pg_ref
  13.6 1.4 shard_map.254
  15.0 6.5 %collective-permute-done.1 = bf16[1,104,768]{2,1,0:T(8,128)(2,1)} collective-permute-done((bf16[1,104,768]{2,1,0:T(8,128)(2,1)}, bf16[1,104,768]{2,1,0:T(8,128)(2,1)}, u32[]{:S(2)}, u32[]{:S(2)}) %collective-permute-start.1) | collective-permute-done | bytes 159776 | tf_op jit(solution)/shard_map/ppermute | solution.py:479
  21.5 1.1 pad_maximum_fusion
  22.6 1.6 collective-permute-start.4
  24.3 3.0 %collective-permute-start.6 = (bf16[1,96,768]{2,1,0:T(8,128)(2,1)S(1)}, bf16[1,96,768]{2,1,0:T(8,128)(2,1)S(1)}, u32[]{:S(2)}, u32[]{:S(2)}) collective-permute-start(bf16[1,96,768]{2,1,0:T(8,128)(2,1)S(1)} %bitcast.142), channel_id=1, source_target_pairs={{0,2},{1,3},{2,0},{3,1},{4,6},{5,7},{6,4},{7,5},{8,10},{9,11},{10,... | collective-permute-start | bytes 442376 | tf_op jit(solution)/shard_map/ppermute | solution.py:479
  27.3 1.3 collective-permute-start.7
  28.7 0.9 constant_dynamic-update-slice_fusion.3
  29.6 0.9 constant_dynamic-update-slice_fusion.2
  30.6 2.5 %collective-permute-done.4 = bf16[4,104,768]{2,1,0:T(8,128)(2,1)S(1)} collective-permute-done((bf16[4,104,768]{2,1,0:T(8,128)(2,1)S(1)}, bf16[4,104,768]{2,1,0:T(8,128)(2,1)S(1)}, u32[]{:S(2)}, u32[]{:S(2)}) %collective-permute-start.4) | collective-permute-done | bytes 639008 | tf_op jit(solution)/shard_map/ppermute | solution.py:479
  33.1 4.5 %collective-permute-done.6 = bf16[1,96,768]{2,1,0:T(8,128)(2,1)S(1)} collective-permute-done((bf16[1,96,768]{2,1,0:T(8,128)(2,1)S(1)}, bf16[1,96,768]{2,1,0:T(8,128)(2,1)S(1)}, u32[]{:S(2)}, u32[]{:S(2)}) %collective-permute-start.6) | collective-permute-done | bytes 147488 | tf_op jit(solution)/shard_map/ppermute | solution.py:479
  37.6 0.7 collective-permute-start.9
  38.4 1.4 collective-permute-start.10
  39.9 0.7 constant_dynamic-update-slice_fusion.9
  40.5 1.7 pad_maximum_fusion.2
  42.2 2.3 %collective-permute-start.11 = (bf16[2,96,768]{2,1,0:T(8,128)(2,1)}, bf16[2,96,768]{2,1,0:T(8,128)(2,1)S(1)}, u32[]{:S(2)}, u32[]{:S(2)}) collective-permute-start(bf16[2,96,768]{2,1,0:T(8,128)(2,1)} %pad_maximum_fusion.2), channel_id=1, source_target_pairs={{0,1},{1,0},{2,3},{3,2},{4,5},{5,4},{6,7},{7,6},{8,9},{9,8},{10,11... | collective-permute-start | bytes 884744 | tf_op jit(solution)/shard_map/ppermute | solution.py:479
  44.5 0.8 collective-permute-start.12
  45.3 0.7 constant_dynamic-update-slice_fusion.8
  46.0 0.7 constant_dynamic-update-slice_fusion.7
  47.3 8.6 %collective-permute-done.11 = bf16[2,96,768]{2,1,0:T(8,128)(2,1)S(1)} collective-permute-done((bf16[2,96,768]{2,1,0:T(8,128)(2,1)}, bf16[2,96,768]{2,1,0:T(8,128)(2,1)S(1)}, u32[]{:S(2)}, u32[]{:S(2)}) %collective-permute-start.11) | collective-permute-done | bytes 294944 | tf_op jit(solution)/shard_map/ppermute | solution.py:479
  56.0 2.8 %collective-permute-done.12 = bf16[2,96,768]{2,1,0:T(8,128)(2,1)S(1)} collective-permute-done((bf16[2,96,768]{2,1,0:T(8,128)(2,1)}, bf16[2,96,768]{2,1,0:T(8,128)(2,1)S(1)}, u32[]{:S(2)}, u32[]{:S(2)}) %collective-permute-start.12) | collective-permute-done | bytes 294944 | tf_op jit(solution)/shard_map/ppermute | solution.py:479
  59.5 0.9 constant_dynamic-update-slice_fusion.5
  60.3 1.7 collective-permute-start.15
  62.1 2.2 %collective-permute-start.16 = (bf16[2,96,768]{2,1,0:T(8,128)(2,1)}, bf16[2,96,768]{2,1,0:T(8,128)(2,1)}, u32[]{:S(2)}, u32[]{:S(2)}) collective-permute-start(bf16[2,96,768]{2,1,0:T(8,128)(2,1)} %pad_maximum_fusion.2), channel_id=1, source_target_pairs={{0,3},{1,2},{2,1},{3,0},{4,7},{5,6},{6,5},{7,4},{8,11},{9,10},{10,... | collective-permute-start | bytes 884744 | tf_op jit(solution)/shard_map/ppermute | solution.py:479
  64.5 11.7 %shard_map.256 = (bf16[4,384,576]{2,1,0:T(8,128)(2,1)}, f32[4,3,128,384]{3,2,1,0:T(8,128)}, bf16[4,384,256]{2,1,0:T(8,128)(2,1)}, f32[384,768]{1,0:T(8,128)S(1)}...) custom-call(bf16[384,768]{1,0:T(8,128)(2,1)S(1)} %get-tuple-element., ...), custom_call_target="tpu_custom_call" | custom-call | flops 300000000 | tf_op jit(solution)/shard_map/pallas_call | solution.py:435
  77.4 1.0 constant_dynamic-update-slice_fusion.13
  78.4 1.0 constant_dynamic-update-slice_fusion.10
  79.4 1.8 collective-permute-start.21
  81.2 1.7 collective-permute-done.19.refs_2_
  83.0 4.9 %shard_map.257 = (bf16[4,384,768]{2,1,0:T(8,128)(2,1)S(1)}, f32[4,384,768]{2,1,0:T(8,128)S(1)}) custom-call(bf16[384,768]{1,0:T(8,128)(2,1)S(1)} %get-tuple-element.97.n_ref, bf16[2,4,96,768]{3,2,1,0:T(8,128)(2,1)} %bitcast.23.w0_ref, bf16[2,4,96,768]{3,2,1,0:T(8,128)(2,1)} %bitcast.24.w1_ref, bf16[2,4,96,768]{3,2,1,0:T(8,128)(2,1)S(1)} %bitcast.123, ...), custom_call_target="tpu_custom_call" | custom-call | flops 120000000 | tf_op jit(solution)/shard_map/pallas_call | solution.py:435
  88.4 7.3 %collective-permute-done.21 = bf16[8,96,768]{2,1,0:T(8,128)(2,1)S(1)} collective-permute-done((bf16[8,96,768]{2,1,0:T(8,128)(2,1)S(1)}, bf16[8,96,768]{2,1,0:T(8,128)(2,1)S(1)}, u32[]{:S(2)}, u32[]{:S(2)}) %collective-permute-start.21) | collective-permute-done | bytes 1179680 | tf_op jit(solution)/shard_map/ppermute | solution.py:479
  95.7 2.8 %collective-permute-done.23 = bf16[8,96,768]{2,1,0:T(8,128)(2,1)S(1)} collective-permute-done((bf16[8,96,768]{2,1,0:T(8,128)(2,1)S(1)}, bf16[8,96,768]{2,1,0:T(8,128)(2,1)S(1)}, u32[]{:S(2)}, u32[]{:S(2)}) %collective-permute-start.23) | collective-permute-done | bytes 1179680 | tf_op jit(solution)/shard_map/ppermute | solution.py:479
  98.5 4.7 %shard_map.258 = (f32[3,8,768]{2,1,0:T(8,128)S(1)}, f32[384,768]{1,0:T(8,128)S(1)}, bf16[384,768]{1,0:T(8,128)(2,1)S(1)}, bf16[384,384]{1,0:T(8,128)(2,1)S(1)}, ...) custom-call(bf16[4,384,768]{2,1,0:T(8,128)(2,1)S(1)} %get-tuple-element.107.z_ref.refs_1_, ...), custom_call_target="tpu_custom_call" | custom-call | flops 165000000 | tf_op jit(solution)/shard_map/pallas_call | solution.py:435
  103.4 2.7 %shard_map.259 = (bf16[4,384,768]{2,1,0:T(8,128)(2,1)S(1)}, f32[4,1,768]{2,1,0:T(1,128)S(1)}) custom-call(bf16[384,768]{1,0:T(8,128)(2,1)S(1)} %get-tuple-element.114.dbb_ref, bf16[4,2,96,768]{3,2,1,0:T(8,128)(2,1)S(1)} %bitcast.112, bf16[4,2,96,768]{3,2,1,0:T(8,128)(2,1)S(1)} %bitcast.114, bf16[4,2,96,768]{3,2,1,0:T(8,128)(2,1)S(1)} %bitcast.116, ...), custom_call_target="tpu_custom_call" | custom-call | flops 105000000 | tf_op jit(solution)/shard_map/pallas_call | solution.py:435
  106.6 1.9 shard_map.260
  108.5 1.8 collective-permute-start.28
  110.3 5.5 %shard_map.261 = (f32[384,768]{1,0:T(8,128)S(1)}, bf16[384,768]{1,0:T(8,128)(2,1)S(1)}, bf16[384,384]{1,0:T(8,128)(2,1)S(1)}, bf16[384,384]{1,0:T(8,128)(2,1)S(1)}, f32[3,768]{1,0:T(4,128)S(1)}) custom-call(bf16[4,384,768]{2,1,0:T(8,128)(2,1)S(1)} %get-tuple-element.121.du_ref.refs_1_, bf16[2,4,96,768]{3,2,1,0:T(8,128)(2,1)} %bitcast.23.w0_ref, ...), custom_call_target="tpu_custom_call" | custom-call | flops 60000002048 | tf_op jit(solution)/shard_map/pallas_call | solution.py:435
  115.8 3.3 %shard_map.262 = (bf16[2,4,96,768]{3,2,1,0:T(8,128)(2,1)S(1)}, bf16[2,4,96,768]{3,2,1,0:T(8,128)(2,1)S(1)}) custom-call(bf16[384,384]{1,0:T(8,128)(2,1)S(1)} %copy-done.10, bf16[4,384,768]{2,1,0:T(8,128)(2,1)S(1)} %get-tuple-element.121.du_ref.refs_1_, bf16[384,384]{1,0:T(8,128)(2,1)S(1)} %collective-permute-done.19.refs_2_, ...), custom_call_target="tpu_custom_call" | custom-call | flops 60000000 | tf_op jit(solution)/shard_map/pallas_call | solution.py:435
  119.5 1.9 shard_map.263
  121.4 3.3 %collective-permute-done.28 = bf16[8,96,768]{2,1,0:T(8,128)(2,1)S(1)} collective-permute-done((bf16[8,96,768]{2,1,0:T(8,128)(2,1)S(1)}, bf16[8,96,768]{2,1,0:T(8,128)(2,1)S(1)}, u32[]{:S(2)}, u32[]{:S(2)}) %collective-permute-start.28) | collective-permute-done | bytes 1179680 | tf_op jit(solution)/shard_map/ppermute | solution.py:499
  124.8 8.7 %shard_map.264 = (bf16[2,384,640]{2,1,0:T(8,128)(2,1)S(1)}, bf16[2,384,640]{2,1,0:T(8,128)(2,1)S(1)}, f32[4,4,768]{2,1,0:T(4,128)S(1)}, f32[4,4,768]{2,1,0:T(4,128)S(1)}) custom-call(bf16[384,768]{1,0:T(8,128)(2,1)S(1)} %get-tuple-element.132.dab_ref, bf16[2,4,104,768]{3,2,1,0:T(8,128)(2,1)S(1)} %bitcast.105, bf16[2,4,104,768]{3,2,1,0:T(8,128)(2,1)S(1)} %bitcast.109, ...), custom_call_target="tpu_custom_call" | custom-call | flops 240000000 | tf_op jit(solution)/shard_map/pallas_call | solution.py:435
  134.7 3.0 %collective-permute-done.29 = bf16[8,96,768]{2,1,0:T(8,128)(2,1)S(1)} collective-permute-done((bf16[8,96,768]{2,1,0:T(8,128)(2,1)S(1)}, bf16[8,96,768]{2,1,0:T(8,128)(2,1)S(1)}, u32[]{:S(2)}, u32[]{:S(2)}) %collective-permute-start.29) | collective-permute-done | bytes 1179680 | tf_op jit(solution)/shard_map/ppermute | solution.py:499
  138.5 2.0 fusion
  140.5 5.3 %shard_map.265 = (bf16[2,4,104,768]{3,2,1,0:T(8,128)(2,1)S(1)}, bf16[2,4,104,768]{3,2,1,0:T(8,128)(2,1)S(1)}) custom-call(bf16[384,384]{1,0:T(8,128)(2,1)S(1)} %copy-done.9, bf16[2,384,640]{2,1,0:T(8,128)(2,1)S(1)} %get-tuple-element.144.refs_1_.low_ref, bf16[2,384,640]{2,1,0:T(8,128)(2,1)S(1)} %get-tuple-element.145.refs_2_.high_ref, ...), custom_call_target="tpu_custom_call" | custom-call | flops 60000000 | tf_op jit(solution)/shard_map/pallas_call | solution.py:435
  145.8 4.8 %collective-permute-done.34 = bf16[4,96,768]{2,1,0:T(8,128)(2,1)S(1)} collective-permute-done((bf16[4,96,768]{2,1,0:T(8,128)(2,1)S(1)}, bf16[4,96,768]{2,1,0:T(8,128)(2,1)S(1)}, u32[]{:S(2)}, u32[]{:S(2)}) %collective-permute-start.34) | collective-permute-done | bytes 589856 | tf_op jit(solution)/shard_map/ppermute | solution.py:499
  150.6 1.7 collective-permute-start.35
  152.6 2.6 %collective-permute-start.38 = (bf16[2,96,768]{2,1,0:T(8,128)(2,1)S(1)}, bf16[2,96,768]{2,1,0:T(8,128)(2,1)S(1)}, u32[]{:S(2)}, u32[]{:S(2)}) collective-permute-start(bf16[2,96,768]{2,1,0:T(8,128)(2,1)S(1)} %pad_maximum_fusion.3), channel_id=1, source_target_pairs={{0,1},{1,0},{2,3},{3,2},{4,5},{5,4},{6,7},{7,6},{8,9},{9,8},{10,11... | collective-permute-start | bytes 884744 | tf_op jit(solution)/shard_map/ppermute | solution.py:499
  155.3 0.8 collective-permute-start.39
  156.1 1.7 collective-permute-start.40
  157.8 7.3 %shard_map.266 = f32[384,768]{1,0:T(8,128)} custom-call(bf16[2,384,640]{2,1,0:T(8,128)(2,1)S(1)} %get-tuple-element.144.refs_1_.low_ref, bf16[2,384,640]{2,1,0:T(8,128)(2,1)S(1)} %get-tuple-element.145.refs_2_.high_ref, bf16[2,4,104,768]{3,2,1,0:T(8,128)(2,1)S(1)} %bitcast.106, bf16[2,4,104,768]{3,2,1,0:T(8,128)(2,1)S(1)} %bitcast.110, ...), custom_call_target="tpu_custom_call" | custom-call | flops 120000000 | tf_op jit(solution)/shard_map/pallas_call | solution.py:435
  165.1 2.8 %collective-permute-done.35 = bf16[8,104,768]{2,1,0:T(8,128)(2,1)S(1)} collective-permute-done((bf16[8,104,768]{2,1,0:T(8,128)(2,1)S(1)}, bf16[8,104,768]{2,1,0:T(8,128)(2,1)S(1)}, u32[]{:S(2)}, u32[]{:S(2)}) %collective-permute-start.35) | collective-permute-done | bytes 1277984 | tf_op jit(solution)/shard_map/ppermute | solution.py:499
  168.4 1.7 collective-permute-start.44
  170.4 8.4 %collective-permute-done.39 = bf16[2,96,768]{2,1,0:T(8,128)(2,1)S(1)} collective-permute-done((bf16[2,96,768]{2,1,0:T(8,128)(2,1)S(1)}, bf16[2,96,768]{2,1,0:T(8,128)(2,1)S(1)}, u32[]{:S(2)}, u32[]{:S(2)}) %collective-permute-start.39) | collective-permute-done | bytes 294944 | tf_op jit(solution)/shard_map/ppermute | solution.py:499
  179.0 1.2 collective-permute-start.36
  180.4 2.3 %collective-permute-start.45 = (bf16[1,104,768]{2,1,0:T(8,128)(2,1)S(1)}, bf16[1,104,768]{2,1,0:T(8,128)(2,1)S(1)}, u32[]{:S(2)}, u32[]{:S(2)}) collective-permute-start(bf16[1,104,768]{2,1,0:T(8,128)(2,1)S(1)} %get-tuple-element.155), channel_id=1, source_target_pairs={{0,3},{1,2},{2,1},{3,0},{4,7},{5,6},{6,5},{7,4},{8,11},{9,10},{10,... | collective-permute-start | bytes 479240 | tf_op jit(solution)/shard_map/ppermute | solution.py:499
  182.7 6.5 %collective-permute-start.43 = (bf16[1,104,768]{2,1,0:T(8,128)(2,1)S(1)}, bf16[1,104,768]{2,1,0:T(8,128)(2,1)S(1)}, u32[]{:S(2)}, u32[]{:S(2)}) collective-permute-start(bf16[1,104,768]{2,1,0:T(8,128)(2,1)S(1)} %get-tuple-element.153), channel_id=1, source_target_pairs={{0,2},{1,3},{2,0},{3,1},{4,6},{5,7},{6,4},{7,5},{8,10},{9,11},{10,... | collective-permute-start | bytes 479240 | tf_op jit(solution)/shard_map/ppermute | solution.py:499
  189.1 0.8 slice_bitcast_fusion.2
  190.0 7.8 %collective-permute-done.43 = bf16[1,104,768]{2,1,0:T(8,128)(2,1)S(1)} collective-permute-done((bf16[1,104,768]{2,1,0:T(8,128)(2,1)S(1)}, bf16[1,104,768]{2,1,0:T(8,128)(2,1)S(1)}, u32[]{:S(2)}, u32[]{:S(2)}) %collective-permute-start.43) | collective-permute-done | bytes 159776 | tf_op jit(solution)/shard_map/ppermute | solution.py:499
  199.3 0.7 copy.62
  200.6 0.7 pad_maximum_fusion.6
  (151 shorter events, 12.6 us)
Async XLA Ops:
  0.6 11.8 %copy-start = (f32[3,1,8,768]{3,2,1,0:T(8,128)S(1)}, f32[3,1,8,768]{3,2,1,0:T(8,128)}, u32[]{:S(2)}) copy-start(f32[3,1,8,768]{3,2,1,0:T(8,128)} %param.17) | copy-start | bytes 221188
  2.6 12.4 %collective-permute-start.2 = (bf16[1,104,768]{2,1,0:T(8,128)(2,1)}, bf16[1,104,768]{2,1,0:T(8,128)(2,1)S(1)}, u32[]{:S(2)}, u32[]{:S(2)}) collective-permute-start(bf16[1,104,768]{2,1,0:T(8,128)(2,1)} %bitcast.134), channel_id=1, source_target_pairs={{0,3},{1,2},{2,1},{3,0},{4,7},{5,6},{6,5},{7,4},{8,11},{9,10},{10,... | collective-permute-start | bytes 479240 | tf_op jit(solution)/shard_map/ppermute | solution.py:479
  7.7 13.8 %collective-permute-start.1 = (bf16[1,104,768]{2,1,0:T(8,128)(2,1)}, bf16[1,104,768]{2,1,0:T(8,128)(2,1)}, u32[]{:S(2)}, u32[]{:S(2)}) collective-permute-start(bf16[1,104,768]{2,1,0:T(8,128)(2,1)} %bitcast.135), channel_id=1, source_target_pairs={{0,2},{1,3},{2,0},{3,1},{4,6},{5,7},{6,4},{7,5},{8,10},{9,11},{10,... | collective-permute-start | bytes 479240 | tf_op jit(solution)/shard_map/ppermute | solution.py:479
  7.7 13.8 %collective-permute-start = (bf16[1,104,768]{2,1,0:T(8,128)(2,1)}, bf16[1,104,768]{2,1,0:T(8,128)(2,1)}, u32[]{:S(2)}, u32[]{:S(2)}) collective-permute-start(bf16[1,104,768]{2,1,0:T(8,128)(2,1)} %bitcast.136), channel_id=1, source_target_pairs={{0,1},{1,0},{2,3},{3,2},{4,5},{5,4},{6,7},{7,6},{8,9},{9,8},{10,11... | collective-permute-start | bytes 479240 | tf_op jit(solution)/shard_map/ppermute | solution.py:479
  8.2 14.4 %collective-permute-start.3 = (bf16[1,96,768]{2,1,0:T(8,128)(2,1)}, bf16[1,96,768]{2,1,0:T(8,128)(2,1)}, u32[]{:S(2)}, u32[]{:S(2)}) collective-permute-start(bf16[1,96,768]{2,1,0:T(8,128)(2,1)} %bitcast.145), channel_id=1, source_target_pairs={{0,16},{1,17},{2,18},{3,19},{4,12},{5,13},{6,14},{7,15},{8,24},{9,... | collective-permute-start | bytes 442376 | tf_op jit(solution)/shard_map/ppermute | solution.py:479
  11.7 3.4 %copy-start.2 = (bf16[768,768]{1,0:T(8,128)(2,1)}, bf16[768,768]{1,0:T(8,128)(2,1)S(1)}, u32[]{:S(2)}) copy-start(bf16[768,768]{1,0:T(8,128)(2,1)S(1)} %fusion.2.perm_ref) | copy-start | bytes 3538948
  12.5 9.0 %copy-start.15 = (bf16[104,768]{1,0:T(8,128)(2,1)S(1)}, bf16[104,768]{1,0:T(8,128)(2,1)}, u32[]{:S(2)}) copy-start(bf16[104,768]{1,0:T(8,128)(2,1)} %shard_map.255) | copy-start | bytes 479236
  15.0 15.5 %copy-start.8 = (bf16[384,384]{1,0:T(8,128)(2,1)}, bf16[384,384]{1,0:T(8,128)(2,1)S(1)}, u32[]{:S(2)}) copy-start(bf16[384,384]{1,0:T(8,128)(2,1)S(1)} %get-tuple-element.139.refs_0_) | copy-start | bytes 884740
  15.0 9.2 %copy-start.16 = (bf16[96,768]{1,0:T(8,128)(2,1)S(1)}, bf16[96,768]{1,0:T(8,128)(2,1)}, u32[]{:S(2)}) copy-start(bf16[96,768]{1,0:T(8,128)(2,1)} %param.24) | copy-start | bytes 442372
  22.6 10.5 %collective-permute-start.4 = (bf16[4,104,768]{2,1,0:T(8,128)(2,1)S(1)}, bf16[4,104,768]{2,1,0:T(8,128)(2,1)S(1)}, u32[]{:S(2)}, u32[]{:S(2)}) collective-permute-start(bf16[4,104,768]{2,1,0:T(8,128)(2,1)S(1)} %pad_maximum_fusion), channel_id=1, source_target_pairs={{0,16},{1,17},{2,18},{3,19},{4,12},{5,13},{6,14},{7,15},{8,24},{9,... | collective-permute-start | bytes 1916936 | tf_op jit(solution)/shard_map/ppermute | solution.py:479
  24.2 8.9 %collective-permute-start.5 = (bf16[1,96,768]{2,1,0:T(8,128)(2,1)S(1)}, bf16[1,96,768]{2,1,0:T(8,128)(2,1)S(1)}, u32[]{:S(2)}, u32[]{:S(2)}) collective-permute-start(bf16[1,96,768]{2,1,0:T(8,128)(2,1)S(1)} %bitcast.141), channel_id=1, source_target_pairs={{0,1},{1,0},{2,3},{3,2},{4,5},{5,4},{6,7},{7,6},{8,9},{9,8},{10,11... | collective-permute-start | bytes 442376 | tf_op jit(solution)/shard_map/ppermute | solution.py:479
  24.3 13.3 %collective-permute-start.6 = (bf16[1,96,768]{2,1,0:T(8,128)(2,1)S(1)}, bf16[1,96,768]{2,1,0:T(8,128)(2,1)S(1)}, u32[]{:S(2)}, u32[]{:S(2)}) collective-permute-start(bf16[1,96,768]{2,1,0:T(8,128)(2,1)S(1)} %bitcast.142), channel_id=1, source_target_pairs={{0,2},{1,3},{2,0},{3,1},{4,6},{5,7},{6,4},{7,5},{8,10},{9,11},{10,... | collective-permute-start | bytes 442376 | tf_op jit(solution)/shard_map/ppermute | solution.py:479
  27.3 10.3 %collective-permute-start.7 = (bf16[1,96,768]{2,1,0:T(8,128)(2,1)S(1)}, bf16[1,96,768]{2,1,0:T(8,128)(2,1)S(1)}, u32[]{:S(2)}, u32[]{:S(2)}) collective-permute-start(bf16[1,96,768]{2,1,0:T(8,128)(2,1)S(1)} %bitcast.143), channel_id=1, source_target_pairs={{0,3},{1,2},{2,1},{3,0},{4,7},{5,6},{6,5},{7,4},{8,11},{9,10},{10,... | collective-permute-start | bytes 442376 | tf_op jit(solution)/shard_map/ppermute | solution.py:479
  30.6 10.0 %copy-start.17 = (bf16[768,96]{0,1:T(8,128)(2,1)S(1)}, bf16[768,96]{0,1:T(8,128)(2,1)}, u32[]{:S(2)}) copy-start(bf16[768,96]{0,1:T(8,128)(2,1)} %param.26) | copy-start | bytes 442372
  37.6 21.2 %collective-permute-start.9 = (bf16[8,104,768]{2,1,0:T(8,128)(2,1)S(1)}, bf16[8,104,768]{2,1,0:T(8,128)(2,1)S(1)}, u32[]{:S(2)}, u32[]{:S(2)}) collective-permute-start(bf16[8,104,768]{2,1,0:T(8,128)(2,1)S(1)} %constant_dynamic-update-slice_fusion), channel_id=1, source_target_pairs={{0,8},{1,9},{2,10},{3,11},{4,20},{5,21},{6,22},{7,23},{8,0},{9,1},... | collective-permute-start | bytes 3833864 | tf_op jit(solution)/shard_map/ppermute | solution.py:479
  38.4 20.4 %collective-permute-start.10 = (bf16[4,96,768]{2,1,0:T(8,128)(2,1)S(1)}, bf16[4,96,768]{2,1,0:T(8,128)(2,1)S(1)}, u32[]{:S(2)}, u32[]{:S(2)}) collective-permute-start(bf16[4,96,768]{2,1,0:T(8,128)(2,1)S(1)} %pad_maximum_fusion.1), channel_id=1, source_target_pairs={{0,16},{1,17},{2,18},{3,19},{4,12},{5,13},{6,14},{7,15},{8,24},{9,... | collective-permute-start | bytes 1769480 | tf_op jit(solution)/shard_map/ppermute | solution.py:479
  42.2 22.1 %copy-start.23 = (s32[3,1,128]{2,1,0:T(1,128)S(1)}, s32[3,1,128]{2,1,0:T(1,128)}, u32[]{:S(2)}) copy-start(s32[3,1,128]{2,1,0:T(1,128)} %param.16) | copy-start | bytes 4612
  42.2 13.8 %collective-permute-start.11 = (bf16[2,96,768]{2,1,0:T(8,128)(2,1)}, bf16[2,96,768]{2,1,0:T(8,128)(2,1)S(1)}, u32[]{:S(2)}, u32[]{:S(2)}) collective-permute-start(bf16[2,96,768]{2,1,0:T(8,128)(2,1)} %pad_maximum_fusion.2), channel_id=1, source_target_pairs={{0,1},{1,0},{2,3},{3,2},{4,5},{5,4},{6,7},{7,6},{8,9},{9,8},{10,11... | collective-permute-start | bytes 884744 | tf_op jit(solution)/shard_map/ppermute | solution.py:479
  44.5 14.3 %collective-permute-start.12 = (bf16[2,96,768]{2,1,0:T(8,128)(2,1)}, bf16[2,96,768]{2,1,0:T(8,128)(2,1)S(1)}, u32[]{:S(2)}, u32[]{:S(2)}) collective-permute-start(bf16[2,96,768]{2,1,0:T(8,128)(2,1)} %pad_maximum_fusion.2), channel_id=1, source_target_pairs={{0,2},{1,3},{2,0},{3,1},{4,6},{5,7},{6,4},{7,5},{8,10},{9,11},{10,... | collective-permute-start | bytes 884744 | tf_op jit(solution)/shard_map/ppermute | solution.py:479
  58.9 5.6 %collective-permute-start.13 = (bf16[8,104,768]{2,1,0:T(8,128)(2,1)S(1)}, bf16[8,104,768]{2,1,0:T(8,128)(2,1)}, u32[]{:S(2)}, u32[]{:S(2)}) collective-permute-start(bf16[8,104,768]{2,1,0:T(8,128)(2,1)S(1)} %constant_dynamic-update-slice_fusion), channel_id=1, source_target_pairs={{0,4},{1,5},{2,6},{3,7},{4,0},{5,1},{6,2},{7,3},{8,12},{9,13},{10,... | collective-permute-start | bytes 3833864 | tf_op jit(solution)/shard_map/ppermute | solution.py:479
  59.5 5.0 %collective-permute-start.14 = (bf16[8,104,768]{2,1,0:T(8,128)(2,1)S(1)}, bf16[8,104,768]{2,1,0:T(8,128)(2,1)}, u32[]{:S(2)}, u32[]{:S(2)}) collective-permute-start(bf16[8,104,768]{2,1,0:T(8,128)(2,1)S(1)} %collective-permute-done.9), channel_id=1, source_target_pairs={{0,4},{1,5},{2,6},{3,7},{4,0},{5,1},{6,2},{7,3},{8,12},{9,13},{10,... | collective-permute-start | bytes 3833864 | tf_op jit(solution)/shard_map/ppermute | solution.py:479
  60.3 16.5 %collective-permute-start.15 = (bf16[8,96,768]{2,1,0:T(8,128)(2,1)}, bf16[8,96,768]{2,1,0:T(8,128)(2,1)}, u32[]{:S(2)}, u32[]{:S(2)}) collective-permute-start(bf16[8,96,768]{2,1,0:T(8,128)(2,1)} %constant_dynamic-update-slice_fusion.5), channel_id=1, source_target_pairs={{0,8},{1,9},{2,10},{3,11},{4,20},{5,21},{6,22},{7,23},{8,0},{9,1},... | collective-permute-start | bytes 3538952 | tf_op jit(solution)/shard_map/ppermute | solution.py:479
  62.1 2.4 %collective-permute-start.8 = (bf16[384,384]{1,0:T(8,128)(2,1)}, bf16[384,384]{1,0:T(8,128)(2,1)}, u32[]{:S(2)}, u32[]{:S(2)}) collective-permute-start(bf16[384,384]{1,0:T(8,128)(2,1)} %get-tuple-element.90), channel_id=1, source_target_pairs={{0,4},{1,5},{2,6},{3,7},{4,0},{5,1},{6,2},{7,3},{8,12},{9,13},{10,... | collective-permute-start | bytes 884744 | tf_op jit(solution)/shard_map/ppermute | solution.py:470
  62.1 14.8 %collective-permute-start.16 = (bf16[2,96,768]{2,1,0:T(8,128)(2,1)}, bf16[2,96,768]{2,1,0:T(8,128)(2,1)}, u32[]{:S(2)}, u32[]{:S(2)}) collective-permute-start(bf16[2,96,768]{2,1,0:T(8,128)(2,1)} %pad_maximum_fusion.2), channel_id=1, source_target_pairs={{0,3},{1,2},{2,1},{3,0},{4,7},{5,6},{6,5},{7,4},{8,11},{9,10},{10,... | collective-permute-start | bytes 884744 | tf_op jit(solution)/shard_map/ppermute | solution.py:479
  64.5 12.9 %copy-start.18 = (bf16[768,96]{0,1:T(8,128)(2,1)S(1)}, bf16[768,96]{0,1:T(8,128)(2,1)}, u32[]{:S(2)}) copy-start(bf16[768,96]{0,1:T(8,128)(2,1)} %param.26) | copy-start | bytes 442372
  64.5 13.9 %copy-start.20 = (bf16[2,96,768]{2,1,0:T(8,128)(2,1)S(1)}, bf16[2,96,768]{2,1,0:T(8,128)(2,1)}, u32[]{:S(2)}) copy-start(bf16[2,96,768]{2,1,0:T(8,128)(2,1)} %copy-done.19) | copy-start | bytes 884740
  76.9 6.1 %collective-permute-start.17 = (bf16[8,96,768]{2,1,0:T(8,128)(2,1)}, bf16[8,96,768]{2,1,0:T(8,128)(2,1)S(1)}, u32[]{:S(2)}, u32[]{:S(2)}) collective-permute-start(bf16[8,96,768]{2,1,0:T(8,128)(2,1)} %constant_dynamic-update-slice_fusion.5), channel_id=1, source_target_pairs={{0,4},{1,5},{2,6},{3,7},{4,0},{5,1},{6,2},{7,3},{8,12},{9,13},{10,... | collective-permute-start | bytes 3538952 | tf_op jit(solution)/shard_map/ppermute | solution.py:479
  76.9 6.1 %collective-permute-start.18 = (bf16[8,96,768]{2,1,0:T(8,128)(2,1)}, bf16[8,96,768]{2,1,0:T(8,128)(2,1)S(1)}, u32[]{:S(2)}, u32[]{:S(2)}) collective-permute-start(bf16[8,96,768]{2,1,0:T(8,128)(2,1)} %collective-permute-done.15), channel_id=1, source_target_pairs={{0,4},{1,5},{2,6},{3,7},{4,0},{5,1},{6,2},{7,3},{8,12},{9,13},{10,... | collective-permute-start | bytes 3538952 | tf_op jit(solution)/shard_map/ppermute | solution.py:479
  77.4 3.9 %copy-start.24 = (bf16[384,384]{1,0:T(8,128)(2,1)S(1)}, bf16[384,384]{1,0:T(8,128)(2,1)}, u32[]{:S(2)}) copy-start(bf16[384,384]{1,0:T(8,128)(2,1)} %get-tuple-element.104) | copy-start | bytes 884740
  77.4 5.6 %collective-permute-start.20 = (bf16[4,384,256]{2,1,0:T(8,128)(2,1)}, bf16[4,384,256]{2,1,0:T(8,128)(2,1)S(1)}, u32[]{:S(2)}, u32[]{:S(2)}) collective-permute-start(bf16[4,384,256]{2,1,0:T(8,128)(2,1)} %get-tuple-element.105.refs_7_), channel_id=1, source_target_pairs={{0,4},{1,5},{2,6},{3,7},{4,0},{5,1},{6,2},{7,3},{8,12},{9,13},{10,... | collective-permute-start | bytes 2359304 | tf_op jit(solution)/shard_map/ppermute | solution.py:470
  79.4 16.3 %collective-permute-start.21 = (bf16[8,96,768]{2,1,0:T(8,128)(2,1)S(1)}, bf16[8,96,768]{2,1,0:T(8,128)(2,1)S(1)}, u32[]{:S(2)}, u32[]{:S(2)}) collective-permute-start(bf16[8,96,768]{2,1,0:T(8,128)(2,1)S(1)} %constant_dynamic-update-slice_fusion.10), channel_id=1, source_target_pairs={{0,8},{1,9},{2,10},{3,11},{4,20},{5,21},{6,22},{7,23},{8,0},{9,1},... | collective-permute-start | bytes 3538952 | tf_op jit(solution)/shard_map/ppermute | solution.py:479
  81.2 1.7 collective-permute-start.19
  87.9 18.7 %collective-permute-start.25 = (bf16[4,384,768]{2,1,0:T(8,128)(2,1)S(1)}, bf16[4,384,768]{2,1,0:T(8,128)(2,1)S(1)}, u32[]{:S(2)}, u32[]{:S(2)}) collective-permute-start(bf16[4,384,768]{2,1,0:T(8,128)(2,1)S(1)} %get-tuple-element.107.z_ref.refs_1_), channel_id=1, source_target_pairs={{0,4},{1,5},{2,6},{3,7},{4,0},{5,1},{6,2},{7,3},{8,12},{9,13},{10,... | collective-permute-start | bytes 7077896 | tf_op jit(solution)/shard_map/ppermute | solution.py:470
  88.1 7.6 %collective-permute-start.22 = (bf16[8,96,768]{2,1,0:T(8,128)(2,1)S(1)}, bf16[8,96,768]{2,1,0:T(8,128)(2,1)S(1)}, u32[]{:S(2)}, u32[]{:S(2)}) collective-permute-start(bf16[8,96,768]{2,1,0:T(8,128)(2,1)S(1)} %constant_dynamic-update-slice_fusion.10), channel_id=1, source_target_pairs={{0,4},{1,5},{2,6},{3,7},{4,0},{5,1},{6,2},{7,3},{8,12},{9,13},{10,... | collective-permute-start | bytes 3538952 | tf_op jit(solution)/shard_map/ppermute | solution.py:479
  95.7 2.8 %collective-permute-start.23 = (bf16[8,96,768]{2,1,0:T(8,128)(2,1)S(1)}, bf16[8,96,768]{2,1,0:T(8,128)(2,1)S(1)}, u32[]{:S(2)}, u32[]{:S(2)}) collective-permute-start(bf16[8,96,768]{2,1,0:T(8,128)(2,1)S(1)} %collective-permute-done.21), channel_id=1, source_target_pairs={{0,4},{1,5},{2,6},{3,7},{4,0},{5,1},{6,2},{7,3},{8,12},{9,13},{10,... | collective-permute-start | bytes 3538952 | tf_op jit(solution)/shard_map/ppermute | solution.py:479
  103.2 3.3 %collective-permute-start.24 = (bf16[384,384]{1,0:T(8,128)(2,1)S(1)}, bf16[384,384]{1,0:T(8,128)(2,1)S(1)}, u32[]{:S(2)}, u32[]{:S(2)}) collective-permute-start(bf16[384,384]{1,0:T(8,128)(2,1)S(1)} %get-tuple-element.120), channel_id=1, source_target_pairs={{0,4},{1,5},{2,6},{3,7},{4,0},{5,1},{6,2},{7,3},{8,12},{9,13},{10,... | collective-permute-start | bytes 884744 | tf_op jit(solution)/shard_map/ppermute | solution.py:470
  106.1 4.2 %copy-start.11 = (f32[384,768]{1,0:T(8,128)S(1)}, f32[384,768]{1,0:T(8,128)}, u32[]{:S(2)}) copy-start(f32[384,768]{1,0:T(8,128)} %get-tuple-element.123.x1_ref) | copy-start | bytes 3538948
  106.1 4.2 %copy-start.12 = (f32[384,1]{1,0:T(8,128)S(1)}, f32[384,1]{1,0:T(8,128)}, u32[]{:S(2)}) copy-start(f32[384,1]{1,0:T(8,128)} %get-tuple-element.124.r1_ref) | copy-start | bytes 4612
  106.1 9.7 %collective-permute-start.26 = (bf16[4,384,768]{2,1,0:T(8,128)(2,1)S(1)}, bf16[4,384,768]{2,1,0:T(8,128)(2,1)S(1)}, u32[]{:S(2)}, u32[]{:S(2)}) collective-permute-start(bf16[4,384,768]{2,1,0:T(8,128)(2,1)S(1)} %get-tuple-element.121.du_ref.refs_1_), channel_id=1, source_target_pairs={{0,4},{1,5},{2,6},{3,7},{4,0},{5,1},{6,2},{7,3},{8,12},{9,13},{10,... | collective-permute-start | bytes 7077896 | tf_op jit(solution)/shard_map/ppermute | solution.py:470
  108.5 16.3 %collective-permute-start.28 = (bf16[8,96,768]{2,1,0:T(8,128)(2,1)S(1)}, bf16[8,96,768]{2,1,0:T(8,128)(2,1)S(1)}, u32[]{:S(2)}, u32[]{:S(2)}) collective-permute-start(bf16[8,96,768]{2,1,0:T(8,128)(2,1)S(1)} %bitcast.122), channel_id=1, source_target_pairs={{0,8},{1,9},{2,10},{3,11},{4,20},{5,21},{6,22},{7,23},{8,0},{9,1},... | collective-permute-start | bytes 3538952 | tf_op jit(solution)/shard_map/ppermute | solution.py:499
  110.3 5.5 %copy-start.10 = (bf16[384,384]{1,0:T(8,128)(2,1)S(1)}, bf16[384,384]{1,0:T(8,128)(2,1)}, u32[]{:S(2)}) copy-start(bf16[384,384]{1,0:T(8,128)(2,1)} %get-tuple-element.128.refs_0_) | copy-start | bytes 884740
  119.1 18.5 %collective-permute-start.29 = (bf16[8,96,768]{2,1,0:T(8,128)(2,1)S(1)}, bf16[8,96,768]{2,1,0:T(8,128)(2,1)S(1)}, u32[]{:S(2)}, u32[]{:S(2)}) collective-permute-start(bf16[8,96,768]{2,1,0:T(8,128)(2,1)S(1)} %bitcast.131), channel_id=1, source_target_pairs={{0,8},{1,9},{2,10},{3,11},{4,20},{5,21},{6,22},{7,23},{8,0},{9,1},... | collective-permute-start | bytes 3538952 | tf_op jit(solution)/shard_map/ppermute | solution.py:499
  119.5 1.9 collective-permute-start.27
  119.5 5.3 %copy-start.4 = (f32[4,3,128,384]{3,2,1,0:T(8,128)S(1)}, f32[4,3,128,384]{3,2,1,0:T(8,128)}, u32[]{:S(2)}) copy-start(f32[4,3,128,384]{3,2,1,0:T(8,128)} %get-tuple-element.134.p_ref) | copy-start | bytes 7077892
  119.5 5.3 %copy-start.5 = (bf16[4,384,576]{2,1,0:T(8,128)(2,1)S(1)}, bf16[4,384,576]{2,1,0:T(8,128)(2,1)}, u32[]{:S(2)}) copy-start(bf16[4,384,576]{2,1,0:T(8,128)(2,1)} %get-tuple-element.133.qkv_ref) | copy-start | bytes 5308420
  133.5 7.0 %collective-permute-start.30 = (bf16[2,384,640]{2,1,0:T(8,128)(2,1)S(1)}, bf16[2,384,640]{2,1,0:T(8,128)(2,1)S(1)}, u32[]{:S(2)}, u32[]{:S(2)}) collective-permute-start(bf16[2,384,640]{2,1,0:T(8,128)(2,1)S(1)} %get-tuple-element.144.refs_1_.low_ref), channel_id=1, source_target_pairs={{0,4},{1,5},{2,6},{3,7},{4,0},{5,1},{6,2},{7,3},{8,12},{9,13},{10,... | collective-permute-start | bytes 2949128 | tf_op jit(solution)/shard_map/ppermute | solution.py:470
  133.5 6.9 %collective-permute-start.31 = (bf16[2,384,640]{2,1,0:T(8,128)(2,1)S(1)}, bf16[2,384,640]{2,1,0:T(8,128)(2,1)S(1)}, u32[]{:S(2)}, u32[]{:S(2)}) collective-permute-start(bf16[2,384,640]{2,1,0:T(8,128)(2,1)S(1)} %get-tuple-element.145.refs_2_.high_ref), channel_id=1, source_target_pairs={{0,4},{1,5},{2,6},{3,7},{4,0},{5,1},{6,2},{7,3},{8,12},{9,13},{10,... | collective-permute-start | bytes 2949128 | tf_op jit(solution)/shard_map/ppermute | solution.py:470
  134.3 4.2 %copy-start.14 = (pred[768,768]{1,0:T(32,128)(4,1)S(1)}, pred[768,768]{1,0:T(32,128)(4,1)}, u32[]{:S(2)}) copy-start(pred[768,768]{1,0:T(32,128)(4,1)} %copy-done.13) | copy-start | bytes 1769476
  134.3 11.4 %collective-permute-start.33 = (bf16[4,96,768]{2,1,0:T(8,128)(2,1)S(1)}, bf16[4,96,768]{2,1,0:T(8,128)(2,1)S(1)}, u32[]{:S(2)}, u32[]{:S(2)}) collective-permute-start(bf16[4,96,768]{2,1,0:T(8,128)(2,1)S(1)} %get-tuple-element.208), channel_id=1, source_target_pairs={{0,16},{1,17},{2,18},{3,19},{4,12},{5,13},{6,14},{7,15},{8,24},{9,... | collective-permute-start | bytes 1769480 | tf_op jit(solution)/shard_map/ppermute | solution.py:499
  137.9 12.7 %collective-permute-start.34 = (bf16[4,96,768]{2,1,0:T(8,128)(2,1)S(1)}, bf16[4,96,768]{2,1,0:T(8,128)(2,1)S(1)}, u32[]{:S(2)}, u32[]{:S(2)}) collective-permute-start(bf16[4,96,768]{2,1,0:T(8,128)(2,1)S(1)} %get-tuple-element.210), channel_id=1, source_target_pairs={{0,16},{1,17},{2,18},{3,19},{4,12},{5,13},{6,14},{7,15},{8,24},{9,... | collective-permute-start | bytes 1769480 | tf_op jit(solution)/shard_map/ppermute | solution.py:499
  138.3 2.1 %collective-permute-start.32 = (f32[4,4,768]{2,1,0:T(4,128)S(1)}, f32[4,4,768]{2,1,0:T(4,128)S(1)}, u32[]{:S(2)}, u32[]{:S(2)}) collective-permute-start(f32[4,4,768]{2,1,0:T(4,128)S(1)} %get-tuple-element.142), channel_id=1, source_target_pairs={{0,4},{1,5},{2,6},{3,7},{4,0},{5,1},{6,2},{7,3},{8,12},{9,13},{10,... | collective-permute-start | bytes 147464 | tf_op jit(solution)/shard_map/ppermute | solution.py:470
  150.6 17.3 %collective-permute-start.35 = (bf16[8,104,768]{2,1,0:T(8,128)(2,1)S(1)}, bf16[8,104,768]{2,1,0:T(8,128)(2,1)S(1)}, u32[]{:S(2)}, u32[]{:S(2)}) collective-permute-start(bf16[8,104,768]{2,1,0:T(8,128)(2,1)S(1)} %bitcast.130), channel_id=1, source_target_pairs={{0,8},{1,9},{2,10},{3,11},{4,20},{5,21},{6,22},{7,23},{8,0},{9,1},... | collective-permute-start | bytes 3833864 | tf_op jit(solution)/shard_map/ppermute | solution.py:499
  152.6 5.2 %copy-start.3 = (bf16[768,768]{1,0:T(8,128)(2,1)S(1)}, bf16[768,768]{1,0:T(8,128)(2,1)}, u32[]{:S(2)}) copy-start(bf16[768,768]{1,0:T(8,128)(2,1)} %copy-done.2) | copy-start | bytes 3538948
  152.6 17.5 %collective-permute-start.38 = (bf16[2,96,768]{2,1,0:T(8,128)(2,1)S(1)}, bf16[2,96,768]{2,1,0:T(8,128)(2,1)S(1)}, u32[]{:S(2)}, u32[]{:S(2)}) collective-permute-start(bf16[2,96,768]{2,1,0:T(8,128)(2,1)S(1)} %pad_maximum_fusion.3), channel_id=1, source_target_pairs={{0,1},{1,0},{2,3},{3,2},{4,5},{5,4},{6,7},{7,6},{8,9},{9,8},{10,11... | collective-permute-start | bytes 884744 | tf_op jit(solution)/shard_map/ppermute | solution.py:499
  155.3 23.6 %collective-permute-start.39 = (bf16[2,96,768]{2,1,0:T(8,128)(2,1)S(1)}, bf16[2,96,768]{2,1,0:T(8,128)(2,1)S(1)}, u32[]{:S(2)}, u32[]{:S(2)}) collective-permute-start(bf16[2,96,768]{2,1,0:T(8,128)(2,1)S(1)} %pad_maximum_fusion.4), channel_id=1, source_target_pairs={{0,2},{1,3},{2,0},{3,1},{4,6},{5,7},{6,4},{7,5},{8,10},{9,11},{10,... | collective-permute-start | bytes 884744 | tf_op jit(solution)/shard_map/ppermute | solution.py:499
  156.1 22.7 %collective-permute-start.40 = (bf16[2,96,768]{2,1,0:T(8,128)(2,1)S(1)}, bf16[2,96,768]{2,1,0:T(8,128)(2,1)S(1)}, u32[]{:S(2)}, u32[]{:S(2)}) collective-permute-start(bf16[2,96,768]{2,1,0:T(8,128)(2,1)S(1)} %pad_maximum_fusion.5), channel_id=1, source_target_pairs={{0,3},{1,2},{2,1},{3,0},{4,7},{5,6},{6,5},{7,4},{8,11},{9,10},{10,... | collective-permute-start | bytes 884744 | tf_op jit(solution)/shard_map/ppermute | solution.py:499
  168.0 12.2 %collective-permute-start.37 = (bf16[1,104,768]{2,1,0:T(8,128)(2,1)S(1)}, bf16[1,104,768]{2,1,0:T(8,128)(2,1)S(1)}, u32[]{:S(2)}, u32[]{:S(2)}) collective-permute-start(bf16[1,104,768]{2,1,0:T(8,128)(2,1)S(1)} %get-tuple-element.150), channel_id=1, source_target_pairs={{0,16},{1,17},{2,18},{3,19},{4,12},{5,13},{6,14},{7,15},{8,24},{9,... | collective-permute-start | bytes 479240 | tf_op jit(solution)/shard_map/ppermute | solution.py:499
  168.4 11.8 %collective-permute-start.44 = (bf16[1,104,768]{2,1,0:T(8,128)(2,1)S(1)}, bf16[1,104,768]{2,1,0:T(8,128)(2,1)S(1)}, u32[]{:S(2)}, u32[]{:S(2)}) collective-permute-start(bf16[1,104,768]{2,1,0:T(8,128)(2,1)S(1)} %get-tuple-element.154), channel_id=1, source_target_pairs={{0,16},{1,17},{2,18},{3,19},{4,12},{5,13},{6,14},{7,15},{8,24},{9,... | collective-permute-start | bytes 479240 | tf_op jit(solution)/shard_map/ppermute | solution.py:499
  170.1 10.1 %collective-permute-start.42 = (bf16[1,104,768]{2,1,0:T(8,128)(2,1)S(1)}, bf16[1,104,768]{2,1,0:T(8,128)(2,1)S(1)}, u32[]{:S(2)}, u32[]{:S(2)}) collective-permute-start(bf16[1,104,768]{2,1,0:T(8,128)(2,1)S(1)} %get-tuple-element.152), channel_id=1, source_target_pairs={{0,16},{1,17},{2,18},{3,19},{4,12},{5,13},{6,14},{7,15},{8,24},{9,... | collective-permute-start | bytes 479240 | tf_op jit(solution)/shard_map/ppermute | solution.py:499
  179.0 11.0 %collective-permute-start.36 = (bf16[1,104,768]{2,1,0:T(8,128)(2,1)S(1)}, bf16[1,104,768]{2,1,0:T(8,128)(2,1)S(1)}, u32[]{:S(2)}, u32[]{:S(2)}) collective-permute-start(bf16[1,104,768]{2,1,0:T(8,128)(2,1)S(1)} %get-tuple-element.149), channel_id=1, source_target_pairs={{0,16},{1,17},{2,18},{3,19},{4,12},{5,13},{6,14},{7,15},{8,24},{9,... | collective-permute-start | bytes 479240 | tf_op jit(solution)/shard_map/ppermute | solution.py:499
  180.4 9.6 %collective-permute-start.45 = (bf16[1,104,768]{2,1,0:T(8,128)(2,1)S(1)}, bf16[1,104,768]{2,1,0:T(8,128)(2,1)S(1)}, u32[]{:S(2)}, u32[]{:S(2)}) collective-permute-start(bf16[1,104,768]{2,1,0:T(8,128)(2,1)S(1)} %get-tuple-element.155), channel_id=1, source_target_pairs={{0,3},{1,2},{2,1},{3,0},{4,7},{5,6},{6,5},{7,4},{8,11},{9,10},{10,... | collective-permute-start | bytes 479240 | tf_op jit(solution)/shard_map/ppermute | solution.py:499
  182.7 15.2 %collective-permute-start.43 = (bf16[1,104,768]{2,1,0:T(8,128)(2,1)S(1)}, bf16[1,104,768]{2,1,0:T(8,128)(2,1)S(1)}, u32[]{:S(2)}, u32[]{:S(2)}) collective-permute-start(bf16[1,104,768]{2,1,0:T(8,128)(2,1)S(1)} %get-tuple-element.153), channel_id=1, source_target_pairs={{0,2},{1,3},{2,0},{3,1},{4,6},{5,7},{6,4},{7,5},{8,10},{9,11},{10,... | collective-permute-start | bytes 479240 | tf_op jit(solution)/shard_map/ppermute | solution.py:499
  189.1 8.7 %collective-permute-start.41 = (bf16[1,104,768]{2,1,0:T(8,128)(2,1)S(1)}, bf16[1,104,768]{2,1,0:T(8,128)(2,1)S(1)}, u32[]{:S(2)}, u32[]{:S(2)}) collective-permute-start(bf16[1,104,768]{2,1,0:T(8,128)(2,1)S(1)} %get-tuple-element.151), channel_id=1, source_target_pairs={{0,1},{1,0},{2,3},{3,2},{4,5},{5,4},{6,7},{7,6},{8,9},{9,8},{10,11... | collective-permute-start | bytes 479240 | tf_op jit(solution)/shard_map/ppermute | solution.py:499
  197.8 3.5 %copy-start.1 = (f32[3,1,8,768]{3,2,1,0:T(8,128)S(1)}, f32[3,1,8,768]{3,2,1,0:T(8,128)}, u32[]{:S(2)}) copy-start(f32[3,1,8,768]{3,2,1,0:T(8,128)} %param.17) | copy-start | bytes 221188
  (7 other events, 14.3 us)

commit v9 on v8

--- a/solution.py
+++ b/solution.py
@@ -237,10 +237,10 @@
     d_ref[0] = phi + u * (jnp.exp(-0.5 * u * u) * 0.3989422804014327)
 
 
-def down_forward(z_ref, w0_ref, w1_ref, w2_ref, w3_ref, n1_ref, vec_ref, segc_ref, segr_ref, pg_ref,
+def down_forward(z_ref, w0_ref, w1_ref, w2_ref, w3_ref, w4_ref, w5_ref, w6_ref, w7_ref, n1_ref, vec_ref, segc_ref, segr_ref, pg_ref,
                  pooled_ref, db_ref, dbb_ref, dbt_ref, dbs_ref, sums_ref, acc_ref):
     step = pl.program_id(0)
-    add = nt(z_ref[0], rows_of((w0_ref, w1_ref, w2_ref, w3_ref)))
+    add = nt(z_ref[0, 0], rows_of((w0_ref, w1_ref, w2_ref, w3_ref))) + nt(z_ref[1, 0], rows_of((w4_ref, w5_ref, w6_ref, w7_ref)))
 
     accumulate(acc_ref, step, add)
 
@@ -277,10 +277,11 @@
     ref[:, :, :BLK, :] = grad.astype(bf16).reshape(grad.shape[0] // BLK, 1, BLK, grad.shape[1])
 
 
-def hidden_backward(dbb_ref, w0_ref, w1_ref, w2_ref, w3_ref, d_ref, du_ref, bu_ref):
-    du = (nn(dbb_ref[...], rows_of((w0_ref, w1_ref, w2_ref, w3_ref))) * d_ref[0]).astype(bf16)
-    du_ref[0] = du
-    bu_ref[0] = col_sum(du.astype(f32))
+def hidden_backward(dbb_ref, w0_ref, w1_ref, w2_ref, w3_ref, w4_ref, w5_ref, w6_ref, w7_ref, d_ref, du_ref, bu_ref):
+    for n, refs in enumerate(((w0_ref, w1_ref, w2_ref, w3_ref), (w4_ref, w5_ref, w6_ref, w7_ref))):
+        du = (nn(dbb_ref[...], rows_of(refs)) * d_ref[n, 0]).astype(bf16)
+        du_ref[n, 0] = du
+        bu_ref[n, 0] = col_sum(du.astype(f32))
 
 
 def step_value(refs, width):
@@ -415,10 +416,6 @@
     return pl.BlockSpec((a.shape[0], 1, BLK, a.shape[3]), lambda s: (0, s, 0, 0))
 
 
-def weight_t(a):
-    return pl.BlockSpec((1, a.shape[1], BLK, a.shape[3]), lambda s: (s, 0, 0, 0))
-
-
 def half_spec(h):
     return pl.BlockSpec((h.shape[0], 1) + h.shape[2:], lambda s: (0, s, 0, 0))
 
@@ -543,8 +540,15 @@
         tables = flips(n_dp, n_t)
         packed = (qkv_weight, out_weight, *[p[None] for p in d_parts], qv_bias, up_bias[None])
         packed = pl.pallas_call(pack, out_shape=sds((BLK + 8, 4 * hc), bf16))(*packed)
-        first, middle, last = Gather(packed, tables), Gather(up_weight, tables), Gather(down_weight_in.T, tables)
-        done = first.stage("Z") + last.stage("2")
+        first, middle = Gather(packed, tables), Gather(up_weight, tables)
+        own = down_weight_in.T[None]
+
+        def move(value, name, *done, way=0):
+            return lax.ppermute(after(value, *done), AXES, tables[name][way])
+
+        own2 = move(own, "2")
+        done = first.stage("Z") + [own2]
+        own2 = jnp.concatenate([own, own2])
 
         core = (at_dp & 1) ^ (rel >> 2)
         s3, s2 = (rel >> 1) & 1, rel & 1
@@ -572,11 +576,13 @@
     if pairwise:
         done = first.stage("2", *done, x, x_keep, x_send, pg, hot_d, hot_e) + middle.stage("Z", *done)
         x_other = swap(x_send, tables, *done)
-        near_z = last.send("Z", *done, tables=slice(0, 2))
-        done = first.stage("3", *done) + middle.stage("2", *done) + near_z
-        first.stage("C", *done)
-        x = after(x, x_other)
-        got_u3, far_z = middle.send("3", *done), last.send("Z", *done, tables=slice(2, None))
+        z_one, z_two = move(own2, "Z", *done, way=0), move(own2, "Z", *done, way=1)
+        got_q3, got_u2 = first.stage("3", *done), middle.stage("2", *done)
+        first.stage("C", *got_u2, z_one, z_two)
+        got_u3 = middle.send("3")
+        z_three = move(own2, "Z", *got_q3, z_one, z_two, way=2)
+        low = jnp.concatenate([own2, z_one])
+        low_far = move(low, "3", *got_q3)
         w_qo = first.pieces(2, n_t)
     else:
         heads_in = [qkv_weight[0], qkv_weight[1], qkv_weight[2], out_weight.T]
@@ -595,6 +601,7 @@
         ]
         w_up = [w[..., 4 * hc : 4 * hc + fc] for w in quarters]
         w_down = [w[..., 4 * hc + fc :].transpose(1, 0, 2, 3) for w in quarters]
+        w_down = [w[: n_t // 2] for w in w_down] + [w[n_t // 2 :] for w in w_down]
 
     hl = hc // HD * L
     o_wide, q_wide = -(-hc // 128) * 128, -(-3 * hc // 128) * 128
@@ -609,7 +616,13 @@
         return [(a, weight(a)) for a in arrays]
 
     def weights_t(*arrays):
-        return [(a, weight_t(a)) for a in arrays]
+        return [(a, pl.BlockSpec((1, a.shape[1], BLK, a.shape[3]), lambda s: (s, 0, 0, 0))) for a in arrays]
+
+    def paired(*arrays):
+        return [(a, pl.BlockSpec((2, 1) + a.shape[2:], lambda s: (0, s, 0, 0))) for a in arrays]
+
+    def folded(a):
+        return a.reshape(2, n_t // 2, *a.shape[1:])
 
     tails = [
         (w, pl.BlockSpec((w.shape[0], n_t, 8, w.shape[3]), lambda s: (0, 0, BLK // 8, 0), pipeline_mode=pl.Buffered(1)))
@@ -624,24 +637,27 @@
         [pltpu.VMEM((T, D), f32), pltpu.VMEM((n_t, 1, hc), f32), pltpu.VMEM((n_t, 1, hc), f32)],
     )
     if pairwise:
-        last.take("Z", near_z + [after(g, n1b) for g in far_z])
         middle.take("3", [after(g, n1b) for g in got_u3])
-        last.stage("3", *got_u3)
-        middle.stage("C", n1b, *far_z)
-        last.take("C", last.send("C", n1b, parts=(0,)))
-        last.take("C", last.send("C", parts=(1,)))
-        w_up, w_down = middle.pieces(2, n_t), last.pieces(n_t, 2)
+        middle.stage("C", n1b, z_three)
+        high = jnp.concatenate([z_two, after(z_three, n1b)])
+        high_far = move(high, "3")
+        w_up = middle.pieces(2, n_t)
+        low_other = [swap(low, tables, n1b), swap(after(low_far, n1b), tables)]
         n1_other = swap(n1_send, tables)
         o_other = swap(o, tables)
-        b_u = after(b_u, n1_other, o_other)
+        b_u = after(b_u, *low_other)
     z, dgelu = call(
         up_forward, n_t, 4, wholes(n1b) + weights(*w_up) + leads(b_u),
         leads(sds((n_t, T, fc), bf16), sds((n_t, T, fc), f32)),
     )
     if pairwise:
-        z_other = swap(z, tables)
+        high_other = [swap(high, tables), swap(after(high_far, z), tables)]
+        w_down = [low, low_far, *low_other, high, high_far, *high_other]
+        w_down = [w.reshape(n_t // 2, 2, BLK, fc) for w in w_down]
+        z_other = swap(z, tables, *high_other)
+        dgelu = after(dgelu, x_other, n1_other, o_other)
     pooled, db, dbb, db_keep, db_send, sums2 = call(
-        down_forward, n_t, 5.5, leads(z) + weights_t(*w_down) + wholes(n1, vec_d, seg_c, seg_r, pg),
+        down_forward, n_t // 2, 5.5, paired(folded(z)) + weights_t(*w_down) + wholes(n1, vec_d, seg_c, seg_r, pg),
         wholes(sds((G, segs, D), f32), sds((T, D), f32), sds((T, D), bf16), sds(turned, bf16), sds(turned, bf16), sds((3, D), f32)),
         [pltpu.VMEM((T, D), f32)],
     )
@@ -673,9 +689,10 @@
         return a.reshape((-1,) + a.shape[2:])
 
     du, g_bu = call(
-        hidden_backward, n_t, 3.5, wholes(dbb) + weights_t(*w_down) + leads(dgelu),
-        leads(sds((n_t, T, fc), bf16), sds((n_t, 1, fc), f32)),
+        hidden_backward, n_t // 2, 3.5, wholes(dbb) + weights_t(*w_down) + paired(folded(dgelu)),
+        paired(sds((2, n_t // 2, T, fc), bf16), sds((2, n_t // 2, 1, fc), f32)),
     )
+    du, g_bu = du.reshape(n_t, T, fc), g_bu.reshape(n_t, 1, fc)
     if pairwise:
         db_other = swap(db_send, tables)
         du_other = swap(du, tables)

time: 202 us -> 200 us (0.990)
  waiting for transfers between devices: 67.8 us -> 63.5 us
  starting transfers between devices: 48.9 us -> 51.9 us
    ppermute x21 -> x14, waiting for transfers between devices: 35.8 us -> 17.1 us  [send(): lax.ppermute(after(h, *done), AXES, t)]
    ppermute x0 -> x6, waiting for transfers between devices: none -> 13.8 us  [move(): return lax.ppermute(after(value, *done), AXES, tables[name][way])]
    ppermute x0 -> x6, starting transfers between devices: none -> 10.5 us  [move(): return lax.ppermute(after(value, *done), AXES, tables[name][way])]
    ppermute x21 -> x14, starting transfers between devices: 25.2 us -> 15.3 us  [send(): lax.ppermute(after(h, *done), AXES, t)]
    concatenate x3 -> x2, other arithmetic: 2.8 us -> 0.16 us  [take(): jnp.concatenate(self.held + got)]
    concatenate x0 -> x2, other arithmetic: none -> 2.62 us  [the longest x1 1.65 us: per_device(): own2 = jnp.concatenate([own, own2])]
    unnamed x64 -> x63, local copies, waits for them, and re-layouts: 7.04 us -> 6.86 us
  transfers between devices with their start and end apart: 46 -> 49, of which waited for: 16 -> 16; matrix products, arithmetic and copies ran while one was open for 9% -> 8% of each run, Pallas kernels for 29% -> 29%
where the time goes in v9:
time: 200 us; the launch traced here: 199 us
  waiting for transfers between devices  63.5 us (32%)
  Pallas kernels  60.7 us (30%)
  starting transfers between devices  51.9 us (26%)
  local copies, waits for them, and re-layouts  12.4 us (6%)
  other arithmetic  6.68 us (3%)
  matrix products  2.99 us (1%)
    pallas_call x11, Pallas kernels, call(): pl.pallas_call(body, grid=(n_t,), in_specs=[s for _, s in ins], out_specs...  58 us
    ppermute x15, waiting for transfers between devices, stage(): lax.ppermute(after(s, *done), AXES, tables[n // pieces])  28.9 us
    ppermute x15, starting transfers between devices, stage(): lax.ppermute(after(s, *done), AXES, tables[n // pieces])  23.5 us
    ppermute x14, waiting for transfers between devices, send(): lax.ppermute(after(h, *done), AXES, t)  17.1 us
    ppermute x14, starting transfers between devices, send(): lax.ppermute(after(h, *done), AXES, t)  15.3 us
    ppermute x6, waiting for transfers between devices, move(): return lax.ppermute(after(value, *done), AXES, tables[name][way])  13.8 us
    ppermute x6, starting transfers between devices, move(): return lax.ppermute(after(value, *done), AXES, tables[name][way])  10.5 us
    unnamed x63, local copies, waits for them, and re-layouts  6.86 us
  transfers between devices with their start and end apart: 49, of which 16 were waited for; matrix products, arithmetic and copies ran while one was open for 8% of the time, Pallas kernels for 29%

profile of v9, /device:TPU:0, one launch (start us, length us, event | category | flops | bytes accessed | tf_op | source)
XLA Modules:
  0.0 199.3 jit_solution(6054283771836137556)
XLA Ops:
  0.7 2.0 shard_map.255
  2.6 3.0 %collective-permute-start = (bf16[1,104,768]{2,1,0:T(8,128)(2,1)}, bf16[1,104,768]{2,1,0:T(8,128)(2,1)S(1)}, u32[]{:S(2)}, u32[]{:S(2)}) collective-permute-start(bf16[1,104,768]{2,1,0:T(8,128)(2,1)} %bitcast.153), channel_id=1, source_target_pairs={{0,1},{1,0},{2,3},{3,2},{4,5},{5,4},{6,7},{7,6},{8,9},{9,8},{10,11... | collective-permute-start | bytes 479240 | tf_op jit(solution)/shard_map/ppermute | solution.py:476
  5.6 2.6 %collective-permute-start.1 = (bf16[1,104,768]{2,1,0:T(8,128)(2,1)}, bf16[1,104,768]{2,1,0:T(8,128)(2,1)S(1)}, u32[]{:S(2)}, u32[]{:S(2)}) collective-permute-start(bf16[1,104,768]{2,1,0:T(8,128)(2,1)} %bitcast.154), channel_id=1, source_target_pairs={{0,2},{1,3},{2,0},{3,1},{4,6},{5,7},{6,4},{7,5},{8,10},{9,11},{10,... | collective-permute-start | bytes 479240 | tf_op jit(solution)/shard_map/ppermute | solution.py:476
  8.2 1.7 collective-permute-start.3
  10.5 0.7 copy.57
  12.5 1.0 convolution_bitcast_fusion.pg_ref
  13.6 0.7 shard_map.254
  14.3 0.8 copy-done.7
  15.1 0.7 copy-done.10
  15.8 0.7 copy-done.14
  16.5 4.1 %collective-permute-done.1 = bf16[1,104,768]{2,1,0:T(8,128)(2,1)S(1)} collective-permute-done((bf16[1,104,768]{2,1,0:T(8,128)(2,1)}, bf16[1,104,768]{2,1,0:T(8,128)(2,1)S(1)}, u32[]{:S(2)}, u32[]{:S(2)}) %collective-permute-start.1) | collective-permute-done | bytes 159776 | tf_op jit(solution)/shard_map/ppermute | solution.py:476
  20.7 1.6 collective-permute-start.4
  22.4 2.6 %collective-permute-start.5 = (bf16[1,96,768]{2,1,0:T(8,128)(2,1)S(1)}, bf16[1,96,768]{2,1,0:T(8,128)(2,1)S(1)}, u32[]{:S(2)}, u32[]{:S(2)}) collective-permute-start(bf16[1,96,768]{2,1,0:T(8,128)(2,1)S(1)} %bitcast.160), channel_id=1, source_target_pairs={{0,1},{1,0},{2,3},{3,2},{4,5},{5,4},{6,7},{7,6},{8,9},{9,8},{10,11... | collective-permute-start | bytes 442376 | tf_op jit(solution)/shard_map/ppermute | solution.py:476
  25.0 1.1 collective-permute-start.6
  26.1 1.4 collective-permute-start.7
  27.5 3.7 %collective-permute-done.4 = bf16[4,104,768]{2,1,0:T(8,128)(2,1)S(1)} collective-permute-done((bf16[4,104,768]{2,1,0:T(8,128)(2,1)S(1)}, bf16[4,104,768]{2,1,0:T(8,128)(2,1)S(1)}, u32[]{:S(2)}, u32[]{:S(2)}) %collective-permute-start.4) | collective-permute-done | bytes 639008 | tf_op jit(solution)/shard_map/ppermute | solution.py:476
  31.3 6.4 %collective-permute-done.6 = bf16[1,96,768]{2,1,0:T(8,128)(2,1)S(1)} collective-permute-done((bf16[1,96,768]{2,1,0:T(8,128)(2,1)S(1)}, bf16[1,96,768]{2,1,0:T(8,128)(2,1)S(1)}, u32[]{:S(2)}, u32[]{:S(2)}) %collective-permute-start.6) | collective-permute-done | bytes 147488 | tf_op jit(solution)/shard_map/ppermute | solution.py:476
  38.3 1.6 collective-permute-start.9
  39.9 0.7 constant_dynamic-update-slice_fusion.9
  40.6 1.7 pad_maximum_fusion.3
  42.2 2.1 %collective-permute-start.10 = (bf16[2,96,768]{2,1,0:T(8,128)(2,1)}, bf16[2,96,768]{2,1,0:T(8,128)(2,1)S(1)}, u32[]{:S(2)}, u32[]{:S(2)}) collective-permute-start(bf16[2,96,768]{2,1,0:T(8,128)(2,1)} %pad_maximum_fusion.3), channel_id=1, source_target_pairs={{0,1},{1,0},{2,3},{3,2},{4,5},{5,4},{6,7},{7,6},{8,9},{9,8},{10,11... | collective-permute-start | bytes 884744 | tf_op jit(solution)/shard_map/ppermute | solution.py:547
  44.4 1.1 collective-permute-start.11
  45.5 0.7 constant_dynamic-update-slice_fusion.8
  46.2 0.7 constant_dynamic-update-slice_fusion.7
  46.8 0.7 constant_dynamic-update-slice_fusion.6
  47.5 8.4 %collective-permute-done.10 = bf16[2,96,768]{2,1,0:T(8,128)(2,1)S(1)} collective-permute-done((bf16[2,96,768]{2,1,0:T(8,128)(2,1)}, bf16[2,96,768]{2,1,0:T(8,128)(2,1)S(1)}, u32[]{:S(2)}, u32[]{:S(2)}) %collective-permute-start.10) | collective-permute-done | bytes 294944 | tf_op jit(solution)/shard_map/ppermute | solution.py:547
  56.0 2.8 %collective-permute-done.8 = bf16[8,104,768]{2,1,0:T(8,128)(2,1)S(1)} collective-permute-done((bf16[8,104,768]{2,1,0:T(8,128)(2,1)S(1)}, bf16[8,104,768]{2,1,0:T(8,128)(2,1)S(1)}, u32[]{:S(2)}, u32[]{:S(2)}) %collective-permute-start.8) | collective-permute-done | bytes 1277984 | tf_op jit(solution)/shard_map/ppermute | solution.py:476
  58.8 0.9 constant_dynamic-update-slice_fusion.5
  59.9 4.6 %collective-permute-start.15 = (bf16[2,96,768]{2,1,0:T(8,128)(2,1)}, bf16[2,96,768]{2,1,0:T(8,128)(2,1)}, u32[]{:S(2)}, u32[]{:S(2)}) collective-permute-start(bf16[2,96,768]{2,1,0:T(8,128)(2,1)} %pad_maximum_fusion.3), channel_id=1, source_target_pairs={{0,3},{1,2},{2,1},{3,0},{4,7},{5,6},{6,5},{7,4},{8,11},{9,10},{10,... | collective-permute-start | bytes 884744 | tf_op jit(solution)/shard_map/ppermute | solution.py:547
  64.5 1.0 pad_maximum_fusion.2
  66.2 1.1 copy-done.8
  67.3 11.7 %shard_map.256 = (bf16[4,384,576]{2,1,0:T(8,128)(2,1)}, f32[4,3,128,384]{3,2,1,0:T(8,128)}, bf16[4,384,256]{2,1,0:T(8,128)(2,1)}, f32[384,768]{1,0:T(8,128)S(1)}...) custom-call(bf16[384,768]{1,0:T(8,128)(2,1)S(1)} %copy-done.8, ...), custom_call_target="tpu_custom_call" | custom-call | flops 300000000 | tf_op jit(solution)/shard_map/pallas_call | solution.py:432
  79.8 2.7 %collective-permute-done.19 = bf16[4,96,768]{2,1,0:T(8,128)(2,1)} collective-permute-done((bf16[4,96,768]{2,1,0:T(8,128)(2,1)S(1)}, bf16[4,96,768]{2,1,0:T(8,128)(2,1)}, u32[]{:S(2)}, u32[]{:S(2)}) %collective-permute-start.19) | collective-permute-done | bytes 589856 | tf_op jit(solution)/shard_map/ppermute | solution.py:547
  82.5 1.0 constant_dynamic-update-slice_fusion.10
  84.1 1.4 collective-permute-done.20
  85.6 5.0 %shard_map.257 = (bf16[4,384,768]{2,1,0:T(8,128)(2,1)S(1)}, f32[4,384,768]{2,1,0:T(8,128)S(1)}) custom-call(bf16[384,768]{1,0:T(8,128)(2,1)S(1)} %get-tuple-element.97.n_ref, bf16[2,4,96,768]{3,2,1,0:T(8,128)(2,1)} %bitcast.23.w0_ref, bf16[2,4,96,768]{3,2,1,0:T(8,128)(2,1)} %bitcast.24.w1_ref, bf16[2,4,96,768]{3,2,1,0:T(8,128)(2,1)S(1)} %bitcast.141, ...), custom_call_target="tpu_custom_call" | custom-call | flops 120000000 | tf_op jit(solution)/shard_map/pallas_call | solution.py:432
  90.6 2.8 %collective-permute-done.21 = bf16[4,96,768]{2,1,0:T(8,128)(2,1)S(1)} collective-permute-done((bf16[4,96,768]{2,1,0:T(8,128)(2,1)S(1)}, bf16[4,96,768]{2,1,0:T(8,128)(2,1)S(1)}, u32[]{:S(2)}, u32[]{:S(2)}) %collective-permute-start.21) | collective-permute-done | bytes 589856 | tf_op jit(solution)/shard_map/ppermute | solution.py:547
  93.4 2.0 %collective-permute-done.23 = bf16[4,96,768]{2,1,0:T(8,128)(2,1)S(1)} collective-permute-done((bf16[4,96,768]{2,1,0:T(8,128)(2,1)S(1)}, bf16[4,96,768]{2,1,0:T(8,128)(2,1)S(1)}, u32[]{:S(2)}, u32[]{:S(2)}) %collective-permute-start.23) | collective-permute-done | bytes 589856 | tf_op jit(solution)/shard_map/ppermute | solution.py:467
  96.4 5.0 %shard_map.258 = (f32[3,8,768]{2,1,0:T(8,128)S(1)}, f32[384,768]{1,0:T(8,128)S(1)}, bf16[384,768]{1,0:T(8,128)(2,1)S(1)}, bf16[384,384]{1,0:T(8,128)(2,1)S(1)}, ...) custom-call(bf16[2,2,384,768]{3,2,1,0:T(8,128)(2,1)S(1)} %bitcast.114, bf16[2,2,96,768]{3,2,1,0:T(8,128)(2,1)S(1)} %bitcast.119, ...), custom_call_target="tpu_custom_call" | custom-call | flops 165000000 | tf_op jit(solution)/shard_map/pallas_call | solution.py:432
  101.9 3.4 %shard_map.259 = (bf16[2,2,384,768]{3,2,1,0:T(8,128)(2,1)S(1)}, f32[2,2,1,768]{3,2,1,0:T(1,128)S(1)}) custom-call(bf16[384,768]{1,0:T(8,128)(2,1)S(1)} %get-tuple-element.113.dbb_ref, bf16[2,2,96,768]{3,2,1,0:T(8,128)(2,1)S(1)} %bitcast.120, bf16[2,2,96,768]{3,2,1,0:T(8,128)(2,1)} %bitcast.29.w1_ref, bf16[2,2,96,768]{3,2,1,0:T(8,128)(2,1)S(1)} %bitcast.125, ...), custom_call_target="tpu_custom_call" | custom-call | flops 105000000 | tf_op jit(solution)/shard_map/pallas_call | solution.py:432
  105.5 1.9 shard_map.260
  107.8 5.5 %shard_map.261 = (f32[384,768]{1,0:T(8,128)S(1)}, bf16[384,768]{1,0:T(8,128)(2,1)S(1)}, bf16[384,384]{1,0:T(8,128)(2,1)S(1)}, bf16[384,384]{1,0:T(8,128)(2,1)S(1)}, f32[3,768]{1,0:T(4,128)S(1)}) custom-call(bf16[4,384,768]{2,1,0:T(8,128)(2,1)S(1)} %bitcast.135, bf16[2,4,96,768]{3,2,1,0:T(8,128)(2,1)} %bitcast.23.w0_ref, ...), custom_call_target="tpu_custom_call" | custom-call | flops 60000002048 | tf_op jit(solution)/shard_map/pallas_call | solution.py:432
  113.4 3.3 %shard_map.262 = (bf16[2,4,96,768]{3,2,1,0:T(8,128)(2,1)S(1)}, bf16[2,4,96,768]{3,2,1,0:T(8,128)(2,1)S(1)}) custom-call(bf16[384,384]{1,0:T(8,128)(2,1)S(1)} %copy-done.12, bf16[4,384,768]{2,1,0:T(8,128)(2,1)S(1)} %bitcast.136, bf16[384,384]{1,0:T(8,128)(2,1)S(1)} %collective-permute-done.25.refs_2_, bf16[4,384,768]{2,1,0:T(8,128)(2,1)S(1)} %collective-permute-done.29.refs_3_), custom_call_target="tpu_custom_call" | custom-call | flops 60000000 | tf_op jit(solution)/shard_map/pallas_call | solution.py:432
  116.7 1.8 collective-permute-start.32
  118.5 1.9 shard_map.263
  120.4 3.3 %collective-permute-done.31 = bf16[8,96,768]{2,1,0:T(8,128)(2,1)S(1)} collective-permute-done((bf16[8,96,768]{2,1,0:T(8,128)(2,1)S(1)}, bf16[8,96,768]{2,1,0:T(8,128)(2,1)S(1)}, u32[]{:S(2)}, u32[]{:S(2)}) %collective-permute-start.31) | collective-permute-done | bytes 1179680 | tf_op jit(solution)/shard_map/ppermute | solution.py:496
  123.8 8.7 %shard_map.264 = (bf16[2,384,640]{2,1,0:T(8,128)(2,1)S(1)}, bf16[2,384,640]{2,1,0:T(8,128)(2,1)S(1)}, f32[4,4,768]{2,1,0:T(4,128)S(1)}, f32[4,4,768]{2,1,0:T(4,128)S(1)}) custom-call(bf16[384,768]{1,0:T(8,128)(2,1)S(1)} %get-tuple-element.136.dab_ref, bf16[2,4,104,768]{3,2,1,0:T(8,128)(2,1)S(1)} %bitcast.112, bf16[2,4,104,768]{3,2,1,0:T(8,128)(2,1)S(1)} %bitcast.117, ...), custom_call_target="tpu_custom_call" | custom-call | flops 240000000 | tf_op jit(solution)/shard_map/pallas_call | solution.py:432
  133.7 3.0 %collective-permute-done.32 = bf16[8,96,768]{2,1,0:T(8,128)(2,1)S(1)} collective-permute-done((bf16[8,96,768]{2,1,0:T(8,128)(2,1)S(1)}, bf16[8,96,768]{2,1,0:T(8,128)(2,1)S(1)}, u32[]{:S(2)}, u32[]{:S(2)}) %collective-permute-start.32) | collective-permute-done | bytes 1179680 | tf_op jit(solution)/shard_map/ppermute | solution.py:496
  137.3 2.0 fusion
  139.3 4.3 %shard_map.265 = (bf16[2,4,104,768]{3,2,1,0:T(8,128)(2,1)S(1)}, bf16[2,4,104,768]{3,2,1,0:T(8,128)(2,1)S(1)}) custom-call(bf16[384,384]{1,0:T(8,128)(2,1)S(1)} %copy-done.11, bf16[2,384,640]{2,1,0:T(8,128)(2,1)S(1)} %get-tuple-element.148.refs_1_.low_ref, bf16[2,384,640]{2,1,0:T(8,128)(2,1)S(1)} %get-tuple-element.149.refs_2_.high_ref, ...), custom_call_target="tpu_custom_call" | custom-call | flops 60000000 | tf_op jit(solution)/shard_map/pallas_call | solution.py:432
  143.6 6.0 %collective-permute-done.37 = bf16[4,96,768]{2,1,0:T(8,128)(2,1)S(1)} collective-permute-done((bf16[4,96,768]{2,1,0:T(8,128)(2,1)S(1)}, bf16[4,96,768]{2,1,0:T(8,128)(2,1)S(1)}, u32[]{:S(2)}, u32[]{:S(2)}) %collective-permute-start.37) | collective-permute-done | bytes 589856 | tf_op jit(solution)/shard_map/ppermute | solution.py:496
  150.2 3.7 %collective-permute-start.41 = (bf16[2,96,768]{2,1,0:T(8,128)(2,1)S(1)}, bf16[2,96,768]{2,1,0:T(8,128)(2,1)S(1)}, u32[]{:S(2)}, u32[]{:S(2)}) collective-permute-start(bf16[2,96,768]{2,1,0:T(8,128)(2,1)S(1)} %pad_maximum_fusion.4), channel_id=1, source_target_pairs={{0,1},{1,0},{2,3},{3,2},{4,5},{5,4},{6,7},{7,6},{8,9},{9,8},{10,11... | collective-permute-start | bytes 884744 | tf_op jit(solution)/shard_map/ppermute | solution.py:496
  153.9 2.0 %collective-permute-start.42 = (bf16[2,96,768]{2,1,0:T(8,128)(2,1)S(1)}, bf16[2,96,768]{2,1,0:T(8,128)(2,1)S(1)}, u32[]{:S(2)}, u32[]{:S(2)}) collective-permute-start(bf16[2,96,768]{2,1,0:T(8,128)(2,1)S(1)} %pad_maximum_fusion.5), channel_id=1, source_target_pairs={{0,2},{1,3},{2,0},{3,1},{4,6},{5,7},{6,4},{7,5},{8,10},{9,11},{10,... | collective-permute-start | bytes 884744 | tf_op jit(solution)/shard_map/ppermute | solution.py:496
  156.0 1.5 collective-permute-start.43
  157.5 7.3 %shard_map.266 = f32[384,768]{1,0:T(8,128)} custom-call(bf16[2,384,640]{2,1,0:T(8,128)(2,1)S(1)} %get-tuple-element.148.refs_1_.low_ref, bf16[2,384,640]{2,1,0:T(8,128)(2,1)S(1)} %get-tuple-element.149.refs_2_.high_ref, bf16[2,4,104,768]{3,2,1,0:T(8,128)(2,1)S(1)} %bitcast.113, bf16[2,4,104,768]{3,2,1,0:T(8,128)(2,1)S(1)} %bitcast.118, ...), custom_call_target="tpu_custom_call" | custom-call | flops 120000000 | tf_op jit(solution)/shard_map/pallas_call | solution.py:432
  164.8 2.0 %collective-permute-done.38 = bf16[8,104,768]{2,1,0:T(8,128)(2,1)S(1)} collective-permute-done((bf16[8,104,768]{2,1,0:T(8,128)(2,1)S(1)}, bf16[8,104,768]{2,1,0:T(8,128)(2,1)S(1)}, u32[]{:S(2)}, u32[]{:S(2)}) %collective-permute-start.38) | collective-permute-done | bytes 1277984 | tf_op jit(solution)/shard_map/ppermute | solution.py:496
  167.3 1.7 collective-permute-start.47
  169.4 8.1 %collective-permute-done.42 = bf16[2,96,768]{2,1,0:T(8,128)(2,1)S(1)} collective-permute-done((bf16[2,96,768]{2,1,0:T(8,128)(2,1)S(1)}, bf16[2,96,768]{2,1,0:T(8,128)(2,1)S(1)}, u32[]{:S(2)}, u32[]{:S(2)}) %collective-permute-start.42) | collective-permute-done | bytes 294944 | tf_op jit(solution)/shard_map/ppermute | solution.py:496
  178.4 3.4 %collective-permute-start.48 = (bf16[1,104,768]{2,1,0:T(8,128)(2,1)S(1)}, bf16[1,104,768]{2,1,0:T(8,128)(2,1)S(1)}, u32[]{:S(2)}, u32[]{:S(2)}) collective-permute-start(bf16[1,104,768]{2,1,0:T(8,128)(2,1)S(1)} %get-tuple-element.159), channel_id=1, source_target_pairs={{0,3},{1,2},{2,1},{3,0},{4,7},{5,6},{6,5},{7,4},{8,11},{9,10},{10,... | collective-permute-start | bytes 479240 | tf_op jit(solution)/shard_map/ppermute | solution.py:496
  181.9 6.2 %collective-permute-start.46 = (bf16[1,104,768]{2,1,0:T(8,128)(2,1)S(1)}, bf16[1,104,768]{2,1,0:T(8,128)(2,1)S(1)}, u32[]{:S(2)}, u32[]{:S(2)}) collective-permute-start(bf16[1,104,768]{2,1,0:T(8,128)(2,1)S(1)} %get-tuple-element.157), channel_id=1, source_target_pairs={{0,2},{1,3},{2,0},{3,1},{4,6},{5,7},{6,4},{7,5},{8,10},{9,11},{10,... | collective-permute-start | bytes 479240 | tf_op jit(solution)/shard_map/ppermute | solution.py:496
  188.6 0.8 slice_bitcast_fusion.2
  189.4 6.4 %collective-permute-done.46 = bf16[1,104,768]{2,1,0:T(8,128)(2,1)S(1)} collective-permute-done((bf16[1,104,768]{2,1,0:T(8,128)(2,1)S(1)}, bf16[1,104,768]{2,1,0:T(8,128)(2,1)S(1)}, u32[]{:S(2)}, u32[]{:S(2)}) %collective-permute-start.46) | collective-permute-done | bytes 159776 | tf_op jit(solution)/shard_map/ppermute | solution.py:496
  197.3 0.7 copy.62
  198.6 0.7 pad_maximum_fusion.7
  (157 shorter events, 13.9 us)
Async XLA Ops:
  0.6 11.8 %copy-start = (f32[3,1,8,768]{3,2,1,0:T(8,128)S(1)}, f32[3,1,8,768]{3,2,1,0:T(8,128)}, u32[]{:S(2)}) copy-start(f32[3,1,8,768]{3,2,1,0:T(8,128)} %param.17) | copy-start | bytes 221188
  2.6 13.9 %collective-permute-start = (bf16[1,104,768]{2,1,0:T(8,128)(2,1)}, bf16[1,104,768]{2,1,0:T(8,128)(2,1)S(1)}, u32[]{:S(2)}, u32[]{:S(2)}) collective-permute-start(bf16[1,104,768]{2,1,0:T(8,128)(2,1)} %bitcast.153), channel_id=1, source_target_pairs={{0,1},{1,0},{2,3},{3,2},{4,5},{5,4},{6,7},{7,6},{8,9},{9,8},{10,11... | collective-permute-start | bytes 479240 | tf_op jit(solution)/shard_map/ppermute | solution.py:476
  5.6 15.0 %collective-permute-start.1 = (bf16[1,104,768]{2,1,0:T(8,128)(2,1)}, bf16[1,104,768]{2,1,0:T(8,128)(2,1)S(1)}, u32[]{:S(2)}, u32[]{:S(2)}) collective-permute-start(bf16[1,104,768]{2,1,0:T(8,128)(2,1)} %bitcast.154), channel_id=1, source_target_pairs={{0,2},{1,3},{2,0},{3,1},{4,6},{5,7},{6,4},{7,5},{8,10},{9,11},{10,... | collective-permute-start | bytes 479240 | tf_op jit(solution)/shard_map/ppermute | solution.py:476
  8.2 12.4 %collective-permute-start.2 = (bf16[1,104,768]{2,1,0:T(8,128)(2,1)}, bf16[1,104,768]{2,1,0:T(8,128)(2,1)S(1)}, u32[]{:S(2)}, u32[]{:S(2)}) collective-permute-start(bf16[1,104,768]{2,1,0:T(8,128)(2,1)} %bitcast.155), channel_id=1, source_target_pairs={{0,3},{1,2},{2,1},{3,0},{4,7},{5,6},{6,5},{7,4},{8,11},{9,10},{10,... | collective-permute-start | bytes 479240 | tf_op jit(solution)/shard_map/ppermute | solution.py:476
  8.2 12.5 %collective-permute-start.3 = (bf16[1,96,768]{2,1,0:T(8,128)(2,1)}, bf16[1,96,768]{2,1,0:T(8,128)(2,1)}, u32[]{:S(2)}, u32[]{:S(2)}) collective-permute-start(bf16[1,96,768]{2,1,0:T(8,128)(2,1)} %bitcast.164), channel_id=1, source_target_pairs={{0,16},{1,17},{2,18},{3,19},{4,12},{5,13},{6,14},{7,15},{8,24},{9,... | collective-permute-start | bytes 442376 | tf_op jit(solution)/shard_map/ppermute | solution.py:547
  12.5 8.2 %copy-start.19 = (bf16[104,768]{1,0:T(8,128)(2,1)S(1)}, bf16[104,768]{1,0:T(8,128)(2,1)}, u32[]{:S(2)}) copy-start(bf16[104,768]{1,0:T(8,128)(2,1)} %shard_map.255) | copy-start | bytes 479236
  16.5 5.8 %copy-start.20 = (bf16[96,768]{1,0:T(8,128)(2,1)S(1)}, bf16[96,768]{1,0:T(8,128)(2,1)}, u32[]{:S(2)}) copy-start(bf16[96,768]{1,0:T(8,128)(2,1)} %param.24) | copy-start | bytes 442372
  20.7 10.5 %collective-permute-start.4 = (bf16[4,104,768]{2,1,0:T(8,128)(2,1)S(1)}, bf16[4,104,768]{2,1,0:T(8,128)(2,1)S(1)}, u32[]{:S(2)}, u32[]{:S(2)}) collective-permute-start(bf16[4,104,768]{2,1,0:T(8,128)(2,1)S(1)} %pad_maximum_fusion), channel_id=1, source_target_pairs={{0,16},{1,17},{2,18},{3,19},{4,12},{5,13},{6,14},{7,15},{8,24},{9,... | collective-permute-start | bytes 1916936 | tf_op jit(solution)/shard_map/ppermute | solution.py:476
  22.4 8.9 %collective-permute-start.5 = (bf16[1,96,768]{2,1,0:T(8,128)(2,1)S(1)}, bf16[1,96,768]{2,1,0:T(8,128)(2,1)S(1)}, u32[]{:S(2)}, u32[]{:S(2)}) collective-permute-start(bf16[1,96,768]{2,1,0:T(8,128)(2,1)S(1)} %bitcast.160), channel_id=1, source_target_pairs={{0,1},{1,0},{2,3},{3,2},{4,5},{5,4},{6,7},{7,6},{8,9},{9,8},{10,11... | collective-permute-start | bytes 442376 | tf_op jit(solution)/shard_map/ppermute | solution.py:476
  25.0 12.7 %collective-permute-start.6 = (bf16[1,96,768]{2,1,0:T(8,128)(2,1)S(1)}, bf16[1,96,768]{2,1,0:T(8,128)(2,1)S(1)}, u32[]{:S(2)}, u32[]{:S(2)}) collective-permute-start(bf16[1,96,768]{2,1,0:T(8,128)(2,1)S(1)} %bitcast.161), channel_id=1, source_target_pairs={{0,2},{1,3},{2,0},{3,1},{4,6},{5,7},{6,4},{7,5},{8,10},{9,11},{10,... | collective-permute-start | bytes 442376 | tf_op jit(solution)/shard_map/ppermute | solution.py:476
  26.1 11.6 %collective-permute-start.7 = (bf16[1,96,768]{2,1,0:T(8,128)(2,1)S(1)}, bf16[1,96,768]{2,1,0:T(8,128)(2,1)S(1)}, u32[]{:S(2)}, u32[]{:S(2)}) collective-permute-start(bf16[1,96,768]{2,1,0:T(8,128)(2,1)S(1)} %bitcast.162), channel_id=1, source_target_pairs={{0,3},{1,2},{2,1},{3,0},{4,7},{5,6},{6,5},{7,4},{8,11},{9,10},{10,... | collective-permute-start | bytes 442376 | tf_op jit(solution)/shard_map/ppermute | solution.py:476
  27.5 13.1 %copy-start.21 = (bf16[768,96]{0,1:T(8,128)(2,1)S(1)}, bf16[768,96]{0,1:T(8,128)(2,1)}, u32[]{:S(2)}) copy-start(bf16[768,96]{0,1:T(8,128)(2,1)} %param.26) | copy-start | bytes 442372
  37.7 21.1 %collective-permute-start.8 = (bf16[8,104,768]{2,1,0:T(8,128)(2,1)S(1)}, bf16[8,104,768]{2,1,0:T(8,128)(2,1)S(1)}, u32[]{:S(2)}, u32[]{:S(2)}) collective-permute-start(bf16[8,104,768]{2,1,0:T(8,128)(2,1)S(1)} %constant_dynamic-update-slice_fusion), channel_id=1, source_target_pairs={{0,8},{1,9},{2,10},{3,11},{4,20},{5,21},{6,22},{7,23},{8,0},{9,1},... | collective-permute-start | bytes 3833864 | tf_op jit(solution)/shard_map/ppermute | solution.py:476
  38.3 17.6 %collective-permute-start.9 = (bf16[4,96,768]{2,1,0:T(8,128)(2,1)S(1)}, bf16[4,96,768]{2,1,0:T(8,128)(2,1)S(1)}, u32[]{:S(2)}, u32[]{:S(2)}) collective-permute-start(bf16[4,96,768]{2,1,0:T(8,128)(2,1)S(1)} %pad_maximum_fusion.1), channel_id=1, source_target_pairs={{0,16},{1,17},{2,18},{3,19},{4,12},{5,13},{6,14},{7,15},{8,24},{9,... | collective-permute-start | bytes 1769480 | tf_op jit(solution)/shard_map/ppermute | solution.py:476
  42.2 13.6 %collective-permute-start.10 = (bf16[2,96,768]{2,1,0:T(8,128)(2,1)}, bf16[2,96,768]{2,1,0:T(8,128)(2,1)S(1)}, u32[]{:S(2)}, u32[]{:S(2)}) collective-permute-start(bf16[2,96,768]{2,1,0:T(8,128)(2,1)} %pad_maximum_fusion.3), channel_id=1, source_target_pairs={{0,1},{1,0},{2,3},{3,2},{4,5},{5,4},{6,7},{7,6},{8,9},{9,8},{10,11... | collective-permute-start | bytes 884744 | tf_op jit(solution)/shard_map/ppermute | solution.py:547
  44.4 11.5 %collective-permute-start.11 = (bf16[2,96,768]{2,1,0:T(8,128)(2,1)}, bf16[2,96,768]{2,1,0:T(8,128)(2,1)S(1)}, u32[]{:S(2)}, u32[]{:S(2)}) collective-permute-start(bf16[2,96,768]{2,1,0:T(8,128)(2,1)} %pad_maximum_fusion.3), channel_id=1, source_target_pairs={{0,2},{1,3},{2,0},{3,1},{4,6},{5,7},{6,4},{7,5},{8,10},{9,11},{10,... | collective-permute-start | bytes 884744 | tf_op jit(solution)/shard_map/ppermute | solution.py:547
  47.5 18.6 %copy-start.24 = (s32[3,1,128]{2,1,0:T(1,128)S(1)}, s32[3,1,128]{2,1,0:T(1,128)}, u32[]{:S(2)}) copy-start(s32[3,1,128]{2,1,0:T(1,128)} %param.16) | copy-start | bytes 4612
  55.9 4.0 %copy-start.22 = (bf16[2,96,768]{2,1,0:T(8,128)(2,1)}, bf16[2,96,768]{2,1,0:T(8,128)(2,1)S(1)}, u32[]{:S(2)}) copy-start(bf16[2,96,768]{2,1,0:T(8,128)(2,1)S(1)} %collective-permute-done.11) | copy-start | bytes 884740
  55.9 10.3 %collective-permute-start.12 = (bf16[8,104,768]{2,1,0:T(8,128)(2,1)S(1)}, bf16[8,104,768]{2,1,0:T(8,128)(2,1)}, u32[]{:S(2)}, u32[]{:S(2)}) collective-permute-start(bf16[8,104,768]{2,1,0:T(8,128)(2,1)S(1)} %constant_dynamic-update-slice_fusion), channel_id=1, source_target_pairs={{0,4},{1,5},{2,6},{3,7},{4,0},{5,1},{6,2},{7,3},{8,12},{9,13},{10,... | collective-permute-start | bytes 3833864 | tf_op jit(solution)/shard_map/ppermute | solution.py:476
  58.8 7.5 %collective-permute-start.13 = (bf16[8,104,768]{2,1,0:T(8,128)(2,1)S(1)}, bf16[8,104,768]{2,1,0:T(8,128)(2,1)}, u32[]{:S(2)}, u32[]{:S(2)}) collective-permute-start(bf16[8,104,768]{2,1,0:T(8,128)(2,1)S(1)} %collective-permute-done.8), channel_id=1, source_target_pairs={{0,4},{1,5},{2,6},{3,7},{4,0},{5,1},{6,2},{7,3},{8,12},{9,13},{10,... | collective-permute-start | bytes 3833864 | tf_op jit(solution)/shard_map/ppermute | solution.py:476
  59.6 19.4 %collective-permute-start.14 = (bf16[8,96,768]{2,1,0:T(8,128)(2,1)}, bf16[8,96,768]{2,1,0:T(8,128)(2,1)}, u32[]{:S(2)}, u32[]{:S(2)}) collective-permute-start(bf16[8,96,768]{2,1,0:T(8,128)(2,1)} %constant_dynamic-update-slice_fusion.5), channel_id=1, source_target_pairs={{0,8},{1,9},{2,10},{3,11},{4,20},{5,21},{6,22},{7,23},{8,0},{9,1},... | collective-permute-start | bytes 3538952 | tf_op jit(solution)/shard_map/ppermute | solution.py:476
  59.9 19.1 %collective-permute-start.15 = (bf16[2,96,768]{2,1,0:T(8,128)(2,1)}, bf16[2,96,768]{2,1,0:T(8,128)(2,1)}, u32[]{:S(2)}, u32[]{:S(2)}) collective-permute-start(bf16[2,96,768]{2,1,0:T(8,128)(2,1)} %pad_maximum_fusion.3), channel_id=1, source_target_pairs={{0,3},{1,2},{2,1},{3,0},{4,7},{5,6},{6,5},{7,4},{8,11},{9,10},{10,... | collective-permute-start | bytes 884744 | tf_op jit(solution)/shard_map/ppermute | solution.py:547
  65.5 17.0 %collective-permute-start.19 = (bf16[4,96,768]{2,1,0:T(8,128)(2,1)S(1)}, bf16[4,96,768]{2,1,0:T(8,128)(2,1)}, u32[]{:S(2)}, u32[]{:S(2)}) collective-permute-start(bf16[4,96,768]{2,1,0:T(8,128)(2,1)S(1)} %pad_maximum_fusion.2), channel_id=1, source_target_pairs={{0,8},{1,9},{2,10},{3,11},{4,20},{5,21},{6,22},{7,23},{8,0},{9,1},... | collective-permute-start | bytes 1769480 | tf_op jit(solution)/shard_map/ppermute | solution.py:547
  67.3 12.3 %copy-start.23 = (bf16[2,96,768]{2,1,0:T(8,128)(2,1)S(1)}, bf16[2,96,768]{2,1,0:T(8,128)(2,1)}, u32[]{:S(2)}) copy-start(bf16[2,96,768]{2,1,0:T(8,128)(2,1)} %copy-done.22) | copy-start | bytes 884740
  79.1 6.5 %collective-permute-start.16 = (bf16[8,96,768]{2,1,0:T(8,128)(2,1)}, bf16[8,96,768]{2,1,0:T(8,128)(2,1)S(1)}, u32[]{:S(2)}, u32[]{:S(2)}) collective-permute-start(bf16[8,96,768]{2,1,0:T(8,128)(2,1)} %constant_dynamic-update-slice_fusion.5), channel_id=1, source_target_pairs={{0,4},{1,5},{2,6},{3,7},{4,0},{5,1},{6,2},{7,3},{8,12},{9,13},{10,... | collective-permute-start | bytes 3538952 | tf_op jit(solution)/shard_map/ppermute | solution.py:476
  79.1 6.4 %collective-permute-start.17 = (bf16[8,96,768]{2,1,0:T(8,128)(2,1)}, bf16[8,96,768]{2,1,0:T(8,128)(2,1)S(1)}, u32[]{:S(2)}, u32[]{:S(2)}) collective-permute-start(bf16[8,96,768]{2,1,0:T(8,128)(2,1)} %collective-permute-done.14), channel_id=1, source_target_pairs={{0,4},{1,5},{2,6},{3,7},{4,0},{5,1},{6,2},{7,3},{8,12},{9,13},{10,... | collective-permute-start | bytes 3538952 | tf_op jit(solution)/shard_map/ppermute | solution.py:476
  79.7 4.2 %collective-permute-start.18 = (bf16[4,96,768]{2,1,0:T(8,128)(2,1)S(1)}, bf16[4,96,768]{2,1,0:T(8,128)(2,1)S(1)}, u32[]{:S(2)}, u32[]{:S(2)}) collective-permute-start(bf16[4,96,768]{2,1,0:T(8,128)(2,1)S(1)} %pad_maximum_fusion.2), channel_id=1, source_target_pairs={{0,4},{1,5},{2,6},{3,7},{4,0},{5,1},{6,2},{7,3},{8,12},{9,13},{10,... | collective-permute-start | bytes 1769480 | tf_op jit(solution)/shard_map/ppermute | solution.py:467
  82.5 3.1 %collective-permute-start.20 = (bf16[4,96,768]{2,1,0:T(8,128)(2,1)}, bf16[4,96,768]{2,1,0:T(8,128)(2,1)S(1)}, u32[]{:S(2)}, u32[]{:S(2)}) collective-permute-start(bf16[4,96,768]{2,1,0:T(8,128)(2,1)} %collective-permute-done.19), channel_id=1, source_target_pairs={{0,4},{1,5},{2,6},{3,7},{4,0},{5,1},{6,2},{7,3},{8,12},{9,13},{10,... | collective-permute-start | bytes 1769480 | tf_op jit(solution)/shard_map/ppermute | solution.py:467
  83.5 9.9 %collective-permute-start.21 = (bf16[4,96,768]{2,1,0:T(8,128)(2,1)S(1)}, bf16[4,96,768]{2,1,0:T(8,128)(2,1)S(1)}, u32[]{:S(2)}, u32[]{:S(2)}) collective-permute-start(bf16[4,96,768]{2,1,0:T(8,128)(2,1)S(1)} %constant_dynamic-update-slice_fusion.10), channel_id=1, source_target_pairs={{0,8},{1,9},{2,10},{3,11},{4,20},{5,21},{6,22},{7,23},{8,0},{9,1},... | collective-permute-start | bytes 1769480 | tf_op jit(solution)/shard_map/ppermute | solution.py:547
  83.8 9.6 %collective-permute-start.22 = (bf16[4,96,768]{2,1,0:T(8,128)(2,1)S(1)}, bf16[4,96,768]{2,1,0:T(8,128)(2,1)S(1)}, u32[]{:S(2)}, u32[]{:S(2)}) collective-permute-start(bf16[4,96,768]{2,1,0:T(8,128)(2,1)S(1)} %constant_dynamic-update-slice_fusion.10), channel_id=1, source_target_pairs={{0,4},{1,5},{2,6},{3,7},{4,0},{5,1},{6,2},{7,3},{8,12},{9,13},{10,... | collective-permute-start | bytes 1769480 | tf_op jit(solution)/shard_map/ppermute | solution.py:467
  85.6 10.0 %copy-start.6 = (bf16[4,384,256]{2,1,0:T(8,128)(2,1)S(1)}, bf16[4,384,256]{2,1,0:T(8,128)(2,1)}, u32[]{:S(2)}) copy-start(bf16[4,384,256]{2,1,0:T(8,128)(2,1)} %get-tuple-element.117.refs_7_) | copy-start | bytes 2359300
  85.6 10.4 %copy-start.15 = (bf16[384,384]{1,0:T(8,128)(2,1)S(1)}, bf16[384,384]{1,0:T(8,128)(2,1)}, u32[]{:S(2)}) copy-start(bf16[384,384]{1,0:T(8,128)(2,1)} %copy-done.14) | copy-start | bytes 884740
  85.6 10.5 %copy-start.25 = (bf16[384,384]{1,0:T(8,128)(2,1)S(1)}, bf16[384,384]{1,0:T(8,128)(2,1)}, u32[]{:S(2)}) copy-start(bf16[384,384]{1,0:T(8,128)(2,1)} %get-tuple-element.116) | copy-start | bytes 884740
  93.4 2.0 %collective-permute-start.23 = (bf16[4,96,768]{2,1,0:T(8,128)(2,1)S(1)}, bf16[4,96,768]{2,1,0:T(8,128)(2,1)S(1)}, u32[]{:S(2)}, u32[]{:S(2)}) collective-permute-start(bf16[4,96,768]{2,1,0:T(8,128)(2,1)S(1)} %collective-permute-done.21), channel_id=1, source_target_pairs={{0,4},{1,5},{2,6},{3,7},{4,0},{5,1},{6,2},{7,3},{8,12},{9,13},{10,... | collective-permute-start | bytes 1769480 | tf_op jit(solution)/shard_map/ppermute | solution.py:467
  95.4 10.1 %collective-permute-start.28 = (bf16[4,384,768]{2,1,0:T(8,128)(2,1)S(1)}, bf16[4,384,768]{2,1,0:T(8,128)(2,1)S(1)}, u32[]{:S(2)}, u32[]{:S(2)}) collective-permute-start(bf16[4,384,768]{2,1,0:T(8,128)(2,1)S(1)} %get-tuple-element.124.refs_1_), channel_id=1, source_target_pairs={{0,4},{1,5},{2,6},{3,7},{4,0},{5,1},{6,2},{7,3},{8,12},{9,13},{10,... | collective-permute-start | bytes 7077896 | tf_op jit(solution)/shard_map/ppermute | solution.py:467
  95.6 6.4 %collective-permute-start.26 = (bf16[4,384,256]{2,1,0:T(8,128)(2,1)S(1)}, bf16[4,384,256]{2,1,0:T(8,128)(2,1)S(1)}, u32[]{:S(2)}, u32[]{:S(2)}) collective-permute-start(bf16[4,384,256]{2,1,0:T(8,128)(2,1)S(1)} %copy-done.6), channel_id=1, source_target_pairs={{0,4},{1,5},{2,6},{3,7},{4,0},{5,1},{6,2},{7,3},{8,12},{9,13},{10,... | collective-permute-start | bytes 2359304 | tf_op jit(solution)/shard_map/ppermute | solution.py:467
  95.9 5.8 %collective-permute-start.24 = (bf16[384,384]{1,0:T(8,128)(2,1)S(1)}, bf16[384,384]{1,0:T(8,128)(2,1)S(1)}, u32[]{:S(2)}, u32[]{:S(2)}) collective-permute-start(bf16[384,384]{1,0:T(8,128)(2,1)S(1)} %copy-done.15), channel_id=1, source_target_pairs={{0,4},{1,5},{2,6},{3,7},{4,0},{5,1},{6,2},{7,3},{8,12},{9,13},{10,... | collective-permute-start | bytes 884744 | tf_op jit(solution)/shard_map/ppermute | solution.py:467
  96.1 5.8 %collective-permute-start.25 = (bf16[384,384]{1,0:T(8,128)(2,1)S(1)}, bf16[384,384]{1,0:T(8,128)(2,1)S(1)}, u32[]{:S(2)}, u32[]{:S(2)}) collective-permute-start(bf16[384,384]{1,0:T(8,128)(2,1)S(1)} %copy-done.25), channel_id=1, source_target_pairs={{0,4},{1,5},{2,6},{3,7},{4,0},{5,1},{6,2},{7,3},{8,12},{9,13},{10,... | collective-permute-start | bytes 884744 | tf_op jit(solution)/shard_map/ppermute | solution.py:467
  101.5 4.1 %collective-permute-start.27 = (bf16[384,384]{1,0:T(8,128)(2,1)S(1)}, bf16[384,384]{1,0:T(8,128)(2,1)S(1)}, u32[]{:S(2)}, u32[]{:S(2)}) collective-permute-start(bf16[384,384]{1,0:T(8,128)(2,1)S(1)} %get-tuple-element.123), channel_id=1, source_target_pairs={{0,4},{1,5},{2,6},{3,7},{4,0},{5,1},{6,2},{7,3},{8,12},{9,13},{10,... | collective-permute-start | bytes 884744 | tf_op jit(solution)/shard_map/ppermute | solution.py:467
  105.3 8.1 %collective-permute-start.29 = (bf16[4,384,768]{2,1,0:T(8,128)(2,1)S(1)}, bf16[4,384,768]{2,1,0:T(8,128)(2,1)S(1)}, u32[]{:S(2)}, u32[]{:S(2)}) collective-permute-start(bf16[4,384,768]{2,1,0:T(8,128)(2,1)S(1)} %bitcast.134), channel_id=1, source_target_pairs={{0,4},{1,5},{2,6},{3,7},{4,0},{5,1},{6,2},{7,3},{8,12},{9,13},{10,... | collective-permute-start | bytes 7077896 | tf_op jit(solution)/shard_map/ppermute | solution.py:467
  107.5 16.3 %collective-permute-start.31 = (bf16[8,96,768]{2,1,0:T(8,128)(2,1)S(1)}, bf16[8,96,768]{2,1,0:T(8,128)(2,1)S(1)}, u32[]{:S(2)}, u32[]{:S(2)}) collective-permute-start(bf16[8,96,768]{2,1,0:T(8,128)(2,1)S(1)} %bitcast.140), channel_id=1, source_target_pairs={{0,8},{1,9},{2,10},{3,11},{4,20},{5,21},{6,22},{7,23},{8,0},{9,1},... | collective-permute-start | bytes 3538952 | tf_op jit(solution)/shard_map/ppermute | solution.py:496
  107.8 5.5 %copy-start.12 = (bf16[384,384]{1,0:T(8,128)(2,1)S(1)}, bf16[384,384]{1,0:T(8,128)(2,1)}, u32[]{:S(2)}) copy-start(bf16[384,384]{1,0:T(8,128)(2,1)} %get-tuple-element.132.refs_0_) | copy-start | bytes 884740
  116.7 20.0 %collective-permute-start.32 = (bf16[8,96,768]{2,1,0:T(8,128)(2,1)S(1)}, bf16[8,96,768]{2,1,0:T(8,128)(2,1)S(1)}, u32[]{:S(2)}, u32[]{:S(2)}) collective-permute-start(bf16[8,96,768]{2,1,0:T(8,128)(2,1)S(1)} %bitcast.150), channel_id=1, source_target_pairs={{0,8},{1,9},{2,10},{3,11},{4,20},{5,21},{6,22},{7,23},{8,0},{9,1},... | collective-permute-start | bytes 3538952 | tf_op jit(solution)/shard_map/ppermute | solution.py:496
  118.5 1.9 collective-permute-start.30
  118.5 5.3 %copy-start.4 = (f32[4,3,128,384]{3,2,1,0:T(8,128)S(1)}, f32[4,3,128,384]{3,2,1,0:T(8,128)}, u32[]{:S(2)}) copy-start(f32[4,3,128,384]{3,2,1,0:T(8,128)} %get-tuple-element.138.p_ref) | copy-start | bytes 7077892
  118.5 5.3 %copy-start.5 = (bf16[4,384,576]{2,1,0:T(8,128)(2,1)S(1)}, bf16[4,384,576]{2,1,0:T(8,128)(2,1)}, u32[]{:S(2)}) copy-start(bf16[4,384,576]{2,1,0:T(8,128)(2,1)} %get-tuple-element.137.qkv_ref) | copy-start | bytes 5308420
  132.4 6.8 %collective-permute-start.33 = (bf16[2,384,640]{2,1,0:T(8,128)(2,1)S(1)}, bf16[2,384,640]{2,1,0:T(8,128)(2,1)S(1)}, u32[]{:S(2)}, u32[]{:S(2)}) collective-permute-start(bf16[2,384,640]{2,1,0:T(8,128)(2,1)S(1)} %get-tuple-element.148.refs_1_.low_ref), channel_id=1, source_target_pairs={{0,4},{1,5},{2,6},{3,7},{4,0},{5,1},{6,2},{7,3},{8,12},{9,13},{10,... | collective-permute-start | bytes 2949128 | tf_op jit(solution)/shard_map/ppermute | solution.py:467
  132.5 6.8 %collective-permute-start.34 = (bf16[2,384,640]{2,1,0:T(8,128)(2,1)S(1)}, bf16[2,384,640]{2,1,0:T(8,128)(2,1)S(1)}, u32[]{:S(2)}, u32[]{:S(2)}) collective-permute-start(bf16[2,384,640]{2,1,0:T(8,128)(2,1)S(1)} %get-tuple-element.149.refs_2_.high_ref), channel_id=1, source_target_pairs={{0,4},{1,5},{2,6},{3,7},{4,0},{5,1},{6,2},{7,3},{8,12},{9,13},{10,... | collective-permute-start | bytes 2949128 | tf_op jit(solution)/shard_map/ppermute | solution.py:467
  133.3 4.0 %copy-start.18 = (pred[768,768]{1,0:T(32,128)(4,1)S(1)}, pred[768,768]{1,0:T(32,128)(4,1)}, u32[]{:S(2)}) copy-start(pred[768,768]{1,0:T(32,128)(4,1)} %copy-done.17) | copy-start | bytes 1769476
  133.3 10.3 %collective-permute-start.36 = (bf16[4,96,768]{2,1,0:T(8,128)(2,1)S(1)}, bf16[4,96,768]{2,1,0:T(8,128)(2,1)S(1)}, u32[]{:S(2)}, u32[]{:S(2)}) collective-permute-start(bf16[4,96,768]{2,1,0:T(8,128)(2,1)S(1)} %get-tuple-element.212), channel_id=1, source_target_pairs={{0,16},{1,17},{2,18},{3,19},{4,12},{5,13},{6,14},{7,15},{8,24},{9,... | collective-permute-start | bytes 1769480 | tf_op jit(solution)/shard_map/ppermute | solution.py:496
  136.9 12.6 %collective-permute-start.37 = (bf16[4,96,768]{2,1,0:T(8,128)(2,1)S(1)}, bf16[4,96,768]{2,1,0:T(8,128)(2,1)S(1)}, u32[]{:S(2)}, u32[]{:S(2)}) collective-permute-start(bf16[4,96,768]{2,1,0:T(8,128)(2,1)S(1)} %get-tuple-element.214), channel_id=1, source_target_pairs={{0,16},{1,17},{2,18},{3,19},{4,12},{5,13},{6,14},{7,15},{8,24},{9,... | collective-permute-start | bytes 1769480 | tf_op jit(solution)/shard_map/ppermute | solution.py:496
  137.3 2.0 collective-permute-start.35
  149.6 17.3 %collective-permute-start.38 = (bf16[8,104,768]{2,1,0:T(8,128)(2,1)S(1)}, bf16[8,104,768]{2,1,0:T(8,128)(2,1)S(1)}, u32[]{:S(2)}, u32[]{:S(2)}) collective-permute-start(bf16[8,104,768]{2,1,0:T(8,128)(2,1)S(1)} %bitcast.149), channel_id=1, source_target_pairs={{0,8},{1,9},{2,10},{3,11},{4,20},{5,21},{6,22},{7,23},{8,0},{9,1},... | collective-permute-start | bytes 3833864 | tf_op jit(solution)/shard_map/ppermute | solution.py:496
  150.1 7.4 %copy-start.3 = (bf16[768,768]{1,0:T(8,128)(2,1)S(1)}, bf16[768,768]{1,0:T(8,128)(2,1)}, u32[]{:S(2)}) copy-start(bf16[768,768]{1,0:T(8,128)(2,1)} %copy-done.2) | copy-start | bytes 3538948
  150.2 18.9 %collective-permute-start.41 = (bf16[2,96,768]{2,1,0:T(8,128)(2,1)S(1)}, bf16[2,96,768]{2,1,0:T(8,128)(2,1)S(1)}, u32[]{:S(2)}, u32[]{:S(2)}) collective-permute-start(bf16[2,96,768]{2,1,0:T(8,128)(2,1)S(1)} %pad_maximum_fusion.4), channel_id=1, source_target_pairs={{0,1},{1,0},{2,3},{3,2},{4,5},{5,4},{6,7},{7,6},{8,9},{9,8},{10,11... | collective-permute-start | bytes 884744 | tf_op jit(solution)/shard_map/ppermute | solution.py:496
  153.9 23.6 %collective-permute-start.42 = (bf16[2,96,768]{2,1,0:T(8,128)(2,1)S(1)}, bf16[2,96,768]{2,1,0:T(8,128)(2,1)S(1)}, u32[]{:S(2)}, u32[]{:S(2)}) collective-permute-start(bf16[2,96,768]{2,1,0:T(8,128)(2,1)S(1)} %pad_maximum_fusion.5), channel_id=1, source_target_pairs={{0,2},{1,3},{2,0},{3,1},{4,6},{5,7},{6,4},{7,5},{8,10},{9,11},{10,... | collective-permute-start | bytes 884744 | tf_op jit(solution)/shard_map/ppermute | solution.py:496
  156.0 21.5 %collective-permute-start.43 = (bf16[2,96,768]{2,1,0:T(8,128)(2,1)S(1)}, bf16[2,96,768]{2,1,0:T(8,128)(2,1)S(1)}, u32[]{:S(2)}, u32[]{:S(2)}) collective-permute-start(bf16[2,96,768]{2,1,0:T(8,128)(2,1)S(1)} %pad_maximum_fusion.6), channel_id=1, source_target_pairs={{0,3},{1,2},{2,1},{3,0},{4,7},{5,6},{6,5},{7,4},{8,11},{9,10},{10,... | collective-permute-start | bytes 884744 | tf_op jit(solution)/shard_map/ppermute | solution.py:496
  167.0 11.2 %collective-permute-start.40 = (bf16[1,104,768]{2,1,0:T(8,128)(2,1)S(1)}, bf16[1,104,768]{2,1,0:T(8,128)(2,1)S(1)}, u32[]{:S(2)}, u32[]{:S(2)}) collective-permute-start(bf16[1,104,768]{2,1,0:T(8,128)(2,1)S(1)} %get-tuple-element.154), channel_id=1, source_target_pairs={{0,16},{1,17},{2,18},{3,19},{4,12},{5,13},{6,14},{7,15},{8,24},{9,... | collective-permute-start | bytes 479240 | tf_op jit(solution)/shard_map/ppermute | solution.py:496
  167.3 10.9 %collective-permute-start.47 = (bf16[1,104,768]{2,1,0:T(8,128)(2,1)S(1)}, bf16[1,104,768]{2,1,0:T(8,128)(2,1)S(1)}, u32[]{:S(2)}, u32[]{:S(2)}) collective-permute-start(bf16[1,104,768]{2,1,0:T(8,128)(2,1)S(1)} %get-tuple-element.158), channel_id=1, source_target_pairs={{0,16},{1,17},{2,18},{3,19},{4,12},{5,13},{6,14},{7,15},{8,24},{9,... | collective-permute-start | bytes 479240 | tf_op jit(solution)/shard_map/ppermute | solution.py:496
  169.1 9.1 %collective-permute-start.45 = (bf16[1,104,768]{2,1,0:T(8,128)(2,1)S(1)}, bf16[1,104,768]{2,1,0:T(8,128)(2,1)S(1)}, u32[]{:S(2)}, u32[]{:S(2)}) collective-permute-start(bf16[1,104,768]{2,1,0:T(8,128)(2,1)S(1)} %get-tuple-element.156), channel_id=1, source_target_pairs={{0,16},{1,17},{2,18},{3,19},{4,12},{5,13},{6,14},{7,15},{8,24},{9,... | collective-permute-start | bytes 479240 | tf_op jit(solution)/shard_map/ppermute | solution.py:496
  177.6 11.8 %collective-permute-start.39 = (bf16[1,104,768]{2,1,0:T(8,128)(2,1)S(1)}, bf16[1,104,768]{2,1,0:T(8,128)(2,1)S(1)}, u32[]{:S(2)}, u32[]{:S(2)}) collective-permute-start(bf16[1,104,768]{2,1,0:T(8,128)(2,1)S(1)} %get-tuple-element.153), channel_id=1, source_target_pairs={{0,16},{1,17},{2,18},{3,19},{4,12},{5,13},{6,14},{7,15},{8,24},{9,... | collective-permute-start | bytes 479240 | tf_op jit(solution)/shard_map/ppermute | solution.py:496
  178.4 11.0 %collective-permute-start.48 = (bf16[1,104,768]{2,1,0:T(8,128)(2,1)S(1)}, bf16[1,104,768]{2,1,0:T(8,128)(2,1)S(1)}, u32[]{:S(2)}, u32[]{:S(2)}) collective-permute-start(bf16[1,104,768]{2,1,0:T(8,128)(2,1)S(1)} %get-tuple-element.159), channel_id=1, source_target_pairs={{0,3},{1,2},{2,1},{3,0},{4,7},{5,6},{6,5},{7,4},{8,11},{9,10},{10,... | collective-permute-start | bytes 479240 | tf_op jit(solution)/shard_map/ppermute | solution.py:496
  181.9 14.0 %collective-permute-start.46 = (bf16[1,104,768]{2,1,0:T(8,128)(2,1)S(1)}, bf16[1,104,768]{2,1,0:T(8,128)(2,1)S(1)}, u32[]{:S(2)}, u32[]{:S(2)}) collective-permute-start(bf16[1,104,768]{2,1,0:T(8,128)(2,1)S(1)} %get-tuple-element.157), channel_id=1, source_target_pairs={{0,2},{1,3},{2,0},{3,1},{4,6},{5,7},{6,4},{7,5},{8,10},{9,11},{10,... | collective-permute-start | bytes 479240 | tf_op jit(solution)/shard_map/ppermute | solution.py:496
  188.1 7.7 %collective-permute-start.44 = (bf16[1,104,768]{2,1,0:T(8,128)(2,1)S(1)}, bf16[1,104,768]{2,1,0:T(8,128)(2,1)S(1)}, u32[]{:S(2)}, u32[]{:S(2)}) collective-permute-start(bf16[1,104,768]{2,1,0:T(8,128)(2,1)S(1)} %get-tuple-element.155), channel_id=1, source_target_pairs={{0,1},{1,0},{2,3},{3,2},{4,5},{5,4},{6,7},{7,6},{8,9},{9,8},{10,11... | collective-permute-start | bytes 479240 | tf_op jit(solution)/shard_map/ppermute | solution.py:496
  (11 other events, 20.3 us)

commit v10 on v9

--- a/solution.py
+++ b/solution.py
@@ -400,6 +400,23 @@
         dx = acc_ref[...] + da_ref[...]
         perm = perm_ref[...]
         dx_ref[...] = sum(nt(part, perm) for part in thirds(dx))
+
+
+def finish(total_ref, qkv_ref, out_ref, qv_ref, *vector_refs):
+    total = total_ref[...]
+    rows, hc = qkv_ref.shape[1:]
+    for c in range(3):
+        qkv_ref[c] = total[:rows, c * hc : (c + 1) * hc]
+    out_ref[...] = total[:rows, 3 * hc :].T
+    row = total[rows : rows + 1]
+    at = 0
+    for n, ref in enumerate(vector_refs):
+        if n == 6:
+            size = qv_ref.shape[1]
+            qv_ref[...] = jnp.concatenate([row[:, at : at + size], row[:, at + size : at + 2 * size]], axis=0)
+            at += 2 * size
+        ref[...] = row[:, at : at + ref.shape[1]]
+        at += ref.shape[1]
 
 
 def whole(a):
@@ -749,9 +766,14 @@
     if pairwise:
         s_qo.stage("2", n_t, dx)
         s_qo.stage("Z", 1, *got_z)
-        g_down, g_up, g_qo = both.keep[0], both.keep[1], s_qo.keep[0]
-        g_v = g_qo[BLK, :n_vec]
-        g_qo = g_qo[:BLK]
+        g_qkv, g_out, g_qv, *vo = pl.pallas_call(
+            finish,
+            out_shape=[sds(qkv_weight.shape, f32), sds(out_weight.shape, f32), sds(qv_bias.shape, f32)]
+            + [sds((1, dv), f32)] * 6 + [sds((1, up_bias.shape[0]), f32)],
+            compiler_params=SMALL,
+        )(s_qo.keep[0])
+        vo = [v[0] for v in vo]
+        g_down, g_up = both.keep[0], both.keep[1]
     else:
         def joined(*halves_of):
             g = jnp.concatenate([part[:, :, :BLK] for half in halves_of for part in half])
@@ -773,18 +795,14 @@
             [g_rows[:, a:b].reshape(n_dp * n_t, -1) for a, b in zip(cuts[:-1], cuts[1:])], axis=1
         )
         g_v = lax.psum_scatter(g_v, AXES, scatter_dimension=0)
-    vo = [g_v[j * dv : (j + 1) * dv] for j in range(8)]
+        g_qkv = jnp.stack([g_qo[:, c * hc : (c + 1) * hc] for c in range(3)])
+        g_out = g_qo[:, 3 * hc :].T
+        vo = [g_v[j * dv : (j + 1) * dv] for j in range(6)] + [g_v[8 * dv :]]
+        g_qv = jnp.stack([g_v[6 * dv : 7 * dv], g_v[7 * dv : 8 * dv]])
     return (
         pooled.reshape(micro, seqs, segs, D),
         dx.reshape(micro, tokens, D),
-        jnp.stack([g_qo[:, c * hc : (c + 1) * hc] for c in range(3)]),
-        jnp.stack([vo[6], vo[7]]),
-        g_qo[:, 3 * hc :].T,
-        vo[0], vo[1], vo[2],
-        g_up,
-        g_v[8 * dv :],
-        g_down.T,
-        vo[3], vo[4], vo[5],
+        g_qkv, g_qv, g_out, vo[0], vo[1], vo[2], g_up, vo[6], g_down.T, vo[3], vo[4], vo[5],
     )
 
 

time: 200 us -> 198 us (0.990)
  local copies, waits for them, and re-layouts: 12.4 us -> 10.3 us
    unnamed x63 -> x62, local copies, waits for them, and re-layouts: 6.86 us -> 6.1 us
  transfers between devices with their start and end apart: 49 -> 49, of which waited for: 16 -> 16; matrix products, arithmetic and copies ran while one was open for 8% -> 8% of each run, Pallas kernels for 29% -> 30%
where the time goes in v10:
time: 198 us; the launch traced here: 197 us
  waiting for transfers between devices  63.5 us (32%)
  Pallas kernels  61.6 us (31%)
  starting transfers between devices  51.8 us (26%)
  local copies, waits for them, and re-layouts  10.3 us (5%)
  other arithmetic  5.39 us (3%)
  matrix products  2.99 us (2%)
    pallas_call x11, Pallas kernels, call(): pl.pallas_call(body, grid=(n_t,), in_specs=[s for _, s in ins], out_specs...  58 us
    ppermute x15, waiting for transfers between devices, stage(): lax.ppermute(after(s, *done), AXES, tables[n // pieces])  28.9 us
    ppermute x15, starting transfers between devices, stage(): lax.ppermute(after(s, *done), AXES, tables[n // pieces])  23.5 us
    ppermute x14, waiting for transfers between devices, send(): lax.ppermute(after(h, *done), AXES, t)  17.1 us
    ppermute x14, starting transfers between devices, send(): lax.ppermute(after(h, *done), AXES, t)  15.3 us
    ppermute x6, waiting for transfers between devices, move(): return lax.ppermute(after(value, *done), AXES, tables[name][way])  13.9 us
    ppermute x6, starting transfers between devices, move(): return lax.ppermute(after(value, *done), AXES, tables[name][way])  10.5 us
    unnamed x62, local copies, waits for them, and re-layouts  6.1 us
  transfers between devices with their start and end apart: 49, of which 16 were waited for; matrix products, arithmetic and copies ran while one was open for 8% of the time, Pallas kernels for 30%

profile of v10, /device:TPU:0, one launch (start us, length us, event | category | flops | bytes accessed | tf_op | source)
XLA Modules:
  0.0 197.0 jit_solution(3449852969107006486)
XLA Ops:
  0.7 2.0 shard_map.255
  2.6 3.0 %collective-permute-start = (bf16[1,104,768]{2,1,0:T(8,128)(2,1)}, bf16[1,104,768]{2,1,0:T(8,128)(2,1)S(1)}, u32[]{:S(2)}, u32[]{:S(2)}) collective-permute-start(bf16[1,104,768]{2,1,0:T(8,128)(2,1)} %bitcast.137), channel_id=1, source_target_pairs={{0,1},{1,0},{2,3},{3,2},{4,5},{5,4},{6,7},{7,6},{8,9},{9,8},{10,11... | collective-permute-start | bytes 479240 | tf_op jit(solution)/shard_map/ppermute | solution.py:493
  5.6 2.6 %collective-permute-start.1 = (bf16[1,104,768]{2,1,0:T(8,128)(2,1)}, bf16[1,104,768]{2,1,0:T(8,128)(2,1)S(1)}, u32[]{:S(2)}, u32[]{:S(2)}) collective-permute-start(bf16[1,104,768]{2,1,0:T(8,128)(2,1)} %bitcast.138), channel_id=1, source_target_pairs={{0,2},{1,3},{2,0},{3,1},{4,6},{5,7},{6,4},{7,5},{8,10},{9,11},{10,... | collective-permute-start | bytes 479240 | tf_op jit(solution)/shard_map/ppermute | solution.py:493
  8.2 1.7 collective-permute-start.3
  10.4 0.7 copy.30
  12.5 1.0 convolution_bitcast_fusion.pg_ref
  13.6 0.7 shard_map.254
  14.3 0.8 copy-done.7
  15.1 0.7 copy-done.10
  15.8 0.7 copy-done.14
  16.6 4.1 %collective-permute-done.1 = bf16[1,104,768]{2,1,0:T(8,128)(2,1)S(1)} collective-permute-done((bf16[1,104,768]{2,1,0:T(8,128)(2,1)}, bf16[1,104,768]{2,1,0:T(8,128)(2,1)S(1)}, u32[]{:S(2)}, u32[]{:S(2)}) %collective-permute-start.1) | collective-permute-done | bytes 159776 | tf_op jit(solution)/shard_map/ppermute | solution.py:493
  20.7 1.6 collective-permute-start.4
  22.4 2.6 %collective-permute-start.5 = (bf16[1,96,768]{2,1,0:T(8,128)(2,1)S(1)}, bf16[1,96,768]{2,1,0:T(8,128)(2,1)S(1)}, u32[]{:S(2)}, u32[]{:S(2)}) collective-permute-start(bf16[1,96,768]{2,1,0:T(8,128)(2,1)S(1)} %bitcast.142), channel_id=1, source_target_pairs={{0,1},{1,0},{2,3},{3,2},{4,5},{5,4},{6,7},{7,6},{8,9},{9,8},{10,11... | collective-permute-start | bytes 442376 | tf_op jit(solution)/shard_map/ppermute | solution.py:493
  25.0 1.1 collective-permute-start.6
  26.1 1.4 collective-permute-start.7
  27.5 3.7 %collective-permute-done.4 = bf16[4,104,768]{2,1,0:T(8,128)(2,1)S(1)} collective-permute-done((bf16[4,104,768]{2,1,0:T(8,128)(2,1)S(1)}, bf16[4,104,768]{2,1,0:T(8,128)(2,1)S(1)}, u32[]{:S(2)}, u32[]{:S(2)}) %collective-permute-start.4) | collective-permute-done | bytes 639008 | tf_op jit(solution)/shard_map/ppermute | solution.py:493
  31.3 6.4 %collective-permute-done.6 = bf16[1,96,768]{2,1,0:T(8,128)(2,1)S(1)} collective-permute-done((bf16[1,96,768]{2,1,0:T(8,128)(2,1)S(1)}, bf16[1,96,768]{2,1,0:T(8,128)(2,1)S(1)}, u32[]{:S(2)}, u32[]{:S(2)}) %collective-permute-start.6) | collective-permute-done | bytes 147488 | tf_op jit(solution)/shard_map/ppermute | solution.py:493
  38.3 1.6 collective-permute-start.9
  39.9 0.7 constant_dynamic-update-slice_fusion.9
  40.6 1.7 pad_maximum_fusion.3
  42.2 2.1 %collective-permute-start.10 = (bf16[2,96,768]{2,1,0:T(8,128)(2,1)}, bf16[2,96,768]{2,1,0:T(8,128)(2,1)S(1)}, u32[]{:S(2)}, u32[]{:S(2)}) collective-permute-start(bf16[2,96,768]{2,1,0:T(8,128)(2,1)} %pad_maximum_fusion.3), channel_id=1, source_target_pairs={{0,1},{1,0},{2,3},{3,2},{4,5},{5,4},{6,7},{7,6},{8,9},{9,8},{10,11... | collective-permute-start | bytes 884744 | tf_op jit(solution)/shard_map/ppermute | solution.py:564
  44.4 1.1 collective-permute-start.11
  45.5 0.7 constant_dynamic-update-slice_fusion.8
  46.2 0.7 constant_dynamic-update-slice_fusion.7
  46.8 0.7 constant_dynamic-update-slice_fusion.6
  47.5 8.4 %collective-permute-done.10 = bf16[2,96,768]{2,1,0:T(8,128)(2,1)S(1)} collective-permute-done((bf16[2,96,768]{2,1,0:T(8,128)(2,1)}, bf16[2,96,768]{2,1,0:T(8,128)(2,1)S(1)}, u32[]{:S(2)}, u32[]{:S(2)}) %collective-permute-start.10) | collective-permute-done | bytes 294944 | tf_op jit(solution)/shard_map/ppermute | solution.py:564
  56.0 2.8 %collective-permute-done.8 = bf16[8,104,768]{2,1,0:T(8,128)(2,1)S(1)} collective-permute-done((bf16[8,104,768]{2,1,0:T(8,128)(2,1)S(1)}, bf16[8,104,768]{2,1,0:T(8,128)(2,1)S(1)}, u32[]{:S(2)}, u32[]{:S(2)}) %collective-permute-start.8) | collective-permute-done | bytes 1277984 | tf_op jit(solution)/shard_map/ppermute | solution.py:493
  58.8 0.9 constant_dynamic-update-slice_fusion.5
  59.9 4.6 %collective-permute-start.15 = (bf16[2,96,768]{2,1,0:T(8,128)(2,1)}, bf16[2,96,768]{2,1,0:T(8,128)(2,1)}, u32[]{:S(2)}, u32[]{:S(2)}) collective-permute-start(bf16[2,96,768]{2,1,0:T(8,128)(2,1)} %pad_maximum_fusion.3), channel_id=1, source_target_pairs={{0,3},{1,2},{2,1},{3,0},{4,7},{5,6},{6,5},{7,4},{8,11},{9,10},{10,... | collective-permute-start | bytes 884744 | tf_op jit(solution)/shard_map/ppermute | solution.py:564
  64.5 1.0 pad_maximum_fusion.2
  66.2 1.1 copy-done.8
  67.3 11.7 %shard_map.256 = (bf16[4,384,576]{2,1,0:T(8,128)(2,1)}, f32[4,3,128,384]{3,2,1,0:T(8,128)}, bf16[4,384,256]{2,1,0:T(8,128)(2,1)}, f32[384,768]{1,0:T(8,128)S(1)}...) custom-call(bf16[384,768]{1,0:T(8,128)(2,1)S(1)} %copy-done.8, ...), custom_call_target="tpu_custom_call" | custom-call | flops 300000000 | tf_op jit(solution)/shard_map/pallas_call | solution.py:449
  79.8 2.7 %collective-permute-done.19 = bf16[4,96,768]{2,1,0:T(8,128)(2,1)} collective-permute-done((bf16[4,96,768]{2,1,0:T(8,128)(2,1)S(1)}, bf16[4,96,768]{2,1,0:T(8,128)(2,1)}, u32[]{:S(2)}, u32[]{:S(2)}) %collective-permute-start.19) | collective-permute-done | bytes 589856 | tf_op jit(solution)/shard_map/ppermute | solution.py:564
  82.5 1.0 constant_dynamic-update-slice_fusion.10
  84.1 1.4 collective-permute-done.20
  85.6 5.0 %shard_map.257 = (bf16[4,384,768]{2,1,0:T(8,128)(2,1)S(1)}, f32[4,384,768]{2,1,0:T(8,128)S(1)}) custom-call(bf16[384,768]{1,0:T(8,128)(2,1)S(1)} %get-tuple-element.107.n_ref, bf16[2,4,96,768]{3,2,1,0:T(8,128)(2,1)} %bitcast.23.w0_ref, bf16[2,4,96,768]{3,2,1,0:T(8,128)(2,1)} %bitcast.24.w1_ref, bf16[2,4,96,768]{3,2,1,0:T(8,128)(2,1)S(1)} %bitcast.125, ...), custom_call_target="tpu_custom_call" | custom-call | flops 120000000 | tf_op jit(solution)/shard_map/pallas_call | solution.py:449
  90.6 2.8 %collective-permute-done.21 = bf16[4,96,768]{2,1,0:T(8,128)(2,1)S(1)} collective-permute-done((bf16[4,96,768]{2,1,0:T(8,128)(2,1)S(1)}, bf16[4,96,768]{2,1,0:T(8,128)(2,1)S(1)}, u32[]{:S(2)}, u32[]{:S(2)}) %collective-permute-start.21) | collective-permute-done | bytes 589856 | tf_op jit(solution)/shard_map/ppermute | solution.py:564
  93.4 2.0 %collective-permute-done.23 = bf16[4,96,768]{2,1,0:T(8,128)(2,1)S(1)} collective-permute-done((bf16[4,96,768]{2,1,0:T(8,128)(2,1)S(1)}, bf16[4,96,768]{2,1,0:T(8,128)(2,1)S(1)}, u32[]{:S(2)}, u32[]{:S(2)}) %collective-permute-start.23) | collective-permute-done | bytes 589856 | tf_op jit(solution)/shard_map/ppermute | solution.py:484
  96.5 5.0 %shard_map.258 = (f32[3,8,768]{2,1,0:T(8,128)S(1)}, f32[384,768]{1,0:T(8,128)S(1)}, bf16[384,768]{1,0:T(8,128)(2,1)S(1)}, bf16[384,384]{1,0:T(8,128)(2,1)S(1)}, ...) custom-call(bf16[2,2,384,768]{3,2,1,0:T(8,128)(2,1)S(1)} %bitcast.98, bf16[2,2,96,768]{3,2,1,0:T(8,128)(2,1)S(1)} %bitcast.103, ...), custom_call_target="tpu_custom_call" | custom-call | flops 165000000 | tf_op jit(solution)/shard_map/pallas_call | solution.py:449
  101.9 3.4 %shard_map.259 = (bf16[2,2,384,768]{3,2,1,0:T(8,128)(2,1)S(1)}, f32[2,2,1,768]{3,2,1,0:T(1,128)S(1)}) custom-call(bf16[384,768]{1,0:T(8,128)(2,1)S(1)} %get-tuple-element.123.dbb_ref, bf16[2,2,96,768]{3,2,1,0:T(8,128)(2,1)S(1)} %bitcast.104, bf16[2,2,96,768]{3,2,1,0:T(8,128)(2,1)} %bitcast.29.w1_ref, bf16[2,2,96,768]{3,2,1,0:T(8,128)(2,1)S(1)} %bitcast.109, ...), custom_call_target="tpu_custom_call" | custom-call | flops 105000000 | tf_op jit(solution)/shard_map/pallas_call | solution.py:449
  105.6 1.9 shard_map.260
  107.9 5.5 %shard_map.261 = (f32[384,768]{1,0:T(8,128)S(1)}, bf16[384,768]{1,0:T(8,128)(2,1)S(1)}, bf16[384,384]{1,0:T(8,128)(2,1)S(1)}, bf16[384,384]{1,0:T(8,128)(2,1)S(1)}, f32[3,768]{1,0:T(4,128)S(1)}) custom-call(bf16[4,384,768]{2,1,0:T(8,128)(2,1)S(1)} %bitcast.119, bf16[2,4,96,768]{3,2,1,0:T(8,128)(2,1)} %bitcast.23.w0_ref, ...), custom_call_target="tpu_custom_call" | custom-call | flops 60000002048 | tf_op jit(solution)/shard_map/pallas_call | solution.py:449
  113.4 3.3 %shard_map.262 = (bf16[2,4,96,768]{3,2,1,0:T(8,128)(2,1)S(1)}, bf16[2,4,96,768]{3,2,1,0:T(8,128)(2,1)S(1)}) custom-call(bf16[384,384]{1,0:T(8,128)(2,1)S(1)} %copy-done.12, bf16[4,384,768]{2,1,0:T(8,128)(2,1)S(1)} %bitcast.120, bf16[384,384]{1,0:T(8,128)(2,1)S(1)} %collective-permute-done.25.refs_2_, bf16[4,384,768]{2,1,0:T(8,128)(2,1)S(1)} %collective-permute-done.29.refs_3_), custom_call_target="tpu_custom_call" | custom-call | flops 60000000 | tf_op jit(solution)/shard_map/pallas_call | solution.py:449
  116.7 1.8 collective-permute-start.32
  118.5 1.9 shard_map.263
  120.5 3.3 %collective-permute-done.31 = bf16[8,96,768]{2,1,0:T(8,128)(2,1)S(1)} collective-permute-done((bf16[8,96,768]{2,1,0:T(8,128)(2,1)S(1)}, bf16[8,96,768]{2,1,0:T(8,128)(2,1)S(1)}, u32[]{:S(2)}, u32[]{:S(2)}) %collective-permute-start.31) | collective-permute-done | bytes 1179680 | tf_op jit(solution)/shard_map/ppermute | solution.py:513
  123.8 8.7 %shard_map.264 = (bf16[2,384,640]{2,1,0:T(8,128)(2,1)S(1)}, bf16[2,384,640]{2,1,0:T(8,128)(2,1)S(1)}, f32[4,4,768]{2,1,0:T(4,128)S(1)}, f32[4,4,768]{2,1,0:T(4,128)S(1)}) custom-call(bf16[384,768]{1,0:T(8,128)(2,1)S(1)} %get-tuple-element.146.dab_ref, bf16[2,4,104,768]{3,2,1,0:T(8,128)(2,1)S(1)} %bitcast.96, bf16[2,4,104,768]{3,2,1,0:T(8,128)(2,1)S(1)} %bitcast.101, ...), custom_call_target="tpu_custom_call" | custom-call | flops 240000000 | tf_op jit(solution)/shard_map/pallas_call | solution.py:449
  133.7 3.0 %collective-permute-done.32 = bf16[8,96,768]{2,1,0:T(8,128)(2,1)S(1)} collective-permute-done((bf16[8,96,768]{2,1,0:T(8,128)(2,1)S(1)}, bf16[8,96,768]{2,1,0:T(8,128)(2,1)S(1)}, u32[]{:S(2)}, u32[]{:S(2)}) %collective-permute-start.32) | collective-permute-done | bytes 1179680 | tf_op jit(solution)/shard_map/ppermute | solution.py:513
  137.3 2.0 fusion
  139.3 4.3 %shard_map.265 = (bf16[2,4,104,768]{3,2,1,0:T(8,128)(2,1)S(1)}, bf16[2,4,104,768]{3,2,1,0:T(8,128)(2,1)S(1)}) custom-call(bf16[384,384]{1,0:T(8,128)(2,1)S(1)} %copy-done.11, bf16[2,384,640]{2,1,0:T(8,128)(2,1)S(1)} %get-tuple-element.158.refs_1_.low_ref, bf16[2,384,640]{2,1,0:T(8,128)(2,1)S(1)} %get-tuple-element.159.refs_2_.high_ref, ...), custom_call_target="tpu_custom_call" | custom-call | flops 60000000 | tf_op jit(solution)/shard_map/pallas_call | solution.py:449
  143.6 6.0 %collective-permute-done.37 = bf16[4,96,768]{2,1,0:T(8,128)(2,1)S(1)} collective-permute-done((bf16[4,96,768]{2,1,0:T(8,128)(2,1)S(1)}, bf16[4,96,768]{2,1,0:T(8,128)(2,1)S(1)}, u32[]{:S(2)}, u32[]{:S(2)}) %collective-permute-start.37) | collective-permute-done | bytes 589856 | tf_op jit(solution)/shard_map/ppermute | solution.py:513
  150.2 3.7 %collective-permute-start.41 = (bf16[2,96,768]{2,1,0:T(8,128)(2,1)S(1)}, bf16[2,96,768]{2,1,0:T(8,128)(2,1)S(1)}, u32[]{:S(2)}, u32[]{:S(2)}) collective-permute-start(bf16[2,96,768]{2,1,0:T(8,128)(2,1)S(1)} %pad_maximum_fusion.4), channel_id=1, source_target_pairs={{0,1},{1,0},{2,3},{3,2},{4,5},{5,4},{6,7},{7,6},{8,9},{9,8},{10,11... | collective-permute-start | bytes 884744 | tf_op jit(solution)/shard_map/ppermute | solution.py:513
  153.9 2.0 %collective-permute-start.42 = (bf16[2,96,768]{2,1,0:T(8,128)(2,1)S(1)}, bf16[2,96,768]{2,1,0:T(8,128)(2,1)S(1)}, u32[]{:S(2)}, u32[]{:S(2)}) collective-permute-start(bf16[2,96,768]{2,1,0:T(8,128)(2,1)S(1)} %pad_maximum_fusion.5), channel_id=1, source_target_pairs={{0,2},{1,3},{2,0},{3,1},{4,6},{5,7},{6,4},{7,5},{8,10},{9,11},{10,... | collective-permute-start | bytes 884744 | tf_op jit(solution)/shard_map/ppermute | solution.py:513
  156.0 1.5 collective-permute-start.43
  157.5 7.3 %shard_map.266 = f32[384,768]{1,0:T(8,128)} custom-call(bf16[2,384,640]{2,1,0:T(8,128)(2,1)S(1)} %get-tuple-element.158.refs_1_.low_ref, bf16[2,384,640]{2,1,0:T(8,128)(2,1)S(1)} %get-tuple-element.159.refs_2_.high_ref, bf16[2,4,104,768]{3,2,1,0:T(8,128)(2,1)S(1)} %bitcast.97, bf16[2,4,104,768]{3,2,1,0:T(8,128)(2,1)S(1)} %bitcast.102, ...), custom_call_target="tpu_custom_call" | custom-call | flops 120000000 | tf_op jit(solution)/shard_map/pallas_call | solution.py:449
  164.8 2.1 %collective-permute-done.38 = bf16[8,104,768]{2,1,0:T(8,128)(2,1)S(1)} collective-permute-done((bf16[8,104,768]{2,1,0:T(8,128)(2,1)S(1)}, bf16[8,104,768]{2,1,0:T(8,128)(2,1)S(1)}, u32[]{:S(2)}, u32[]{:S(2)}) %collective-permute-start.38) | collective-permute-done | bytes 1277984 | tf_op jit(solution)/shard_map/ppermute | solution.py:513
  167.4 1.7 collective-permute-start.47
  169.4 8.1 %collective-permute-done.42 = bf16[2,96,768]{2,1,0:T(8,128)(2,1)S(1)} collective-permute-done((bf16[2,96,768]{2,1,0:T(8,128)(2,1)S(1)}, bf16[2,96,768]{2,1,0:T(8,128)(2,1)S(1)}, u32[]{:S(2)}, u32[]{:S(2)}) %collective-permute-start.42) | collective-permute-done | bytes 294944 | tf_op jit(solution)/shard_map/ppermute | solution.py:513
  177.6 0.6 collective-permute-start.39
  178.4 3.4 %collective-permute-start.48 = (bf16[1,104,768]{2,1,0:T(8,128)(2,1)S(1)}, bf16[1,104,768]{2,1,0:T(8,128)(2,1)S(1)}, u32[]{:S(2)}, u32[]{:S(2)}) collective-permute-start(bf16[1,104,768]{2,1,0:T(8,128)(2,1)S(1)} %get-tuple-element.169), channel_id=1, source_target_pairs={{0,3},{1,2},{2,1},{3,0},{4,7},{5,6},{6,5},{7,4},{8,11},{9,10},{10,... | collective-permute-start | bytes 479240 | tf_op jit(solution)/shard_map/ppermute | solution.py:513
  181.9 6.2 %collective-permute-start.46 = (bf16[1,104,768]{2,1,0:T(8,128)(2,1)S(1)}, bf16[1,104,768]{2,1,0:T(8,128)(2,1)S(1)}, u32[]{:S(2)}, u32[]{:S(2)}) collective-permute-start(bf16[1,104,768]{2,1,0:T(8,128)(2,1)S(1)} %get-tuple-element.167), channel_id=1, source_target_pairs={{0,2},{1,3},{2,0},{3,1},{4,6},{5,7},{6,4},{7,5},{8,10},{9,11},{10,... | collective-permute-start | bytes 479240 | tf_op jit(solution)/shard_map/ppermute | solution.py:513
  188.6 0.8 slice_bitcast_fusion.2
  189.5 6.4 %collective-permute-done.46 = bf16[1,104,768]{2,1,0:T(8,128)(2,1)S(1)} collective-permute-done((bf16[1,104,768]{2,1,0:T(8,128)(2,1)S(1)}, bf16[1,104,768]{2,1,0:T(8,128)(2,1)S(1)}, u32[]{:S(2)}, u32[]{:S(2)}) %collective-permute-start.46) | collective-permute-done | bytes 159776 | tf_op jit(solution)/shard_map/ppermute | solution.py:513
  196.0 0.9 shard_map.267
  (151 shorter events, 11.3 us)
Async XLA Ops:
  0.6 11.8 %copy-start = (f32[3,1,8,768]{3,2,1,0:T(8,128)S(1)}, f32[3,1,8,768]{3,2,1,0:T(8,128)}, u32[]{:S(2)}) copy-start(f32[3,1,8,768]{3,2,1,0:T(8,128)} %param.17) | copy-start | bytes 221188
  2.6 13.9 %collective-permute-start = (bf16[1,104,768]{2,1,0:T(8,128)(2,1)}, bf16[1,104,768]{2,1,0:T(8,128)(2,1)S(1)}, u32[]{:S(2)}, u32[]{:S(2)}) collective-permute-start(bf16[1,104,768]{2,1,0:T(8,128)(2,1)} %bitcast.137), channel_id=1, source_target_pairs={{0,1},{1,0},{2,3},{3,2},{4,5},{5,4},{6,7},{7,6},{8,9},{9,8},{10,11... | collective-permute-start | bytes 479240 | tf_op jit(solution)/shard_map/ppermute | solution.py:493
  5.6 15.0 %collective-permute-start.1 = (bf16[1,104,768]{2,1,0:T(8,128)(2,1)}, bf16[1,104,768]{2,1,0:T(8,128)(2,1)S(1)}, u32[]{:S(2)}, u32[]{:S(2)}) collective-permute-start(bf16[1,104,768]{2,1,0:T(8,128)(2,1)} %bitcast.138), channel_id=1, source_target_pairs={{0,2},{1,3},{2,0},{3,1},{4,6},{5,7},{6,4},{7,5},{8,10},{9,11},{10,... | collective-permute-start | bytes 479240 | tf_op jit(solution)/shard_map/ppermute | solution.py:493
  8.2 12.4 %collective-permute-start.2 = (bf16[1,104,768]{2,1,0:T(8,128)(2,1)}, bf16[1,104,768]{2,1,0:T(8,128)(2,1)S(1)}, u32[]{:S(2)}, u32[]{:S(2)}) collective-permute-start(bf16[1,104,768]{2,1,0:T(8,128)(2,1)} %bitcast.139), channel_id=1, source_target_pairs={{0,3},{1,2},{2,1},{3,0},{4,7},{5,6},{6,5},{7,4},{8,11},{9,10},{10,... | collective-permute-start | bytes 479240 | tf_op jit(solution)/shard_map/ppermute | solution.py:493
  8.2 12.5 %collective-permute-start.3 = (bf16[1,96,768]{2,1,0:T(8,128)(2,1)}, bf16[1,96,768]{2,1,0:T(8,128)(2,1)}, u32[]{:S(2)}, u32[]{:S(2)}) collective-permute-start(bf16[1,96,768]{2,1,0:T(8,128)(2,1)} %bitcast.146), channel_id=1, source_target_pairs={{0,16},{1,17},{2,18},{3,19},{4,12},{5,13},{6,14},{7,15},{8,24},{9,... | collective-permute-start | bytes 442376 | tf_op jit(solution)/shard_map/ppermute | solution.py:564
  12.5 8.2 %copy-start.19 = (bf16[104,768]{1,0:T(8,128)(2,1)S(1)}, bf16[104,768]{1,0:T(8,128)(2,1)}, u32[]{:S(2)}) copy-start(bf16[104,768]{1,0:T(8,128)(2,1)} %shard_map.255) | copy-start | bytes 479236
  16.5 5.8 %copy-start.20 = (bf16[96,768]{1,0:T(8,128)(2,1)S(1)}, bf16[96,768]{1,0:T(8,128)(2,1)}, u32[]{:S(2)}) copy-start(bf16[96,768]{1,0:T(8,128)(2,1)} %param.24) | copy-start | bytes 442372
  20.7 10.5 %collective-permute-start.4 = (bf16[4,104,768]{2,1,0:T(8,128)(2,1)S(1)}, bf16[4,104,768]{2,1,0:T(8,128)(2,1)S(1)}, u32[]{:S(2)}, u32[]{:S(2)}) collective-permute-start(bf16[4,104,768]{2,1,0:T(8,128)(2,1)S(1)} %pad_maximum_fusion), channel_id=1, source_target_pairs={{0,16},{1,17},{2,18},{3,19},{4,12},{5,13},{6,14},{7,15},{8,24},{9,... | collective-permute-start | bytes 1916936 | tf_op jit(solution)/shard_map/ppermute | solution.py:493
  22.4 8.9 %collective-permute-start.5 = (bf16[1,96,768]{2,1,0:T(8,128)(2,1)S(1)}, bf16[1,96,768]{2,1,0:T(8,128)(2,1)S(1)}, u32[]{:S(2)}, u32[]{:S(2)}) collective-permute-start(bf16[1,96,768]{2,1,0:T(8,128)(2,1)S(1)} %bitcast.142), channel_id=1, source_target_pairs={{0,1},{1,0},{2,3},{3,2},{4,5},{5,4},{6,7},{7,6},{8,9},{9,8},{10,11... | collective-permute-start | bytes 442376 | tf_op jit(solution)/shard_map/ppermute | solution.py:493
  25.0 12.7 %collective-permute-start.6 = (bf16[1,96,768]{2,1,0:T(8,128)(2,1)S(1)}, bf16[1,96,768]{2,1,0:T(8,128)(2,1)S(1)}, u32[]{:S(2)}, u32[]{:S(2)}) collective-permute-start(bf16[1,96,768]{2,1,0:T(8,128)(2,1)S(1)} %bitcast.143), channel_id=1, source_target_pairs={{0,2},{1,3},{2,0},{3,1},{4,6},{5,7},{6,4},{7,5},{8,10},{9,11},{10,... | collective-permute-start | bytes 442376 | tf_op jit(solution)/shard_map/ppermute | solution.py:493
  26.1 11.6 %collective-permute-start.7 = (bf16[1,96,768]{2,1,0:T(8,128)(2,1)S(1)}, bf16[1,96,768]{2,1,0:T(8,128)(2,1)S(1)}, u32[]{:S(2)}, u32[]{:S(2)}) collective-permute-start(bf16[1,96,768]{2,1,0:T(8,128)(2,1)S(1)} %bitcast.144), channel_id=1, source_target_pairs={{0,3},{1,2},{2,1},{3,0},{4,7},{5,6},{6,5},{7,4},{8,11},{9,10},{10,... | collective-permute-start | bytes 442376 | tf_op jit(solution)/shard_map/ppermute | solution.py:493
  27.5 13.1 %copy-start.21 = (bf16[768,96]{0,1:T(8,128)(2,1)S(1)}, bf16[768,96]{0,1:T(8,128)(2,1)}, u32[]{:S(2)}) copy-start(bf16[768,96]{0,1:T(8,128)(2,1)} %param.26) | copy-start | bytes 442372
  37.7 21.1 %collective-permute-start.8 = (bf16[8,104,768]{2,1,0:T(8,128)(2,1)S(1)}, bf16[8,104,768]{2,1,0:T(8,128)(2,1)S(1)}, u32[]{:S(2)}, u32[]{:S(2)}) collective-permute-start(bf16[8,104,768]{2,1,0:T(8,128)(2,1)S(1)} %constant_dynamic-update-slice_fusion), channel_id=1, source_target_pairs={{0,8},{1,9},{2,10},{3,11},{4,20},{5,21},{6,22},{7,23},{8,0},{9,1},... | collective-permute-start | bytes 3833864 | tf_op jit(solution)/shard_map/ppermute | solution.py:493
  38.3 17.6 %collective-permute-start.9 = (bf16[4,96,768]{2,1,0:T(8,128)(2,1)S(1)}, bf16[4,96,768]{2,1,0:T(8,128)(2,1)S(1)}, u32[]{:S(2)}, u32[]{:S(2)}) collective-permute-start(bf16[4,96,768]{2,1,0:T(8,128)(2,1)S(1)} %pad_maximum_fusion.1), channel_id=1, source_target_pairs={{0,16},{1,17},{2,18},{3,19},{4,12},{5,13},{6,14},{7,15},{8,24},{9,... | collective-permute-start | bytes 1769480 | tf_op jit(solution)/shard_map/ppermute | solution.py:493
  42.2 13.6 %collective-permute-start.10 = (bf16[2,96,768]{2,1,0:T(8,128)(2,1)}, bf16[2,96,768]{2,1,0:T(8,128)(2,1)S(1)}, u32[]{:S(2)}, u32[]{:S(2)}) collective-permute-start(bf16[2,96,768]{2,1,0:T(8,128)(2,1)} %pad_maximum_fusion.3), channel_id=1, source_target_pairs={{0,1},{1,0},{2,3},{3,2},{4,5},{5,4},{6,7},{7,6},{8,9},{9,8},{10,11... | collective-permute-start | bytes 884744 | tf_op jit(solution)/shard_map/ppermute | solution.py:564
  44.4 11.5 %collective-permute-start.11 = (bf16[2,96,768]{2,1,0:T(8,128)(2,1)}, bf16[2,96,768]{2,1,0:T(8,128)(2,1)S(1)}, u32[]{:S(2)}, u32[]{:S(2)}) collective-permute-start(bf16[2,96,768]{2,1,0:T(8,128)(2,1)} %pad_maximum_fusion.3), channel_id=1, source_target_pairs={{0,2},{1,3},{2,0},{3,1},{4,6},{5,7},{6,4},{7,5},{8,10},{9,11},{10,... | collective-permute-start | bytes 884744 | tf_op jit(solution)/shard_map/ppermute | solution.py:564
  47.5 18.6 %copy-start.24 = (s32[3,1,128]{2,1,0:T(1,128)S(1)}, s32[3,1,128]{2,1,0:T(1,128)}, u32[]{:S(2)}) copy-start(s32[3,1,128]{2,1,0:T(1,128)} %param.16) | copy-start | bytes 4612
  55.9 4.1 %copy-start.22 = (bf16[2,96,768]{2,1,0:T(8,128)(2,1)}, bf16[2,96,768]{2,1,0:T(8,128)(2,1)S(1)}, u32[]{:S(2)}) copy-start(bf16[2,96,768]{2,1,0:T(8,128)(2,1)S(1)} %collective-permute-done.11) | copy-start | bytes 884740
  55.9 10.3 %collective-permute-start.12 = (bf16[8,104,768]{2,1,0:T(8,128)(2,1)S(1)}, bf16[8,104,768]{2,1,0:T(8,128)(2,1)}, u32[]{:S(2)}, u32[]{:S(2)}) collective-permute-start(bf16[8,104,768]{2,1,0:T(8,128)(2,1)S(1)} %constant_dynamic-update-slice_fusion), channel_id=1, source_target_pairs={{0,4},{1,5},{2,6},{3,7},{4,0},{5,1},{6,2},{7,3},{8,12},{9,13},{10,... | collective-permute-start | bytes 3833864 | tf_op jit(solution)/shard_map/ppermute | solution.py:493
  58.8 7.4 %collective-permute-start.13 = (bf16[8,104,768]{2,1,0:T(8,128)(2,1)S(1)}, bf16[8,104,768]{2,1,0:T(8,128)(2,1)}, u32[]{:S(2)}, u32[]{:S(2)}) collective-permute-start(bf16[8,104,768]{2,1,0:T(8,128)(2,1)S(1)} %collective-permute-done.8), channel_id=1, source_target_pairs={{0,4},{1,5},{2,6},{3,7},{4,0},{5,1},{6,2},{7,3},{8,12},{9,13},{10,... | collective-permute-start | bytes 3833864 | tf_op jit(solution)/shard_map/ppermute | solution.py:493
  59.7 19.4 %collective-permute-start.14 = (bf16[8,96,768]{2,1,0:T(8,128)(2,1)}, bf16[8,96,768]{2,1,0:T(8,128)(2,1)}, u32[]{:S(2)}, u32[]{:S(2)}) collective-permute-start(bf16[8,96,768]{2,1,0:T(8,128)(2,1)} %constant_dynamic-update-slice_fusion.5), channel_id=1, source_target_pairs={{0,8},{1,9},{2,10},{3,11},{4,20},{5,21},{6,22},{7,23},{8,0},{9,1},... | collective-permute-start | bytes 3538952 | tf_op jit(solution)/shard_map/ppermute | solution.py:493
  59.9 19.1 %collective-permute-start.15 = (bf16[2,96,768]{2,1,0:T(8,128)(2,1)}, bf16[2,96,768]{2,1,0:T(8,128)(2,1)}, u32[]{:S(2)}, u32[]{:S(2)}) collective-permute-start(bf16[2,96,768]{2,1,0:T(8,128)(2,1)} %pad_maximum_fusion.3), channel_id=1, source_target_pairs={{0,3},{1,2},{2,1},{3,0},{4,7},{5,6},{6,5},{7,4},{8,11},{9,10},{10,... | collective-permute-start | bytes 884744 | tf_op jit(solution)/shard_map/ppermute | solution.py:564
  65.5 17.0 %collective-permute-start.19 = (bf16[4,96,768]{2,1,0:T(8,128)(2,1)S(1)}, bf16[4,96,768]{2,1,0:T(8,128)(2,1)}, u32[]{:S(2)}, u32[]{:S(2)}) collective-permute-start(bf16[4,96,768]{2,1,0:T(8,128)(2,1)S(1)} %pad_maximum_fusion.2), channel_id=1, source_target_pairs={{0,8},{1,9},{2,10},{3,11},{4,20},{5,21},{6,22},{7,23},{8,0},{9,1},... | collective-permute-start | bytes 1769480 | tf_op jit(solution)/shard_map/ppermute | solution.py:564
  67.3 12.3 %copy-start.23 = (bf16[2,96,768]{2,1,0:T(8,128)(2,1)S(1)}, bf16[2,96,768]{2,1,0:T(8,128)(2,1)}, u32[]{:S(2)}) copy-start(bf16[2,96,768]{2,1,0:T(8,128)(2,1)} %copy-done.22) | copy-start | bytes 884740
  79.1 6.5 %collective-permute-start.16 = (bf16[8,96,768]{2,1,0:T(8,128)(2,1)}, bf16[8,96,768]{2,1,0:T(8,128)(2,1)S(1)}, u32[]{:S(2)}, u32[]{:S(2)}) collective-permute-start(bf16[8,96,768]{2,1,0:T(8,128)(2,1)} %constant_dynamic-update-slice_fusion.5), channel_id=1, source_target_pairs={{0,4},{1,5},{2,6},{3,7},{4,0},{5,1},{6,2},{7,3},{8,12},{9,13},{10,... | collective-permute-start | bytes 3538952 | tf_op jit(solution)/shard_map/ppermute | solution.py:493
  79.1 6.4 %collective-permute-start.17 = (bf16[8,96,768]{2,1,0:T(8,128)(2,1)}, bf16[8,96,768]{2,1,0:T(8,128)(2,1)S(1)}, u32[]{:S(2)}, u32[]{:S(2)}) collective-permute-start(bf16[8,96,768]{2,1,0:T(8,128)(2,1)} %collective-permute-done.14), channel_id=1, source_target_pairs={{0,4},{1,5},{2,6},{3,7},{4,0},{5,1},{6,2},{7,3},{8,12},{9,13},{10,... | collective-permute-start | bytes 3538952 | tf_op jit(solution)/shard_map/ppermute | solution.py:493
  79.7 4.2 %collective-permute-start.18 = (bf16[4,96,768]{2,1,0:T(8,128)(2,1)S(1)}, bf16[4,96,768]{2,1,0:T(8,128)(2,1)S(1)}, u32[]{:S(2)}, u32[]{:S(2)}) collective-permute-start(bf16[4,96,768]{2,1,0:T(8,128)(2,1)S(1)} %pad_maximum_fusion.2), channel_id=1, source_target_pairs={{0,4},{1,5},{2,6},{3,7},{4,0},{5,1},{6,2},{7,3},{8,12},{9,13},{10,... | collective-permute-start | bytes 1769480 | tf_op jit(solution)/shard_map/ppermute | solution.py:484
  82.5 3.1 %collective-permute-start.20 = (bf16[4,96,768]{2,1,0:T(8,128)(2,1)}, bf16[4,96,768]{2,1,0:T(8,128)(2,1)S(1)}, u32[]{:S(2)}, u32[]{:S(2)}) collective-permute-start(bf16[4,96,768]{2,1,0:T(8,128)(2,1)} %collective-permute-done.19), channel_id=1, source_target_pairs={{0,4},{1,5},{2,6},{3,7},{4,0},{5,1},{6,2},{7,3},{8,12},{9,13},{10,... | collective-permute-start | bytes 1769480 | tf_op jit(solution)/shard_map/ppermute | solution.py:484
  83.5 9.9 %collective-permute-start.21 = (bf16[4,96,768]{2,1,0:T(8,128)(2,1)S(1)}, bf16[4,96,768]{2,1,0:T(8,128)(2,1)S(1)}, u32[]{:S(2)}, u32[]{:S(2)}) collective-permute-start(bf16[4,96,768]{2,1,0:T(8,128)(2,1)S(1)} %constant_dynamic-update-slice_fusion.10), channel_id=1, source_target_pairs={{0,8},{1,9},{2,10},{3,11},{4,20},{5,21},{6,22},{7,23},{8,0},{9,1},... | collective-permute-start | bytes 1769480 | tf_op jit(solution)/shard_map/ppermute | solution.py:564
  83.8 9.6 %collective-permute-start.22 = (bf16[4,96,768]{2,1,0:T(8,128)(2,1)S(1)}, bf16[4,96,768]{2,1,0:T(8,128)(2,1)S(1)}, u32[]{:S(2)}, u32[]{:S(2)}) collective-permute-start(bf16[4,96,768]{2,1,0:T(8,128)(2,1)S(1)} %constant_dynamic-update-slice_fusion.10), channel_id=1, source_target_pairs={{0,4},{1,5},{2,6},{3,7},{4,0},{5,1},{6,2},{7,3},{8,12},{9,13},{10,... | collective-permute-start | bytes 1769480 | tf_op jit(solution)/shard_map/ppermute | solution.py:484
  85.6 10.0 %copy-start.6 = (bf16[4,384,256]{2,1,0:T(8,128)(2,1)S(1)}, bf16[4,384,256]{2,1,0:T(8,128)(2,1)}, u32[]{:S(2)}) copy-start(bf16[4,384,256]{2,1,0:T(8,128)(2,1)} %get-tuple-element.127.refs_7_) | copy-start | bytes 2359300
  85.6 10.4 %copy-start.15 = (bf16[384,384]{1,0:T(8,128)(2,1)S(1)}, bf16[384,384]{1,0:T(8,128)(2,1)}, u32[]{:S(2)}) copy-start(bf16[384,384]{1,0:T(8,128)(2,1)} %copy-done.14) | copy-start | bytes 884740
  85.6 10.5 %copy-start.25 = (bf16[384,384]{1,0:T(8,128)(2,1)S(1)}, bf16[384,384]{1,0:T(8,128)(2,1)}, u32[]{:S(2)}) copy-start(bf16[384,384]{1,0:T(8,128)(2,1)} %get-tuple-element.126) | copy-start | bytes 884740
  93.4 2.0 %collective-permute-start.23 = (bf16[4,96,768]{2,1,0:T(8,128)(2,1)S(1)}, bf16[4,96,768]{2,1,0:T(8,128)(2,1)S(1)}, u32[]{:S(2)}, u32[]{:S(2)}) collective-permute-start(bf16[4,96,768]{2,1,0:T(8,128)(2,1)S(1)} %collective-permute-done.21), channel_id=1, source_target_pairs={{0,4},{1,5},{2,6},{3,7},{4,0},{5,1},{6,2},{7,3},{8,12},{9,13},{10,... | collective-permute-start | bytes 1769480 | tf_op jit(solution)/shard_map/ppermute | solution.py:484
  95.4 10.1 %collective-permute-start.28 = (bf16[4,384,768]{2,1,0:T(8,128)(2,1)S(1)}, bf16[4,384,768]{2,1,0:T(8,128)(2,1)S(1)}, u32[]{:S(2)}, u32[]{:S(2)}) collective-permute-start(bf16[4,384,768]{2,1,0:T(8,128)(2,1)S(1)} %get-tuple-element.134.refs_1_), channel_id=1, source_target_pairs={{0,4},{1,5},{2,6},{3,7},{4,0},{5,1},{6,2},{7,3},{8,12},{9,13},{10,... | collective-permute-start | bytes 7077896 | tf_op jit(solution)/shard_map/ppermute | solution.py:484
  95.6 6.4 %collective-permute-start.26 = (bf16[4,384,256]{2,1,0:T(8,128)(2,1)S(1)}, bf16[4,384,256]{2,1,0:T(8,128)(2,1)S(1)}, u32[]{:S(2)}, u32[]{:S(2)}) collective-permute-start(bf16[4,384,256]{2,1,0:T(8,128)(2,1)S(1)} %copy-done.6), channel_id=1, source_target_pairs={{0,4},{1,5},{2,6},{3,7},{4,0},{5,1},{6,2},{7,3},{8,12},{9,13},{10,... | collective-permute-start | bytes 2359304 | tf_op jit(solution)/shard_map/ppermute | solution.py:484
  96.0 5.8 %collective-permute-start.24 = (bf16[384,384]{1,0:T(8,128)(2,1)S(1)}, bf16[384,384]{1,0:T(8,128)(2,1)S(1)}, u32[]{:S(2)}, u32[]{:S(2)}) collective-permute-start(bf16[384,384]{1,0:T(8,128)(2,1)S(1)} %copy-done.15), channel_id=1, source_target_pairs={{0,4},{1,5},{2,6},{3,7},{4,0},{5,1},{6,2},{7,3},{8,12},{9,13},{10,... | collective-permute-start | bytes 884744 | tf_op jit(solution)/shard_map/ppermute | solution.py:484
  96.1 5.8 %collective-permute-start.25 = (bf16[384,384]{1,0:T(8,128)(2,1)S(1)}, bf16[384,384]{1,0:T(8,128)(2,1)S(1)}, u32[]{:S(2)}, u32[]{:S(2)}) collective-permute-start(bf16[384,384]{1,0:T(8,128)(2,1)S(1)} %copy-done.25), channel_id=1, source_target_pairs={{0,4},{1,5},{2,6},{3,7},{4,0},{5,1},{6,2},{7,3},{8,12},{9,13},{10,... | collective-permute-start | bytes 884744 | tf_op jit(solution)/shard_map/ppermute | solution.py:484
  101.5 4.1 %collective-permute-start.27 = (bf16[384,384]{1,0:T(8,128)(2,1)S(1)}, bf16[384,384]{1,0:T(8,128)(2,1)S(1)}, u32[]{:S(2)}, u32[]{:S(2)}) collective-permute-start(bf16[384,384]{1,0:T(8,128)(2,1)S(1)} %get-tuple-element.133), channel_id=1, source_target_pairs={{0,4},{1,5},{2,6},{3,7},{4,0},{5,1},{6,2},{7,3},{8,12},{9,13},{10,... | collective-permute-start | bytes 884744 | tf_op jit(solution)/shard_map/ppermute | solution.py:484
  105.3 8.0 %collective-permute-start.29 = (bf16[4,384,768]{2,1,0:T(8,128)(2,1)S(1)}, bf16[4,384,768]{2,1,0:T(8,128)(2,1)S(1)}, u32[]{:S(2)}, u32[]{:S(2)}) collective-permute-start(bf16[4,384,768]{2,1,0:T(8,128)(2,1)S(1)} %bitcast.118), channel_id=1, source_target_pairs={{0,4},{1,5},{2,6},{3,7},{4,0},{5,1},{6,2},{7,3},{8,12},{9,13},{10,... | collective-permute-start | bytes 7077896 | tf_op jit(solution)/shard_map/ppermute | solution.py:484
  107.5 16.3 %collective-permute-start.31 = (bf16[8,96,768]{2,1,0:T(8,128)(2,1)S(1)}, bf16[8,96,768]{2,1,0:T(8,128)(2,1)S(1)}, u32[]{:S(2)}, u32[]{:S(2)}) collective-permute-start(bf16[8,96,768]{2,1,0:T(8,128)(2,1)S(1)} %bitcast.124), channel_id=1, source_target_pairs={{0,8},{1,9},{2,10},{3,11},{4,20},{5,21},{6,22},{7,23},{8,0},{9,1},... | collective-permute-start | bytes 3538952 | tf_op jit(solution)/shard_map/ppermute | solution.py:513
  107.9 5.5 %copy-start.12 = (bf16[384,384]{1,0:T(8,128)(2,1)S(1)}, bf16[384,384]{1,0:T(8,128)(2,1)}, u32[]{:S(2)}) copy-start(bf16[384,384]{1,0:T(8,128)(2,1)} %get-tuple-element.142.refs_0_) | copy-start | bytes 884740
  116.7 20.0 %collective-permute-start.32 = (bf16[8,96,768]{2,1,0:T(8,128)(2,1)S(1)}, bf16[8,96,768]{2,1,0:T(8,128)(2,1)S(1)}, u32[]{:S(2)}, u32[]{:S(2)}) collective-permute-start(bf16[8,96,768]{2,1,0:T(8,128)(2,1)S(1)} %bitcast.134), channel_id=1, source_target_pairs={{0,8},{1,9},{2,10},{3,11},{4,20},{5,21},{6,22},{7,23},{8,0},{9,1},... | collective-permute-start | bytes 3538952 | tf_op jit(solution)/shard_map/ppermute | solution.py:513
  118.5 1.9 collective-permute-start.30
  118.5 5.3 %copy-start.4 = (f32[4,3,128,384]{3,2,1,0:T(8,128)S(1)}, f32[4,3,128,384]{3,2,1,0:T(8,128)}, u32[]{:S(2)}) copy-start(f32[4,3,128,384]{3,2,1,0:T(8,128)} %get-tuple-element.148.p_ref) | copy-start | bytes 7077892
  118.5 5.3 %copy-start.5 = (bf16[4,384,576]{2,1,0:T(8,128)(2,1)S(1)}, bf16[4,384,576]{2,1,0:T(8,128)(2,1)}, u32[]{:S(2)}) copy-start(bf16[4,384,576]{2,1,0:T(8,128)(2,1)} %get-tuple-element.147.qkv_ref) | copy-start | bytes 5308420
  132.5 6.8 %collective-permute-start.33 = (bf16[2,384,640]{2,1,0:T(8,128)(2,1)S(1)}, bf16[2,384,640]{2,1,0:T(8,128)(2,1)S(1)}, u32[]{:S(2)}, u32[]{:S(2)}) collective-permute-start(bf16[2,384,640]{2,1,0:T(8,128)(2,1)S(1)} %get-tuple-element.158.refs_1_.low_ref), channel_id=1, source_target_pairs={{0,4},{1,5},{2,6},{3,7},{4,0},{5,1},{6,2},{7,3},{8,12},{9,13},{10,... | collective-permute-start | bytes 2949128 | tf_op jit(solution)/shard_map/ppermute | solution.py:484
  132.5 6.7 %collective-permute-start.34 = (bf16[2,384,640]{2,1,0:T(8,128)(2,1)S(1)}, bf16[2,384,640]{2,1,0:T(8,128)(2,1)S(1)}, u32[]{:S(2)}, u32[]{:S(2)}) collective-permute-start(bf16[2,384,640]{2,1,0:T(8,128)(2,1)S(1)} %get-tuple-element.159.refs_2_.high_ref), channel_id=1, source_target_pairs={{0,4},{1,5},{2,6},{3,7},{4,0},{5,1},{6,2},{7,3},{8,12},{9,13},{10,... | collective-permute-start | bytes 2949128 | tf_op jit(solution)/shard_map/ppermute | solution.py:484
  133.3 10.3 %collective-permute-start.36 = (bf16[4,96,768]{2,1,0:T(8,128)(2,1)S(1)}, bf16[4,96,768]{2,1,0:T(8,128)(2,1)S(1)}, u32[]{:S(2)}, u32[]{:S(2)}) collective-permute-start(bf16[4,96,768]{2,1,0:T(8,128)(2,1)S(1)} %get-tuple-element.218), channel_id=1, source_target_pairs={{0,16},{1,17},{2,18},{3,19},{4,12},{5,13},{6,14},{7,15},{8,24},{9,... | collective-permute-start | bytes 1769480 | tf_op jit(solution)/shard_map/ppermute | solution.py:513
  137.0 12.6 %collective-permute-start.37 = (bf16[4,96,768]{2,1,0:T(8,128)(2,1)S(1)}, bf16[4,96,768]{2,1,0:T(8,128)(2,1)S(1)}, u32[]{:S(2)}, u32[]{:S(2)}) collective-permute-start(bf16[4,96,768]{2,1,0:T(8,128)(2,1)S(1)} %get-tuple-element.220), channel_id=1, source_target_pairs={{0,16},{1,17},{2,18},{3,19},{4,12},{5,13},{6,14},{7,15},{8,24},{9,... | collective-permute-start | bytes 1769480 | tf_op jit(solution)/shard_map/ppermute | solution.py:513
  137.3 2.0 collective-permute-start.35
  149.6 17.3 %collective-permute-start.38 = (bf16[8,104,768]{2,1,0:T(8,128)(2,1)S(1)}, bf16[8,104,768]{2,1,0:T(8,128)(2,1)S(1)}, u32[]{:S(2)}, u32[]{:S(2)}) collective-permute-start(bf16[8,104,768]{2,1,0:T(8,128)(2,1)S(1)} %bitcast.133), channel_id=1, source_target_pairs={{0,8},{1,9},{2,10},{3,11},{4,20},{5,21},{6,22},{7,23},{8,0},{9,1},... | collective-permute-start | bytes 3833864 | tf_op jit(solution)/shard_map/ppermute | solution.py:513
  150.1 7.4 %copy-start.3 = (bf16[768,768]{1,0:T(8,128)(2,1)S(1)}, bf16[768,768]{1,0:T(8,128)(2,1)}, u32[]{:S(2)}) copy-start(bf16[768,768]{1,0:T(8,128)(2,1)} %copy-done.2) | copy-start | bytes 3538948
  150.2 18.9 %collective-permute-start.41 = (bf16[2,96,768]{2,1,0:T(8,128)(2,1)S(1)}, bf16[2,96,768]{2,1,0:T(8,128)(2,1)S(1)}, u32[]{:S(2)}, u32[]{:S(2)}) collective-permute-start(bf16[2,96,768]{2,1,0:T(8,128)(2,1)S(1)} %pad_maximum_fusion.4), channel_id=1, source_target_pairs={{0,1},{1,0},{2,3},{3,2},{4,5},{5,4},{6,7},{7,6},{8,9},{9,8},{10,11... | collective-permute-start | bytes 884744 | tf_op jit(solution)/shard_map/ppermute | solution.py:513
  153.9 23.6 %collective-permute-start.42 = (bf16[2,96,768]{2,1,0:T(8,128)(2,1)S(1)}, bf16[2,96,768]{2,1,0:T(8,128)(2,1)S(1)}, u32[]{:S(2)}, u32[]{:S(2)}) collective-permute-start(bf16[2,96,768]{2,1,0:T(8,128)(2,1)S(1)} %pad_maximum_fusion.5), channel_id=1, source_target_pairs={{0,2},{1,3},{2,0},{3,1},{4,6},{5,7},{6,4},{7,5},{8,10},{9,11},{10,... | collective-permute-start | bytes 884744 | tf_op jit(solution)/shard_map/ppermute | solution.py:513
  156.0 21.5 %collective-permute-start.43 = (bf16[2,96,768]{2,1,0:T(8,128)(2,1)S(1)}, bf16[2,96,768]{2,1,0:T(8,128)(2,1)S(1)}, u32[]{:S(2)}, u32[]{:S(2)}) collective-permute-start(bf16[2,96,768]{2,1,0:T(8,128)(2,1)S(1)} %pad_maximum_fusion.6), channel_id=1, source_target_pairs={{0,3},{1,2},{2,1},{3,0},{4,7},{5,6},{6,5},{7,4},{8,11},{9,10},{10,... | collective-permute-start | bytes 884744 | tf_op jit(solution)/shard_map/ppermute | solution.py:513
  167.0 11.2 %collective-permute-start.40 = (bf16[1,104,768]{2,1,0:T(8,128)(2,1)S(1)}, bf16[1,104,768]{2,1,0:T(8,128)(2,1)S(1)}, u32[]{:S(2)}, u32[]{:S(2)}) collective-permute-start(bf16[1,104,768]{2,1,0:T(8,128)(2,1)S(1)} %get-tuple-element.164), channel_id=1, source_target_pairs={{0,16},{1,17},{2,18},{3,19},{4,12},{5,13},{6,14},{7,15},{8,24},{9,... | collective-permute-start | bytes 479240 | tf_op jit(solution)/shard_map/ppermute | solution.py:513
  167.4 10.9 %collective-permute-start.47 = (bf16[1,104,768]{2,1,0:T(8,128)(2,1)S(1)}, bf16[1,104,768]{2,1,0:T(8,128)(2,1)S(1)}, u32[]{:S(2)}, u32[]{:S(2)}) collective-permute-start(bf16[1,104,768]{2,1,0:T(8,128)(2,1)S(1)} %get-tuple-element.168), channel_id=1, source_target_pairs={{0,16},{1,17},{2,18},{3,19},{4,12},{5,13},{6,14},{7,15},{8,24},{9,... | collective-permute-start | bytes 479240 | tf_op jit(solution)/shard_map/ppermute | solution.py:513
  169.1 9.1 %collective-permute-start.45 = (bf16[1,104,768]{2,1,0:T(8,128)(2,1)S(1)}, bf16[1,104,768]{2,1,0:T(8,128)(2,1)S(1)}, u32[]{:S(2)}, u32[]{:S(2)}) collective-permute-start(bf16[1,104,768]{2,1,0:T(8,128)(2,1)S(1)} %get-tuple-element.166), channel_id=1, source_target_pairs={{0,16},{1,17},{2,18},{3,19},{4,12},{5,13},{6,14},{7,15},{8,24},{9,... | collective-permute-start | bytes 479240 | tf_op jit(solution)/shard_map/ppermute | solution.py:513
  177.6 11.8 %collective-permute-start.39 = (bf16[1,104,768]{2,1,0:T(8,128)(2,1)S(1)}, bf16[1,104,768]{2,1,0:T(8,128)(2,1)S(1)}, u32[]{:S(2)}, u32[]{:S(2)}) collective-permute-start(bf16[1,104,768]{2,1,0:T(8,128)(2,1)S(1)} %get-tuple-element.163), channel_id=1, source_target_pairs={{0,16},{1,17},{2,18},{3,19},{4,12},{5,13},{6,14},{7,15},{8,24},{9,... | collective-permute-start | bytes 479240 | tf_op jit(solution)/shard_map/ppermute | solution.py:513
  178.4 11.0 %collective-permute-start.48 = (bf16[1,104,768]{2,1,0:T(8,128)(2,1)S(1)}, bf16[1,104,768]{2,1,0:T(8,128)(2,1)S(1)}, u32[]{:S(2)}, u32[]{:S(2)}) collective-permute-start(bf16[1,104,768]{2,1,0:T(8,128)(2,1)S(1)} %get-tuple-element.169), channel_id=1, source_target_pairs={{0,3},{1,2},{2,1},{3,0},{4,7},{5,6},{6,5},{7,4},{8,11},{9,10},{10,... | collective-permute-start | bytes 479240 | tf_op jit(solution)/shard_map/ppermute | solution.py:513
  181.9 14.0 %collective-permute-start.46 = (bf16[1,104,768]{2,1,0:T(8,128)(2,1)S(1)}, bf16[1,104,768]{2,1,0:T(8,128)(2,1)S(1)}, u32[]{:S(2)}, u32[]{:S(2)}) collective-permute-start(bf16[1,104,768]{2,1,0:T(8,128)(2,1)S(1)} %get-tuple-element.167), channel_id=1, source_target_pairs={{0,2},{1,3},{2,0},{3,1},{4,6},{5,7},{6,4},{7,5},{8,10},{9,11},{10,... | collective-permute-start | bytes 479240 | tf_op jit(solution)/shard_map/ppermute | solution.py:513
  188.1 8.8 %copy-start.1 = (f32[3,1,8,768]{3,2,1,0:T(8,128)S(1)}, f32[3,1,8,768]{3,2,1,0:T(8,128)}, u32[]{:S(2)}) copy-start(f32[3,1,8,768]{3,2,1,0:T(8,128)} %param.17) | copy-start | bytes 221188
  188.1 7.7 %collective-permute-start.44 = (bf16[1,104,768]{2,1,0:T(8,128)(2,1)S(1)}, bf16[1,104,768]{2,1,0:T(8,128)(2,1)S(1)}, u32[]{:S(2)}, u32[]{:S(2)}) collective-permute-start(bf16[1,104,768]{2,1,0:T(8,128)(2,1)S(1)} %get-tuple-element.165), channel_id=1, source_target_pairs={{0,1},{1,0},{2,3},{3,2},{4,5},{5,4},{6,7},{7,6},{8,9},{9,8},{10,11... | collective-permute-start | bytes 479240 | tf_op jit(solution)/shard_map/ppermute | solution.py:513
  (11 other events, 20.8 us)

commit v11 on v10

--- a/solution.py
+++ b/solution.py
@@ -672,7 +672,6 @@
         w_down = [low, low_far, *low_other, high, high_far, *high_other]
         w_down = [w.reshape(n_t // 2, 2, BLK, fc) for w in w_down]
         z_other = swap(z, tables, *high_other)
-        dgelu = after(dgelu, x_other, n1_other, o_other)
     pooled, db, dbb, db_keep, db_send, sums2 = call(
         down_forward, n_t // 2, 5.5, paired(folded(z)) + weights_t(*w_down) + wholes(n1, vec_d, seg_c, seg_r, pg),
         wholes(sds((G, segs, D), f32), sds((T, D), f32), sds((T, D), bf16), sds(turned, bf16), sds(turned, bf16), sds((3, D), f32)),
@@ -733,7 +732,7 @@
         dab = after(dab, up_keep)
     rows = sds((n_t, n_i // 2, 4 * hc), f32)
     if pairwise:
-        dab = after(dab, da_other, dab_after, *got_d3)
+        dab = after(dab, da_other, dab_after, x_other, o_other, *got_d3)
     dq_half = sds((n_t // 2, T, q_wide), bf16)
     *dq, v_keep, v_send = call(
         partial(attention_backward, sizes), n_t, 8,

time: 198 us -> 197 us (level)
  transfers between devices with their start and end apart: 49 -> 49, of which waited for: 16 -> 17; matrix products, arithmetic and copies ran while one was open for 8% -> 8% of each run, Pallas kernels for 30% -> 30%
where the time goes in v11:
time: 197 us
  waiting for transfers between devices  62.8 us (32%)
  Pallas kernels  61.5 us (31%)
  starting transfers between devices  52.1 us (26%)
  local copies, waits for them, and re-layouts  10.3 us (5%)
  other arithmetic  5.41 us (3%)
  matrix products  2.99 us (2%)
    pallas_call x11, Pallas kernels, call(): pl.pallas_call(body, grid=(n_t,), in_specs=[s for _, s in ins], out_specs...  58 us
    ppermute x15, waiting for transfers between devices, stage(): lax.ppermute(after(s, *done), AXES, tables[n // pieces])  27.7 us
    ppermute x15, starting transfers between devices, stage(): lax.ppermute(after(s, *done), AXES, tables[n // pieces])  23.5 us
    ppermute x14, waiting for transfers between devices, send(): lax.ppermute(after(h, *done), AXES, t)  17.1 us
    ppermute x14, starting transfers between devices, send(): lax.ppermute(after(h, *done), AXES, t)  15.4 us
    ppermute x6, waiting for transfers between devices, move(): return lax.ppermute(after(value, *done), AXES, tables[name][way])  14 us
    ppermute x6, starting transfers between devices, move(): return lax.ppermute(after(value, *done), AXES, tables[name][way])  10.5 us
    unnamed x62, local copies, waits for them, and re-layouts  6.1 us
  transfers between devices with their start and end apart: 49, of which 17 were waited for; matrix products, arithmetic and copies ran while one was open for 8% of the time, Pallas kernels for 30%

profile of v11, /device:TPU:0, one launch (start us, length us, event | category | flops | bytes accessed | tf_op | source)
XLA Modules:
  0.0 196.6 jit_solution(5757964130893011291)
XLA Ops:
  0.7 2.0 shard_map.255
  2.6 3.0 %collective-permute-start = (bf16[1,104,768]{2,1,0:T(8,128)(2,1)}, bf16[1,104,768]{2,1,0:T(8,128)(2,1)S(1)}, u32[]{:S(2)}, u32[]{:S(2)}) collective-permute-start(bf16[1,104,768]{2,1,0:T(8,128)(2,1)} %bitcast.137), channel_id=1, source_target_pairs={{0,1},{1,0},{2,3},{3,2},{4,5},{5,4},{6,7},{7,6},{8,9},{9,8},{10,11... | collective-permute-start | bytes 479240 | tf_op jit(solution)/shard_map/ppermute | solution.py:493
  5.6 2.6 %collective-permute-start.1 = (bf16[1,104,768]{2,1,0:T(8,128)(2,1)}, bf16[1,104,768]{2,1,0:T(8,128)(2,1)S(1)}, u32[]{:S(2)}, u32[]{:S(2)}) collective-permute-start(bf16[1,104,768]{2,1,0:T(8,128)(2,1)} %bitcast.138), channel_id=1, source_target_pairs={{0,2},{1,3},{2,0},{3,1},{4,6},{5,7},{6,4},{7,5},{8,10},{9,11},{10,... | collective-permute-start | bytes 479240 | tf_op jit(solution)/shard_map/ppermute | solution.py:493
  8.2 1.7 collective-permute-start.3
  10.4 0.7 copy.30
  12.5 1.0 convolution_bitcast_fusion.pg_ref
  13.6 0.7 shard_map.254
  14.3 0.8 copy-done.7
  15.1 0.7 copy-done.10
  15.8 0.7 copy-done.14
  16.6 4.1 %collective-permute-done.1 = bf16[1,104,768]{2,1,0:T(8,128)(2,1)S(1)} collective-permute-done((bf16[1,104,768]{2,1,0:T(8,128)(2,1)}, bf16[1,104,768]{2,1,0:T(8,128)(2,1)S(1)}, u32[]{:S(2)}, u32[]{:S(2)}) %collective-permute-start.1) | collective-permute-done | bytes 159776 | tf_op jit(solution)/shard_map/ppermute | solution.py:493
  20.7 1.6 collective-permute-start.4
  22.4 2.6 %collective-permute-start.5 = (bf16[1,96,768]{2,1,0:T(8,128)(2,1)S(1)}, bf16[1,96,768]{2,1,0:T(8,128)(2,1)S(1)}, u32[]{:S(2)}, u32[]{:S(2)}) collective-permute-start(bf16[1,96,768]{2,1,0:T(8,128)(2,1)S(1)} %bitcast.142), channel_id=1, source_target_pairs={{0,1},{1,0},{2,3},{3,2},{4,5},{5,4},{6,7},{7,6},{8,9},{9,8},{10,11... | collective-permute-start | bytes 442376 | tf_op jit(solution)/shard_map/ppermute | solution.py:493
  25.0 1.1 collective-permute-start.6
  26.1 1.4 collective-permute-start.7
  27.5 3.7 %collective-permute-done.4 = bf16[4,104,768]{2,1,0:T(8,128)(2,1)S(1)} collective-permute-done((bf16[4,104,768]{2,1,0:T(8,128)(2,1)S(1)}, bf16[4,104,768]{2,1,0:T(8,128)(2,1)S(1)}, u32[]{:S(2)}, u32[]{:S(2)}) %collective-permute-start.4) | collective-permute-done | bytes 639008 | tf_op jit(solution)/shard_map/ppermute | solution.py:493
  31.3 6.4 %collective-permute-done.6 = bf16[1,96,768]{2,1,0:T(8,128)(2,1)S(1)} collective-permute-done((bf16[1,96,768]{2,1,0:T(8,128)(2,1)S(1)}, bf16[1,96,768]{2,1,0:T(8,128)(2,1)S(1)}, u32[]{:S(2)}, u32[]{:S(2)}) %collective-permute-start.6) | collective-permute-done | bytes 147488 | tf_op jit(solution)/shard_map/ppermute | solution.py:493
  38.3 1.6 collective-permute-start.9
  39.9 0.7 constant_dynamic-update-slice_fusion.9
  40.6 1.7 pad_maximum_fusion.3
  42.2 2.1 %collective-permute-start.10 = (bf16[2,96,768]{2,1,0:T(8,128)(2,1)}, bf16[2,96,768]{2,1,0:T(8,128)(2,1)S(1)}, u32[]{:S(2)}, u32[]{:S(2)}) collective-permute-start(bf16[2,96,768]{2,1,0:T(8,128)(2,1)} %pad_maximum_fusion.3), channel_id=1, source_target_pairs={{0,1},{1,0},{2,3},{3,2},{4,5},{5,4},{6,7},{7,6},{8,9},{9,8},{10,11... | collective-permute-start | bytes 884744 | tf_op jit(solution)/shard_map/ppermute | solution.py:564
  44.4 1.1 collective-permute-start.11
  45.5 0.7 constant_dynamic-update-slice_fusion.8
  46.2 0.7 constant_dynamic-update-slice_fusion.7
  46.8 0.7 constant_dynamic-update-slice_fusion.6
  47.5 8.4 %collective-permute-done.10 = bf16[2,96,768]{2,1,0:T(8,128)(2,1)S(1)} collective-permute-done((bf16[2,96,768]{2,1,0:T(8,128)(2,1)}, bf16[2,96,768]{2,1,0:T(8,128)(2,1)S(1)}, u32[]{:S(2)}, u32[]{:S(2)}) %collective-permute-start.10) | collective-permute-done | bytes 294944 | tf_op jit(solution)/shard_map/ppermute | solution.py:564
  56.0 2.8 %collective-permute-done.8 = bf16[8,104,768]{2,1,0:T(8,128)(2,1)S(1)} collective-permute-done((bf16[8,104,768]{2,1,0:T(8,128)(2,1)S(1)}, bf16[8,104,768]{2,1,0:T(8,128)(2,1)S(1)}, u32[]{:S(2)}, u32[]{:S(2)}) %collective-permute-start.8) | collective-permute-done | bytes 1277984 | tf_op jit(solution)/shard_map/ppermute | solution.py:493
  58.8 0.9 constant_dynamic-update-slice_fusion.5
  59.9 4.6 %collective-permute-start.15 = (bf16[2,96,768]{2,1,0:T(8,128)(2,1)}, bf16[2,96,768]{2,1,0:T(8,128)(2,1)}, u32[]{:S(2)}, u32[]{:S(2)}) collective-permute-start(bf16[2,96,768]{2,1,0:T(8,128)(2,1)} %pad_maximum_fusion.3), channel_id=1, source_target_pairs={{0,3},{1,2},{2,1},{3,0},{4,7},{5,6},{6,5},{7,4},{8,11},{9,10},{10,... | collective-permute-start | bytes 884744 | tf_op jit(solution)/shard_map/ppermute | solution.py:564
  64.5 1.0 pad_maximum_fusion.2
  66.2 1.1 copy-done.8
  67.3 11.7 %shard_map.256 = (bf16[4,384,576]{2,1,0:T(8,128)(2,1)}, f32[4,3,128,384]{3,2,1,0:T(8,128)}, bf16[4,384,256]{2,1,0:T(8,128)(2,1)}, f32[384,768]{1,0:T(8,128)S(1)}...) custom-call(bf16[384,768]{1,0:T(8,128)(2,1)S(1)} %copy-done.8, ...), custom_call_target="tpu_custom_call" | custom-call | flops 300000000 | tf_op jit(solution)/shard_map/pallas_call | solution.py:449
  79.8 2.7 %collective-permute-done.19 = bf16[4,96,768]{2,1,0:T(8,128)(2,1)} collective-permute-done((bf16[4,96,768]{2,1,0:T(8,128)(2,1)S(1)}, bf16[4,96,768]{2,1,0:T(8,128)(2,1)}, u32[]{:S(2)}, u32[]{:S(2)}) %collective-permute-start.19) | collective-permute-done | bytes 589856 | tf_op jit(solution)/shard_map/ppermute | solution.py:564
  82.5 1.0 constant_dynamic-update-slice_fusion.10
  84.1 1.4 collective-permute-done.20
  85.6 4.9 %shard_map.257 = (bf16[4,384,768]{2,1,0:T(8,128)(2,1)S(1)}, f32[4,384,768]{2,1,0:T(8,128)S(1)}) custom-call(bf16[384,768]{1,0:T(8,128)(2,1)S(1)} %get-tuple-element.106.n_ref, bf16[2,4,96,768]{3,2,1,0:T(8,128)(2,1)} %bitcast.23.w0_ref, bf16[2,4,96,768]{3,2,1,0:T(8,128)(2,1)} %bitcast.24.w1_ref, bf16[2,4,96,768]{3,2,1,0:T(8,128)(2,1)S(1)} %bitcast.125, ...), custom_call_target="tpu_custom_call" | custom-call | flops 120000000 | tf_op jit(solution)/shard_map/pallas_call | solution.py:449
  90.5 3.0 %collective-permute-done.21 = bf16[4,96,768]{2,1,0:T(8,128)(2,1)S(1)} collective-permute-done((bf16[4,96,768]{2,1,0:T(8,128)(2,1)S(1)}, bf16[4,96,768]{2,1,0:T(8,128)(2,1)S(1)}, u32[]{:S(2)}, u32[]{:S(2)}) %collective-permute-start.21) | collective-permute-done | bytes 589856 | tf_op jit(solution)/shard_map/ppermute | solution.py:564
  93.4 2.0 %collective-permute-done.23 = bf16[4,96,768]{2,1,0:T(8,128)(2,1)S(1)} collective-permute-done((bf16[4,96,768]{2,1,0:T(8,128)(2,1)S(1)}, bf16[4,96,768]{2,1,0:T(8,128)(2,1)S(1)}, u32[]{:S(2)}, u32[]{:S(2)}) %collective-permute-start.23) | collective-permute-done | bytes 589856 | tf_op jit(solution)/shard_map/ppermute | solution.py:484
  95.6 5.1 %shard_map.258 = (f32[3,8,768]{2,1,0:T(8,128)S(1)}, f32[384,768]{1,0:T(8,128)S(1)}, bf16[384,768]{1,0:T(8,128)(2,1)S(1)}, bf16[384,384]{1,0:T(8,128)(2,1)S(1)}, ...) custom-call(bf16[2,2,384,768]{3,2,1,0:T(8,128)(2,1)S(1)} %bitcast.98, bf16[2,2,96,768]{3,2,1,0:T(8,128)(2,1)S(1)} %bitcast.103, ...), custom_call_target="tpu_custom_call" | custom-call | flops 165000000 | tf_op jit(solution)/shard_map/pallas_call | solution.py:449
  101.2 3.4 %shard_map.259 = (bf16[2,2,384,768]{3,2,1,0:T(8,128)(2,1)S(1)}, f32[2,2,1,768]{3,2,1,0:T(1,128)S(1)}) custom-call(bf16[384,768]{1,0:T(8,128)(2,1)S(1)} %get-tuple-element.122.dbb_ref, bf16[2,2,96,768]{3,2,1,0:T(8,128)(2,1)S(1)} %bitcast.104, bf16[2,2,96,768]{3,2,1,0:T(8,128)(2,1)} %bitcast.29.w1_ref, bf16[2,2,96,768]{3,2,1,0:T(8,128)(2,1)S(1)} %bitcast.109, ...), custom_call_target="tpu_custom_call" | custom-call | flops 105000000 | tf_op jit(solution)/shard_map/pallas_call | solution.py:449
  105.1 1.9 shard_map.260
  107.4 5.5 %shard_map.261 = (f32[384,768]{1,0:T(8,128)S(1)}, bf16[384,768]{1,0:T(8,128)(2,1)S(1)}, bf16[384,384]{1,0:T(8,128)(2,1)S(1)}, bf16[384,384]{1,0:T(8,128)(2,1)S(1)}, f32[3,768]{1,0:T(4,128)S(1)}) custom-call(bf16[4,384,768]{2,1,0:T(8,128)(2,1)S(1)} %bitcast.119, bf16[2,4,96,768]{3,2,1,0:T(8,128)(2,1)} %bitcast.23.w0_ref, ...), custom_call_target="tpu_custom_call" | custom-call | flops 60000002048 | tf_op jit(solution)/shard_map/pallas_call | solution.py:449
  112.9 3.3 %shard_map.262 = (bf16[2,4,96,768]{3,2,1,0:T(8,128)(2,1)S(1)}, bf16[2,4,96,768]{3,2,1,0:T(8,128)(2,1)S(1)}) custom-call(bf16[384,384]{1,0:T(8,128)(2,1)S(1)} %copy-done.12, bf16[4,384,768]{2,1,0:T(8,128)(2,1)S(1)} %bitcast.120, bf16[384,384]{1,0:T(8,128)(2,1)S(1)} %collective-permute-done.26.refs_2_, bf16[4,384,768]{2,1,0:T(8,128)(2,1)S(1)} %collective-permute-done.27.refs_3_), custom_call_target="tpu_custom_call" | custom-call | flops 60000000 | tf_op jit(solution)/shard_map/pallas_call | solution.py:449
  116.2 1.8 collective-permute-start.32
  118.6 1.9 shard_map.263
  121.2 2.1 %collective-permute-done.31 = bf16[8,96,768]{2,1,0:T(8,128)(2,1)S(1)} collective-permute-done((bf16[8,96,768]{2,1,0:T(8,128)(2,1)S(1)}, bf16[8,96,768]{2,1,0:T(8,128)(2,1)S(1)}, u32[]{:S(2)}, u32[]{:S(2)}) %collective-permute-start.31) | collective-permute-done | bytes 1179680 | tf_op jit(solution)/shard_map/ppermute | solution.py:513
  123.3 8.7 %shard_map.264 = (bf16[2,384,640]{2,1,0:T(8,128)(2,1)S(1)}, bf16[2,384,640]{2,1,0:T(8,128)(2,1)S(1)}, f32[4,4,768]{2,1,0:T(4,128)S(1)}, f32[4,4,768]{2,1,0:T(4,128)S(1)}) custom-call(bf16[384,768]{1,0:T(8,128)(2,1)S(1)} %get-tuple-element.144.dab_ref, bf16[2,4,104,768]{3,2,1,0:T(8,128)(2,1)S(1)} %bitcast.96, bf16[2,4,104,768]{3,2,1,0:T(8,128)(2,1)S(1)} %bitcast.101, ...), custom_call_target="tpu_custom_call" | custom-call | flops 240000000 | tf_op jit(solution)/shard_map/pallas_call | solution.py:449
  133.2 3.0 %collective-permute-done.32 = bf16[8,96,768]{2,1,0:T(8,128)(2,1)S(1)} collective-permute-done((bf16[8,96,768]{2,1,0:T(8,128)(2,1)S(1)}, bf16[8,96,768]{2,1,0:T(8,128)(2,1)S(1)}, u32[]{:S(2)}, u32[]{:S(2)}) %collective-permute-start.32) | collective-permute-done | bytes 1179680 | tf_op jit(solution)/shard_map/ppermute | solution.py:513
  136.8 2.0 fusion
  138.8 4.3 %shard_map.265 = (bf16[2,4,104,768]{3,2,1,0:T(8,128)(2,1)S(1)}, bf16[2,4,104,768]{3,2,1,0:T(8,128)(2,1)S(1)}) custom-call(bf16[384,384]{1,0:T(8,128)(2,1)S(1)} %copy-done.11, bf16[2,384,640]{2,1,0:T(8,128)(2,1)S(1)} %get-tuple-element.156.refs_1_.low_ref, bf16[2,384,640]{2,1,0:T(8,128)(2,1)S(1)} %get-tuple-element.157.refs_2_.high_ref, ...), custom_call_target="tpu_custom_call" | custom-call | flops 60000000 | tf_op jit(solution)/shard_map/pallas_call | solution.py:449
  143.1 6.0 %collective-permute-done.37 = bf16[4,96,768]{2,1,0:T(8,128)(2,1)S(1)} collective-permute-done((bf16[4,96,768]{2,1,0:T(8,128)(2,1)S(1)}, bf16[4,96,768]{2,1,0:T(8,128)(2,1)S(1)}, u32[]{:S(2)}, u32[]{:S(2)}) %collective-permute-start.37) | collective-permute-done | bytes 589856 | tf_op jit(solution)/shard_map/ppermute | solution.py:513
  149.7 3.7 %collective-permute-start.41 = (bf16[2,96,768]{2,1,0:T(8,128)(2,1)S(1)}, bf16[2,96,768]{2,1,0:T(8,128)(2,1)S(1)}, u32[]{:S(2)}, u32[]{:S(2)}) collective-permute-start(bf16[2,96,768]{2,1,0:T(8,128)(2,1)S(1)} %pad_maximum_fusion.4), channel_id=1, source_target_pairs={{0,1},{1,0},{2,3},{3,2},{4,5},{5,4},{6,7},{7,6},{8,9},{9,8},{10,11... | collective-permute-start | bytes 884744 | tf_op jit(solution)/shard_map/ppermute | solution.py:513
  153.4 2.0 %collective-permute-start.42 = (bf16[2,96,768]{2,1,0:T(8,128)(2,1)S(1)}, bf16[2,96,768]{2,1,0:T(8,128)(2,1)S(1)}, u32[]{:S(2)}, u32[]{:S(2)}) collective-permute-start(bf16[2,96,768]{2,1,0:T(8,128)(2,1)S(1)} %pad_maximum_fusion.5), channel_id=1, source_target_pairs={{0,2},{1,3},{2,0},{3,1},{4,6},{5,7},{6,4},{7,5},{8,10},{9,11},{10,... | collective-permute-start | bytes 884744 | tf_op jit(solution)/shard_map/ppermute | solution.py:513
  155.5 1.5 collective-permute-start.43
  157.0 7.3 %shard_map.266 = f32[384,768]{1,0:T(8,128)} custom-call(bf16[2,384,640]{2,1,0:T(8,128)(2,1)S(1)} %get-tuple-element.156.refs_1_.low_ref, bf16[2,384,640]{2,1,0:T(8,128)(2,1)S(1)} %get-tuple-element.157.refs_2_.high_ref, bf16[2,4,104,768]{3,2,1,0:T(8,128)(2,1)S(1)} %bitcast.97, bf16[2,4,104,768]{3,2,1,0:T(8,128)(2,1)S(1)} %bitcast.102, ...), custom_call_target="tpu_custom_call" | custom-call | flops 120000000 | tf_op jit(solution)/shard_map/pallas_call | solution.py:449
  164.3 2.1 %collective-permute-done.38 = bf16[8,104,768]{2,1,0:T(8,128)(2,1)S(1)} collective-permute-done((bf16[8,104,768]{2,1,0:T(8,128)(2,1)S(1)}, bf16[8,104,768]{2,1,0:T(8,128)(2,1)S(1)}, u32[]{:S(2)}, u32[]{:S(2)}) %collective-permute-start.38) | collective-permute-done | bytes 1277984 | tf_op jit(solution)/shard_map/ppermute | solution.py:513
  166.8 1.7 collective-permute-start.47
  168.9 8.1 %collective-permute-done.42 = bf16[2,96,768]{2,1,0:T(8,128)(2,1)S(1)} collective-permute-done((bf16[2,96,768]{2,1,0:T(8,128)(2,1)S(1)}, bf16[2,96,768]{2,1,0:T(8,128)(2,1)S(1)}, u32[]{:S(2)}, u32[]{:S(2)}) %collective-permute-start.42) | collective-permute-done | bytes 294944 | tf_op jit(solution)/shard_map/ppermute | solution.py:513
  177.1 0.6 collective-permute-start.39
  177.9 3.4 %collective-permute-start.48 = (bf16[1,104,768]{2,1,0:T(8,128)(2,1)S(1)}, bf16[1,104,768]{2,1,0:T(8,128)(2,1)S(1)}, u32[]{:S(2)}, u32[]{:S(2)}) collective-permute-start(bf16[1,104,768]{2,1,0:T(8,128)(2,1)S(1)} %get-tuple-element.167), channel_id=1, source_target_pairs={{0,3},{1,2},{2,1},{3,0},{4,7},{5,6},{6,5},{7,4},{8,11},{9,10},{10,... | collective-permute-start | bytes 479240 | tf_op jit(solution)/shard_map/ppermute | solution.py:513
  181.4 6.2 %collective-permute-start.46 = (bf16[1,104,768]{2,1,0:T(8,128)(2,1)S(1)}, bf16[1,104,768]{2,1,0:T(8,128)(2,1)S(1)}, u32[]{:S(2)}, u32[]{:S(2)}) collective-permute-start(bf16[1,104,768]{2,1,0:T(8,128)(2,1)S(1)} %get-tuple-element.165), channel_id=1, source_target_pairs={{0,2},{1,3},{2,0},{3,1},{4,6},{5,7},{6,4},{7,5},{8,10},{9,11},{10,... | collective-permute-start | bytes 479240 | tf_op jit(solution)/shard_map/ppermute | solution.py:513
  188.1 0.8 slice_bitcast_fusion.2
  189.0 6.4 %collective-permute-done.46 = bf16[1,104,768]{2,1,0:T(8,128)(2,1)S(1)} collective-permute-done((bf16[1,104,768]{2,1,0:T(8,128)(2,1)S(1)}, bf16[1,104,768]{2,1,0:T(8,128)(2,1)S(1)}, u32[]{:S(2)}, u32[]{:S(2)}) %collective-permute-start.46) | collective-permute-done | bytes 159776 | tf_op jit(solution)/shard_map/ppermute | solution.py:513
  195.5 0.9 shard_map.267
  (151 shorter events, 12.0 us)
Async XLA Ops:
  0.6 11.8 %copy-start = (f32[3,1,8,768]{3,2,1,0:T(8,128)S(1)}, f32[3,1,8,768]{3,2,1,0:T(8,128)}, u32[]{:S(2)}) copy-start(f32[3,1,8,768]{3,2,1,0:T(8,128)} %param.17) | copy-start | bytes 221188
  2.6 13.9 %collective-permute-start = (bf16[1,104,768]{2,1,0:T(8,128)(2,1)}, bf16[1,104,768]{2,1,0:T(8,128)(2,1)S(1)}, u32[]{:S(2)}, u32[]{:S(2)}) collective-permute-start(bf16[1,104,768]{2,1,0:T(8,128)(2,1)} %bitcast.137), channel_id=1, source_target_pairs={{0,1},{1,0},{2,3},{3,2},{4,5},{5,4},{6,7},{7,6},{8,9},{9,8},{10,11... | collective-permute-start | bytes 479240 | tf_op jit(solution)/shard_map/ppermute | solution.py:493
  5.6 15.0 %collective-permute-start.1 = (bf16[1,104,768]{2,1,0:T(8,128)(2,1)}, bf16[1,104,768]{2,1,0:T(8,128)(2,1)S(1)}, u32[]{:S(2)}, u32[]{:S(2)}) collective-permute-start(bf16[1,104,768]{2,1,0:T(8,128)(2,1)} %bitcast.138), channel_id=1, source_target_pairs={{0,2},{1,3},{2,0},{3,1},{4,6},{5,7},{6,4},{7,5},{8,10},{9,11},{10,... | collective-permute-start | bytes 479240 | tf_op jit(solution)/shard_map/ppermute | solution.py:493
  8.2 12.4 %collective-permute-start.2 = (bf16[1,104,768]{2,1,0:T(8,128)(2,1)}, bf16[1,104,768]{2,1,0:T(8,128)(2,1)S(1)}, u32[]{:S(2)}, u32[]{:S(2)}) collective-permute-start(bf16[1,104,768]{2,1,0:T(8,128)(2,1)} %bitcast.139), channel_id=1, source_target_pairs={{0,3},{1,2},{2,1},{3,0},{4,7},{5,6},{6,5},{7,4},{8,11},{9,10},{10,... | collective-permute-start | bytes 479240 | tf_op jit(solution)/shard_map/ppermute | solution.py:493
  8.2 12.5 %collective-permute-start.3 = (bf16[1,96,768]{2,1,0:T(8,128)(2,1)}, bf16[1,96,768]{2,1,0:T(8,128)(2,1)}, u32[]{:S(2)}, u32[]{:S(2)}) collective-permute-start(bf16[1,96,768]{2,1,0:T(8,128)(2,1)} %bitcast.146), channel_id=1, source_target_pairs={{0,16},{1,17},{2,18},{3,19},{4,12},{5,13},{6,14},{7,15},{8,24},{9,... | collective-permute-start | bytes 442376 | tf_op jit(solution)/shard_map/ppermute | solution.py:564
  12.5 8.2 %copy-start.19 = (bf16[104,768]{1,0:T(8,128)(2,1)S(1)}, bf16[104,768]{1,0:T(8,128)(2,1)}, u32[]{:S(2)}) copy-start(bf16[104,768]{1,0:T(8,128)(2,1)} %shard_map.255) | copy-start | bytes 479236
  16.5 5.8 %copy-start.20 = (bf16[96,768]{1,0:T(8,128)(2,1)S(1)}, bf16[96,768]{1,0:T(8,128)(2,1)}, u32[]{:S(2)}) copy-start(bf16[96,768]{1,0:T(8,128)(2,1)} %param.24) | copy-start | bytes 442372
  20.7 10.5 %collective-permute-start.4 = (bf16[4,104,768]{2,1,0:T(8,128)(2,1)S(1)}, bf16[4,104,768]{2,1,0:T(8,128)(2,1)S(1)}, u32[]{:S(2)}, u32[]{:S(2)}) collective-permute-start(bf16[4,104,768]{2,1,0:T(8,128)(2,1)S(1)} %pad_maximum_fusion), channel_id=1, source_target_pairs={{0,16},{1,17},{2,18},{3,19},{4,12},{5,13},{6,14},{7,15},{8,24},{9,... | collective-permute-start | bytes 1916936 | tf_op jit(solution)/shard_map/ppermute | solution.py:493
  22.4 8.9 %collective-permute-start.5 = (bf16[1,96,768]{2,1,0:T(8,128)(2,1)S(1)}, bf16[1,96,768]{2,1,0:T(8,128)(2,1)S(1)}, u32[]{:S(2)}, u32[]{:S(2)}) collective-permute-start(bf16[1,96,768]{2,1,0:T(8,128)(2,1)S(1)} %bitcast.142), channel_id=1, source_target_pairs={{0,1},{1,0},{2,3},{3,2},{4,5},{5,4},{6,7},{7,6},{8,9},{9,8},{10,11... | collective-permute-start | bytes 442376 | tf_op jit(solution)/shard_map/ppermute | solution.py:493
  25.0 12.7 %collective-permute-start.6 = (bf16[1,96,768]{2,1,0:T(8,128)(2,1)S(1)}, bf16[1,96,768]{2,1,0:T(8,128)(2,1)S(1)}, u32[]{:S(2)}, u32[]{:S(2)}) collective-permute-start(bf16[1,96,768]{2,1,0:T(8,128)(2,1)S(1)} %bitcast.143), channel_id=1, source_target_pairs={{0,2},{1,3},{2,0},{3,1},{4,6},{5,7},{6,4},{7,5},{8,10},{9,11},{10,... | collective-permute-start | bytes 442376 | tf_op jit(solution)/shard_map/ppermute | solution.py:493
  26.1 11.6 %collective-permute-start.7 = (bf16[1,96,768]{2,1,0:T(8,128)(2,1)S(1)}, bf16[1,96,768]{2,1,0:T(8,128)(2,1)S(1)}, u32[]{:S(2)}, u32[]{:S(2)}) collective-permute-start(bf16[1,96,768]{2,1,0:T(8,128)(2,1)S(1)} %bitcast.144), channel_id=1, source_target_pairs={{0,3},{1,2},{2,1},{3,0},{4,7},{5,6},{6,5},{7,4},{8,11},{9,10},{10,... | collective-permute-start | bytes 442376 | tf_op jit(solution)/shard_map/ppermute | solution.py:493
  27.5 13.1 %copy-start.21 = (bf16[768,96]{0,1:T(8,128)(2,1)S(1)}, bf16[768,96]{0,1:T(8,128)(2,1)}, u32[]{:S(2)}) copy-start(bf16[768,96]{0,1:T(8,128)(2,1)} %param.26) | copy-start | bytes 442372
  37.7 21.1 %collective-permute-start.8 = (bf16[8,104,768]{2,1,0:T(8,128)(2,1)S(1)}, bf16[8,104,768]{2,1,0:T(8,128)(2,1)S(1)}, u32[]{:S(2)}, u32[]{:S(2)}) collective-permute-start(bf16[8,104,768]{2,1,0:T(8,128)(2,1)S(1)} %constant_dynamic-update-slice_fusion), channel_id=1, source_target_pairs={{0,8},{1,9},{2,10},{3,11},{4,20},{5,21},{6,22},{7,23},{8,0},{9,1},... | collective-permute-start | bytes 3833864 | tf_op jit(solution)/shard_map/ppermute | solution.py:493
  38.3 17.6 %collective-permute-start.9 = (bf16[4,96,768]{2,1,0:T(8,128)(2,1)S(1)}, bf16[4,96,768]{2,1,0:T(8,128)(2,1)S(1)}, u32[]{:S(2)}, u32[]{:S(2)}) collective-permute-start(bf16[4,96,768]{2,1,0:T(8,128)(2,1)S(1)} %pad_maximum_fusion.1), channel_id=1, source_target_pairs={{0,16},{1,17},{2,18},{3,19},{4,12},{5,13},{6,14},{7,15},{8,24},{9,... | collective-permute-start | bytes 1769480 | tf_op jit(solution)/shard_map/ppermute | solution.py:493
  42.2 13.6 %collective-permute-start.10 = (bf16[2,96,768]{2,1,0:T(8,128)(2,1)}, bf16[2,96,768]{2,1,0:T(8,128)(2,1)S(1)}, u32[]{:S(2)}, u32[]{:S(2)}) collective-permute-start(bf16[2,96,768]{2,1,0:T(8,128)(2,1)} %pad_maximum_fusion.3), channel_id=1, source_target_pairs={{0,1},{1,0},{2,3},{3,2},{4,5},{5,4},{6,7},{7,6},{8,9},{9,8},{10,11... | collective-permute-start | bytes 884744 | tf_op jit(solution)/shard_map/ppermute | solution.py:564
  44.4 11.5 %collective-permute-start.11 = (bf16[2,96,768]{2,1,0:T(8,128)(2,1)}, bf16[2,96,768]{2,1,0:T(8,128)(2,1)S(1)}, u32[]{:S(2)}, u32[]{:S(2)}) collective-permute-start(bf16[2,96,768]{2,1,0:T(8,128)(2,1)} %pad_maximum_fusion.3), channel_id=1, source_target_pairs={{0,2},{1,3},{2,0},{3,1},{4,6},{5,7},{6,4},{7,5},{8,10},{9,11},{10,... | collective-permute-start | bytes 884744 | tf_op jit(solution)/shard_map/ppermute | solution.py:564
  47.5 18.6 %copy-start.24 = (s32[3,1,128]{2,1,0:T(1,128)S(1)}, s32[3,1,128]{2,1,0:T(1,128)}, u32[]{:S(2)}) copy-start(s32[3,1,128]{2,1,0:T(1,128)} %param.16) | copy-start | bytes 4612
  55.9 4.1 %copy-start.22 = (bf16[2,96,768]{2,1,0:T(8,128)(2,1)}, bf16[2,96,768]{2,1,0:T(8,128)(2,1)S(1)}, u32[]{:S(2)}) copy-start(bf16[2,96,768]{2,1,0:T(8,128)(2,1)S(1)} %collective-permute-done.11) | copy-start | bytes 884740
  55.9 10.3 %collective-permute-start.12 = (bf16[8,104,768]{2,1,0:T(8,128)(2,1)S(1)}, bf16[8,104,768]{2,1,0:T(8,128)(2,1)}, u32[]{:S(2)}, u32[]{:S(2)}) collective-permute-start(bf16[8,104,768]{2,1,0:T(8,128)(2,1)S(1)} %constant_dynamic-update-slice_fusion), channel_id=1, source_target_pairs={{0,4},{1,5},{2,6},{3,7},{4,0},{5,1},{6,2},{7,3},{8,12},{9,13},{10,... | collective-permute-start | bytes 3833864 | tf_op jit(solution)/shard_map/ppermute | solution.py:493
  58.8 7.4 %collective-permute-start.13 = (bf16[8,104,768]{2,1,0:T(8,128)(2,1)S(1)}, bf16[8,104,768]{2,1,0:T(8,128)(2,1)}, u32[]{:S(2)}, u32[]{:S(2)}) collective-permute-start(bf16[8,104,768]{2,1,0:T(8,128)(2,1)S(1)} %collective-permute-done.8), channel_id=1, source_target_pairs={{0,4},{1,5},{2,6},{3,7},{4,0},{5,1},{6,2},{7,3},{8,12},{9,13},{10,... | collective-permute-start | bytes 3833864 | tf_op jit(solution)/shard_map/ppermute | solution.py:493
  59.7 19.4 %collective-permute-start.14 = (bf16[8,96,768]{2,1,0:T(8,128)(2,1)}, bf16[8,96,768]{2,1,0:T(8,128)(2,1)}, u32[]{:S(2)}, u32[]{:S(2)}) collective-permute-start(bf16[8,96,768]{2,1,0:T(8,128)(2,1)} %constant_dynamic-update-slice_fusion.5), channel_id=1, source_target_pairs={{0,8},{1,9},{2,10},{3,11},{4,20},{5,21},{6,22},{7,23},{8,0},{9,1},... | collective-permute-start | bytes 3538952 | tf_op jit(solution)/shard_map/ppermute | solution.py:493
  59.9 19.1 %collective-permute-start.15 = (bf16[2,96,768]{2,1,0:T(8,128)(2,1)}, bf16[2,96,768]{2,1,0:T(8,128)(2,1)}, u32[]{:S(2)}, u32[]{:S(2)}) collective-permute-start(bf16[2,96,768]{2,1,0:T(8,128)(2,1)} %pad_maximum_fusion.3), channel_id=1, source_target_pairs={{0,3},{1,2},{2,1},{3,0},{4,7},{5,6},{6,5},{7,4},{8,11},{9,10},{10,... | collective-permute-start | bytes 884744 | tf_op jit(solution)/shard_map/ppermute | solution.py:564
  65.5 17.0 %collective-permute-start.19 = (bf16[4,96,768]{2,1,0:T(8,128)(2,1)S(1)}, bf16[4,96,768]{2,1,0:T(8,128)(2,1)}, u32[]{:S(2)}, u32[]{:S(2)}) collective-permute-start(bf16[4,96,768]{2,1,0:T(8,128)(2,1)S(1)} %pad_maximum_fusion.2), channel_id=1, source_target_pairs={{0,8},{1,9},{2,10},{3,11},{4,20},{5,21},{6,22},{7,23},{8,0},{9,1},... | collective-permute-start | bytes 1769480 | tf_op jit(solution)/shard_map/ppermute | solution.py:564
  67.3 12.3 %copy-start.23 = (bf16[2,96,768]{2,1,0:T(8,128)(2,1)S(1)}, bf16[2,96,768]{2,1,0:T(8,128)(2,1)}, u32[]{:S(2)}) copy-start(bf16[2,96,768]{2,1,0:T(8,128)(2,1)} %copy-done.22) | copy-start | bytes 884740
  79.1 6.5 %collective-permute-start.16 = (bf16[8,96,768]{2,1,0:T(8,128)(2,1)}, bf16[8,96,768]{2,1,0:T(8,128)(2,1)S(1)}, u32[]{:S(2)}, u32[]{:S(2)}) collective-permute-start(bf16[8,96,768]{2,1,0:T(8,128)(2,1)} %constant_dynamic-update-slice_fusion.5), channel_id=1, source_target_pairs={{0,4},{1,5},{2,6},{3,7},{4,0},{5,1},{6,2},{7,3},{8,12},{9,13},{10,... | collective-permute-start | bytes 3538952 | tf_op jit(solution)/shard_map/ppermute | solution.py:493
  79.1 6.4 %collective-permute-start.17 = (bf16[8,96,768]{2,1,0:T(8,128)(2,1)}, bf16[8,96,768]{2,1,0:T(8,128)(2,1)S(1)}, u32[]{:S(2)}, u32[]{:S(2)}) collective-permute-start(bf16[8,96,768]{2,1,0:T(8,128)(2,1)} %collective-permute-done.14), channel_id=1, source_target_pairs={{0,4},{1,5},{2,6},{3,7},{4,0},{5,1},{6,2},{7,3},{8,12},{9,13},{10,... | collective-permute-start | bytes 3538952 | tf_op jit(solution)/shard_map/ppermute | solution.py:493
  79.7 4.2 %collective-permute-start.18 = (bf16[4,96,768]{2,1,0:T(8,128)(2,1)S(1)}, bf16[4,96,768]{2,1,0:T(8,128)(2,1)S(1)}, u32[]{:S(2)}, u32[]{:S(2)}) collective-permute-start(bf16[4,96,768]{2,1,0:T(8,128)(2,1)S(1)} %pad_maximum_fusion.2), channel_id=1, source_target_pairs={{0,4},{1,5},{2,6},{3,7},{4,0},{5,1},{6,2},{7,3},{8,12},{9,13},{10,... | collective-permute-start | bytes 1769480 | tf_op jit(solution)/shard_map/ppermute | solution.py:484
  82.5 3.1 %collective-permute-start.20 = (bf16[4,96,768]{2,1,0:T(8,128)(2,1)}, bf16[4,96,768]{2,1,0:T(8,128)(2,1)S(1)}, u32[]{:S(2)}, u32[]{:S(2)}) collective-permute-start(bf16[4,96,768]{2,1,0:T(8,128)(2,1)} %collective-permute-done.19), channel_id=1, source_target_pairs={{0,4},{1,5},{2,6},{3,7},{4,0},{5,1},{6,2},{7,3},{8,12},{9,13},{10,... | collective-permute-start | bytes 1769480 | tf_op jit(solution)/shard_map/ppermute | solution.py:484
  83.5 9.9 %collective-permute-start.21 = (bf16[4,96,768]{2,1,0:T(8,128)(2,1)S(1)}, bf16[4,96,768]{2,1,0:T(8,128)(2,1)S(1)}, u32[]{:S(2)}, u32[]{:S(2)}) collective-permute-start(bf16[4,96,768]{2,1,0:T(8,128)(2,1)S(1)} %constant_dynamic-update-slice_fusion.10), channel_id=1, source_target_pairs={{0,8},{1,9},{2,10},{3,11},{4,20},{5,21},{6,22},{7,23},{8,0},{9,1},... | collective-permute-start | bytes 1769480 | tf_op jit(solution)/shard_map/ppermute | solution.py:564
  83.8 9.6 %collective-permute-start.22 = (bf16[4,96,768]{2,1,0:T(8,128)(2,1)S(1)}, bf16[4,96,768]{2,1,0:T(8,128)(2,1)S(1)}, u32[]{:S(2)}, u32[]{:S(2)}) collective-permute-start(bf16[4,96,768]{2,1,0:T(8,128)(2,1)S(1)} %constant_dynamic-update-slice_fusion.10), channel_id=1, source_target_pairs={{0,4},{1,5},{2,6},{3,7},{4,0},{5,1},{6,2},{7,3},{8,12},{9,13},{10,... | collective-permute-start | bytes 1769480 | tf_op jit(solution)/shard_map/ppermute | solution.py:484
  93.4 2.0 %collective-permute-start.23 = (bf16[4,96,768]{2,1,0:T(8,128)(2,1)S(1)}, bf16[4,96,768]{2,1,0:T(8,128)(2,1)S(1)}, u32[]{:S(2)}, u32[]{:S(2)}) collective-permute-start(bf16[4,96,768]{2,1,0:T(8,128)(2,1)S(1)} %collective-permute-done.21), channel_id=1, source_target_pairs={{0,4},{1,5},{2,6},{3,7},{4,0},{5,1},{6,2},{7,3},{8,12},{9,13},{10,... | collective-permute-start | bytes 1769480 | tf_op jit(solution)/shard_map/ppermute | solution.py:484
  95.4 9.6 %collective-permute-start.25 = (bf16[4,384,768]{2,1,0:T(8,128)(2,1)S(1)}, bf16[4,384,768]{2,1,0:T(8,128)(2,1)S(1)}, u32[]{:S(2)}, u32[]{:S(2)}) collective-permute-start(bf16[4,384,768]{2,1,0:T(8,128)(2,1)S(1)} %get-tuple-element.129.refs_1_), channel_id=1, source_target_pairs={{0,4},{1,5},{2,6},{3,7},{4,0},{5,1},{6,2},{7,3},{8,12},{9,13},{10,... | collective-permute-start | bytes 7077896 | tf_op jit(solution)/shard_map/ppermute | solution.py:484
  95.6 5.5 %copy-start.25 = (bf16[384,384]{1,0:T(8,128)(2,1)S(1)}, bf16[384,384]{1,0:T(8,128)(2,1)}, u32[]{:S(2)}) copy-start(bf16[384,384]{1,0:T(8,128)(2,1)} %get-tuple-element.138) | copy-start | bytes 884740
  100.6 4.4 %collective-permute-start.24 = (bf16[384,384]{1,0:T(8,128)(2,1)S(1)}, bf16[384,384]{1,0:T(8,128)(2,1)S(1)}, u32[]{:S(2)}, u32[]{:S(2)}) collective-permute-start(bf16[384,384]{1,0:T(8,128)(2,1)S(1)} %get-tuple-element.128), channel_id=1, source_target_pairs={{0,4},{1,5},{2,6},{3,7},{4,0},{5,1},{6,2},{7,3},{8,12},{9,13},{10,... | collective-permute-start | bytes 884744 | tf_op jit(solution)/shard_map/ppermute | solution.py:484
  101.1 11.8 %collective-permute-start.26 = (bf16[384,384]{1,0:T(8,128)(2,1)S(1)}, bf16[384,384]{1,0:T(8,128)(2,1)S(1)}, u32[]{:S(2)}, u32[]{:S(2)}) collective-permute-start(bf16[384,384]{1,0:T(8,128)(2,1)S(1)} %copy-done.25), channel_id=1, source_target_pairs={{0,4},{1,5},{2,6},{3,7},{4,0},{5,1},{6,2},{7,3},{8,12},{9,13},{10,... | collective-permute-start | bytes 884744 | tf_op jit(solution)/shard_map/ppermute | solution.py:484
  104.6 8.3 %collective-permute-start.27 = (bf16[4,384,768]{2,1,0:T(8,128)(2,1)S(1)}, bf16[4,384,768]{2,1,0:T(8,128)(2,1)S(1)}, u32[]{:S(2)}, u32[]{:S(2)}) collective-permute-start(bf16[4,384,768]{2,1,0:T(8,128)(2,1)S(1)} %bitcast.118), channel_id=1, source_target_pairs={{0,4},{1,5},{2,6},{3,7},{4,0},{5,1},{6,2},{7,3},{8,12},{9,13},{10,... | collective-permute-start | bytes 7077896 | tf_op jit(solution)/shard_map/ppermute | solution.py:484
  107.0 16.3 %collective-permute-start.31 = (bf16[8,96,768]{2,1,0:T(8,128)(2,1)S(1)}, bf16[8,96,768]{2,1,0:T(8,128)(2,1)S(1)}, u32[]{:S(2)}, u32[]{:S(2)}) collective-permute-start(bf16[8,96,768]{2,1,0:T(8,128)(2,1)S(1)} %bitcast.124), channel_id=1, source_target_pairs={{0,8},{1,9},{2,10},{3,11},{4,20},{5,21},{6,22},{7,23},{8,0},{9,1},... | collective-permute-start | bytes 3538952 | tf_op jit(solution)/shard_map/ppermute | solution.py:513
  107.4 5.6 %copy-start.12 = (bf16[384,384]{1,0:T(8,128)(2,1)S(1)}, bf16[384,384]{1,0:T(8,128)(2,1)}, u32[]{:S(2)}) copy-start(bf16[384,384]{1,0:T(8,128)(2,1)} %get-tuple-element.137.refs_0_) | copy-start | bytes 884740
  112.9 5.2 %copy-start.6 = (bf16[4,384,256]{2,1,0:T(8,128)(2,1)S(1)}, bf16[4,384,256]{2,1,0:T(8,128)(2,1)}, u32[]{:S(2)}) copy-start(bf16[4,384,256]{2,1,0:T(8,128)(2,1)} %get-tuple-element.143.refs_7_) | copy-start | bytes 2359300
  112.9 5.2 %copy-start.15 = (bf16[384,384]{1,0:T(8,128)(2,1)S(1)}, bf16[384,384]{1,0:T(8,128)(2,1)}, u32[]{:S(2)}) copy-start(bf16[384,384]{1,0:T(8,128)(2,1)} %copy-done.14) | copy-start | bytes 884740
  116.2 20.0 %collective-permute-start.32 = (bf16[8,96,768]{2,1,0:T(8,128)(2,1)S(1)}, bf16[8,96,768]{2,1,0:T(8,128)(2,1)S(1)}, u32[]{:S(2)}, u32[]{:S(2)}) collective-permute-start(bf16[8,96,768]{2,1,0:T(8,128)(2,1)S(1)} %bitcast.134), channel_id=1, source_target_pairs={{0,8},{1,9},{2,10},{3,11},{4,20},{5,21},{6,22},{7,23},{8,0},{9,1},... | collective-permute-start | bytes 3538952 | tf_op jit(solution)/shard_map/ppermute | solution.py:513
  118.0 2.7 %collective-permute-start.30 = (bf16[4,384,256]{2,1,0:T(8,128)(2,1)S(1)}, bf16[4,384,256]{2,1,0:T(8,128)(2,1)S(1)}, u32[]{:S(2)}, u32[]{:S(2)}) collective-permute-start(bf16[4,384,256]{2,1,0:T(8,128)(2,1)S(1)} %copy-done.6), channel_id=1, source_target_pairs={{0,4},{1,5},{2,6},{3,7},{4,0},{5,1},{6,2},{7,3},{8,12},{9,13},{10,... | collective-permute-start | bytes 2359304 | tf_op jit(solution)/shard_map/ppermute | solution.py:484
  118.0 2.7 %collective-permute-start.29 = (bf16[384,384]{1,0:T(8,128)(2,1)S(1)}, bf16[384,384]{1,0:T(8,128)(2,1)S(1)}, u32[]{:S(2)}, u32[]{:S(2)}) collective-permute-start(bf16[384,384]{1,0:T(8,128)(2,1)S(1)} %copy-done.15), channel_id=1, source_target_pairs={{0,4},{1,5},{2,6},{3,7},{4,0},{5,1},{6,2},{7,3},{8,12},{9,13},{10,... | collective-permute-start | bytes 884744 | tf_op jit(solution)/shard_map/ppermute | solution.py:484
  118.6 2.6 %collective-permute-start.28 = (bf16[384,384]{1,0:T(8,128)(2,1)S(1)}, bf16[384,384]{1,0:T(8,128)(2,1)S(1)}, u32[]{:S(2)}, u32[]{:S(2)}) collective-permute-start(bf16[384,384]{1,0:T(8,128)(2,1)S(1)} %get-tuple-element.141), channel_id=1, source_target_pairs={{0,4},{1,5},{2,6},{3,7},{4,0},{5,1},{6,2},{7,3},{8,12},{9,13},{10,... | collective-permute-start | bytes 884744 | tf_op jit(solution)/shard_map/ppermute | solution.py:484
  118.6 4.6 %copy-start.4 = (f32[4,3,128,384]{3,2,1,0:T(8,128)S(1)}, f32[4,3,128,384]{3,2,1,0:T(8,128)}, u32[]{:S(2)}) copy-start(f32[4,3,128,384]{3,2,1,0:T(8,128)} %get-tuple-element.146.p_ref) | copy-start | bytes 7077892
  118.6 4.6 %copy-start.5 = (bf16[4,384,576]{2,1,0:T(8,128)(2,1)S(1)}, bf16[4,384,576]{2,1,0:T(8,128)(2,1)}, u32[]{:S(2)}) copy-start(bf16[4,384,576]{2,1,0:T(8,128)(2,1)} %get-tuple-element.145.qkv_ref) | copy-start | bytes 5308420
  131.9 6.8 %collective-permute-start.33 = (bf16[2,384,640]{2,1,0:T(8,128)(2,1)S(1)}, bf16[2,384,640]{2,1,0:T(8,128)(2,1)S(1)}, u32[]{:S(2)}, u32[]{:S(2)}) collective-permute-start(bf16[2,384,640]{2,1,0:T(8,128)(2,1)S(1)} %get-tuple-element.156.refs_1_.low_ref), channel_id=1, source_target_pairs={{0,4},{1,5},{2,6},{3,7},{4,0},{5,1},{6,2},{7,3},{8,12},{9,13},{10,... | collective-permute-start | bytes 2949128 | tf_op jit(solution)/shard_map/ppermute | solution.py:484
  132.0 6.7 %collective-permute-start.34 = (bf16[2,384,640]{2,1,0:T(8,128)(2,1)S(1)}, bf16[2,384,640]{2,1,0:T(8,128)(2,1)S(1)}, u32[]{:S(2)}, u32[]{:S(2)}) collective-permute-start(bf16[2,384,640]{2,1,0:T(8,128)(2,1)S(1)} %get-tuple-element.157.refs_2_.high_ref), channel_id=1, source_target_pairs={{0,4},{1,5},{2,6},{3,7},{4,0},{5,1},{6,2},{7,3},{8,12},{9,13},{10,... | collective-permute-start | bytes 2949128 | tf_op jit(solution)/shard_map/ppermute | solution.py:484
  132.8 10.3 %collective-permute-start.36 = (bf16[4,96,768]{2,1,0:T(8,128)(2,1)S(1)}, bf16[4,96,768]{2,1,0:T(8,128)(2,1)S(1)}, u32[]{:S(2)}, u32[]{:S(2)}) collective-permute-start(bf16[4,96,768]{2,1,0:T(8,128)(2,1)S(1)} %get-tuple-element.216), channel_id=1, source_target_pairs={{0,16},{1,17},{2,18},{3,19},{4,12},{5,13},{6,14},{7,15},{8,24},{9,... | collective-permute-start | bytes 1769480 | tf_op jit(solution)/shard_map/ppermute | solution.py:513
  136.5 12.6 %collective-permute-start.37 = (bf16[4,96,768]{2,1,0:T(8,128)(2,1)S(1)}, bf16[4,96,768]{2,1,0:T(8,128)(2,1)S(1)}, u32[]{:S(2)}, u32[]{:S(2)}) collective-permute-start(bf16[4,96,768]{2,1,0:T(8,128)(2,1)S(1)} %get-tuple-element.218), channel_id=1, source_target_pairs={{0,16},{1,17},{2,18},{3,19},{4,12},{5,13},{6,14},{7,15},{8,24},{9,... | collective-permute-start | bytes 1769480 | tf_op jit(solution)/shard_map/ppermute | solution.py:513
  136.8 2.0 collective-permute-start.35
  149.1 17.3 %collective-permute-start.38 = (bf16[8,104,768]{2,1,0:T(8,128)(2,1)S(1)}, bf16[8,104,768]{2,1,0:T(8,128)(2,1)S(1)}, u32[]{:S(2)}, u32[]{:S(2)}) collective-permute-start(bf16[8,104,768]{2,1,0:T(8,128)(2,1)S(1)} %bitcast.133), channel_id=1, source_target_pairs={{0,8},{1,9},{2,10},{3,11},{4,20},{5,21},{6,22},{7,23},{8,0},{9,1},... | collective-permute-start | bytes 3833864 | tf_op jit(solution)/shard_map/ppermute | solution.py:513
  149.6 7.4 %copy-start.3 = (bf16[768,768]{1,0:T(8,128)(2,1)S(1)}, bf16[768,768]{1,0:T(8,128)(2,1)}, u32[]{:S(2)}) copy-start(bf16[768,768]{1,0:T(8,128)(2,1)} %copy-done.2) | copy-start | bytes 3538948
  149.7 18.9 %collective-permute-start.41 = (bf16[2,96,768]{2,1,0:T(8,128)(2,1)S(1)}, bf16[2,96,768]{2,1,0:T(8,128)(2,1)S(1)}, u32[]{:S(2)}, u32[]{:S(2)}) collective-permute-start(bf16[2,96,768]{2,1,0:T(8,128)(2,1)S(1)} %pad_maximum_fusion.4), channel_id=1, source_target_pairs={{0,1},{1,0},{2,3},{3,2},{4,5},{5,4},{6,7},{7,6},{8,9},{9,8},{10,11... | collective-permute-start | bytes 884744 | tf_op jit(solution)/shard_map/ppermute | solution.py:513
  153.4 23.6 %collective-permute-start.42 = (bf16[2,96,768]{2,1,0:T(8,128)(2,1)S(1)}, bf16[2,96,768]{2,1,0:T(8,128)(2,1)S(1)}, u32[]{:S(2)}, u32[]{:S(2)}) collective-permute-start(bf16[2,96,768]{2,1,0:T(8,128)(2,1)S(1)} %pad_maximum_fusion.5), channel_id=1, source_target_pairs={{0,2},{1,3},{2,0},{3,1},{4,6},{5,7},{6,4},{7,5},{8,10},{9,11},{10,... | collective-permute-start | bytes 884744 | tf_op jit(solution)/shard_map/ppermute | solution.py:513
  155.5 21.5 %collective-permute-start.43 = (bf16[2,96,768]{2,1,0:T(8,128)(2,1)S(1)}, bf16[2,96,768]{2,1,0:T(8,128)(2,1)S(1)}, u32[]{:S(2)}, u32[]{:S(2)}) collective-permute-start(bf16[2,96,768]{2,1,0:T(8,128)(2,1)S(1)} %pad_maximum_fusion.6), channel_id=1, source_target_pairs={{0,3},{1,2},{2,1},{3,0},{4,7},{5,6},{6,5},{7,4},{8,11},{9,10},{10,... | collective-permute-start | bytes 884744 | tf_op jit(solution)/shard_map/ppermute | solution.py:513
  166.5 11.2 %collective-permute-start.40 = (bf16[1,104,768]{2,1,0:T(8,128)(2,1)S(1)}, bf16[1,104,768]{2,1,0:T(8,128)(2,1)S(1)}, u32[]{:S(2)}, u32[]{:S(2)}) collective-permute-start(bf16[1,104,768]{2,1,0:T(8,128)(2,1)S(1)} %get-tuple-element.162), channel_id=1, source_target_pairs={{0,16},{1,17},{2,18},{3,19},{4,12},{5,13},{6,14},{7,15},{8,24},{9,... | collective-permute-start | bytes 479240 | tf_op jit(solution)/shard_map/ppermute | solution.py:513
  166.8 10.9 %collective-permute-start.47 = (bf16[1,104,768]{2,1,0:T(8,128)(2,1)S(1)}, bf16[1,104,768]{2,1,0:T(8,128)(2,1)S(1)}, u32[]{:S(2)}, u32[]{:S(2)}) collective-permute-start(bf16[1,104,768]{2,1,0:T(8,128)(2,1)S(1)} %get-tuple-element.166), channel_id=1, source_target_pairs={{0,16},{1,17},{2,18},{3,19},{4,12},{5,13},{6,14},{7,15},{8,24},{9,... | collective-permute-start | bytes 479240 | tf_op jit(solution)/shard_map/ppermute | solution.py:513
  168.6 9.1 %collective-permute-start.45 = (bf16[1,104,768]{2,1,0:T(8,128)(2,1)S(1)}, bf16[1,104,768]{2,1,0:T(8,128)(2,1)S(1)}, u32[]{:S(2)}, u32[]{:S(2)}) collective-permute-start(bf16[1,104,768]{2,1,0:T(8,128)(2,1)S(1)} %get-tuple-element.164), channel_id=1, source_target_pairs={{0,16},{1,17},{2,18},{3,19},{4,12},{5,13},{6,14},{7,15},{8,24},{9,... | collective-permute-start | bytes 479240 | tf_op jit(solution)/shard_map/ppermute | solution.py:513
  177.1 11.8 %collective-permute-start.39 = (bf16[1,104,768]{2,1,0:T(8,128)(2,1)S(1)}, bf16[1,104,768]{2,1,0:T(8,128)(2,1)S(1)}, u32[]{:S(2)}, u32[]{:S(2)}) collective-permute-start(bf16[1,104,768]{2,1,0:T(8,128)(2,1)S(1)} %get-tuple-element.161), channel_id=1, source_target_pairs={{0,16},{1,17},{2,18},{3,19},{4,12},{5,13},{6,14},{7,15},{8,24},{9,... | collective-permute-start | bytes 479240 | tf_op jit(solution)/shard_map/ppermute | solution.py:513
  177.9 11.0 %collective-permute-start.48 = (bf16[1,104,768]{2,1,0:T(8,128)(2,1)S(1)}, bf16[1,104,768]{2,1,0:T(8,128)(2,1)S(1)}, u32[]{:S(2)}, u32[]{:S(2)}) collective-permute-start(bf16[1,104,768]{2,1,0:T(8,128)(2,1)S(1)} %get-tuple-element.167), channel_id=1, source_target_pairs={{0,3},{1,2},{2,1},{3,0},{4,7},{5,6},{6,5},{7,4},{8,11},{9,10},{10,... | collective-permute-start | bytes 479240 | tf_op jit(solution)/shard_map/ppermute | solution.py:513
  181.4 14.0 %collective-permute-start.46 = (bf16[1,104,768]{2,1,0:T(8,128)(2,1)S(1)}, bf16[1,104,768]{2,1,0:T(8,128)(2,1)S(1)}, u32[]{:S(2)}, u32[]{:S(2)}) collective-permute-start(bf16[1,104,768]{2,1,0:T(8,128)(2,1)S(1)} %get-tuple-element.165), channel_id=1, source_target_pairs={{0,2},{1,3},{2,0},{3,1},{4,6},{5,7},{6,4},{7,5},{8,10},{9,11},{10,... | collective-permute-start | bytes 479240 | tf_op jit(solution)/shard_map/ppermute | solution.py:513
  187.6 8.8 %copy-start.1 = (f32[3,1,8,768]{3,2,1,0:T(8,128)S(1)}, f32[3,1,8,768]{3,2,1,0:T(8,128)}, u32[]{:S(2)}) copy-start(f32[3,1,8,768]{3,2,1,0:T(8,128)} %param.17) | copy-start | bytes 221188
  187.6 7.7 %collective-permute-start.44 = (bf16[1,104,768]{2,1,0:T(8,128)(2,1)S(1)}, bf16[1,104,768]{2,1,0:T(8,128)(2,1)S(1)}, u32[]{:S(2)}, u32[]{:S(2)}) collective-permute-start(bf16[1,104,768]{2,1,0:T(8,128)(2,1)S(1)} %get-tuple-element.163), channel_id=1, source_target_pairs={{0,1},{1,0},{2,3},{3,2},{4,5},{5,4},{6,7},{7,6},{8,9},{9,8},{10,11... | collective-permute-start | bytes 479240 | tf_op jit(solution)/shard_map/ppermute | solution.py:513
  (11 other events, 21.2 us)

commit v12 on v11

--- a/solution.py
+++ b/solution.py
@@ -660,7 +660,6 @@
         high_far = move(high, "3")
         w_up = middle.pieces(2, n_t)
         low_other = [swap(low, tables, n1b), swap(after(low_far, n1b), tables)]
-        n1_other = swap(n1_send, tables)
         o_other = swap(o, tables)
         b_u = after(b_u, *low_other)
     z, dgelu = call(
@@ -713,6 +712,7 @@
         db_other = swap(db_send, tables)
         du_other = swap(du, tables)
         down_keep, down_send = gradient([[fc, (after(db_keep, g_bu), [z]), (db_other, [z_other])]], at_once=False)
+        n1_other = swap(n1_send, tables, down_send)
         s_down = Scatter(flat(down_keep), flat(down_send), tables)
         got_d3 = s_down.stage("3", 2)
         du_next = after(du, down_send)

time: 197 us -> 197 us (level)
  no operation moved by 1% of the time
where the time goes in v12:
time: 197 us
  waiting for transfers between devices  62.8 us (32%)
  Pallas kernels  61.5 us (31%)
  starting transfers between devices  52.1 us (26%)
  local copies, waits for them, and re-layouts  10.3 us (5%)
  other arithmetic  5.41 us (3%)
  matrix products  2.99 us (2%)
    pallas_call x11, Pallas kernels, call(): pl.pallas_call(body, grid=(n_t,), in_specs=[s for _, s in ins], out_specs...  57.9 us
    ppermute x15, waiting for transfers between devices, stage(): lax.ppermute(after(s, *done), AXES, tables[n // pieces])  27.7 us
    ppermute x15, starting transfers between devices, stage(): lax.ppermute(after(s, *done), AXES, tables[n // pieces])  23.4 us
    ppermute x14, waiting for transfers between devices, send(): lax.ppermute(after(h, *done), AXES, t)  17.1 us
    ppermute x14, starting transfers between devices, send(): lax.ppermute(after(h, *done), AXES, t)  15.4 us
    ppermute x6, waiting for transfers between devices, move(): return lax.ppermute(after(value, *done), AXES, tables[name][way])  14 us
    ppermute x6, starting transfers between devices, move(): return lax.ppermute(after(value, *done), AXES, tables[name][way])  10.5 us
    unnamed x62, local copies, waits for them, and re-layouts  6.1 us
  transfers between devices with their start and end apart: 49, of which 17 were waited for; matrix products, arithmetic and copies ran while one was open for 8% of the time, Pallas kernels for 30%

profile of v12, /device:TPU:0, one launch (start us, length us, event | category | flops | bytes accessed | tf_op | source)
XLA Modules:
  0.0 196.5 jit_solution(629318193115422818)
XLA Ops:
  0.7 2.0 shard_map.255
  2.6 3.0 %collective-permute-start = (bf16[1,104,768]{2,1,0:T(8,128)(2,1)}, bf16[1,104,768]{2,1,0:T(8,128)(2,1)S(1)}, u32[]{:S(2)}, u32[]{:S(2)}) collective-permute-start(bf16[1,104,768]{2,1,0:T(8,128)(2,1)} %bitcast.137), channel_id=1, source_target_pairs={{0,1},{1,0},{2,3},{3,2},{4,5},{5,4},{6,7},{7,6},{8,9},{9,8},{10,11... | collective-permute-start | bytes 479240 | tf_op jit(solution)/shard_map/ppermute | solution.py:493
  5.6 2.6 %collective-permute-start.1 = (bf16[1,104,768]{2,1,0:T(8,128)(2,1)}, bf16[1,104,768]{2,1,0:T(8,128)(2,1)S(1)}, u32[]{:S(2)}, u32[]{:S(2)}) collective-permute-start(bf16[1,104,768]{2,1,0:T(8,128)(2,1)} %bitcast.138), channel_id=1, source_target_pairs={{0,2},{1,3},{2,0},{3,1},{4,6},{5,7},{6,4},{7,5},{8,10},{9,11},{10,... | collective-permute-start | bytes 479240 | tf_op jit(solution)/shard_map/ppermute | solution.py:493
  8.2 1.7 collective-permute-start.3
  10.4 0.7 copy.30
  12.5 1.0 convolution_bitcast_fusion.pg_ref
  13.6 0.7 shard_map.254
  14.3 0.8 copy-done.7
  15.1 0.7 copy-done.10
  15.8 0.7 copy-done.14
  16.6 4.1 %collective-permute-done.1 = bf16[1,104,768]{2,1,0:T(8,128)(2,1)S(1)} collective-permute-done((bf16[1,104,768]{2,1,0:T(8,128)(2,1)}, bf16[1,104,768]{2,1,0:T(8,128)(2,1)S(1)}, u32[]{:S(2)}, u32[]{:S(2)}) %collective-permute-start.1) | collective-permute-done | bytes 159776 | tf_op jit(solution)/shard_map/ppermute | solution.py:493
  20.7 1.6 collective-permute-start.4
  22.4 2.6 %collective-permute-start.5 = (bf16[1,96,768]{2,1,0:T(8,128)(2,1)S(1)}, bf16[1,96,768]{2,1,0:T(8,128)(2,1)S(1)}, u32[]{:S(2)}, u32[]{:S(2)}) collective-permute-start(bf16[1,96,768]{2,1,0:T(8,128)(2,1)S(1)} %bitcast.142), channel_id=1, source_target_pairs={{0,1},{1,0},{2,3},{3,2},{4,5},{5,4},{6,7},{7,6},{8,9},{9,8},{10,11... | collective-permute-start | bytes 442376 | tf_op jit(solution)/shard_map/ppermute | solution.py:493
  25.0 1.1 collective-permute-start.6
  26.1 1.4 collective-permute-start.7
  27.5 3.7 %collective-permute-done.4 = bf16[4,104,768]{2,1,0:T(8,128)(2,1)S(1)} collective-permute-done((bf16[4,104,768]{2,1,0:T(8,128)(2,1)S(1)}, bf16[4,104,768]{2,1,0:T(8,128)(2,1)S(1)}, u32[]{:S(2)}, u32[]{:S(2)}) %collective-permute-start.4) | collective-permute-done | bytes 639008 | tf_op jit(solution)/shard_map/ppermute | solution.py:493
  31.3 6.4 %collective-permute-done.6 = bf16[1,96,768]{2,1,0:T(8,128)(2,1)S(1)} collective-permute-done((bf16[1,96,768]{2,1,0:T(8,128)(2,1)S(1)}, bf16[1,96,768]{2,1,0:T(8,128)(2,1)S(1)}, u32[]{:S(2)}, u32[]{:S(2)}) %collective-permute-start.6) | collective-permute-done | bytes 147488 | tf_op jit(solution)/shard_map/ppermute | solution.py:493
  38.3 1.6 collective-permute-start.9
  39.9 0.7 constant_dynamic-update-slice_fusion.9
  40.6 1.7 pad_maximum_fusion.3
  42.2 2.1 %collective-permute-start.10 = (bf16[2,96,768]{2,1,0:T(8,128)(2,1)}, bf16[2,96,768]{2,1,0:T(8,128)(2,1)S(1)}, u32[]{:S(2)}, u32[]{:S(2)}) collective-permute-start(bf16[2,96,768]{2,1,0:T(8,128)(2,1)} %pad_maximum_fusion.3), channel_id=1, source_target_pairs={{0,1},{1,0},{2,3},{3,2},{4,5},{5,4},{6,7},{7,6},{8,9},{9,8},{10,11... | collective-permute-start | bytes 884744 | tf_op jit(solution)/shard_map/ppermute | solution.py:564
  44.4 1.1 collective-permute-start.11
  45.5 0.7 constant_dynamic-update-slice_fusion.8
  46.2 0.7 constant_dynamic-update-slice_fusion.7
  46.8 0.7 constant_dynamic-update-slice_fusion.6
  47.5 8.4 %collective-permute-done.10 = bf16[2,96,768]{2,1,0:T(8,128)(2,1)S(1)} collective-permute-done((bf16[2,96,768]{2,1,0:T(8,128)(2,1)}, bf16[2,96,768]{2,1,0:T(8,128)(2,1)S(1)}, u32[]{:S(2)}, u32[]{:S(2)}) %collective-permute-start.10) | collective-permute-done | bytes 294944 | tf_op jit(solution)/shard_map/ppermute | solution.py:564
  56.0 2.8 %collective-permute-done.8 = bf16[8,104,768]{2,1,0:T(8,128)(2,1)S(1)} collective-permute-done((bf16[8,104,768]{2,1,0:T(8,128)(2,1)S(1)}, bf16[8,104,768]{2,1,0:T(8,128)(2,1)S(1)}, u32[]{:S(2)}, u32[]{:S(2)}) %collective-permute-start.8) | collective-permute-done | bytes 1277984 | tf_op jit(solution)/shard_map/ppermute | solution.py:493
  58.8 0.9 constant_dynamic-update-slice_fusion.5
  59.9 4.6 %collective-permute-start.15 = (bf16[2,96,768]{2,1,0:T(8,128)(2,1)}, bf16[2,96,768]{2,1,0:T(8,128)(2,1)}, u32[]{:S(2)}, u32[]{:S(2)}) collective-permute-start(bf16[2,96,768]{2,1,0:T(8,128)(2,1)} %pad_maximum_fusion.3), channel_id=1, source_target_pairs={{0,3},{1,2},{2,1},{3,0},{4,7},{5,6},{6,5},{7,4},{8,11},{9,10},{10,... | collective-permute-start | bytes 884744 | tf_op jit(solution)/shard_map/ppermute | solution.py:564
  64.5 1.0 pad_maximum_fusion.2
  66.2 1.1 copy-done.8
  67.3 11.7 %shard_map.256 = (bf16[4,384,576]{2,1,0:T(8,128)(2,1)}, f32[4,3,128,384]{3,2,1,0:T(8,128)}, bf16[4,384,256]{2,1,0:T(8,128)(2,1)}, f32[384,768]{1,0:T(8,128)S(1)}...) custom-call(bf16[384,768]{1,0:T(8,128)(2,1)S(1)} %copy-done.8, ...), custom_call_target="tpu_custom_call" | custom-call | flops 300000000 | tf_op jit(solution)/shard_map/pallas_call | solution.py:449
  79.8 2.7 %collective-permute-done.19 = bf16[4,96,768]{2,1,0:T(8,128)(2,1)} collective-permute-done((bf16[4,96,768]{2,1,0:T(8,128)(2,1)S(1)}, bf16[4,96,768]{2,1,0:T(8,128)(2,1)}, u32[]{:S(2)}, u32[]{:S(2)}) %collective-permute-start.19) | collective-permute-done | bytes 589856 | tf_op jit(solution)/shard_map/ppermute | solution.py:564
  82.5 1.0 constant_dynamic-update-slice_fusion.10
  84.1 1.4 collective-permute-done.20
  85.6 4.9 %shard_map.257 = (bf16[4,384,768]{2,1,0:T(8,128)(2,1)S(1)}, f32[4,384,768]{2,1,0:T(8,128)S(1)}) custom-call(bf16[384,768]{1,0:T(8,128)(2,1)S(1)} %get-tuple-element.107.n_ref, bf16[2,4,96,768]{3,2,1,0:T(8,128)(2,1)} %bitcast.23.w0_ref, bf16[2,4,96,768]{3,2,1,0:T(8,128)(2,1)} %bitcast.24.w1_ref, bf16[2,4,96,768]{3,2,1,0:T(8,128)(2,1)S(1)} %bitcast.125, ...), custom_call_target="tpu_custom_call" | custom-call | flops 120000000 | tf_op jit(solution)/shard_map/pallas_call | solution.py:449
  90.5 3.0 %collective-permute-done.21 = bf16[4,96,768]{2,1,0:T(8,128)(2,1)S(1)} collective-permute-done((bf16[4,96,768]{2,1,0:T(8,128)(2,1)S(1)}, bf16[4,96,768]{2,1,0:T(8,128)(2,1)S(1)}, u32[]{:S(2)}, u32[]{:S(2)}) %collective-permute-start.21) | collective-permute-done | bytes 589856 | tf_op jit(solution)/shard_map/ppermute | solution.py:564
  93.4 2.0 %collective-permute-done.23 = bf16[4,96,768]{2,1,0:T(8,128)(2,1)S(1)} collective-permute-done((bf16[4,96,768]{2,1,0:T(8,128)(2,1)S(1)}, bf16[4,96,768]{2,1,0:T(8,128)(2,1)S(1)}, u32[]{:S(2)}, u32[]{:S(2)}) %collective-permute-start.23) | collective-permute-done | bytes 589856 | tf_op jit(solution)/shard_map/ppermute | solution.py:484
  95.6 5.0 %shard_map.258 = (f32[3,8,768]{2,1,0:T(8,128)S(1)}, f32[384,768]{1,0:T(8,128)S(1)}, bf16[384,768]{1,0:T(8,128)(2,1)S(1)}, bf16[384,384]{1,0:T(8,128)(2,1)S(1)}, ...) custom-call(bf16[2,2,384,768]{3,2,1,0:T(8,128)(2,1)S(1)} %bitcast.98, bf16[2,2,96,768]{3,2,1,0:T(8,128)(2,1)S(1)} %bitcast.103, ...), custom_call_target="tpu_custom_call" | custom-call | flops 165000000 | tf_op jit(solution)/shard_map/pallas_call | solution.py:449
  101.1 3.4 %shard_map.259 = (bf16[2,2,384,768]{3,2,1,0:T(8,128)(2,1)S(1)}, f32[2,2,1,768]{3,2,1,0:T(1,128)S(1)}) custom-call(bf16[384,768]{1,0:T(8,128)(2,1)S(1)} %get-tuple-element.123.dbb_ref, bf16[2,2,96,768]{3,2,1,0:T(8,128)(2,1)S(1)} %bitcast.104, bf16[2,2,96,768]{3,2,1,0:T(8,128)(2,1)} %bitcast.29.w1_ref, bf16[2,2,96,768]{3,2,1,0:T(8,128)(2,1)S(1)} %bitcast.109, ...), custom_call_target="tpu_custom_call" | custom-call | flops 105000000 | tf_op jit(solution)/shard_map/pallas_call | solution.py:449
  104.7 1.9 shard_map.260
  107.3 5.5 %shard_map.261 = (f32[384,768]{1,0:T(8,128)S(1)}, bf16[384,768]{1,0:T(8,128)(2,1)S(1)}, bf16[384,384]{1,0:T(8,128)(2,1)S(1)}, bf16[384,384]{1,0:T(8,128)(2,1)S(1)}, f32[3,768]{1,0:T(4,128)S(1)}) custom-call(bf16[4,384,768]{2,1,0:T(8,128)(2,1)S(1)} %bitcast.119, bf16[2,4,96,768]{3,2,1,0:T(8,128)(2,1)} %bitcast.23.w0_ref, ...), custom_call_target="tpu_custom_call" | custom-call | flops 60000002048 | tf_op jit(solution)/shard_map/pallas_call | solution.py:449
  112.9 3.3 %shard_map.262 = (bf16[2,4,96,768]{3,2,1,0:T(8,128)(2,1)S(1)}, bf16[2,4,96,768]{3,2,1,0:T(8,128)(2,1)S(1)}) custom-call(bf16[384,384]{1,0:T(8,128)(2,1)S(1)} %copy-done.12, bf16[4,384,768]{2,1,0:T(8,128)(2,1)S(1)} %bitcast.120, bf16[384,384]{1,0:T(8,128)(2,1)S(1)} %collective-permute-done.26.refs_2_, bf16[4,384,768]{2,1,0:T(8,128)(2,1)S(1)} %collective-permute-done.27.refs_3_), custom_call_target="tpu_custom_call" | custom-call | flops 60000000 | tf_op jit(solution)/shard_map/pallas_call | solution.py:449
  116.2 1.8 collective-permute-start.32
  118.6 1.9 shard_map.263
  121.1 2.1 %collective-permute-done.31 = bf16[8,96,768]{2,1,0:T(8,128)(2,1)S(1)} collective-permute-done((bf16[8,96,768]{2,1,0:T(8,128)(2,1)S(1)}, bf16[8,96,768]{2,1,0:T(8,128)(2,1)S(1)}, u32[]{:S(2)}, u32[]{:S(2)}) %collective-permute-start.31) | collective-permute-done | bytes 1179680 | tf_op jit(solution)/shard_map/ppermute | solution.py:513
  123.3 8.7 %shard_map.264 = (bf16[2,384,640]{2,1,0:T(8,128)(2,1)S(1)}, bf16[2,384,640]{2,1,0:T(8,128)(2,1)S(1)}, f32[4,4,768]{2,1,0:T(4,128)S(1)}, f32[4,4,768]{2,1,0:T(4,128)S(1)}) custom-call(bf16[384,768]{1,0:T(8,128)(2,1)S(1)} %get-tuple-element.146.dab_ref, bf16[2,4,104,768]{3,2,1,0:T(8,128)(2,1)S(1)} %bitcast.96, bf16[2,4,104,768]{3,2,1,0:T(8,128)(2,1)S(1)} %bitcast.101, ...), custom_call_target="tpu_custom_call" | custom-call | flops 240000000 | tf_op jit(solution)/shard_map/pallas_call | solution.py:449
  133.1 3.0 %collective-permute-done.32 = bf16[8,96,768]{2,1,0:T(8,128)(2,1)S(1)} collective-permute-done((bf16[8,96,768]{2,1,0:T(8,128)(2,1)S(1)}, bf16[8,96,768]{2,1,0:T(8,128)(2,1)S(1)}, u32[]{:S(2)}, u32[]{:S(2)}) %collective-permute-start.32) | collective-permute-done | bytes 1179680 | tf_op jit(solution)/shard_map/ppermute | solution.py:513
  136.8 2.0 fusion
  138.8 4.3 %shard_map.265 = (bf16[2,4,104,768]{3,2,1,0:T(8,128)(2,1)S(1)}, bf16[2,4,104,768]{3,2,1,0:T(8,128)(2,1)S(1)}) custom-call(bf16[384,384]{1,0:T(8,128)(2,1)S(1)} %copy-done.11, bf16[2,384,640]{2,1,0:T(8,128)(2,1)S(1)} %get-tuple-element.158.refs_1_.low_ref, bf16[2,384,640]{2,1,0:T(8,128)(2,1)S(1)} %get-tuple-element.159.refs_2_.high_ref, ...), custom_call_target="tpu_custom_call" | custom-call | flops 60000000 | tf_op jit(solution)/shard_map/pallas_call | solution.py:449
  143.1 6.0 %collective-permute-done.37 = bf16[4,96,768]{2,1,0:T(8,128)(2,1)S(1)} collective-permute-done((bf16[4,96,768]{2,1,0:T(8,128)(2,1)S(1)}, bf16[4,96,768]{2,1,0:T(8,128)(2,1)S(1)}, u32[]{:S(2)}, u32[]{:S(2)}) %collective-permute-start.37) | collective-permute-done | bytes 589856 | tf_op jit(solution)/shard_map/ppermute | solution.py:513
  149.7 3.7 %collective-permute-start.41 = (bf16[2,96,768]{2,1,0:T(8,128)(2,1)S(1)}, bf16[2,96,768]{2,1,0:T(8,128)(2,1)S(1)}, u32[]{:S(2)}, u32[]{:S(2)}) collective-permute-start(bf16[2,96,768]{2,1,0:T(8,128)(2,1)S(1)} %pad_maximum_fusion.4), channel_id=1, source_target_pairs={{0,1},{1,0},{2,3},{3,2},{4,5},{5,4},{6,7},{7,6},{8,9},{9,8},{10,11... | collective-permute-start | bytes 884744 | tf_op jit(solution)/shard_map/ppermute | solution.py:513
  153.4 2.0 %collective-permute-start.42 = (bf16[2,96,768]{2,1,0:T(8,128)(2,1)S(1)}, bf16[2,96,768]{2,1,0:T(8,128)(2,1)S(1)}, u32[]{:S(2)}, u32[]{:S(2)}) collective-permute-start(bf16[2,96,768]{2,1,0:T(8,128)(2,1)S(1)} %pad_maximum_fusion.5), channel_id=1, source_target_pairs={{0,2},{1,3},{2,0},{3,1},{4,6},{5,7},{6,4},{7,5},{8,10},{9,11},{10,... | collective-permute-start | bytes 884744 | tf_op jit(solution)/shard_map/ppermute | solution.py:513
  155.5 1.5 collective-permute-start.43
  157.0 7.3 %shard_map.266 = f32[384,768]{1,0:T(8,128)} custom-call(bf16[2,384,640]{2,1,0:T(8,128)(2,1)S(1)} %get-tuple-element.158.refs_1_.low_ref, bf16[2,384,640]{2,1,0:T(8,128)(2,1)S(1)} %get-tuple-element.159.refs_2_.high_ref, bf16[2,4,104,768]{3,2,1,0:T(8,128)(2,1)S(1)} %bitcast.97, bf16[2,4,104,768]{3,2,1,0:T(8,128)(2,1)S(1)} %bitcast.102, ...), custom_call_target="tpu_custom_call" | custom-call | flops 120000000 | tf_op jit(solution)/shard_map/pallas_call | solution.py:449
  164.3 2.1 %collective-permute-done.38 = bf16[8,104,768]{2,1,0:T(8,128)(2,1)S(1)} collective-permute-done((bf16[8,104,768]{2,1,0:T(8,128)(2,1)S(1)}, bf16[8,104,768]{2,1,0:T(8,128)(2,1)S(1)}, u32[]{:S(2)}, u32[]{:S(2)}) %collective-permute-start.38) | collective-permute-done | bytes 1277984 | tf_op jit(solution)/shard_map/ppermute | solution.py:513
  166.8 1.8 collective-permute-start.47
  168.9 8.1 %collective-permute-done.42 = bf16[2,96,768]{2,1,0:T(8,128)(2,1)S(1)} collective-permute-done((bf16[2,96,768]{2,1,0:T(8,128)(2,1)S(1)}, bf16[2,96,768]{2,1,0:T(8,128)(2,1)S(1)}, u32[]{:S(2)}, u32[]{:S(2)}) %collective-permute-start.42) | collective-permute-done | bytes 294944 | tf_op jit(solution)/shard_map/ppermute | solution.py:513
  177.1 0.6 collective-permute-start.39
  177.9 3.4 %collective-permute-start.48 = (bf16[1,104,768]{2,1,0:T(8,128)(2,1)S(1)}, bf16[1,104,768]{2,1,0:T(8,128)(2,1)S(1)}, u32[]{:S(2)}, u32[]{:S(2)}) collective-permute-start(bf16[1,104,768]{2,1,0:T(8,128)(2,1)S(1)} %get-tuple-element.169), channel_id=1, source_target_pairs={{0,3},{1,2},{2,1},{3,0},{4,7},{5,6},{6,5},{7,4},{8,11},{9,10},{10,... | collective-permute-start | bytes 479240 | tf_op jit(solution)/shard_map/ppermute | solution.py:513
  181.4 6.2 %collective-permute-start.46 = (bf16[1,104,768]{2,1,0:T(8,128)(2,1)S(1)}, bf16[1,104,768]{2,1,0:T(8,128)(2,1)S(1)}, u32[]{:S(2)}, u32[]{:S(2)}) collective-permute-start(bf16[1,104,768]{2,1,0:T(8,128)(2,1)S(1)} %get-tuple-element.167), channel_id=1, source_target_pairs={{0,2},{1,3},{2,0},{3,1},{4,6},{5,7},{6,4},{7,5},{8,10},{9,11},{10,... | collective-permute-start | bytes 479240 | tf_op jit(solution)/shard_map/ppermute | solution.py:513
  188.1 0.8 slice_bitcast_fusion.2
  189.0 6.4 %collective-permute-done.46 = bf16[1,104,768]{2,1,0:T(8,128)(2,1)S(1)} collective-permute-done((bf16[1,104,768]{2,1,0:T(8,128)(2,1)S(1)}, bf16[1,104,768]{2,1,0:T(8,128)(2,1)S(1)}, u32[]{:S(2)}, u32[]{:S(2)}) %collective-permute-start.46) | collective-permute-done | bytes 159776 | tf_op jit(solution)/shard_map/ppermute | solution.py:513
  195.5 0.9 shard_map.267
  (151 shorter events, 12.0 us)
Async XLA Ops:
  0.6 11.8 %copy-start = (f32[3,1,8,768]{3,2,1,0:T(8,128)S(1)}, f32[3,1,8,768]{3,2,1,0:T(8,128)}, u32[]{:S(2)}) copy-start(f32[3,1,8,768]{3,2,1,0:T(8,128)} %param.17) | copy-start | bytes 221188
  2.6 13.9 %collective-permute-start = (bf16[1,104,768]{2,1,0:T(8,128)(2,1)}, bf16[1,104,768]{2,1,0:T(8,128)(2,1)S(1)}, u32[]{:S(2)}, u32[]{:S(2)}) collective-permute-start(bf16[1,104,768]{2,1,0:T(8,128)(2,1)} %bitcast.137), channel_id=1, source_target_pairs={{0,1},{1,0},{2,3},{3,2},{4,5},{5,4},{6,7},{7,6},{8,9},{9,8},{10,11... | collective-permute-start | bytes 479240 | tf_op jit(solution)/shard_map/ppermute | solution.py:493
  5.6 15.0 %collective-permute-start.1 = (bf16[1,104,768]{2,1,0:T(8,128)(2,1)}, bf16[1,104,768]{2,1,0:T(8,128)(2,1)S(1)}, u32[]{:S(2)}, u32[]{:S(2)}) collective-permute-start(bf16[1,104,768]{2,1,0:T(8,128)(2,1)} %bitcast.138), channel_id=1, source_target_pairs={{0,2},{1,3},{2,0},{3,1},{4,6},{5,7},{6,4},{7,5},{8,10},{9,11},{10,... | collective-permute-start | bytes 479240 | tf_op jit(solution)/shard_map/ppermute | solution.py:493
  8.2 12.4 %collective-permute-start.2 = (bf16[1,104,768]{2,1,0:T(8,128)(2,1)}, bf16[1,104,768]{2,1,0:T(8,128)(2,1)S(1)}, u32[]{:S(2)}, u32[]{:S(2)}) collective-permute-start(bf16[1,104,768]{2,1,0:T(8,128)(2,1)} %bitcast.139), channel_id=1, source_target_pairs={{0,3},{1,2},{2,1},{3,0},{4,7},{5,6},{6,5},{7,4},{8,11},{9,10},{10,... | collective-permute-start | bytes 479240 | tf_op jit(solution)/shard_map/ppermute | solution.py:493
  8.2 12.5 %collective-permute-start.3 = (bf16[1,96,768]{2,1,0:T(8,128)(2,1)}, bf16[1,96,768]{2,1,0:T(8,128)(2,1)}, u32[]{:S(2)}, u32[]{:S(2)}) collective-permute-start(bf16[1,96,768]{2,1,0:T(8,128)(2,1)} %bitcast.146), channel_id=1, source_target_pairs={{0,16},{1,17},{2,18},{3,19},{4,12},{5,13},{6,14},{7,15},{8,24},{9,... | collective-permute-start | bytes 442376 | tf_op jit(solution)/shard_map/ppermute | solution.py:564
  12.5 8.2 %copy-start.19 = (bf16[104,768]{1,0:T(8,128)(2,1)S(1)}, bf16[104,768]{1,0:T(8,128)(2,1)}, u32[]{:S(2)}) copy-start(bf16[104,768]{1,0:T(8,128)(2,1)} %shard_map.255) | copy-start | bytes 479236
  16.5 5.8 %copy-start.20 = (bf16[96,768]{1,0:T(8,128)(2,1)S(1)}, bf16[96,768]{1,0:T(8,128)(2,1)}, u32[]{:S(2)}) copy-start(bf16[96,768]{1,0:T(8,128)(2,1)} %param.24) | copy-start | bytes 442372
  20.7 10.5 %collective-permute-start.4 = (bf16[4,104,768]{2,1,0:T(8,128)(2,1)S(1)}, bf16[4,104,768]{2,1,0:T(8,128)(2,1)S(1)}, u32[]{:S(2)}, u32[]{:S(2)}) collective-permute-start(bf16[4,104,768]{2,1,0:T(8,128)(2,1)S(1)} %pad_maximum_fusion), channel_id=1, source_target_pairs={{0,16},{1,17},{2,18},{3,19},{4,12},{5,13},{6,14},{7,15},{8,24},{9,... | collective-permute-start | bytes 1916936 | tf_op jit(solution)/shard_map/ppermute | solution.py:493
  22.4 8.9 %collective-permute-start.5 = (bf16[1,96,768]{2,1,0:T(8,128)(2,1)S(1)}, bf16[1,96,768]{2,1,0:T(8,128)(2,1)S(1)}, u32[]{:S(2)}, u32[]{:S(2)}) collective-permute-start(bf16[1,96,768]{2,1,0:T(8,128)(2,1)S(1)} %bitcast.142), channel_id=1, source_target_pairs={{0,1},{1,0},{2,3},{3,2},{4,5},{5,4},{6,7},{7,6},{8,9},{9,8},{10,11... | collective-permute-start | bytes 442376 | tf_op jit(solution)/shard_map/ppermute | solution.py:493
  25.0 12.7 %collective-permute-start.6 = (bf16[1,96,768]{2,1,0:T(8,128)(2,1)S(1)}, bf16[1,96,768]{2,1,0:T(8,128)(2,1)S(1)}, u32[]{:S(2)}, u32[]{:S(2)}) collective-permute-start(bf16[1,96,768]{2,1,0:T(8,128)(2,1)S(1)} %bitcast.143), channel_id=1, source_target_pairs={{0,2},{1,3},{2,0},{3,1},{4,6},{5,7},{6,4},{7,5},{8,10},{9,11},{10,... | collective-permute-start | bytes 442376 | tf_op jit(solution)/shard_map/ppermute | solution.py:493
  26.1 11.6 %collective-permute-start.7 = (bf16[1,96,768]{2,1,0:T(8,128)(2,1)S(1)}, bf16[1,96,768]{2,1,0:T(8,128)(2,1)S(1)}, u32[]{:S(2)}, u32[]{:S(2)}) collective-permute-start(bf16[1,96,768]{2,1,0:T(8,128)(2,1)S(1)} %bitcast.144), channel_id=1, source_target_pairs={{0,3},{1,2},{2,1},{3,0},{4,7},{5,6},{6,5},{7,4},{8,11},{9,10},{10,... | collective-permute-start | bytes 442376 | tf_op jit(solution)/shard_map/ppermute | solution.py:493
  27.5 13.1 %copy-start.21 = (bf16[768,96]{0,1:T(8,128)(2,1)S(1)}, bf16[768,96]{0,1:T(8,128)(2,1)}, u32[]{:S(2)}) copy-start(bf16[768,96]{0,1:T(8,128)(2,1)} %param.26) | copy-start | bytes 442372
  37.7 21.1 %collective-permute-start.8 = (bf16[8,104,768]{2,1,0:T(8,128)(2,1)S(1)}, bf16[8,104,768]{2,1,0:T(8,128)(2,1)S(1)}, u32[]{:S(2)}, u32[]{:S(2)}) collective-permute-start(bf16[8,104,768]{2,1,0:T(8,128)(2,1)S(1)} %constant_dynamic-update-slice_fusion), channel_id=1, source_target_pairs={{0,8},{1,9},{2,10},{3,11},{4,20},{5,21},{6,22},{7,23},{8,0},{9,1},... | collective-permute-start | bytes 3833864 | tf_op jit(solution)/shard_map/ppermute | solution.py:493
  38.3 17.6 %collective-permute-start.9 = (bf16[4,96,768]{2,1,0:T(8,128)(2,1)S(1)}, bf16[4,96,768]{2,1,0:T(8,128)(2,1)S(1)}, u32[]{:S(2)}, u32[]{:S(2)}) collective-permute-start(bf16[4,96,768]{2,1,0:T(8,128)(2,1)S(1)} %pad_maximum_fusion.1), channel_id=1, source_target_pairs={{0,16},{1,17},{2,18},{3,19},{4,12},{5,13},{6,14},{7,15},{8,24},{9,... | collective-permute-start | bytes 1769480 | tf_op jit(solution)/shard_map/ppermute | solution.py:493
  42.2 13.6 %collective-permute-start.10 = (bf16[2,96,768]{2,1,0:T(8,128)(2,1)}, bf16[2,96,768]{2,1,0:T(8,128)(2,1)S(1)}, u32[]{:S(2)}, u32[]{:S(2)}) collective-permute-start(bf16[2,96,768]{2,1,0:T(8,128)(2,1)} %pad_maximum_fusion.3), channel_id=1, source_target_pairs={{0,1},{1,0},{2,3},{3,2},{4,5},{5,4},{6,7},{7,6},{8,9},{9,8},{10,11... | collective-permute-start | bytes 884744 | tf_op jit(solution)/shard_map/ppermute | solution.py:564
  44.4 11.5 %collective-permute-start.11 = (bf16[2,96,768]{2,1,0:T(8,128)(2,1)}, bf16[2,96,768]{2,1,0:T(8,128)(2,1)S(1)}, u32[]{:S(2)}, u32[]{:S(2)}) collective-permute-start(bf16[2,96,768]{2,1,0:T(8,128)(2,1)} %pad_maximum_fusion.3), channel_id=1, source_target_pairs={{0,2},{1,3},{2,0},{3,1},{4,6},{5,7},{6,4},{7,5},{8,10},{9,11},{10,... | collective-permute-start | bytes 884744 | tf_op jit(solution)/shard_map/ppermute | solution.py:564
  47.5 18.6 %copy-start.24 = (s32[3,1,128]{2,1,0:T(1,128)S(1)}, s32[3,1,128]{2,1,0:T(1,128)}, u32[]{:S(2)}) copy-start(s32[3,1,128]{2,1,0:T(1,128)} %param.16) | copy-start | bytes 4612
  55.9 4.1 %copy-start.22 = (bf16[2,96,768]{2,1,0:T(8,128)(2,1)}, bf16[2,96,768]{2,1,0:T(8,128)(2,1)S(1)}, u32[]{:S(2)}) copy-start(bf16[2,96,768]{2,1,0:T(8,128)(2,1)S(1)} %collective-permute-done.11) | copy-start | bytes 884740
  55.9 10.3 %collective-permute-start.12 = (bf16[8,104,768]{2,1,0:T(8,128)(2,1)S(1)}, bf16[8,104,768]{2,1,0:T(8,128)(2,1)}, u32[]{:S(2)}, u32[]{:S(2)}) collective-permute-start(bf16[8,104,768]{2,1,0:T(8,128)(2,1)S(1)} %constant_dynamic-update-slice_fusion), channel_id=1, source_target_pairs={{0,4},{1,5},{2,6},{3,7},{4,0},{5,1},{6,2},{7,3},{8,12},{9,13},{10,... | collective-permute-start | bytes 3833864 | tf_op jit(solution)/shard_map/ppermute | solution.py:493
  58.8 7.4 %collective-permute-start.13 = (bf16[8,104,768]{2,1,0:T(8,128)(2,1)S(1)}, bf16[8,104,768]{2,1,0:T(8,128)(2,1)}, u32[]{:S(2)}, u32[]{:S(2)}) collective-permute-start(bf16[8,104,768]{2,1,0:T(8,128)(2,1)S(1)} %collective-permute-done.8), channel_id=1, source_target_pairs={{0,4},{1,5},{2,6},{3,7},{4,0},{5,1},{6,2},{7,3},{8,12},{9,13},{10,... | collective-permute-start | bytes 3833864 | tf_op jit(solution)/shard_map/ppermute | solution.py:493
  59.7 19.4 %collective-permute-start.14 = (bf16[8,96,768]{2,1,0:T(8,128)(2,1)}, bf16[8,96,768]{2,1,0:T(8,128)(2,1)}, u32[]{:S(2)}, u32[]{:S(2)}) collective-permute-start(bf16[8,96,768]{2,1,0:T(8,128)(2,1)} %constant_dynamic-update-slice_fusion.5), channel_id=1, source_target_pairs={{0,8},{1,9},{2,10},{3,11},{4,20},{5,21},{6,22},{7,23},{8,0},{9,1},... | collective-permute-start | bytes 3538952 | tf_op jit(solution)/shard_map/ppermute | solution.py:493
  59.9 19.1 %collective-permute-start.15 = (bf16[2,96,768]{2,1,0:T(8,128)(2,1)}, bf16[2,96,768]{2,1,0:T(8,128)(2,1)}, u32[]{:S(2)}, u32[]{:S(2)}) collective-permute-start(bf16[2,96,768]{2,1,0:T(8,128)(2,1)} %pad_maximum_fusion.3), channel_id=1, source_target_pairs={{0,3},{1,2},{2,1},{3,0},{4,7},{5,6},{6,5},{7,4},{8,11},{9,10},{10,... | collective-permute-start | bytes 884744 | tf_op jit(solution)/shard_map/ppermute | solution.py:564
  65.5 17.0 %collective-permute-start.19 = (bf16[4,96,768]{2,1,0:T(8,128)(2,1)S(1)}, bf16[4,96,768]{2,1,0:T(8,128)(2,1)}, u32[]{:S(2)}, u32[]{:S(2)}) collective-permute-start(bf16[4,96,768]{2,1,0:T(8,128)(2,1)S(1)} %pad_maximum_fusion.2), channel_id=1, source_target_pairs={{0,8},{1,9},{2,10},{3,11},{4,20},{5,21},{6,22},{7,23},{8,0},{9,1},... | collective-permute-start | bytes 1769480 | tf_op jit(solution)/shard_map/ppermute | solution.py:564
  67.3 12.3 %copy-start.23 = (bf16[2,96,768]{2,1,0:T(8,128)(2,1)S(1)}, bf16[2,96,768]{2,1,0:T(8,128)(2,1)}, u32[]{:S(2)}) copy-start(bf16[2,96,768]{2,1,0:T(8,128)(2,1)} %copy-done.22) | copy-start | bytes 884740
  79.1 6.5 %collective-permute-start.16 = (bf16[8,96,768]{2,1,0:T(8,128)(2,1)}, bf16[8,96,768]{2,1,0:T(8,128)(2,1)S(1)}, u32[]{:S(2)}, u32[]{:S(2)}) collective-permute-start(bf16[8,96,768]{2,1,0:T(8,128)(2,1)} %constant_dynamic-update-slice_fusion.5), channel_id=1, source_target_pairs={{0,4},{1,5},{2,6},{3,7},{4,0},{5,1},{6,2},{7,3},{8,12},{9,13},{10,... | collective-permute-start | bytes 3538952 | tf_op jit(solution)/shard_map/ppermute | solution.py:493
  79.1 6.4 %collective-permute-start.17 = (bf16[8,96,768]{2,1,0:T(8,128)(2,1)}, bf16[8,96,768]{2,1,0:T(8,128)(2,1)S(1)}, u32[]{:S(2)}, u32[]{:S(2)}) collective-permute-start(bf16[8,96,768]{2,1,0:T(8,128)(2,1)} %collective-permute-done.14), channel_id=1, source_target_pairs={{0,4},{1,5},{2,6},{3,7},{4,0},{5,1},{6,2},{7,3},{8,12},{9,13},{10,... | collective-permute-start | bytes 3538952 | tf_op jit(solution)/shard_map/ppermute | solution.py:493
  79.7 4.2 %collective-permute-start.18 = (bf16[4,96,768]{2,1,0:T(8,128)(2,1)S(1)}, bf16[4,96,768]{2,1,0:T(8,128)(2,1)S(1)}, u32[]{:S(2)}, u32[]{:S(2)}) collective-permute-start(bf16[4,96,768]{2,1,0:T(8,128)(2,1)S(1)} %pad_maximum_fusion.2), channel_id=1, source_target_pairs={{0,4},{1,5},{2,6},{3,7},{4,0},{5,1},{6,2},{7,3},{8,12},{9,13},{10,... | collective-permute-start | bytes 1769480 | tf_op jit(solution)/shard_map/ppermute | solution.py:484
  82.5 3.1 %collective-permute-start.20 = (bf16[4,96,768]{2,1,0:T(8,128)(2,1)}, bf16[4,96,768]{2,1,0:T(8,128)(2,1)S(1)}, u32[]{:S(2)}, u32[]{:S(2)}) collective-permute-start(bf16[4,96,768]{2,1,0:T(8,128)(2,1)} %collective-permute-done.19), channel_id=1, source_target_pairs={{0,4},{1,5},{2,6},{3,7},{4,0},{5,1},{6,2},{7,3},{8,12},{9,13},{10,... | collective-permute-start | bytes 1769480 | tf_op jit(solution)/shard_map/ppermute | solution.py:484
  83.5 9.9 %collective-permute-start.21 = (bf16[4,96,768]{2,1,0:T(8,128)(2,1)S(1)}, bf16[4,96,768]{2,1,0:T(8,128)(2,1)S(1)}, u32[]{:S(2)}, u32[]{:S(2)}) collective-permute-start(bf16[4,96,768]{2,1,0:T(8,128)(2,1)S(1)} %constant_dynamic-update-slice_fusion.10), channel_id=1, source_target_pairs={{0,8},{1,9},{2,10},{3,11},{4,20},{5,21},{6,22},{7,23},{8,0},{9,1},... | collective-permute-start | bytes 1769480 | tf_op jit(solution)/shard_map/ppermute | solution.py:564
  83.8 9.6 %collective-permute-start.22 = (bf16[4,96,768]{2,1,0:T(8,128)(2,1)S(1)}, bf16[4,96,768]{2,1,0:T(8,128)(2,1)S(1)}, u32[]{:S(2)}, u32[]{:S(2)}) collective-permute-start(bf16[4,96,768]{2,1,0:T(8,128)(2,1)S(1)} %constant_dynamic-update-slice_fusion.10), channel_id=1, source_target_pairs={{0,4},{1,5},{2,6},{3,7},{4,0},{5,1},{6,2},{7,3},{8,12},{9,13},{10,... | collective-permute-start | bytes 1769480 | tf_op jit(solution)/shard_map/ppermute | solution.py:484
  93.4 2.0 %collective-permute-start.23 = (bf16[4,96,768]{2,1,0:T(8,128)(2,1)S(1)}, bf16[4,96,768]{2,1,0:T(8,128)(2,1)S(1)}, u32[]{:S(2)}, u32[]{:S(2)}) collective-permute-start(bf16[4,96,768]{2,1,0:T(8,128)(2,1)S(1)} %collective-permute-done.21), channel_id=1, source_target_pairs={{0,4},{1,5},{2,6},{3,7},{4,0},{5,1},{6,2},{7,3},{8,12},{9,13},{10,... | collective-permute-start | bytes 1769480 | tf_op jit(solution)/shard_map/ppermute | solution.py:484
  95.4 9.2 %collective-permute-start.25 = (bf16[4,384,768]{2,1,0:T(8,128)(2,1)S(1)}, bf16[4,384,768]{2,1,0:T(8,128)(2,1)S(1)}, u32[]{:S(2)}, u32[]{:S(2)}) collective-permute-start(bf16[4,384,768]{2,1,0:T(8,128)(2,1)S(1)} %get-tuple-element.130.refs_1_), channel_id=1, source_target_pairs={{0,4},{1,5},{2,6},{3,7},{4,0},{5,1},{6,2},{7,3},{8,12},{9,13},{10,... | collective-permute-start | bytes 7077896 | tf_op jit(solution)/shard_map/ppermute | solution.py:484
  100.6 4.1 %collective-permute-start.24 = (bf16[384,384]{1,0:T(8,128)(2,1)S(1)}, bf16[384,384]{1,0:T(8,128)(2,1)S(1)}, u32[]{:S(2)}, u32[]{:S(2)}) collective-permute-start(bf16[384,384]{1,0:T(8,128)(2,1)S(1)} %get-tuple-element.129), channel_id=1, source_target_pairs={{0,4},{1,5},{2,6},{3,7},{4,0},{5,1},{6,2},{7,3},{8,12},{9,13},{10,... | collective-permute-start | bytes 884744 | tf_op jit(solution)/shard_map/ppermute | solution.py:484
  104.5 8.4 %collective-permute-start.27 = (bf16[4,384,768]{2,1,0:T(8,128)(2,1)S(1)}, bf16[4,384,768]{2,1,0:T(8,128)(2,1)S(1)}, u32[]{:S(2)}, u32[]{:S(2)}) collective-permute-start(bf16[4,384,768]{2,1,0:T(8,128)(2,1)S(1)} %bitcast.118), channel_id=1, source_target_pairs={{0,4},{1,5},{2,6},{3,7},{4,0},{5,1},{6,2},{7,3},{8,12},{9,13},{10,... | collective-permute-start | bytes 7077896 | tf_op jit(solution)/shard_map/ppermute | solution.py:484
  106.6 6.3 %collective-permute-start.26 = (bf16[384,384]{1,0:T(8,128)(2,1)S(1)}, bf16[384,384]{1,0:T(8,128)(2,1)S(1)}, u32[]{:S(2)}, u32[]{:S(2)}) collective-permute-start(bf16[384,384]{1,0:T(8,128)(2,1)S(1)} %copy-done.25), channel_id=1, source_target_pairs={{0,4},{1,5},{2,6},{3,7},{4,0},{5,1},{6,2},{7,3},{8,12},{9,13},{10,... | collective-permute-start | bytes 884744 | tf_op jit(solution)/shard_map/ppermute | solution.py:484
  107.0 16.2 %collective-permute-start.31 = (bf16[8,96,768]{2,1,0:T(8,128)(2,1)S(1)}, bf16[8,96,768]{2,1,0:T(8,128)(2,1)S(1)}, u32[]{:S(2)}, u32[]{:S(2)}) collective-permute-start(bf16[8,96,768]{2,1,0:T(8,128)(2,1)S(1)} %bitcast.124), channel_id=1, source_target_pairs={{0,8},{1,9},{2,10},{3,11},{4,20},{5,21},{6,22},{7,23},{8,0},{9,1},... | collective-permute-start | bytes 3538952 | tf_op jit(solution)/shard_map/ppermute | solution.py:513
  107.3 5.6 %copy-start.12 = (bf16[384,384]{1,0:T(8,128)(2,1)S(1)}, bf16[384,384]{1,0:T(8,128)(2,1)}, u32[]{:S(2)}) copy-start(bf16[384,384]{1,0:T(8,128)(2,1)} %get-tuple-element.138.refs_0_) | copy-start | bytes 884740
  112.9 5.2 %copy-start.6 = (bf16[4,384,256]{2,1,0:T(8,128)(2,1)S(1)}, bf16[4,384,256]{2,1,0:T(8,128)(2,1)}, u32[]{:S(2)}) copy-start(bf16[4,384,256]{2,1,0:T(8,128)(2,1)} %get-tuple-element.145.refs_7_) | copy-start | bytes 2359300
  112.9 5.2 %copy-start.15 = (bf16[384,384]{1,0:T(8,128)(2,1)S(1)}, bf16[384,384]{1,0:T(8,128)(2,1)}, u32[]{:S(2)}) copy-start(bf16[384,384]{1,0:T(8,128)(2,1)} %copy-done.14) | copy-start | bytes 884740
  116.2 20.0 %collective-permute-start.32 = (bf16[8,96,768]{2,1,0:T(8,128)(2,1)S(1)}, bf16[8,96,768]{2,1,0:T(8,128)(2,1)S(1)}, u32[]{:S(2)}, u32[]{:S(2)}) collective-permute-start(bf16[8,96,768]{2,1,0:T(8,128)(2,1)S(1)} %bitcast.134), channel_id=1, source_target_pairs={{0,8},{1,9},{2,10},{3,11},{4,20},{5,21},{6,22},{7,23},{8,0},{9,1},... | collective-permute-start | bytes 3538952 | tf_op jit(solution)/shard_map/ppermute | solution.py:513
  118.0 2.7 %collective-permute-start.30 = (bf16[4,384,256]{2,1,0:T(8,128)(2,1)S(1)}, bf16[4,384,256]{2,1,0:T(8,128)(2,1)S(1)}, u32[]{:S(2)}, u32[]{:S(2)}) collective-permute-start(bf16[4,384,256]{2,1,0:T(8,128)(2,1)S(1)} %copy-done.6), channel_id=1, source_target_pairs={{0,4},{1,5},{2,6},{3,7},{4,0},{5,1},{6,2},{7,3},{8,12},{9,13},{10,... | collective-permute-start | bytes 2359304 | tf_op jit(solution)/shard_map/ppermute | solution.py:484
  118.0 2.7 %collective-permute-start.29 = (bf16[384,384]{1,0:T(8,128)(2,1)S(1)}, bf16[384,384]{1,0:T(8,128)(2,1)S(1)}, u32[]{:S(2)}, u32[]{:S(2)}) collective-permute-start(bf16[384,384]{1,0:T(8,128)(2,1)S(1)} %copy-done.15), channel_id=1, source_target_pairs={{0,4},{1,5},{2,6},{3,7},{4,0},{5,1},{6,2},{7,3},{8,12},{9,13},{10,... | collective-permute-start | bytes 884744 | tf_op jit(solution)/shard_map/ppermute | solution.py:484
  118.5 2.6 %collective-permute-start.28 = (bf16[384,384]{1,0:T(8,128)(2,1)S(1)}, bf16[384,384]{1,0:T(8,128)(2,1)S(1)}, u32[]{:S(2)}, u32[]{:S(2)}) collective-permute-start(bf16[384,384]{1,0:T(8,128)(2,1)S(1)} %get-tuple-element.143), channel_id=1, source_target_pairs={{0,4},{1,5},{2,6},{3,7},{4,0},{5,1},{6,2},{7,3},{8,12},{9,13},{10,... | collective-permute-start | bytes 884744 | tf_op jit(solution)/shard_map/ppermute | solution.py:484
  118.6 4.7 %copy-start.4 = (f32[4,3,128,384]{3,2,1,0:T(8,128)S(1)}, f32[4,3,128,384]{3,2,1,0:T(8,128)}, u32[]{:S(2)}) copy-start(f32[4,3,128,384]{3,2,1,0:T(8,128)} %get-tuple-element.148.p_ref) | copy-start | bytes 7077892
  118.6 4.7 %copy-start.5 = (bf16[4,384,576]{2,1,0:T(8,128)(2,1)S(1)}, bf16[4,384,576]{2,1,0:T(8,128)(2,1)}, u32[]{:S(2)}) copy-start(bf16[4,384,576]{2,1,0:T(8,128)(2,1)} %get-tuple-element.147.qkv_ref) | copy-start | bytes 5308420
  131.9 6.8 %collective-permute-start.33 = (bf16[2,384,640]{2,1,0:T(8,128)(2,1)S(1)}, bf16[2,384,640]{2,1,0:T(8,128)(2,1)S(1)}, u32[]{:S(2)}, u32[]{:S(2)}) collective-permute-start(bf16[2,384,640]{2,1,0:T(8,128)(2,1)S(1)} %get-tuple-element.158.refs_1_.low_ref), channel_id=1, source_target_pairs={{0,4},{1,5},{2,6},{3,7},{4,0},{5,1},{6,2},{7,3},{8,12},{9,13},{10,... | collective-permute-start | bytes 2949128 | tf_op jit(solution)/shard_map/ppermute | solution.py:484
  132.0 6.7 %collective-permute-start.34 = (bf16[2,384,640]{2,1,0:T(8,128)(2,1)S(1)}, bf16[2,384,640]{2,1,0:T(8,128)(2,1)S(1)}, u32[]{:S(2)}, u32[]{:S(2)}) collective-permute-start(bf16[2,384,640]{2,1,0:T(8,128)(2,1)S(1)} %get-tuple-element.159.refs_2_.high_ref), channel_id=1, source_target_pairs={{0,4},{1,5},{2,6},{3,7},{4,0},{5,1},{6,2},{7,3},{8,12},{9,13},{10,... | collective-permute-start | bytes 2949128 | tf_op jit(solution)/shard_map/ppermute | solution.py:484
  132.8 4.0 %copy-start.18 = (pred[768,768]{1,0:T(32,128)(4,1)S(1)}, pred[768,768]{1,0:T(32,128)(4,1)}, u32[]{:S(2)}) copy-start(pred[768,768]{1,0:T(32,128)(4,1)} %copy-done.17) | copy-start | bytes 1769476
  132.8 10.3 %collective-permute-start.36 = (bf16[4,96,768]{2,1,0:T(8,128)(2,1)S(1)}, bf16[4,96,768]{2,1,0:T(8,128)(2,1)S(1)}, u32[]{:S(2)}, u32[]{:S(2)}) collective-permute-start(bf16[4,96,768]{2,1,0:T(8,128)(2,1)S(1)} %get-tuple-element.218), channel_id=1, source_target_pairs={{0,16},{1,17},{2,18},{3,19},{4,12},{5,13},{6,14},{7,15},{8,24},{9,... | collective-permute-start | bytes 1769480 | tf_op jit(solution)/shard_map/ppermute | solution.py:513
  136.4 12.7 %collective-permute-start.37 = (bf16[4,96,768]{2,1,0:T(8,128)(2,1)S(1)}, bf16[4,96,768]{2,1,0:T(8,128)(2,1)S(1)}, u32[]{:S(2)}, u32[]{:S(2)}) collective-permute-start(bf16[4,96,768]{2,1,0:T(8,128)(2,1)S(1)} %get-tuple-element.220), channel_id=1, source_target_pairs={{0,16},{1,17},{2,18},{3,19},{4,12},{5,13},{6,14},{7,15},{8,24},{9,... | collective-permute-start | bytes 1769480 | tf_op jit(solution)/shard_map/ppermute | solution.py:513
  136.8 2.0 collective-permute-start.35
  149.1 17.3 %collective-permute-start.38 = (bf16[8,104,768]{2,1,0:T(8,128)(2,1)S(1)}, bf16[8,104,768]{2,1,0:T(8,128)(2,1)S(1)}, u32[]{:S(2)}, u32[]{:S(2)}) collective-permute-start(bf16[8,104,768]{2,1,0:T(8,128)(2,1)S(1)} %bitcast.133), channel_id=1, source_target_pairs={{0,8},{1,9},{2,10},{3,11},{4,20},{5,21},{6,22},{7,23},{8,0},{9,1},... | collective-permute-start | bytes 3833864 | tf_op jit(solution)/shard_map/ppermute | solution.py:513
  149.6 7.4 %copy-start.3 = (bf16[768,768]{1,0:T(8,128)(2,1)S(1)}, bf16[768,768]{1,0:T(8,128)(2,1)}, u32[]{:S(2)}) copy-start(bf16[768,768]{1,0:T(8,128)(2,1)} %copy-done.2) | copy-start | bytes 3538948
  149.7 18.9 %collective-permute-start.41 = (bf16[2,96,768]{2,1,0:T(8,128)(2,1)S(1)}, bf16[2,96,768]{2,1,0:T(8,128)(2,1)S(1)}, u32[]{:S(2)}, u32[]{:S(2)}) collective-permute-start(bf16[2,96,768]{2,1,0:T(8,128)(2,1)S(1)} %pad_maximum_fusion.4), channel_id=1, source_target_pairs={{0,1},{1,0},{2,3},{3,2},{4,5},{5,4},{6,7},{7,6},{8,9},{9,8},{10,11... | collective-permute-start | bytes 884744 | tf_op jit(solution)/shard_map/ppermute | solution.py:513
  153.4 23.5 %collective-permute-start.42 = (bf16[2,96,768]{2,1,0:T(8,128)(2,1)S(1)}, bf16[2,96,768]{2,1,0:T(8,128)(2,1)S(1)}, u32[]{:S(2)}, u32[]{:S(2)}) collective-permute-start(bf16[2,96,768]{2,1,0:T(8,128)(2,1)S(1)} %pad_maximum_fusion.5), channel_id=1, source_target_pairs={{0,2},{1,3},{2,0},{3,1},{4,6},{5,7},{6,4},{7,5},{8,10},{9,11},{10,... | collective-permute-start | bytes 884744 | tf_op jit(solution)/shard_map/ppermute | solution.py:513
  155.5 21.5 %collective-permute-start.43 = (bf16[2,96,768]{2,1,0:T(8,128)(2,1)S(1)}, bf16[2,96,768]{2,1,0:T(8,128)(2,1)S(1)}, u32[]{:S(2)}, u32[]{:S(2)}) collective-permute-start(bf16[2,96,768]{2,1,0:T(8,128)(2,1)S(1)} %pad_maximum_fusion.6), channel_id=1, source_target_pairs={{0,3},{1,2},{2,1},{3,0},{4,7},{5,6},{6,5},{7,4},{8,11},{9,10},{10,... | collective-permute-start | bytes 884744 | tf_op jit(solution)/shard_map/ppermute | solution.py:513
  166.5 11.2 %collective-permute-start.40 = (bf16[1,104,768]{2,1,0:T(8,128)(2,1)S(1)}, bf16[1,104,768]{2,1,0:T(8,128)(2,1)S(1)}, u32[]{:S(2)}, u32[]{:S(2)}) collective-permute-start(bf16[1,104,768]{2,1,0:T(8,128)(2,1)S(1)} %get-tuple-element.164), channel_id=1, source_target_pairs={{0,16},{1,17},{2,18},{3,19},{4,12},{5,13},{6,14},{7,15},{8,24},{9,... | collective-permute-start | bytes 479240 | tf_op jit(solution)/shard_map/ppermute | solution.py:513
  166.8 10.9 %collective-permute-start.47 = (bf16[1,104,768]{2,1,0:T(8,128)(2,1)S(1)}, bf16[1,104,768]{2,1,0:T(8,128)(2,1)S(1)}, u32[]{:S(2)}, u32[]{:S(2)}) collective-permute-start(bf16[1,104,768]{2,1,0:T(8,128)(2,1)S(1)} %get-tuple-element.168), channel_id=1, source_target_pairs={{0,16},{1,17},{2,18},{3,19},{4,12},{5,13},{6,14},{7,15},{8,24},{9,... | collective-permute-start | bytes 479240 | tf_op jit(solution)/shard_map/ppermute | solution.py:513
  168.6 9.1 %collective-permute-start.45 = (bf16[1,104,768]{2,1,0:T(8,128)(2,1)S(1)}, bf16[1,104,768]{2,1,0:T(8,128)(2,1)S(1)}, u32[]{:S(2)}, u32[]{:S(2)}) collective-permute-start(bf16[1,104,768]{2,1,0:T(8,128)(2,1)S(1)} %get-tuple-element.166), channel_id=1, source_target_pairs={{0,16},{1,17},{2,18},{3,19},{4,12},{5,13},{6,14},{7,15},{8,24},{9,... | collective-permute-start | bytes 479240 | tf_op jit(solution)/shard_map/ppermute | solution.py:513
  177.1 11.8 %collective-permute-start.39 = (bf16[1,104,768]{2,1,0:T(8,128)(2,1)S(1)}, bf16[1,104,768]{2,1,0:T(8,128)(2,1)S(1)}, u32[]{:S(2)}, u32[]{:S(2)}) collective-permute-start(bf16[1,104,768]{2,1,0:T(8,128)(2,1)S(1)} %get-tuple-element.163), channel_id=1, source_target_pairs={{0,16},{1,17},{2,18},{3,19},{4,12},{5,13},{6,14},{7,15},{8,24},{9,... | collective-permute-start | bytes 479240 | tf_op jit(solution)/shard_map/ppermute | solution.py:513
  177.9 11.0 %collective-permute-start.48 = (bf16[1,104,768]{2,1,0:T(8,128)(2,1)S(1)}, bf16[1,104,768]{2,1,0:T(8,128)(2,1)S(1)}, u32[]{:S(2)}, u32[]{:S(2)}) collective-permute-start(bf16[1,104,768]{2,1,0:T(8,128)(2,1)S(1)} %get-tuple-element.169), channel_id=1, source_target_pairs={{0,3},{1,2},{2,1},{3,0},{4,7},{5,6},{6,5},{7,4},{8,11},{9,10},{10,... | collective-permute-start | bytes 479240 | tf_op jit(solution)/shard_map/ppermute | solution.py:513
  181.4 14.0 %collective-permute-start.46 = (bf16[1,104,768]{2,1,0:T(8,128)(2,1)S(1)}, bf16[1,104,768]{2,1,0:T(8,128)(2,1)S(1)}, u32[]{:S(2)}, u32[]{:S(2)}) collective-permute-start(bf16[1,104,768]{2,1,0:T(8,128)(2,1)S(1)} %get-tuple-element.167), channel_id=1, source_target_pairs={{0,2},{1,3},{2,0},{3,1},{4,6},{5,7},{6,4},{7,5},{8,10},{9,11},{10,... | collective-permute-start | bytes 479240 | tf_op jit(solution)/shard_map/ppermute | solution.py:513
  187.6 8.8 %copy-start.1 = (f32[3,1,8,768]{3,2,1,0:T(8,128)S(1)}, f32[3,1,8,768]{3,2,1,0:T(8,128)}, u32[]{:S(2)}) copy-start(f32[3,1,8,768]{3,2,1,0:T(8,128)} %param.17) | copy-start | bytes 221188
  187.6 7.7 %collective-permute-start.44 = (bf16[1,104,768]{2,1,0:T(8,128)(2,1)S(1)}, bf16[1,104,768]{2,1,0:T(8,128)(2,1)S(1)}, u32[]{:S(2)}, u32[]{:S(2)}) collective-permute-start(bf16[1,104,768]{2,1,0:T(8,128)(2,1)S(1)} %get-tuple-element.165), channel_id=1, source_target_pairs={{0,1},{1,0},{2,3},{3,2},{4,5},{5,4},{6,7},{7,6},{8,9},{9,8},{10,11... | collective-permute-start | bytes 479240 | tf_op jit(solution)/shard_map/ppermute | solution.py:513
  (11 other events, 19.7 us)
